TPU v7x, 32 devices: a whole 2x2x4 slice. The times are simulated.
32 devices in a mesh: clip: 16 (over z, x, core), frame: 2 (over y).
Axes of the slice: x: 2, y: 2, z: 4, core: 2. Of those that a mesh axis runs over, the one named last changes fastest.
Arguments:
- inputs: bfloat16 [16, 1500, 768], P('clip', 'frame'), may hold values from -6 to 6
- cotangent: bfloat16 [16, 1500, 768], P('clip', 'frame'), may hold values from -2 to 2
- project_in: float32 [768, 2304], P(('clip', 'frame'))
- project_out: float32 [768, 768], P(('clip', 'frame')), may hold values from -0.1875 to 0.1875
- expand_weight: float32 [768, 3072], P(('clip', 'frame')), may hold values from -0.21875 to 0.21875
- shrink_weight: float32 [3072, 768], P(('clip', 'frame')), may hold values from -0.15625 to 0.15625
- expand_bias: float32 [3072], P(('clip', 'frame')), may hold values from -3 to 3
- vectors: float32 [768, 8], P(('clip', 'frame'))
- moments_in: float32 [2, 768, 2304], P(None, ('clip', 'frame')), as said below
- moments_out: float32 [2, 768, 768], P(None, ('clip', 'frame'))
- moments_expand: float32 [2, 768, 3072], P(None, ('clip', 'frame'))
- moments_shrink: float32 [2, 3072, 768], P(None, ('clip', 'frame'))
- moments_bias: float32 [2, 3072], P(None, ('clip', 'frame'))
- moments_vectors: float32 [2, 768, 8], P(None, ('clip', 'frame'))
Outputs:
- output: bfloat16 [16, 1500, 768], P('clip', 'frame')
- grad_inputs: bfloat16 [16, 1500, 768], P('clip', 'frame')
- grad_project_in: float32 [768, 2304], P(('clip', 'frame'))
- grad_project_out: float32 [768, 768], P(('clip', 'frame'))
- grad_expand: float32 [768, 3072], P(('clip', 'frame'))
- grad_shrink: float32 [3072, 768], P(('clip', 'frame'))
- grad_bias: float32 [3072], P(('clip', 'frame'))
- grad_vectors: float32 [768, 8], P(('clip', 'frame'))
- new_project_in: float32 [768, 2304], P(('clip', 'frame'))
- new_project_out: float32 [768, 768], P(('clip', 'frame'))
- new_expand: float32 [768, 3072], P(('clip', 'frame'))
- new_shrink: float32 [3072, 768], P(('clip', 'frame'))
- new_bias: float32 [3072], P(('clip', 'frame'))
- new_vectors: float32 [768, 8], P(('clip', 'frame'))
- new_moments_in: float32 [2, 768, 2304], P(None, ('clip', 'frame'))
- new_moments_out: float32 [2, 768, 768], P(None, ('clip', 'frame'))
- new_moments_expand: float32 [2, 768, 3072], P(None, ('clip', 'frame'))
- new_moments_shrink: float32 [2, 3072, 768], P(None, ('clip', 'frame'))
- new_moments_bias: float32 [2, 3072], P(None, ('clip', 'frame'))
- new_moments_vectors: float32 [2, 768, 8], P(None, ('clip', 'frame'))
Inputs may be any that keep to these rules, and one draw needn't show every extreme that they name: `moments_in`: the first row of each moments array is signed, the second positive.
All inputs are finite; a program needn't handle non-finite values.
Results may differ from a plain program's by a relative error of at most 0.013.
The roundings to bfloat16 on the way count: a program that leaves them out, or rounds other values in their place, can miss the bound.
Values may be sent and summed in bfloat16 or wider, within the bound.
A program may use at most 192 MiB of HBM per device.

v0:
```python
import math

import jax
import jax.numpy as jnp
from jax import lax
from jax.sharding import PartitionSpec as P

HEADS = 12
ADAM_STEP = 4


epsilon_norm = 1e-05
beta_first = 0.9
beta_second = 0.99
learn_rate = 0.03
decay_rate = 0.01
epsilon_adam = 1e-08
root_half = 0.7071067811865476
inv_root_two_pi = 0.3989422804014327


def norm_parts(inputs, norm_gain, norm_shift):
    average = jnp.mean(inputs, axis=-1, keepdims=True)
    centered = inputs - average
    spread = jnp.mean(centered * centered, axis=-1, keepdims=True)
    inv_std = lax.rsqrt(spread + epsilon_norm)
    normed = centered * inv_std
    return (normed * norm_gain + norm_shift, normed, inv_std)


def norm_backward(grad_normed, normed, inv_std, norm_gain):
    grad_gain = jnp.sum(grad_normed * normed, axis=0)
    grad_shift = jnp.sum(grad_normed, axis=0)
    scaled = grad_normed * norm_gain
    grad_input = inv_std * (
        scaled
        - jnp.mean(scaled, axis=-1, keepdims=True)
        - normed * jnp.mean(scaled * normed, axis=-1, keepdims=True)
    )
    return (grad_input, grad_gain, grad_shift)


def gelu_exact(inputs):
    return 0.5 * inputs * (1.0 + jax.scipy.special.erf(inputs * root_half))


def gelu_slope(inputs):
    return (
        0.5 * (1.0 + jax.scipy.special.erf(inputs * root_half))
        + inputs * jnp.exp(-0.5 * inputs * inputs) * inv_root_two_pi
    )


def attend_forward(queries, keys_values, head_count):
    model_width = queries.shape[2]
    head_size = model_width // head_count
    score_scale = 1.0 / math.sqrt(head_size)

    def one_head(head_index):
        offset = head_index * head_size
        query_block = lax.dynamic_slice_in_dim(queries, offset, head_size, 2)
        key_block = lax.dynamic_slice_in_dim(keys_values, offset, head_size, 2)
        value_block = lax.dynamic_slice_in_dim(keys_values, model_width + offset, head_size, 2)
        scores = (
            jnp.einsum("cqd,ckd->cqk", query_block, key_block, preferred_element_type=jnp.float32)
            * score_scale
        )
        highest = jnp.max(scores, axis=-1, keepdims=True)
        exponent = jnp.exp(scores - highest)
        denominator = jnp.sum(exponent, axis=-1, keepdims=True)
        weights_soft = (exponent / denominator).astype(jnp.bfloat16)
        mixed = jnp.einsum(
            "cqk,ckd->cqd", weights_soft, value_block, preferred_element_type=jnp.float32
        )
        return (mixed, (highest + jnp.log(denominator))[..., 0])

    mixed, log_totals = lax.map(one_head, jnp.arange(head_count))
    clip_count, frame_count = (queries.shape[0], queries.shape[1])
    mixed = jnp.transpose(mixed, (1, 2, 0, 3)).reshape(clip_count, frame_count, model_width)
    return (mixed, log_totals)


def attend_backward(queries, keys_values, grad_mixed, log_totals, head_count):
    model_width = queries.shape[2]
    head_size = model_width // head_count
    score_scale = 1.0 / math.sqrt(head_size)

    def one_head_back(head_index):
        offset = head_index * head_size
        query_block = lax.dynamic_slice_in_dim(queries, offset, head_size, 2)
        key_block = lax.dynamic_slice_in_dim(keys_values, offset, head_size, 2)
        value_block = lax.dynamic_slice_in_dim(keys_values, model_width + offset, head_size, 2)
        grad_block = lax.dynamic_slice_in_dim(grad_mixed, offset, head_size, 2)
        totals = lax.dynamic_index_in_dim(log_totals, head_index, 0, keepdims=False)
        scores = (
            jnp.einsum("cqd,ckd->cqk", query_block, key_block, preferred_element_type=jnp.float32)
            * score_scale
        )
        weights_soft = jnp.exp(scores - totals[..., None])
        grad_weights = jnp.einsum(
            "cqd,ckd->cqk", grad_block, value_block, preferred_element_type=jnp.float32
        )
        delta = jnp.sum(weights_soft * grad_weights, axis=-1, keepdims=True)
        grad_scores = (weights_soft * (grad_weights - delta)).astype(jnp.bfloat16)
        grad_query = (
            jnp.einsum("cqk,ckd->cqd", grad_scores, key_block, preferred_element_type=jnp.float32)
            * score_scale
        )
        grad_key = (
            jnp.einsum("cqk,cqd->ckd", grad_scores, query_block, preferred_element_type=jnp.float32)
            * score_scale
        )
        grad_value = jnp.einsum(
            "cqk,cqd->ckd",
            weights_soft.astype(jnp.bfloat16),
            grad_block,
            preferred_element_type=jnp.float32,
        )
        return (grad_query, delta[..., 0], grad_key, grad_value)

    pieces = lax.map(one_head_back, jnp.arange(head_count))
    clip_count, frame_count = (queries.shape[0], queries.shape[1])
    clip_frames = keys_values.shape[1]
    grad_query = jnp.transpose(pieces[0], (1, 2, 0, 3)).reshape(
        clip_count, frame_count, model_width
    )
    grad_key = jnp.transpose(pieces[2], (1, 2, 0, 3)).reshape(clip_count, clip_frames, model_width)
    grad_value = jnp.transpose(pieces[3], (1, 2, 0, 3)).reshape(
        clip_count, clip_frames, model_width
    )
    return (grad_query, pieces[1], jnp.concatenate([grad_key, grad_value], axis=2))


def adam_step(weight, moments, gradient):
    first = beta_first * moments[0] + (1.0 - beta_first) * gradient
    second = beta_second * moments[1] + (1.0 - beta_second) * gradient * gradient
    first_hat = first / (1.0 - beta_first**ADAM_STEP)
    second_hat = second / (1.0 - beta_second**ADAM_STEP)
    change = -learn_rate * (first_hat / (jnp.sqrt(second_hat) + epsilon_adam) + decay_rate * weight)
    return (change, jnp.stack([first, second]))


def body(
    inputs,
    cotangent,
    project_in,
    project_out,
    expand_weight,
    shrink_weight,
    expand_bias,
    vectors,
    moments_in,
    moments_out,
    moments_expand,
    moments_shrink,
    moments_bias,
    moments_vectors,
):
    clip_count, frame_count, model_width = inputs.shape
    row_count = clip_count * frame_count
    head_count = HEADS
    low_in = project_in.astype(jnp.bfloat16)
    low_out = project_out.astype(jnp.bfloat16)
    low_expand = expand_weight.astype(jnp.bfloat16)
    low_shrink = shrink_weight.astype(jnp.bfloat16)
    low_vectors = vectors.astype(jnp.bfloat16)
    full_in, full_out, full_expand, full_shrink, full_bias, full_vectors = (
        lax.all_gather(low_in, ("clip", "frame"), axis=0, tiled=True),
        lax.all_gather(low_out, ("clip", "frame"), axis=0, tiled=True),
        lax.all_gather(low_expand, ("clip", "frame"), axis=0, tiled=True),
        lax.all_gather(low_shrink, ("clip", "frame"), axis=0, tiled=True),
        lax.all_gather(expand_bias.astype(jnp.bfloat16), ("clip", "frame"), axis=0, tiled=True),
        lax.all_gather(low_vectors, ("clip", "frame"), axis=0, tiled=True),
    )
    column_set = full_vectors.astype(jnp.float32)
    frames_rows = inputs.reshape(row_count, model_width).astype(jnp.float32)
    normed_first, plain_first, inv_first = norm_parts(
        frames_rows, column_set[:, 0], column_set[:, 1]
    )
    hidden_first = normed_first.astype(jnp.bfloat16)
    bias_in = jnp.concatenate(
        [column_set[:, 2], jnp.zeros((model_width,), jnp.float32), column_set[:, 3]]
    )
    projected = (
        jnp.dot(hidden_first, full_in, preferred_element_type=jnp.float32) + bias_in
    ).astype(jnp.bfloat16)
    queries = projected[:, :model_width].reshape(clip_count, frame_count, model_width)
    local_pairs = projected[:, model_width:].reshape(clip_count, frame_count, 2 * model_width)
    clip_pairs = lax.all_gather(local_pairs, "frame", axis=1, tiled=True)
    mixed, log_totals = attend_forward(queries, clip_pairs, head_count)
    mixed_low = mixed.reshape(row_count, model_width).astype(jnp.bfloat16)
    attended = jnp.dot(mixed_low, full_out, preferred_element_type=jnp.float32) + column_set[:, 4]
    residual = frames_rows + attended
    normed_second, plain_second, inv_second = norm_parts(
        residual, column_set[:, 5], column_set[:, 6]
    )
    hidden_second = normed_second.astype(jnp.bfloat16)
    preact = jnp.dot(
        hidden_second, full_expand, preferred_element_type=jnp.float32
    ) + full_bias.astype(jnp.float32)
    activated = gelu_exact(preact).astype(jnp.bfloat16)
    result = (
        residual
        + jnp.dot(activated, full_shrink, preferred_element_type=jnp.float32)
        + column_set[:, 7]
    )
    output = result.astype(jnp.bfloat16).reshape(inputs.shape)
    back_in, back_out, back_expand, back_shrink, back_vectors = (
        lax.all_gather(low_in, ("clip", "frame"), axis=0, tiled=True),
        lax.all_gather(low_out, ("clip", "frame"), axis=0, tiled=True),
        lax.all_gather(low_expand, ("clip", "frame"), axis=0, tiled=True),
        lax.all_gather(low_shrink, ("clip", "frame"), axis=0, tiled=True),
        lax.all_gather(low_vectors, ("clip", "frame"), axis=0, tiled=True),
    )
    back_columns = back_vectors.astype(jnp.float32)
    grad_result = cotangent.reshape(row_count, model_width)
    grad_shrink_term = jnp.dot(activated.T, grad_result, preferred_element_type=jnp.float32)
    grad_down_bias = jnp.sum(grad_result.astype(jnp.float32), axis=0)
    grad_activated = jnp.dot(grad_result, back_shrink.T, preferred_element_type=jnp.float32)
    grad_preact = (grad_activated * gelu_slope(preact)).astype(jnp.bfloat16)
    grad_expand_term = jnp.dot(hidden_second.T, grad_preact, preferred_element_type=jnp.float32)
    grad_bias_term = jnp.sum(grad_preact.astype(jnp.float32), axis=0)
    grad_hidden_second = jnp.dot(grad_preact, back_expand.T, preferred_element_type=jnp.float32)
    norm_term_second, gain_second, shift_second = norm_backward(
        grad_hidden_second, plain_second, inv_second, back_columns[:, 5]
    )
    grad_residual = grad_result.astype(jnp.float32) + norm_term_second
    grad_attended = grad_residual.astype(jnp.bfloat16)
    grad_out_term = jnp.dot(mixed_low.T, grad_attended, preferred_element_type=jnp.float32)
    grad_out_bias = jnp.sum(grad_attended.astype(jnp.float32), axis=0)
    grad_mixed = jnp.dot(grad_attended, back_out.T, preferred_element_type=jnp.float32).astype(
        jnp.bfloat16
    )
    grad_mixed = grad_mixed.reshape(clip_count, frame_count, model_width)
    pairs_back = lax.all_gather(local_pairs, "frame", axis=1, tiled=True)
    grad_query, delta_rows, grad_pairs_terms = attend_backward(
        queries, pairs_back, grad_mixed, log_totals, head_count
    )
    block_count = grad_pairs_terms.shape[1] // frame_count
    blocked_terms = grad_pairs_terms.reshape(clip_count, block_count, frame_count, 2 * model_width)
    blocked_terms = jnp.swapaxes(blocked_terms, 0, 1)
    owned_pairs = lax.psum_scatter(blocked_terms, "frame", scatter_dimension=0, tiled=True)
    grad_pairs = owned_pairs.reshape(clip_count, frame_count, 2 * model_width)
    grad_projected = (
        jnp.concatenate([grad_query, grad_pairs], axis=2)
        .reshape(row_count, 3 * model_width)
        .astype(jnp.bfloat16)
    )
    grad_in_term = jnp.dot(hidden_first.T, grad_projected, preferred_element_type=jnp.float32)
    projected_sums = jnp.sum(grad_projected.astype(jnp.float32), axis=0)
    grad_query_bias = projected_sums[:model_width]
    grad_value_bias = projected_sums[2 * model_width :]
    grad_hidden_first = jnp.dot(grad_projected, back_in.T, preferred_element_type=jnp.float32)
    norm_term_first, gain_first, shift_first = norm_backward(
        grad_hidden_first, plain_first, inv_first, back_columns[:, 0]
    )
    grad_inputs = (grad_residual + norm_term_first).astype(jnp.bfloat16).reshape(inputs.shape)
    grad_columns = jnp.stack(
        [
            gain_first,
            shift_first,
            grad_query_bias,
            grad_value_bias,
            grad_out_bias,
            gain_second,
            shift_second,
            grad_down_bias,
        ],
        axis=1,
    )
    owned_in, owned_out, owned_expand, owned_shrink, owned_bias, owned_vectors = (
        lax.psum_scatter(grad_in_term, ("clip", "frame"), scatter_dimension=0, tiled=True),
        lax.psum_scatter(grad_out_term, ("clip", "frame"), scatter_dimension=0, tiled=True),
        lax.psum_scatter(grad_expand_term, ("clip", "frame"), scatter_dimension=0, tiled=True),
        lax.psum_scatter(grad_shrink_term, ("clip", "frame"), scatter_dimension=0, tiled=True),
        lax.psum_scatter(grad_bias_term, ("clip", "frame"), scatter_dimension=0, tiled=True),
        lax.psum_scatter(grad_columns, ("clip", "frame"), scatter_dimension=0, tiled=True),
    )
    new_in, mom_in = adam_step(project_in, moments_in, owned_in)
    new_out, mom_out = adam_step(project_out, moments_out, owned_out)
    new_expand, mom_expand = adam_step(expand_weight, moments_expand, owned_expand)
    new_shrink, mom_shrink = adam_step(shrink_weight, moments_shrink, owned_shrink)
    new_bias, mom_bias = adam_step(expand_bias, moments_bias, owned_bias)
    new_vectors, mom_vectors = adam_step(vectors, moments_vectors, owned_vectors)
    return (
        output,
        grad_inputs,
        owned_in,
        owned_out,
        owned_expand,
        owned_shrink,
        owned_bias,
        owned_vectors,
        new_in,
        new_out,
        new_expand,
        new_shrink,
        new_bias,
        new_vectors,
        mom_in,
        mom_out,
        mom_expand,
        mom_shrink,
        mom_bias,
        mom_vectors,
    )


def solution(mesh):
    in_specs = (
        P("clip", "frame", None),
        P("clip", "frame", None),
        P(("clip", "frame"), None),
        P(("clip", "frame"), None),
        P(("clip", "frame"), None),
        P(("clip", "frame"), None),
        P(("clip", "frame")),
        P(("clip", "frame"), None),
        P(None, ("clip", "frame"), None),
        P(None, ("clip", "frame"), None),
        P(None, ("clip", "frame"), None),
        P(None, ("clip", "frame"), None),
        P(None, ("clip", "frame")),
        P(None, ("clip", "frame"), None),
    )
    out_specs = (
        P("clip", "frame", None),
        P("clip", "frame", None),
        P(("clip", "frame"), None),
        P(("clip", "frame"), None),
        P(("clip", "frame"), None),
        P(("clip", "frame"), None),
        P(("clip", "frame")),
        P(("clip", "frame"), None),
        P(("clip", "frame"), None),
        P(("clip", "frame"), None),
        P(("clip", "frame"), None),
        P(("clip", "frame"), None),
        P(("clip", "frame")),
        P(("clip", "frame"), None),
        P(None, ("clip", "frame"), None),
        P(None, ("clip", "frame"), None),
        P(None, ("clip", "frame"), None),
        P(None, ("clip", "frame"), None),
        P(None, ("clip", "frame")),
        P(None, ("clip", "frame"), None),
    )
    return jax.shard_map(body, mesh=mesh, in_specs=in_specs, out_specs=out_specs, check_vma=False)
```

profile of v0, /device:TPU:0, one launch (start us, length us, event | category | flops | bytes accessed | tf_op | source)
XLA Modules:
  0.0 2759.8 jit_solution(13350167980061855374)
XLA Ops:
  9.7 70.5 %all-gather.1 = bf16[32,24,8]{1,2,0:T(8,128)(2,1)S(1)} all-gather(bf16[1,24,8]{1,2,0:T(8,128)(2,1)S(1)} %convert_bitcast_fusion.1), channel_id=1, replica_groups=mesh['clip'=16,'frame'=2] {'clip','frame'}, dimensions={0}, use_global_device_ids=true | all-gather | bytes 12672 | tf_op jit(solution)/shard_map/all_gather | solution.py:173
  83.2 5.5 add_convert_fusion
  94.7 37.7 %all-reduce = bf16[3072]{0:T(1024)(128)(2,1)S(1)} all-reduce(bf16[3072]{0:T(1024)(128)(2,1)S(1)} %dynamic-update-slice), channel_id=1, replica_groups=mesh['clip'=16,'frame'=2] {'clip','frame'}, use_global_device_ids=true, to_apply=%add | all-reduce | flops 3072 | bytes 12288
  133.7 16.9 all-gather.17.cloned.1.call-done
  150.6 5.3 reshape.337
  156.0 119.2 %while.30 = (s32[]{:T(128)}, bf16[12,1,750,64]{2,3,1,0:T(8,128)(2,1)S(1)}, f32[12,1,750]{2,1,0:T(1,128)S(1)}, s32[12]{0:T(128)S(1)}, bf16[1,750,768]{2,1,0:T(8,1...) while((s32[]{:T(128)}, ...), condition=%wide.region_5.6_spmd, body=%wide.region_2.5_spmd.sunk | while | flops 298124256 | bytes 32813104 | solution.py:77
  162.2 3.6 fusion.151
  172.1 3.6 fusion.151
  182.0 3.7 fusion.151
  192.0 3.7 fusion.151
  201.9 3.6 fusion.151
  211.8 3.6 fusion.151
  221.7 3.6 fusion.151
  231.6 3.6 fusion.151
  241.6 3.6 fusion.151
  261.3 3.6 fusion.151
  271.3 3.8 fusion.151
  279.8 9.7 multiply_convert_fusion.1
  291.7 6.4 fusion.78
  298.2 135.3 %reduce-scatter.12.cloned.1.call-done = f32[96,768]{1,0:T(8,128)} async-done(((f32[3072,768]{1,0:T(8,128)}), f32[96,768]{1,0:T(8,128)}) %reduce-scatter.12.cloned.1.call-update) | async-done | bytes 294928 | tf_op jit(solution)/shard_map/reduce_scatter | solution.py:275
  437.0 63.2 %all-gather.15.cloned.1.call-done = bf16[3072,768]{1,0:T(8,128)(2,1)} async-done(((bf16[96,768]{1,0:T(8,128)(2,1)}), bf16[3072,768]{1,0:T(8,128)(2,1)}) %all-gather.15.cloned.1.call-update) | async-done | bytes 4718608 | tf_op jit(solution)/shard_map/all_gather | solution.py:171
  500.2 10.2 convert_reduce_fusion
  510.4 8.9 multiply_reduce_fusion.2
  524.5 4.1 fusion.72
  529.7 217.2 %while.31 = (s32[]{:T(128)}, bf16[12,1,750,64]{2,3,1,0:T(8,128)(2,1)}, f32[12,1,1500,64]{2,3,1,0:T(8,128)}, f32[12,1,1500,64]{2,3,1,0:T(8,128)}, s32[12]{0:T(128...) while((s32[]{:T(128)}, ...), condition=%wide.region_12.13_spmd, body=%wide.region_10.12_spmd.sunk | while | flops 729143232 | bytes 50715952 | solution.py:121
  530.9 4.1 fusion.160
  537.1 3.9 multiply_reduce_fusion.10
  549.0 4.1 fusion.160
  555.2 3.9 multiply_reduce_fusion.10
  567.1 4.1 fusion.160
  573.2 3.9 multiply_reduce_fusion.10
  585.2 4.1 fusion.160
  591.3 3.9 multiply_reduce_fusion.10
  603.3 4.1 fusion.160
  609.4 3.9 multiply_reduce_fusion.10
  621.4 4.1 fusion.160
  627.5 3.9 multiply_reduce_fusion.10
  639.5 4.1 fusion.160
  645.6 3.9 multiply_reduce_fusion.10
  657.6 4.1 fusion.160
  663.7 3.9 multiply_reduce_fusion.10
  675.7 4.1 fusion.160
  681.8 3.9 multiply_reduce_fusion.10
  693.7 4.1 fusion.160
  699.9 3.9 multiply_reduce_fusion.10
  711.8 4.1 fusion.160
  718.0 3.9 multiply_reduce_fusion.10
  729.9 4.1 fusion.160
  736.1 3.9 multiply_reduce_fusion.10
  746.8 7.6 concatenate.27
  754.4 7.4 concatenate.26
  761.8 19.7 pad_maximum_fusion
  781.5 23.4 copy.51
  805.0 1659.9 %all-reduce.6 = bf16[2,1,750,1536]{3,1,2,0:T(2,128)(2,1)} all-reduce(f32[2,1,750,1536]{3,1,2,0:T(1,128)} %copy.51), channel_id=3, replica_groups=mesh['clip'=16,'frame'=2] {'frame'}, use_global_device_ids=true, to_apply=%region_13.14.clone | all-reduce | flops 2304000 | bytes 13824000
  2464.9 9.9 constant_dynamic-slice_fusion.1
  2474.8 4.3 copy.62
  2480.8 8.3 fusion.46
  2489.2 8.9 fusion.114
  2501.5 8.9 fusion.65
  2511.1 42.0 %all-reduce.4 = (f32[3072]{0:T(1024)S(1)}, f32[768,8]{0,1:T(8,128)}) all-reduce(f32[3072]{0:T(1024)} %get-tuple-element.304, f32[768,8]{0,1:T(8,128)S(1)} %stack.89), channel_id=8, replica_groups=mesh['clip'=16,'frame'=2] {'clip','frame'}, use_global_device_ids=true, to_apply=%region_21.22.clone | all-reduce | flops 9216 | bytes 73728
  2558.5 3.6 fusion.76
  2562.1 8.6 fusion.73
  2573.1 34.8 %reduce-scatter.6.cloned.1.call-done = f32[24,2304]{1,0:T(8,128)} async-done(((f32[768,2304]{1,0:T(8,128)}), f32[24,2304]{1,0:T(8,128)}) %reduce-scatter.6.cloned.1.call-update) | async-done | bytes 221200 | tf_op jit(solution)/shard_map/reduce_scatter | solution.py:272
  2610.6 139.6 %reduce-scatter.10.cloned.1.call-done = f32[24,3072]{1,0:T(8,128)} async-done(((f32[768,3072]{1,0:T(8,128)}), f32[24,3072]{1,0:T(8,128)}) %reduce-scatter.10.cloned.1.call-update) | async-done | bytes 294928 | tf_op jit(solution)/shard_map/reduce_scatter | solution.py:274
  (379 shorter events, 207.0 us)
Async XLA Ops:
  7.2 75.4 %copy-start.2 = (bf16[1,750,768]{2,1,0:T(8,128)(2,1)S(1)}, bf16[1,750,768]{2,1,0:T(8,128)(2,1)}, u32[]{:S(2)}) copy-start(bf16[1,750,768]{2,1,0:T(8,128)(2,1)} %param.18) | copy-start | bytes 3456004
  7.2 76.0 %all-gather.9.cloned.1.call-start = ((), (), s32[]{:S(2)}) async-start(), calls=%async_computation.4 | async-start | bytes 3649536 | tf_op jit(solution)/shard_map/all_gather | solution.py:168
  9.0 141.6 %all-gather.17.cloned.1.call-start = ((), (), s32[]{:S(2)}) async-start(), calls=%async_computation.12 | async-start | bytes 6930432 | tf_op jit(solution)/shard_map/all_gather | solution.py:189
  81.1 7.6 copy-start.24
  81.1 7.6 copy-start.31
  82.6 6.1 copy-start.21
  83.2 5.6 copy-start.26
  92.0 2.4 copy-start.36
  92.1 183.1 %all-gather.11.cloned.1.call-start = ((), (), s32[]{:S(2)}) async-start(), calls=%async_computation.5 | async-start | bytes 1216512 | tf_op jit(solution)/shard_map/all_gather | solution.py:169
  93.6 186.3 %all-gather.13.cloned.1.call-start = ((), (), s32[]{:S(2)}) async-start(), calls=%async_computation.6 | async-start | bytes 4866048 | tf_op jit(solution)/shard_map/all_gather | solution.py:170
  94.3 339.2 %reduce-scatter.12.cloned.1.call-start = ((), (), s32[]{:S(2)}) async-start(), calls=%async_computation.11 | async-start | bytes 9732096 | tf_op jit(solution)/shard_map/reduce_scatter | solution.py:275
  169.1 2.2 copy-start
  178.9 2.2 copy-start
  198.8 2.2 copy-start
  208.8 2.2 copy-start
  268.2 2.2 copy-start
  279.8 11.9 copy-start.13
  298.1 138.3 %copy-start.37 = (u32[32]{0:T(128)S(1)}, u32[32]{0:T(128)}, u32[]{:S(2)}) copy-start(u32[32]{0:T(128)} %constant.226) | copy-start | bytes 388
  298.1 202.1 %all-gather.15.cloned.1.call-start = ((), (), s32[]{:S(2)}) async-start(), calls=%async_computation.7 | async-start | bytes 4866048 | tf_op jit(solution)/shard_map/all_gather | solution.py:171
  436.0 2134.8 %reduce-scatter.8.cloned.1.call-start = ((), (), s32[]{:S(2)}) async-start(), calls=%async_computation.9 | async-start | bytes 2433024 | tf_op jit(solution)/shard_map/reduce_scatter | solution.py:273
  510.4 8.9 copy-start.6
  510.4 8.9 copy-start.14
  519.3 2.6 copy-start.10
  537.0 4.0 slice-start
  537.1 4.0 slice-start.1
  555.1 4.0 slice-start
  555.1 4.0 slice-start.1
  573.2 4.0 slice-start
  573.2 3.9 slice-start.1
  591.3 4.0 slice-start
  591.3 3.9 slice-start.1
  609.4 4.0 slice-start
  609.4 4.0 slice-start.1
  627.5 4.0 slice-start
  627.5 4.0 slice-start.1
  645.6 4.0 slice-start
  645.6 4.0 slice-start.1
  663.7 4.0 slice-start
  663.7 4.0 slice-start.1
  681.8 4.0 slice-start
  681.8 4.0 slice-start.1
  699.8 4.0 slice-start
  699.8 4.0 slice-start.1
  718.0 4.0 slice-start
  718.0 4.0 slice-start.1
  736.1 4.0 slice-start
  736.1 4.0 slice-start.1
  805.0 1803.0 %reduce-scatter.6.cloned.1.call-start = ((), (), s32[]{:S(2)}) async-start(), calls=%async_computation.8 | async-start | bytes 7299072 | tf_op jit(solution)/shard_map/reduce_scatter | solution.py:272
  2474.8 4.3 copy-start.1
  2489.2 261.0 %reduce-scatter.10.cloned.1.call-start = ((), (), s32[]{:S(2)}) async-start(), calls=%async_computation.10 | async-start | bytes 9732096 | tf_op jit(solution)/shard_map/reduce_scatter | solution.py:274
  2501.5 8.9 copy-start.5
  2501.5 8.9 copy-start.7
  2510.4 45.4 %copy-start.23 = (f32[2,24,8]{1,2,0:T(8,128)S(1)}, f32[2,24,8]{1,2,0:T(8,128)}, u32[]{:S(2)}) copy-start(f32[2,24,8]{1,2,0:T(8,128)} %param.31) | copy-start | bytes 4612
  2510.4 46.2 %copy-start.28 = (f32[24,8]{0,1:T(8,128)S(1)}, f32[24,8]{0,1:T(8,128)}, u32[]{:S(2)}) copy-start(f32[24,8]{0,1:T(8,128)} %param.25) | copy-start | bytes 2308
  2510.4 48.1 %copy-start.3 = (bf16[1,750,768]{2,1,0:T(8,128)(2,1)S(1)}, bf16[1,750,768]{2,1,0:T(8,128)(2,1)}, u32[]{:S(2)}) copy-start(bf16[1,750,768]{2,1,0:T(8,128)(2,1)} %param.18) | copy-start | bytes 3456004
  2553.9 8.2 copy-start.35
  2556.5 5.5 copy-start.29
  2558.5 3.6 copy-start.30
  2562.1 8.7 copy-start.19
  2562.1 8.7 copy-start.20
  2562.1 45.9 %copy-start.15 = (f32[24,2304]{1,0:T(8,128)S(1)}, f32[24,2304]{1,0:T(8,128)}, u32[]{:S(2)}) copy-start(f32[24,2304]{1,0:T(8,128)} %param.20) | copy-start | bytes 663556
  2562.1 45.8 %copy-start.17 = (f32[2,24,2304]{2,1,0:T(8,128)S(1)}, f32[2,24,2304]{2,1,0:T(8,128)}, u32[]{:S(2)}) copy-start(f32[2,24,2304]{2,1,0:T(8,128)} %param.26) | copy-start | bytes 1327108
  2570.8 179.4 %copy-start.12 = (f32[24,3072]{1,0:T(8,128)S(1)}, f32[24,3072]{1,0:T(8,128)}, u32[]{:S(2)}) copy-start(f32[24,3072]{1,0:T(8,128)} %param.22) | copy-start | bytes 884740
  2570.8 179.4 %copy-start.16 = (f32[2,24,3072]{2,1,0:T(8,128)S(1)}, f32[2,24,3072]{2,1,0:T(8,128)}, u32[]{:S(2)}) copy-start(f32[2,24,3072]{2,1,0:T(8,128)} %param.28) | copy-start | bytes 1769476
  (19 other events, 31.8 us)
Sparse Core Ops, SparseCore 0:
  11.5 62.9 all-gather.8
  92.2 58.3 all-gather.16
  154.1 54.0 all-gather.10
  211.5 62.6 all-gather.12
  298.2 135.2 reduce-scatter.11
  437.3 62.8 all-gather.14
  805.1 103.6 reduce-scatter.7
  2489.3 118.6 reduce-scatter.5
  2615.4 134.7 reduce-scatter.9
where the time goes:
time: 2770 us; the launch traced here: 2760 us
  blocking collectives  1810 us (65%)
  waiting for transfers between devices  390 us (14%)
  matrix products  324 us (12%)
  local copies, waits for them, and re-layouts  115 us (4%)
  other arithmetic  64.8 us (2%)
  loops' own time  40.6 us (1%)
    unnamed x3, blocking collectives  1740 us
    reduce_scatter x1, waiting for transfers between devices, body(): lax.psum_scatter(grad_expand_term, ('clip', 'frame'), scatter_dimension=0...  140 us
    reduce_scatter x1, waiting for transfers between devices, body(): lax.psum_scatter(grad_shrink_term, ('clip', 'frame'), scatter_dimension=0...  135 us
    all_gather x1, blocking collectives, body(): lax.all_gather(low_vectors, ('clip', 'frame'), axis=0, tiled=True)  70.5 us
    all_gather x1, waiting for transfers between devices, body(): lax.all_gather(low_shrink, ('clip', 'frame'), axis=0, tiled=True)  63.2 us
  transfers between devices with their start and end apart: 9, of which 5 were waited for; matrix products, arithmetic and copies ran while one was open for 6% of the time, Pallas kernels for 0%

commit v1 on v0

--- a/solution.py
+++ b/solution.py
@@ -159,34 +159,54 @@
     clip_count, frame_count, model_width = inputs.shape
     row_count = clip_count * frame_count
     head_count = HEADS
-    low_in = project_in.astype(jnp.bfloat16)
-    low_out = project_out.astype(jnp.bfloat16)
-    low_expand = expand_weight.astype(jnp.bfloat16)
-    low_shrink = shrink_weight.astype(jnp.bfloat16)
-    low_vectors = vectors.astype(jnp.bfloat16)
-    full_in, full_out, full_expand, full_shrink, full_bias, full_vectors = (
-        lax.all_gather(low_in, ("clip", "frame"), axis=0, tiled=True),
-        lax.all_gather(low_out, ("clip", "frame"), axis=0, tiled=True),
-        lax.all_gather(low_expand, ("clip", "frame"), axis=0, tiled=True),
-        lax.all_gather(low_shrink, ("clip", "frame"), axis=0, tiled=True),
-        lax.all_gather(expand_bias.astype(jnp.bfloat16), ("clip", "frame"), axis=0, tiled=True),
-        lax.all_gather(low_vectors, ("clip", "frame"), axis=0, tiled=True),
-    )
-    column_set = full_vectors.astype(jnp.float32)
+    shard_rows = project_in.shape[0]
+    wide_in = project_in.shape[1]
+    ff_width = expand_weight.shape[1]
+    swap = [(0, 1), (1, 0)]
+    everyone = ("clip", "frame")
+
+    small = jnp.concatenate(
+        [
+            vectors,
+            expand_bias.reshape(shard_rows, -1),
+            jnp.zeros((shard_rows, 128 - vectors.shape[1] - expand_bias.shape[0] // shard_rows), jnp.float32),
+        ],
+        axis=1,
+    )
+    first_pack = jnp.concatenate([project_in, small], axis=1).astype(jnp.bfloat16)
+    second_pack = jnp.concatenate(
+        [project_out, expand_weight, shrink_weight.reshape(shard_rows, -1)], axis=1
+    ).astype(jnp.bfloat16)
+    first_full = lax.all_gather(first_pack, everyone, axis=0, tiled=True)
+    second_full = lax.all_gather(second_pack, everyone, axis=0, tiled=True)
+    full_in = first_full[:, :wide_in]
+    small_full = first_full[:, wide_in:].astype(jnp.float32)
+    column_set = small_full[:, : vectors.shape[1]]
+    full_bias = small_full[:, vectors.shape[1] : vectors.shape[1] + ff_width // model_width].reshape(-1)
+    full_out = second_full[:, :model_width]
+    full_expand = second_full[:, model_width : model_width + ff_width]
+    full_shrink = second_full[:, model_width + ff_width :].reshape(ff_width, model_width)
+
     frames_rows = inputs.reshape(row_count, model_width).astype(jnp.float32)
     normed_first, plain_first, inv_first = norm_parts(
         frames_rows, column_set[:, 0], column_set[:, 1]
     )
     hidden_first = normed_first.astype(jnp.bfloat16)
+    hidden_partner = lax.ppermute(hidden_first, "frame", swap)
     bias_in = jnp.concatenate(
         [column_set[:, 2], jnp.zeros((model_width,), jnp.float32), column_set[:, 3]]
     )
     projected = (
         jnp.dot(hidden_first, full_in, preferred_element_type=jnp.float32) + bias_in
     ).astype(jnp.bfloat16)
+    partner_pairs = (
+        jnp.dot(hidden_partner, full_in[:, model_width:], preferred_element_type=jnp.float32)
+        + bias_in[model_width:]
+    ).astype(jnp.bfloat16)
     queries = projected[:, :model_width].reshape(clip_count, frame_count, model_width)
-    local_pairs = projected[:, model_width:].reshape(clip_count, frame_count, 2 * model_width)
-    clip_pairs = lax.all_gather(local_pairs, "frame", axis=1, tiled=True)
+    clip_pairs = jnp.concatenate([projected[:, model_width:], partner_pairs], axis=0).reshape(
+        clip_count, 2 * frame_count, 2 * model_width
+    )
     mixed, log_totals = attend_forward(queries, clip_pairs, head_count)
     mixed_low = mixed.reshape(row_count, model_width).astype(jnp.bfloat16)
     attended = jnp.dot(mixed_low, full_out, preferred_element_type=jnp.float32) + column_set[:, 4]
@@ -195,9 +215,7 @@
         residual, column_set[:, 5], column_set[:, 6]
     )
     hidden_second = normed_second.astype(jnp.bfloat16)
-    preact = jnp.dot(
-        hidden_second, full_expand, preferred_element_type=jnp.float32
-    ) + full_bias.astype(jnp.float32)
+    preact = jnp.dot(hidden_second, full_expand, preferred_element_type=jnp.float32) + full_bias
     activated = gelu_exact(preact).astype(jnp.bfloat16)
     result = (
         residual
@@ -205,42 +223,40 @@
         + column_set[:, 7]
     )
     output = result.astype(jnp.bfloat16).reshape(inputs.shape)
-    back_in, back_out, back_expand, back_shrink, back_vectors = (
-        lax.all_gather(low_in, ("clip", "frame"), axis=0, tiled=True),
-        lax.all_gather(low_out, ("clip", "frame"), axis=0, tiled=True),
-        lax.all_gather(low_expand, ("clip", "frame"), axis=0, tiled=True),
-        lax.all_gather(low_shrink, ("clip", "frame"), axis=0, tiled=True),
-        lax.all_gather(low_vectors, ("clip", "frame"), axis=0, tiled=True),
-    )
-    back_columns = back_vectors.astype(jnp.float32)
+
     grad_result = cotangent.reshape(row_count, model_width)
     grad_shrink_term = jnp.dot(activated.T, grad_result, preferred_element_type=jnp.float32)
     grad_down_bias = jnp.sum(grad_result.astype(jnp.float32), axis=0)
-    grad_activated = jnp.dot(grad_result, back_shrink.T, preferred_element_type=jnp.float32)
+    grad_activated = jnp.dot(grad_result, full_shrink.T, preferred_element_type=jnp.float32)
     grad_preact = (grad_activated * gelu_slope(preact)).astype(jnp.bfloat16)
     grad_expand_term = jnp.dot(hidden_second.T, grad_preact, preferred_element_type=jnp.float32)
     grad_bias_term = jnp.sum(grad_preact.astype(jnp.float32), axis=0)
-    grad_hidden_second = jnp.dot(grad_preact, back_expand.T, preferred_element_type=jnp.float32)
+    grad_hidden_second = jnp.dot(grad_preact, full_expand.T, preferred_element_type=jnp.float32)
     norm_term_second, gain_second, shift_second = norm_backward(
-        grad_hidden_second, plain_second, inv_second, back_columns[:, 5]
+        grad_hidden_second, plain_second, inv_second, column_set[:, 5]
     )
     grad_residual = grad_result.astype(jnp.float32) + norm_term_second
     grad_attended = grad_residual.astype(jnp.bfloat16)
     grad_out_term = jnp.dot(mixed_low.T, grad_attended, preferred_element_type=jnp.float32)
     grad_out_bias = jnp.sum(grad_attended.astype(jnp.float32), axis=0)
-    grad_mixed = jnp.dot(grad_attended, back_out.T, preferred_element_type=jnp.float32).astype(
+    owned_late = lax.psum_scatter(
+        jnp.concatenate(
+            [grad_shrink_term.reshape(model_width, -1), grad_expand_term, grad_out_term], axis=1
+        ),
+        everyone,
+        scatter_dimension=0,
+        tiled=True,
+    )
+    grad_mixed = jnp.dot(grad_attended, full_out.T, preferred_element_type=jnp.float32).astype(
         jnp.bfloat16
     )
     grad_mixed = grad_mixed.reshape(clip_count, frame_count, model_width)
-    pairs_back = lax.all_gather(local_pairs, "frame", axis=1, tiled=True)
     grad_query, delta_rows, grad_pairs_terms = attend_backward(
-        queries, pairs_back, grad_mixed, log_totals, head_count
-    )
-    block_count = grad_pairs_terms.shape[1] // frame_count
-    blocked_terms = grad_pairs_terms.reshape(clip_count, block_count, frame_count, 2 * model_width)
-    blocked_terms = jnp.swapaxes(blocked_terms, 0, 1)
-    owned_pairs = lax.psum_scatter(blocked_terms, "frame", scatter_dimension=0, tiled=True)
-    grad_pairs = owned_pairs.reshape(clip_count, frame_count, 2 * model_width)
+        queries, clip_pairs, grad_mixed, log_totals, head_count
+    )
+    partner_terms = grad_pairs_terms[:, frame_count:].astype(jnp.bfloat16)
+    returned_terms = lax.ppermute(partner_terms, "frame", swap)
+    grad_pairs = grad_pairs_terms[:, :frame_count] + returned_terms.astype(jnp.float32)
     grad_projected = (
         jnp.concatenate([grad_query, grad_pairs], axis=2)
         .reshape(row_count, 3 * model_width)
@@ -250,9 +266,9 @@
     projected_sums = jnp.sum(grad_projected.astype(jnp.float32), axis=0)
     grad_query_bias = projected_sums[:model_width]
     grad_value_bias = projected_sums[2 * model_width :]
-    grad_hidden_first = jnp.dot(grad_projected, back_in.T, preferred_element_type=jnp.float32)
+    grad_hidden_first = jnp.dot(grad_projected, full_in.T, preferred_element_type=jnp.float32)
     norm_term_first, gain_first, shift_first = norm_backward(
-        grad_hidden_first, plain_first, inv_first, back_columns[:, 0]
+        grad_hidden_first, plain_first, inv_first, column_set[:, 0]
     )
     grad_inputs = (grad_residual + norm_term_first).astype(jnp.bfloat16).reshape(inputs.shape)
     grad_columns = jnp.stack(
@@ -268,14 +284,23 @@
         ],
         axis=1,
     )
-    owned_in, owned_out, owned_expand, owned_shrink, owned_bias, owned_vectors = (
-        lax.psum_scatter(grad_in_term, ("clip", "frame"), scatter_dimension=0, tiled=True),
-        lax.psum_scatter(grad_out_term, ("clip", "frame"), scatter_dimension=0, tiled=True),
-        lax.psum_scatter(grad_expand_term, ("clip", "frame"), scatter_dimension=0, tiled=True),
-        lax.psum_scatter(grad_shrink_term, ("clip", "frame"), scatter_dimension=0, tiled=True),
-        lax.psum_scatter(grad_bias_term, ("clip", "frame"), scatter_dimension=0, tiled=True),
-        lax.psum_scatter(grad_columns, ("clip", "frame"), scatter_dimension=0, tiled=True),
-    )
+    small_grads = jnp.concatenate(
+        [
+            grad_columns,
+            grad_bias_term.reshape(model_width, -1),
+            jnp.zeros((model_width, 128 - grad_columns.shape[1] - ff_width // model_width), jnp.float32),
+        ],
+        axis=1,
+    )
+    owned_in = lax.psum_scatter(grad_in_term, everyone, scatter_dimension=0, tiled=True)
+    owned_small = lax.psum_scatter(small_grads, everyone, scatter_dimension=0, tiled=True)
+    owned_vectors = owned_small[:, : vectors.shape[1]]
+    owned_bias = owned_small[
+        :, vectors.shape[1] : vectors.shape[1] + ff_width // model_width
+    ].reshape(-1)
+    owned_shrink = owned_late[:, :ff_width].reshape(shrink_weight.shape)
+    owned_expand = owned_late[:, ff_width : 2 * ff_width]
+    owned_out = owned_late[:, 2 * ff_width :]
     new_in, mom_in = adam_step(project_in, moments_in, owned_in)
     new_out, mom_out = adam_step(project_out, moments_out, owned_out)
     new_expand, mom_expand = adam_step(expand_weight, moments_expand, owned_expand)

time: 2770 us -> 1090 us (0.39)
  blocking collectives: 1810 us -> 0 us
  waiting for transfers between devices: 390 us -> 539 us
    unnamed x3 -> x0, blocking collectives: 1740 us -> none
    all_gather x1 -> x0, blocking collectives: 70.5 us -> none  [body(): lax.all_gather(low_vectors, ('clip', 'frame'), axis=0, tiled=True)]
    unnamed x9 -> x6, waiting for transfers between devices: 0.15 us -> 67.4 us
    ppermute x0 -> x2, waiting for transfers between devices: none -> 67.2 us  [the longest x1 48.4 us: body(): returned_terms = lax.ppermute(partner_terms, 'frame', swap)]
    concatenate x4 -> x3, local copies, waits for them, and re-layouts: 40 us -> 3.76 us  [the longest x1 3.02 us: body(): jnp.concatenate([grad_columns, grad_bias_term.reshape(model_width, -1), j...]
    reduce_scatter x4 -> x2, waiting for transfers between devices: 310 us -> 344 us  [the longest x1 223 us: body(): lax.psum_scatter(jnp.concatenate([grad_shrink_term.reshape(model_width, -...]
    all_gather x5 -> x2, waiting for transfers between devices: 80.1 us -> 60.6 us  [the longest x1 60.6 us: body(): first_full = lax.all_gather(first_pack, everyone, axis=0, tiled=True)]
  transfers between devices with their start and end apart: 9 -> 7, of which waited for: 5 -> 6; matrix products, arithmetic and copies ran while one was open for 6% -> 16% of each run, Pallas kernels for 0% -> 0%
where the time goes in v1:
time: 1090 us
  waiting for transfers between devices  539 us (49%)
  matrix products  337 us (31%)
  local copies, waits for them, and re-layouts  92 us (8%)
  other arithmetic  60.1 us (6%)
  loops' own time  40.4 us (4%)
  between operations  14.8 us (1%)
    reduce_scatter x1, waiting for transfers between devices, body(): lax.psum_scatter(jnp.concatenate([grad_shrink_term.reshape(model_width, -...  223 us
    reduce_scatter x1, waiting for transfers between devices, body(): lax.psum_scatter(grad_in_term, everyone, scatter_dimension=0, tiled=True)  121 us
    unnamed x6, waiting for transfers between devices  67.4 us
    all_gather x1, waiting for transfers between devices, body(): first_full = lax.all_gather(first_pack, everyone, axis=0, tiled=True)  60.6 us
    dot_general x12, matrix products, one_head(): jnp.einsum('cqk,ckd->cqd', weights_soft, value_block, preferred_element_t...  51.5 us
    dot_general x12, matrix products, one_head_back(): jnp.einsum('cqd,ckd->cqk', grad_block, value_block, preferred_element_typ...  48.4 us
    ppermute x1, waiting for transfers between devices, body(): returned_terms = lax.ppermute(partner_terms, 'frame', swap)  48.4 us
    dot_general x12, matrix products, one_head_back(): jnp.einsum('cqd,ckd->cqk', query_block, key_block, preferred_element_type...  48.3 us
  transfers between devices with their start and end apart: 7, of which 6 were waited for; matrix products, arithmetic and copies ran while one was open for 16% of the time, Pallas kernels for 0%

profile of v1, /device:TPU:0, one launch (start us, length us, event | category | flops | bytes accessed | tf_op | source)
XLA Modules:
  0.0 1087.3 jit_solution(1372982773338665000)
XLA Ops:
  14.4 60.6 %all-gather.3.cloned.1.call-done = bf16[768,2432]{1,0:T(8,128)(2,1)} async-done(((bf16[24,2432]{1,0:T(8,128)(2,1)}), bf16[768,2432]{1,0:T(8,128)(2,1)}) %all-gather.3.cloned.1.call-update) | async-done | bytes 3735568 | tf_op jit(solution)/shard_map/all_gather | solution.py:180
  80.9 5.1 add_convert_fusion
  89.3 18.9 %collective-permute-done = bf16[750,768]{1,0:T(8,128)(2,1)} collective-permute-done((bf16[750,768]{1,0:T(8,128)(2,1)S(1)}, bf16[750,768]{1,0:T(8,128)(2,1)}, u32[]{:S(2)}, u32[]{:S(2)}) %collective-permute-start) | collective-permute-done | bytes 1152032 | tf_op jit(solution)/shard_map/ppermute | solution.py:195
  108.2 4.0 add_convert_fusion.1
  116.0 126.8 %while.30 = (s32[]{:T(128)}, bf16[12,1,750,64]{2,3,1,0:T(8,128)(2,1)}, f32[12,1,750]{2,1,0:T(1,128)S(1)}, s32[12]{0:T(128)S(1)}, bf16[1,750,768]{2,1,0:T(8,128)(...) while((s32[]{:T(128)}, ...), condition=%wide.region_5.6_spmd, body=%wide.region_2.5_spmd.sunk | while | flops 298124256 | bytes 32810912 | solution.py:77
  122.3 4.2 fusion.159
  132.8 4.4 fusion.159
  143.5 4.3 fusion.159
  154.1 4.5 fusion.159
  164.9 4.4 fusion.159
  175.6 4.2 fusion.159
  186.0 4.2 fusion.159
  196.5 4.2 fusion.159
  207.1 4.2 fusion.159
  217.6 4.2 fusion.159
  228.1 4.2 fusion.159
  238.6 4.2 fusion.159
  247.1 4.9 slice.182
  252.0 8.5 reshape.414
  260.5 10.2 multiply_convert_fusion.1
  270.7 8.8 convert_reduce_fusion
  279.6 4.8 multiply_reduce_fusion.2
  288.8 228.1 %while.31 = (s32[]{:T(128)}, bf16[12,1,750,64]{2,3,1,0:T(8,128)(2,1)}, f32[12,1,1500,64]{2,3,1,0:T(8,128)}, f32[12,1,1500,64]{2,3,1,0:T(8,128)}, s32[12]{0:T(128...) while((s32[]{:T(128)}, ...), condition=%wide.region_12.13_spmd, body=%wide.region_10.12_spmd.sunk | while | flops 729143232 | bytes 50654712 | solution.py:121
  290.0 4.0 fusion.168
  296.1 4.0 multiply_reduce_fusion.10
  309.0 4.0 fusion.168
  315.1 4.0 multiply_reduce_fusion.10
  328.0 4.0 fusion.168
  334.1 4.0 multiply_reduce_fusion.10
  347.1 4.0 fusion.168
  353.1 4.0 multiply_reduce_fusion.10
  366.1 4.0 fusion.168
  372.1 4.0 multiply_reduce_fusion.10
  385.1 4.0 fusion.168
  391.1 4.0 multiply_reduce_fusion.10
  404.1 4.0 fusion.168
  410.1 4.0 multiply_reduce_fusion.10
  423.1 4.0 fusion.168
  429.1 4.0 multiply_reduce_fusion.10
  442.1 4.0 fusion.168
  448.1 4.0 multiply_reduce_fusion.10
  461.1 4.0 fusion.168
  467.1 4.0 multiply_reduce_fusion.10
  480.1 4.0 fusion.168
  486.2 4.0 multiply_reduce_fusion.10
  499.1 4.0 fusion.168
  505.2 4.0 multiply_reduce_fusion.10
  516.9 5.0 fusion.49
  521.9 4.3 copy.53
  530.5 48.4 %collective-permute-done.1 = bf16[1,750,1536]{2,1,0:T(8,128)(2,1)} collective-permute-done((bf16[1,750,1536]{2,1,0:T(8,128)(2,1)}, bf16[1,750,1536]{2,1,0:T(8,128)(2,1)}, u32[]{:S(2)}, u32[]{:S(2)}) %collective-permute-start.1) | collective-permute-done | bytes 2304032 | tf_op jit(solution)/shard_map/ppermute | solution.py:258
  578.8 4.4 copy.54
  583.3 3.8 fusion.48
  588.0 4.8 fusion.77
  593.7 3.0 concatenate.51
  596.8 8.2 fusion.54
  605.0 10.1 fusion.88
  615.2 11.7 %reshape.422 = f32[768,3072]{1,0:T(8,128)} reshape(f32[3072,768]{1,0:T(8,128)} %fusion.88) | data formatting | bytes 18874368 | tf_op jit(solution)/shard_map/reshape | solution.py:244
  626.8 3.3 fusion.124
  630.1 6.6 fusion.127
  636.8 7.4 pad_maximum_fusion
  644.8 8.6 fusion.84
  655.4 67.3 %all-reduce.4.cloned.1.call-done = f32[768,128]{0,1:T(8,128)} async-done(((f32[768,128]{0,1:T(8,128)}), f32[768,128]{0,1:T(8,128)}) %all-reduce.4.cloned.1.call-update) | async-done | bytes 393232
  726.9 121.0 %reduce-scatter.4.cloned.1.call-done = f32[24,2304]{1,0:T(8,128)} async-done(((f32[768,2304]{1,0:T(8,128)}), f32[24,2304]{1,0:T(8,128)}) %reduce-scatter.4.cloned.1.call-update) | async-done | bytes 221200 | tf_op jit(solution)/shard_map/reduce_scatter | solution.py:295
  850.5 222.7 %reduce-scatter.6.cloned.1.call-done = f32[24,6912]{1,0:T(8,128)} async-done(((f32[768,6912]{1,0:T(8,128)}), f32[24,6912]{1,0:T(8,128)}) %reduce-scatter.6.cloned.1.call-update) | async-done | bytes 663568 | tf_op jit(solution)/shard_map/reduce_scatter | solution.py:242
  (402 shorter events, 217.7 us)
Async XLA Ops:
  7.2 6.4 copy-start.1
  7.2 67.7 %all-gather.3.cloned.1.call-start = ((), (), s32[]{:S(2)}) async-start(), calls=%async_computation.2 | async-start | bytes 3852288 | tf_op jit(solution)/shard_map/all_gather | solution.py:180
  10.6 232.3 %all-gather.5.cloned.1.call-start = ((), (), s32[]{:S(2)}) async-start(), calls=%async_computation.3 | async-start | bytes 10948608 | tf_op jit(solution)/shard_map/all_gather | solution.py:181
  13.9 63.7 %copy-start.23 = (f32[750]{0:T(1024)}, f32[750]{0:T(1024)S(1)}, u32[]{:S(2)}) copy-start(f32[750]{0:T(1024)S(1)} %broadcast_multiply_fusion.5) | copy-start | bytes 9004
  14.4 63.7 %copy-start.27 = (f32[750]{0:T(1024)}, f32[750]{0:T(1024)S(1)}, u32[]{:S(2)}) copy-start(f32[750]{0:T(1024)S(1)} %add_rsqrt_fusion.1) | copy-start | bytes 9004
  77.5 8.4 copy-start.25
  78.0 30.2 %collective-permute-start = (bf16[750,768]{1,0:T(8,128)(2,1)S(1)}, bf16[750,768]{1,0:T(8,128)(2,1)}, u32[]{:S(2)}, u32[]{:S(2)}) collective-permute-start(bf16[750,768]{1,0:T(8,128)(2,1)S(1)} %fusion.71), channel_id=1, source_target_pairs={{0,1},{1,0},{2,3},{3,2},{4,5},{5,4},{6,7},{7,6},{8,9},{9,8},{10,11... | collective-permute-start | bytes 3456008 | tf_op jit(solution)/shard_map/ppermute | solution.py:195
  80.4 642.3 %all-reduce.4.cloned.1.call-start = ((), (), s32[]{:S(2)}) async-start(), calls=%async_computation.6 | async-start | bytes 786432
  89.3 22.9 %slice-start.5 = ((bf16[750,2304]{1,0:T(8,128)(2,1)}), bf16[750,1536]{1,0:T(8,128)(2,1)S(1)}, s32[]{:S(2)}) async-start(bf16[750,2304]{1,0:T(8,128)(2,1)} %copy-done.6), calls=%async_computation.12 | async-start | bytes 4620288 | tf_op jit(solution)/shard_map/slice | solution.py:207
  260.5 10.2 copy-start.7
  260.5 10.2 copy-start.17
  260.5 19.0 %slice-start.6 = ((s8[10616832]{0:T(1024)(128)(4,1)}), s8[4194304]{0:T(1024)(128)(4,1)S(1)}, s32[]{:S(2)}) async-start(s8[10616832]{0:T(1024)(128)(4,1)} %bitcast.288), calls=%async_computation.13 | async-start | bytes 8388608
  260.5 19.0 %slice-start.7 = ((s8[10616832]{0:T(1024)(128)(4,1)}), s8[4194304]{0:T(1024)(128)(4,1)S(1)}, s32[]{:S(2)}) async-start(s8[10616832]{0:T(1024)(128)(4,1)} %bitcast.288), calls=%async_computation.14 | async-start | bytes 8388608
  270.7 8.8 slice-start.8
  279.5 4.8 copy-start.9
  296.1 4.0 slice-start
  296.1 4.0 slice-start.1
  315.0 4.0 slice-start
  315.1 4.0 slice-start.1
  334.0 4.1 slice-start
  334.1 4.1 slice-start.1
  353.1 4.0 slice-start
  353.1 4.0 slice-start.1
  372.1 4.1 slice-start
  372.1 4.1 slice-start.1
  391.1 4.0 slice-start
  391.1 4.0 slice-start.1
  410.1 4.1 slice-start
  410.1 4.1 slice-start.1
  429.1 4.1 slice-start
  429.1 4.1 slice-start.1
  448.1 4.0 slice-start
  448.1 4.0 slice-start.1
  467.1 4.0 slice-start
  486.1 4.1 slice-start
  486.2 4.0 slice-start.1
  505.1 4.0 slice-start
  505.1 4.0 slice-start.1
  521.9 6.3 copy-start.36
  526.3 52.6 %collective-permute-start.1 = (bf16[1,750,1536]{2,1,0:T(8,128)(2,1)}, bf16[1,750,1536]{2,1,0:T(8,128)(2,1)}, u32[]{:S(2)}, u32[]{:S(2)}) collective-permute-start(bf16[1,750,1536]{2,1,0:T(8,128)(2,1)} %copy.53), channel_id=1, source_target_pairs={{0,1},{1,0},{2,3},{3,2},{4,5},{5,4},{6,7},{7,6},{8,9},{9,8},{10,11... | collective-permute-start | bytes 6912008 | tf_op jit(solution)/shard_map/ppermute | solution.py:258
  583.3 4.5 copy-start.34
  587.0 5.8 copy-start.3
  588.0 8.7 copy-start.31
  596.7 251.2 %reduce-scatter.4.cloned.1.call-start = ((), (), s32[]{:S(2)}) async-start(), calls=%async_computation.4 | async-start | bytes 7299072 | tf_op jit(solution)/shard_map/reduce_scatter | solution.py:295
  605.0 468.2 %reduce-scatter.6.cloned.1.call-start = ((), (), s32[]{:S(2)}) async-start(), calls=%async_computation.5 | async-start | bytes 21897216 | tf_op jit(solution)/shard_map/reduce_scatter | solution.py:242
  626.8 9.9 slice-start.2
  626.8 9.9 slice-start.3
  630.1 6.6 slice-start.4
  644.8 8.6 copy-start.5
  644.8 8.6 copy-start.11
  653.5 70.3 %copy-start.37 = (f32[2,96]{1,0:T(2,128)S(1)}, f32[2,96]{1,0:T(2,128)}, u32[]{:S(2)}) copy-start(f32[2,96]{1,0:T(2,128)} %param.30) | copy-start | bytes 2308
  653.5 70.9 %copy-start.29 = (f32[2,24,8]{1,2,0:T(8,128)S(1)}, f32[2,24,8]{1,2,0:T(8,128)}, u32[]{:S(2)}) copy-start(f32[2,24,8]{1,2,0:T(8,128)} %param.31) | copy-start | bytes 4612
  653.5 71.6 %copy-start.32 = (f32[24,8]{0,1:T(8,128)S(1)}, f32[24,8]{0,1:T(8,128)}, u32[]{:S(2)}) copy-start(f32[24,8]{0,1:T(8,128)} %param.25) | copy-start | bytes 2308
  653.5 72.8 %copy-start.39 = (f32[96]{0:T(128)S(1)}, f32[96]{0:T(128)}, u32[]{:S(2)}) copy-start(f32[96]{0:T(128)} %param.24) | copy-start | bytes 1156
  653.5 194.4 %copy-start.18 = (f32[24,2304]{1,0:T(8,128)S(1)}, f32[24,2304]{1,0:T(8,128)}, u32[]{:S(2)}) copy-start(f32[24,2304]{1,0:T(8,128)} %param.20) | copy-start | bytes 663556
  653.5 194.4 %copy-start.19 = (f32[2,24,2304]{2,1,0:T(8,128)S(1)}, f32[2,24,2304]{2,1,0:T(8,128)}, u32[]{:S(2)}) copy-start(f32[2,24,2304]{2,1,0:T(8,128)} %param.26) | copy-start | bytes 1327108
  655.4 417.8 %copy-start.12 = (f32[2,24,3072]{2,1,0:T(8,128)S(1)}, f32[2,24,3072]{2,1,0:T(8,128)}, u32[]{:S(2)}) copy-start(f32[2,24,3072]{2,1,0:T(8,128)} %param.28) | copy-start | bytes 1769476
  723.6 350.8 %copy-start.38 = (f32[96]{0:T(128)}, f32[96]{0:T(128)S(1)}, u32[]{:S(2)}) copy-start(f32[96]{0:T(128)S(1)} %reshape.425) | copy-start | bytes 1156
  725.1 349.3 %copy-start.33 = (f32[24,8]{0,1:T(8,128)}, f32[24,8]{0,1:T(8,128)S(1)}, u32[]{:S(2)}) copy-start(f32[24,8]{0,1:T(8,128)S(1)} %get-tuple-element.265) | copy-start | bytes 2308
  726.9 347.7 %copy-start.20 = (f32[2,24,768]{2,1,0:T(8,128)S(1)}, f32[2,24,768]{2,1,0:T(8,128)}, u32[]{:S(2)}) copy-start(f32[2,24,768]{2,1,0:T(8,128)} %param.27) | copy-start | bytes 442372
  849.7 225.8 %copy-start.21 = (f32[24,768]{1,0:T(8,128)S(1)}, f32[24,768]{1,0:T(8,128)}, u32[]{:S(2)}) copy-start(f32[24,768]{1,0:T(8,128)} %param.21) | copy-start | bytes 221188
  849.7 226.5 %copy-start.14 = (f32[24,3072]{1,0:T(8,128)S(1)}, f32[24,3072]{1,0:T(8,128)}, u32[]{:S(2)}) copy-start(f32[24,3072]{1,0:T(8,128)} %param.22) | copy-start | bytes 884740
  850.5 226.6 %copy-start.10 = (f32[2,96,768]{2,1,0:T(8,128)S(1)}, f32[2,96,768]{2,1,0:T(8,128)}, u32[]{:S(2)}) copy-start(f32[2,96,768]{2,1,0:T(8,128)} %param.29) | copy-start | bytes 1769476
  850.5 226.6 %copy-start.15 = (f32[96,768]{1,0:T(8,128)S(1)}, f32[96,768]{1,0:T(8,128)}, u32[]{:S(2)}) copy-start(f32[96,768]{1,0:T(8,128)} %param.23) | copy-start | bytes 884740
  (25 other events, 55.5 us)
Sparse Core Ops, SparseCore 0:
  11.5 63.4 all-gather.2
  80.5 87.9 all-gather.4
  596.8 125.7 all-reduce.3
  729.7 118.1 reduce-scatter.3
  854.2 218.9 reduce-scatter.5

commit v2 on v1

--- a/solution.py
+++ b/solution.py
@@ -288,16 +288,17 @@
         [
             grad_columns,
             grad_bias_term.reshape(model_width, -1),
-            jnp.zeros((model_width, 128 - grad_columns.shape[1] - ff_width // model_width), jnp.float32),
+            jnp.zeros((model_width, 256 - 12), jnp.float32),
         ],
         axis=1,
     )
-    owned_in = lax.psum_scatter(grad_in_term, everyone, scatter_dimension=0, tiled=True)
-    owned_small = lax.psum_scatter(small_grads, everyone, scatter_dimension=0, tiled=True)
-    owned_vectors = owned_small[:, : vectors.shape[1]]
-    owned_bias = owned_small[
-        :, vectors.shape[1] : vectors.shape[1] + ff_width // model_width
-    ].reshape(-1)
+    first_terms, owned_late = lax.optimization_barrier(
+        (jnp.concatenate([grad_in_term, small_grads], axis=1), owned_late)
+    )
+    owned_first = lax.psum_scatter(first_terms, everyone, scatter_dimension=0, tiled=True)
+    owned_in = owned_first[:, :wide_in]
+    owned_vectors = owned_first[:, wide_in : wide_in + vectors.shape[1]]
+    owned_bias = owned_first[:, wide_in + vectors.shape[1] : wide_in + 12].reshape(-1)
     owned_shrink = owned_late[:, :ff_width].reshape(shrink_weight.shape)
     owned_expand = owned_late[:, ff_width : 2 * ff_width]
     owned_out = owned_late[:, 2 * ff_width :]

time: 1090 us -> 803 us (0.74)
  waiting for transfers between devices: 539 us -> 228 us
  local copies, waits for them, and re-layouts: 92 us -> 109 us
    reduce_scatter x1, waiting for transfers between devices: 223 us -> 0.02 us  [body(): lax.psum_scatter(jnp.concatenate([grad_shrink_term.reshape(model_width, -...]
    unnamed x6 -> x4, waiting for transfers between devices: 67.4 us -> 0.07 us
    reduce_scatter x1, waiting for transfers between devices: 121 us -> 103 us  [body(): lax.psum_scatter(first_terms, everyone, scatter_dimension=0, tiled=True)]
  transfers between devices with their start and end apart: 7 -> 6, of which waited for: 6 -> 4; matrix products, arithmetic and copies ran while one was open for 16% -> 48% of each run, Pallas kernels for 0% -> 0%
where the time goes in v2:
time: 803 us; the launch traced here: 796 us
  matrix products  334 us (42%)
  waiting for transfers between devices  228 us (28%)
  local copies, waits for them, and re-layouts  109 us (14%)
  other arithmetic  66.2 us (8%)
  loops' own time  40.4 us (5%)
  between operations  14.7 us (2%)
    reduce_scatter x1, waiting for transfers between devices, body(): lax.psum_scatter(first_terms, everyone, scatter_dimension=0, tiled=True)  103 us
    all_gather x1, waiting for transfers between devices, body(): first_full = lax.all_gather(first_pack, everyone, axis=0, tiled=True)  60.6 us
    dot_general x12, matrix products, one_head(): jnp.einsum('cqk,ckd->cqd', weights_soft, value_block, preferred_element_t...  51.6 us
    dot_general x12, matrix products, one_head_back(): jnp.einsum('cqd,ckd->cqk', query_block, key_block, preferred_element_type...  50 us
    dot_general x12, matrix products, one_head_back(): jnp.einsum('cqd,ckd->cqk', grad_block, value_block, preferred_element_typ...  49.6 us
    ppermute x1, waiting for transfers between devices, body(): returned_terms = lax.ppermute(partner_terms, 'frame', swap)  45.8 us
    another operation x1, loops' own time, attend_backward(): pieces = lax.map(one_head_back, jnp.arange(head_count))  32.1 us
    dot_general x12, matrix products, one_head_back(): jnp.einsum('cqk,ckd->cqd', grad_scores, key_block, preferred_element_type...  30.7 us
  transfers between devices with their start and end apart: 6, of which 4 were waited for; matrix products, arithmetic and copies ran while one was open for 48% of the time, Pallas kernels for 0%

profile of v2, /device:TPU:0, one launch (start us, length us, event | category | flops | bytes accessed | tf_op | source)
XLA Modules:
  0.0 796.2 jit_solution(1115466514428548295)
XLA Ops:
  14.4 60.6 %all-gather.3.cloned.1.call-done = bf16[768,2432]{1,0:T(8,128)(2,1)} async-done(((bf16[24,2432]{1,0:T(8,128)(2,1)}), bf16[768,2432]{1,0:T(8,128)(2,1)}) %all-gather.3.cloned.1.call-update) | async-done | bytes 3735568 | tf_op jit(solution)/shard_map/all_gather | solution.py:180
  80.9 5.1 add_convert_fusion
  89.3 18.9 %collective-permute-done = bf16[750,768]{1,0:T(8,128)(2,1)} collective-permute-done((bf16[750,768]{1,0:T(8,128)(2,1)S(1)}, bf16[750,768]{1,0:T(8,128)(2,1)}, u32[]{:S(2)}, u32[]{:S(2)}) %collective-permute-start) | collective-permute-done | bytes 1152032 | tf_op jit(solution)/shard_map/ppermute | solution.py:195
  108.2 4.0 add_convert_fusion.1
  112.2 2.8 maximum_bitcast_fusion
  116.1 126.1 %while.30 = (s32[]{:T(128)}, bf16[12,1,750,64]{2,3,1,0:T(8,128)(2,1)}, f32[12,1,750]{2,1,0:T(1,128)S(1)}, s32[12]{0:T(128)S(1)}, bf16[1,750,768]{2,1,0:T(8,128)(...) while((s32[]{:T(128)}, ...), condition=%wide.region_5.6_spmd, body=%wide.region_2.5_spmd.sunk | while | flops 298124256 | bytes 32810912 | solution.py:77
  122.3 4.2 fusion.160
  132.8 4.5 fusion.160
  143.5 4.3 fusion.160
  154.0 4.5 fusion.160
  164.7 4.4 fusion.160
  175.3 4.2 fusion.160
  185.8 4.2 fusion.160
  196.2 4.2 fusion.160
  206.7 4.2 fusion.160
  217.1 4.2 fusion.160
  227.6 4.2 fusion.160
  238.0 4.2 fusion.160
  243.3 2.9 fusion.130
  246.6 4.8 slice.186
  251.4 8.7 %reshape.414 = bf16[3072,768]{1,0:T(8,128)(2,1)} reshape(bf16[768,3072]{1,0:T(8,128)(2,1)} %slice.186) | data formatting | bytes 9437184 | tf_op jit(solution)/shard_map/reshape | solution.py:188
  260.1 7.1 multiply_convert_fusion.1
  267.2 7.6 convert_reduce_fusion
  274.9 7.0 fusion.127
  281.8 6.7 multiply_reduce_fusion.2
  292.3 6.9 fusion.88
  299.2 11.4 %reshape.423 = f32[768,3072]{1,0:T(8,128)} reshape(f32[3072,768]{1,0:T(8,128)} %fusion.88) | data formatting | bytes 18874368 | tf_op jit(solution)/shard_map/reshape | solution.py:244
  310.6 15.0 %pad_maximum_fusion = f32[768,6912]{1,0:T(8,128)} fusion(f32[768,768]{1,0:T(8,128)} %fusion.124, f32[768,3072]{1,0:T(8,128)} %fusion.127, f32[768,3072]{1,0:T(8,128)} %reshape.423), kind=kLoop, calls=%fused_computation.52 | loop fusion | flops 10616832 | bytes 42467328 | tf_op jit(solution)/shard_map/concatenate | solution.py:243
  325.7 4.1 fusion.83
  330.9 231.7 %while.31 = (s32[]{:T(128)}, bf16[12,1,750,64]{2,3,1,0:T(8,128)(2,1)}, f32[12,1,1500,64]{2,3,1,0:T(8,128)}, f32[12,1,1500,64]{2,3,1,0:T(8,128)}, s32[12]{0:T(128...) while((s32[]{:T(128)}, ...), condition=%wide.region_12.13_spmd, body=%wide.region_10.12_spmd.sunk | while | flops 729143232 | bytes 50654712 | solution.py:121
  332.2 4.2 fusion.169
  338.3 4.5 multiply_reduce_fusion.10
  352.1 4.2 fusion.169
  358.3 4.5 multiply_reduce_fusion.10
  372.1 4.2 fusion.169
  378.3 4.0 multiply_reduce_fusion.10
  391.3 4.1 fusion.169
  397.4 4.1 multiply_reduce_fusion.10
  410.4 4.1 fusion.169
  416.5 4.3 multiply_reduce_fusion.10
  429.8 4.1 fusion.169
  435.9 4.1 multiply_reduce_fusion.10
  448.9 4.1 fusion.169
  455.1 4.2 multiply_reduce_fusion.10
  468.2 4.1 fusion.169
  474.3 4.0 multiply_reduce_fusion.10
  487.3 4.1 fusion.169
  493.4 4.1 multiply_reduce_fusion.10
  506.5 4.1 fusion.169
  512.6 4.1 multiply_reduce_fusion.10
  525.7 4.1 fusion.169
  531.8 4.1 multiply_reduce_fusion.10
  544.8 4.1 fusion.169
  550.9 4.0 multiply_reduce_fusion.10
  562.6 5.0 fusion.49
  567.6 4.4 copy.80
  578.9 45.8 %collective-permute-done.1 = bf16[1,750,1536]{2,1,0:T(8,128)(2,1)} collective-permute-done((bf16[1,750,1536]{2,1,0:T(8,128)(2,1)}, bf16[1,750,1536]{2,1,0:T(8,128)(2,1)}, u32[]{:S(2)}, u32[]{:S(2)}) %collective-permute-start.1) | collective-permute-done | bytes 2304032 | tf_op jit(solution)/shard_map/ppermute | solution.py:258
  624.7 4.4 copy.81
  629.1 3.8 fusion.48
  633.7 4.8 fusion.77
  642.7 6.3 fusion.54
  650.0 10.7 %concatenate.50 = f32[768,2560]{1,0:T(8,128)} concatenate(f32[768,2304]{1,0:T(8,128)} %fusion.54, f32[768,1]{1,0:T(8,128)} %stack.92, f32[768,1]{1,0:T(8,128)} %stack.93, f32[768,1]{1,0:T(8,128)} %stack.94, f32[768,1]{1,0:T(8,128)} %stack.95, f32[768,1]{1,0:T(8,128)} %stack.96, f32[768,1]{1,0:T(8,128)} %stack.97, f32[768,1]{1,0:T(8,128)} %stack.98, f32[768,1]{1,0:T(8,128)} %stack.99, ...), dimensions={1} | concatenate | bytes 15728640 | tf_op jit(solution)/shard_map/concatenate | solution.py:296
  661.6 8.8 %fusion.84 = bf16[1,750,768]{2,1,0:T(8,128)(2,1)} fusion(f32[750,768]{1,0:T(8,128)S(1)} %get-tuple-element.381, bf16[750,3072]{1,0:T(8,128)(2,1)} %copy-done.39, bf16[3072,768]{1,0:T(8,128)(2,1)} %reshape.414, f32[768]{0:T(1024)S(1)} %copy-done.35), kind=kOutput, calls=%fused_computation.124 | convolution fusion | flops 3540672000 | bytes 12785664 | tf_op jit(solution)/shard_map/dot_general | solution.py:222
  679.2 102.7 %reduce-scatter.5.cloned.1.call-done = f32[24,2560]{1,0:T(8,128)} async-done(((f32[768,2560]{1,0:T(8,128)}), f32[24,2560]{1,0:T(8,128)}) %reduce-scatter.5.cloned.1.call-update) | async-done | bytes 245776 | tf_op jit(solution)/shard_map/reduce_scatter | solution.py:298
  (391 shorter events, 220.0 us)
Async XLA Ops:
  7.2 6.4 copy-start.1
  7.2 67.7 %all-gather.3.cloned.1.call-start = ((), (), s32[]{:S(2)}) async-start(), calls=%async_computation.2 | async-start | bytes 3852288 | tf_op jit(solution)/shard_map/all_gather | solution.py:180
  10.6 231.7 %all-gather.5.cloned.1.call-start = ((), (), s32[]{:S(2)}) async-start(), calls=%async_computation.3 | async-start | bytes 10948608 | tf_op jit(solution)/shard_map/all_gather | solution.py:181
  13.9 63.7 %copy-start.24 = (f32[750]{0:T(1024)}, f32[750]{0:T(1024)S(1)}, u32[]{:S(2)}) copy-start(f32[750]{0:T(1024)S(1)} %broadcast_multiply_fusion.5) | copy-start | bytes 9004
  14.4 63.7 %copy-start.28 = (f32[750]{0:T(1024)}, f32[750]{0:T(1024)S(1)}, u32[]{:S(2)}) copy-start(f32[750]{0:T(1024)S(1)} %add_rsqrt_fusion.1) | copy-start | bytes 9004
  77.5 3.1 copy-start.30
  77.5 8.4 %copy-start.26 = (f32[768]{0:T(1024)}, f32[768]{0:T(1024)S(1)}, u32[]{:S(2)}) copy-start(f32[768]{0:T(1024)S(1)} %get-tuple-element.317) | copy-start | bytes 9220
  78.0 30.2 %collective-permute-start = (bf16[750,768]{1,0:T(8,128)(2,1)S(1)}, bf16[750,768]{1,0:T(8,128)(2,1)}, u32[]{:S(2)}, u32[]{:S(2)}) collective-permute-start(bf16[750,768]{1,0:T(8,128)(2,1)S(1)} %fusion.71), channel_id=1, source_target_pairs={{0,1},{1,0},{2,3},{3,2},{4,5},{5,4},{6,7},{7,6},{8,9},{9,8},{10,11... | collective-permute-start | bytes 3456008 | tf_op jit(solution)/shard_map/ppermute | solution.py:195
  80.3 580.4 %reduce-scatter.3.cloned.1.call-start = ((), (), s32[]{:S(2)}) async-start(), calls=%async_computation.4 | async-start | bytes 21897216 | tf_op jit(solution)/shard_map/reduce_scatter | solution.py:242
  89.3 22.9 %slice-start.2 = ((bf16[750,2304]{1,0:T(8,128)(2,1)}), bf16[750,1536]{1,0:T(8,128)(2,1)S(1)}, s32[]{:S(2)}) async-start(bf16[750,2304]{1,0:T(8,128)(2,1)} %copy-done.5), calls=%async_computation.8 | async-start | bytes 4620288 | tf_op jit(solution)/shard_map/slice | solution.py:207
  119.3 2.1 copy-start
  140.4 2.1 copy-start
  151.0 2.1 copy-start
  224.5 2.1 copy-start
  260.1 7.1 copy-start.6
  260.1 7.1 copy-start.16
  267.2 25.1 %copy-start.39 = (bf16[750,3072]{1,0:T(8,128)(2,1)}, bf16[750,3072]{1,0:T(8,128)(2,1)S(1)}, u32[]{:S(2)}) copy-start(bf16[750,3072]{1,0:T(8,128)(2,1)S(1)} %get-tuple-element.386) | copy-start | bytes 13824004
  289.7 2.6 copy-start.3
  325.7 456.2 %reduce-scatter.5.cloned.1.call-start = ((), (), s32[]{:S(2)}) async-start(), calls=%async_computation.5 | async-start | bytes 8110080 | tf_op jit(solution)/shard_map/reduce_scatter | solution.py:298
  338.3 4.7 slice-start
  338.3 4.8 slice-start.1
  358.3 4.7 slice-start
  358.3 4.8 slice-start.1
  378.3 4.1 slice-start
  378.3 4.0 slice-start.1
  397.4 4.1 slice-start
  397.4 4.1 slice-start.1
  416.5 4.3 slice-start
  416.5 4.4 slice-start.1
  435.9 4.1 slice-start
  435.9 4.1 slice-start.1
  455.0 4.2 slice-start
  455.1 4.3 slice-start.1
  474.3 4.1 slice-start
  474.3 4.0 slice-start.1
  493.4 4.1 slice-start
  493.4 4.1 slice-start.1
  512.6 4.1 slice-start
  512.6 4.1 slice-start.1
  531.8 4.1 slice-start
  531.8 4.1 slice-start.1
  550.9 4.0 slice-start
  550.9 4.0 slice-start.1
  572.0 52.7 %collective-permute-start.1 = (bf16[1,750,1536]{2,1,0:T(8,128)(2,1)}, bf16[1,750,1536]{2,1,0:T(8,128)(2,1)}, u32[]{:S(2)}, u32[]{:S(2)}) collective-permute-start(bf16[1,750,1536]{2,1,0:T(8,128)(2,1)} %copy.80), channel_id=1, source_target_pairs={{0,1},{1,0},{2,3},{3,2},{4,5},{5,4},{6,7},{7,6},{8,9},{9,8},{10,11... | collective-permute-start | bytes 6912008 | tf_op jit(solution)/shard_map/ppermute | solution.py:258
  629.1 3.8 copy-start.7
  629.1 3.8 copy-start.25
  629.1 3.8 copy-start.27
  629.1 3.8 copy-start.29
  629.1 4.5 copy-start.33
  639.4 3.4 copy-start.31
  661.6 8.8 %copy-start.4 = (f32[750,768]{1,0:T(8,128)S(1)}, f32[750,768]{1,0:T(8,128)}, u32[]{:S(2)}) copy-start(f32[750,768]{1,0:T(8,128)} %copy-done.3) | copy-start | bytes 6912004
  661.6 8.8 %copy-start.9 = (f32[750,768]{1,0:T(8,128)S(1)}, f32[750,768]{1,0:T(8,128)}, u32[]{:S(2)}) copy-start(f32[750,768]{1,0:T(8,128)} %get-tuple-element.383) | copy-start | bytes 6912004
  672.3 3.2 copy-start.8
  672.4 5.0 copy-start.11
  672.4 4.1 copy-start.14
  672.5 4.9 copy-start.15
  674.1 3.3 copy-start.23
  674.1 3.3 copy-start.12
  676.5 107.8 %copy-start.17 = (f32[2,24,2304]{2,1,0:T(8,128)S(1)}, f32[2,24,2304]{2,1,0:T(8,128)}, u32[]{:S(2)}) copy-start(f32[2,24,2304]{2,1,0:T(8,128)} %param.26) | copy-start | bytes 1327108
  677.4 107.9 %copy-start.19 = (f32[24,2304]{1,0:T(8,128)S(1)}, f32[24,2304]{1,0:T(8,128)}, u32[]{:S(2)}) copy-start(f32[24,2304]{1,0:T(8,128)} %param.20) | copy-start | bytes 663556
  677.4 109.4 %copy-start.36 = (f32[2,96]{1,0:T(2,128)S(1)}, f32[2,96]{1,0:T(2,128)}, u32[]{:S(2)}) copy-start(f32[2,96]{1,0:T(2,128)} %param.30) | copy-start | bytes 2308
  677.4 109.4 %copy-start.38 = (f32[96]{0:T(128)S(1)}, f32[96]{0:T(128)}, u32[]{:S(2)}) copy-start(f32[96]{0:T(128)} %param.24) | copy-start | bytes 1156
  782.8 6.7 copy-start.37
  785.3 4.2 copy-start.18
  (18 other events, 29.6 us)
Sparse Core Ops, SparseCore 0:
  11.5 63.4 all-gather.2
  80.5 87.9 all-gather.4
  325.8 219.9 reduce-scatter.2
  660.9 120.9 reduce-scatter.4

commit v3 on v2

--- a/solution.py
+++ b/solution.py
@@ -3,6 +3,8 @@
 import jax
 import jax.numpy as jnp
 from jax import lax
+from jax.experimental import pallas as pl
+from jax.experimental.pallas import tpu as pltpu
 from jax.sharding import PartitionSpec as P
 
 HEADS = 12
@@ -49,6 +51,134 @@
         0.5 * (1.0 + jax.scipy.special.erf(inputs * root_half))
         + inputs * jnp.exp(-0.5 * inputs * inputs) * inv_root_two_pi
     )
+
+
+QUERY_CHUNK = 256
+MASKED = -1e30
+
+
+def attention_forward_kernel(q_ref, k_ref, v_ref, kbias_ref, o_ref, l_ref):
+    head_size = q_ref.shape[1] // 2
+    rows = q_ref.shape[0]
+    kbias = kbias_ref[...]
+    lane = lax.broadcasted_iota(jnp.int32, (QUERY_CHUNK, 2 * head_size), 1)
+    for chunk in range(rows // QUERY_CHUNK):
+        span = pl.ds(chunk * QUERY_CHUNK, QUERY_CHUNK)
+        mixed_parts = []
+        totals = []
+        for half in range(2):
+            cols = pl.ds(half * head_size, head_size)
+            query = q_ref[span, cols]
+            key = k_ref[:, cols]
+            value = v_ref[:, cols]
+            scores = (
+                lax.dot_general(
+                    query, key, (((1,), (1,)), ((), ())), preferred_element_type=jnp.float32
+                )
+                + kbias
+            )
+            highest = jnp.max(scores, axis=1, keepdims=True)
+            exponent = jnp.exp(scores - highest)
+            denominator = jnp.sum(exponent, axis=1, keepdims=True)
+            weights = (exponent * (1.0 / denominator)).astype(jnp.bfloat16)
+            mixed_parts.append(jnp.dot(weights, value, preferred_element_type=jnp.float32))
+            totals.append(highest + jnp.log(denominator))
+        o_ref[span, :] = jnp.concatenate(mixed_parts, axis=1).astype(o_ref.dtype)
+        l_ref[span, :] = jnp.where(lane < head_size, totals[0], totals[1])
+
+
+def attention_backward_kernel(
+    q_ref, k_ref, v_ref, do_ref, l_ref, kbias_ref, dq_ref, dk_ref, dv_ref
+):
+    head_size = q_ref.shape[1] // 2
+    rows = q_ref.shape[0]
+    kbias = kbias_ref[...]
+    for half in range(2):
+        cols = pl.ds(half * head_size, head_size)
+        key = k_ref[:, cols]
+        value = v_ref[:, cols]
+        grad_key = None
+        grad_value = None
+        for chunk in range(rows // QUERY_CHUNK):
+            span = pl.ds(chunk * QUERY_CHUNK, QUERY_CHUNK)
+            query = q_ref[span, cols]
+            grad_out = do_ref[span, cols]
+            total = l_ref[span, pl.ds(half * head_size, 1)]
+            scores = (
+                lax.dot_general(
+                    query, key, (((1,), (1,)), ((), ())), preferred_element_type=jnp.float32
+                )
+                + kbias
+            )
+            weights = jnp.exp(scores - total)
+            grad_weights = lax.dot_general(
+                grad_out, value, (((1,), (1,)), ((), ())), preferred_element_type=jnp.float32
+            )
+            delta = jnp.sum(weights * grad_weights, axis=1, keepdims=True)
+            grad_scores = (weights * (grad_weights - delta)).astype(jnp.bfloat16)
+            dq_ref[span, cols] = jnp.dot(
+                grad_scores, key, preferred_element_type=jnp.float32
+            ).astype(dq_ref.dtype)
+            key_part = lax.dot_general(
+                grad_scores, query, (((0,), (0,)), ((), ())), preferred_element_type=jnp.float32
+            )
+            value_part = lax.dot_general(
+                weights.astype(jnp.bfloat16),
+                grad_out,
+                (((0,), (0,)), ((), ())),
+                preferred_element_type=jnp.float32,
+            )
+            grad_key = key_part if grad_key is None else grad_key + key_part
+            grad_value = value_part if grad_value is None else grad_value + value_part
+        dk_ref[:, cols] = grad_key
+        dv_ref[:, cols] = grad_value
+
+
+def pad_rows(values, rows):
+    return jnp.pad(values, ((0, rows - values.shape[0]), (0, 0)))
+
+
+def attention_pallas(queries, pairs, grad_out=None, totals=None):
+    query_rows, model_width = queries.shape
+    key_rows = pairs.shape[0]
+    padded_q = -(-query_rows // QUERY_CHUNK) * QUERY_CHUNK
+    padded_k = -(-key_rows // 128) * 128
+    pair_count = model_width // 128
+    q_pad = pad_rows(queries, padded_q)
+    kv_pad = pad_rows(pairs, padded_k)
+    kbias = jnp.where(jnp.arange(padded_k) < key_rows, 0.0, MASKED).astype(jnp.float32)[None, :]
+    q_spec = pl.BlockSpec((padded_q, 128), lambda j: (0, j))
+    k_spec = pl.BlockSpec((padded_k, 128), lambda j: (0, j))
+    v_spec = pl.BlockSpec((padded_k, 128), lambda j: (0, j + pair_count))
+    b_spec = pl.BlockSpec((1, padded_k), lambda j: (0, 0))
+    params = pltpu.CompilerParams(vmem_limit_bytes=48 * 1024 * 1024)
+    if grad_out is None:
+        mixed, log_totals = pl.pallas_call(
+            attention_forward_kernel,
+            grid=(pair_count,),
+            in_specs=[q_spec, k_spec, v_spec, b_spec],
+            out_specs=[q_spec, q_spec],
+            out_shape=[
+                jax.ShapeDtypeStruct((padded_q, model_width), jnp.bfloat16),
+                jax.ShapeDtypeStruct((padded_q, model_width), jnp.float32),
+            ],
+            compiler_params=params,
+        )(q_pad, kv_pad, kv_pad, kbias)
+        return mixed[:query_rows], log_totals
+    do_pad = pad_rows(grad_out, padded_q)
+    dq, dk, dv = pl.pallas_call(
+        attention_backward_kernel,
+        grid=(pair_count,),
+        in_specs=[q_spec, k_spec, v_spec, q_spec, q_spec, b_spec],
+        out_specs=[q_spec, k_spec, k_spec],
+        out_shape=[
+            jax.ShapeDtypeStruct((padded_q, model_width), jnp.float32),
+            jax.ShapeDtypeStruct((padded_k, model_width), jnp.float32),
+            jax.ShapeDtypeStruct((padded_k, model_width), jnp.float32),
+        ],
+        compiler_params=params,
+    )(q_pad, kv_pad, kv_pad, do_pad, totals, kbias)
+    return dq[:query_rows], dk[:key_rows], dv[:key_rows]
 
 
 def attend_forward(queries, keys_values, head_count):
@@ -207,8 +337,10 @@
     clip_pairs = jnp.concatenate([projected[:, model_width:], partner_pairs], axis=0).reshape(
         clip_count, 2 * frame_count, 2 * model_width
     )
-    mixed, log_totals = attend_forward(queries, clip_pairs, head_count)
-    mixed_low = mixed.reshape(row_count, model_width).astype(jnp.bfloat16)
+    score_scale = 1.0 / math.sqrt(model_width // head_count)
+    scaled_queries = (projected[:, :model_width] * score_scale).astype(jnp.bfloat16)
+    pair_rows = clip_pairs.reshape(2 * row_count, 2 * model_width)
+    mixed_low, log_totals = attention_pallas(scaled_queries, pair_rows)
     attended = jnp.dot(mixed_low, full_out, preferred_element_type=jnp.float32) + column_set[:, 4]
     residual = frames_rows + attended
     normed_second, plain_second, inv_second = norm_parts(
@@ -250,17 +382,15 @@
     grad_mixed = jnp.dot(grad_attended, full_out.T, preferred_element_type=jnp.float32).astype(
         jnp.bfloat16
     )
-    grad_mixed = grad_mixed.reshape(clip_count, frame_count, model_width)
-    grad_query, delta_rows, grad_pairs_terms = attend_backward(
-        queries, clip_pairs, grad_mixed, log_totals, head_count
-    )
-    partner_terms = grad_pairs_terms[:, frame_count:].astype(jnp.bfloat16)
+    grad_query, grad_keys, grad_values = attention_pallas(
+        scaled_queries, pair_rows, grad_mixed, log_totals
+    )
+    grad_pairs_terms = jnp.concatenate([grad_keys, grad_values], axis=1)
+    partner_terms = grad_pairs_terms[row_count:].astype(jnp.bfloat16)
     returned_terms = lax.ppermute(partner_terms, "frame", swap)
-    grad_pairs = grad_pairs_terms[:, :frame_count] + returned_terms.astype(jnp.float32)
-    grad_projected = (
-        jnp.concatenate([grad_query, grad_pairs], axis=2)
-        .reshape(row_count, 3 * model_width)
-        .astype(jnp.bfloat16)
+    grad_pairs = grad_pairs_terms[:row_count] + returned_terms.astype(jnp.float32)
+    grad_projected = jnp.concatenate(
+        [(grad_query * score_scale).astype(jnp.bfloat16), grad_pairs.astype(jnp.bfloat16)], axis=1
     )
     grad_in_term = jnp.dot(hidden_first.T, grad_projected, preferred_element_type=jnp.float32)
     projected_sums = jnp.sum(grad_projected.astype(jnp.float32), axis=0)

time: 803 us -> 628 us (0.78)
  matrix products: 334 us -> 72.6 us
  waiting for transfers between devices: 228 us -> 332 us
  Pallas kernels: 0 us -> 87 us
  local copies, waits for them, and re-layouts: 109 us -> 63.5 us
  loops' own time: 40.4 us -> 0 us
  other arithmetic: 66.2 us -> 48.5 us
    dot_general x84 -> x0, matrix products: 261 us -> none  [the longest x12 51.6 us: one_head(): jnp.einsum('cqk,ckd->cqd', weights_soft, value_block, preferred_element_t...]
    pallas_call x0 -> x2, Pallas kernels: none -> 87 us  [the longest x1 52.7 us: attention_pallas(): pl.pallas_call(attention_backward_kernel, grid=(pair_count,), in_specs=[q...]
    reduce_scatter x1, waiting for transfers between devices: 0.02 us -> 58.5 us  [body(): lax.psum_scatter(jnp.concatenate([grad_shrink_term.reshape(model_width, -...]
    another operation x2 -> x0, loops' own time: 40.4 us -> none  [the longest x1 32.1 us: attend_backward(): pieces = lax.map(one_head_back, jnp.arange(head_count))]
    while x72 -> x0, local copies, waits for them, and re-layouts: 25.9 us -> none
    ppermute x1, waiting for transfers between devices: 45.8 us -> 68.7 us  [body(): returned_terms = lax.ppermute(partner_terms, 'frame', swap)]
    dynamic_slice x36 -> x0, local copies, waits for them, and re-layouts: 14.3 us -> none  [the longest x24 14 us: attend_forward(): mixed, log_totals = lax.map(one_head, jnp.arange(head_count))]
    all_gather x1, waiting for transfers between devices: 0.02 us -> 12.1 us  [body(): second_full = lax.all_gather(second_pack, everyone, axis=0, tiled=True)]
  transfers between devices with their start and end apart: 6 -> 6, of which waited for: 4 -> 6; matrix products, arithmetic and copies ran while one was open for 48% -> 13% of each run, Pallas kernels for 0% -> 14%
where the time goes in v3:
time: 628 us; the launch traced here: 622 us
  waiting for transfers between devices  332 us (53%)
  Pallas kernels  87 us (14%)
  matrix products  72.6 us (12%)
  local copies, waits for them, and re-layouts  63.5 us (10%)
  other arithmetic  48.5 us (8%)
  between operations  14.9 us (2%)
    reduce_scatter x1, waiting for transfers between devices, body(): lax.psum_scatter(first_terms, everyone, scatter_dimension=0, tiled=True)  110 us
    ppermute x1, waiting for transfers between devices, body(): returned_terms = lax.ppermute(partner_terms, 'frame', swap)  68.7 us
    all_gather x1, waiting for transfers between devices, body(): first_full = lax.all_gather(first_pack, everyone, axis=0, tiled=True)  59.7 us
    reduce_scatter x1, waiting for transfers between devices, body(): lax.psum_scatter(jnp.concatenate([grad_shrink_term.reshape(model_width, -...  58.5 us
    pallas_call x1, Pallas kernels, attention_pallas(): pl.pallas_call(attention_backward_kernel, grid=(pair_count,), in_specs=[q...  52.7 us
    pallas_call x1, Pallas kernels, attention_pallas(): pl.pallas_call(attention_forward_kernel, grid=(pair_count,), in_specs=[q_...  34.3 us
    ppermute x1, waiting for transfers between devices, body(): hidden_partner = lax.ppermute(hidden_first, 'frame', swap)  22.5 us
    concatenate x1, other arithmetic, body(): jnp.concatenate([grad_shrink_term.reshape(model_width, -1), grad_expand_t...  14.2 us
  transfers between devices with their start and end apart: 6, of which 6 were waited for; matrix products, arithmetic and copies ran while one was open for 13% of the time, Pallas kernels for 14%

profile of v3, /device:TPU:0, one launch (start us, length us, event | category | flops | bytes accessed | tf_op | source)
XLA Modules:
  0.0 621.5 jit_solution(10585543618045189755)
XLA Ops:
  7.2 1.0 convert.25
  10.7 1.0 convert.30
  11.7 1.0 convert.29
  12.7 0.9 convert.28
  15.2 59.7 %all-gather.3.cloned.1.call-done = bf16[768,2432]{1,0:T(8,128)(2,1)} async-done(((bf16[24,2432]{1,0:T(8,128)(2,1)}), bf16[768,2432]{1,0:T(8,128)(2,1)}) %all-gather.3.cloned.1.call-update) | async-done | bytes 3735568 | tf_op jit(solution)/shard_map/all_gather | solution.py:310
  74.9 1.0 slice_convert_fusion
  75.9 2.0 slice_reduce_fusion
  77.9 1.5 fusion.30
  79.4 1.5 collective-permute-start
  80.9 0.9 slice.201
  81.8 4.2 add_convert_fusion
  86.1 1.6 copy-done.12
  87.8 1.2 add.234
  89.0 22.5 %collective-permute-done = bf16[750,768]{1,0:T(8,128)(2,1)} collective-permute-done((bf16[750,768]{1,0:T(8,128)(2,1)}, bf16[750,768]{1,0:T(8,128)(2,1)}, u32[]{:S(2)}, u32[]{:S(2)}) %collective-permute-start) | collective-permute-done | bytes 1152032 | tf_op jit(solution)/shard_map/ppermute | solution.py:325
  111.5 4.0 add_convert_fusion.1
  115.5 3.1 fusion.8.k_ref.v_ref
  118.6 34.3 %shard_map.293 = (bf16[768,768]{1,0:T(8,128)(2,1)S(1)}, f32[768,768]{1,0:T(8,128)S(1)}) custom-call(bf16[768,768]{1,0:T(8,128)(2,1)S(1)} %pad.14.q_ref, bf16[1536,1536]{1,0:T(8,128)(2,1)} %fusion.8.k_ref.v_ref, bf16[1536,1536]{1,0:T(8,128)(2,1)} %fusion.8.k_ref.v_ref, f32[1,1536]{1,0:T(1,128)S(1)} %compare_select_fusion.kbias_ref), custom_call_target="tpu_custom_call" | custom-call | tf_op jit(solution)/shard_map/pallas_call | solution.py:156
  153.0 1.4 copy-done
  154.3 12.1 %all-gather.5.cloned.1.call-done = bf16[768,6912]{1,0:T(8,128)(2,1)} async-done(((bf16[24,6912]{1,0:T(8,128)(2,1)}), bf16[768,6912]{1,0:T(8,128)(2,1)}) %all-gather.5.cloned.1.call-update) | async-done | bytes 10616848 | tf_op jit(solution)/shard_map/all_gather | solution.py:311
  166.5 2.5 fusion.81
  169.0 1.4 copy-done.6
  170.8 4.8 slice.202
  175.6 8.5 %reshape.221 = bf16[3072,768]{1,0:T(8,128)(2,1)} reshape(bf16[768,3072]{1,0:T(8,128)(2,1)} %slice.202) | data formatting | bytes 9437184 | tf_op jit(solution)/shard_map/reshape | solution.py:318
  184.1 7.8 %multiply_convert_fusion = (bf16[750,3072]{1,0:T(8,128)(2,1)S(1)}, f32[750,3072]{1,0:T(8,128)S(1)}) fusion(f32[3072]{0:T(1024)S(1)} %add.234, bf16[768,6912]{1,0:T(8,128)(2,1)} %all-gather.5.cloned.1.call-done, f32[750,768]{1,0:T(8,128)} %copy-done.6, f32[768]{0:T(1024)S(1)} %get-tuple-element.103, f32[768]{0:T(1024)S(1)} %get-tuple-element.104, ...), kind=kOutput, calls=%fused_computation.14 | convolution fusion | flops 3555648000 | bytes 20877168 | tf_op jit(solution)/shard_map/dot_general | solution.py:350
  191.9 8.4 %convert_reduce_fusion = (f32[3072]{0:T(1024)}, bf16[750,3072]{1,0:T(8,128)(2,1)S(1)}) fusion(f32[750,3072]{1,0:T(8,128)S(1)} %get-tuple-element.145, f32[3072]{0:T(1024)S(1)} %add.234, bf16[3072,768]{1,0:T(8,128)(2,1)S(1)} %copy-done.13, bf16[1,750,768]{2,1,0:T(8,128)(2,1)S(1)} %copy-done.24), kind=kOutput, calls=%fused_computation.13 | convolution fusion | flops 3568892928 | bytes 19719168 | tf_op jit(solution)/shard_map/dot_general | solution.py:362
  200.3 7.0 %fusion.78 = f32[768,3072]{1,0:T(8,128)} fusion(bf16[750,3072]{1,0:T(8,128)(2,1)S(1)} %get-tuple-element.143, f32[750,768]{1,0:T(8,128)S(1)} %copy-done.7, f32[768]{0:T(1024)S(1)} %get-tuple-element.103, f32[768]{0:T(1024)S(1)} %get-tuple-element.104, f32[750]{0:T(1024)S(1)} %add_rsqrt_fusion, f32[750]{0:T(1024)S(1)} %broadcast_multiply_fusion.4), kind=kOutput, calls=%fused_computation.158 | convolution fusion | flops 3541824000 | bytes 16361328 | tf_op jit(solution)/shard_map/dot_general | solution.py:364
  207.3 7.3 %multiply_reduce_fusion = (f32[768]{0:T(1024)}, f32[750]{0:T(1024)S(1)}, f32[750]{0:T(1024)S(1)}, f32[768]{0:T(1024)}, f32[750,768]{1,0:T(8,128)S(1)}) fusion(f32[750,768]{1,0:T(8,128)S(1)} %copy-done.7, f32[750]{0:T(1024)S(1)} %add_rsqrt_fusion, f32[750]{0:T(1024)S(1)} %broadcast_multiply_fusion.4, f32[768]{0:T(1024)S(1)} %get-tuple-element.104, ...), kind=kOutput, calls=%fused_computation.55 | convolution fusion | flops 3544124928 | bytes 13955808 | tf_op jit(solution)/shard_map/dot_general | solution.py:366
  214.6 1.8 convert_reduce_fusion.4
  216.4 2.5 fusion.45
  218.9 6.4 %fusion.40 = f32[3072,768]{1,0:T(8,128)} fusion(bf16[750,3072]{1,0:T(8,128)(2,1)S(1)} %get-tuple-element.144, bf16[1,750,768]{2,1,0:T(8,128)(2,1)S(1)} %copy-done.24), kind=kOutput, calls=%fused_computation.69 | convolution fusion | flops 3538944000 | bytes 15197184 | tf_op jit(solution)/shard_map/dot_general | solution.py:360
  225.4 11.6 %reshape.226 = f32[768,3072]{1,0:T(8,128)} reshape(f32[3072,768]{1,0:T(8,128)} %fusion.40) | data formatting | bytes 18874368 | tf_op jit(solution)/shard_map/reshape | solution.py:376
  237.0 14.2 %pad_maximum_fusion = f32[768,6912]{1,0:T(8,128)} fusion(f32[768,768]{1,0:T(8,128)S(1)} %copy-done.11, f32[768,3072]{1,0:T(8,128)} %fusion.78, f32[768,3072]{1,0:T(8,128)} %reshape.226), kind=kLoop, calls=%fused_computation | loop fusion | flops 10616832 | bytes 42467328 | tf_op jit(solution)/shard_map/concatenate | solution.py:375
  251.4 1.4 copy-done.4
  252.8 2.4 convolution_convert_fusion
  255.3 52.7 %shard_map.294 = (f32[768,768]{1,0:T(8,128)S(1)}, f32[1536,768]{1,0:T(8,128)}, f32[1536,768]{1,0:T(8,128)}) custom-call(bf16[768,768]{1,0:T(8,128)(2,1)S(1)} %pad.14.q_ref, bf16[1536,1536]{1,0:T(8,128)(2,1)} %fusion.8.k_ref.v_ref, bf16[1536,1536]{1,0:T(8,128)(2,1)} %fusion.8.k_ref.v_ref, bf16[768,768]{1,0:T(8,128)(2,1)S(1)} %pad.16.do_ref, ...), custom_call_target="tpu_custom_call" | custom-call | tf_op jit(solution)/shard_map/pallas_call | solution.py:169
  308.0 2.8 slice.163
  310.8 2.8 copy-done.14
  314.0 2.2 fusion.12
  316.8 1.0 collective-permute-start.1
  317.9 0.9 stack.97
  318.8 0.9 stack.98
  319.8 0.9 stack.99
  320.7 1.1 reshape.225
  322.1 68.7 %collective-permute-done.1 = bf16[750,1536]{1,0:T(8,128)(2,1)} collective-permute-done((bf16[750,1536]{1,0:T(8,128)(2,1)}, bf16[750,1536]{1,0:T(8,128)(2,1)}, u32[]{:S(2)}, u32[]{:S(2)}) %collective-permute-start.1) | collective-permute-done | bytes 2304032 | tf_op jit(solution)/shard_map/ppermute | solution.py:390
  390.8 3.9 fusion.11
  394.7 4.6 fusion.36
  399.3 0.9 stack.92
  400.3 0.9 stack.93
  401.7 0.9 stack.94
  402.6 0.9 stack.95
  403.6 6.9 %fusion.48 = f32[768,2304]{1,0:T(8,128)} fusion(bf16[750,768]{1,0:T(8,128)(2,1)} %fusion.30, bf16[750,1536]{1,0:T(8,128)(2,1)S(1)} %fusion.11, bf16[750,768]{1,0:T(8,128)(2,1)S(1)} %multiply_convert_fusion.1), kind=kOutput, calls=%fused_computation.77 | convolution fusion | flops 2661120000 | bytes 11685888 | tf_op jit(solution)/shard_map/dot_general | solution.py:395
  410.6 9.7 %concatenate.36 = f32[768,2560]{1,0:T(8,128)} concatenate(f32[768,2304]{1,0:T(8,128)} %fusion.48, f32[768,1]{1,0:T(8,128)} %stack.92, f32[768,1]{1,0:T(8,128)} %stack.93, f32[768,1]{1,0:T(8,128)} %stack.94, f32[768,1]{1,0:T(8,128)} %stack.95, f32[768,1]{1,0:T(8,128)S(1)} %stack.96, f32[768,1]{1,0:T(8,128)S(1)} %copy-done.17, f32[768,1]{1,0:T(8,128)S(1)} %copy-done.18, ...), dimensions={1} | concatenate | bytes 15728640 | tf_op jit(solution)/shard_map/concatenate | solution.py:426
  420.3 58.5 %reduce-scatter.3.cloned.1.call-done = f32[24,6912]{1,0:T(8,128)} async-done(((f32[768,6912]{1,0:T(8,128)}), f32[24,6912]{1,0:T(8,128)}) %reduce-scatter.3.cloned.1.call-update) | async-done | bytes 663568 | tf_op jit(solution)/shard_map/reduce_scatter | solution.py:374
  479.0 8.6 %fusion.38 = bf16[1,750,768]{2,1,0:T(8,128)(2,1)} fusion(f32[750,768]{1,0:T(8,128)S(1)} %copy-done.8, bf16[750,3072]{1,0:T(8,128)(2,1)} %copy-done.48, bf16[3072,768]{1,0:T(8,128)(2,1)} %reshape.221, f32[768]{0:T(1024)S(1)} %copy-done.41), kind=kOutput, calls=%fused_computation.66 | convolution fusion | flops 3540672000 | bytes 12785664 | tf_op jit(solution)/shard_map/dot_general | solution.py:354
  487.7 1.8 fusion.39
  490.4 0.9 fusion.65
  492.8 0.9 pad_maximum_fusion.6
  493.7 0.9 fusion.58
  494.7 0.9 fusion.62
  495.6 0.9 pad_maximum_fusion.5
  496.5 110.5 %reduce-scatter.5.cloned.1.call-done = f32[24,2560]{1,0:T(8,128)} async-done(((f32[768,2560]{1,0:T(8,128)}), f32[24,2560]{1,0:T(8,128)}) %reduce-scatter.5.cloned.1.call-update) | async-done | bytes 245776 | tf_op jit(solution)/shard_map/reduce_scatter | solution.py:428
  609.4 1.0 fusion.63
  610.4 0.9 fusion.64
  612.6 0.8 pad_maximum_fusion.7
  (156 shorter events, 14.5 us)
Async XLA Ops:
  7.2 7.3 %copy-start.9 = (bf16[1,750,768]{2,1,0:T(8,128)(2,1)S(1)}, bf16[1,750,768]{2,1,0:T(8,128)(2,1)}, u32[]{:S(2)}) copy-start(bf16[1,750,768]{2,1,0:T(8,128)(2,1)} %param.14) | copy-start | bytes 3456004
  7.2 67.7 %all-gather.3.cloned.1.call-start = ((), (), s32[]{:S(2)}) async-start(), calls=%async_computation.2 | async-start | bytes 3852288 | tf_op jit(solution)/shard_map/all_gather | solution.py:310
  10.6 155.9 %all-gather.5.cloned.1.call-start = ((), (), s32[]{:S(2)}) async-start(), calls=%async_computation.3 | async-start | bytes 10948608 | tf_op jit(solution)/shard_map/all_gather | solution.py:311
  14.4 464.4 %reduce-scatter.3.cloned.1.call-start = ((), (), s32[]{:S(2)}) async-start(), calls=%async_computation.4 | async-start | bytes 21897216 | tf_op jit(solution)/shard_map/reduce_scatter | solution.py:374
  15.2 64.2 %copy-start.32 = (f32[750]{0:T(1024)}, f32[750]{0:T(1024)S(1)}, u32[]{:S(2)}) copy-start(f32[750]{0:T(1024)S(1)} %add_rsqrt_fusion.1) | copy-start | bytes 9004
  75.9 5.9 copy-start.38
  79.4 32.1 %collective-permute-start = (bf16[750,768]{1,0:T(8,128)(2,1)}, bf16[750,768]{1,0:T(8,128)(2,1)}, u32[]{:S(2)}, u32[]{:S(2)}) collective-permute-start(bf16[750,768]{1,0:T(8,128)(2,1)} %fusion.30), channel_id=1, source_target_pairs={{0,1},{1,0},{2,3},{3,2},{4,5},{5,4},{6,7},{7,6},{8,9},{9,8},{10,11... | collective-permute-start | bytes 3456008 | tf_op jit(solution)/shard_map/ppermute | solution.py:325
  86.0 1.7 copy-start.12
  89.0 26.5 %slice-start = ((bf16[750,2304]{1,0:T(8,128)(2,1)}), bf16[750,1536]{1,0:T(8,128)(2,1)S(1)}, s32[]{:S(2)}) async-start(bf16[750,2304]{1,0:T(8,128)(2,1)} %copy-done.12), calls=%async_computation.6 | async-start | bytes 4620288 | tf_op jit(solution)/shard_map/slice | solution.py:337
  118.6 47.9 %copy-start.44 = (f32[768]{0:T(1024)S(1)}, f32[768]{0:T(1024)}, u32[]{:S(2)}) copy-start(f32[768]{0:T(1024)} %get-tuple-element.105) | copy-start | bytes 9220
  153.0 1.4 copy-start
  168.9 1.4 copy-start.6
  184.1 7.8 %copy-start.13 = (bf16[3072,768]{1,0:T(8,128)(2,1)S(1)}, bf16[3072,768]{1,0:T(8,128)(2,1)}, u32[]{:S(2)}) copy-start(bf16[3072,768]{1,0:T(8,128)(2,1)} %reshape.221) | copy-start | bytes 14155780
  184.1 7.8 %copy-start.24 = (bf16[1,750,768]{2,1,0:T(8,128)(2,1)S(1)}, bf16[1,750,768]{2,1,0:T(8,128)(2,1)}, u32[]{:S(2)}) copy-start(bf16[1,750,768]{2,1,0:T(8,128)(2,1)} %param.15) | copy-start | bytes 3456004
  191.9 27.1 %copy-start.48 = (bf16[750,3072]{1,0:T(8,128)(2,1)}, bf16[750,3072]{1,0:T(8,128)(2,1)S(1)}, u32[]{:S(2)}) copy-start(bf16[750,3072]{1,0:T(8,128)(2,1)S(1)} %get-tuple-element.144) | copy-start | bytes 13824004
  191.9 8.4 %copy-start.7 = (f32[750,768]{1,0:T(8,128)S(1)}, f32[750,768]{1,0:T(8,128)}, u32[]{:S(2)}) copy-start(f32[750,768]{1,0:T(8,128)} %copy-done.6) | copy-start | bytes 6912004
  216.4 2.5 copy-start.3
  225.4 11.6 %copy-start.11 = (f32[768,768]{1,0:T(8,128)S(1)}, f32[768,768]{1,0:T(8,128)}, u32[]{:S(2)}) copy-start(f32[768,768]{1,0:T(8,128)} %fusion.45) | copy-start | bytes 7077892
  251.2 1.7 copy-start.4
  251.2 355.8 %reduce-scatter.5.cloned.1.call-start = ((), (), s32[]{:S(2)}) async-start(), calls=%async_computation.5 | async-start | bytes 8110080 | tf_op jit(solution)/shard_map/reduce_scatter | solution.py:428
  308.0 5.6 copy-start.14
  310.8 3.1 copy-start.1
  313.9 2.9 copy-start.2
  313.9 3.8 copy-start.35
  313.9 4.0 copy-start.43
  313.9 4.9 copy-start.42
  313.9 5.8 copy-start.34
  314.0 6.7 %copy-start.37 = (f32[3072]{0:T(1024)S(1)}, f32[3072]{0:T(1024)}, u32[]{:S(2)}) copy-start(f32[3072]{0:T(1024)} %get-tuple-element.142) | copy-start | bytes 36868
  316.8 74.0 %collective-permute-start.1 = (bf16[750,1536]{1,0:T(8,128)(2,1)}, bf16[750,1536]{1,0:T(8,128)(2,1)}, u32[]{:S(2)}, u32[]{:S(2)}) collective-permute-start(bf16[750,1536]{1,0:T(8,128)(2,1)} %fusion.12), channel_id=1, source_target_pairs={{0,1},{1,0},{2,3},{3,2},{4,5},{5,4},{6,7},{7,6},{8,9},{9,8},{10,11... | collective-permute-start | bytes 6912008 | tf_op jit(solution)/shard_map/ppermute | solution.py:390
  322.0 72.7 %copy-start.10 = (bf16[1,750,768]{2,1,0:T(8,128)(2,1)S(1)}, bf16[1,750,768]{2,1,0:T(8,128)(2,1)}, u32[]{:S(2)}) copy-start(bf16[1,750,768]{2,1,0:T(8,128)(2,1)} %param.14) | copy-start | bytes 3456004
  322.0 72.7 %copy-start.33 = (f32[750]{0:T(1024)S(1)}, f32[750]{0:T(1024)}, u32[]{:S(2)}) copy-start(f32[750]{0:T(1024)} %copy-done.32) | copy-start | bytes 9004
  322.1 72.7 %copy-start.39 = (bf16[768,2432]{1,0:T(8,128)(2,1)S(1)}, bf16[768,2432]{1,0:T(8,128)(2,1)}, u32[]{:S(2)}) copy-start(bf16[768,2432]{1,0:T(8,128)(2,1)} %all-gather.3.cloned.1.call-done) | copy-start | bytes 11206660
  403.6 7.0 %copy-start.17 = (f32[768,1]{1,0:T(8,128)S(1)}, f32[768,1]{1,0:T(8,128)}, u32[]{:S(2)}) copy-start(f32[768,1]{1,0:T(8,128)} %stack.97) | copy-start | bytes 9220
  403.6 7.0 %copy-start.18 = (f32[768,1]{1,0:T(8,128)S(1)}, f32[768,1]{1,0:T(8,128)}, u32[]{:S(2)}) copy-start(f32[768,1]{1,0:T(8,128)} %stack.98) | copy-start | bytes 9220
  420.2 58.5 %copy-start.36 = (f32[24,8]{0,1:T(8,128)S(1)}, f32[24,8]{0,1:T(8,128)}, u32[]{:S(2)}) copy-start(f32[24,8]{0,1:T(8,128)} %param.21) | copy-start | bytes 2308
  420.2 58.6 %copy-start.40 = (f32[2,24,8]{1,2,0:T(8,128)S(1)}, f32[2,24,8]{1,2,0:T(8,128)}, u32[]{:S(2)}) copy-start(f32[2,24,8]{1,2,0:T(8,128)} %param.27) | copy-start | bytes 4612
  420.2 58.8 %copy-start.8 = (f32[750,768]{1,0:T(8,128)S(1)}, f32[750,768]{1,0:T(8,128)}, u32[]{:S(2)}) copy-start(f32[750,768]{1,0:T(8,128)} %copy-done.6) | copy-start | bytes 6912004
  420.3 58.8 %copy-start.41 = (f32[768]{0:T(1024)S(1)}, f32[768]{0:T(1024)}, u32[]{:S(2)}) copy-start(f32[768]{0:T(1024)} %get-tuple-element.102) | copy-start | bytes 9220
  479.0 8.6 %copy-start.5 = (f32[750,768]{1,0:T(8,128)S(1)}, f32[750,768]{1,0:T(8,128)}, u32[]{:S(2)}) copy-start(f32[750,768]{1,0:T(8,128)} %copy-done.3) | copy-start | bytes 6912004
  479.0 8.6 %copy-start.16 = (f32[750,768]{1,0:T(8,128)S(1)}, f32[750,768]{1,0:T(8,128)}, u32[]{:S(2)}) copy-start(f32[750,768]{1,0:T(8,128)} %get-tuple-element.141) | copy-start | bytes 6912004
  487.7 1.8 copy-start.19
  487.7 1.8 copy-start.28
  489.5 0.9 copy-start.29
  489.5 1.8 copy-start.30
  489.5 3.2 copy-start.15
  489.6 5.0 copy-start.20
  489.6 4.1 copy-start.22
  489.7 4.9 copy-start.23
  491.3 3.3 copy-start.31
  492.1 2.6 copy-start.21
  493.7 115.7 %copy-start.25 = (f32[2,24,2304]{2,1,0:T(8,128)S(1)}, f32[2,24,2304]{2,1,0:T(8,128)}, u32[]{:S(2)}) copy-start(f32[2,24,2304]{2,1,0:T(8,128)} %param.22) | copy-start | bytes 1327108
  494.6 115.7 %copy-start.27 = (f32[24,2304]{1,0:T(8,128)S(1)}, f32[24,2304]{1,0:T(8,128)}, u32[]{:S(2)}) copy-start(f32[24,2304]{1,0:T(8,128)} %param.16) | copy-start | bytes 663556
  494.7 117.2 %copy-start.45 = (f32[2,96]{1,0:T(2,128)S(1)}, f32[2,96]{1,0:T(2,128)}, u32[]{:S(2)}) copy-start(f32[2,96]{1,0:T(2,128)} %param.26) | copy-start | bytes 2308
  494.7 117.2 %copy-start.47 = (f32[96]{0:T(128)S(1)}, f32[96]{0:T(128)}, u32[]{:S(2)}) copy-start(f32[96]{0:T(128)} %param.20) | copy-start | bytes 1156
  607.8 6.7 %copy-start.46 = (f32[96]{0:T(128)}, f32[96]{0:T(128)S(1)}, u32[]{:S(2)}) copy-start(f32[96]{0:T(128)S(1)} %reshape.228) | copy-start | bytes 1156
  610.3 4.2 copy-start.26
Sparse Core Ops, SparseCore 0:
  11.5 63.4 all-gather.2
  78.4 88.0 all-gather.4
  251.3 227.4 reduce-scatter.2
  485.2 121.7 reduce-scatter.4

commit v4 on v3

--- a/solution.py
+++ b/solution.py
@@ -374,11 +374,11 @@
     owned_late = lax.psum_scatter(
         jnp.concatenate(
             [grad_shrink_term.reshape(model_width, -1), grad_expand_term, grad_out_term], axis=1
-        ),
+        ).astype(jnp.bfloat16),
         everyone,
         scatter_dimension=0,
         tiled=True,
-    )
+    ).astype(jnp.float32)
     grad_mixed = jnp.dot(grad_attended, full_out.T, preferred_element_type=jnp.float32).astype(
         jnp.bfloat16
     )
@@ -425,7 +425,9 @@
     first_terms, owned_late = lax.optimization_barrier(
         (jnp.concatenate([grad_in_term, small_grads], axis=1), owned_late)
     )
-    owned_first = lax.psum_scatter(first_terms, everyone, scatter_dimension=0, tiled=True)
+    owned_first = lax.psum_scatter(
+        first_terms.astype(jnp.bfloat16), everyone, scatter_dimension=0, tiled=True
+    ).astype(jnp.float32)
     owned_in = owned_first[:, :wide_in]
     owned_vectors = owned_first[:, wide_in : wide_in + vectors.shape[1]]
     owned_bias = owned_first[:, wide_in + vectors.shape[1] : wide_in + 12].reshape(-1)

time: 628 us -> 534 us (0.85)
  waiting for transfers between devices: 332 us -> 247 us
    reduce_scatter x1, waiting for transfers between devices: 58.5 us -> 0.02 us  [body(): lax.psum_scatter(jnp.concatenate([grad_shrink_term.reshape(model_width, -...]
    reduce_scatter x1, waiting for transfers between devices: 110 us -> 86.9 us  [body(): lax.psum_scatter(first_terms.astype(jnp.bfloat16), everyone, scatter_dime...]
    unnamed x103 -> x111, local copies, waits for them, and re-layouts: 11.5 us -> 14.2 us
  transfers between devices with their start and end apart: 6 -> 6, of which waited for: 6 -> 5; matrix products, arithmetic and copies ran while one was open for 13% -> 14% of each run, Pallas kernels for 14% -> 16%
where the time goes in v4:
time: 534 us; the launch traced here: 528 us
  waiting for transfers between devices  247 us (46%)
  Pallas kernels  86.9 us (16%)
  matrix products  70.9 us (13%)
  local copies, waits for them, and re-layouts  59.6 us (11%)
  other arithmetic  44.6 us (8%)
  between operations  14.9 us (3%)
    reduce_scatter x1, waiting for transfers between devices, body(): lax.psum_scatter(first_terms.astype(jnp.bfloat16), everyone, scatter_dime...  86.9 us
    ppermute x1, waiting for transfers between devices, body(): returned_terms = lax.ppermute(partner_terms, 'frame', swap)  65.5 us
    all_gather x1, waiting for transfers between devices, body(): first_full = lax.all_gather(first_pack, everyone, axis=0, tiled=True)  59.7 us
    pallas_call x1, Pallas kernels, attention_pallas(): pl.pallas_call(attention_backward_kernel, grid=(pair_count,), in_specs=[q...  52.6 us
    pallas_call x1, Pallas kernels, attention_pallas(): pl.pallas_call(attention_forward_kernel, grid=(pair_count,), in_specs=[q_...  34.3 us
    ppermute x1, waiting for transfers between devices, body(): hidden_partner = lax.ppermute(hidden_first, 'frame', swap)  22.5 us
    unnamed x111, local copies, waits for them, and re-layouts  14.2 us
    all_gather x1, waiting for transfers between devices, body(): second_full = lax.all_gather(second_pack, everyone, axis=0, tiled=True)  12.8 us
  transfers between devices with their start and end apart: 6, of which 5 were waited for; matrix products, arithmetic and copies ran while one was open for 14% of the time, Pallas kernels for 16%

profile of v4, /device:TPU:0, one launch (start us, length us, event | category | flops | bytes accessed | tf_op | source)
XLA Modules:
  0.0 527.8 jit_solution(4123439791336186414)
XLA Ops:
  8.9 1.0 convert.35
  10.7 0.9 convert.38
  11.5 1.0 convert.39
  12.5 1.0 convert.40
  15.2 59.7 %all-gather.3.cloned.1.call-done = bf16[768,2432]{1,0:T(8,128)(2,1)} async-done(((bf16[24,2432]{1,0:T(8,128)(2,1)}), bf16[768,2432]{1,0:T(8,128)(2,1)}) %all-gather.3.cloned.1.call-update) | async-done | bytes 3735568 | tf_op jit(solution)/shard_map/all_gather | solution.py:310
  74.9 1.0 slice_convert_fusion
  75.9 2.0 slice_reduce_fusion
  77.9 1.5 fusion.30
  79.4 1.5 collective-permute-start
  81.0 0.8 add.234
  81.9 5.2 add_convert_fusion
  87.2 1.6 copy-done.5
  89.0 22.5 %collective-permute-done = bf16[750,768]{1,0:T(8,128)(2,1)} collective-permute-done((bf16[750,768]{1,0:T(8,128)(2,1)}, bf16[750,768]{1,0:T(8,128)(2,1)}, u32[]{:S(2)}, u32[]{:S(2)}) %collective-permute-start) | collective-permute-done | bytes 1152032 | tf_op jit(solution)/shard_map/ppermute | solution.py:325
  111.5 3.2 add_convert_fusion.1
  114.7 3.2 fusion.8.k_ref.v_ref
  118.0 34.3 %shard_map.293 = (bf16[768,768]{1,0:T(8,128)(2,1)S(1)}, f32[768,768]{1,0:T(8,128)S(1)}) custom-call(bf16[768,768]{1,0:T(8,128)(2,1)S(1)} %pad.14.q_ref, bf16[1536,1536]{1,0:T(8,128)(2,1)} %fusion.8.k_ref.v_ref, bf16[1536,1536]{1,0:T(8,128)(2,1)} %fusion.8.k_ref.v_ref, f32[1,1536]{1,0:T(1,128)S(1)} %compare_select_fusion.kbias_ref), custom_call_target="tpu_custom_call" | custom-call | tf_op jit(solution)/shard_map/pallas_call | solution.py:156
  152.3 1.4 copy-done
  153.7 12.8 %all-gather.5.cloned.1.call-done = bf16[768,6912]{1,0:T(8,128)(2,1)} async-done(((bf16[24,6912]{1,0:T(8,128)(2,1)}), bf16[768,6912]{1,0:T(8,128)(2,1)}) %all-gather.5.cloned.1.call-update) | async-done | bytes 10616848 | tf_op jit(solution)/shard_map/all_gather | solution.py:311
  166.5 2.5 fusion.78
  169.0 1.4 copy-done.6
  170.8 4.8 slice.202
  175.5 8.5 %reshape.222 = bf16[3072,768]{1,0:T(8,128)(2,1)} reshape(bf16[768,3072]{1,0:T(8,128)(2,1)} %slice.202) | data formatting | bytes 9437184 | tf_op jit(solution)/shard_map/reshape | solution.py:318
  184.1 9.1 %multiply_convert_fusion = (bf16[750,3072]{1,0:T(8,128)(2,1)S(1)}, f32[750,3072]{1,0:T(8,128)}) fusion(f32[3072]{0:T(1024)S(1)} %copy-done.36, bf16[768,6912]{1,0:T(8,128)(2,1)} %all-gather.5.cloned.1.call-done, f32[750,768]{1,0:T(8,128)} %copy-done.6, f32[768]{0:T(1024)} %get-tuple-element.103, f32[768]{0:T(1024)S(1)} %get-tuple-element.104, ...), kind=kOutput, calls=%fused_computation.14 | convolution fusion | flops 3555648000 | bytes 20878192 | tf_op jit(solution)/shard_map/dot_general | solution.py:350
  193.2 2.1 copy-done.50
  195.3 5.6 %convolution_convert_fusion.1 = bf16[3072,768]{1,0:T(8,128)(2,1)} fusion(bf16[750,3072]{1,0:T(8,128)(2,1)S(1)} %get-tuple-element.143, bf16[1,750,768]{2,1,0:T(8,128)(2,1)S(1)} %copy-done.21), kind=kOutput, calls=%fused_computation.19 | convolution fusion | flops 3541303296 | bytes 10478592 | tf_op jit(solution)/shard_map/dot_general | solution.py:360
  200.9 8.6 %reshape.227 = bf16[768,3072]{1,0:T(8,128)(2,1)} reshape(bf16[3072,768]{1,0:T(8,128)(2,1)} %convolution_convert_fusion.1) | data formatting | bytes 9437184 | tf_op jit(solution)/shard_map/reshape | solution.py:376
  209.5 10.0 %convert_reduce_fusion = (bf16[3072]{0:T(1024)(128)(2,1)}, bf16[750,3072]{1,0:T(8,128)(2,1)S(1)}) fusion(f32[750,3072]{1,0:T(8,128)} %get-tuple-element.144, f32[3072]{0:T(1024)S(1)} %copy-done.36, bf16[3072,768]{1,0:T(8,128)(2,1)} %reshape.222, bf16[1,750,768]{2,1,0:T(8,128)(2,1)S(1)} %copy-done.21), kind=kOutput, calls=%fused_computation.13 | convolution fusion | flops 3568892928 | bytes 19713024 | tf_op jit(solution)/shard_map/dot_general | solution.py:362
  219.6 4.9 convolution_convert_fusion
  224.5 7.3 %multiply_reduce_fusion = (bf16[768]{0:T(1024)(128)(2,1)}, f32[750]{0:T(1024)S(1)}, f32[750]{0:T(1024)S(1)}, bf16[768]{0:T(1024)(128)(2,1)}, f32[750,768]{1,0:T(8,128)S(1)}) fusion(f32[750,768]{1,0:T(8,128)S(1)} %copy-done.7, f32[750]{0:T(1024)S(1)} %add_rsqrt_fusion, f32[750]{0:T(1024)S(1)} %broadcast_multiply_fusion.4, f32[768]{0:T(1024)S(1)} %get-tuple-element.104, ...), kind=kOutput, calls=%fused_computation.57 | convolution fusion | flops 3544124928 | bytes 13952736 | tf_op jit(solution)/shard_map/dot_general | solution.py:366
  231.8 1.8 convert_reduce_fusion.4
  233.6 1.4 copy-done.9
  235.0 1.1 convolution_convert_fusion.2
  236.2 8.0 %pad_maximum_fusion = bf16[768,6912]{1,0:T(8,128)(2,1)} fusion(bf16[768,768]{1,0:T(8,128)(2,1)S(1)} %convolution_convert_fusion.2, bf16[768,3072]{1,0:T(8,128)(2,1)S(1)} %convolution_convert_fusion, bf16[768,3072]{1,0:T(8,128)(2,1)S(1)} %bitcast.152), kind=kLoop, calls=%fused_computation.1 | loop fusion | flops 31850496 | bytes 21233664 | tf_op jit(solution)/shard_map/concatenate | solution.py:375
  244.5 1.4 copy-done.10
  245.9 2.4 convolution_convert_fusion.3
  248.3 52.6 %shard_map.294 = (f32[768,768]{1,0:T(8,128)S(1)}, f32[1536,768]{1,0:T(8,128)}, f32[1536,768]{1,0:T(8,128)}) custom-call(bf16[768,768]{1,0:T(8,128)(2,1)S(1)} %pad.14.q_ref, bf16[1536,1536]{1,0:T(8,128)(2,1)} %fusion.8.k_ref.v_ref, bf16[1536,1536]{1,0:T(8,128)(2,1)} %fusion.8.k_ref.v_ref, bf16[768,768]{1,0:T(8,128)(2,1)S(1)} %pad.16.do_ref, ...), custom_call_target="tpu_custom_call" | custom-call | tf_op jit(solution)/shard_map/pallas_call | solution.py:169
  301.0 2.8 slice.163
  303.8 1.1 copy-done.12
  305.9 2.1 fusion.12
  308.7 1.5 collective-permute-start.1
  310.2 1.1 reshape.226
  311.3 0.8 stack.96
  312.2 0.8 stack.97
  313.0 0.8 stack.99
  313.9 0.8 stack.98
  314.9 65.5 %collective-permute-done.1 = bf16[750,1536]{1,0:T(8,128)(2,1)} collective-permute-done((bf16[750,1536]{1,0:T(8,128)(2,1)}, bf16[750,1536]{1,0:T(8,128)(2,1)}, u32[]{:S(2)}, u32[]{:S(2)}) %collective-permute-start.1) | collective-permute-done | bytes 2304032 | tf_op jit(solution)/shard_map/ppermute | solution.py:390
  380.4 3.9 fusion.11
  385.6 4.6 fusion.36
  390.8 6.3 %fusion.46 = bf16[768,2304]{1,0:T(8,128)(2,1)} fusion(bf16[750,768]{1,0:T(8,128)(2,1)} %fusion.30, bf16[750,1536]{1,0:T(8,128)(2,1)S(1)} %fusion.11, bf16[750,768]{1,0:T(8,128)(2,1)S(1)} %multiply_convert_fusion.1), kind=kOutput, calls=%fused_computation.78 | convolution fusion | flops 2661120000 | bytes 8146944 | tf_op jit(solution)/shard_map/dot_general | solution.py:395
  397.1 7.7 %concatenate.37 = bf16[768,2560]{1,0:T(8,128)(2,1)} concatenate(bf16[768,2304]{1,0:T(8,128)(2,1)} %fusion.46, bf16[768,1]{1,0:T(8,128)(2,1)S(1)} %stack.92, bf16[768,1]{1,0:T(8,128)(2,1)S(1)} %stack.93, bf16[768,1]{1,0:T(8,128)(2,1)S(1)} %stack.94, bf16[768,1]{1,0:T(8,128)(2,1)S(1)} %stack.95, bf16[768,1]{1,0:T(8,128)(2,1)S(1)} %copy-done.26, bf16[768,1]{1,0:T(8,128)(2,1)S(1)} %copy-done.27, ...), dimensions={1} | concatenate | bytes 7864320 | tf_op jit(solution)/shard_map/concatenate | solution.py:426
  404.9 2.0 convert_element_type.101
  407.2 8.6 %fusion.38 = bf16[1,750,768]{2,1,0:T(8,128)(2,1)} fusion(f32[750,768]{1,0:T(8,128)S(1)} %copy-done.8, bf16[750,3072]{1,0:T(8,128)(2,1)} %copy-done.50, bf16[3072,768]{1,0:T(8,128)(2,1)} %reshape.222, f32[768]{0:T(1024)S(1)} %copy-done.43), kind=kOutput, calls=%fused_computation.69 | convolution fusion | flops 3540672000 | bytes 12785664 | tf_op jit(solution)/shard_map/dot_general | solution.py:354
  415.8 1.8 fusion.39
  417.8 0.8 reshape.228
  418.6 0.8 reshape.230
  420.8 1.1 multiply_add_fusion
  421.9 0.9 pad_maximum_fusion.6
  422.7 0.9 fusion.56
  423.7 0.9 fusion.60
  424.6 0.9 pad_maximum_fusion.5
  425.5 86.9 %reduce-scatter.5.cloned.1.call-done = bf16[24,2560]{1,0:T(8,128)(2,1)} async-done(((bf16[768,2560]{1,0:T(8,128)(2,1)}), bf16[24,2560]{1,0:T(8,128)(2,1)}) %reduce-scatter.5.cloned.1.call-update) | async-done | bytes 122896 | tf_op jit(solution)/shard_map/reduce_scatter | solution.py:428
  515.3 0.9 convert_element_type.103
  517.0 0.9 fusion.61
  518.0 0.9 fusion.62
  (168 shorter events, 16.6 us)
Async XLA Ops:
  7.2 7.3 %copy-start.3 = (bf16[1,750,768]{2,1,0:T(8,128)(2,1)S(1)}, bf16[1,750,768]{2,1,0:T(8,128)(2,1)}, u32[]{:S(2)}) copy-start(bf16[1,750,768]{2,1,0:T(8,128)(2,1)} %param.14) | copy-start | bytes 3456004
  7.2 67.7 %all-gather.3.cloned.1.call-start = ((), (), s32[]{:S(2)}) async-start(), calls=%async_computation.2 | async-start | bytes 3852288 | tf_op jit(solution)/shard_map/all_gather | solution.py:310
  10.6 155.9 %all-gather.5.cloned.1.call-start = ((), (), s32[]{:S(2)}) async-start(), calls=%async_computation.3 | async-start | bytes 10948608 | tf_op jit(solution)/shard_map/all_gather | solution.py:311
  14.4 390.5 %reduce-scatter.3.cloned.1.call-start = ((), (), s32[]{:S(2)}) async-start(), calls=%async_computation.4 | async-start | bytes 10948608 | tf_op jit(solution)/shard_map/reduce_scatter | solution.py:374
  15.2 64.2 %copy-start.33 = (f32[750]{0:T(1024)}, f32[750]{0:T(1024)S(1)}, u32[]{:S(2)}) copy-start(f32[750]{0:T(1024)S(1)} %add_rsqrt_fusion.1) | copy-start | bytes 9004
  79.4 32.1 %collective-permute-start = (bf16[750,768]{1,0:T(8,128)(2,1)}, bf16[750,768]{1,0:T(8,128)(2,1)}, u32[]{:S(2)}, u32[]{:S(2)}) collective-permute-start(bf16[750,768]{1,0:T(8,128)(2,1)} %fusion.30), channel_id=1, source_target_pairs={{0,1},{1,0},{2,3},{3,2},{4,5},{5,4},{6,7},{7,6},{8,9},{9,8},{10,11... | collective-permute-start | bytes 3456008 | tf_op jit(solution)/shard_map/ppermute | solution.py:325
  87.1 1.8 copy-start.5
  87.1 24.4 %copy-start.37 = (bf16[768,2432]{1,0:T(8,128)(2,1)S(1)}, bf16[768,2432]{1,0:T(8,128)(2,1)}, u32[]{:S(2)}) copy-start(bf16[768,2432]{1,0:T(8,128)(2,1)} %all-gather.3.cloned.1.call-done) | copy-start | bytes 11206660
  88.9 25.8 %slice-start.2 = ((bf16[750,2304]{1,0:T(8,128)(2,1)}), bf16[750,1536]{1,0:T(8,128)(2,1)S(1)}, s32[]{:S(2)}) async-start(bf16[750,2304]{1,0:T(8,128)(2,1)} %copy-done.5), calls=%async_computation.8 | async-start | bytes 4620288 | tf_op jit(solution)/shard_map/slice | solution.py:337
  152.3 1.4 copy-start
  168.9 1.4 copy-start.6
  175.5 8.5 %copy-start.36 = (f32[3072]{0:T(1024)S(1)}, f32[3072]{0:T(1024)}, u32[]{:S(2)}) copy-start(f32[3072]{0:T(1024)} %add.234) | copy-start | bytes 36868
  184.1 11.2 %copy-start.21 = (bf16[1,750,768]{2,1,0:T(8,128)(2,1)S(1)}, bf16[1,750,768]{2,1,0:T(8,128)(2,1)}, u32[]{:S(2)}) copy-start(bf16[1,750,768]{2,1,0:T(8,128)(2,1)} %param.15) | copy-start | bytes 3456004
  193.2 2.1 copy-start.50
  209.5 10.0 %copy-start.7 = (f32[750,768]{1,0:T(8,128)S(1)}, f32[750,768]{1,0:T(8,128)}, u32[]{:S(2)}) copy-start(f32[750,768]{1,0:T(8,128)} %copy-done.6) | copy-start | bytes 6912004
  209.5 10.0 %copy-start.44 = (f32[768]{0:T(1024)S(1)}, f32[768]{0:T(1024)}, u32[]{:S(2)}) copy-start(f32[768]{0:T(1024)} %get-tuple-element.103) | copy-start | bytes 9220
  219.5 16.6 %slice-start = ((s8[4718592]{0:T(1024)(128)(4,1)}), s8[4194304]{0:T(1024)(128)(4,1)S(1)}, s32[]{:S(2)}) async-start(s8[4718592]{0:T(1024)(128)(4,1)} %bitcast.151), calls=%async_computation.6 | async-start | bytes 8388608
  224.5 11.7 %slice-start.1 = ((s8[4718592]{0:T(1024)(128)(4,1)}), s8[524288]{0:T(1024)(128)(4,1)S(1)}, s32[]{:S(2)}) async-start(s8[4718592]{0:T(1024)(128)(4,1)} %bitcast.151), calls=%async_computation.7 | async-start | bytes 1048576
  233.6 1.4 copy-start.9
  244.2 1.7 copy-start.10
  244.2 268.1 %reduce-scatter.5.cloned.1.call-start = ((), (), s32[]{:S(2)}) async-start(), calls=%async_computation.5 | async-start | bytes 4055040 | tf_op jit(solution)/shard_map/reduce_scatter | solution.py:428
  301.0 3.9 copy-start.12
  303.8 2.1 copy-start.1
  305.9 2.9 copy-start.2
  305.9 4.4 copy-start.42
  305.9 5.5 %copy-start.41 = (bf16[768]{0:T(1024)(128)(2,1)S(1)}, bf16[768]{0:T(1024)(128)(2,1)}, u32[]{:S(2)}) copy-start(bf16[768]{0:T(1024)(128)(2,1)} %get-tuple-element.116) | copy-start | bytes 4612
  305.9 6.3 %copy-start.47 = (bf16[768]{0:T(1024)(128)(2,1)S(1)}, bf16[768]{0:T(1024)(128)(2,1)}, u32[]{:S(2)}) copy-start(bf16[768]{0:T(1024)(128)(2,1)} %get-tuple-element.94) | copy-start | bytes 4612
  305.9 7.2 %copy-start.40 = (bf16[768]{0:T(1024)(128)(2,1)S(1)}, bf16[768]{0:T(1024)(128)(2,1)}, u32[]{:S(2)}) copy-start(bf16[768]{0:T(1024)(128)(2,1)} %get-tuple-element.118) | copy-start | bytes 4612
  305.9 8.0 %copy-start.46 = (bf16[768]{0:T(1024)(128)(2,1)S(1)}, bf16[768]{0:T(1024)(128)(2,1)}, u32[]{:S(2)}) copy-start(bf16[768]{0:T(1024)(128)(2,1)} %get-tuple-element.100) | copy-start | bytes 4612
  308.7 71.7 %collective-permute-start.1 = (bf16[750,1536]{1,0:T(8,128)(2,1)}, bf16[750,1536]{1,0:T(8,128)(2,1)}, u32[]{:S(2)}, u32[]{:S(2)}) collective-permute-start(bf16[750,1536]{1,0:T(8,128)(2,1)} %fusion.12), channel_id=1, source_target_pairs={{0,1},{1,0},{2,3},{3,2},{4,5},{5,4},{6,7},{7,6},{8,9},{9,8},{10,11... | collective-permute-start | bytes 6912008 | tf_op jit(solution)/shard_map/ppermute | solution.py:390
  380.4 4.6 copy-start.38
  384.3 1.4 copy-start.4
  384.3 1.3 copy-start.34
  390.7 6.4 %copy-start.25 = (bf16[768,4]{1,0:T(8,128)(2,1)S(1)}, bf16[768,4]{1,0:T(8,128)(2,1)}, u32[]{:S(2)}) copy-start(bf16[768,4]{1,0:T(8,128)(2,1)} %reshape.226) | copy-start | bytes 18436
  390.7 6.4 %copy-start.26 = (bf16[768,1]{1,0:T(8,128)(2,1)S(1)}, bf16[768,1]{1,0:T(8,128)(2,1)}, u32[]{:S(2)}) copy-start(bf16[768,1]{1,0:T(8,128)(2,1)} %stack.96) | copy-start | bytes 4612
  390.8 6.4 %copy-start.27 = (bf16[768,1]{1,0:T(8,128)(2,1)S(1)}, bf16[768,1]{1,0:T(8,128)(2,1)}, u32[]{:S(2)}) copy-start(bf16[768,1]{1,0:T(8,128)(2,1)} %stack.97) | copy-start | bytes 4612
  390.8 6.4 %copy-start.28 = (bf16[768,1]{1,0:T(8,128)(2,1)S(1)}, bf16[768,1]{1,0:T(8,128)(2,1)}, u32[]{:S(2)}) copy-start(bf16[768,1]{1,0:T(8,128)(2,1)} %stack.99) | copy-start | bytes 4612
  390.8 6.3 %copy-start.29 = (bf16[768,1]{1,0:T(8,128)(2,1)S(1)}, bf16[768,1]{1,0:T(8,128)(2,1)}, u32[]{:S(2)}) copy-start(bf16[768,1]{1,0:T(8,128)(2,1)} %stack.98) | copy-start | bytes 4612
  404.8 2.1 copy-start.35
  404.8 2.2 copy-start.39
  404.8 2.3 copy-start.8
  404.8 2.3 copy-start.43
  407.1 8.7 %copy-start.11 = (f32[750,768]{1,0:T(8,128)S(1)}, f32[750,768]{1,0:T(8,128)}, u32[]{:S(2)}) copy-start(f32[750,768]{1,0:T(8,128)} %copy-done.9) | copy-start | bytes 6912004
  407.1 8.7 %copy-start.15 = (f32[750,768]{1,0:T(8,128)S(1)}, f32[750,768]{1,0:T(8,128)}, u32[]{:S(2)}) copy-start(f32[750,768]{1,0:T(8,128)} %get-tuple-element.140) | copy-start | bytes 6912004
  415.8 1.8 copy-start.13
  415.8 1.8 copy-start.16
  417.7 1.7 copy-start.30
  417.7 1.8 copy-start.31
  417.7 3.1 copy-start.14
  417.8 5.9 %copy-start.17 = (f32[24,3072]{1,0:T(8,128)}, f32[24,3072]{1,0:T(8,128)S(1)}, u32[]{:S(2)}) copy-start(f32[24,3072]{1,0:T(8,128)S(1)} %get-tuple-element.111) | copy-start | bytes 884740
  417.8 4.9 copy-start.19
  419.4 3.3 copy-start.20
  419.4 4.3 copy-start.32
  420.1 3.6 copy-start.18
  422.7 90.6 %copy-start.45 = (f32[2,96]{1,0:T(2,128)S(1)}, f32[2,96]{1,0:T(2,128)}, u32[]{:S(2)}) copy-start(f32[2,96]{1,0:T(2,128)} %param.26) | copy-start | bytes 2308
  422.7 90.6 %copy-start.49 = (f32[96]{0:T(128)S(1)}, f32[96]{0:T(128)}, u32[]{:S(2)}) copy-start(f32[96]{0:T(128)} %param.20) | copy-start | bytes 1156
  423.7 93.4 %copy-start.22 = (f32[2,24,2304]{2,1,0:T(8,128)S(1)}, f32[2,24,2304]{2,1,0:T(8,128)}, u32[]{:S(2)}) copy-start(f32[2,24,2304]{2,1,0:T(8,128)} %param.22) | copy-start | bytes 1327108
  423.7 94.3 %copy-start.24 = (f32[24,2304]{1,0:T(8,128)S(1)}, f32[24,2304]{1,0:T(8,128)}, u32[]{:S(2)}) copy-start(f32[24,2304]{1,0:T(8,128)} %param.16) | copy-start | bytes 663556
  513.2 7.6 %copy-start.48 = (f32[96]{0:T(128)}, f32[96]{0:T(128)S(1)}, u32[]{:S(2)}) copy-start(f32[96]{0:T(128)S(1)} %reshape.229) | copy-start | bytes 1156
  518.0 2.9 copy-start.23
Sparse Core Ops, SparseCore 0:
  11.5 63.4 all-gather.2
  78.4 88.0 all-gather.4
  244.4 159.5 reduce-scatter.2
  409.3 103.0 reduce-scatter.4

commit v5 on v4

--- a/solution.py
+++ b/solution.py
@@ -138,7 +138,7 @@
     return jnp.pad(values, ((0, rows - values.shape[0]), (0, 0)))
 
 
-def attention_pallas(queries, pairs, grad_out=None, totals=None):
+def attention_pallas(queries, pairs, grad_out=None, totals=None, first_pair=0, pair_span=None):
     query_rows, model_width = queries.shape
     key_rows = pairs.shape[0]
     padded_q = -(-query_rows // QUERY_CHUNK) * QUERY_CHUNK
@@ -166,15 +166,21 @@
         )(q_pad, kv_pad, kv_pad, kbias)
         return mixed[:query_rows], log_totals
     do_pad = pad_rows(grad_out, padded_q)
+    span = pair_count if pair_span is None else pair_span
+    qi_spec = pl.BlockSpec((padded_q, 128), lambda j: (0, j + first_pair))
+    ki_spec = pl.BlockSpec((padded_k, 128), lambda j: (0, j + first_pair))
+    vi_spec = pl.BlockSpec((padded_k, 128), lambda j: (0, j + first_pair + pair_count))
+    qo_spec = pl.BlockSpec((padded_q, 128), lambda j: (0, j))
+    ko_spec = pl.BlockSpec((padded_k, 128), lambda j: (0, j))
     dq, dk, dv = pl.pallas_call(
         attention_backward_kernel,
-        grid=(pair_count,),
-        in_specs=[q_spec, k_spec, v_spec, q_spec, q_spec, b_spec],
-        out_specs=[q_spec, k_spec, k_spec],
+        grid=(span,),
+        in_specs=[qi_spec, ki_spec, vi_spec, qi_spec, qi_spec, b_spec],
+        out_specs=[qo_spec, ko_spec, ko_spec],
         out_shape=[
-            jax.ShapeDtypeStruct((padded_q, model_width), jnp.float32),
-            jax.ShapeDtypeStruct((padded_k, model_width), jnp.float32),
-            jax.ShapeDtypeStruct((padded_k, model_width), jnp.float32),
+            jax.ShapeDtypeStruct((padded_q, 128 * span), jnp.float32),
+            jax.ShapeDtypeStruct((padded_k, 128 * span), jnp.float32),
+            jax.ShapeDtypeStruct((padded_k, 128 * span), jnp.float32),
         ],
         compiler_params=params,
     )(q_pad, kv_pad, kv_pad, do_pad, totals, kbias)
@@ -322,7 +328,10 @@
         frames_rows, column_set[:, 0], column_set[:, 1]
     )
     hidden_first = normed_first.astype(jnp.bfloat16)
-    hidden_partner = lax.ppermute(hidden_first, "frame", swap)
+    partner_rows = lax.ppermute(inputs, "frame", swap).reshape(row_count, model_width)
+    hidden_partner = norm_parts(
+        partner_rows.astype(jnp.float32), column_set[:, 0], column_set[:, 1]
+    )[0].astype(jnp.bfloat16)
     bias_in = jnp.concatenate(
         [column_set[:, 2], jnp.zeros((model_width,), jnp.float32), column_set[:, 3]]
     )
@@ -382,15 +391,30 @@
     grad_mixed = jnp.dot(grad_attended, full_out.T, preferred_element_type=jnp.float32).astype(
         jnp.bfloat16
     )
-    grad_query, grad_keys, grad_values = attention_pallas(
-        scaled_queries, pair_rows, grad_mixed, log_totals
-    )
-    grad_pairs_terms = jnp.concatenate([grad_keys, grad_values], axis=1)
-    partner_terms = grad_pairs_terms[row_count:].astype(jnp.bfloat16)
-    returned_terms = lax.ppermute(partner_terms, "frame", swap)
-    grad_pairs = grad_pairs_terms[:row_count] + returned_terms.astype(jnp.float32)
+    halves = []
+    half_pairs = model_width // 256
+    for first_pair in (0, half_pairs):
+        grad_query, grad_keys, grad_values = attention_pallas(
+            scaled_queries, pair_rows, grad_mixed, log_totals, first_pair, half_pairs
+        )
+        terms = jnp.concatenate([grad_keys, grad_values], axis=1)
+        returned = lax.ppermute(terms[row_count:].astype(jnp.bfloat16), "frame", swap)
+        halves.append((grad_query, terms[:row_count] + returned.astype(jnp.float32)))
+    half_width = model_width // 2
     grad_projected = jnp.concatenate(
-        [(grad_query * score_scale).astype(jnp.bfloat16), grad_pairs.astype(jnp.bfloat16)], axis=1
+        [
+            (jnp.concatenate([halves[0][0], halves[1][0]], axis=1) * score_scale).astype(jnp.bfloat16),
+            jnp.concatenate(
+                [
+                    halves[0][1][:, :half_width],
+                    halves[1][1][:, :half_width],
+                    halves[0][1][:, half_width:],
+                    halves[1][1][:, half_width:],
+                ],
+                axis=1,
+            ).astype(jnp.bfloat16),
+        ],
+        axis=1,
     )
     grad_in_term = jnp.dot(hidden_first.T, grad_projected, preferred_element_type=jnp.float32)
     projected_sums = jnp.sum(grad_projected.astype(jnp.float32), axis=0)

time: 534 us -> 528 us (0.989)
  waiting for transfers between devices: 247 us -> 236 us
  local copies, waits for them, and re-layouts: 59.6 us -> 65.9 us
    ppermute x2 -> x3, waiting for transfers between devices: 88 us -> 55.4 us  [the longest x2 28.3 us: body(): lax.ppermute(terms[row_count:].astype(jnp.bfloat16), 'frame', swap)]
    all_gather x1, waiting for transfers between devices: 59.7 us -> 29 us  [body(): first_full = lax.all_gather(first_pack, everyone, axis=0, tiled=True)]
    reduce_scatter x1, waiting for transfers between devices: 0.02 us -> 27.4 us  [body(): lax.psum_scatter(jnp.concatenate([grad_shrink_term.reshape(model_width, -...]
    all_gather x1, waiting for transfers between devices: 12.8 us -> 36 us  [body(): second_full = lax.all_gather(second_pack, everyone, axis=0, tiled=True)]
    unnamed x111 -> x138, local copies, waits for them, and re-layouts: 14.2 us -> 23 us
    convert_element_type x3 -> x0, other arithmetic: 5.54 us -> none  [the longest x1 3.86 us: body(): grad_pairs.astype(jnp.bfloat16)]
    pallas_call x1 -> x2, Pallas kernels: 52.6 us -> 55.5 us  [attention_pallas(): pl.pallas_call(attention_backward_kernel, grid=(span,), in_specs=[qi_spec...]
  transfers between devices with their start and end apart: 6 -> 7, of which waited for: 5 -> 6; matrix products, arithmetic and copies ran while one was open for 14% -> 13% of each run, Pallas kernels for 16% -> 17%
where the time goes in v5:
time: 528 us; the launch traced here: 523 us
  waiting for transfers between devices  236 us (45%)
  Pallas kernels  89.8 us (17%)
  matrix products  69.4 us (13%)
  local copies, waits for them, and re-layouts  65.9 us (12%)
  other arithmetic  42 us (8%)
  between operations  14.9 us (3%)
    reduce_scatter x1, waiting for transfers between devices, body(): lax.psum_scatter(first_terms.astype(jnp.bfloat16), everyone, scatter_dime...  87.8 us
    pallas_call x2, Pallas kernels, attention_pallas(): pl.pallas_call(attention_backward_kernel, grid=(span,), in_specs=[qi_spec...  55.5 us
    all_gather x1, waiting for transfers between devices, body(): second_full = lax.all_gather(second_pack, everyone, axis=0, tiled=True)  36 us
    pallas_call x1, Pallas kernels, attention_pallas(): pl.pallas_call(attention_forward_kernel, grid=(pair_count,), in_specs=[q_...  34.3 us
    all_gather x1, waiting for transfers between devices, body(): first_full = lax.all_gather(first_pack, everyone, axis=0, tiled=True)  29 us
    ppermute x2, waiting for transfers between devices, body(): lax.ppermute(terms[row_count:].astype(jnp.bfloat16), 'frame', swap)  28.3 us
    reduce_scatter x1, waiting for transfers between devices, body(): lax.psum_scatter(jnp.concatenate([grad_shrink_term.reshape(model_width, -...  27.4 us
    ppermute x1, waiting for transfers between devices, body(): lax.ppermute(inputs, 'frame', swap).reshape(row_count, model_width)  27.2 us
  transfers between devices with their start and end apart: 7, of which 6 were waited for; matrix products, arithmetic and copies ran while one was open for 13% of the time, Pallas kernels for 17%

profile of v5, /device:TPU:0, one launch (start us, length us, event | category | flops | bytes accessed | tf_op | source)
XLA Modules:
  0.0 523.0 jit_solution(1733567131073350138)
XLA Ops:
  8.9 1.0 convert.50
  10.7 0.9 convert.53
  11.5 1.0 convert.54
  12.5 1.0 convert.55
  14.4 3.0 collective-permute-start
  18.3 27.2 %collective-permute-done = bf16[1,750,768]{2,1,0:T(8,128)(2,1)S(1)} collective-permute-done((bf16[1,750,768]{2,1,0:T(8,128)(2,1)S(1)}, bf16[1,750,768]{2,1,0:T(8,128)(2,1)S(1)}, u32[]{:S(2)}, u32[]{:S(2)}) %collective-permute-start) | collective-permute-done | bytes 1152032 | tf_op jit(solution)/shard_map/ppermute | solution.py:331
  46.4 29.0 %all-gather.3.cloned.1.call-done = bf16[768,2432]{1,0:T(8,128)(2,1)} async-done(((bf16[24,2432]{1,0:T(8,128)(2,1)}), bf16[768,2432]{1,0:T(8,128)(2,1)}) %all-gather.3.cloned.1.call-update) | async-done | bytes 3735568 | tf_op jit(solution)/shard_map/all_gather | solution.py:316
  75.5 1.0 slice_convert_fusion
  77.4 1.8 slice_reduce_fusion
  79.3 5.7 %add_convert_fusion = bf16[750,2304]{1,0:T(8,128)(2,1)S(1)} fusion(f32[2304]{0:T(1024)S(1)} %pad_maximum_fusion.8, bf16[768,2432]{1,0:T(8,128)(2,1)} %all-gather.3.cloned.1.call-done, bf16[1,750,768]{2,1,0:T(8,128)(2,1)S(1)} %copy-done.9, f32[768]{0:T(1024)S(1)} %get-tuple-element.114, f32[768]{0:T(1024)S(1)} %get-tuple-element.115, ...), kind=kOutput, calls=%fused_computation.15 | convolution fusion | flops 2661120000 | bytes 8168304 | tf_op jit(solution)/shard_map/dot_general | solution.py:339
  85.1 1.6 copy-done.11
  86.8 1.5 copy-done.46
  88.7 2.1 add_convert_fusion.1
  90.8 2.7 fusion.8.k_ref.v_ref
  93.5 34.3 %shard_map.293 = (bf16[768,768]{1,0:T(8,128)(2,1)S(1)}, f32[768,768]{1,0:T(8,128)S(1)}) custom-call(bf16[768,768]{1,0:T(8,128)(2,1)S(1)} %pad.17.q_ref, bf16[1536,1536]{1,0:T(8,128)(2,1)} %fusion.8.k_ref.v_ref, bf16[1536,1536]{1,0:T(8,128)(2,1)} %fusion.8.k_ref.v_ref, f32[1,1536]{1,0:T(1,128)S(1)} %compare_select_fusion.kbias_ref), custom_call_target="tpu_custom_call" | custom-call | tf_op jit(solution)/shard_map/pallas_call | solution.py:156
  127.8 1.4 copy-done
  129.2 36.0 %all-gather.5.cloned.1.call-done = bf16[768,6912]{1,0:T(8,128)(2,1)} async-done(((bf16[24,6912]{1,0:T(8,128)(2,1)}), bf16[768,6912]{1,0:T(8,128)(2,1)}) %all-gather.5.cloned.1.call-update) | async-done | bytes 10616848 | tf_op jit(solution)/shard_map/all_gather | solution.py:317
  165.3 2.5 fusion.96
  167.8 1.3 copy-done.12
  169.5 4.8 slice.245
  174.3 8.5 %reshape.236 = bf16[3072,768]{1,0:T(8,128)(2,1)} reshape(bf16[768,3072]{1,0:T(8,128)(2,1)} %slice.245) | data formatting | bytes 9437184 | tf_op jit(solution)/shard_map/reshape | solution.py:324
  182.8 9.4 %multiply_convert_fusion = (bf16[750,3072]{1,0:T(8,128)(2,1)S(1)}, f32[750,3072]{1,0:T(8,128)}) fusion(f32[3072]{0:T(1024)S(1)} %copy-done.45, bf16[768,6912]{1,0:T(8,128)(2,1)} %all-gather.5.cloned.1.call-done, f32[750,768]{1,0:T(8,128)} %copy-done.12, f32[768]{0:T(1024)} %get-tuple-element.109, f32[768]{0:T(1024)S(1)} %get-tuple-element.110, ...), kind=kOutput, calls=%fused_computation.12 | convolution fusion | flops 3555648000 | bytes 20878192 | tf_op jit(solution)/shard_map/dot_general | solution.py:359
  192.3 2.1 copy-done.62
  194.4 5.6 %convolution_convert_fusion.1 = bf16[3072,768]{1,0:T(8,128)(2,1)} fusion(bf16[750,3072]{1,0:T(8,128)(2,1)S(1)} %get-tuple-element.149, bf16[1,750,768]{2,1,0:T(8,128)(2,1)S(1)} %copy-done.30), kind=kOutput, calls=%fused_computation.17 | convolution fusion | flops 3541303296 | bytes 10478592 | tf_op jit(solution)/shard_map/dot_general | solution.py:369
  200.0 8.5 %reshape.241 = bf16[768,3072]{1,0:T(8,128)(2,1)} reshape(bf16[3072,768]{1,0:T(8,128)(2,1)} %convolution_convert_fusion.1) | data formatting | bytes 9437184 | tf_op jit(solution)/shard_map/reshape | solution.py:385
  208.4 10.2 %convert_reduce_fusion = (bf16[3072]{0:T(1024)(128)(2,1)}, bf16[750,3072]{1,0:T(8,128)(2,1)S(1)}) fusion(f32[750,3072]{1,0:T(8,128)} %get-tuple-element.150, f32[3072]{0:T(1024)S(1)} %copy-done.45, bf16[3072,768]{1,0:T(8,128)(2,1)} %reshape.236, bf16[1,750,768]{2,1,0:T(8,128)(2,1)S(1)} %copy-done.30), kind=kOutput, calls=%fused_computation.11 | convolution fusion | flops 3568892928 | bytes 19713024 | tf_op jit(solution)/shard_map/dot_general | solution.py:371
  218.6 5.2 convolution_convert_fusion
  223.8 7.3 %multiply_reduce_fusion = (bf16[768]{0:T(1024)(128)(2,1)}, f32[750]{0:T(1024)S(1)}, f32[750]{0:T(1024)S(1)}, bf16[768]{0:T(1024)(128)(2,1)}, f32[750,768]{1,0:T(8,128)S(1)}) fusion(f32[750,768]{1,0:T(8,128)S(1)} %copy-done.13, f32[750]{0:T(1024)S(1)} %add_rsqrt_fusion, f32[750]{0:T(1024)S(1)} %broadcast_multiply_fusion.4, f32[768]{0:T(1024)S(1)} %get-tuple-element.110, ...), kind=kOutput, calls=%fused_computation.74 | convolution fusion | flops 3544124928 | bytes 13952736 | tf_op jit(solution)/shard_map/dot_general | solution.py:375
  231.1 1.8 convert_reduce_fusion.5
  232.9 1.5 copy-done.15
  234.3 1.1 convolution_convert_fusion.2
  235.5 8.0 %pad_maximum_fusion = bf16[768,6912]{1,0:T(8,128)(2,1)} fusion(bf16[768,768]{1,0:T(8,128)(2,1)S(1)} %convolution_convert_fusion.2, bf16[768,3072]{1,0:T(8,128)(2,1)S(1)} %convolution_convert_fusion, bf16[768,3072]{1,0:T(8,128)(2,1)S(1)} %bitcast.170), kind=kLoop, calls=%fused_computation.1 | loop fusion | flops 31850496 | bytes 21233664 | tf_op jit(solution)/shard_map/concatenate | solution.py:384
  243.6 1.6 copy-done.16
  245.1 2.4 convolution_convert_fusion.3
  247.6 27.8 %shard_map.294 = (f32[768,384]{1,0:T(8,128)S(1)}, f32[1536,384]{1,0:T(8,128)S(1)}, f32[1536,384]{1,0:T(8,128)}) custom-call(bf16[768,768]{1,0:T(8,128)(2,1)S(1)} %pad.17.q_ref, bf16[1536,1536]{1,0:T(8,128)(2,1)} %fusion.8.k_ref.v_ref, bf16[1536,1536]{1,0:T(8,128)(2,1)} %fusion.8.k_ref.v_ref, bf16[768,768]{1,0:T(8,128)(2,1)S(1)} %pad.19.do_ref, ...), custom_call_target="tpu_custom_call" | custom-call | tf_op jit(solution)/shard_map/pallas_call | solution.py:175
  275.6 2.5 copy-done.24
  278.2 1.3 fusion.48
  279.9 1.4 collective-permute-start.1
  281.4 27.7 %shard_map.295 = (f32[768,384]{1,0:T(8,128)S(1)}, f32[1536,384]{1,0:T(8,128)S(1)}, f32[1536,384]{1,0:T(8,128)}) custom-call(bf16[768,768]{1,0:T(8,128)(2,1)S(1)} %pad.17.q_ref, bf16[1536,1536]{1,0:T(8,128)(2,1)} %fusion.8.k_ref.v_ref, bf16[1536,1536]{1,0:T(8,128)(2,1)} %fusion.8.k_ref.v_ref, bf16[768,768]{1,0:T(8,128)(2,1)S(1)} %pad.19.do_ref, ...), custom_call_target="tpu_custom_call" | custom-call | tf_op jit(solution)/shard_map/pallas_call | solution.py:175
  309.3 2.3 copy-done.23
  311.8 1.2 fusion.47
  314.1 1.1 reshape.240
  315.2 0.8 stack.96
  316.9 0.8 stack.99
  319.0 1.4 copy-done.4
  321.2 2.0 fusion.46
  323.2 28.3 %collective-permute-done.2 = bf16[750,768]{1,0:T(8,128)(2,1)S(1)} collective-permute-done((bf16[750,768]{1,0:T(8,128)(2,1)}, bf16[750,768]{1,0:T(8,128)(2,1)S(1)}, u32[]{:S(2)}, u32[]{:S(2)}) %collective-permute-start.2) | collective-permute-done | bytes 1152032 | tf_op jit(solution)/shard_map/ppermute | solution.py:401
  352.9 1.1 copy-done.47
  354.3 4.6 fusion.32
  359.5 4.7 fusion.91
  364.3 7.7 %concatenate.48 = bf16[768,2560]{1,0:T(8,128)(2,1)} concatenate(bf16[768,2304]{1,0:T(8,128)(2,1)} %fusion.91, bf16[768,1]{1,0:T(8,128)(2,1)S(1)} %stack.92, bf16[768,1]{1,0:T(8,128)(2,1)S(1)} %stack.93, bf16[768,1]{1,0:T(8,128)(2,1)S(1)} %stack.94, bf16[768,1]{1,0:T(8,128)(2,1)S(1)} %stack.95, bf16[768,1]{1,0:T(8,128)(2,1)S(1)} %copy-done.35, bf16[768,1]{1,0:T(8,128)(2,1)S(1)} %copy-done.36, ...), dimensions={1} | concatenate | bytes 7864320 | tf_op jit(solution)/shard_map/concatenate | solution.py:450
  372.0 27.4 %reduce-scatter.3.cloned.1.call-done = bf16[24,6912]{1,0:T(8,128)(2,1)} async-done(((bf16[768,6912]{1,0:T(8,128)(2,1)}), bf16[24,6912]{1,0:T(8,128)(2,1)}) %reduce-scatter.3.cloned.1.call-update) | async-done | bytes 331792 | tf_op jit(solution)/shard_map/reduce_scatter | solution.py:383
  399.5 1.8 convert_element_type.118
  401.6 8.6 %fusion.50 = bf16[1,750,768]{2,1,0:T(8,128)(2,1)} fusion(f32[750,768]{1,0:T(8,128)S(1)} %copy-done.14, bf16[750,3072]{1,0:T(8,128)(2,1)} %copy-done.62, bf16[3072,768]{1,0:T(8,128)(2,1)} %reshape.236, f32[768]{0:T(1024)S(1)} %copy-done.52), kind=kOutput, calls=%fused_computation.85 | convolution fusion | flops 3540672000 | bytes 12785664 | tf_op jit(solution)/shard_map/dot_general | solution.py:363
  410.3 1.8 fusion.53
  415.2 1.1 multiply_add_fusion
  416.3 0.9 pad_maximum_fusion.4
  417.2 0.9 fusion.73
  418.1 0.9 fusion.77
  419.1 0.9 pad_maximum_fusion.3
  419.9 87.8 %reduce-scatter.5.cloned.1.call-done = bf16[24,2560]{1,0:T(8,128)(2,1)} async-done(((bf16[768,2560]{1,0:T(8,128)(2,1)}), bf16[24,2560]{1,0:T(8,128)(2,1)}) %reduce-scatter.5.cloned.1.call-update) | async-done | bytes 122896 | tf_op jit(solution)/shard_map/reduce_scatter | solution.py:452
  510.7 0.9 convert_element_type.120
  512.4 0.9 fusion.78
  513.4 0.9 fusion.79
  (208 shorter events, 23.4 us)
Async XLA Ops:
  7.2 7.3 %copy-start.9 = (bf16[1,750,768]{2,1,0:T(8,128)(2,1)S(1)}, bf16[1,750,768]{2,1,0:T(8,128)(2,1)}, u32[]{:S(2)}) copy-start(bf16[1,750,768]{2,1,0:T(8,128)(2,1)} %param.14) | copy-start | bytes 3456004
  7.2 68.3 %all-gather.3.cloned.1.call-start = ((), (), s32[]{:S(2)}) async-start(), calls=%async_computation.2 | async-start | bytes 3852288 | tf_op jit(solution)/shard_map/all_gather | solution.py:316
  10.6 154.7 %all-gather.5.cloned.1.call-start = ((), (), s32[]{:S(2)}) async-start(), calls=%async_computation.3 | async-start | bytes 10948608 | tf_op jit(solution)/shard_map/all_gather | solution.py:317
  14.4 385.1 %reduce-scatter.3.cloned.1.call-start = ((), (), s32[]{:S(2)}) async-start(), calls=%async_computation.4 | async-start | bytes 10948608 | tf_op jit(solution)/shard_map/reduce_scatter | solution.py:383
  14.4 31.0 %collective-permute-start = (bf16[1,750,768]{2,1,0:T(8,128)(2,1)S(1)}, bf16[1,750,768]{2,1,0:T(8,128)(2,1)S(1)}, u32[]{:S(2)}, u32[]{:S(2)}) collective-permute-start(bf16[1,750,768]{2,1,0:T(8,128)(2,1)S(1)} %copy-done.9), channel_id=1, source_target_pairs={{0,1},{1,0},{2,3},{3,2},{4,5},{5,4},{6,7},{7,6},{8,9},{9,8},{10,11... | collective-permute-start | bytes 3456008 | tf_op jit(solution)/shard_map/ppermute | solution.py:331
  18.2 61.0 %copy-start.42 = (f32[750]{0:T(1024)}, f32[750]{0:T(1024)S(1)}, u32[]{:S(2)}) copy-start(f32[750]{0:T(1024)S(1)} %add_rsqrt_fusion.2) | copy-start | bytes 9004
  79.2 7.6 %copy-start.53 = (f32[768]{0:T(1024)}, f32[768]{0:T(1024)S(1)}, u32[]{:S(2)}) copy-start(f32[768]{0:T(1024)S(1)} %get-tuple-element.114) | copy-start | bytes 9220
  84.9 1.8 copy-start.11
  84.9 3.4 copy-start.46
  85.0 3.7 copy-start.19
  88.7 2.1 slice-start.2
  93.5 71.7 %copy-start.56 = (f32[768]{0:T(1024)S(1)}, f32[768]{0:T(1024)}, u32[]{:S(2)}) copy-start(f32[768]{0:T(1024)} %get-tuple-element.111) | copy-start | bytes 9220
  174.3 8.5 %copy-start.45 = (f32[3072]{0:T(1024)S(1)}, f32[3072]{0:T(1024)}, u32[]{:S(2)}) copy-start(f32[3072]{0:T(1024)} %add.253) | copy-start | bytes 36868
  182.8 11.5 %copy-start.30 = (bf16[1,750,768]{2,1,0:T(8,128)(2,1)S(1)}, bf16[1,750,768]{2,1,0:T(8,128)(2,1)}, u32[]{:S(2)}) copy-start(bf16[1,750,768]{2,1,0:T(8,128)(2,1)} %param.15) | copy-start | bytes 3456004
  192.3 2.1 copy-start.62
  208.4 10.2 %copy-start.13 = (f32[750,768]{1,0:T(8,128)S(1)}, f32[750,768]{1,0:T(8,128)}, u32[]{:S(2)}) copy-start(f32[750,768]{1,0:T(8,128)} %copy-done.12) | copy-start | bytes 6912004
  208.4 10.2 %copy-start.55 = (f32[768]{0:T(1024)S(1)}, f32[768]{0:T(1024)}, u32[]{:S(2)}) copy-start(f32[768]{0:T(1024)} %get-tuple-element.109) | copy-start | bytes 9220
  218.6 16.9 %slice-start = ((s8[4718592]{0:T(1024)(128)(4,1)}), s8[4194304]{0:T(1024)(128)(4,1)S(1)}, s32[]{:S(2)}) async-start(s8[4718592]{0:T(1024)(128)(4,1)} %bitcast.169), calls=%async_computation.6 | async-start | bytes 8388608
  223.8 11.7 %slice-start.1 = ((s8[4718592]{0:T(1024)(128)(4,1)}), s8[524288]{0:T(1024)(128)(4,1)S(1)}, s32[]{:S(2)}) async-start(s8[4718592]{0:T(1024)(128)(4,1)} %bitcast.169), calls=%async_computation.7 | async-start | bytes 1048576
  243.5 264.3 %reduce-scatter.5.cloned.1.call-start = ((), (), s32[]{:S(2)}) async-start(), calls=%async_computation.5 | async-start | bytes 4055040 | tf_op jit(solution)/shard_map/reduce_scatter | solution.py:452
  275.4 2.6 copy-start.24
  275.6 2.6 copy-start.1
  279.9 39.0 %collective-permute-start.1 = (bf16[750,768]{1,0:T(8,128)(2,1)}, bf16[750,768]{1,0:T(8,128)(2,1)}, u32[]{:S(2)}, u32[]{:S(2)}) collective-permute-start(bf16[750,768]{1,0:T(8,128)(2,1)} %fusion.48), channel_id=1, source_target_pairs={{0,1},{1,0},{2,3},{3,2},{4,5},{5,4},{6,7},{7,6},{8,9},{9,8},{10,11... | collective-permute-start | bytes 3456008 | tf_op jit(solution)/shard_map/ppermute | solution.py:401
  309.1 2.5 copy-start.23
  309.2 2.5 copy-start.5
  311.8 2.3 copy-start.51
  311.8 3.4 copy-start.50
  311.8 4.3 copy-start.59
  311.8 5.1 copy-start.49
  311.8 6.0 %copy-start.58 = (bf16[768]{0:T(1024)(128)(2,1)S(1)}, bf16[768]{0:T(1024)(128)(2,1)}, u32[]{:S(2)}) copy-start(bf16[768]{0:T(1024)(128)(2,1)} %get-tuple-element.106) | copy-start | bytes 4612
  313.5 38.0 %collective-permute-start.2 = (bf16[750,768]{1,0:T(8,128)(2,1)}, bf16[750,768]{1,0:T(8,128)(2,1)S(1)}, u32[]{:S(2)}, u32[]{:S(2)}) collective-permute-start(bf16[750,768]{1,0:T(8,128)(2,1)} %fusion.47), channel_id=1, source_target_pairs={{0,1},{1,0},{2,3},{3,2},{4,5},{5,4},{6,7},{7,6},{8,9},{9,8},{10,11... | collective-permute-start | bytes 3456008 | tf_op jit(solution)/shard_map/ppermute | solution.py:401
  318.7 1.8 copy-start.4
  318.8 2.4 copy-start.2
  319.0 32.5 %copy-start.6 = (f32[1500,384]{1,0:T(8,128)S(1)}, f32[1500,384]{1,0:T(8,128)}, u32[]{:S(2)}) copy-start(f32[1500,384]{1,0:T(8,128)} %copy-done.5) | copy-start | bytes 6912004
  319.0 32.5 %copy-start.8 = (f32[1500,384]{1,0:T(8,128)S(1)}, f32[1500,384]{1,0:T(8,128)}, u32[]{:S(2)}) copy-start(f32[1500,384]{1,0:T(8,128)} %copy-done.7) | copy-start | bytes 6912004
  351.9 2.1 copy-start.47
  352.0 2.3 copy-start.10
  352.0 2.3 copy-start.43
  354.3 5.1 copy-start.54
  359.4 4.8 copy-start.34
  359.4 4.8 copy-start.35
  359.4 4.8 copy-start.36
  359.4 4.8 copy-start.37
  359.5 4.8 copy-start.38
  372.0 29.3 %copy-start.44 = (f32[24,8]{0,1:T(8,128)S(1)}, f32[24,8]{0,1:T(8,128)}, u32[]{:S(2)}) copy-start(f32[24,8]{0,1:T(8,128)} %param.21) | copy-start | bytes 2308
  372.0 29.4 %copy-start.48 = (f32[2,24,8]{1,2,0:T(8,128)S(1)}, f32[2,24,8]{1,2,0:T(8,128)}, u32[]{:S(2)}) copy-start(f32[2,24,8]{1,2,0:T(8,128)} %param.27) | copy-start | bytes 4612
  372.0 29.6 %copy-start.14 = (f32[750,768]{1,0:T(8,128)S(1)}, f32[750,768]{1,0:T(8,128)}, u32[]{:S(2)}) copy-start(f32[750,768]{1,0:T(8,128)} %copy-done.12) | copy-start | bytes 6912004
  372.0 29.6 %copy-start.52 = (f32[768]{0:T(1024)S(1)}, f32[768]{0:T(1024)}, u32[]{:S(2)}) copy-start(f32[768]{0:T(1024)} %get-tuple-element.108) | copy-start | bytes 9220
  401.6 8.7 %copy-start.17 = (f32[750,768]{1,0:T(8,128)S(1)}, f32[750,768]{1,0:T(8,128)}, u32[]{:S(2)}) copy-start(f32[750,768]{1,0:T(8,128)} %copy-done.15) | copy-start | bytes 6912004
  401.6 8.7 %copy-start.22 = (f32[750,768]{1,0:T(8,128)S(1)}, f32[750,768]{1,0:T(8,128)}, u32[]{:S(2)}) copy-start(f32[750,768]{1,0:T(8,128)} %get-tuple-element.146) | copy-start | bytes 6912004
  410.3 1.8 copy-start.20
  410.3 1.8 copy-start.25
  412.1 3.1 copy-start.21
  412.2 5.9 %copy-start.26 = (f32[24,3072]{1,0:T(8,128)}, f32[24,3072]{1,0:T(8,128)S(1)}, u32[]{:S(2)}) copy-start(f32[24,3072]{1,0:T(8,128)S(1)} %get-tuple-element.117) | copy-start | bytes 884740
  412.2 4.9 copy-start.28
  413.8 3.3 copy-start.29
  413.8 4.3 copy-start.41
  414.6 3.6 copy-start.27
  417.2 91.6 %copy-start.57 = (f32[2,96]{1,0:T(2,128)S(1)}, f32[2,96]{1,0:T(2,128)}, u32[]{:S(2)}) copy-start(f32[2,96]{1,0:T(2,128)} %param.26) | copy-start | bytes 2308
  417.2 91.6 %copy-start.61 = (f32[96]{0:T(128)S(1)}, f32[96]{0:T(128)}, u32[]{:S(2)}) copy-start(f32[96]{0:T(128)} %param.20) | copy-start | bytes 1156
  418.1 94.3 %copy-start.31 = (f32[2,24,2304]{2,1,0:T(8,128)S(1)}, f32[2,24,2304]{2,1,0:T(8,128)}, u32[]{:S(2)}) copy-start(f32[2,24,2304]{2,1,0:T(8,128)} %param.22) | copy-start | bytes 1327108
  418.1 95.3 %copy-start.33 = (f32[24,2304]{1,0:T(8,128)S(1)}, f32[24,2304]{1,0:T(8,128)}, u32[]{:S(2)}) copy-start(f32[24,2304]{1,0:T(8,128)} %param.16) | copy-start | bytes 663556
  508.6 7.6 %copy-start.60 = (f32[96]{0:T(128)}, f32[96]{0:T(128)S(1)}, u32[]{:S(2)}) copy-start(f32[96]{0:T(128)S(1)} %reshape.243) | copy-start | bytes 1156
  513.4 2.9 copy-start.32
  (9 other events, 13.9 us)
Sparse Core Ops, SparseCore 0:
  11.5 63.9 all-gather.2
  79.0 86.2 all-gather.4
  243.6 155.8 reduce-scatter.2
  404.7 102.9 reduce-scatter.4

commit v6 on v5

--- a/solution.py
+++ b/solution.py
@@ -1,3 +1,4 @@
+import functools
 import math
 
 import jax
@@ -267,6 +268,59 @@
     return (grad_query, pieces[1], jnp.concatenate([grad_key, grad_value], axis=2))
 
 
+def link_plan(mesh):
+    devices = list(mesh.devices.reshape(-1))
+    bit_count = len(devices).bit_length() - 1
+    core_bit = 1
+    for bit in range(bit_count):
+        first, other = devices[0], devices[1 << bit]
+        if getattr(first, "coords", None) is not None and tuple(first.coords) == tuple(other.coords):
+            core_bit = bit
+    others = [bit for bit in range(bit_count) if bit != core_bit]
+    near, far = others[:-1], others[-1:]
+    rotated = tuple(tuple(near[k:] + near[:k] + far) for k in range(3))
+    inner = [bit for bit in near if bit != 0]
+    late = tuple(tuple(inner[k:] + inner[:k] + [0] + far) for k in range(2))
+    return bit_count, core_bit, rotated, late
+
+
+def tree_reduce_scatter(terms, part_columns, orders, plan_bits, hooks=None):
+    hooks = dict(hooks or {})
+    tied = {}
+    bit_count, core_bit = plan_bits
+    device = lax.axis_index("clip") * lax.axis_size("frame") + lax.axis_index("frame")
+    blocks = 1 << bit_count
+    block_rows = terms.shape[0] // blocks
+    data = terms.reshape((2,) * bit_count + (block_rows, terms.shape[1]))
+    parts = [(data, list(range(bit_count - 1, -1, -1)))]
+    plan = [(core_bit,)] + [tuple(order[stage] for order in orders) for stage in range(len(orders[0]))]
+    for stage, stage_bits in enumerate(plan):
+        if stage == 1:
+            whole, bits = parts[0]
+            parts = []
+            offset = 0
+            for width in part_columns:
+                parts.append((whole[..., offset : offset + width], bits))
+                offset += width
+        keeps, sends = [], []
+        for (part, part_bits), bit in zip(parts, stage_bits):
+            axis = part_bits.index(bit)
+            mine = (device >> bit) & 1
+            keeps.append(lax.dynamic_index_in_dim(part, mine, axis=axis, keepdims=False))
+            sends.append(
+                lax.dynamic_index_in_dim(part, 1 - mine, axis=axis, keepdims=False).astype(jnp.bfloat16)
+            )
+        if stage in hooks:
+            sends, tied[stage] = lax.optimization_barrier((sends, hooks[stage](tied)))
+        new_parts = []
+        for keep, send, (part, part_bits), bit in zip(keeps, sends, parts, stage_bits):
+            pairs = [(index, index ^ (1 << bit)) for index in range(blocks)]
+            got = lax.ppermute(send, ("clip", "frame"), pairs)
+            new_parts.append((keep + got.astype(jnp.float32), [b for b in part_bits if b != bit]))
+        parts = new_parts
+    return jnp.concatenate([part for part, _ in parts], axis=-1).astype(jnp.float32), tied
+
+
 def adam_step(weight, moments, gradient):
     first = beta_first * moments[0] + (1.0 - beta_first) * gradient
     second = beta_second * moments[1] + (1.0 - beta_second) * gradient * gradient
@@ -277,6 +331,7 @@
 
 
 def body(
+    plan,
     inputs,
     cotangent,
     project_in,
@@ -380,25 +435,42 @@
     grad_attended = grad_residual.astype(jnp.bfloat16)
     grad_out_term = jnp.dot(mixed_low.T, grad_attended, preferred_element_type=jnp.float32)
     grad_out_bias = jnp.sum(grad_attended.astype(jnp.float32), axis=0)
-    owned_late = lax.psum_scatter(
-        jnp.concatenate(
-            [grad_shrink_term.reshape(model_width, -1), grad_expand_term, grad_out_term], axis=1
-        ).astype(jnp.bfloat16),
-        everyone,
-        scatter_dimension=0,
-        tiled=True,
-    ).astype(jnp.float32)
+    late_terms = jnp.concatenate(
+        [grad_shrink_term.reshape(model_width, -1), grad_expand_term, grad_out_term], axis=1
+    )
     grad_mixed = jnp.dot(grad_attended, full_out.T, preferred_element_type=jnp.float32).astype(
         jnp.bfloat16
     )
+    def first_backward_half(tied):
+        mixed_grads = tied[0]
+        first = attention_pallas(
+            scaled_queries, pair_rows, mixed_grads, log_totals, 0, model_width // 256
+        )
+        send = jnp.concatenate([first[1], first[2]], axis=1)[row_count:].astype(jnp.bfloat16)
+        return (first, send, mixed_grads)
+
+    bit_count, core_bit, rotated_orders, late_orders = plan
+    owned_late, tied = tree_reduce_scatter(
+        late_terms,
+        (3456, 3456),
+        late_orders,
+        (bit_count, core_bit),
+        {0: lambda tied: grad_mixed, 1: first_backward_half},
+    )
+    first_half, first_send, grad_mixed = tied[1]
     halves = []
     half_pairs = model_width // 256
     for first_pair in (0, half_pairs):
-        grad_query, grad_keys, grad_values = attention_pallas(
-            scaled_queries, pair_rows, grad_mixed, log_totals, first_pair, half_pairs
-        )
+        if first_pair == 0:
+            grad_query, grad_keys, grad_values = first_half
+            send = first_send
+        else:
+            grad_query, grad_keys, grad_values = attention_pallas(
+                scaled_queries, pair_rows, grad_mixed, log_totals, first_pair, half_pairs
+            )
+            send = jnp.concatenate([grad_keys, grad_values], axis=1)[row_count:].astype(jnp.bfloat16)
         terms = jnp.concatenate([grad_keys, grad_values], axis=1)
-        returned = lax.ppermute(terms[row_count:].astype(jnp.bfloat16), "frame", swap)
+        returned = lax.ppermute(send, "frame", swap)
         halves.append((grad_query, terms[:row_count] + returned.astype(jnp.float32)))
     half_width = model_width // 2
     grad_projected = jnp.concatenate(
@@ -442,16 +514,16 @@
         [
             grad_columns,
             grad_bias_term.reshape(model_width, -1),
-            jnp.zeros((model_width, 256 - 12), jnp.float32),
+            jnp.zeros((model_width, 128 - 12), jnp.float32),
         ],
         axis=1,
     )
-    first_terms, owned_late = lax.optimization_barrier(
-        (jnp.concatenate([grad_in_term, small_grads], axis=1), owned_late)
-    )
-    owned_first = lax.psum_scatter(
-        first_terms.astype(jnp.bfloat16), everyone, scatter_dimension=0, tiled=True
-    ).astype(jnp.float32)
+    owned_first = tree_reduce_scatter(
+        jnp.concatenate([grad_in_term, small_grads], axis=1),
+        (896, 768, 768),
+        rotated_orders,
+        (bit_count, core_bit),
+    )[0]
     owned_in = owned_first[:, :wide_in]
     owned_vectors = owned_first[:, wide_in : wide_in + vectors.shape[1]]
     owned_bias = owned_first[:, wide_in + vectors.shape[1] : wide_in + 12].reshape(-1)
@@ -527,4 +599,10 @@
         P(None, ("clip", "frame")),
         P(None, ("clip", "frame"), None),
     )
-    return jax.shard_map(body, mesh=mesh, in_specs=in_specs, out_specs=out_specs, check_vma=False)
+    return jax.shard_map(
+        functools.partial(body, link_plan(mesh)),
+        mesh=mesh,
+        in_specs=in_specs,
+        out_specs=out_specs,
+        check_vma=False,
+    )

time: 528 us -> 526 us (level)
  waiting for transfers between devices: 236 us -> 149 us
  local copies, waits for them, and re-layouts: 65.9 us -> 97.4 us
  other arithmetic: 42 us -> 71.3 us
  starting transfers between devices: 5.23 us -> 30 us
    reduce_scatter x2 -> x0, waiting for transfers between devices: 115 us -> none  [the longest x1 87.8 us: body(): lax.psum_scatter(first_terms.astype(jnp.bfloat16), everyone, scatter_dime...]
    ppermute x2 -> x24, waiting for transfers between devices: 28.3 us -> 57 us  [the longest x22 46 us: tree_reduce_scatter(): got = lax.ppermute(send, ('clip', 'frame'), pairs)]
    ppermute x2 -> x24, starting transfers between devices: 2.03 us -> 26.9 us  [the longest x22 24.8 us: tree_reduce_scatter(): got = lax.ppermute(send, ('clip', 'frame'), pairs)]
    add x0 -> x22, other arithmetic: none -> 17.5 us  [tree_reduce_scatter(): keep + got.astype(jnp.float32)]
    convert_element_type x0 -> x22, local copies, waits for them, and re-layouts: none -> 14.4 us  [tree_reduce_scatter(): lax.dynamic_index_in_dim(part, 1 - mine, axis=axis, keepdims=False)]
    concatenate x1 -> x10, local copies, waits for them, and re-layouts: 7.73 us -> 19.4 us  [body(): jnp.concatenate([grad_in_term, small_grads], axis=1)]
    concatenate x0 -> x1, local copies, waits for them, and re-layouts: none -> 11.5 us  [body(): jnp.concatenate([grad_shrink_term.reshape(model_width, -1), grad_expand_t...]
    reshape x2 -> x0, local copies, waits for them, and re-layouts: 9.57 us -> none  [the longest x1 8.46 us: body(): grad_shrink_term.reshape(model_width, -1)]
  transfers between devices with their start and end apart: 7 -> 27, of which waited for: 6 -> 17; matrix products, arithmetic and copies ran while one was open for 13% -> 20% of each run, Pallas kernels for 17% -> 17%
where the time goes in v6:
time: 526 us; the launch traced here: 521 us
  waiting for transfers between devices  149 us (28%)
  local copies, waits for them, and re-layouts  97.4 us (19%)
  Pallas kernels  89.4 us (17%)
  other arithmetic  71.3 us (14%)
  matrix products  68.4 us (13%)
  starting transfers between devices  30 us (6%)
  between operations  15.4 us (3%)
    pallas_call x2, Pallas kernels, attention_pallas(): pl.pallas_call(attention_backward_kernel, grid=(span,), in_specs=[qi_spec...  55.1 us
    ppermute x22, waiting for transfers between devices, tree_reduce_scatter(): got = lax.ppermute(send, ('clip', 'frame'), pairs)  46 us
    all_gather x1, waiting for transfers between devices, body(): second_full = lax.all_gather(second_pack, everyone, axis=0, tiled=True)  36.1 us
    pallas_call x1, Pallas kernels, attention_pallas(): pl.pallas_call(attention_forward_kernel, grid=(pair_count,), in_specs=[q_...  34.3 us
    all_gather x1, waiting for transfers between devices, body(): first_full = lax.all_gather(first_pack, everyone, axis=0, tiled=True)  28.8 us
    ppermute x1, waiting for transfers between devices, body(): lax.ppermute(inputs, 'frame', swap).reshape(row_count, model_width)  27.2 us
    ppermute x22, starting transfers between devices, tree_reduce_scatter(): got = lax.ppermute(send, ('clip', 'frame'), pairs)  24.8 us
    concatenate x10, local copies, waits for them, and re-layouts, body(): jnp.concatenate([grad_in_term, small_grads], axis=1)  19.4 us
  transfers between devices with their start and end apart: 27, of which 17 were waited for; matrix products, arithmetic and copies ran while one was open for 20% of the time, Pallas kernels for 17%

profile of v6, /device:TPU:0, one launch (start us, length us, event | category | flops | bytes accessed | tf_op | source)
XLA Modules:
  0.0 521.0 jit_solution(6395477919208574375)
XLA Ops:
  14.4 3.0 collective-permute-start
  18.2 27.2 %collective-permute-done = bf16[1,750,768]{2,1,0:T(8,128)(2,1)S(1)} collective-permute-done((bf16[1,750,768]{2,1,0:T(8,128)(2,1)S(1)}, bf16[1,750,768]{2,1,0:T(8,128)(2,1)S(1)}, u32[]{:S(2)}, u32[]{:S(2)}) %collective-permute-start) | collective-permute-done | bytes 1152032 | tf_op jit(solution)/shard_map/ppermute | solution.py:386
  46.7 28.8 %all-gather.3.cloned.1.call-done = bf16[768,2432]{1,0:T(8,128)(2,1)} async-done(((bf16[24,2432]{1,0:T(8,128)(2,1)}), bf16[768,2432]{1,0:T(8,128)(2,1)}) %all-gather.3.cloned.1.call-update) | async-done | bytes 3735568 | tf_op jit(solution)/shard_map/all_gather | solution.py:371
  76.8 2.0 slice_reduce_fusion
  78.9 6.0 %add_convert_fusion = bf16[750,2304]{1,0:T(8,128)(2,1)S(1)} fusion(f32[2304]{0:T(1024)S(1)} %pad_maximum_fusion.12, bf16[768,2432]{1,0:T(8,128)(2,1)} %all-gather.3.cloned.1.call-done, bf16[1,750,768]{2,1,0:T(8,128)(2,1)S(1)} %copy-done.11, f32[768]{0:T(1024)S(1)} %get-tuple-element.128, f32[768]{0:T(1024)S(1)} %get-tuple-element.129, ...), kind=kOutput, calls=%fused_computation.18 | convolution fusion | flops 2661120000 | bytes 8168304 | tf_op jit(solution)/shard_map/dot_general | solution.py:394
  85.1 1.6 copy-done.14
  86.8 1.6 copy-done.44
  88.7 2.1 add_convert_fusion.1
  90.8 2.7 fusion.10.k_ref.v_ref
  93.5 34.3 %shard_map.293 = (bf16[768,768]{1,0:T(8,128)(2,1)S(1)}, f32[768,768]{1,0:T(8,128)S(1)}) custom-call(bf16[768,768]{1,0:T(8,128)(2,1)S(1)} %pad.19.q_ref, bf16[1536,1536]{1,0:T(8,128)(2,1)} %fusion.10.k_ref.v_ref, bf16[1536,1536]{1,0:T(8,128)(2,1)} %fusion.10.k_ref.v_ref, f32[1,1536]{1,0:T(1,128)S(1)} %compare_select_fusion.kbias_ref), custom_call_target="tpu_custom_call" | custom-call | tf_op jit(solution)/shard_map/pallas_call | solution.py:157
  129.3 36.1 %all-gather.5.cloned.1.call-done = bf16[768,6912]{1,0:T(8,128)(2,1)} async-done(((bf16[24,6912]{1,0:T(8,128)(2,1)}), bf16[768,6912]{1,0:T(8,128)(2,1)}) %all-gather.5.cloned.1.call-update) | async-done | bytes 10616848 | tf_op jit(solution)/shard_map/all_gather | solution.py:372
  165.4 2.5 fusion.123
  169.7 4.9 slice.277
  174.5 8.6 %reshape.292 = bf16[3072,768]{1,0:T(8,128)(2,1)} reshape(bf16[768,3072]{1,0:T(8,128)(2,1)} %slice.277) | data formatting | bytes 9437184 | tf_op jit(solution)/shard_map/reshape | solution.py:379
  183.2 7.8 %multiply_convert_fusion = (bf16[750,3072]{1,0:T(8,128)(2,1)S(1)}, f32[750,3072]{1,0:T(8,128)S(1)}) fusion(f32[3072]{0:T(1024)S(1)} %add.407, bf16[768,6912]{1,0:T(8,128)(2,1)} %all-gather.5.cloned.1.call-done, f32[750,768]{1,0:T(8,128)} %copy-done.4, f32[768]{0:T(1024)S(1)} %get-tuple-element.123, f32[768]{0:T(1024)S(1)} %get-tuple-element.124, ...), kind=kOutput, calls=%fused_computation.15 | convolution fusion | flops 3555648000 | bytes 20877168 | tf_op jit(solution)/shard_map/dot_general | solution.py:414
  191.0 8.2 %convert_reduce_fusion = (f32[3072]{0:T(1024)}, bf16[750,3072]{1,0:T(8,128)(2,1)S(1)}) fusion(f32[750,3072]{1,0:T(8,128)S(1)} %get-tuple-element.166, f32[3072]{0:T(1024)S(1)} %add.407, bf16[3072,768]{1,0:T(8,128)(2,1)S(1)} %copy-done.19, bf16[1,750,768]{2,1,0:T(8,128)(2,1)S(1)} %copy-done.27), kind=kOutput, calls=%fused_computation.14 | convolution fusion | flops 3568892928 | bytes 19719168 | tf_op jit(solution)/shard_map/dot_general | solution.py:426
  199.3 7.0 %fusion.118 = f32[768,3072]{1,0:T(8,128)} fusion(bf16[750,3072]{1,0:T(8,128)(2,1)S(1)} %get-tuple-element.169, f32[750,768]{1,0:T(8,128)S(1)} %copy-done.5, f32[768]{0:T(1024)S(1)} %get-tuple-element.123, f32[768]{0:T(1024)S(1)} %get-tuple-element.124, f32[750]{0:T(1024)S(1)} %add_rsqrt_fusion, f32[750]{0:T(1024)S(1)} %broadcast_multiply_fusion.4), kind=kOutput, calls=%fused_computation.256 | convolution fusion | flops 3541824000 | bytes 16361328 | tf_op jit(solution)/shard_map/dot_general | solution.py:428
  206.2 7.3 %multiply_reduce_fusion = (f32[768]{0:T(1024)}, f32[750]{0:T(1024)S(1)}, f32[750]{0:T(1024)S(1)}, f32[768]{0:T(1024)}, f32[750,768]{1,0:T(8,128)S(1)}) fusion(f32[750,768]{1,0:T(8,128)S(1)} %copy-done.5, f32[750]{0:T(1024)S(1)} %add_rsqrt_fusion, f32[750]{0:T(1024)S(1)} %broadcast_multiply_fusion.4, f32[768]{0:T(1024)S(1)} %get-tuple-element.124, ...), kind=kOutput, calls=%fused_computation.80 | convolution fusion | flops 3544124928 | bytes 13955808 | tf_op jit(solution)/shard_map/dot_general | solution.py:430
  213.6 1.8 convert_reduce_fusion.5
  215.3 2.6 fusion.68
  217.9 6.6 %fusion.59 = f32[3072,768]{1,0:T(8,128)} fusion(bf16[750,3072]{1,0:T(8,128)(2,1)S(1)} %get-tuple-element.165, bf16[1,750,768]{2,1,0:T(8,128)(2,1)S(1)} %copy-done.27), kind=kOutput, calls=%fused_computation.102 | convolution fusion | flops 3538944000 | bytes 15197184 | tf_op jit(solution)/shard_map/dot_general | solution.py:424
  224.6 11.5 %concatenate.80 = f32[2,2,2,2,2,24,3072]{6,5,4,3,2,1,0:T(8,128)} reshape(f32[3072,768]{1,0:T(8,128)} %fusion.59) | data formatting | bytes 18874368 | tf_op jit(solution)/shard_map/concatenate | solution.py:438
  236.0 15.2 %pad_maximum_fusion = f32[2,2,2,2,2,24,6912]{6,5,4,3,2,1,0:T(8,128)} fusion(f32[2,2,2,2,2,24,768]{6,5,4,3,2,1,0:T(8,128)} %bitcast.275, f32[2,2,2,2,2,24,3072]{6,5,4,3,2,1,0:T(8,128)} %bitcast.270, f32[2,2,2,2,2,24,3072]{6,5,4,3,2,1,0:T(8,128)} %concatenate.80), kind=kLoop, calls=%fused_computation | loop fusion | flops 10616832 | bytes 42467328 | tf_op jit(solution)/shard_map/concatenate | solution.py:438
  251.2 7.0 %fusion.9 = bf16[2,2,2,2,24,6912]{5,4,0,3,2,1:T(8,128)(2,1)} fusion(f32[2,2,2,2,2,24,6912]{6,5,4,3,2,1,0:T(8,128)} %pad_maximum_fusion, s32[]{:T(128)S(6)} %select_n.100), kind=kLoop, calls=%fused_computation.19 | loop fusion | bytes 10616836 | tf_op jit(solution)/shard_map/convert_element_type | solution.py:311
  258.2 2.4 convolution_convert_fusion
  261.9 27.3 %shard_map.294 = (f32[768,384]{1,0:T(8,128)S(1)}, f32[1536,384]{1,0:T(8,128)S(1)}, f32[1536,384]{1,0:T(8,128)}) custom-call(bf16[768,768]{1,0:T(8,128)(2,1)S(1)} %pad.19.q_ref, bf16[1536,1536]{1,0:T(8,128)(2,1)} %fusion.10.k_ref.v_ref, bf16[1536,1536]{1,0:T(8,128)(2,1)} %fusion.10.k_ref.v_ref, bf16[768,768]{1,0:T(8,128)(2,1)S(1)} %pad.21.do_ref, ...), custom_call_target="tpu_custom_call" | custom-call | tf_op jit(solution)/shard_map/pallas_call | solution.py:176
  289.3 1.6 slice.226
  291.9 1.5 slice.227
  295.8 10.7 %fusion = f32[2,2,2,2,24,6912]{5,4,0,3,2,1:T(8,128)} fusion(bf16[2,2,2,2,24,6912]{5,4,0,3,2,1:T(8,128)(2,1)} %collective-permute-done.1, f32[2,2,2,2,2,24,6912]{6,5,4,3,2,1,0:T(8,128)} %pad_maximum_fusion, s32[]{:T(128)S(6)} %select_n.99), kind=kLoop, calls=%fused_computation.4 | loop fusion | flops 5308416 | bytes 26542084 | tf_op jit(solution)/shard_map/add | solution.py:319
  306.5 4.9 fusion.119
  312.8 1.7 fusion.54
  316.1 27.8 %shard_map.295 = (f32[768,384]{1,0:T(8,128)S(1)}, f32[1536,384]{1,0:T(8,128)S(1)}, f32[1536,384]{1,0:T(8,128)}) custom-call(bf16[768,768]{1,0:T(8,128)(2,1)S(1)} %pad.19.q_ref, bf16[1536,1536]{1,0:T(8,128)(2,1)} %fusion.10.k_ref.v_ref, bf16[1536,1536]{1,0:T(8,128)(2,1)} %fusion.10.k_ref.v_ref, bf16[768,768]{1,0:T(8,128)(2,1)S(1)} %pad.22.do_ref, ...), custom_call_target="tpu_custom_call" | custom-call | tf_op jit(solution)/shard_map/pallas_call | solution.py:176
  344.2 2.7 slice.233
  351.2 4.7 fusion.53
  363.6 1.7 fusion.50
  365.4 11.0 %collective-permute-done.3 = bf16[750,768]{1,0:T(8,128)(2,1)} collective-permute-done((bf16[750,768]{1,0:T(8,128)(2,1)}, bf16[750,768]{1,0:T(8,128)(2,1)}, u32[]{:S(2)}, u32[]{:S(2)}) %collective-permute-start.3) | collective-permute-done | bytes 1152032 | tf_op jit(solution)/shard_map/ppermute | solution.py:473
  376.4 1.6 fusion.47
  378.8 2.6 copy-done.45
  381.4 2.9 fusion.17
  384.4 2.2 fusion.36
  386.6 2.6 copy.68
  389.2 8.2 %fusion.15 = f32[2,2,2,2,2,24,2304]{6,5,4,3,2,1,0:T(8,128)} fusion(bf16[2,2,2,2,2,24,750]{6,5,4,3,2,1,0:T(8,128)(2,1)} %bitcast.278, bf16[750,2304]{1,0:T(8,128)(2,1)} %copy-done.17), kind=kOutput, calls=%fused_computation.30 | convolution fusion | flops 2654208000 | bytes 11685888 | tf_op jit(solution)/shard_map/dot_general | solution.py:491
  402.2 10.1 %concatenate.98 = f32[2,2,2,2,2,24,2432]{6,5,4,3,2,1,0:T(8,128)} concatenate(f32[2,2,2,2,2,24,2304]{6,5,4,3,2,1,0:T(8,128)} %fusion.15, f32[2,2,2,2,2,24,1]{6,5,4,3,2,1,0:T(8,128)} %concatenate.102, f32[2,2,2,2,2,24,1]{6,5,4,3,2,1,0:T(8,128)} %concatenate.103, f32[2,2,2,2,2,24,1]{6,5,4,3,2,1,0:T(8,128)} %concatenate.104, f32[2,2,2,2,2,24,1]{6,5,4,3,2,1,0:T(8,128)} %concatenate.105, ...), dimensions={6} | concatenate | bytes 14942208 | tf_op jit(solution)/shard_map/concatenate | solution.py:522
  412.3 3.6 fusion.52
  416.0 1.8 fusion.58
  417.9 2.5 bitcast_add_fusion.2
  421.4 1.6 bitcast_add_fusion.1
  424.5 13.4 %collective-permute-done.18 = bf16[2,2,24,3456]{3,2,0,1:T(8,128)(2,1)S(1)} collective-permute-done((bf16[2,2,24,3456]{3,2,0,1:T(8,128)(2,1)S(1)}, bf16[2,2,24,3456]{3,2,0,1:T(8,128)(2,1)S(1)}, u32[]{:S(2)}, u32[]{:S(2)}) %collective-permute-start.18) | collective-permute-done | bytes 663584 | tf_op jit(solution)/shard_map/ppermute | solution.py:318
  441.6 7.2 %collective-permute-done.19 = bf16[2,24,3456]{2,1,0:T(8,128)(2,1)S(1)} collective-permute-done((bf16[2,24,3456]{2,1,0:T(8,128)(2,1)S(1)}, bf16[2,24,3456]{2,1,0:T(8,128)(2,1)S(1)}, u32[]{:S(2)}, u32[]{:S(2)}) %collective-permute-start.19) | collective-permute-done | bytes 331808 | tf_op jit(solution)/shard_map/ppermute | solution.py:318
  448.9 1.8 collective-permute-start.20
  450.8 3.9 collective-permute-done.23
  454.7 1.8 collective-permute-start.24
  457.2 7.1 %collective-permute-done.24 = bf16[24,3456]{1,0:T(8,128)(2,1)S(1)} collective-permute-done((bf16[24,3456]{1,0:T(8,128)(2,1)S(1)}, bf16[24,3456]{1,0:T(8,128)(2,1)S(1)}, u32[]{:S(2)}, u32[]{:S(2)}) %collective-permute-start.24) | collective-permute-done | bytes 165920 | tf_op jit(solution)/shard_map/ppermute | solution.py:318
  465.3 1.8 reshape.296
  467.1 1.8 reshape.298
  472.7 2.2 fusion.87
  474.9 2.0 fusion.99
  477.7 1.8 bitcast_add_fusion
  483.0 5.2 %collective-permute-done.13 = bf16[2,2,2,24,768]{4,3,2,1,0:T(8,128)(2,1)S(1)} collective-permute-done((bf16[2,2,2,24,768]{4,3,2,1,0:T(8,128)(2,1)S(1)}, bf16[2,2,2,24,768]{4,3,2,1,0:T(8,128)(2,1)S(1)}, u32[]{:S(2)}, u32[]{:S(2)}) %collective-permute-start.13) | collective-permute-done | bytes 294944 | tf_op jit(solution)/shard_map/ppermute | solution.py:318
  489.4 1.6 collective-permute-start.10
  496.4 2.5 collective-permute-done.15
  498.9 1.9 collective-permute-start.16
  502.0 1.8 collective-permute-start.7
  510.4 1.8 collective-permute-done.8
  (296 shorter events, 71.9 us)
Async XLA Ops:
  7.2 7.2 %copy-start.11 = (bf16[1,750,768]{2,1,0:T(8,128)(2,1)S(1)}, bf16[1,750,768]{2,1,0:T(8,128)(2,1)}, u32[]{:S(2)}) copy-start(bf16[1,750,768]{2,1,0:T(8,128)(2,1)} %param.14) | copy-start | bytes 3456004
  7.2 68.3 %all-gather.3.cloned.1.call-start = ((), (), s32[]{:S(2)}) async-start(), calls=%async_computation | async-start | bytes 3852288 | tf_op jit(solution)/shard_map/all_gather | solution.py:371
  10.6 154.8 %all-gather.5.cloned.1.call-start = ((), (), s32[]{:S(2)}) async-start(), calls=%async_computation.1 | async-start | bytes 10948608 | tf_op jit(solution)/shard_map/all_gather | solution.py:372
  14.4 31.0 %collective-permute-start = (bf16[1,750,768]{2,1,0:T(8,128)(2,1)S(1)}, bf16[1,750,768]{2,1,0:T(8,128)(2,1)S(1)}, u32[]{:S(2)}, u32[]{:S(2)}) collective-permute-start(bf16[1,750,768]{2,1,0:T(8,128)(2,1)S(1)} %copy-done.11), channel_id=1, source_target_pairs={{0,1},{1,0},{2,3},{3,2},{4,5},{5,4},{6,7},{7,6},{8,9},{9,8},{10,11... | collective-permute-start | bytes 3456008 | tf_op jit(solution)/shard_map/ppermute | solution.py:386
  18.2 60.7 %copy-start.37 = (f32[750]{0:T(1024)}, f32[750]{0:T(1024)S(1)}, u32[]{:S(2)}) copy-start(f32[750]{0:T(1024)S(1)} %add_rsqrt_fusion.2) | copy-start | bytes 9004
  78.8 7.9 %copy-start.35 = (f32[768]{0:T(1024)}, f32[768]{0:T(1024)S(1)}, u32[]{:S(2)}) copy-start(f32[768]{0:T(1024)S(1)} %get-tuple-element.129) | copy-start | bytes 9220
  78.8 7.9 %copy-start.40 = (f32[768]{0:T(1024)}, f32[768]{0:T(1024)S(1)}, u32[]{:S(2)}) copy-start(f32[768]{0:T(1024)S(1)} %get-tuple-element.128) | copy-start | bytes 9220
  93.5 71.9 %copy-start.50 = (f32[768]{0:T(1024)S(1)}, f32[768]{0:T(1024)}, u32[]{:S(2)}) copy-start(f32[768]{0:T(1024)} %get-tuple-element.125) | copy-start | bytes 9220
  183.2 7.9 %copy-start.19 = (bf16[3072,768]{1,0:T(8,128)(2,1)S(1)}, bf16[3072,768]{1,0:T(8,128)(2,1)}, u32[]{:S(2)}) copy-start(bf16[3072,768]{1,0:T(8,128)(2,1)} %reshape.292) | copy-start | bytes 14155780
  183.2 7.9 %copy-start.27 = (bf16[1,750,768]{2,1,0:T(8,128)(2,1)S(1)}, bf16[1,750,768]{2,1,0:T(8,128)(2,1)}, u32[]{:S(2)}) copy-start(bf16[1,750,768]{2,1,0:T(8,128)(2,1)} %param.15) | copy-start | bytes 3456004
  191.0 26.9 %copy-start.55 = (bf16[750,3072]{1,0:T(8,128)(2,1)}, bf16[750,3072]{1,0:T(8,128)(2,1)S(1)}, u32[]{:S(2)}) copy-start(bf16[750,3072]{1,0:T(8,128)(2,1)S(1)} %get-tuple-element.165) | copy-start | bytes 13824004
  191.0 8.3 %copy-start.5 = (f32[750,768]{1,0:T(8,128)S(1)}, f32[750,768]{1,0:T(8,128)}, u32[]{:S(2)}) copy-start(f32[750,768]{1,0:T(8,128)} %copy-done.4) | copy-start | bytes 6912004
  251.2 7.0 %copy-start.2 = (f32[750,768]{1,0:T(8,128)S(1)}, f32[750,768]{1,0:T(8,128)}, u32[]{:S(2)}) copy-start(f32[750,768]{1,0:T(8,128)} %copy-done.1) | copy-start | bytes 6912004
  260.6 35.1 %collective-permute-start.1 = (bf16[2,2,2,2,24,6912]{5,4,0,3,2,1:T(8,128)(2,1)}, bf16[2,2,2,2,24,6912]{5,4,0,3,2,1:T(8,128)(2,1)}, u32[]{:S(2)}, u32[]{:S(2)}) collective-permute-start(bf16[2,2,2,2,24,6912]{5,4,0,3,2,1:T(8,128)(2,1)} %fusion.9), channel_id=1, source_target_pairs={{0,2},{1,3},{2,0},{3,1},{4,6},{5,7},{6,4},{7,5},{8,10},{9,11},{10,... | collective-permute-start | bytes 15925256 | tf_op jit(solution)/shard_map/ppermute | solution.py:318
  311.4 32.6 %copy-start.13 = (f32[2,2,2,2,24,3456]{5,4,0,3,2,1:T(8,128)}, f32[2,2,2,2,24,3456]{5,4,0,3,2,1:T(8,128)S(1)}, u32[]{:S(2)}) copy-start(f32[2,2,2,2,24,3456]{5,4,0,3,2,1:T(8,128)S(1)} %get-tuple-element.138) | copy-start | bytes 15925252
  314.5 48.9 %collective-permute-start.2 = (bf16[750,768]{1,0:T(8,128)(2,1)}, bf16[750,768]{1,0:T(8,128)(2,1)}, u32[]{:S(2)}, u32[]{:S(2)}) collective-permute-start(bf16[750,768]{1,0:T(8,128)(2,1)} %pad_maximum_fusion.3), channel_id=1, source_target_pairs={{0,1},{1,0},{2,3},{3,2},{4,5},{5,4},{6,7},{7,6},{8,9},{9,8},{10,11... | collective-permute-start | bytes 3456008 | tf_op jit(solution)/shard_map/ppermute | solution.py:473
  316.1 33.2 %slice-start.7 = ((s8[4620288]{0:T(1024)(128)(4,1)}), s8[425984]{0:T(1024)(128)(4,1)S(1)}, s32[]{:S(2)}) async-start(s8[4620288]{0:T(1024)(128)(4,1)} %bitcast.279), calls=%async_computation.9 | async-start | bytes 851968
  344.0 5.3 %slice-start.5 = ((s8[4718592]{0:T(1024)(128)(4,1)}), s8[4194304]{0:T(1024)(128)(4,1)S(1)}, s32[]{:S(2)}) async-start(s8[4718592]{0:T(1024)(128)(4,1)} %bitcast.276), calls=%async_computation.7 | async-start | bytes 8388608
  344.0 6.2 %slice-start.8 = ((s8[4620288]{0:T(1024)(128)(4,1)}), s8[4194304]{0:T(1024)(128)(4,1)S(1)}, s32[]{:S(2)}) async-start(s8[4620288]{0:T(1024)(128)(4,1)} %bitcast.279), calls=%async_computation.10 | async-start | bytes 8388608
  344.1 6.1 %slice-start.6 = ((s8[4718592]{0:T(1024)(128)(4,1)}), s8[524288]{0:T(1024)(128)(4,1)S(1)}, s32[]{:S(2)}) async-start(s8[4718592]{0:T(1024)(128)(4,1)} %bitcast.276), calls=%async_computation.8 | async-start | bytes 1048576
  348.7 27.7 %collective-permute-start.3 = (bf16[750,768]{1,0:T(8,128)(2,1)}, bf16[750,768]{1,0:T(8,128)(2,1)}, u32[]{:S(2)}, u32[]{:S(2)}) collective-permute-start(bf16[750,768]{1,0:T(8,128)(2,1)} %fusion.48), channel_id=1, source_target_pairs={{0,1},{1,0},{2,3},{3,2},{4,5},{5,4},{6,7},{7,6},{8,9},{9,8},{10,11... | collective-permute-start | bytes 3456008 | tf_op jit(solution)/shard_map/ppermute | solution.py:473
  351.2 5.9 %copy-start.39 = (f32[768]{0:T(1024)S(1)}, f32[768]{0:T(1024)}, u32[]{:S(2)}) copy-start(f32[768]{0:T(1024)} %get-tuple-element.136) | copy-start | bytes 9220
  351.2 7.0 %copy-start.49 = (f32[768]{0:T(1024)S(1)}, f32[768]{0:T(1024)}, u32[]{:S(2)}) copy-start(f32[768]{0:T(1024)} %get-tuple-element.114) | copy-start | bytes 9220
  351.2 9.0 %copy-start.48 = (f32[768]{0:T(1024)S(1)}, f32[768]{0:T(1024)}, u32[]{:S(2)}) copy-start(f32[768]{0:T(1024)} %get-tuple-element.120) | copy-start | bytes 9220
  356.0 7.3 %copy-start.22 = (f32[750,384]{1,0:T(8,128)S(1)}, f32[750,384]{1,0:T(8,128)}, u32[]{:S(2)}) copy-start(f32[750,384]{1,0:T(8,128)} %slice.225) | copy-start | bytes 3456004
  361.3 56.5 %collective-permute-start.17 = (bf16[2,2,2,24,3456]{4,3,0,2,1:T(8,128)(2,1)}, bf16[2,2,2,24,3456]{4,3,0,2,1:T(8,128)(2,1)}, u32[]{:S(2)}, u32[]{:S(2)}) collective-permute-start(bf16[2,2,2,24,3456]{4,3,0,2,1:T(8,128)(2,1)} %fusion.55), channel_id=1, source_target_pairs={{0,8},{1,9},{2,10},{3,11},{4,12},{5,13},{6,14},{7,15},{8,0},{9,1},... | collective-permute-start | bytes 3981320 | tf_op jit(solution)/shard_map/ppermute | solution.py:318
  362.6 58.8 %collective-permute-start.21 = (bf16[2,2,2,24,3456]{4,3,0,2,1:T(8,128)(2,1)}, bf16[2,2,2,24,3456]{4,3,0,2,1:T(8,128)(2,1)}, u32[]{:S(2)}, u32[]{:S(2)}) collective-permute-start(bf16[2,2,2,24,3456]{4,3,0,2,1:T(8,128)(2,1)} %fusion.54), channel_id=1, source_target_pairs={{0,4},{1,5},{2,6},{3,7},{4,0},{5,1},{6,2},{7,3},{8,12},{9,13},{10,... | collective-permute-start | bytes 3981320 | tf_op jit(solution)/shard_map/ppermute | solution.py:318
  363.4 12.9 %copy-start.8 = (f32[1500,384]{1,0:T(8,128)S(1)}, f32[1500,384]{1,0:T(8,128)}, u32[]{:S(2)}) copy-start(f32[1500,384]{1,0:T(8,128)} %copy-done.7) | copy-start | bytes 6912004
  363.4 12.9 %copy-start.10 = (f32[1500,384]{1,0:T(8,128)S(1)}, f32[1500,384]{1,0:T(8,128)}, u32[]{:S(2)}) copy-start(f32[1500,384]{1,0:T(8,128)} %copy-done.9) | copy-start | bytes 6912004
  378.2 6.1 %copy-start.17 = (bf16[750,2304]{1,0:T(8,128)(2,1)}, bf16[750,2304]{1,0:T(8,128)(2,1)S(1)}, u32[]{:S(2)}) copy-start(bf16[750,2304]{1,0:T(8,128)(2,1)S(1)} %slice_dynamic-update-slice_fusion) | copy-start | bytes 10368004
  416.0 61.7 %collective-permute-start.4 = (bf16[2,2,2,2,24,2432]{5,4,3,2,1,0:T(8,128)(2,1)}, bf16[2,2,2,2,24,2432]{5,4,3,2,1,0:T(8,128)(2,1)}, u32[]{:S(2)}, u32[]{:S(2)}) collective-permute-start(bf16[2,2,2,2,24,2432]{5,4,3,2,1,0:T(8,128)(2,1)} %fusion.52), channel_id=1, source_target_pairs={{0,2},{1,3},{2,0},{3,1},{4,6},{5,7},{6,4},{7,5},{8,10},{9,11},{10,... | collective-permute-start | bytes 5603336 | tf_op jit(solution)/shard_map/ppermute | solution.py:318
  416.0 5.4 %slice-start.2 = ((s8[5308416]{0:T(1024)(128)(4,1)}), s8[1114112]{0:T(1024)(128)(4,1)S(1)}, s32[]{:S(2)}) async-start(s8[5308416]{0:T(1024)(128)(4,1)} %bitcast.273), calls=%async_computation.4 | async-start | bytes 2228224
  420.5 17.4 %collective-permute-start.18 = (bf16[2,2,24,3456]{3,2,0,1:T(8,128)(2,1)S(1)}, bf16[2,2,24,3456]{3,2,0,1:T(8,128)(2,1)S(1)}, u32[]{:S(2)}, u32[]{:S(2)}) collective-permute-start(bf16[2,2,24,3456]{3,2,0,1:T(8,128)(2,1)S(1)} %fusion.71), channel_id=1, source_target_pairs={{0,4},{1,5},{2,6},{3,7},{4,0},{5,1},{6,2},{7,3},{8,12},{9,13},{10,... | collective-permute-start | bytes 1990664 | tf_op jit(solution)/shard_map/ppermute | solution.py:318
  423.1 17.2 %collective-permute-start.22 = (bf16[2,2,24,3456]{3,2,0,1:T(8,128)(2,1)S(1)}, bf16[2,2,24,3456]{3,2,0,1:T(8,128)(2,1)S(1)}, u32[]{:S(2)}, u32[]{:S(2)}) collective-permute-start(bf16[2,2,24,3456]{3,2,0,1:T(8,128)(2,1)S(1)} %fusion.72), channel_id=1, source_target_pairs={{0,8},{1,9},{2,10},{3,11},{4,12},{5,13},{6,14},{7,15},{8,0},{9,1},... | collective-permute-start | bytes 1990664 | tf_op jit(solution)/shard_map/ppermute | solution.py:318
  438.0 10.8 %collective-permute-start.19 = (bf16[2,24,3456]{2,1,0:T(8,128)(2,1)S(1)}, bf16[2,24,3456]{2,1,0:T(8,128)(2,1)S(1)}, u32[]{:S(2)}, u32[]{:S(2)}) collective-permute-start(bf16[2,24,3456]{2,1,0:T(8,128)(2,1)S(1)} %fusion.74), channel_id=1, source_target_pairs={{0,1},{1,0},{2,3},{3,2},{4,5},{5,4},{6,7},{7,6},{8,9},{9,8},{10,11... | collective-permute-start | bytes 995336 | tf_op jit(solution)/shard_map/ppermute | solution.py:318
  440.5 14.1 %collective-permute-start.23 = (bf16[2,24,3456]{2,1,0:T(8,128)(2,1)S(1)}, bf16[2,24,3456]{2,1,0:T(8,128)(2,1)S(1)}, u32[]{:S(2)}, u32[]{:S(2)}) collective-permute-start(bf16[2,24,3456]{2,1,0:T(8,128)(2,1)S(1)} %fusion.75), channel_id=1, source_target_pairs={{0,1},{1,0},{2,3},{3,2},{4,5},{5,4},{6,7},{7,6},{8,9},{9,8},{10,11... | collective-permute-start | bytes 995336 | tf_op jit(solution)/shard_map/ppermute | solution.py:318
  448.9 15.4 %copy-start.24 = (f32[2,24,3072]{2,1,0:T(8,128)S(1)}, f32[2,24,3072]{2,1,0:T(8,128)}, u32[]{:S(2)}) copy-start(f32[2,24,3072]{2,1,0:T(8,128)} %param.24) | copy-start | bytes 1769476
  448.9 8.2 %collective-permute-start.20 = (bf16[24,3456]{1,0:T(8,128)(2,1)S(1)}, bf16[24,3456]{1,0:T(8,128)(2,1)S(1)}, u32[]{:S(2)}, u32[]{:S(2)}) collective-permute-start(bf16[24,3456]{1,0:T(8,128)(2,1)S(1)} %fusion.90), channel_id=1, source_target_pairs={{0,16},{1,17},{2,18},{3,19},{4,20},{5,21},{6,22},{7,23},{8,24},{9,... | collective-permute-start | bytes 497672 | tf_op jit(solution)/shard_map/ppermute | solution.py:318
  454.6 23.1 %slice-start = ((s8[7471104]{0:T(1024)(128)(4,1)}), s8[3276800]{0:T(1024)(128)(4,1)S(1)}, s32[]{:S(2)}) async-start(s8[7471104]{0:T(1024)(128)(4,1)} %bitcast.271), calls=%async_computation.2 | async-start | bytes 6553600
  454.7 9.5 %collective-permute-start.24 = (bf16[24,3456]{1,0:T(8,128)(2,1)S(1)}, bf16[24,3456]{1,0:T(8,128)(2,1)S(1)}, u32[]{:S(2)}, u32[]{:S(2)}) collective-permute-start(bf16[24,3456]{1,0:T(8,128)(2,1)S(1)} %fusion.91), channel_id=1, source_target_pairs={{0,16},{1,17},{2,18},{3,19},{4,20},{5,21},{6,22},{7,23},{8,24},{9,... | collective-permute-start | bytes 497672 | tf_op jit(solution)/shard_map/ppermute | solution.py:318
  457.2 8.1 %copy-start.23 = (f32[24,3456]{1,0:T(8,128)}, f32[24,3456]{1,0:T(8,128)S(1)}, u32[]{:S(2)}) copy-start(f32[24,3456]{1,0:T(8,128)S(1)} %bitcast_add_fusion.12) | copy-start | bytes 995332
  465.3 5.8 %copy-start.31 = (f32[2,24,768]{2,1,0:T(8,128)S(1)}, f32[2,24,768]{2,1,0:T(8,128)}, u32[]{:S(2)}) copy-start(f32[2,24,768]{2,1,0:T(8,128)} %param.23) | copy-start | bytes 442372
  465.3 6.7 %copy-start.32 = (f32[24,768]{1,0:T(8,128)S(1)}, f32[24,768]{1,0:T(8,128)}, u32[]{:S(2)}) copy-start(f32[24,768]{1,0:T(8,128)} %param.17) | copy-start | bytes 221188
  468.8 6.0 %copy-start.25 = (f32[2,24,3072]{2,1,0:T(8,128)S(1)}, f32[2,24,3072]{2,1,0:T(8,128)}, u32[]{:S(2)}) copy-start(f32[2,24,3072]{2,1,0:T(8,128)} %param.24) | copy-start | bytes 1769476
  468.8 8.9 %slice-start.1 = ((s8[7471104]{0:T(1024)(128)(4,1)}), s8[4194304]{0:T(1024)(128)(4,1)S(1)}, s32[]{:S(2)}) async-start(s8[7471104]{0:T(1024)(128)(4,1)} %bitcast.271), calls=%async_computation.3 | async-start | bytes 8388608
  470.2 6.7 %copy-start.26 = (f32[1,24,3072]{2,1,0:T(8,128)S(1)}, f32[1,24,3072]{2,1,0:T(8,128)}, u32[]{:S(2)}) copy-start(f32[1,24,3072]{2,1,0:T(8,128)} %get-tuple-element.130) | copy-start | bytes 884740
  479.9 8.3 %collective-permute-start.13 = (bf16[2,2,2,24,768]{4,3,2,1,0:T(8,128)(2,1)S(1)}, bf16[2,2,2,24,768]{4,3,2,1,0:T(8,128)(2,1)S(1)}, u32[]{:S(2)}, u32[]{:S(2)}) collective-permute-start(bf16[2,2,2,24,768]{4,3,2,1,0:T(8,128)(2,1)S(1)} %fusion.85), channel_id=1, source_target_pairs={{0,8},{1,9},{2,10},{3,11},{4,12},{5,13},{6,14},{7,15},{8,0},{9,1},... | collective-permute-start | bytes 884744 | tf_op jit(solution)/shard_map/ppermute | solution.py:318
  480.8 8.5 %collective-permute-start.9 = (bf16[2,2,2,24,768]{4,3,2,1,0:T(8,128)(2,1)S(1)}, bf16[2,2,2,24,768]{4,3,2,1,0:T(8,128)(2,1)S(1)}, u32[]{:S(2)}, u32[]{:S(2)}) collective-permute-start(bf16[2,2,2,24,768]{4,3,2,1,0:T(8,128)(2,1)S(1)} %fusion.84), channel_id=1, source_target_pairs={{0,4},{1,5},{2,6},{3,7},{4,0},{5,1},{6,2},{7,3},{8,12},{9,13},{10,... | collective-permute-start | bytes 884744 | tf_op jit(solution)/shard_map/ppermute | solution.py:318
  481.8 10.5 %collective-permute-start.5 = (bf16[2,2,2,24,896]{4,3,2,1,0:T(8,128)(2,1)S(1)}, bf16[2,2,2,24,896]{4,3,2,1,0:T(8,128)(2,1)S(1)}, u32[]{:S(2)}, u32[]{:S(2)}) collective-permute-start(bf16[2,2,2,24,896]{4,3,2,1,0:T(8,128)(2,1)S(1)} %fusion.73), channel_id=1, source_target_pairs={{0,1},{1,0},{2,3},{3,2},{4,5},{5,4},{6,7},{7,6},{8,9},{9,8},{10,11... | collective-permute-start | bytes 1032200 | tf_op jit(solution)/shard_map/ppermute | solution.py:318
  488.3 5.7 %collective-permute-start.14 = (bf16[2,2,24,768]{3,2,1,0:T(8,128)(2,1)S(1)}, bf16[2,2,24,768]{3,2,1,0:T(8,128)(2,1)S(1)}, u32[]{:S(2)}, u32[]{:S(2)}) collective-permute-start(bf16[2,2,24,768]{3,2,1,0:T(8,128)(2,1)S(1)} %fusion.93), channel_id=1, source_target_pairs={{0,1},{1,0},{2,3},{3,2},{4,5},{5,4},{6,7},{7,6},{8,9},{9,8},{10,11... | collective-permute-start | bytes 442376 | tf_op jit(solution)/shard_map/ppermute | solution.py:318
  489.4 5.9 %collective-permute-start.10 = (bf16[2,2,24,768]{3,2,1,0:T(8,128)(2,1)S(1)}, bf16[2,2,24,768]{3,2,1,0:T(8,128)(2,1)S(1)}, u32[]{:S(2)}, u32[]{:S(2)}) collective-permute-start(bf16[2,2,24,768]{3,2,1,0:T(8,128)(2,1)S(1)} %fusion.92), channel_id=1, source_target_pairs={{0,8},{1,9},{2,10},{3,11},{4,12},{5,13},{6,14},{7,15},{8,0},{9,1},... | collective-permute-start | bytes 442376 | tf_op jit(solution)/shard_map/ppermute | solution.py:318
  492.4 11.8 %copy-start.52 = (f32[2,96]{1,0:T(2,128)S(1)}, f32[2,96]{1,0:T(2,128)}, u32[]{:S(2)}) copy-start(f32[2,96]{1,0:T(2,128)} %param.26) | copy-start | bytes 2308
  492.4 11.8 %copy-start.54 = (f32[96]{0:T(128)S(1)}, f32[96]{0:T(128)}, u32[]{:S(2)}) copy-start(f32[96]{0:T(128)} %param.20) | copy-start | bytes 1156
  492.4 12.3 %copy-start.34 = (f32[1,24,8]{2,1,0:T(8,128)S(1)}, f32[1,24,8]{2,1,0:T(8,128)}, u32[]{:S(2)}) copy-start(f32[1,24,8]{2,1,0:T(8,128)} %copy.88) | copy-start | bytes 2308
  492.5 9.5 %collective-permute-start.6 = (bf16[2,2,24,896]{3,2,1,0:T(8,128)(2,1)S(1)}, bf16[2,2,24,896]{3,2,1,0:T(8,128)(2,1)S(1)}, u32[]{:S(2)}, u32[]{:S(2)}) collective-permute-start(bf16[2,2,24,896]{3,2,1,0:T(8,128)(2,1)S(1)} %fusion.89), channel_id=1, source_target_pairs={{0,4},{1,5},{2,6},{3,7},{4,0},{5,1},{6,2},{7,3},{8,12},{9,13},{10,... | collective-permute-start | bytes 516104 | tf_op jit(solution)/shard_map/ppermute | solution.py:318
  494.1 18.1 %copy-start.28 = (f32[2,24,2304]{2,1,0:T(8,128)S(1)}, f32[2,24,2304]{2,1,0:T(8,128)}, u32[]{:S(2)}) copy-start(f32[2,24,2304]{2,1,0:T(8,128)} %param.22) | copy-start | bytes 1327108
  494.1 4.7 collective-permute-start.15
  495.3 16.9 %copy-start.30 = (f32[24,2304]{1,0:T(8,128)S(1)}, f32[24,2304]{1,0:T(8,128)}, u32[]{:S(2)}) copy-start(f32[24,2304]{1,0:T(8,128)} %param.16) | copy-start | bytes 663556
  495.4 5.4 %collective-permute-start.11 = (bf16[2,24,768]{2,1,0:T(8,128)(2,1)S(1)}, bf16[2,24,768]{2,1,0:T(8,128)(2,1)S(1)}, u32[]{:S(2)}, u32[]{:S(2)}) collective-permute-start(bf16[2,24,768]{2,1,0:T(8,128)(2,1)S(1)} %fusion.97), channel_id=1, source_target_pairs={{0,1},{1,0},{2,3},{3,2},{4,5},{5,4},{6,7},{7,6},{8,9},{9,8},{10,11... | collective-permute-start | bytes 221192 | tf_op jit(solution)/shard_map/ppermute | solution.py:318
  498.9 5.0 collective-permute-start.16
  500.8 5.4 %collective-permute-start.12 = (bf16[24,768]{1,0:T(8,128)(2,1)S(1)}, bf16[24,768]{1,0:T(8,128)(2,1)S(1)}, u32[]{:S(2)}, u32[]{:S(2)}) collective-permute-start(bf16[24,768]{1,0:T(8,128)(2,1)S(1)} %fusion.103), channel_id=1, source_target_pairs={{0,16},{1,17},{2,18},{3,19},{4,20},{5,21},{6,22},{7,23},{8,24},{9,... | collective-permute-start | bytes 110600 | tf_op jit(solution)/shard_map/ppermute | solution.py:318
  502.0 5.1 collective-permute-start.7
  504.0 9.9 %copy-start.53 = (f32[96]{0:T(128)}, f32[96]{0:T(128)S(1)}, u32[]{:S(2)}) copy-start(f32[96]{0:T(128)S(1)} %reshape.297) | copy-start | bytes 1156
  507.2 5.0 collective-permute-start.8
  (28 other events, 79.0 us)
Sparse Core Ops, SparseCore 0:
  11.5 63.9 all-gather.2
  79.0 86.4 all-gather.4

commit v7 on v6

--- a/solution.py
+++ b/solution.py
@@ -365,18 +365,23 @@
         axis=1,
     )
     first_pack = jnp.concatenate([project_in, small], axis=1).astype(jnp.bfloat16)
+    ff_per_row = ff_width // model_width
+    expand_local = expand_weight.reshape(shard_rows, model_width, ff_per_row)
+    expand_local = jnp.swapaxes(expand_local, 1, 2).reshape(shard_rows, ff_width)
     second_pack = jnp.concatenate(
-        [project_out, expand_weight, shrink_weight.reshape(shard_rows, -1)], axis=1
+        [project_out, expand_local, shrink_weight.reshape(shard_rows, -1)], axis=1
     ).astype(jnp.bfloat16)
     first_full = lax.all_gather(first_pack, everyone, axis=0, tiled=True)
     second_full = lax.all_gather(second_pack, everyone, axis=0, tiled=True)
     full_in = first_full[:, :wide_in]
     small_full = first_full[:, wide_in:].astype(jnp.float32)
     column_set = small_full[:, : vectors.shape[1]]
-    full_bias = small_full[:, vectors.shape[1] : vectors.shape[1] + ff_width // model_width].reshape(-1)
+    full_bias = small_full[:, vectors.shape[1] : vectors.shape[1] + ff_width // model_width].T.reshape(-1)
     full_out = second_full[:, :model_width]
     full_expand = second_full[:, model_width : model_width + ff_width]
-    full_shrink = second_full[:, model_width + ff_width :].reshape(ff_width, model_width)
+    shrink_blocks = second_full[:, model_width + ff_width :].reshape(
+        model_width, ff_width // model_width, model_width
+    )
 
     frames_rows = inputs.reshape(row_count, model_width).astype(jnp.float32)
     normed_first, plain_first, inv_first = norm_parts(
@@ -413,19 +418,28 @@
     hidden_second = normed_second.astype(jnp.bfloat16)
     preact = jnp.dot(hidden_second, full_expand, preferred_element_type=jnp.float32) + full_bias
     activated = gelu_exact(preact).astype(jnp.bfloat16)
+    activated_blocks = activated.reshape(row_count, ff_width // model_width, model_width)
     result = (
         residual
-        + jnp.dot(activated, full_shrink, preferred_element_type=jnp.float32)
+        + jnp.einsum(
+            "tjr,rjc->tc", activated_blocks, shrink_blocks, preferred_element_type=jnp.float32
+        )
         + column_set[:, 7]
     )
     output = result.astype(jnp.bfloat16).reshape(inputs.shape)
 
     grad_result = cotangent.reshape(row_count, model_width)
-    grad_shrink_term = jnp.dot(activated.T, grad_result, preferred_element_type=jnp.float32)
+    grad_shrink_term = jnp.einsum(
+        "tjr,tc->rjc", activated_blocks, grad_result, preferred_element_type=jnp.float32
+    ).astype(jnp.bfloat16)
     grad_down_bias = jnp.sum(grad_result.astype(jnp.float32), axis=0)
-    grad_activated = jnp.dot(grad_result, full_shrink.T, preferred_element_type=jnp.float32)
+    grad_activated = jnp.einsum(
+        "tc,rjc->tjr", grad_result, shrink_blocks, preferred_element_type=jnp.float32
+    ).reshape(row_count, ff_width)
     grad_preact = (grad_activated * gelu_slope(preact)).astype(jnp.bfloat16)
-    grad_expand_term = jnp.dot(hidden_second.T, grad_preact, preferred_element_type=jnp.float32)
+    grad_expand_term = jnp.dot(
+        hidden_second.T, grad_preact, preferred_element_type=jnp.float32
+    ).astype(jnp.bfloat16)
     grad_bias_term = jnp.sum(grad_preact.astype(jnp.float32), axis=0)
     grad_hidden_second = jnp.dot(grad_preact, full_expand.T, preferred_element_type=jnp.float32)
     norm_term_second, gain_second, shift_second = norm_backward(
@@ -433,7 +447,9 @@
     )
     grad_residual = grad_result.astype(jnp.float32) + norm_term_second
     grad_attended = grad_residual.astype(jnp.bfloat16)
-    grad_out_term = jnp.dot(mixed_low.T, grad_attended, preferred_element_type=jnp.float32)
+    grad_out_term = jnp.dot(
+        mixed_low.T, grad_attended, preferred_element_type=jnp.float32
+    ).astype(jnp.bfloat16)
     grad_out_bias = jnp.sum(grad_attended.astype(jnp.float32), axis=0)
     late_terms = jnp.concatenate(
         [grad_shrink_term.reshape(model_width, -1), grad_expand_term, grad_out_term], axis=1
@@ -513,7 +529,7 @@
     small_grads = jnp.concatenate(
         [
             grad_columns,
-            grad_bias_term.reshape(model_width, -1),
+            grad_bias_term.reshape(-1, model_width).T,
             jnp.zeros((model_width, 128 - 12), jnp.float32),
         ],
         axis=1,
@@ -528,7 +544,9 @@
     owned_vectors = owned_first[:, wide_in : wide_in + vectors.shape[1]]
     owned_bias = owned_first[:, wide_in + vectors.shape[1] : wide_in + 12].reshape(-1)
     owned_shrink = owned_late[:, :ff_width].reshape(shrink_weight.shape)
-    owned_expand = owned_late[:, ff_width : 2 * ff_width]
+    owned_expand = jnp.swapaxes(
+        owned_late[:, ff_width : 2 * ff_width].reshape(shard_rows, ff_per_row, model_width), 1, 2
+    ).reshape(shard_rows, ff_width)
     owned_out = owned_late[:, 2 * ff_width :]
     new_in, mom_in = adam_step(project_in, moments_in, owned_in)
     new_out, mom_out = adam_step(project_out, moments_out, owned_out)

time: 526 us -> 626 us (1.19)
  local copies, waits for them, and re-layouts: 97.4 us -> 173 us
  waiting for transfers between devices: 149 us -> 167 us
  matrix products: 68.4 us -> 77.3 us
  other arithmetic: 71.3 us -> 64.2 us
    unnamed x136 -> x146, local copies, waits for them, and re-layouts: 15 us -> 53.2 us
    ppermute x2, waiting for transfers between devices: 11 us -> 29 us  [body(): returned = lax.ppermute(send, 'frame', swap)]
    transpose x0 -> x5, local copies, waits for them, and re-layouts: none -> 14.8 us  [the longest x1 13.1 us: body(): jnp.einsum('tc,rjc->tjr', grad_result, shrink_blocks, preferred_element_t...]
    concatenate x1, other arithmetic: 15.2 us -> 5.22 us  [body(): jnp.concatenate([grad_shrink_term.reshape(model_width, -1), grad_expand_t...]
    slice x2 -> x3, local copies, waits for them, and re-layouts: 5.01 us -> 13.6 us  [the longest x2 11.7 us: body(): second_full[:, model_width + ff_width:]]
    convert_element_type x22 -> x21, local copies, waits for them, and re-layouts: 14.4 us -> 10.2 us  [tree_reduce_scatter(): lax.dynamic_index_in_dim(part, 1 - mine, axis=axis, keepdims=False)]
    concatenate x10 -> x9, local copies, waits for them, and re-layouts: 19.4 us -> 18.3 us  [body(): jnp.concatenate([grad_in_term, small_grads], axis=1)]
  transfers between devices with their start and end apart: 27 -> 27, of which waited for: 17 -> 18; matrix products, arithmetic and copies ran while one was open for 20% -> 22% of each run, Pallas kernels for 17% -> 10%
where the time goes in v7:
time: 626 us; the launch traced here: 618 us
  local copies, waits for them, and re-layouts  173 us (28%)
  waiting for transfers between devices  167 us (27%)
  Pallas kernels  89.9 us (14%)
  matrix products  77.3 us (12%)
  other arithmetic  64.2 us (10%)
  starting transfers between devices  30.6 us (5%)
  between operations  15.7 us (3%)
    pallas_call x2, Pallas kernels, attention_pallas(): pl.pallas_call(attention_backward_kernel, grid=(span,), in_specs=[qi_spec...  55.3 us
    unnamed x146, local copies, waits for them, and re-layouts  53.2 us
    ppermute x22, waiting for transfers between devices, tree_reduce_scatter(): got = lax.ppermute(send, ('clip', 'frame'), pairs)  45.1 us
    all_gather x1, waiting for transfers between devices, body(): second_full = lax.all_gather(second_pack, everyone, axis=0, tiled=True)  36.7 us
    pallas_call x1, Pallas kernels, attention_pallas(): pl.pallas_call(attention_forward_kernel, grid=(pair_count,), in_specs=[q_...  34.5 us
    all_gather x1, waiting for transfers between devices, body(): first_full = lax.all_gather(first_pack, everyone, axis=0, tiled=True)  29.3 us
    ppermute x2, waiting for transfers between devices, body(): returned = lax.ppermute(send, 'frame', swap)  29 us
    ppermute x1, waiting for transfers between devices, body(): lax.ppermute(inputs, 'frame', swap).reshape(row_count, model_width)  27.2 us
  transfers between devices with their start and end apart: 27, of which 18 were waited for; matrix products, arithmetic and copies ran while one was open for 22% of the time, Pallas kernels for 10%

profile of v7, /device:TPU:0, one launch (start us, length us, event | category | flops | bytes accessed | tf_op | source)
XLA Modules:
  0.0 617.8 jit_solution(10470456661086847890)
XLA Ops:
  14.5 3.0 collective-permute-start
  18.3 27.2 %collective-permute-done = bf16[1,750,768]{2,1,0:T(8,128)(2,1)S(1)} collective-permute-done((bf16[1,750,768]{2,1,0:T(8,128)(2,1)S(1)}, bf16[1,750,768]{2,1,0:T(8,128)(2,1)S(1)}, u32[]{:S(2)}, u32[]{:S(2)}) %collective-permute-start) | collective-permute-done | bytes 1152032 | tf_op jit(solution)/shard_map/ppermute | solution.py:391
  46.2 29.3 %all-gather.3.cloned.1.call-done = bf16[768,2432]{1,0:T(8,128)(2,1)} async-done(((bf16[24,2432]{1,0:T(8,128)(2,1)}), bf16[768,2432]{1,0:T(8,128)(2,1)}) %all-gather.3.cloned.1.call-update) | async-done | bytes 3735568 | tf_op jit(solution)/shard_map/all_gather | solution.py:374
  76.6 2.0 slice_reduce_fusion
  78.7 3.6 add_convert_fusion
  85.1 4.4 add_convert_fusion.1
  89.5 2.9 fusion.8.k_ref.v_ref
  92.4 34.5 %shard_map.293 = (bf16[768,768]{1,0:T(8,128)(2,1)S(1)}, f32[768,768]{1,0:T(8,128)S(1)}) custom-call(bf16[768,768]{1,0:T(8,128)(2,1)S(1)} %pad.19.q_ref, bf16[1536,1536]{1,0:T(8,128)(2,1)} %fusion.8.k_ref.v_ref, bf16[1536,1536]{1,0:T(8,128)(2,1)} %fusion.8.k_ref.v_ref, f32[1,1536]{1,0:T(1,128)S(1)} %compare_select_fusion.kbias_ref), custom_call_target="tpu_custom_call" | custom-call | tf_op jit(solution)/shard_map/pallas_call | solution.py:157
  128.3 36.7 %all-gather.5.cloned.1.call-done = bf16[768,6912]{1,0:T(8,128)(2,1)} async-done(((bf16[24,6912]{1,0:T(8,128)(2,1)}), bf16[768,6912]{1,0:T(8,128)(2,1)}) %all-gather.5.cloned.1.call-update) | async-done | bytes 10616848 | tf_op jit(solution)/shard_map/all_gather | solution.py:375
  165.0 4.8 slice.277
  169.8 6.9 %copy.122 = bf16[768,3072]{0,1:T(8,128)(2,1)} copy(bf16[768,3072]{1,0:T(8,128)(2,1)} %slice.277) | data formatting | bytes 9437184 | tf_op jit(solution)/shard_map/slice | solution.py:382
  176.7 9.9 %convolution_bitcast_fusion = f32[750,4,768]{2,0,1:T(8,128)} fusion(bf16[768,4,768]{0,2,1:T(8,128)(2,1)} %bitcast.299, bf16[1,750,768]{2,1,0:T(8,128)(2,1)} %param.15), kind=kOutput, calls=%fused_computation.36 | convolution fusion | flops 3538944000 | bytes 15086592 | tf_op jit(solution)/shard_map/tc,rjc->tjr/dot_general | solution.py:436
  186.7 13.1 %copy.126 = f32[750,4,768]{2,1,0:T(4,128)} copy(f32[750,4,768]{2,0,1:T(8,128)} %convolution_bitcast_fusion) | data formatting | bytes 18432000 | tf_op jit(solution)/shard_map/tc,rjc->tjr/transpose | solution.py:436
  199.7 8.7 %pad.72 = f32[752,4,768]{2,1,0:T(4,128)} pad(f32[750,4,768]{2,1,0:T(4,128)} %copy.126, f32[]{:T(128)} %constant.225.clone.1), padding=0_2x0_0x0_0 | pad | bytes 18456580
  208.4 17.8 %copy.166 = f32[94,8,4,768]{3,1,2,0:T(8,128)S(1)} copy(f32[94,8,4,768]{3,2,1,0:T(4,128)} %bitcast.292) | data formatting | bytes 18481152
  226.2 2.5 fusion.140
  229.4 12.6 %convert_reduce_fusion = (f32[3072]{0:T(1024)}, bf16[750,3072]{1,0:T(8,128)(2,1)}, bf16[750,3072]{1,0:T(8,128)(2,1)}) fusion(f32[750,3072]{1,0:T(8,128)S(1)} %bitcast.298, f32[3072]{0:T(1024)S(1)} %copy-done.47, bf16[768,6912]{1,0:T(8,128)(2,1)} %all-gather.5.cloned.1.call-done, f32[750,768]{1,0:T(8,128)S(1)} %get-tuple-element.188, ...), kind=kOutput, calls=%fused_computation.12 | convolution fusion | flops 3578684928 | bytes 25491312 | tf_op jit(solution)/shard_map/dot_general | solution.py:419
  242.0 9.6 %reshape.347 = bf16[750,4,768]{2,1,0:T(4,128)(2,1)} reshape(bf16[750,3072]{1,0:T(8,128)(2,1)} %get-tuple-element.160) | data formatting | bytes 9216000 | tf_op jit(solution)/shard_map/reshape | solution.py:421
  251.6 9.5 %convolution_convert_fusion = bf16[768,3072]{1,0:T(8,128)(2,1)} fusion(bf16[750,3072]{1,0:T(8,128)(2,1)} %get-tuple-element.155, f32[750,768]{1,0:T(8,128)} %copy-done.13, f32[768]{0:T(1024)S(1)} %get-tuple-element.143, f32[768]{0:T(1024)S(1)} %get-tuple-element.144, f32[750]{0:T(1024)S(1)} %add_rsqrt_fusion, f32[750]{0:T(1024)S(1)} %broadcast_multiply_fusion.4), kind=kOutput, calls=%fused_computation.18 | convolution fusion | flops 3544183296 | bytes 11642736 | tf_op jit(solution)/shard_map/dot_general | solution.py:440
  261.2 7.5 %multiply_reduce_fusion = (f32[768]{0:T(1024)}, f32[750]{0:T(1024)S(1)}, f32[750]{0:T(1024)S(1)}, f32[768]{0:T(1024)}, f32[750,768]{1,0:T(8,128)S(1)}) fusion(f32[750,768]{1,0:T(8,128)S(1)} %copy-done.14, f32[750]{0:T(1024)S(1)} %add_rsqrt_fusion, f32[750]{0:T(1024)S(1)} %broadcast_multiply_fusion.4, f32[768]{0:T(1024)S(1)} %get-tuple-element.144, ...), kind=kOutput, calls=%fused_computation.91 | convolution fusion | flops 3544124928 | bytes 13955808 | tf_op jit(solution)/shard_map/dot_general | solution.py:444
  271.8 2.3 convolution_convert_fusion.1
  274.0 4.4 convert_bitcast_fusion
  278.4 5.8 copy.128
  284.3 9.4 %concatenate.80 = bf16[2,2,2,2,2,24,3072]{6,5,4,3,2,1,0:T(8,128)(2,1)} reshape(bf16[768,4,768]{2,1,0:T(4,128)(2,1)} %copy.128) | data formatting | bytes 9437184 | tf_op jit(solution)/shard_map/concatenate | solution.py:454
  293.7 5.2 pad_maximum_fusion
  298.9 2.7 dynamic-slice_bitcast_fusion
  301.6 3.2 copy-done.1
  304.9 2.4 convolution_convert_fusion.2
  307.7 2.6 copy.143
  312.9 2.7 copy.162
  315.6 2.6 copy.161
  318.3 27.7 %shard_map.294 = (f32[768,384]{1,0:T(8,128)S(1)}, f32[1536,384]{1,0:T(8,128)S(1)}, f32[1536,384]{1,0:T(8,128)}) custom-call(bf16[768,768]{1,0:T(8,128)(2,1)S(1)} %pad.19.q_ref, bf16[1536,1536]{1,0:T(8,128)(2,1)} %fusion.8.k_ref.v_ref, bf16[1536,1536]{1,0:T(8,128)(2,1)} %fusion.8.k_ref.v_ref, bf16[768,768]{1,0:T(8,128)(2,1)S(1)} %pad.21.do_ref, ...), custom_call_target="tpu_custom_call" | custom-call | tf_op jit(solution)/shard_map/pallas_call | solution.py:176
  346.0 3.2 slice.227
  355.1 5.4 convert_add_fusion
  360.4 4.8 fusion.134
  365.2 3.0 fusion.75
  368.2 3.0 fusion.74
  371.3 27.6 %shard_map.295 = (f32[768,384]{1,0:T(8,128)S(1)}, f32[1536,384]{1,0:T(8,128)S(1)}, f32[1536,384]{1,0:T(8,128)}) custom-call(bf16[768,768]{1,0:T(8,128)(2,1)S(1)} %pad.19.q_ref, bf16[1536,1536]{1,0:T(8,128)(2,1)} %fusion.8.k_ref.v_ref, bf16[1536,1536]{1,0:T(8,128)(2,1)} %fusion.8.k_ref.v_ref, bf16[768,768]{1,0:T(8,128)(2,1)S(1)} %pad.22.do_ref, ...), custom_call_target="tpu_custom_call" | custom-call | tf_op jit(solution)/shard_map/pallas_call | solution.py:176
  400.6 2.7 slice.233
  406.6 7.1 %fusion.71 = bf16[1,750,768]{2,1,0:T(8,128)(2,1)} fusion(f32[750,768]{1,0:T(8,128)S(1)} %copy-done.15, bf16[768,4,768]{0,2,1:T(8,128)(2,1)S(1)} %bitcast.302, bf16[750,4,768]{2,1,0:T(4,128)(2,1)} %reshape.347, f32[768]{0:T(1024)S(1)} %copy-done.51), kind=kOutput, calls=%fused_computation.113 | convolution fusion | flops 3540672000 | bytes 12785664 | tf_op jit(solution)/shard_map/tjr,rjc->tc/dot_general | solution.py:424
  421.0 6.5 %collective-permute-done.2 = bf16[750,768]{1,0:T(8,128)(2,1)} collective-permute-done((bf16[750,768]{1,0:T(8,128)(2,1)}, bf16[750,768]{1,0:T(8,128)(2,1)}, u32[]{:S(2)}, u32[]{:S(2)}) %collective-permute-start.2) | collective-permute-done | bytes 1152032 | tf_op jit(solution)/shard_map/ppermute | solution.py:489
  429.2 22.4 %collective-permute-done.3 = bf16[750,768]{1,0:T(8,128)(2,1)} collective-permute-done((bf16[750,768]{1,0:T(8,128)(2,1)}, bf16[750,768]{1,0:T(8,128)(2,1)}, u32[]{:S(2)}, u32[]{:S(2)}) %collective-permute-start.3) | collective-permute-done | bytes 1152032 | tf_op jit(solution)/shard_map/ppermute | solution.py:489
  454.1 2.6 copy-done.49
  456.7 2.9 fusion.19
  459.7 2.2 fusion.41
  461.9 2.6 copy.130
  464.5 8.2 %fusion.17 = f32[2,2,2,2,2,24,2304]{6,5,4,3,2,1,0:T(8,128)} fusion(bf16[2,2,2,2,2,24,750]{6,5,4,3,2,1,0:T(8,128)(2,1)} %bitcast.308, bf16[750,2304]{1,0:T(8,128)(2,1)} %copy-done.21), kind=kOutput, calls=%fused_computation.34 | convolution fusion | flops 2654208000 | bytes 11685888 | tf_op jit(solution)/shard_map/dot_general | solution.py:507
  477.6 10.1 %concatenate.98 = f32[2,2,2,2,2,24,2432]{6,5,4,3,2,1,0:T(8,128)} concatenate(f32[2,2,2,2,2,24,2304]{6,5,4,3,2,1,0:T(8,128)} %fusion.17, f32[2,2,2,2,2,24,1]{6,5,4,3,2,1,0:T(8,128)} %concatenate.101, f32[2,2,2,2,2,24,1]{6,5,4,3,2,1,0:T(8,128)} %concatenate.102, f32[2,2,2,2,2,24,1]{6,5,4,3,2,1,0:T(8,128)} %concatenate.103, f32[2,2,2,2,2,24,1]{6,5,4,3,2,1,0:T(8,128)} %concatenate.104, ...), dimensions={6} | concatenate | bytes 14942208 | tf_op jit(solution)/shard_map/concatenate | solution.py:538
  487.7 3.7 fusion.59
  493.2 2.5 bitcast_add_fusion.1
  500.3 12.8 %collective-permute-done.18 = bf16[2,2,24,3456]{3,2,1,0:T(8,128)(2,1)S(1)} collective-permute-done((bf16[2,2,24,3456]{3,2,1,0:T(8,128)(2,1)S(1)}, bf16[2,2,24,3456]{3,2,1,0:T(8,128)(2,1)S(1)}, u32[]{:S(2)}, u32[]{:S(2)}) %collective-permute-start.18) | collective-permute-done | bytes 663584 | tf_op jit(solution)/shard_map/ppermute | solution.py:318
  516.9 7.2 %collective-permute-done.19 = bf16[2,24,3456]{2,1,0:T(8,128)(2,1)S(1)} collective-permute-done((bf16[2,24,3456]{2,1,0:T(8,128)(2,1)S(1)}, bf16[2,24,3456]{2,1,0:T(8,128)(2,1)S(1)}, u32[]{:S(2)}, u32[]{:S(2)}) %collective-permute-start.19) | collective-permute-done | bytes 331808 | tf_op jit(solution)/shard_map/ppermute | solution.py:318
  526.1 3.9 collective-permute-done.23
  532.5 7.1 %collective-permute-done.24 = bf16[24,3456]{1,0:T(8,128)(2,1)S(1)} collective-permute-done((bf16[24,3456]{1,0:T(8,128)(2,1)S(1)}, bf16[24,3456]{1,0:T(8,128)(2,1)S(1)}, u32[]{:S(2)}, u32[]{:S(2)}) %collective-permute-start.24) | collective-permute-done | bytes 165920 | tf_op jit(solution)/shard_map/ppermute | solution.py:318
  543.2 2.0 multiply_add_fusion.1
  545.2 3.6 multiply_add_fusion
  553.0 2.6 copy.147
  555.6 2.1 pad_maximum_fusion.5
  559.3 2.2 fusion.104
  563.3 2.4 fusion.70
  565.7 2.9 bitcast_add_fusion
  586.8 2.0 collective-permute-done.5
  592.7 2.5 collective-permute-done.15
  606.7 2.0 collective-permute-done.8
  (318 shorter events, 109.1 us)
Async XLA Ops:
  7.2 6.5 %copy-start.34 = (f32[24,768]{1,0:T(8,128)S(1)}, f32[24,768]{1,0:T(8,128)}, u32[]{:S(2)}) copy-start(f32[24,768]{1,0:T(8,128)} %param.17) | copy-start | bytes 221188
  7.2 68.3 %all-gather.3.cloned.1.call-start = ((), (), s32[]{:S(2)}) async-start(), calls=%async_computation | async-start | bytes 3852288 | tf_op jit(solution)/shard_map/all_gather | solution.py:374
  10.5 154.5 %all-gather.5.cloned.1.call-start = ((), (), s32[]{:S(2)}) async-start(), calls=%async_computation.1 | async-start | bytes 10948608 | tf_op jit(solution)/shard_map/all_gather | solution.py:375
  14.5 31.0 %collective-permute-start = (bf16[1,750,768]{2,1,0:T(8,128)(2,1)S(1)}, bf16[1,750,768]{2,1,0:T(8,128)(2,1)S(1)}, u32[]{:S(2)}, u32[]{:S(2)}) collective-permute-start(bf16[1,750,768]{2,1,0:T(8,128)(2,1)S(1)} %copy-done.6), channel_id=1, source_target_pairs={{0,1},{1,0},{2,3},{3,2},{4,5},{5,4},{6,7},{7,6},{8,9},{9,8},{10,11... | collective-permute-start | bytes 3456008 | tf_op jit(solution)/shard_map/ppermute | solution.py:391
  17.7 60.9 %copy-start.37 = (f32[750]{0:T(1024)}, f32[750]{0:T(1024)S(1)}, u32[]{:S(2)}) copy-start(f32[750]{0:T(1024)S(1)} %broadcast_multiply_fusion.6) | copy-start | bytes 9004
  18.3 60.4 %copy-start.40 = (f32[750]{0:T(1024)}, f32[750]{0:T(1024)S(1)}, u32[]{:S(2)}) copy-start(f32[750]{0:T(1024)S(1)} %add_rsqrt_fusion.2) | copy-start | bytes 9004
  45.4 33.1 %copy-start.22 = (bf16[1,750,768]{2,1,0:T(8,128)(2,1)}, bf16[1,750,768]{2,1,0:T(8,128)(2,1)S(1)}, u32[]{:S(2)}) copy-start(bf16[1,750,768]{2,1,0:T(8,128)(2,1)S(1)} %collective-permute-done) | copy-start | bytes 3456004
  78.6 6.5 %copy-start.43 = (f32[768]{0:T(1024)}, f32[768]{0:T(1024)S(1)}, u32[]{:S(2)}) copy-start(f32[768]{0:T(1024)S(1)} %get-tuple-element.148) | copy-start | bytes 9220
  208.4 17.8 %copy-start.54 = (f32[768]{0:T(1024)S(1)}, f32[768]{0:T(1024)}, u32[]{:S(2)}) copy-start(f32[768]{0:T(1024)} %get-tuple-element.145) | copy-start | bytes 9220
  228.7 13.3 %copy-start.13 = (f32[750,768]{1,0:T(8,128)}, f32[750,768]{1,0:T(8,128)S(1)}, u32[]{:S(2)}) copy-start(f32[750,768]{1,0:T(8,128)S(1)} %get-tuple-element.188) | copy-start | bytes 6912004
  251.6 9.5 %copy-start.14 = (f32[750,768]{1,0:T(8,128)S(1)}, f32[750,768]{1,0:T(8,128)}, u32[]{:S(2)}) copy-start(f32[750,768]{1,0:T(8,128)} %copy-done.13) | copy-start | bytes 6912004
  251.6 9.5 %copy-start.58 = (bf16[750,3072]{1,0:T(8,128)(2,1)S(1)}, bf16[750,3072]{1,0:T(8,128)(2,1)}, u32[]{:S(2)}) copy-start(bf16[750,3072]{1,0:T(8,128)(2,1)} %get-tuple-element.155) | copy-start | bytes 13824004
  251.6 22.4 %slice-start.5 = ((s8[4608000]{0:T(1024)(128)(4,1)}), s8[4194304]{0:T(1024)(128)(4,1)S(1)}, s32[]{:S(2)}) async-start(s8[4608000]{0:T(1024)(128)(4,1)} %bitcast.304), calls=%async_computation.7 | async-start | bytes 8388608
  261.2 7.5 %copy-start.29 = (bf16[1,750,768]{2,1,0:T(8,128)(2,1)S(1)}, bf16[1,750,768]{2,1,0:T(8,128)(2,1)}, u32[]{:S(2)}) copy-start(bf16[1,750,768]{2,1,0:T(8,128)(2,1)} %param.15) | copy-start | bytes 3456004
  261.2 12.9 %slice-start.6 = ((s8[4608000]{0:T(1024)(128)(4,1)}), s8[413696]{0:T(1024)(128)(4,1)S(1)}, s32[]{:S(2)}) async-start(s8[4608000]{0:T(1024)(128)(4,1)} %bitcast.304), calls=%async_computation.8 | async-start | bytes 827392
  284.3 9.4 %copy-start.28 = (bf16[768,768]{1,0:T(8,128)(2,1)S(1)}, bf16[768,768]{1,0:T(8,128)(2,1)}, u32[]{:S(2)}) copy-start(bf16[768,768]{1,0:T(8,128)(2,1)} %convolution_convert_fusion.1) | copy-start | bytes 3538948
  298.9 6.0 copy-start.1
  298.9 5.9 copy-start.11
  307.3 47.8 %collective-permute-start.1 = (bf16[2,2,2,2,24,6912]{5,4,3,2,1,0:T(8,128)(2,1)}, bf16[2,2,2,2,24,6912]{5,4,3,2,1,0:T(8,128)(2,1)}, u32[]{:S(2)}, u32[]{:S(2)}) collective-permute-start(bf16[2,2,2,2,24,6912]{5,4,3,2,1,0:T(8,128)(2,1)} %dynamic-slice_bitcast_fusion), channel_id=1, source_target_pairs={{0,2},{1,3},{2,0},{3,1},{4,6},{5,7},{6,4},{7,5},{8,10},{9,11},{10,... | collective-permute-start | bytes 15925256 | tf_op jit(solution)/shard_map/ppermute | solution.py:318
  398.9 28.7 %collective-permute-start.2 = (bf16[750,768]{1,0:T(8,128)(2,1)}, bf16[750,768]{1,0:T(8,128)(2,1)}, u32[]{:S(2)}, u32[]{:S(2)}) collective-permute-start(bf16[750,768]{1,0:T(8,128)(2,1)} %pad_maximum_fusion.3), channel_id=1, source_target_pairs={{0,1},{1,0},{2,3},{3,2},{4,5},{5,4},{6,7},{7,6},{8,9},{9,8},{10,11... | collective-permute-start | bytes 3456008 | tf_op jit(solution)/shard_map/ppermute | solution.py:489
  405.1 46.5 %collective-permute-start.3 = (bf16[750,768]{1,0:T(8,128)(2,1)}, bf16[750,768]{1,0:T(8,128)(2,1)}, u32[]{:S(2)}, u32[]{:S(2)}) collective-permute-start(bf16[750,768]{1,0:T(8,128)(2,1)} %fusion.53), channel_id=1, source_target_pairs={{0,1},{1,0},{2,3},{3,2},{4,5},{5,4},{6,7},{7,6},{8,9},{9,8},{10,11... | collective-permute-start | bytes 3456008 | tf_op jit(solution)/shard_map/ppermute | solution.py:489
  406.5 7.2 %copy-start.42 = (f32[768]{0:T(1024)S(1)}, f32[768]{0:T(1024)}, u32[]{:S(2)}) copy-start(f32[768]{0:T(1024)} %get-tuple-element.156) | copy-start | bytes 9220
  406.5 8.2 %copy-start.53 = (f32[768]{0:T(1024)S(1)}, f32[768]{0:T(1024)}, u32[]{:S(2)}) copy-start(f32[768]{0:T(1024)} %get-tuple-element.134) | copy-start | bytes 9220
  406.5 9.2 %copy-start.52 = (f32[768]{0:T(1024)S(1)}, f32[768]{0:T(1024)}, u32[]{:S(2)}) copy-start(f32[768]{0:T(1024)} %get-tuple-element.140) | copy-start | bytes 9220
  406.5 11.3 %copy-start.46 = (f32[3072]{0:T(1024)S(1)}, f32[3072]{0:T(1024)}, u32[]{:S(2)}) copy-start(f32[3072]{0:T(1024)} %get-tuple-element.154) | copy-start | bytes 36868
  413.7 7.1 %copy-start.23 = (f32[750,384]{1,0:T(8,128)S(1)}, f32[750,384]{1,0:T(8,128)}, u32[]{:S(2)}) copy-start(f32[750,384]{1,0:T(8,128)} %slice.225) | copy-start | bytes 3456004
  418.8 8.8 %copy-start.17 = (f32[1500,384]{1,0:T(8,128)S(1)}, f32[1500,384]{1,0:T(8,128)}, u32[]{:S(2)}) copy-start(f32[1500,384]{1,0:T(8,128)} %slice.227) | copy-start | bytes 6912004
  418.8 8.8 %copy-start.18 = (f32[1500,384]{1,0:T(8,128)S(1)}, f32[1500,384]{1,0:T(8,128)}, u32[]{:S(2)}) copy-start(f32[1500,384]{1,0:T(8,128)} %slice.226) | copy-start | bytes 6912004
  418.9 74.4 %collective-permute-start.17 = (bf16[2,2,2,24,3456]{4,3,2,1,0:T(8,128)(2,1)}, bf16[2,2,2,24,3456]{4,3,2,1,0:T(8,128)(2,1)}, u32[]{:S(2)}, u32[]{:S(2)}) collective-permute-start(bf16[2,2,2,24,3456]{4,3,2,1,0:T(8,128)(2,1)} %fusion.74), channel_id=1, source_target_pairs={{0,8},{1,9},{2,10},{3,11},{4,12},{5,13},{6,14},{7,15},{8,0},{9,1},... | collective-permute-start | bytes 3981320 | tf_op jit(solution)/shard_map/ppermute | solution.py:318
  420.2 77.1 %collective-permute-start.21 = (bf16[2,2,2,24,3456]{4,3,0,2,1:T(8,128)(2,1)}, bf16[2,2,2,24,3456]{4,3,0,2,1:T(8,128)(2,1)}, u32[]{:S(2)}, u32[]{:S(2)}) collective-permute-start(bf16[2,2,2,24,3456]{4,3,0,2,1:T(8,128)(2,1)} %fusion.75), channel_id=1, source_target_pairs={{0,4},{1,5},{2,6},{3,7},{4,0},{5,1},{6,2},{7,3},{8,12},{9,13},{10,... | collective-permute-start | bytes 3981320 | tf_op jit(solution)/shard_map/ppermute | solution.py:318
  421.0 30.6 %copy-start.3 = (f32[1500,384]{1,0:T(8,128)S(1)}, f32[1500,384]{1,0:T(8,128)}, u32[]{:S(2)}) copy-start(f32[1500,384]{1,0:T(8,128)} %copy-done.2) | copy-start | bytes 6912004
  421.0 30.6 %copy-start.5 = (f32[1500,384]{1,0:T(8,128)S(1)}, f32[1500,384]{1,0:T(8,128)}, u32[]{:S(2)}) copy-start(f32[1500,384]{1,0:T(8,128)} %copy-done.4) | copy-start | bytes 6912004
  453.5 6.1 copy-start.21
  491.3 74.4 %collective-permute-start.4 = (bf16[2,2,2,2,24,2432]{5,4,3,2,1,0:T(8,128)(2,1)}, bf16[2,2,2,2,24,2432]{5,4,3,2,1,0:T(8,128)(2,1)}, u32[]{:S(2)}, u32[]{:S(2)}) collective-permute-start(bf16[2,2,2,2,24,2432]{5,4,3,2,1,0:T(8,128)(2,1)} %fusion.59), channel_id=1, source_target_pairs={{0,2},{1,3},{2,0},{3,1},{4,6},{5,7},{6,4},{7,5},{8,10},{9,11},{10,... | collective-permute-start | bytes 5603336 | tf_op jit(solution)/shard_map/ppermute | solution.py:318
  491.4 5.9 slice-start
  495.8 17.4 %collective-permute-start.18 = (bf16[2,2,24,3456]{3,2,1,0:T(8,128)(2,1)S(1)}, bf16[2,2,24,3456]{3,2,1,0:T(8,128)(2,1)S(1)}, u32[]{:S(2)}, u32[]{:S(2)}) collective-permute-start(bf16[2,2,24,3456]{3,2,1,0:T(8,128)(2,1)S(1)} %fusion.89), channel_id=1, source_target_pairs={{0,4},{1,5},{2,6},{3,7},{4,0},{5,1},{6,2},{7,3},{8,12},{9,13},{10,... | collective-permute-start | bytes 1990664 | tf_op jit(solution)/shard_map/ppermute | solution.py:318
  499.0 17.1 %collective-permute-start.22 = (bf16[2,2,24,3456]{3,2,0,1:T(8,128)(2,1)S(1)}, bf16[2,2,24,3456]{3,2,0,1:T(8,128)(2,1)S(1)}, u32[]{:S(2)}, u32[]{:S(2)}) collective-permute-start(bf16[2,2,24,3456]{3,2,0,1:T(8,128)(2,1)S(1)} %fusion.90), channel_id=1, source_target_pairs={{0,8},{1,9},{2,10},{3,11},{4,12},{5,13},{6,14},{7,15},{8,0},{9,1},... | collective-permute-start | bytes 1990664 | tf_op jit(solution)/shard_map/ppermute | solution.py:318
  513.3 10.8 %collective-permute-start.19 = (bf16[2,24,3456]{2,1,0:T(8,128)(2,1)S(1)}, bf16[2,24,3456]{2,1,0:T(8,128)(2,1)S(1)}, u32[]{:S(2)}, u32[]{:S(2)}) collective-permute-start(bf16[2,24,3456]{2,1,0:T(8,128)(2,1)S(1)} %fusion.92), channel_id=1, source_target_pairs={{0,1},{1,0},{2,3},{3,2},{4,5},{5,4},{6,7},{7,6},{8,9},{9,8},{10,11... | collective-permute-start | bytes 995336 | tf_op jit(solution)/shard_map/ppermute | solution.py:318
  516.3 13.7 %collective-permute-start.23 = (bf16[2,24,3456]{2,1,0:T(8,128)(2,1)S(1)}, bf16[2,24,3456]{2,1,0:T(8,128)(2,1)S(1)}, u32[]{:S(2)}, u32[]{:S(2)}) collective-permute-start(bf16[2,24,3456]{2,1,0:T(8,128)(2,1)S(1)} %fusion.93), channel_id=1, source_target_pairs={{0,1},{1,0},{2,3},{3,2},{4,5},{5,4},{6,7},{7,6},{8,9},{9,8},{10,11... | collective-permute-start | bytes 995336 | tf_op jit(solution)/shard_map/ppermute | solution.py:318
  524.2 8.2 %collective-permute-start.20 = (bf16[24,3456]{1,0:T(8,128)(2,1)S(1)}, bf16[24,3456]{1,0:T(8,128)(2,1)S(1)}, u32[]{:S(2)}, u32[]{:S(2)}) collective-permute-start(bf16[24,3456]{1,0:T(8,128)(2,1)S(1)} %fusion.107), channel_id=1, source_target_pairs={{0,16},{1,17},{2,18},{3,19},{4,20},{5,21},{6,22},{7,23},{8,24},{9,... | collective-permute-start | bytes 497672 | tf_op jit(solution)/shard_map/ppermute | solution.py:318
  530.0 9.5 %collective-permute-start.24 = (bf16[24,3456]{1,0:T(8,128)(2,1)S(1)}, bf16[24,3456]{1,0:T(8,128)(2,1)S(1)}, u32[]{:S(2)}, u32[]{:S(2)}) collective-permute-start(bf16[24,3456]{1,0:T(8,128)(2,1)S(1)} %fusion.108), channel_id=1, source_target_pairs={{0,16},{1,17},{2,18},{3,19},{4,20},{5,21},{6,22},{7,23},{8,24},{9,... | collective-permute-start | bytes 497672 | tf_op jit(solution)/shard_map/ppermute | solution.py:318
  532.4 7.2 %copy-start.27 = (f32[24,3456]{1,0:T(8,128)}, f32[24,3456]{1,0:T(8,128)S(1)}, u32[]{:S(2)}) copy-start(f32[24,3456]{1,0:T(8,128)S(1)} %bitcast_add_fusion.13) | copy-start | bytes 995332
  539.6 5.6 copy-start.8
  551.2 6.5 %copy-start.35 = (f32[24,768]{1,0:T(8,128)S(1)}, f32[24,768]{1,0:T(8,128)}, u32[]{:S(2)}) copy-start(f32[24,768]{1,0:T(8,128)} %param.17) | copy-start | bytes 221188
  555.6 7.7 %copy-start.9 = (f32[1,24,3072]{1,2,0:T(8,128)S(1)}, f32[1,24,3072]{1,2,0:T(8,128)}, u32[]{:S(2)}) copy-start(f32[1,24,3072]{1,2,0:T(8,128)} %copy.161) | copy-start | bytes 884740
  555.6 7.7 %copy-start.19 = (f32[24,3072]{0,1:T(8,128)S(1)}, f32[24,3072]{0,1:T(8,128)}, u32[]{:S(2)}) copy-start(f32[24,3072]{0,1:T(8,128)} %copy.143) | copy-start | bytes 884740
  572.0 8.3 %collective-permute-start.13 = (bf16[2,2,2,24,768]{4,3,2,1,0:T(8,128)(2,1)S(1)}, bf16[2,2,2,24,768]{4,3,2,1,0:T(8,128)(2,1)}, u32[]{:S(2)}, u32[]{:S(2)}) collective-permute-start(bf16[2,2,2,24,768]{4,3,2,1,0:T(8,128)(2,1)S(1)} %fusion.102), channel_id=1, source_target_pairs={{0,8},{1,9},{2,10},{3,11},{4,12},{5,13},{6,14},{7,15},{8,0},{9,1},... | collective-permute-start | bytes 884744 | tf_op jit(solution)/shard_map/ppermute | solution.py:318
  576.7 8.2 %collective-permute-start.9 = (bf16[2,2,2,24,768]{4,3,2,1,0:T(8,128)(2,1)S(1)}, bf16[2,2,2,24,768]{4,3,2,1,0:T(8,128)(2,1)S(1)}, u32[]{:S(2)}, u32[]{:S(2)}) collective-permute-start(bf16[2,2,2,24,768]{4,3,2,1,0:T(8,128)(2,1)S(1)} %fusion.101), channel_id=1, source_target_pairs={{0,4},{1,5},{2,6},{3,7},{4,0},{5,1},{6,2},{7,3},{8,12},{9,13},{10,... | collective-permute-start | bytes 884744 | tf_op jit(solution)/shard_map/ppermute | solution.py:318
  578.2 10.6 %collective-permute-start.5 = (bf16[2,2,2,24,896]{4,3,2,1,0:T(8,128)(2,1)S(1)}, bf16[2,2,2,24,896]{4,3,2,1,0:T(8,128)(2,1)S(1)}, u32[]{:S(2)}, u32[]{:S(2)}) collective-permute-start(bf16[2,2,2,24,896]{4,3,2,1,0:T(8,128)(2,1)S(1)} %fusion.91), channel_id=1, source_target_pairs={{0,1},{1,0},{2,3},{3,2},{4,5},{5,4},{6,7},{7,6},{8,9},{9,8},{10,11... | collective-permute-start | bytes 1032200 | tf_op jit(solution)/shard_map/ppermute | solution.py:318
  581.4 9.0 %collective-permute-start.14 = (bf16[2,2,24,768]{3,2,1,0:T(8,128)(2,1)S(1)}, bf16[2,2,24,768]{3,2,1,0:T(8,128)(2,1)S(1)}, u32[]{:S(2)}, u32[]{:S(2)}) collective-permute-start(bf16[2,2,24,768]{3,2,1,0:T(8,128)(2,1)S(1)} %fusion.110), channel_id=1, source_target_pairs={{0,1},{1,0},{2,3},{3,2},{4,5},{5,4},{6,7},{7,6},{8,9},{9,8},{10,11... | collective-permute-start | bytes 442376 | tf_op jit(solution)/shard_map/ppermute | solution.py:318
  585.0 6.1 collective-permute-start.10
  588.8 11.6 %copy-start.55 = (f32[2,96]{1,0:T(2,128)S(1)}, f32[2,96]{1,0:T(2,128)}, u32[]{:S(2)}) copy-start(f32[2,96]{1,0:T(2,128)} %param.26) | copy-start | bytes 2308
  588.8 11.6 %copy-start.57 = (f32[96]{0:T(128)S(1)}, f32[96]{0:T(128)}, u32[]{:S(2)}) copy-start(f32[96]{0:T(128)} %param.20) | copy-start | bytes 1156
  588.8 12.2 %copy-start.39 = (f32[1,24,8]{2,1,0:T(8,128)S(1)}, f32[1,24,8]{2,1,0:T(8,128)}, u32[]{:S(2)}) copy-start(f32[1,24,8]{2,1,0:T(8,128)} %copy.164) | copy-start | bytes 2308
  588.9 9.4 %collective-permute-start.6 = (bf16[2,2,24,896]{3,2,1,0:T(8,128)(2,1)S(1)}, bf16[2,2,24,896]{3,2,1,0:T(8,128)(2,1)S(1)}, u32[]{:S(2)}, u32[]{:S(2)}) collective-permute-start(bf16[2,2,24,896]{3,2,1,0:T(8,128)(2,1)S(1)} %fusion.106), channel_id=1, source_target_pairs={{0,4},{1,5},{2,6},{3,7},{4,0},{5,1},{6,2},{7,3},{8,12},{9,13},{10,... | collective-permute-start | bytes 516104 | tf_op jit(solution)/shard_map/ppermute | solution.py:318
  590.4 18.4 %copy-start.30 = (f32[2,24,2304]{2,1,0:T(8,128)S(1)}, f32[2,24,2304]{2,1,0:T(8,128)}, u32[]{:S(2)}) copy-start(f32[2,24,2304]{2,1,0:T(8,128)} %param.22) | copy-start | bytes 1327108
  590.4 4.8 collective-permute-start.15
  591.2 17.6 %copy-start.32 = (f32[24,2304]{1,0:T(8,128)S(1)}, f32[24,2304]{1,0:T(8,128)}, u32[]{:S(2)}) copy-start(f32[24,2304]{1,0:T(8,128)} %param.16) | copy-start | bytes 663556
  591.2 5.9 collective-permute-start.11
  595.2 5.0 collective-permute-start.16
  597.1 5.9 collective-permute-start.12
  598.4 5.3 collective-permute-start.7
  600.4 10.1 %copy-start.56 = (f32[96]{0:T(128)}, f32[96]{0:T(128)S(1)}, u32[]{:S(2)}) copy-start(f32[96]{0:T(128)S(1)} %reshape.357) | copy-start | bytes 1156
  603.7 5.0 collective-permute-start.8
  (29 other events, 89.0 us)
Sparse Core Ops, SparseCore 0:
  11.5 63.9 all-gather.2
  79.0 85.9 all-gather.4

commit v8 on v6

--- a/solution.py
+++ b/solution.py
@@ -421,11 +421,15 @@
     output = result.astype(jnp.bfloat16).reshape(inputs.shape)
 
     grad_result = cotangent.reshape(row_count, model_width)
-    grad_shrink_term = jnp.dot(activated.T, grad_result, preferred_element_type=jnp.float32)
+    grad_shrink_term = jnp.dot(
+        activated.T, grad_result, preferred_element_type=jnp.float32
+    ).astype(jnp.bfloat16)
     grad_down_bias = jnp.sum(grad_result.astype(jnp.float32), axis=0)
     grad_activated = jnp.dot(grad_result, full_shrink.T, preferred_element_type=jnp.float32)
     grad_preact = (grad_activated * gelu_slope(preact)).astype(jnp.bfloat16)
-    grad_expand_term = jnp.dot(hidden_second.T, grad_preact, preferred_element_type=jnp.float32)
+    grad_expand_term = jnp.dot(
+        hidden_second.T, grad_preact, preferred_element_type=jnp.float32
+    ).astype(jnp.bfloat16)
     grad_bias_term = jnp.sum(grad_preact.astype(jnp.float32), axis=0)
     grad_hidden_second = jnp.dot(grad_preact, full_expand.T, preferred_element_type=jnp.float32)
     norm_term_second, gain_second, shift_second = norm_backward(
@@ -433,7 +437,9 @@
     )
     grad_residual = grad_result.astype(jnp.float32) + norm_term_second
     grad_attended = grad_residual.astype(jnp.bfloat16)
-    grad_out_term = jnp.dot(mixed_low.T, grad_attended, preferred_element_type=jnp.float32)
+    grad_out_term = jnp.dot(
+        mixed_low.T, grad_attended, preferred_element_type=jnp.float32
+    ).astype(jnp.bfloat16)
     grad_out_bias = jnp.sum(grad_attended.astype(jnp.float32), axis=0)
     late_terms = jnp.concatenate(
         [grad_shrink_term.reshape(model_width, -1), grad_expand_term, grad_out_term], axis=1

time: 526 us -> 521 us (level)
  other arithmetic: 71.3 us -> 57.9 us
  local copies, waits for them, and re-layouts: 97.4 us -> 106 us
    dynamic_slice x0 -> x1, local copies, waits for them, and re-layouts: none -> 8.76 us  [tree_reduce_scatter(): lax.dynamic_index_in_dim(part, mine, axis=axis, keepdims=False)]
    concatenate x1, other arithmetic: 15.2 us -> 7.94 us  [body(): jnp.concatenate([grad_shrink_term.reshape(model_width, -1), grad_expand_t...]
    unnamed x136 -> x133, local copies, waits for them, and re-layouts: 15 us -> 21.8 us
    add x22, other arithmetic: 17.5 us -> 12.1 us  [tree_reduce_scatter(): keep + got.astype(jnp.float32)]
    convert_element_type x22 -> x21, local copies, waits for them, and re-layouts: 14.4 us -> 10.2 us  [tree_reduce_scatter(): lax.dynamic_index_in_dim(part, 1 - mine, axis=axis, keepdims=False)]
  transfers between devices with their start and end apart: 27 -> 27, of which waited for: 17 -> 17; matrix products, arithmetic and copies ran while one was open for 20% -> 21% of each run, Pallas kernels for 17% -> 17%
where the time goes in v8:
time: 521 us; the launch traced here: 516 us
  waiting for transfers between devices  147 us (28%)
  local copies, waits for them, and re-layouts  106 us (20%)
  Pallas kernels  89.6 us (17%)
  matrix products  70.5 us (14%)
  other arithmetic  57.9 us (11%)
  starting transfers between devices  30.4 us (6%)
  between operations  15.4 us (3%)
    pallas_call x2, Pallas kernels, attention_pallas(): pl.pallas_call(attention_backward_kernel, grid=(span,), in_specs=[qi_spec...  55.3 us
    ppermute x22, waiting for transfers between devices, tree_reduce_scatter(): got = lax.ppermute(send, ('clip', 'frame'), pairs)  44.9 us
    all_gather x1, waiting for transfers between devices, body(): second_full = lax.all_gather(second_pack, everyone, axis=0, tiled=True)  35.8 us
    pallas_call x1, Pallas kernels, attention_pallas(): pl.pallas_call(attention_forward_kernel, grid=(pair_count,), in_specs=[q_...  34.3 us
    all_gather x1, waiting for transfers between devices, body(): first_full = lax.all_gather(first_pack, everyone, axis=0, tiled=True)  29.1 us
    ppermute x1, waiting for transfers between devices, body(): lax.ppermute(inputs, 'frame', swap).reshape(row_count, model_width)  27.2 us
    ppermute x22, starting transfers between devices, tree_reduce_scatter(): got = lax.ppermute(send, ('clip', 'frame'), pairs)  25.3 us
    unnamed x133, local copies, waits for them, and re-layouts  21.8 us
  transfers between devices with their start and end apart: 27, of which 17 were waited for; matrix products, arithmetic and copies ran while one was open for 21% of the time, Pallas kernels for 17%

profile of v8, /device:TPU:0, one launch (start us, length us, event | category | flops | bytes accessed | tf_op | source)
XLA Modules:
  0.0 516.5 jit_solution(9579501307561245694)
XLA Ops:
  14.4 3.0 collective-permute-start
  18.2 27.2 %collective-permute-done = bf16[1,750,768]{2,1,0:T(8,128)(2,1)S(1)} collective-permute-done((bf16[1,750,768]{2,1,0:T(8,128)(2,1)S(1)}, bf16[1,750,768]{2,1,0:T(8,128)(2,1)S(1)}, u32[]{:S(2)}, u32[]{:S(2)}) %collective-permute-start) | collective-permute-done | bytes 1152032 | tf_op jit(solution)/shard_map/ppermute | solution.py:386
  46.4 29.1 %all-gather.3.cloned.1.call-done = bf16[768,2432]{1,0:T(8,128)(2,1)} async-done(((bf16[24,2432]{1,0:T(8,128)(2,1)}), bf16[768,2432]{1,0:T(8,128)(2,1)}) %all-gather.3.cloned.1.call-update) | async-done | bytes 3735568 | tf_op jit(solution)/shard_map/all_gather | solution.py:371
  77.4 1.8 slice_reduce_fusion
  79.3 6.0 %add_convert_fusion = bf16[750,2304]{1,0:T(8,128)(2,1)S(1)} fusion(f32[2304]{0:T(1024)S(1)} %pad_maximum_fusion.12, bf16[768,2432]{1,0:T(8,128)(2,1)} %all-gather.3.cloned.1.call-done, bf16[1,750,768]{2,1,0:T(8,128)(2,1)S(1)} %copy-done.5, f32[768]{0:T(1024)S(1)} %get-tuple-element.128, f32[768]{0:T(1024)S(1)} %get-tuple-element.129, ...), kind=kOutput, calls=%fused_computation.16 | convolution fusion | flops 2661120000 | bytes 8168304 | tf_op jit(solution)/shard_map/dot_general | solution.py:394
  85.4 1.7 copy-done.12
  89.0 2.1 add_convert_fusion.1
  91.1 2.7 fusion.8.k_ref.v_ref
  93.8 34.3 %shard_map.293 = (bf16[768,768]{1,0:T(8,128)(2,1)S(1)}, f32[768,768]{1,0:T(8,128)S(1)}) custom-call(bf16[768,768]{1,0:T(8,128)(2,1)S(1)} %pad.19.q_ref, bf16[1536,1536]{1,0:T(8,128)(2,1)} %fusion.8.k_ref.v_ref, bf16[1536,1536]{1,0:T(8,128)(2,1)} %fusion.8.k_ref.v_ref, f32[1,1536]{1,0:T(1,128)S(1)} %compare_select_fusion.kbias_ref), custom_call_target="tpu_custom_call" | custom-call | tf_op jit(solution)/shard_map/pallas_call | solution.py:157
  129.5 35.8 %all-gather.5.cloned.1.call-done = bf16[768,6912]{1,0:T(8,128)(2,1)} async-done(((bf16[24,6912]{1,0:T(8,128)(2,1)}), bf16[768,6912]{1,0:T(8,128)(2,1)}) %all-gather.5.cloned.1.call-update) | async-done | bytes 10616848 | tf_op jit(solution)/shard_map/all_gather | solution.py:372
  165.3 2.5 fusion.118
  169.6 4.8 slice.277
  174.4 8.5 %reshape.293 = bf16[3072,768]{1,0:T(8,128)(2,1)} reshape(bf16[768,3072]{1,0:T(8,128)(2,1)} %slice.277) | data formatting | bytes 9437184 | tf_op jit(solution)/shard_map/reshape | solution.py:379
  182.9 9.2 %multiply_convert_fusion = (bf16[750,3072]{1,0:T(8,128)(2,1)S(1)}, f32[750,3072]{1,0:T(8,128)}) fusion(f32[3072]{0:T(1024)S(1)} %copy-done.41, bf16[768,6912]{1,0:T(8,128)(2,1)} %all-gather.5.cloned.1.call-done, f32[750,768]{1,0:T(8,128)} %copy-done.9, f32[768]{0:T(1024)} %get-tuple-element.123, f32[768]{0:T(1024)S(1)} %get-tuple-element.124, ...), kind=kOutput, calls=%fused_computation.13 | convolution fusion | flops 3555648000 | bytes 20878192 | tf_op jit(solution)/shard_map/dot_general | solution.py:414
  192.1 2.1 copy-done.53
  194.2 5.7 %convolution_convert_fusion.1 = bf16[3072,768]{1,0:T(8,128)(2,1)} fusion(bf16[750,3072]{1,0:T(8,128)(2,1)S(1)} %get-tuple-element.167, bf16[1,750,768]{2,1,0:T(8,128)(2,1)S(1)} %copy-done.24), kind=kOutput, calls=%fused_computation.20 | convolution fusion | flops 3541303296 | bytes 10478592 | tf_op jit(solution)/shard_map/dot_general | solution.py:424
  199.9 8.5 %concatenate.80 = bf16[2,2,2,2,2,24,3072]{6,5,4,3,2,1,0:T(8,128)(2,1)} reshape(bf16[3072,768]{1,0:T(8,128)(2,1)} %convolution_convert_fusion.1) | data formatting | bytes 9437184 | tf_op jit(solution)/shard_map/concatenate | solution.py:444
  208.4 10.7 %convert_reduce_fusion = (f32[3072]{0:T(1024)}, bf16[750,3072]{1,0:T(8,128)(2,1)S(1)}) fusion(f32[750,3072]{1,0:T(8,128)} %get-tuple-element.168, f32[3072]{0:T(1024)S(1)} %copy-done.41, bf16[3072,768]{1,0:T(8,128)(2,1)} %reshape.293, bf16[1,750,768]{2,1,0:T(8,128)(2,1)} %param.15), kind=kOutput, calls=%fused_computation.12 | convolution fusion | flops 3568892928 | bytes 19719168 | tf_op jit(solution)/shard_map/dot_general | solution.py:428
  219.2 5.1 convolution_convert_fusion
  224.3 7.4 %multiply_reduce_fusion = (f32[768]{0:T(1024)}, f32[750]{0:T(1024)S(1)}, f32[750]{0:T(1024)S(1)}, f32[768]{0:T(1024)}, f32[750,768]{1,0:T(8,128)S(1)}) fusion(f32[750,768]{1,0:T(8,128)S(1)} %copy-done.10, f32[750]{0:T(1024)S(1)} %add_rsqrt_fusion, f32[750]{0:T(1024)S(1)} %broadcast_multiply_fusion.4, f32[768]{0:T(1024)S(1)} %get-tuple-element.124, ...), kind=kOutput, calls=%fused_computation.81 | convolution fusion | flops 3544124928 | bytes 13955808 | tf_op jit(solution)/shard_map/dot_general | solution.py:434
  231.7 1.8 convert_reduce_fusion.5
  234.9 7.9 %pad_maximum_fusion = bf16[2,2,2,2,2,24,6912]{6,5,4,3,2,1,0:T(8,128)(2,1)} fusion(bf16[2,2,2,2,2,24,768]{6,5,4,3,2,1,0:T(8,128)(2,1)S(1)} %bitcast.282, bf16[2,2,2,2,2,24,3072]{6,5,4,3,2,1,0:T(8,128)(2,1)S(1)} %bitcast.280, bf16[2,2,2,2,2,24,3072]{6,5,4,3,2,1,0:T(8,128)(2,1)S(1)} %bitcast.275), kind=kLoop, calls=%fused_computation.1 | loop fusion | flops 31850496 | bytes 21233664 | tf_op jit(solution)/shard_map/concatenate | solution.py:444
  242.8 8.8 %constant_dynamic-slice_fusion.1 = (bf16[2,2,2,1,2,24,6912]{6,5,4,3,2,1,0:T(8,128)(2,1)}, bf16[2,2,2,1,2,24,6912]{6,5,4,3,2,1,0:T(8,128)(2,1)}) fusion(bf16[2,2,2,2,2,24,6912]{6,5,4,3,2,1,0:T(8,128)(2,1)} %pad_maximum_fusion, s32[]{:T(128)S(6)} %select_n.99, s32[]{:T(128)S(6)} %select_n.100), kind=kLoop, calls=%fused_computation.225 | loop fusion | bytes 21233672 | tf_op jit(solution)/shard_map/jit(dynamic_index_in_dim)/dynamic_slice | solution.py:309
  251.6 5.3 %copy.94 = bf16[2,2,2,1,2,24,6912]{6,5,0,4,2,1,3:T(8,128)(2,1)} copy(bf16[2,2,2,1,2,24,6912]{6,5,4,3,2,1,0:T(8,128)(2,1)} %get-tuple-element.141) | data formatting | bytes 10616832
  256.9 2.4 convolution_convert_fusion.3
  260.6 27.7 %shard_map.294 = (f32[768,384]{1,0:T(8,128)S(1)}, f32[1536,384]{1,0:T(8,128)S(1)}, f32[1536,384]{1,0:T(8,128)}) custom-call(bf16[768,768]{1,0:T(8,128)(2,1)S(1)} %pad.19.q_ref, bf16[1536,1536]{1,0:T(8,128)(2,1)} %fusion.8.k_ref.v_ref, bf16[1536,1536]{1,0:T(8,128)(2,1)} %fusion.8.k_ref.v_ref, bf16[768,768]{1,0:T(8,128)(2,1)S(1)} %pad.21.do_ref, ...), custom_call_target="tpu_custom_call" | custom-call | tf_op jit(solution)/shard_map/pallas_call | solution.py:176
  291.0 1.6 slice.227
  295.0 5.3 %convert_add_fusion = f32[2,2,2,2,24,6912]{5,4,0,3,2,1:T(8,128)S(1)} fusion(bf16[2,2,2,2,24,6912]{5,4,0,3,2,1:T(8,128)(2,1)} %collective-permute-done.1, bf16[2,2,2,1,2,24,6912]{6,5,4,3,2,1,0:T(8,128)(2,1)} %get-tuple-element.140), kind=kLoop, calls=%fused_computation.2 | loop fusion | flops 7962624 | bytes 21233664 | tf_op jit(solution)/shard_map/add | solution.py:319
  300.3 4.8 fusion.114
  305.1 3.0 fusion.53
  308.0 3.0 fusion.52
  312.5 27.6 %shard_map.295 = (f32[768,384]{1,0:T(8,128)S(1)}, f32[1536,384]{1,0:T(8,128)S(1)}, f32[1536,384]{1,0:T(8,128)}) custom-call(bf16[768,768]{1,0:T(8,128)(2,1)S(1)} %pad.19.q_ref, bf16[1536,1536]{1,0:T(8,128)(2,1)} %fusion.8.k_ref.v_ref, bf16[1536,1536]{1,0:T(8,128)(2,1)} %fusion.8.k_ref.v_ref, bf16[768,768]{1,0:T(8,128)(2,1)S(1)} %pad.22.do_ref, ...), custom_call_target="tpu_custom_call" | custom-call | tf_op jit(solution)/shard_map/pallas_call | solution.py:176
  340.4 2.7 slice.233
  346.3 7.1 %fusion.51 = bf16[1,750,768]{2,1,0:T(8,128)(2,1)} fusion(f32[750,768]{1,0:T(8,128)S(1)} %copy-done.11, bf16[750,3072]{1,0:T(8,128)(2,1)} %copy-done.53, bf16[3072,768]{1,0:T(8,128)(2,1)S(1)} %bitcast.279, f32[768]{0:T(1024)S(1)} %copy-done.45), kind=kOutput, calls=%fused_computation.93 | convolution fusion | flops 3540672000 | bytes 12785664 | tf_op jit(solution)/shard_map/dot_general | solution.py:418
  361.1 1.7 fusion.48
  362.9 9.6 %collective-permute-done.3 = bf16[750,768]{1,0:T(8,128)(2,1)} collective-permute-done((bf16[750,768]{1,0:T(8,128)(2,1)}, bf16[750,768]{1,0:T(8,128)(2,1)}, u32[]{:S(2)}, u32[]{:S(2)}) %collective-permute-start.3) | collective-permute-done | bytes 1152032 | tf_op jit(solution)/shard_map/ppermute | solution.py:479
  375.0 2.6 copy-done.43
  377.6 2.9 fusion.15
  380.5 2.2 fusion.34
  382.8 2.6 copy.68
  385.4 8.2 %fusion.13 = f32[2,2,2,2,2,24,2304]{6,5,4,3,2,1,0:T(8,128)} fusion(bf16[2,2,2,2,2,24,750]{6,5,4,3,2,1,0:T(8,128)(2,1)} %bitcast.281, bf16[750,2304]{1,0:T(8,128)(2,1)} %copy-done.15), kind=kOutput, calls=%fused_computation.31 | convolution fusion | flops 2654208000 | bytes 11685888 | tf_op jit(solution)/shard_map/dot_general | solution.py:497
  398.5 10.1 %concatenate.98 = f32[2,2,2,2,2,24,2432]{6,5,4,3,2,1,0:T(8,128)} concatenate(f32[2,2,2,2,2,24,2304]{6,5,4,3,2,1,0:T(8,128)} %fusion.13, f32[2,2,2,2,2,24,1]{6,5,4,3,2,1,0:T(8,128)} %concatenate.102, f32[2,2,2,2,2,24,1]{6,5,4,3,2,1,0:T(8,128)} %concatenate.103, f32[2,2,2,2,2,24,1]{6,5,4,3,2,1,0:T(8,128)} %concatenate.104, f32[2,2,2,2,2,24,1]{6,5,4,3,2,1,0:T(8,128)} %concatenate.105, ...), dimensions={6} | concatenate | bytes 14942208 | tf_op jit(solution)/shard_map/concatenate | solution.py:528
  408.6 3.7 fusion.50
  412.3 1.8 fusion.56
  414.1 2.5 bitcast_add_fusion.2
  417.3 1.6 bitcast_add_fusion.1
  420.3 13.7 %collective-permute-done.18 = bf16[2,2,24,3456]{3,2,0,1:T(8,128)(2,1)S(1)} collective-permute-done((bf16[2,2,24,3456]{3,2,0,1:T(8,128)(2,1)S(1)}, bf16[2,2,24,3456]{3,2,0,1:T(8,128)(2,1)S(1)}, u32[]{:S(2)}, u32[]{:S(2)}) %collective-permute-start.18) | collective-permute-done | bytes 663584 | tf_op jit(solution)/shard_map/ppermute | solution.py:318
  437.8 7.2 %collective-permute-done.19 = bf16[2,24,3456]{2,1,0:T(8,128)(2,1)S(1)} collective-permute-done((bf16[2,24,3456]{2,1,0:T(8,128)(2,1)S(1)}, bf16[2,24,3456]{2,1,0:T(8,128)(2,1)S(1)}, u32[]{:S(2)}, u32[]{:S(2)}) %collective-permute-start.19) | collective-permute-done | bytes 331808 | tf_op jit(solution)/shard_map/ppermute | solution.py:318
  445.1 1.8 collective-permute-start.20
  446.9 3.9 collective-permute-done.23
  450.9 1.8 collective-permute-start.24
  453.4 7.1 %collective-permute-done.24 = bf16[24,3456]{1,0:T(8,128)(2,1)S(1)} collective-permute-done((bf16[24,3456]{1,0:T(8,128)(2,1)S(1)}, bf16[24,3456]{1,0:T(8,128)(2,1)S(1)}, u32[]{:S(2)}, u32[]{:S(2)}) %collective-permute-start.24) | collective-permute-done | bytes 165920 | tf_op jit(solution)/shard_map/ppermute | solution.py:318
  461.4 1.8 reshape.297
  463.2 1.8 reshape.299
  468.9 2.2 fusion.83
  471.0 2.0 fusion.95
  473.9 1.8 bitcast_add_fusion
  479.1 5.2 %collective-permute-done.13 = bf16[2,2,2,24,768]{4,3,2,1,0:T(8,128)(2,1)S(1)} collective-permute-done((bf16[2,2,2,24,768]{4,3,2,1,0:T(8,128)(2,1)S(1)}, bf16[2,2,2,24,768]{4,3,2,1,0:T(8,128)(2,1)S(1)}, u32[]{:S(2)}, u32[]{:S(2)}) %collective-permute-start.13) | collective-permute-done | bytes 294944 | tf_op jit(solution)/shard_map/ppermute | solution.py:318
  485.4 1.8 collective-permute-start.10
  488.1 1.9 collective-permute-start.6
  492.3 2.5 collective-permute-done.15
  494.9 1.7 collective-permute-start.16
  498.0 1.7 collective-permute-start.7
  502.6 1.8 collective-permute-start.8
  (293 shorter events, 72.6 us)
Async XLA Ops:
  7.2 7.2 %copy-start.5 = (bf16[1,750,768]{2,1,0:T(8,128)(2,1)S(1)}, bf16[1,750,768]{2,1,0:T(8,128)(2,1)}, u32[]{:S(2)}) copy-start(bf16[1,750,768]{2,1,0:T(8,128)(2,1)} %param.14) | copy-start | bytes 3456004
  7.2 68.3 %all-gather.3.cloned.1.call-start = ((), (), s32[]{:S(2)}) async-start(), calls=%async_computation | async-start | bytes 3852288 | tf_op jit(solution)/shard_map/all_gather | solution.py:371
  10.6 154.7 %all-gather.5.cloned.1.call-start = ((), (), s32[]{:S(2)}) async-start(), calls=%async_computation.1 | async-start | bytes 10948608 | tf_op jit(solution)/shard_map/all_gather | solution.py:372
  14.4 31.0 %collective-permute-start = (bf16[1,750,768]{2,1,0:T(8,128)(2,1)S(1)}, bf16[1,750,768]{2,1,0:T(8,128)(2,1)S(1)}, u32[]{:S(2)}, u32[]{:S(2)}) collective-permute-start(bf16[1,750,768]{2,1,0:T(8,128)(2,1)S(1)} %copy-done.5), channel_id=1, source_target_pairs={{0,1},{1,0},{2,3},{3,2},{4,5},{5,4},{6,7},{7,6},{8,9},{9,8},{10,11... | collective-permute-start | bytes 3456008 | tf_op jit(solution)/shard_map/ppermute | solution.py:386
  18.2 61.1 %copy-start.33 = (f32[750]{0:T(1024)}, f32[750]{0:T(1024)S(1)}, u32[]{:S(2)}) copy-start(f32[750]{0:T(1024)S(1)} %add_rsqrt_fusion.2) | copy-start | bytes 9004
  79.2 8.0 %copy-start.37 = (f32[768]{0:T(1024)}, f32[768]{0:T(1024)S(1)}, u32[]{:S(2)}) copy-start(f32[768]{0:T(1024)S(1)} %get-tuple-element.128) | copy-start | bytes 9220
  85.3 3.7 copy-start.18
  93.8 71.5 %copy-start.49 = (f32[768]{0:T(1024)S(1)}, f32[768]{0:T(1024)}, u32[]{:S(2)}) copy-start(f32[768]{0:T(1024)} %get-tuple-element.125) | copy-start | bytes 9220
  174.4 8.5 %copy-start.41 = (f32[3072]{0:T(1024)S(1)}, f32[3072]{0:T(1024)}, u32[]{:S(2)}) copy-start(f32[3072]{0:T(1024)} %add.407) | copy-start | bytes 36868
  182.9 11.3 %copy-start.24 = (bf16[1,750,768]{2,1,0:T(8,128)(2,1)S(1)}, bf16[1,750,768]{2,1,0:T(8,128)(2,1)}, u32[]{:S(2)}) copy-start(bf16[1,750,768]{2,1,0:T(8,128)(2,1)} %param.15) | copy-start | bytes 3456004
  208.4 10.8 %copy-start.10 = (f32[750,768]{1,0:T(8,128)S(1)}, f32[750,768]{1,0:T(8,128)}, u32[]{:S(2)}) copy-start(f32[750,768]{1,0:T(8,128)} %copy-done.9) | copy-start | bytes 6912004
  208.4 10.8 %copy-start.48 = (f32[768]{0:T(1024)S(1)}, f32[768]{0:T(1024)}, u32[]{:S(2)}) copy-start(f32[768]{0:T(1024)} %get-tuple-element.123) | copy-start | bytes 9220
  224.3 7.4 %copy-start.25 = (bf16[1,750,768]{2,1,0:T(8,128)(2,1)S(1)}, bf16[1,750,768]{2,1,0:T(8,128)(2,1)}, u32[]{:S(2)}) copy-start(bf16[1,750,768]{2,1,0:T(8,128)(2,1)} %param.15) | copy-start | bytes 3456004
  251.6 5.3 %copy-start.7 = (f32[750,768]{1,0:T(8,128)S(1)}, f32[750,768]{1,0:T(8,128)}, u32[]{:S(2)}) copy-start(f32[750,768]{1,0:T(8,128)} %copy-done.6) | copy-start | bytes 6912004
  259.3 35.6 %collective-permute-start.1 = (bf16[2,2,2,2,24,6912]{5,4,0,3,2,1:T(8,128)(2,1)}, bf16[2,2,2,2,24,6912]{5,4,0,3,2,1:T(8,128)(2,1)}, u32[]{:S(2)}, u32[]{:S(2)}) collective-permute-start(bf16[2,2,2,2,24,6912]{5,4,0,3,2,1:T(8,128)(2,1)} %bitcast.271), channel_id=1, source_target_pairs={{0,2},{1,3},{2,0},{3,1},{4,6},{5,7},{6,4},{7,5},{8,10},{9,11},{10,... | collective-permute-start | bytes 15925256 | tf_op jit(solution)/shard_map/ppermute | solution.py:318
  311.0 50.0 %collective-permute-start.2 = (bf16[750,768]{1,0:T(8,128)(2,1)}, bf16[750,768]{1,0:T(8,128)(2,1)}, u32[]{:S(2)}, u32[]{:S(2)}) collective-permute-start(bf16[750,768]{1,0:T(8,128)(2,1)} %pad_maximum_fusion.3), channel_id=1, source_target_pairs={{0,1},{1,0},{2,3},{3,2},{4,5},{5,4},{6,7},{7,6},{8,9},{9,8},{10,11... | collective-permute-start | bytes 3456008 | tf_op jit(solution)/shard_map/ppermute | solution.py:479
  340.2 5.3 %slice-start.7 = ((s8[4718592]{0:T(1024)(128)(4,1)}), s8[4194304]{0:T(1024)(128)(4,1)S(1)}, s32[]{:S(2)}) async-start(s8[4718592]{0:T(1024)(128)(4,1)} %bitcast.278), calls=%async_computation.9 | async-start | bytes 8388608
  340.3 5.1 slice-start.8
  344.9 27.6 %collective-permute-start.3 = (bf16[750,768]{1,0:T(8,128)(2,1)}, bf16[750,768]{1,0:T(8,128)(2,1)}, u32[]{:S(2)}, u32[]{:S(2)}) collective-permute-start(bf16[750,768]{1,0:T(8,128)(2,1)} %fusion.46), channel_id=1, source_target_pairs={{0,1},{1,0},{2,3},{3,2},{4,5},{5,4},{6,7},{7,6},{8,9},{9,8},{10,11... | collective-permute-start | bytes 3456008 | tf_op jit(solution)/shard_map/ppermute | solution.py:479
  346.3 7.1 %copy-start.40 = (f32[3072]{0:T(1024)S(1)}, f32[3072]{0:T(1024)}, u32[]{:S(2)}) copy-start(f32[3072]{0:T(1024)} %get-tuple-element.170) | copy-start | bytes 36868
  346.3 8.3 %copy-start.36 = (f32[768]{0:T(1024)S(1)}, f32[768]{0:T(1024)}, u32[]{:S(2)}) copy-start(f32[768]{0:T(1024)} %get-tuple-element.136) | copy-start | bytes 9220
  346.3 9.3 %copy-start.47 = (f32[768]{0:T(1024)S(1)}, f32[768]{0:T(1024)}, u32[]{:S(2)}) copy-start(f32[768]{0:T(1024)} %get-tuple-element.114) | copy-start | bytes 9220
  346.3 10.4 %copy-start.35 = (f32[768]{0:T(1024)S(1)}, f32[768]{0:T(1024)}, u32[]{:S(2)}) copy-start(f32[768]{0:T(1024)} %get-tuple-element.145) | copy-start | bytes 9220
  346.3 11.4 %copy-start.46 = (f32[768]{0:T(1024)S(1)}, f32[768]{0:T(1024)}, u32[]{:S(2)}) copy-start(f32[768]{0:T(1024)} %get-tuple-element.120) | copy-start | bytes 9220
  353.4 7.4 %copy-start.19 = (f32[750,384]{1,0:T(8,128)S(1)}, f32[750,384]{1,0:T(8,128)}, u32[]{:S(2)}) copy-start(f32[750,384]{1,0:T(8,128)} %slice.225) | copy-start | bytes 3456004
  358.8 55.3 %collective-permute-start.17 = (bf16[2,2,2,24,3456]{4,3,0,2,1:T(8,128)(2,1)}, bf16[2,2,2,24,3456]{4,3,0,2,1:T(8,128)(2,1)}, u32[]{:S(2)}, u32[]{:S(2)}) collective-permute-start(bf16[2,2,2,24,3456]{4,3,0,2,1:T(8,128)(2,1)} %fusion.53), channel_id=1, source_target_pairs={{0,8},{1,9},{2,10},{3,11},{4,12},{5,13},{6,14},{7,15},{8,0},{9,1},... | collective-permute-start | bytes 3981320 | tf_op jit(solution)/shard_map/ppermute | solution.py:318
  360.2 57.1 %collective-permute-start.21 = (bf16[2,2,2,24,3456]{4,3,0,2,1:T(8,128)(2,1)}, bf16[2,2,2,24,3456]{4,3,0,2,1:T(8,128)(2,1)}, u32[]{:S(2)}, u32[]{:S(2)}) collective-permute-start(bf16[2,2,2,24,3456]{4,3,0,2,1:T(8,128)(2,1)} %fusion.52), channel_id=1, source_target_pairs={{0,4},{1,5},{2,6},{3,7},{4,0},{5,1},{6,2},{7,3},{8,12},{9,13},{10,... | collective-permute-start | bytes 3981320 | tf_op jit(solution)/shard_map/ppermute | solution.py:318
  360.9 11.6 %copy-start.2 = (f32[1500,384]{1,0:T(8,128)S(1)}, f32[1500,384]{1,0:T(8,128)}, u32[]{:S(2)}) copy-start(f32[1500,384]{1,0:T(8,128)} %copy-done.1) | copy-start | bytes 6912004
  361.0 11.6 %copy-start.4 = (f32[1500,384]{1,0:T(8,128)S(1)}, f32[1500,384]{1,0:T(8,128)}, u32[]{:S(2)}) copy-start(f32[1500,384]{1,0:T(8,128)} %copy-done.3) | copy-start | bytes 6912004
  374.4 6.1 %copy-start.15 = (bf16[750,2304]{1,0:T(8,128)(2,1)}, bf16[750,2304]{1,0:T(8,128)(2,1)S(1)}, u32[]{:S(2)}) copy-start(bf16[750,2304]{1,0:T(8,128)(2,1)S(1)} %slice_dynamic-update-slice_fusion) | copy-start | bytes 10368004
  412.2 61.7 %collective-permute-start.4 = (bf16[2,2,2,2,24,2432]{5,4,3,2,1,0:T(8,128)(2,1)}, bf16[2,2,2,2,24,2432]{5,4,3,2,1,0:T(8,128)(2,1)}, u32[]{:S(2)}, u32[]{:S(2)}) collective-permute-start(bf16[2,2,2,2,24,2432]{5,4,3,2,1,0:T(8,128)(2,1)} %fusion.50), channel_id=1, source_target_pairs={{0,2},{1,3},{2,0},{3,1},{4,6},{5,7},{6,4},{7,5},{8,10},{9,11},{10,... | collective-permute-start | bytes 5603336 | tf_op jit(solution)/shard_map/ppermute | solution.py:318
  412.3 5.1 slice-start.4
  416.7 17.4 %collective-permute-start.18 = (bf16[2,2,24,3456]{3,2,0,1:T(8,128)(2,1)S(1)}, bf16[2,2,24,3456]{3,2,0,1:T(8,128)(2,1)S(1)}, u32[]{:S(2)}, u32[]{:S(2)}) collective-permute-start(bf16[2,2,24,3456]{3,2,0,1:T(8,128)(2,1)S(1)} %fusion.67), channel_id=1, source_target_pairs={{0,4},{1,5},{2,6},{3,7},{4,0},{5,1},{6,2},{7,3},{8,12},{9,13},{10,... | collective-permute-start | bytes 1990664 | tf_op jit(solution)/shard_map/ppermute | solution.py:318
  419.0 17.1 %collective-permute-start.22 = (bf16[2,2,24,3456]{3,2,0,1:T(8,128)(2,1)S(1)}, bf16[2,2,24,3456]{3,2,0,1:T(8,128)(2,1)S(1)}, u32[]{:S(2)}, u32[]{:S(2)}) collective-permute-start(bf16[2,2,24,3456]{3,2,0,1:T(8,128)(2,1)S(1)} %fusion.68), channel_id=1, source_target_pairs={{0,8},{1,9},{2,10},{3,11},{4,12},{5,13},{6,14},{7,15},{8,0},{9,1},... | collective-permute-start | bytes 1990664 | tf_op jit(solution)/shard_map/ppermute | solution.py:318
  434.2 10.8 %collective-permute-start.19 = (bf16[2,24,3456]{2,1,0:T(8,128)(2,1)S(1)}, bf16[2,24,3456]{2,1,0:T(8,128)(2,1)S(1)}, u32[]{:S(2)}, u32[]{:S(2)}) collective-permute-start(bf16[2,24,3456]{2,1,0:T(8,128)(2,1)S(1)} %fusion.70), channel_id=1, source_target_pairs={{0,1},{1,0},{2,3},{3,2},{4,5},{5,4},{6,7},{7,6},{8,9},{9,8},{10,11... | collective-permute-start | bytes 995336 | tf_op jit(solution)/shard_map/ppermute | solution.py:318
  436.3 14.5 %collective-permute-start.23 = (bf16[2,24,3456]{2,1,0:T(8,128)(2,1)S(1)}, bf16[2,24,3456]{2,1,0:T(8,128)(2,1)S(1)}, u32[]{:S(2)}, u32[]{:S(2)}) collective-permute-start(bf16[2,24,3456]{2,1,0:T(8,128)(2,1)S(1)} %fusion.71), channel_id=1, source_target_pairs={{0,1},{1,0},{2,3},{3,2},{4,5},{5,4},{6,7},{7,6},{8,9},{9,8},{10,11... | collective-permute-start | bytes 995336 | tf_op jit(solution)/shard_map/ppermute | solution.py:318
  445.1 15.4 %copy-start.21 = (f32[2,24,3072]{2,1,0:T(8,128)S(1)}, f32[2,24,3072]{2,1,0:T(8,128)}, u32[]{:S(2)}) copy-start(f32[2,24,3072]{2,1,0:T(8,128)} %param.24) | copy-start | bytes 1769476
  445.1 8.2 %collective-permute-start.20 = (bf16[24,3456]{1,0:T(8,128)(2,1)S(1)}, bf16[24,3456]{1,0:T(8,128)(2,1)S(1)}, u32[]{:S(2)}, u32[]{:S(2)}) collective-permute-start(bf16[24,3456]{1,0:T(8,128)(2,1)S(1)} %fusion.86), channel_id=1, source_target_pairs={{0,16},{1,17},{2,18},{3,19},{4,20},{5,21},{6,22},{7,23},{8,24},{9,... | collective-permute-start | bytes 497672 | tf_op jit(solution)/shard_map/ppermute | solution.py:318
  450.8 23.1 %slice-start = ((s8[7471104]{0:T(1024)(128)(4,1)}), s8[3276800]{0:T(1024)(128)(4,1)S(1)}, s32[]{:S(2)}) async-start(s8[7471104]{0:T(1024)(128)(4,1)} %bitcast.272), calls=%async_computation.2 | async-start | bytes 6553600
  450.9 9.5 %collective-permute-start.24 = (bf16[24,3456]{1,0:T(8,128)(2,1)S(1)}, bf16[24,3456]{1,0:T(8,128)(2,1)S(1)}, u32[]{:S(2)}, u32[]{:S(2)}) collective-permute-start(bf16[24,3456]{1,0:T(8,128)(2,1)S(1)} %fusion.87), channel_id=1, source_target_pairs={{0,16},{1,17},{2,18},{3,19},{4,20},{5,21},{6,22},{7,23},{8,24},{9,... | collective-permute-start | bytes 497672 | tf_op jit(solution)/shard_map/ppermute | solution.py:318
  453.3 8.1 %copy-start.20 = (f32[24,3456]{1,0:T(8,128)}, f32[24,3456]{1,0:T(8,128)S(1)}, u32[]{:S(2)}) copy-start(f32[24,3456]{1,0:T(8,128)S(1)} %bitcast_add_fusion.12) | copy-start | bytes 995332
  461.4 5.8 %copy-start.29 = (f32[2,24,768]{2,1,0:T(8,128)S(1)}, f32[2,24,768]{2,1,0:T(8,128)}, u32[]{:S(2)}) copy-start(f32[2,24,768]{2,1,0:T(8,128)} %param.23) | copy-start | bytes 442372
  461.4 6.7 %copy-start.30 = (f32[24,768]{1,0:T(8,128)S(1)}, f32[24,768]{1,0:T(8,128)}, u32[]{:S(2)}) copy-start(f32[24,768]{1,0:T(8,128)} %param.17) | copy-start | bytes 221188
  465.0 6.0 %copy-start.22 = (f32[2,24,3072]{2,1,0:T(8,128)S(1)}, f32[2,24,3072]{2,1,0:T(8,128)}, u32[]{:S(2)}) copy-start(f32[2,24,3072]{2,1,0:T(8,128)} %param.24) | copy-start | bytes 1769476
  465.0 8.9 %slice-start.1 = ((s8[7471104]{0:T(1024)(128)(4,1)}), s8[4194304]{0:T(1024)(128)(4,1)S(1)}, s32[]{:S(2)}) async-start(s8[7471104]{0:T(1024)(128)(4,1)} %bitcast.272), calls=%async_computation.3 | async-start | bytes 8388608
  466.4 6.7 %copy-start.23 = (f32[1,24,3072]{2,1,0:T(8,128)S(1)}, f32[1,24,3072]{2,1,0:T(8,128)}, u32[]{:S(2)}) copy-start(f32[1,24,3072]{2,1,0:T(8,128)} %get-tuple-element.130) | copy-start | bytes 884740
  476.1 8.3 %collective-permute-start.13 = (bf16[2,2,2,24,768]{4,3,2,1,0:T(8,128)(2,1)S(1)}, bf16[2,2,2,24,768]{4,3,2,1,0:T(8,128)(2,1)S(1)}, u32[]{:S(2)}, u32[]{:S(2)}) collective-permute-start(bf16[2,2,2,24,768]{4,3,2,1,0:T(8,128)(2,1)S(1)} %fusion.81), channel_id=1, source_target_pairs={{0,8},{1,9},{2,10},{3,11},{4,12},{5,13},{6,14},{7,15},{8,0},{9,1},... | collective-permute-start | bytes 884744 | tf_op jit(solution)/shard_map/ppermute | solution.py:318
  477.0 8.3 %collective-permute-start.9 = (bf16[2,2,2,24,768]{4,3,2,1,0:T(8,128)(2,1)S(1)}, bf16[2,2,2,24,768]{4,3,2,1,0:T(8,128)(2,1)S(1)}, u32[]{:S(2)}, u32[]{:S(2)}) collective-permute-start(bf16[2,2,2,24,768]{4,3,2,1,0:T(8,128)(2,1)S(1)} %fusion.80), channel_id=1, source_target_pairs={{0,4},{1,5},{2,6},{3,7},{4,0},{5,1},{6,2},{7,3},{8,12},{9,13},{10,... | collective-permute-start | bytes 884744 | tf_op jit(solution)/shard_map/ppermute | solution.py:318
  477.7 10.3 %collective-permute-start.5 = (bf16[2,2,2,24,896]{4,3,2,1,0:T(8,128)(2,1)S(1)}, bf16[2,2,2,24,896]{4,3,2,1,0:T(8,128)(2,1)S(1)}, u32[]{:S(2)}, u32[]{:S(2)}) collective-permute-start(bf16[2,2,2,24,896]{4,3,2,1,0:T(8,128)(2,1)S(1)} %fusion.69), channel_id=1, source_target_pairs={{0,1},{1,0},{2,3},{3,2},{4,5},{5,4},{6,7},{7,6},{8,9},{9,8},{10,11... | collective-permute-start | bytes 1032200 | tf_op jit(solution)/shard_map/ppermute | solution.py:318
  484.5 5.5 %collective-permute-start.14 = (bf16[2,2,24,768]{3,2,1,0:T(8,128)(2,1)S(1)}, bf16[2,2,24,768]{3,2,1,0:T(8,128)(2,1)S(1)}, u32[]{:S(2)}, u32[]{:S(2)}) collective-permute-start(bf16[2,2,24,768]{3,2,1,0:T(8,128)(2,1)S(1)} %fusion.89), channel_id=1, source_target_pairs={{0,1},{1,0},{2,3},{3,2},{4,5},{5,4},{6,7},{7,6},{8,9},{9,8},{10,11... | collective-permute-start | bytes 442376 | tf_op jit(solution)/shard_map/ppermute | solution.py:318
  485.4 6.1 %collective-permute-start.10 = (bf16[2,2,24,768]{3,2,1,0:T(8,128)(2,1)S(1)}, bf16[2,2,24,768]{3,2,1,0:T(8,128)(2,1)S(1)}, u32[]{:S(2)}, u32[]{:S(2)}) collective-permute-start(bf16[2,2,24,768]{3,2,1,0:T(8,128)(2,1)S(1)} %fusion.88), channel_id=1, source_target_pairs={{0,8},{1,9},{2,10},{3,11},{4,12},{5,13},{6,14},{7,15},{8,0},{9,1},... | collective-permute-start | bytes 442376 | tf_op jit(solution)/shard_map/ppermute | solution.py:318
  488.0 12.1 %copy-start.50 = (f32[2,96]{1,0:T(2,128)S(1)}, f32[2,96]{1,0:T(2,128)}, u32[]{:S(2)}) copy-start(f32[2,96]{1,0:T(2,128)} %param.26) | copy-start | bytes 2308
  488.0 12.1 %copy-start.52 = (f32[96]{0:T(128)S(1)}, f32[96]{0:T(128)}, u32[]{:S(2)}) copy-start(f32[96]{0:T(128)} %param.20) | copy-start | bytes 1156
  488.0 12.6 %copy-start.32 = (f32[1,24,8]{2,1,0:T(8,128)S(1)}, f32[1,24,8]{2,1,0:T(8,128)}, u32[]{:S(2)}) copy-start(f32[1,24,8]{2,1,0:T(8,128)} %copy.88) | copy-start | bytes 2308
  488.1 9.9 %collective-permute-start.6 = (bf16[2,2,24,896]{3,2,1,0:T(8,128)(2,1)S(1)}, bf16[2,2,24,896]{3,2,1,0:T(8,128)(2,1)S(1)}, u32[]{:S(2)}, u32[]{:S(2)}) collective-permute-start(bf16[2,2,24,896]{3,2,1,0:T(8,128)(2,1)S(1)} %fusion.85), channel_id=1, source_target_pairs={{0,4},{1,5},{2,6},{3,7},{4,0},{5,1},{6,2},{7,3},{8,12},{9,13},{10,... | collective-permute-start | bytes 516104 | tf_op jit(solution)/shard_map/ppermute | solution.py:318
  490.0 17.6 %copy-start.26 = (f32[2,24,2304]{2,1,0:T(8,128)S(1)}, f32[2,24,2304]{2,1,0:T(8,128)}, u32[]{:S(2)}) copy-start(f32[2,24,2304]{2,1,0:T(8,128)} %param.22) | copy-start | bytes 1327108
  490.0 4.8 collective-permute-start.15
  491.5 16.2 %copy-start.28 = (f32[24,2304]{1,0:T(8,128)S(1)}, f32[24,2304]{1,0:T(8,128)}, u32[]{:S(2)}) copy-start(f32[24,2304]{1,0:T(8,128)} %param.16) | copy-start | bytes 663556
  491.6 5.0 collective-permute-start.11
  494.9 4.9 collective-permute-start.16
  496.6 4.9 collective-permute-start.12
  498.0 4.6 collective-permute-start.7
  500.0 9.4 %copy-start.51 = (f32[96]{0:T(128)}, f32[96]{0:T(128)S(1)}, u32[]{:S(2)}) copy-start(f32[96]{0:T(128)S(1)} %reshape.298) | copy-start | bytes 1156
  502.6 5.0 collective-permute-start.8
  (26 other events, 65.2 us)
Sparse Core Ops, SparseCore 0:
  11.5 63.9 all-gather.2
  79.0 86.2 all-gather.4

commit v9 on v8

--- a/solution.py
+++ b/solution.py
@@ -321,6 +321,35 @@
     return jnp.concatenate([part for part, _ in parts], axis=-1).astype(jnp.float32), tied
 
 
+def tree_all_gather(local, part_columns, orders, plan_bits):
+    bit_count, core_bit = plan_bits
+    device = lax.axis_index("clip") * lax.axis_size("frame") + lax.axis_index("frame")
+    canonical = list(range(bit_count - 1, -1, -1))
+
+    def double(data, bits, bit):
+        mine = (device >> bit) & 1
+        pairs = [(index, index ^ (1 << bit)) for index in range(1 << bit_count)]
+        got = lax.ppermute(data, ("clip", "frame"), pairs)
+        new_bits = sorted(bits + [bit], reverse=True)
+        axis = new_bits.index(bit)
+        low_first = jnp.stack([data, got], axis=axis)
+        high_first = jnp.stack([got, data], axis=axis)
+        return jnp.where(mine == 0, low_first, high_first), new_bits
+
+    parts = []
+    offset = 0
+    for width in part_columns:
+        parts.append((local[:, offset : offset + width], []))
+        offset += width
+    reversed_orders = [list(reversed(order)) for order in orders]
+    for stage in range(len(reversed_orders[0])):
+        parts = [double(part, bits, order[stage]) for (part, bits), order in zip(parts, reversed_orders)]
+    whole = jnp.concatenate([part for part, _ in parts], axis=-1)
+    whole, bits = double(whole, parts[0][1], core_bit)
+    assert bits == canonical
+    return whole.reshape((1 << bit_count) * local.shape[0], local.shape[1])
+
+
 def adam_step(weight, moments, gradient):
     first = beta_first * moments[0] + (1.0 - beta_first) * gradient
     second = beta_second * moments[1] + (1.0 - beta_second) * gradient * gradient
@@ -368,7 +397,8 @@
     second_pack = jnp.concatenate(
         [project_out, expand_weight, shrink_weight.reshape(shard_rows, -1)], axis=1
     ).astype(jnp.bfloat16)
-    first_full = lax.all_gather(first_pack, everyone, axis=0, tiled=True)
+    bit_count, core_bit, rotated_orders, late_orders = plan
+    first_full = tree_all_gather(first_pack, (896, 768, 768), rotated_orders, (bit_count, core_bit))
     second_full = lax.all_gather(second_pack, everyone, axis=0, tiled=True)
     full_in = first_full[:, :wide_in]
     small_full = first_full[:, wide_in:].astype(jnp.float32)
@@ -455,7 +485,6 @@
         send = jnp.concatenate([first[1], first[2]], axis=1)[row_count:].astype(jnp.bfloat16)
         return (first, send, mixed_grads)
 
-    bit_count, core_bit, rotated_orders, late_orders = plan
     owned_late, tied = tree_reduce_scatter(
         late_terms,
         (3456, 3456),

time: 521 us -> 496 us (0.952)
  waiting for transfers between devices: 147 us -> 106 us
  other arithmetic: 57.9 us -> 64.5 us
  starting transfers between devices: 30.4 us -> 36.3 us
    ppermute x0 -> x13, waiting for transfers between devices: none -> 42.1 us  [double(): got = lax.ppermute(data, ('clip', 'frame'), pairs)]
    all_gather x1, waiting for transfers between devices: 35.8 us -> 0.01 us  [body(): second_full = lax.all_gather(second_pack, everyone, axis=0, tiled=True)]
    all_gather x1 -> x0, waiting for transfers between devices: 29.1 us -> none  [body(): first_full = lax.all_gather(first_pack, everyone, axis=0, tiled=True)]
    ppermute x1, waiting for transfers between devices: 27.2 us -> 0.01 us  [body(): lax.ppermute(inputs, 'frame', swap).reshape(row_count, model_width)]
    ppermute x0 -> x13, starting transfers between devices: none -> 19.5 us  [double(): got = lax.ppermute(data, ('clip', 'frame'), pairs)]
    ppermute x22, starting transfers between devices: 25.3 us -> 13 us  [tree_reduce_scatter(): got = lax.ppermute(send, ('clip', 'frame'), pairs)]
    ppermute x22, waiting for transfers between devices: 44.9 us -> 55.1 us  [tree_reduce_scatter(): got = lax.ppermute(send, ('clip', 'frame'), pairs)]
    another operation x9 -> x17, other arithmetic: 9.73 us -> 10.9 us
  transfers between devices with their start and end apart: 27 -> 39, of which waited for: 17 -> 21; matrix products, arithmetic and copies ran while one was open for 21% -> 23% of each run, Pallas kernels for 17% -> 18%
where the time goes in v9:
time: 496 us; the launch traced here: 491 us
  local copies, waits for them, and re-layouts  107 us (22%)
  waiting for transfers between devices  106 us (21%)
  Pallas kernels  89.8 us (18%)
  matrix products  71.5 us (14%)
  other arithmetic  64.5 us (13%)
  starting transfers between devices  36.3 us (7%)
  between operations  15.6 us (3%)
    pallas_call x2, Pallas kernels, attention_pallas(): pl.pallas_call(attention_backward_kernel, grid=(span,), in_specs=[qi_spec...  55.3 us
    ppermute x22, waiting for transfers between devices, tree_reduce_scatter(): got = lax.ppermute(send, ('clip', 'frame'), pairs)  55.1 us
    ppermute x13, waiting for transfers between devices, double(): got = lax.ppermute(data, ('clip', 'frame'), pairs)  42.1 us
    pallas_call x1, Pallas kernels, attention_pallas(): pl.pallas_call(attention_forward_kernel, grid=(pair_count,), in_specs=[q_...  34.5 us
    unnamed x133, local copies, waits for them, and re-layouts  23.3 us
    ppermute x13, starting transfers between devices, double(): got = lax.ppermute(data, ('clip', 'frame'), pairs)  19.5 us
    concatenate x10, local copies, waits for them, and re-layouts, body(): jnp.concatenate([grad_in_term, small_grads], axis=1)  19.5 us
    ppermute x22, starting transfers between devices, tree_reduce_scatter(): got = lax.ppermute(send, ('clip', 'frame'), pairs)  13 us
  transfers between devices with their start and end apart: 39, of which 21 were waited for; matrix products, arithmetic and copies ran while one was open for 23% of the time, Pallas kernels for 18%

profile of v9, /device:TPU:0, one launch (start us, length us, event | category | flops | bytes accessed | tf_op | source)
XLA Modules:
  0.0 491.0 jit_solution(2205297850028296502)
XLA Ops:
  12.8 4.1 collective-permute-start.8
  17.0 3.0 collective-permute-start
  25.5 29.5 %collective-permute-done.5 = bf16[2,24,768]{2,1,0:T(8,128)(2,1)S(1)} collective-permute-done((bf16[2,24,768]{2,1,0:T(8,128)(2,1)S(1)}, bf16[2,24,768]{2,1,0:T(8,128)(2,1)S(1)}, u32[]{:S(2)}, u32[]{:S(2)}) %collective-permute-start.5) | collective-permute-done | bytes 73760 | tf_op jit(solution)/shard_map/ppermute | solution.py:332
  60.0 1.8 collective-permute-done.10
  62.4 3.4 collective-permute-done.6
  69.4 3.2 collective-permute-done.7
  72.8 4.0 collective-permute-done.3
  80.8 1.8 fusion.39
  82.7 2.9 maximum_select_fusion
  85.6 1.8 copy-done.18
  88.4 1.8 slice_reduce_fusion
  90.2 5.5 %add_convert_fusion = bf16[750,2304]{1,0:T(8,128)(2,1)S(1)} fusion(f32[2304]{0:T(1024)S(1)} %pad_maximum_fusion.17, bf16[768,2432]{1,0:T(8,128)(2,1)} %bitcast.334, bf16[1,750,768]{2,1,0:T(8,128)(2,1)S(1)} %copy-done.5, f32[768]{0:T(1024)S(1)} %get-tuple-element.148, f32[768]{0:T(1024)S(1)} %get-tuple-element.149, f32[750]{0:T(1024)S(1)} %add_rsqrt_fusion.2, ...), kind=kOutput, calls=%fused_computation.16 | convolution fusion | flops 2661120000 | bytes 8168304 | tf_op jit(solution)/shard_map/dot_general | solution.py:424
  99.1 3.5 add_convert_fusion.1
  102.6 2.9 fusion.8.k_ref.v_ref
  105.5 34.5 %shard_map.293 = (bf16[768,768]{1,0:T(8,128)(2,1)S(1)}, f32[768,768]{1,0:T(8,128)S(1)}) custom-call(bf16[768,768]{1,0:T(8,128)(2,1)S(1)} %pad.19.q_ref, bf16[1536,1536]{1,0:T(8,128)(2,1)} %fusion.8.k_ref.v_ref, bf16[1536,1536]{1,0:T(8,128)(2,1)} %fusion.8.k_ref.v_ref, f32[1,1536]{1,0:T(1,128)S(1)} %compare_select_fusion.kbias_ref), custom_call_target="tpu_custom_call" | custom-call | tf_op jit(solution)/shard_map/pallas_call | solution.py:157
  141.4 2.5 fusion.119
  145.7 4.8 slice.294
  150.5 8.5 %reshape.1177 = bf16[3072,768]{1,0:T(8,128)(2,1)} reshape(bf16[768,3072]{1,0:T(8,128)(2,1)} %slice.294) | data formatting | bytes 9437184 | tf_op jit(solution)/shard_map/reshape | solution.py:409
  159.0 9.1 %multiply_convert_fusion = (bf16[750,3072]{1,0:T(8,128)(2,1)S(1)}, f32[750,3072]{1,0:T(8,128)}) fusion(f32[3072]{0:T(1024)S(1)} %copy-done.43, bf16[768,6912]{1,0:T(8,128)(2,1)} %all-gather.2.cloned.1.call-done, f32[750,768]{1,0:T(8,128)} %copy-done.9, f32[768]{0:T(1024)} %get-tuple-element.143, f32[768]{0:T(1024)S(1)} %get-tuple-element.144, ...), kind=kOutput, calls=%fused_computation.13 | convolution fusion | flops 3555648000 | bytes 20878192 | tf_op jit(solution)/shard_map/dot_general | solution.py:444
  168.1 2.1 copy-done.53
  170.2 5.7 %convolution_convert_fusion.1 = bf16[3072,768]{1,0:T(8,128)(2,1)} fusion(bf16[750,3072]{1,0:T(8,128)(2,1)S(1)} %get-tuple-element.202, bf16[1,750,768]{2,1,0:T(8,128)(2,1)S(1)} %copy-done.25), kind=kOutput, calls=%fused_computation.20 | convolution fusion | flops 3541303296 | bytes 10478592 | tf_op jit(solution)/shard_map/dot_general | solution.py:454
  175.9 8.5 %concatenate.318 = bf16[2,2,2,2,2,24,3072]{6,5,4,3,2,1,0:T(8,128)(2,1)} reshape(bf16[3072,768]{1,0:T(8,128)(2,1)} %convolution_convert_fusion.1) | data formatting | bytes 9437184 | tf_op jit(solution)/shard_map/concatenate | solution.py:474
  184.5 10.7 %convert_reduce_fusion = (f32[3072]{0:T(1024)}, bf16[750,3072]{1,0:T(8,128)(2,1)S(1)}) fusion(f32[750,3072]{1,0:T(8,128)} %get-tuple-element.203, f32[3072]{0:T(1024)S(1)} %copy-done.43, bf16[3072,768]{1,0:T(8,128)(2,1)} %reshape.1177, bf16[1,750,768]{2,1,0:T(8,128)(2,1)} %param.15), kind=kOutput, calls=%fused_computation.12 | convolution fusion | flops 3568892928 | bytes 19719168 | tf_op jit(solution)/shard_map/dot_general | solution.py:458
  195.2 5.3 %convolution_convert_fusion = bf16[768,3072]{1,0:T(8,128)(2,1)S(1)} fusion(bf16[750,3072]{1,0:T(8,128)(2,1)S(1)} %get-tuple-element.206, f32[750,768]{1,0:T(8,128)S(1)} %copy-done.10, f32[768]{0:T(1024)S(1)} %copy-done.48, f32[768]{0:T(1024)S(1)} %get-tuple-element.144, f32[750]{0:T(1024)S(1)} %add_rsqrt_fusion, f32[750]{0:T(1024)S(1)} %broadcast_multiply_fusion.4), kind=kOutput, calls=%fused_computation.19 | convolution fusion | flops 3544183296 | bytes 11642736 | tf_op jit(solution)/shard_map/dot_general | solution.py:460
  200.5 7.4 %multiply_reduce_fusion = (f32[768]{0:T(1024)}, f32[750]{0:T(1024)S(1)}, f32[750]{0:T(1024)S(1)}, f32[768]{0:T(1024)}, f32[750,768]{1,0:T(8,128)S(1)}) fusion(f32[750,768]{1,0:T(8,128)S(1)} %copy-done.10, f32[750]{0:T(1024)S(1)} %add_rsqrt_fusion, f32[750]{0:T(1024)S(1)} %broadcast_multiply_fusion.4, f32[768]{0:T(1024)S(1)} %get-tuple-element.144, ...), kind=kOutput, calls=%fused_computation.82 | convolution fusion | flops 3544124928 | bytes 13955808 | tf_op jit(solution)/shard_map/dot_general | solution.py:464
  207.9 1.8 convert_reduce_fusion.5
  211.2 8.0 %pad_maximum_fusion = bf16[2,2,2,2,2,24,6912]{6,5,4,3,2,1,0:T(8,128)(2,1)} fusion(bf16[2,2,2,2,2,24,768]{6,5,4,3,2,1,0:T(8,128)(2,1)S(1)} %bitcast.339, bf16[2,2,2,2,2,24,3072]{6,5,4,3,2,1,0:T(8,128)(2,1)S(1)} %bitcast.332, bf16[2,2,2,2,2,24,3072]{6,5,4,3,2,1,0:T(8,128)(2,1)S(1)} %bitcast.327), kind=kLoop, calls=%fused_computation.1 | loop fusion | flops 31850496 | bytes 21233664 | tf_op jit(solution)/shard_map/concatenate | solution.py:474
  219.1 8.7 %constant_dynamic-slice_fusion.1 = (bf16[2,2,2,1,2,24,6912]{6,5,4,3,2,1,0:T(8,128)(2,1)}, bf16[2,2,2,1,2,24,6912]{6,5,4,3,2,1,0:T(8,128)(2,1)}) fusion(bf16[2,2,2,2,2,24,6912]{6,5,4,3,2,1,0:T(8,128)(2,1)} %pad_maximum_fusion, s32[]{:T(128)S(6)} %select_n.391, s32[]{:T(128)S(6)} %select_n.392), kind=kLoop, calls=%fused_computation.252 | loop fusion | bytes 21233672 | tf_op jit(solution)/shard_map/jit(dynamic_index_in_dim)/dynamic_slice | solution.py:309
  227.8 5.3 %copy.147 = bf16[2,2,2,1,2,24,6912]{6,5,0,4,2,1,3:T(8,128)(2,1)} copy(bf16[2,2,2,1,2,24,6912]{6,5,4,3,2,1,0:T(8,128)(2,1)} %get-tuple-element.161) | data formatting | bytes 10616832
  233.1 2.4 convolution_convert_fusion.3
  237.2 27.4 %shard_map.294 = (f32[768,384]{1,0:T(8,128)S(1)}, f32[1536,384]{1,0:T(8,128)S(1)}, f32[1536,384]{1,0:T(8,128)}) custom-call(bf16[768,768]{1,0:T(8,128)(2,1)S(1)} %pad.19.q_ref, bf16[1536,1536]{1,0:T(8,128)(2,1)} %fusion.8.k_ref.v_ref, bf16[1536,1536]{1,0:T(8,128)(2,1)} %fusion.8.k_ref.v_ref, bf16[768,768]{1,0:T(8,128)(2,1)S(1)} %pad.21.do_ref, ...), custom_call_target="tpu_custom_call" | custom-call | tf_op jit(solution)/shard_map/pallas_call | solution.py:176
  271.3 5.3 %convert_add_fusion = f32[2,2,2,2,24,6912]{5,4,0,3,2,1:T(8,128)S(1)} fusion(bf16[2,2,2,2,24,6912]{5,4,0,3,2,1:T(8,128)(2,1)} %collective-permute-done.14, bf16[2,2,2,1,2,24,6912]{6,5,4,3,2,1,0:T(8,128)(2,1)} %get-tuple-element.160), kind=kLoop, calls=%fused_computation.2 | loop fusion | flops 7962624 | bytes 21233664 | tf_op jit(solution)/shard_map/add | solution.py:319
  276.6 4.9 fusion.115
  281.5 3.0 fusion.53
  284.5 3.0 fusion.52
  287.5 2.3 collective-permute-start.15
  289.9 27.9 %shard_map.295 = (f32[768,384]{1,0:T(8,128)S(1)}, f32[1536,384]{1,0:T(8,128)S(1)}, f32[1536,384]{1,0:T(8,128)}) custom-call(bf16[768,768]{1,0:T(8,128)(2,1)S(1)} %pad.19.q_ref, bf16[1536,1536]{1,0:T(8,128)(2,1)} %fusion.8.k_ref.v_ref, bf16[1536,1536]{1,0:T(8,128)(2,1)} %fusion.8.k_ref.v_ref, bf16[768,768]{1,0:T(8,128)(2,1)S(1)} %pad.22.do_ref, ...), custom_call_target="tpu_custom_call" | custom-call | tf_op jit(solution)/shard_map/pallas_call | solution.py:176
  317.9 2.7 slice.247
  323.9 7.1 %fusion.51 = bf16[1,750,768]{2,1,0:T(8,128)(2,1)} fusion(f32[750,768]{1,0:T(8,128)S(1)} %copy-done.11, bf16[750,3072]{1,0:T(8,128)(2,1)} %copy-done.53, bf16[3072,768]{1,0:T(8,128)(2,1)S(1)} %bitcast.331, f32[768]{0:T(1024)S(1)} %copy-done.45), kind=kOutput, calls=%fused_computation.95 | convolution fusion | flops 3540672000 | bytes 12785664 | tf_op jit(solution)/shard_map/dot_general | solution.py:448
  338.6 1.9 fusion.48
  340.6 9.2 %collective-permute-done.16 = bf16[750,768]{1,0:T(8,128)(2,1)} collective-permute-done((bf16[750,768]{1,0:T(8,128)(2,1)}, bf16[750,768]{1,0:T(8,128)(2,1)}, u32[]{:S(2)}, u32[]{:S(2)}) %collective-permute-start.16) | collective-permute-done | bytes 1152032 | tf_op jit(solution)/shard_map/ppermute | solution.py:508
  352.3 2.9 fusion.15
  355.9 2.2 fusion.34
  358.1 2.5 copy.113
  360.6 8.2 %fusion.13 = f32[2,2,2,2,2,24,2304]{6,5,4,3,2,1,0:T(8,128)} fusion(bf16[2,2,2,2,2,24,750]{6,5,4,3,2,1,0:T(8,128)(2,1)} %bitcast.338, bf16[750,2304]{1,0:T(8,128)(2,1)} %copy-done.15), kind=kOutput, calls=%fused_computation.32 | convolution fusion | flops 2654208000 | bytes 11685888 | tf_op jit(solution)/shard_map/dot_general | solution.py:526
  373.7 10.1 %concatenate.336 = f32[2,2,2,2,2,24,2432]{6,5,4,3,2,1,0:T(8,128)} concatenate(f32[2,2,2,2,2,24,2304]{6,5,4,3,2,1,0:T(8,128)} %fusion.13, f32[2,2,2,2,2,24,1]{6,5,4,3,2,1,0:T(8,128)} %concatenate.340, f32[2,2,2,2,2,24,1]{6,5,4,3,2,1,0:T(8,128)} %concatenate.341, f32[2,2,2,2,2,24,1]{6,5,4,3,2,1,0:T(8,128)} %concatenate.342, f32[2,2,2,2,2,24,1]{6,5,4,3,2,1,0:T(8,128)} %concatenate.343, ...), dimensions={6} | concatenate | bytes 14942208 | tf_op jit(solution)/shard_map/concatenate | solution.py:557
  383.8 3.6 fusion.50
  387.5 1.8 fusion.56
  389.3 2.5 bitcast_add_fusion.2
  393.8 15.5 %collective-permute-done.31 = bf16[2,2,24,3456]{3,2,0,1:T(8,128)(2,1)S(1)} collective-permute-done((bf16[2,2,24,3456]{3,2,0,1:T(8,128)(2,1)S(1)}, bf16[2,2,24,3456]{3,2,0,1:T(8,128)(2,1)S(1)}, u32[]{:S(2)}, u32[]{:S(2)}) %collective-permute-start.31) | collective-permute-done | bytes 663584 | tf_op jit(solution)/shard_map/ppermute | solution.py:318
  411.8 8.4 %collective-permute-done.32 = bf16[2,24,3456]{2,1,0:T(8,128)(2,1)S(1)} collective-permute-done((bf16[2,24,3456]{2,1,0:T(8,128)(2,1)S(1)}, bf16[2,24,3456]{2,1,0:T(8,128)(2,1)S(1)}, u32[]{:S(2)}, u32[]{:S(2)}) %collective-permute-start.32) | collective-permute-done | bytes 331808 | tf_op jit(solution)/shard_map/ppermute | solution.py:318
  420.4 5.6 %collective-permute-done.36 = bf16[2,24,3456]{2,1,0:T(8,128)(2,1)S(1)} collective-permute-done((bf16[2,24,3456]{2,1,0:T(8,128)(2,1)S(1)}, bf16[2,24,3456]{2,1,0:T(8,128)(2,1)S(1)}, u32[]{:S(2)}, u32[]{:S(2)}) %collective-permute-start.36) | collective-permute-done | bytes 331808 | tf_op jit(solution)/shard_map/ppermute | solution.py:318
  426.2 4.7 collective-permute-done.33
  431.0 2.9 collective-permute-done.37
  434.9 1.8 reshape.1181
  436.7 1.8 reshape.1183
  442.3 2.2 fusion.83
  444.5 2.0 fusion.95
  447.4 1.8 bitcast_add_fusion
  451.6 6.5 %collective-permute-done.26 = bf16[2,2,2,24,768]{4,3,2,1,0:T(8,128)(2,1)S(1)} collective-permute-done((bf16[2,2,2,24,768]{4,3,2,1,0:T(8,128)(2,1)S(1)}, bf16[2,2,2,24,768]{4,3,2,1,0:T(8,128)(2,1)S(1)}, u32[]{:S(2)}, u32[]{:S(2)}) %collective-permute-start.26) | collective-permute-done | bytes 294944 | tf_op jit(solution)/shard_map/ppermute | solution.py:318
  459.1 1.8 collective-permute-start.23
  465.8 3.2 collective-permute-done.28
  469.9 2.2 collective-permute-start.25
  479.6 2.6 collective-permute-done.21
  (348 shorter events, 89.4 us)
Async XLA Ops:
  7.2 12.8 %copy-start.5 = (bf16[1,750,768]{2,1,0:T(8,128)(2,1)S(1)}, bf16[1,750,768]{2,1,0:T(8,128)(2,1)}, u32[]{:S(2)}) copy-start(bf16[1,750,768]{2,1,0:T(8,128)(2,1)} %param.14) | copy-start | bytes 3456004
  7.2 134.2 %all-gather.2.cloned.1.call-start = ((), (), s32[]{:S(2)}) async-start(), calls=%async_computation | async-start | bytes 10948608 | tf_op jit(solution)/shard_map/all_gather | solution.py:402
  12.8 8.7 %collective-permute-start.8 = (bf16[24,768]{1,0:T(8,128)(2,1)S(1)}, bf16[24,768]{1,0:T(8,128)(2,1)S(1)}, u32[]{:S(2)}, u32[]{:S(2)}) collective-permute-start(bf16[24,768]{1,0:T(8,128)(2,1)S(1)} %get-tuple-element.183), channel_id=1, source_target_pairs={{0,16},{1,17},{2,18},{3,19},{4,20},{5,21},{6,22},{7,23},{8,24},{9,... | collective-permute-start | bytes 110600 | tf_op jit(solution)/shard_map/ppermute | solution.py:332
  16.9 6.2 %collective-permute-start.4 = (bf16[24,768]{1,0:T(8,128)(2,1)S(1)}, bf16[24,768]{1,0:T(8,128)(2,1)S(1)}, u32[]{:S(2)}, u32[]{:S(2)}) collective-permute-start(bf16[24,768]{1,0:T(8,128)(2,1)S(1)} %get-tuple-element.189), channel_id=1, source_target_pairs={{0,16},{1,17},{2,18},{3,19},{4,20},{5,21},{6,22},{7,23},{8,24},{9,... | collective-permute-start | bytes 110600 | tf_op jit(solution)/shard_map/ppermute | solution.py:332
  17.0 6.9 %collective-permute-start = (bf16[24,896]{1,0:T(8,128)(2,1)S(1)}, bf16[24,896]{1,0:T(8,128)(2,1)S(1)}, u32[]{:S(2)}, u32[]{:S(2)}) collective-permute-start(bf16[24,896]{1,0:T(8,128)(2,1)S(1)} %get-tuple-element.186), channel_id=1, source_target_pairs={{0,16},{1,17},{2,18},{3,19},{4,20},{5,21},{6,22},{7,23},{8,24},{9,... | collective-permute-start | bytes 129032 | tf_op jit(solution)/shard_map/ppermute | solution.py:332
  20.0 59.3 %collective-permute-start.13 = (bf16[1,750,768]{2,1,0:T(8,128)(2,1)S(1)}, bf16[1,750,768]{2,1,0:T(8,128)(2,1)}, u32[]{:S(2)}, u32[]{:S(2)}) collective-permute-start(bf16[1,750,768]{2,1,0:T(8,128)(2,1)S(1)} %copy-done.5), channel_id=1, source_target_pairs={{0,1},{1,0},{2,3},{3,2},{4,5},{5,4},{6,7},{7,6},{8,9},{9,8},{10,11... | collective-permute-start | bytes 3456008 | tf_op jit(solution)/shard_map/ppermute | solution.py:416
  21.5 35.1 %collective-permute-start.9 = (bf16[2,24,768]{2,1,0:T(8,128)(2,1)S(1)}, bf16[2,24,768]{2,1,0:T(8,128)(2,1)S(1)}, u32[]{:S(2)}, u32[]{:S(2)}) collective-permute-start(bf16[2,24,768]{2,1,0:T(8,128)(2,1)S(1)} %maximum_select_fusion.18), channel_id=1, source_target_pairs={{0,4},{1,5},{2,6},{3,7},{4,0},{5,1},{6,2},{7,3},{8,12},{9,13},{10,... | collective-permute-start | bytes 221192 | tf_op jit(solution)/shard_map/ppermute | solution.py:332
  23.2 31.8 %collective-permute-start.5 = (bf16[2,24,768]{2,1,0:T(8,128)(2,1)S(1)}, bf16[2,24,768]{2,1,0:T(8,128)(2,1)S(1)}, u32[]{:S(2)}, u32[]{:S(2)}) collective-permute-start(bf16[2,24,768]{2,1,0:T(8,128)(2,1)S(1)} %maximum_select_fusion.17), channel_id=1, source_target_pairs={{0,1},{1,0},{2,3},{3,2},{4,5},{5,4},{6,7},{7,6},{8,9},{9,8},{10,11... | collective-permute-start | bytes 221192 | tf_op jit(solution)/shard_map/ppermute | solution.py:332
  23.9 34.4 %collective-permute-start.1 = (bf16[2,24,896]{2,1,0:T(8,128)(2,1)S(1)}, bf16[2,24,896]{2,1,0:T(8,128)(2,1)S(1)}, u32[]{:S(2)}, u32[]{:S(2)}) collective-permute-start(bf16[2,24,896]{2,1,0:T(8,128)(2,1)S(1)} %maximum_select_fusion.15), channel_id=1, source_target_pairs={{0,8},{1,9},{2,10},{3,11},{4,12},{5,13},{6,14},{7,15},{8,0},{9,1},... | collective-permute-start | bytes 258056 | tf_op jit(solution)/shard_map/ppermute | solution.py:332
  55.0 10.8 %collective-permute-start.6 = (bf16[2,2,24,768]{3,2,0,1:T(8,128)(2,1)S(1)}, bf16[2,2,24,768]{3,2,0,1:T(8,128)(2,1)S(1)}, u32[]{:S(2)}, u32[]{:S(2)}) collective-permute-start(bf16[2,2,24,768]{3,2,0,1:T(8,128)(2,1)S(1)} %maximum_select_fusion.12), channel_id=1, source_target_pairs={{0,8},{1,9},{2,10},{3,11},{4,12},{5,13},{6,14},{7,15},{8,0},{9,1},... | collective-permute-start | bytes 442376 | tf_op jit(solution)/shard_map/ppermute | solution.py:332
  56.7 5.2 %collective-permute-start.10 = (bf16[2,2,24,768]{3,2,1,0:T(8,128)(2,1)S(1)}, bf16[2,2,24,768]{3,2,1,0:T(8,128)(2,1)S(1)}, u32[]{:S(2)}, u32[]{:S(2)}) collective-permute-start(bf16[2,2,24,768]{3,2,1,0:T(8,128)(2,1)S(1)} %maximum_select_fusion.13), channel_id=1, source_target_pairs={{0,1},{1,0},{2,3},{3,2},{4,5},{5,4},{6,7},{7,6},{8,9},{9,8},{10,11... | collective-permute-start | bytes 442376 | tf_op jit(solution)/shard_map/ppermute | solution.py:332
  58.5 9.1 %collective-permute-start.2 = (bf16[2,2,24,896]{3,2,0,1:T(8,128)(2,1)S(1)}, bf16[2,2,24,896]{3,2,0,1:T(8,128)(2,1)S(1)}, u32[]{:S(2)}, u32[]{:S(2)}) collective-permute-start(bf16[2,2,24,896]{3,2,0,1:T(8,128)(2,1)S(1)} %maximum_select_fusion.10), channel_id=1, source_target_pairs={{0,4},{1,5},{2,6},{3,7},{4,0},{5,1},{6,2},{7,3},{8,12},{9,13},{10,... | collective-permute-start | bytes 516104 | tf_op jit(solution)/shard_map/ppermute | solution.py:332
  61.9 10.8 %collective-permute-start.11 = (bf16[2,2,2,24,768]{4,3,2,1,0:T(8,128)(2,1)S(1)}, bf16[2,2,2,24,768]{4,3,2,1,0:T(8,128)(2,1)S(1)}, u32[]{:S(2)}, u32[]{:S(2)}) collective-permute-start(bf16[2,2,2,24,768]{4,3,2,1,0:T(8,128)(2,1)S(1)} %maximum_select_fusion.8), channel_id=1, source_target_pairs={{0,8},{1,9},{2,10},{3,11},{4,12},{5,13},{6,14},{7,15},{8,0},{9,1},... | collective-permute-start | bytes 884744 | tf_op jit(solution)/shard_map/ppermute | solution.py:332
  65.9 6.8 %collective-permute-start.7 = (bf16[2,2,2,24,768]{4,3,0,2,1:T(8,128)(2,1)S(1)}, bf16[2,2,2,24,768]{4,3,0,2,1:T(8,128)(2,1)S(1)}, u32[]{:S(2)}, u32[]{:S(2)}) collective-permute-start(bf16[2,2,2,24,768]{4,3,0,2,1:T(8,128)(2,1)S(1)} %maximum_select_fusion.7), channel_id=1, source_target_pairs={{0,4},{1,5},{2,6},{3,7},{4,0},{5,1},{6,2},{7,3},{8,12},{9,13},{10,... | collective-permute-start | bytes 884744 | tf_op jit(solution)/shard_map/ppermute | solution.py:332
  67.7 9.1 %collective-permute-start.3 = (bf16[2,2,2,24,896]{4,3,0,1,2:T(8,128)(2,1)S(1)}, bf16[2,2,2,24,896]{4,3,0,1,2:T(8,128)(2,1)S(1)}, u32[]{:S(2)}, u32[]{:S(2)}) collective-permute-start(bf16[2,2,2,24,896]{4,3,0,1,2:T(8,128)(2,1)S(1)} %maximum_select_fusion.5), channel_id=1, source_target_pairs={{0,1},{1,0},{2,3},{3,2},{4,5},{5,4},{6,7},{7,6},{8,9},{9,8},{10,11... | collective-permute-start | bytes 1032200 | tf_op jit(solution)/shard_map/ppermute | solution.py:332
  78.5 4.2 collective-permute-start.12
  79.2 11.0 %copy-start.35 = (f32[750]{0:T(1024)}, f32[750]{0:T(1024)S(1)}, u32[]{:S(2)}) copy-start(f32[750]{0:T(1024)S(1)} %add_rsqrt_fusion.2) | copy-start | bytes 9004
  90.2 7.5 %copy-start.39 = (f32[768]{0:T(1024)}, f32[768]{0:T(1024)S(1)}, u32[]{:S(2)}) copy-start(f32[768]{0:T(1024)S(1)} %get-tuple-element.148) | copy-start | bytes 9220
  105.5 35.9 %copy-start.49 = (f32[768]{0:T(1024)S(1)}, f32[768]{0:T(1024)}, u32[]{:S(2)}) copy-start(f32[768]{0:T(1024)} %get-tuple-element.145) | copy-start | bytes 9220
  150.5 8.5 %copy-start.43 = (f32[3072]{0:T(1024)S(1)}, f32[3072]{0:T(1024)}, u32[]{:S(2)}) copy-start(f32[3072]{0:T(1024)} %add.409) | copy-start | bytes 36868
  159.0 11.2 %copy-start.25 = (bf16[1,750,768]{2,1,0:T(8,128)(2,1)S(1)}, bf16[1,750,768]{2,1,0:T(8,128)(2,1)}, u32[]{:S(2)}) copy-start(bf16[1,750,768]{2,1,0:T(8,128)(2,1)} %param.15) | copy-start | bytes 3456004
  184.5 10.8 %copy-start.10 = (f32[750,768]{1,0:T(8,128)S(1)}, f32[750,768]{1,0:T(8,128)}, u32[]{:S(2)}) copy-start(f32[750,768]{1,0:T(8,128)} %copy-done.9) | copy-start | bytes 6912004
  184.5 10.8 %copy-start.48 = (f32[768]{0:T(1024)S(1)}, f32[768]{0:T(1024)}, u32[]{:S(2)}) copy-start(f32[768]{0:T(1024)} %get-tuple-element.143) | copy-start | bytes 9220
  200.5 7.4 %copy-start.26 = (bf16[1,750,768]{2,1,0:T(8,128)(2,1)S(1)}, bf16[1,750,768]{2,1,0:T(8,128)(2,1)}, u32[]{:S(2)}) copy-start(bf16[1,750,768]{2,1,0:T(8,128)(2,1)} %param.15) | copy-start | bytes 3456004
  235.6 35.7 %collective-permute-start.14 = (bf16[2,2,2,2,24,6912]{5,4,0,3,2,1:T(8,128)(2,1)}, bf16[2,2,2,2,24,6912]{5,4,0,3,2,1:T(8,128)(2,1)}, u32[]{:S(2)}, u32[]{:S(2)}) collective-permute-start(bf16[2,2,2,2,24,6912]{5,4,0,3,2,1:T(8,128)(2,1)} %bitcast.323), channel_id=1, source_target_pairs={{0,2},{1,3},{2,0},{3,1},{4,6},{5,7},{6,4},{7,5},{8,10},{9,11},{10,... | collective-permute-start | bytes 15925256 | tf_op jit(solution)/shard_map/ppermute | solution.py:318
  287.5 49.2 %collective-permute-start.15 = (bf16[750,768]{1,0:T(8,128)(2,1)}, bf16[750,768]{1,0:T(8,128)(2,1)}, u32[]{:S(2)}, u32[]{:S(2)}) collective-permute-start(bf16[750,768]{1,0:T(8,128)(2,1)} %pad_maximum_fusion.4), channel_id=1, source_target_pairs={{0,1},{1,0},{2,3},{3,2},{4,5},{5,4},{6,7},{7,6},{8,9},{9,8},{10,11... | collective-permute-start | bytes 3456008 | tf_op jit(solution)/shard_map/ppermute | solution.py:508
  322.4 27.4 %collective-permute-start.16 = (bf16[750,768]{1,0:T(8,128)(2,1)}, bf16[750,768]{1,0:T(8,128)(2,1)}, u32[]{:S(2)}, u32[]{:S(2)}) collective-permute-start(bf16[750,768]{1,0:T(8,128)(2,1)} %fusion.46), channel_id=1, source_target_pairs={{0,1},{1,0},{2,3},{3,2},{4,5},{5,4},{6,7},{7,6},{8,9},{9,8},{10,11... | collective-permute-start | bytes 3456008 | tf_op jit(solution)/shard_map/ppermute | solution.py:508
  323.8 7.1 %copy-start.42 = (f32[3072]{0:T(1024)S(1)}, f32[3072]{0:T(1024)}, u32[]{:S(2)}) copy-start(f32[3072]{0:T(1024)} %get-tuple-element.205) | copy-start | bytes 36868
  323.8 8.3 %copy-start.38 = (f32[768]{0:T(1024)S(1)}, f32[768]{0:T(1024)}, u32[]{:S(2)}) copy-start(f32[768]{0:T(1024)} %get-tuple-element.156) | copy-start | bytes 9220
  323.8 9.3 %copy-start.47 = (f32[768]{0:T(1024)S(1)}, f32[768]{0:T(1024)}, u32[]{:S(2)}) copy-start(f32[768]{0:T(1024)} %get-tuple-element.134) | copy-start | bytes 9220
  323.8 10.4 %copy-start.37 = (f32[768]{0:T(1024)S(1)}, f32[768]{0:T(1024)}, u32[]{:S(2)}) copy-start(f32[768]{0:T(1024)} %get-tuple-element.167) | copy-start | bytes 9220
  323.9 11.4 %copy-start.46 = (f32[768]{0:T(1024)S(1)}, f32[768]{0:T(1024)}, u32[]{:S(2)}) copy-start(f32[768]{0:T(1024)} %get-tuple-element.140) | copy-start | bytes 9220
  336.3 53.0 %collective-permute-start.30 = (bf16[2,2,2,24,3456]{4,3,0,2,1:T(8,128)(2,1)}, bf16[2,2,2,24,3456]{4,3,0,2,1:T(8,128)(2,1)}, u32[]{:S(2)}, u32[]{:S(2)}) collective-permute-start(bf16[2,2,2,24,3456]{4,3,0,2,1:T(8,128)(2,1)} %fusion.53), channel_id=1, source_target_pairs={{0,8},{1,9},{2,10},{3,11},{4,12},{5,13},{6,14},{7,15},{8,0},{9,1},... | collective-permute-start | bytes 3981320 | tf_op jit(solution)/shard_map/ppermute | solution.py:318
  336.4 55.6 %collective-permute-start.34 = (bf16[2,2,2,24,3456]{4,3,0,2,1:T(8,128)(2,1)}, bf16[2,2,2,24,3456]{4,3,0,2,1:T(8,128)(2,1)}, u32[]{:S(2)}, u32[]{:S(2)}) collective-permute-start(bf16[2,2,2,24,3456]{4,3,0,2,1:T(8,128)(2,1)} %fusion.52), channel_id=1, source_target_pairs={{0,4},{1,5},{2,6},{3,7},{4,0},{5,1},{6,2},{7,3},{8,12},{9,13},{10,... | collective-permute-start | bytes 3981320 | tf_op jit(solution)/shard_map/ppermute | solution.py:318
  336.7 13.2 %copy-start.2 = (f32[1500,384]{1,0:T(8,128)S(1)}, f32[1500,384]{1,0:T(8,128)}, u32[]{:S(2)}) copy-start(f32[1500,384]{1,0:T(8,128)} %copy-done.1) | copy-start | bytes 6912004
  336.7 13.1 %copy-start.4 = (f32[1500,384]{1,0:T(8,128)S(1)}, f32[1500,384]{1,0:T(8,128)}, u32[]{:S(2)}) copy-start(f32[1500,384]{1,0:T(8,128)} %copy-done.3) | copy-start | bytes 6912004
  387.5 59.9 %collective-permute-start.17 = (bf16[2,2,2,2,24,2432]{5,4,3,2,1,0:T(8,128)(2,1)}, bf16[2,2,2,2,24,2432]{5,4,3,2,1,0:T(8,128)(2,1)}, u32[]{:S(2)}, u32[]{:S(2)}) collective-permute-start(bf16[2,2,2,2,24,2432]{5,4,3,2,1,0:T(8,128)(2,1)} %fusion.50), channel_id=1, source_target_pairs={{0,2},{1,3},{2,0},{3,1},{4,6},{5,7},{6,4},{7,5},{8,10},{9,11},{10,... | collective-permute-start | bytes 5603336 | tf_op jit(solution)/shard_map/ppermute | solution.py:318
  391.9 17.4 %collective-permute-start.31 = (bf16[2,2,24,3456]{3,2,0,1:T(8,128)(2,1)S(1)}, bf16[2,2,24,3456]{3,2,0,1:T(8,128)(2,1)S(1)}, u32[]{:S(2)}, u32[]{:S(2)}) collective-permute-start(bf16[2,2,24,3456]{3,2,0,1:T(8,128)(2,1)S(1)} %fusion.67), channel_id=1, source_target_pairs={{0,4},{1,5},{2,6},{3,7},{4,0},{5,1},{6,2},{7,3},{8,12},{9,13},{10,... | collective-permute-start | bytes 1990664 | tf_op jit(solution)/shard_map/ppermute | solution.py:318
  393.7 17.4 %collective-permute-start.35 = (bf16[2,2,24,3456]{3,2,0,1:T(8,128)(2,1)S(1)}, bf16[2,2,24,3456]{3,2,0,1:T(8,128)(2,1)S(1)}, u32[]{:S(2)}, u32[]{:S(2)}) collective-permute-start(bf16[2,2,24,3456]{3,2,0,1:T(8,128)(2,1)S(1)} %fusion.68), channel_id=1, source_target_pairs={{0,8},{1,9},{2,10},{3,11},{4,12},{5,13},{6,14},{7,15},{8,0},{9,1},... | collective-permute-start | bytes 1990664 | tf_op jit(solution)/shard_map/ppermute | solution.py:318
  409.5 10.8 %collective-permute-start.32 = (bf16[2,24,3456]{2,1,0:T(8,128)(2,1)S(1)}, bf16[2,24,3456]{2,1,0:T(8,128)(2,1)S(1)}, u32[]{:S(2)}, u32[]{:S(2)}) collective-permute-start(bf16[2,24,3456]{2,1,0:T(8,128)(2,1)S(1)} %fusion.70), channel_id=1, source_target_pairs={{0,1},{1,0},{2,3},{3,2},{4,5},{5,4},{6,7},{7,6},{8,9},{9,8},{10,11... | collective-permute-start | bytes 995336 | tf_op jit(solution)/shard_map/ppermute | solution.py:318
  411.3 14.8 %collective-permute-start.36 = (bf16[2,24,3456]{2,1,0:T(8,128)(2,1)S(1)}, bf16[2,24,3456]{2,1,0:T(8,128)(2,1)S(1)}, u32[]{:S(2)}, u32[]{:S(2)}) collective-permute-start(bf16[2,24,3456]{2,1,0:T(8,128)(2,1)S(1)} %fusion.71), channel_id=1, source_target_pairs={{0,1},{1,0},{2,3},{3,2},{4,5},{5,4},{6,7},{7,6},{8,9},{9,8},{10,11... | collective-permute-start | bytes 995336 | tf_op jit(solution)/shard_map/ppermute | solution.py:318
  420.3 13.6 %copy-start.22 = (f32[2,24,3072]{2,1,0:T(8,128)S(1)}, f32[2,24,3072]{2,1,0:T(8,128)}, u32[]{:S(2)}) copy-start(f32[2,24,3072]{2,1,0:T(8,128)} %param.24) | copy-start | bytes 1769476
  420.3 10.6 %collective-permute-start.33 = (bf16[24,3456]{1,0:T(8,128)(2,1)S(1)}, bf16[24,3456]{1,0:T(8,128)(2,1)S(1)}, u32[]{:S(2)}, u32[]{:S(2)}) collective-permute-start(bf16[24,3456]{1,0:T(8,128)(2,1)S(1)} %fusion.86), channel_id=1, source_target_pairs={{0,16},{1,17},{2,18},{3,19},{4,20},{5,21},{6,22},{7,23},{8,24},{9,... | collective-permute-start | bytes 497672 | tf_op jit(solution)/shard_map/ppermute | solution.py:318
  426.0 21.3 %slice-start = ((s8[7471104]{0:T(1024)(128)(4,1)}), s8[3276800]{0:T(1024)(128)(4,1)S(1)}, s32[]{:S(2)}) async-start(s8[7471104]{0:T(1024)(128)(4,1)} %bitcast.324), calls=%async_computation.1 | async-start | bytes 6553600
  426.2 7.7 %collective-permute-start.37 = (bf16[24,3456]{1,0:T(8,128)(2,1)S(1)}, bf16[24,3456]{1,0:T(8,128)(2,1)S(1)}, u32[]{:S(2)}, u32[]{:S(2)}) collective-permute-start(bf16[24,3456]{1,0:T(8,128)(2,1)S(1)} %fusion.87), channel_id=1, source_target_pairs={{0,16},{1,17},{2,18},{3,19},{4,20},{5,21},{6,22},{7,23},{8,24},{9,... | collective-permute-start | bytes 497672 | tf_op jit(solution)/shard_map/ppermute | solution.py:318
  438.5 8.9 %slice-start.1 = ((s8[7471104]{0:T(1024)(128)(4,1)}), s8[4194304]{0:T(1024)(128)(4,1)S(1)}, s32[]{:S(2)}) async-start(s8[7471104]{0:T(1024)(128)(4,1)} %bitcast.324), calls=%async_computation.2 | async-start | bytes 8388608
  449.5 8.5 %collective-permute-start.26 = (bf16[2,2,2,24,768]{4,3,2,1,0:T(8,128)(2,1)S(1)}, bf16[2,2,2,24,768]{4,3,2,1,0:T(8,128)(2,1)S(1)}, u32[]{:S(2)}, u32[]{:S(2)}) collective-permute-start(bf16[2,2,2,24,768]{4,3,2,1,0:T(8,128)(2,1)S(1)} %fusion.81), channel_id=1, source_target_pairs={{0,8},{1,9},{2,10},{3,11},{4,12},{5,13},{6,14},{7,15},{8,0},{9,1},... | collective-permute-start | bytes 884744 | tf_op jit(solution)/shard_map/ppermute | solution.py:318
  450.4 8.5 %collective-permute-start.22 = (bf16[2,2,2,24,768]{4,3,2,1,0:T(8,128)(2,1)S(1)}, bf16[2,2,2,24,768]{4,3,2,1,0:T(8,128)(2,1)S(1)}, u32[]{:S(2)}, u32[]{:S(2)}) collective-permute-start(bf16[2,2,2,24,768]{4,3,2,1,0:T(8,128)(2,1)S(1)} %fusion.80), channel_id=1, source_target_pairs={{0,4},{1,5},{2,6},{3,7},{4,0},{5,1},{6,2},{7,3},{8,12},{9,13},{10,... | collective-permute-start | bytes 884744 | tf_op jit(solution)/shard_map/ppermute | solution.py:318
  451.3 11.0 %collective-permute-start.18 = (bf16[2,2,2,24,896]{4,3,2,1,0:T(8,128)(2,1)S(1)}, bf16[2,2,2,24,896]{4,3,2,1,0:T(8,128)(2,1)S(1)}, u32[]{:S(2)}, u32[]{:S(2)}) collective-permute-start(bf16[2,2,2,24,896]{4,3,2,1,0:T(8,128)(2,1)S(1)} %fusion.69), channel_id=1, source_target_pairs={{0,1},{1,0},{2,3},{3,2},{4,5},{5,4},{6,7},{7,6},{8,9},{9,8},{10,11... | collective-permute-start | bytes 1032200 | tf_op jit(solution)/shard_map/ppermute | solution.py:318
  458.2 5.9 %collective-permute-start.27 = (bf16[2,2,24,768]{3,2,1,0:T(8,128)(2,1)S(1)}, bf16[2,2,24,768]{3,2,1,0:T(8,128)(2,1)S(1)}, u32[]{:S(2)}, u32[]{:S(2)}) collective-permute-start(bf16[2,2,24,768]{3,2,1,0:T(8,128)(2,1)S(1)} %fusion.89), channel_id=1, source_target_pairs={{0,1},{1,0},{2,3},{3,2},{4,5},{5,4},{6,7},{7,6},{8,9},{9,8},{10,11... | collective-permute-start | bytes 442376 | tf_op jit(solution)/shard_map/ppermute | solution.py:318
  459.1 6.1 %collective-permute-start.23 = (bf16[2,2,24,768]{3,2,1,0:T(8,128)(2,1)S(1)}, bf16[2,2,24,768]{3,2,1,0:T(8,128)(2,1)S(1)}, u32[]{:S(2)}, u32[]{:S(2)}) collective-permute-start(bf16[2,2,24,768]{3,2,1,0:T(8,128)(2,1)S(1)} %fusion.88), channel_id=1, source_target_pairs={{0,8},{1,9},{2,10},{3,11},{4,12},{5,13},{6,14},{7,15},{8,0},{9,1},... | collective-permute-start | bytes 442376 | tf_op jit(solution)/shard_map/ppermute | solution.py:318
  462.4 11.9 %copy-start.50 = (f32[2,96]{1,0:T(2,128)S(1)}, f32[2,96]{1,0:T(2,128)}, u32[]{:S(2)}) copy-start(f32[2,96]{1,0:T(2,128)} %param.26) | copy-start | bytes 2308
  462.4 11.9 %copy-start.52 = (f32[96]{0:T(128)S(1)}, f32[96]{0:T(128)}, u32[]{:S(2)}) copy-start(f32[96]{0:T(128)} %param.20) | copy-start | bytes 1156
  462.4 12.4 %copy-start.34 = (f32[1,24,8]{2,1,0:T(8,128)S(1)}, f32[1,24,8]{2,1,0:T(8,128)}, u32[]{:S(2)}) copy-start(f32[1,24,8]{2,1,0:T(8,128)} %copy.133) | copy-start | bytes 2308
  462.5 9.7 %collective-permute-start.19 = (bf16[2,2,24,896]{3,2,1,0:T(8,128)(2,1)S(1)}, bf16[2,2,24,896]{3,2,1,0:T(8,128)(2,1)S(1)}, u32[]{:S(2)}, u32[]{:S(2)}) collective-permute-start(bf16[2,2,24,896]{3,2,1,0:T(8,128)(2,1)S(1)} %fusion.85), channel_id=1, source_target_pairs={{0,4},{1,5},{2,6},{3,7},{4,0},{5,1},{6,2},{7,3},{8,12},{9,13},{10,... | collective-permute-start | bytes 516104 | tf_op jit(solution)/shard_map/ppermute | solution.py:318
  464.1 18.1 %copy-start.27 = (f32[2,24,2304]{2,1,0:T(8,128)S(1)}, f32[2,24,2304]{2,1,0:T(8,128)}, u32[]{:S(2)}) copy-start(f32[2,24,2304]{2,1,0:T(8,128)} %param.22) | copy-start | bytes 1327108
  464.2 4.8 collective-permute-start.28
  465.2 17.1 %copy-start.30 = (f32[24,2304]{1,0:T(8,128)S(1)}, f32[24,2304]{1,0:T(8,128)}, u32[]{:S(2)}) copy-start(f32[24,2304]{1,0:T(8,128)} %param.16) | copy-start | bytes 663556
  465.3 4.6 collective-permute-start.24
  469.0 4.9 %collective-permute-start.29 = (bf16[24,768]{1,0:T(8,128)(2,1)S(1)}, bf16[24,768]{1,0:T(8,128)(2,1)S(1)}, u32[]{:S(2)}, u32[]{:S(2)}) collective-permute-start(bf16[24,768]{1,0:T(8,128)(2,1)S(1)} %fusion.100), channel_id=1, source_target_pairs={{0,16},{1,17},{2,18},{3,19},{4,20},{5,21},{6,22},{7,23},{8,24},{9,... | collective-permute-start | bytes 110600 | tf_op jit(solution)/shard_map/ppermute | solution.py:318
  469.9 5.3 %collective-permute-start.25 = (bf16[24,768]{1,0:T(8,128)(2,1)S(1)}, bf16[24,768]{1,0:T(8,128)(2,1)S(1)}, u32[]{:S(2)}, u32[]{:S(2)}) collective-permute-start(bf16[24,768]{1,0:T(8,128)(2,1)S(1)} %fusion.99), channel_id=1, source_target_pairs={{0,16},{1,17},{2,18},{3,19},{4,20},{5,21},{6,22},{7,23},{8,24},{9,... | collective-permute-start | bytes 110600 | tf_op jit(solution)/shard_map/ppermute | solution.py:318
  472.2 5.0 %collective-permute-start.20 = (bf16[2,24,896]{2,1,0:T(8,128)(2,1)S(1)}, bf16[2,24,896]{2,1,0:T(8,128)(2,1)S(1)}, u32[]{:S(2)}, u32[]{:S(2)}) collective-permute-start(bf16[2,24,896]{2,1,0:T(8,128)(2,1)S(1)} %fusion.90), channel_id=1, source_target_pairs={{0,8},{1,9},{2,10},{3,11},{4,12},{5,13},{6,14},{7,15},{8,0},{9,1},... | collective-permute-start | bytes 258056 | tf_op jit(solution)/shard_map/ppermute | solution.py:318
  474.1 9.9 %copy-start.51 = (f32[96]{0:T(128)}, f32[96]{0:T(128)S(1)}, u32[]{:S(2)}) copy-start(f32[96]{0:T(128)S(1)} %reshape.1182) | copy-start | bytes 1156
  477.2 5.0 %collective-permute-start.21 = (bf16[24,896]{1,0:T(8,128)(2,1)S(1)}, bf16[24,896]{1,0:T(8,128)(2,1)S(1)}, u32[]{:S(2)}, u32[]{:S(2)}) collective-permute-start(bf16[24,896]{1,0:T(8,128)(2,1)S(1)} %fusion.98), channel_id=1, source_target_pairs={{0,16},{1,17},{2,18},{3,19},{4,20},{5,21},{6,22},{7,23},{8,24},{9,... | collective-permute-start | bytes 129032 | tf_op jit(solution)/shard_map/ppermute | solution.py:318
  (38 other events, 123.7 us)
Sparse Core Ops, SparseCore 0:
  11.5 97.3 all-gather.1

commit v10 on v9

--- a/solution.py
+++ b/solution.py
@@ -310,13 +310,16 @@
             sends.append(
                 lax.dynamic_index_in_dim(part, 1 - mine, axis=axis, keepdims=False).astype(jnp.bfloat16)
             )
-        if stage in hooks:
-            sends, tied[stage] = lax.optimization_barrier((sends, hooks[stage](tied)))
         new_parts = []
         for keep, send, (part, part_bits), bit in zip(keeps, sends, parts, stage_bits):
             pairs = [(index, index ^ (1 << bit)) for index in range(blocks)]
             got = lax.ppermute(send, ("clip", "frame"), pairs)
             new_parts.append((keep + got.astype(jnp.float32), [b for b in part_bits if b != bit]))
+        if stage in hooks:
+            values, tied[stage] = lax.optimization_barrier(
+                ([part for part, _ in new_parts], hooks[stage](tied))
+            )
+            new_parts = [(value, part_bits) for value, (_, part_bits) in zip(values, new_parts)]
         parts = new_parts
     return jnp.concatenate([part for part, _ in parts], axis=-1).astype(jnp.float32), tied
 
@@ -477,47 +480,38 @@
     grad_mixed = jnp.dot(grad_attended, full_out.T, preferred_element_type=jnp.float32).astype(
         jnp.bfloat16
     )
-    def first_backward_half(tied):
-        mixed_grads = tied[0]
-        first = attention_pallas(
-            scaled_queries, pair_rows, mixed_grads, log_totals, 0, model_width // 256
-        )
-        send = jnp.concatenate([first[1], first[2]], axis=1)[row_count:].astype(jnp.bfloat16)
-        return (first, send, mixed_grads)
-
+    piece_pairs = 2
+    piece_count = model_width // 128 // piece_pairs
+
+    def run_piece(index, mixed_grads):
+        return attention_pallas(
+            scaled_queries, pair_rows, mixed_grads, log_totals, index * piece_pairs, piece_pairs
+        )
+
+    def piece_hook(index):
+        return lambda tied: (run_piece(index, tied[index - 1][1]), tied[index - 1][1])
+
+    hooks = {0: lambda tied: ((), grad_mixed)}
+    hooks.update({index: piece_hook(index) for index in range(1, piece_count)})
+    pieces = [run_piece(0, grad_mixed)]
     owned_late, tied = tree_reduce_scatter(
-        late_terms,
-        (3456, 3456),
-        late_orders,
-        (bit_count, core_bit),
-        {0: lambda tied: grad_mixed, 1: first_backward_half},
-    )
-    first_half, first_send, grad_mixed = tied[1]
-    halves = []
-    half_pairs = model_width // 256
-    for first_pair in (0, half_pairs):
-        if first_pair == 0:
-            grad_query, grad_keys, grad_values = first_half
-            send = first_send
-        else:
-            grad_query, grad_keys, grad_values = attention_pallas(
-                scaled_queries, pair_rows, grad_mixed, log_totals, first_pair, half_pairs
-            )
-            send = jnp.concatenate([grad_keys, grad_values], axis=1)[row_count:].astype(jnp.bfloat16)
+        late_terms, (3456, 3456), late_orders, (bit_count, core_bit), hooks
+    )
+    pieces += [tied[index][0] for index in range(1, piece_count)]
+    finished = []
+    for grad_query, grad_keys, grad_values in pieces:
         terms = jnp.concatenate([grad_keys, grad_values], axis=1)
-        returned = lax.ppermute(send, "frame", swap)
-        halves.append((grad_query, terms[:row_count] + returned.astype(jnp.float32)))
-    half_width = model_width // 2
+        returned = lax.ppermute(terms[row_count:].astype(jnp.bfloat16), "frame", swap)
+        finished.append((grad_query, terms[:row_count] + returned.astype(jnp.float32)))
+    piece_width = finished[0][0].shape[1]
     grad_projected = jnp.concatenate(
         [
-            (jnp.concatenate([halves[0][0], halves[1][0]], axis=1) * score_scale).astype(jnp.bfloat16),
+            (jnp.concatenate([query for query, _ in finished], axis=1) * score_scale).astype(
+                jnp.bfloat16
+            ),
             jnp.concatenate(
-                [
-                    halves[0][1][:, :half_width],
-                    halves[1][1][:, :half_width],
-                    halves[0][1][:, half_width:],
-                    halves[1][1][:, half_width:],
-                ],
+                [pair[:, :piece_width] for _, pair in finished]
+                + [pair[:, piece_width:] for _, pair in finished],
                 axis=1,
             ).astype(jnp.bfloat16),
         ],

time: 496 us -> 495 us (level)
  waiting for transfers between devices: 106 us -> 92.7 us
  starting transfers between devices: 36.3 us -> 42.2 us
    ppermute x22, waiting for transfers between devices: 55.1 us -> 39 us  [tree_reduce_scatter(): got = lax.ppermute(send, ('clip', 'frame'), pairs)]
    unnamed x133 -> x147, local copies, waits for them, and re-layouts: 23.3 us -> 26.5 us
    pallas_call x2 -> x3, Pallas kernels: 55.3 us -> 58 us  [attention_pallas(): pl.pallas_call(attention_backward_kernel, grid=(span,), in_specs=[qi_spec...]
    ppermute x2 -> x3, waiting for transfers between devices: 9.24 us -> 11.6 us  [body(): lax.ppermute(terms[row_count:].astype(jnp.bfloat16), 'frame', swap)]
    another operation x9 -> x10, other arithmetic: 9.12 us -> 10.3 us
  transfers between devices with their start and end apart: 39 -> 40, of which waited for: 21 -> 21; matrix products, arithmetic and copies ran while one was open for 23% -> 19% of each run, Pallas kernels for 18% -> 19%
where the time goes in v10:
time: 495 us; the launch traced here: 489 us
  local copies, waits for them, and re-layouts  105 us (21%)
  waiting for transfers between devices  92.7 us (19%)
  Pallas kernels  92.6 us (19%)
  matrix products  73.5 us (15%)
  other arithmetic  67.2 us (14%)
  starting transfers between devices  42.2 us (9%)
  between operations  15.8 us (3%)
    pallas_call x3, Pallas kernels, attention_pallas(): pl.pallas_call(attention_backward_kernel, grid=(span,), in_specs=[qi_spec...  58 us
    ppermute x13, waiting for transfers between devices, double(): got = lax.ppermute(data, ('clip', 'frame'), pairs)  42.1 us
    ppermute x22, waiting for transfers between devices, tree_reduce_scatter(): got = lax.ppermute(send, ('clip', 'frame'), pairs)  39 us
    pallas_call x1, Pallas kernels, attention_pallas(): pl.pallas_call(attention_forward_kernel, grid=(pair_count,), in_specs=[q_...  34.6 us
    unnamed x147, local copies, waits for them, and re-layouts  26.5 us
    concatenate x10, local copies, waits for them, and re-layouts, body(): jnp.concatenate([grad_in_term, small_grads], axis=1)  19.7 us
    ppermute x13, starting transfers between devices, double(): got = lax.ppermute(data, ('clip', 'frame'), pairs)  19.5 us
    ppermute x22, starting transfers between devices, tree_reduce_scatter(): got = lax.ppermute(send, ('clip', 'frame'), pairs)  16.5 us
  transfers between devices with their start and end apart: 40, of which 21 were waited for; matrix products, arithmetic and copies ran while one was open for 19% of the time, Pallas kernels for 19%

profile of v10, /device:TPU:0, one launch (start us, length us, event | category | flops | bytes accessed | tf_op | source)
XLA Modules:
  0.0 489.5 jit_solution(5789168074184733218)
XLA Ops:
  12.8 4.1 collective-permute-start.8
  17.0 3.0 collective-permute-start
  25.5 29.5 %collective-permute-done.5 = bf16[2,24,768]{2,1,0:T(8,128)(2,1)S(1)} collective-permute-done((bf16[2,24,768]{2,1,0:T(8,128)(2,1)S(1)}, bf16[2,24,768]{2,1,0:T(8,128)(2,1)S(1)}, u32[]{:S(2)}, u32[]{:S(2)}) %collective-permute-start.5) | collective-permute-done | bytes 73760 | tf_op jit(solution)/shard_map/ppermute | solution.py:335
  60.0 1.8 collective-permute-done.10
  62.4 3.4 collective-permute-done.6
  69.4 3.2 collective-permute-done.7
  72.8 4.0 collective-permute-done.3
  82.6 3.0 maximum_select_fusion
  88.5 2.0 slice_reduce_fusion
  90.6 5.5 %add_convert_fusion = bf16[750,2304]{1,0:T(8,128)(2,1)S(1)} fusion(f32[2304]{0:T(1024)S(1)} %pad_maximum_fusion.15, bf16[768,2432]{1,0:T(8,128)(2,1)} %bitcast.332, bf16[1,750,768]{2,1,0:T(8,128)(2,1)S(1)} %copy-done.2, f32[768]{0:T(1024)S(1)} %get-tuple-element.162, f32[768]{0:T(1024)S(1)} %get-tuple-element.163, f32[750]{0:T(1024)S(1)} %add_rsqrt_fusion.2, ...), kind=kOutput, calls=%fused_computation.16 | convolution fusion | flops 2661120000 | bytes 8168304 | tf_op jit(solution)/shard_map/dot_general | solution.py:427
  99.4 3.5 add_convert_fusion.1
  102.9 2.8 fusion.8.k_ref.v_ref
  105.7 34.6 %shard_map.293 = (bf16[768,768]{1,0:T(8,128)(2,1)S(1)}, f32[768,768]{1,0:T(8,128)S(1)}) custom-call(bf16[768,768]{1,0:T(8,128)(2,1)S(1)} %pad.24.q_ref, bf16[1536,1536]{1,0:T(8,128)(2,1)} %fusion.8.k_ref.v_ref, bf16[1536,1536]{1,0:T(8,128)(2,1)} %fusion.8.k_ref.v_ref, f32[1,1536]{1,0:T(1,128)S(1)} %compare_select_fusion.kbias_ref), custom_call_target="tpu_custom_call" | custom-call | tf_op jit(solution)/shard_map/pallas_call | solution.py:157
  141.7 2.5 fusion.119
  145.9 4.8 slice.325
  150.7 8.5 %reshape.1177 = bf16[3072,768]{1,0:T(8,128)(2,1)} reshape(bf16[768,3072]{1,0:T(8,128)(2,1)} %slice.325) | data formatting | bytes 9437184 | tf_op jit(solution)/shard_map/reshape | solution.py:412
  159.2 9.0 %multiply_convert_fusion = (bf16[750,3072]{1,0:T(8,128)(2,1)S(1)}, f32[750,3072]{1,0:T(8,128)}) fusion(f32[3072]{0:T(1024)S(1)} %copy-done.51, bf16[768,6912]{1,0:T(8,128)(2,1)} %all-gather.2.cloned.1.call-done, f32[750,768]{1,0:T(8,128)} %copy-done.10, f32[768]{0:T(1024)S(1)} %get-tuple-element.157, f32[768]{0:T(1024)S(1)} %get-tuple-element.158, ...), kind=kOutput, calls=%fused_computation.13 | convolution fusion | flops 3555648000 | bytes 20877168 | tf_op jit(solution)/shard_map/dot_general | solution.py:447
  168.2 2.1 copy-done.60
  170.4 5.7 %convolution_convert_fusion.1 = bf16[3072,768]{1,0:T(8,128)(2,1)} fusion(bf16[750,3072]{1,0:T(8,128)(2,1)S(1)} %get-tuple-element.217, bf16[1,750,768]{2,1,0:T(8,128)(2,1)S(1)} %copy-done.33), kind=kOutput, calls=%fused_computation.20 | convolution fusion | flops 3541303296 | bytes 10478592 | tf_op jit(solution)/shard_map/dot_general | solution.py:457
  176.1 8.5 %concatenate.316 = bf16[2,2,2,2,2,24,3072]{6,5,4,3,2,1,0:T(8,128)(2,1)} reshape(bf16[3072,768]{1,0:T(8,128)(2,1)} %convolution_convert_fusion.1) | data formatting | bytes 9437184 | tf_op jit(solution)/shard_map/concatenate | solution.py:477
  184.6 10.8 %convert_reduce_fusion = (f32[3072]{0:T(1024)}, bf16[750,3072]{1,0:T(8,128)(2,1)S(1)}) fusion(f32[750,3072]{1,0:T(8,128)} %get-tuple-element.218, f32[3072]{0:T(1024)S(1)} %copy-done.51, bf16[3072,768]{1,0:T(8,128)(2,1)} %reshape.1177, bf16[1,750,768]{2,1,0:T(8,128)(2,1)} %param.15), kind=kOutput, calls=%fused_computation.12 | convolution fusion | flops 3568892928 | bytes 19719168 | tf_op jit(solution)/shard_map/dot_general | solution.py:461
  195.3 5.4 %convolution_convert_fusion = bf16[768,3072]{1,0:T(8,128)(2,1)S(1)} fusion(bf16[750,3072]{1,0:T(8,128)(2,1)S(1)} %get-tuple-element.220, f32[750,768]{1,0:T(8,128)S(1)} %copy-done.11, f32[768]{0:T(1024)S(1)} %get-tuple-element.157, f32[768]{0:T(1024)S(1)} %get-tuple-element.158, f32[750]{0:T(1024)S(1)} %add_rsqrt_fusion, f32[750]{0:T(1024)S(1)} %broadcast_multiply_fusion.4), kind=kOutput, calls=%fused_computation.19 | convolution fusion | flops 3544183296 | bytes 11642736 | tf_op jit(solution)/shard_map/dot_general | solution.py:463
  200.7 7.4 %multiply_reduce_fusion = (f32[768]{0:T(1024)}, f32[750]{0:T(1024)S(1)}, f32[750]{0:T(1024)S(1)}, f32[768]{0:T(1024)}, f32[750,768]{1,0:T(8,128)S(1)}) fusion(f32[750,768]{1,0:T(8,128)S(1)} %copy-done.11, f32[750]{0:T(1024)S(1)} %add_rsqrt_fusion, f32[750]{0:T(1024)S(1)} %broadcast_multiply_fusion.4, f32[768]{0:T(1024)S(1)} %get-tuple-element.158, ...), kind=kOutput, calls=%fused_computation.74 | convolution fusion | flops 3544124928 | bytes 13955808 | tf_op jit(solution)/shard_map/dot_general | solution.py:467
  211.3 8.0 %pad_maximum_fusion = bf16[2,2,2,2,2,24,6912]{6,5,4,3,2,1,0:T(8,128)(2,1)} fusion(bf16[2,2,2,2,2,24,768]{6,5,4,3,2,1,0:T(8,128)(2,1)S(1)} %bitcast.337, bf16[2,2,2,2,2,24,3072]{6,5,4,3,2,1,0:T(8,128)(2,1)S(1)} %bitcast.330, bf16[2,2,2,2,2,24,3072]{6,5,4,3,2,1,0:T(8,128)(2,1)S(1)} %bitcast.325), kind=kLoop, calls=%fused_computation.1 | loop fusion | flops 31850496 | bytes 21233664 | tf_op jit(solution)/shard_map/concatenate | solution.py:477
  219.3 8.7 %constant_dynamic-slice_fusion.1 = (bf16[2,2,2,1,2,24,6912]{6,5,4,3,2,1,0:T(8,128)(2,1)}, bf16[2,2,2,1,2,24,6912]{6,5,4,3,2,1,0:T(8,128)(2,1)}) fusion(bf16[2,2,2,2,2,24,6912]{6,5,4,3,2,1,0:T(8,128)(2,1)} %pad_maximum_fusion, s32[]{:T(128)S(6)} %select_n.394, s32[]{:T(128)S(6)} %select_n.395), kind=kLoop, calls=%fused_computation.260 | loop fusion | bytes 21233672 | tf_op jit(solution)/shard_map/jit(dynamic_index_in_dim)/dynamic_slice | solution.py:309
  228.1 5.2 %copy.147 = bf16[2,2,2,1,2,24,6912]{6,5,0,4,2,1,3:T(8,128)(2,1)} copy(bf16[2,2,2,1,2,24,6912]{6,5,4,3,2,1,0:T(8,128)(2,1)} %get-tuple-element.175) | data formatting | bytes 10616832
  234.6 3.1 convolution_convert_fusion.3
  238.7 19.2 %shard_map.294 = (f32[768,256]{1,0:T(8,128)S(1)}, f32[1536,256]{1,0:T(8,128)S(1)}, f32[1536,256]{1,0:T(8,128)}) custom-call(bf16[768,768]{1,0:T(8,128)(2,1)S(1)} %pad.24.q_ref, bf16[1536,1536]{1,0:T(8,128)(2,1)} %fusion.8.k_ref.v_ref, bf16[1536,1536]{1,0:T(8,128)(2,1)} %fusion.8.k_ref.v_ref, bf16[768,768]{1,0:T(8,128)(2,1)S(1)} %pad.26.do_ref, ...), custom_call_target="tpu_custom_call" | custom-call | tf_op jit(solution)/shard_map/pallas_call | solution.py:176
  258.0 1.8 copy-done.31
  261.1 2.6 collective-permute-start.19
  263.7 5.3 %convert_add_fusion = f32[2,2,2,2,24,6912]{5,4,0,3,2,1:T(8,128)S(1)} fusion(bf16[2,2,2,2,24,6912]{5,4,0,3,2,1:T(8,128)(2,1)} %collective-permute-done.14, bf16[2,2,2,1,2,24,6912]{6,5,4,3,2,1,0:T(8,128)(2,1)} %get-tuple-element.174), kind=kLoop, calls=%fused_computation.2 | loop fusion | flops 7962624 | bytes 21233664 | tf_op jit(solution)/shard_map/add | solution.py:317
  269.0 4.9 %fusion.115 = (f32[2,2,2,2,24,3456]{5,4,0,3,2,1:T(8,128)}, f32[2,2,2,2,24,3456]{5,4,0,3,2,1:T(8,128)}) fusion(f32[2,2,2,2,24,6912]{5,4,0,3,2,1:T(8,128)S(1)} %convert_add_fusion), kind=kLoop, calls=%fused_computation.296 | loop fusion | bytes 21233664 | tf_op jit(solution)/shard_map/slice | solution.py:303
  274.0 3.1 fusion.52
  277.1 3.0 fusion.53
  280.2 8.5 %fusion.51 = bf16[1,750,768]{2,1,0:T(8,128)(2,1)} fusion(f32[750,768]{1,0:T(8,128)S(1)} %copy-done.12, bf16[750,3072]{1,0:T(8,128)(2,1)} %copy-done.60, bf16[3072,768]{1,0:T(8,128)(2,1)} %reshape.1177, f32[768]{0:T(1024)S(1)} %copy-done.53), kind=kOutput, calls=%fused_computation.98 | convolution fusion | flops 3540672000 | bytes 12785664 | tf_op jit(solution)/shard_map/dot_general | solution.py:451
  295.6 2.5 fusion.47
  298.2 19.3 %shard_map.295 = (f32[768,256]{1,0:T(8,128)S(1)}, f32[1536,256]{1,0:T(8,128)S(1)}, f32[1536,256]{1,0:T(8,128)}) custom-call(bf16[768,768]{1,0:T(8,128)(2,1)S(1)} %pad.24.q_ref, bf16[1536,1536]{1,0:T(8,128)(2,1)} %fusion.8.k_ref.v_ref, bf16[1536,1536]{1,0:T(8,128)(2,1)} %fusion.8.k_ref.v_ref, bf16[768,768]{1,0:T(8,128)(2,1)S(1)} %pad.27.do_ref, ...), custom_call_target="tpu_custom_call" | custom-call | tf_op jit(solution)/shard_map/pallas_call | solution.py:176
  324.6 2.0 collective-permute-start.18
  326.8 2.1 collective-permute-start.17
  328.9 19.5 %shard_map.296 = (f32[768,256]{1,0:T(8,128)S(1)}, f32[1536,256]{1,0:T(8,128)S(1)}, f32[1536,256]{1,0:T(8,128)}) custom-call(bf16[768,768]{1,0:T(8,128)(2,1)S(1)} %pad.24.q_ref, bf16[1536,1536]{1,0:T(8,128)(2,1)} %fusion.8.k_ref.v_ref, bf16[1536,1536]{1,0:T(8,128)(2,1)} %fusion.8.k_ref.v_ref, bf16[768,768]{1,0:T(8,128)(2,1)S(1)} %pad.28.do_ref, ...), custom_call_target="tpu_custom_call" | custom-call | tf_op jit(solution)/shard_map/pallas_call | solution.py:176
  354.4 1.9 collective-permute-start.37
  358.1 1.8 collective-permute-start.21
  360.2 11.6 %collective-permute-done.20 = bf16[750,512]{1,0:T(8,128)(2,1)S(1)} collective-permute-done((bf16[750,512]{1,0:T(8,128)(2,1)S(1)}, bf16[750,512]{1,0:T(8,128)(2,1)S(1)}, u32[]{:S(2)}, u32[]{:S(2)}) %collective-permute-start.20) | collective-permute-done | bytes 768032 | tf_op jit(solution)/shard_map/ppermute | solution.py:504
  372.1 6.8 %collective-permute-done.37 = bf16[2,24,3456]{2,1,0:T(8,128)(2,1)S(1)} collective-permute-done((bf16[2,24,3456]{2,1,0:T(8,128)(2,1)S(1)}, bf16[2,24,3456]{2,1,0:T(8,128)(2,1)S(1)}, u32[]{:S(2)}, u32[]{:S(2)}) %collective-permute-start.37) | collective-permute-done | bytes 331808 | tf_op jit(solution)/shard_map/ppermute | solution.py:316
  379.1 6.9 %collective-permute-done.35 = bf16[2,24,3456]{2,1,0:T(8,128)(2,1)S(1)} collective-permute-done((bf16[2,24,3456]{2,1,0:T(8,128)(2,1)S(1)}, bf16[2,24,3456]{2,1,0:T(8,128)(2,1)S(1)}, u32[]{:S(2)}, u32[]{:S(2)}) %collective-permute-start.35) | collective-permute-done | bytes 331808 | tf_op jit(solution)/shard_map/ppermute | solution.py:316
  386.2 3.8 collective-permute-done.38
  390.1 3.6 collective-permute-done.36
  396.6 2.0 fusion.101
  400.2 2.0 fusion.48
  403.0 2.9 fusion.15
  408.5 2.2 fusion.34
  412.8 2.4 copy.113
  415.2 8.2 %fusion.13 = f32[2,2,2,2,2,24,2304]{6,5,4,3,2,1,0:T(8,128)} fusion(bf16[2,2,2,2,2,24,750]{6,5,4,3,2,1,0:T(8,128)(2,1)} %bitcast.336, bf16[750,2304]{1,0:T(8,128)(2,1)} %copy-done.16), kind=kOutput, calls=%fused_computation.30 | convolution fusion | flops 2654208000 | bytes 11685888 | tf_op jit(solution)/shard_map/dot_general | solution.py:520
  424.2 10.3 %concatenate.334 = f32[2,2,2,2,2,24,2432]{6,5,4,3,2,1,0:T(8,128)} concatenate(f32[2,2,2,2,2,24,2304]{6,5,4,3,2,1,0:T(8,128)} %fusion.13, f32[2,2,2,2,2,24,1]{6,5,4,3,2,1,0:T(8,128)} %concatenate.338, f32[2,2,2,2,2,24,1]{6,5,4,3,2,1,0:T(8,128)} %concatenate.339, f32[2,2,2,2,2,24,1]{6,5,4,3,2,1,0:T(8,128)} %concatenate.340, f32[2,2,2,2,2,24,1]{6,5,4,3,2,1,0:T(8,128)} %concatenate.341, ...), dimensions={6} | concatenate | bytes 14942208 | tf_op jit(solution)/shard_map/concatenate | solution.py:551
  434.5 2.4 fusion.44
  437.0 1.9 pad_maximum_fusion.14
  438.9 2.2 fusion.83
  441.1 2.2 fusion.95
  443.3 1.8 pad_maximum_fusion.3
  449.5 5.4 %collective-permute-done.31 = bf16[2,2,2,24,768]{4,3,2,1,0:T(8,128)(2,1)S(1)} collective-permute-done((bf16[2,2,2,24,768]{4,3,2,1,0:T(8,128)(2,1)S(1)}, bf16[2,2,2,24,768]{4,3,2,1,0:T(8,128)(2,1)S(1)}, u32[]{:S(2)}, u32[]{:S(2)}) %collective-permute-start.31) | collective-permute-done | bytes 294944 | tf_op jit(solution)/shard_map/ppermute | solution.py:316
  455.3 2.9 collective-permute-done.27
  460.3 2.1 collective-permute-start.24
  464.9 2.5 collective-permute-done.33
  478.6 2.0 collective-permute-done.26
  (370 shorter events, 97.9 us)
Async XLA Ops:
  7.2 12.8 %copy-start.2 = (bf16[1,750,768]{2,1,0:T(8,128)(2,1)S(1)}, bf16[1,750,768]{2,1,0:T(8,128)(2,1)}, u32[]{:S(2)}) copy-start(bf16[1,750,768]{2,1,0:T(8,128)(2,1)} %param.14) | copy-start | bytes 3456004
  7.2 134.5 %all-gather.2.cloned.1.call-start = ((), (), s32[]{:S(2)}) async-start(), calls=%async_computation | async-start | bytes 10948608 | tf_op jit(solution)/shard_map/all_gather | solution.py:405
  12.8 8.7 %collective-permute-start.8 = (bf16[24,768]{1,0:T(8,128)(2,1)S(1)}, bf16[24,768]{1,0:T(8,128)(2,1)S(1)}, u32[]{:S(2)}, u32[]{:S(2)}) collective-permute-start(bf16[24,768]{1,0:T(8,128)(2,1)S(1)} %get-tuple-element.197), channel_id=1, source_target_pairs={{0,16},{1,17},{2,18},{3,19},{4,20},{5,21},{6,22},{7,23},{8,24},{9,... | collective-permute-start | bytes 110600 | tf_op jit(solution)/shard_map/ppermute | solution.py:335
  16.9 6.2 %collective-permute-start.4 = (bf16[24,768]{1,0:T(8,128)(2,1)S(1)}, bf16[24,768]{1,0:T(8,128)(2,1)S(1)}, u32[]{:S(2)}, u32[]{:S(2)}) collective-permute-start(bf16[24,768]{1,0:T(8,128)(2,1)S(1)} %get-tuple-element.203), channel_id=1, source_target_pairs={{0,16},{1,17},{2,18},{3,19},{4,20},{5,21},{6,22},{7,23},{8,24},{9,... | collective-permute-start | bytes 110600 | tf_op jit(solution)/shard_map/ppermute | solution.py:335
  17.0 6.9 %collective-permute-start = (bf16[24,896]{1,0:T(8,128)(2,1)S(1)}, bf16[24,896]{1,0:T(8,128)(2,1)S(1)}, u32[]{:S(2)}, u32[]{:S(2)}) collective-permute-start(bf16[24,896]{1,0:T(8,128)(2,1)S(1)} %get-tuple-element.200), channel_id=1, source_target_pairs={{0,16},{1,17},{2,18},{3,19},{4,20},{5,21},{6,22},{7,23},{8,24},{9,... | collective-permute-start | bytes 129032 | tf_op jit(solution)/shard_map/ppermute | solution.py:335
  20.0 59.3 %collective-permute-start.13 = (bf16[1,750,768]{2,1,0:T(8,128)(2,1)S(1)}, bf16[1,750,768]{2,1,0:T(8,128)(2,1)}, u32[]{:S(2)}, u32[]{:S(2)}) collective-permute-start(bf16[1,750,768]{2,1,0:T(8,128)(2,1)S(1)} %copy-done.2), channel_id=1, source_target_pairs={{0,1},{1,0},{2,3},{3,2},{4,5},{5,4},{6,7},{7,6},{8,9},{9,8},{10,11... | collective-permute-start | bytes 3456008 | tf_op jit(solution)/shard_map/ppermute | solution.py:419
  21.5 35.1 %collective-permute-start.9 = (bf16[2,24,768]{2,1,0:T(8,128)(2,1)S(1)}, bf16[2,24,768]{2,1,0:T(8,128)(2,1)S(1)}, u32[]{:S(2)}, u32[]{:S(2)}) collective-permute-start(bf16[2,24,768]{2,1,0:T(8,128)(2,1)S(1)} %maximum_select_fusion.18), channel_id=1, source_target_pairs={{0,4},{1,5},{2,6},{3,7},{4,0},{5,1},{6,2},{7,3},{8,12},{9,13},{10,... | collective-permute-start | bytes 221192 | tf_op jit(solution)/shard_map/ppermute | solution.py:335
  23.2 31.8 %collective-permute-start.5 = (bf16[2,24,768]{2,1,0:T(8,128)(2,1)S(1)}, bf16[2,24,768]{2,1,0:T(8,128)(2,1)S(1)}, u32[]{:S(2)}, u32[]{:S(2)}) collective-permute-start(bf16[2,24,768]{2,1,0:T(8,128)(2,1)S(1)} %maximum_select_fusion.17), channel_id=1, source_target_pairs={{0,1},{1,0},{2,3},{3,2},{4,5},{5,4},{6,7},{7,6},{8,9},{9,8},{10,11... | collective-permute-start | bytes 221192 | tf_op jit(solution)/shard_map/ppermute | solution.py:335
  23.9 34.4 %collective-permute-start.1 = (bf16[2,24,896]{2,1,0:T(8,128)(2,1)S(1)}, bf16[2,24,896]{2,1,0:T(8,128)(2,1)S(1)}, u32[]{:S(2)}, u32[]{:S(2)}) collective-permute-start(bf16[2,24,896]{2,1,0:T(8,128)(2,1)S(1)} %maximum_select_fusion.15), channel_id=1, source_target_pairs={{0,8},{1,9},{2,10},{3,11},{4,12},{5,13},{6,14},{7,15},{8,0},{9,1},... | collective-permute-start | bytes 258056 | tf_op jit(solution)/shard_map/ppermute | solution.py:335
  55.0 10.8 %collective-permute-start.6 = (bf16[2,2,24,768]{3,2,0,1:T(8,128)(2,1)S(1)}, bf16[2,2,24,768]{3,2,0,1:T(8,128)(2,1)S(1)}, u32[]{:S(2)}, u32[]{:S(2)}) collective-permute-start(bf16[2,2,24,768]{3,2,0,1:T(8,128)(2,1)S(1)} %maximum_select_fusion.12), channel_id=1, source_target_pairs={{0,8},{1,9},{2,10},{3,11},{4,12},{5,13},{6,14},{7,15},{8,0},{9,1},... | collective-permute-start | bytes 442376 | tf_op jit(solution)/shard_map/ppermute | solution.py:335
  56.7 5.2 %collective-permute-start.10 = (bf16[2,2,24,768]{3,2,1,0:T(8,128)(2,1)S(1)}, bf16[2,2,24,768]{3,2,1,0:T(8,128)(2,1)S(1)}, u32[]{:S(2)}, u32[]{:S(2)}) collective-permute-start(bf16[2,2,24,768]{3,2,1,0:T(8,128)(2,1)S(1)} %maximum_select_fusion.13), channel_id=1, source_target_pairs={{0,1},{1,0},{2,3},{3,2},{4,5},{5,4},{6,7},{7,6},{8,9},{9,8},{10,11... | collective-permute-start | bytes 442376 | tf_op jit(solution)/shard_map/ppermute | solution.py:335
  58.5 9.1 %collective-permute-start.2 = (bf16[2,2,24,896]{3,2,0,1:T(8,128)(2,1)S(1)}, bf16[2,2,24,896]{3,2,0,1:T(8,128)(2,1)S(1)}, u32[]{:S(2)}, u32[]{:S(2)}) collective-permute-start(bf16[2,2,24,896]{3,2,0,1:T(8,128)(2,1)S(1)} %maximum_select_fusion.10), channel_id=1, source_target_pairs={{0,4},{1,5},{2,6},{3,7},{4,0},{5,1},{6,2},{7,3},{8,12},{9,13},{10,... | collective-permute-start | bytes 516104 | tf_op jit(solution)/shard_map/ppermute | solution.py:335
  61.9 10.8 %collective-permute-start.11 = (bf16[2,2,2,24,768]{4,3,2,1,0:T(8,128)(2,1)S(1)}, bf16[2,2,2,24,768]{4,3,2,1,0:T(8,128)(2,1)S(1)}, u32[]{:S(2)}, u32[]{:S(2)}) collective-permute-start(bf16[2,2,2,24,768]{4,3,2,1,0:T(8,128)(2,1)S(1)} %maximum_select_fusion.8), channel_id=1, source_target_pairs={{0,8},{1,9},{2,10},{3,11},{4,12},{5,13},{6,14},{7,15},{8,0},{9,1},... | collective-permute-start | bytes 884744 | tf_op jit(solution)/shard_map/ppermute | solution.py:335
  65.9 6.8 %collective-permute-start.7 = (bf16[2,2,2,24,768]{4,3,0,2,1:T(8,128)(2,1)S(1)}, bf16[2,2,2,24,768]{4,3,0,2,1:T(8,128)(2,1)S(1)}, u32[]{:S(2)}, u32[]{:S(2)}) collective-permute-start(bf16[2,2,2,24,768]{4,3,0,2,1:T(8,128)(2,1)S(1)} %maximum_select_fusion.7), channel_id=1, source_target_pairs={{0,4},{1,5},{2,6},{3,7},{4,0},{5,1},{6,2},{7,3},{8,12},{9,13},{10,... | collective-permute-start | bytes 884744 | tf_op jit(solution)/shard_map/ppermute | solution.py:335
  67.7 9.1 %collective-permute-start.3 = (bf16[2,2,2,24,896]{4,3,0,1,2:T(8,128)(2,1)S(1)}, bf16[2,2,2,24,896]{4,3,0,1,2:T(8,128)(2,1)S(1)}, u32[]{:S(2)}, u32[]{:S(2)}) collective-permute-start(bf16[2,2,2,24,896]{4,3,0,1,2:T(8,128)(2,1)S(1)} %maximum_select_fusion.5), channel_id=1, source_target_pairs={{0,1},{1,0},{2,3},{3,2},{4,5},{5,4},{6,7},{7,6},{8,9},{9,8},{10,11... | collective-permute-start | bytes 1032200 | tf_op jit(solution)/shard_map/ppermute | solution.py:335
  78.5 4.2 collective-permute-start.12
  78.7 11.8 %copy-start.41 = (f32[750]{0:T(1024)}, f32[750]{0:T(1024)S(1)}, u32[]{:S(2)}) copy-start(f32[750]{0:T(1024)S(1)} %broadcast_multiply_fusion.6) | copy-start | bytes 9004
  79.3 11.3 %copy-start.44 = (f32[750]{0:T(1024)}, f32[750]{0:T(1024)S(1)}, u32[]{:S(2)}) copy-start(f32[750]{0:T(1024)S(1)} %add_rsqrt_fusion.2) | copy-start | bytes 9004
  105.7 36.0 %copy-start.56 = (f32[768]{0:T(1024)S(1)}, f32[768]{0:T(1024)}, u32[]{:S(2)}) copy-start(f32[768]{0:T(1024)} %get-tuple-element.159) | copy-start | bytes 9220
  150.7 8.5 %copy-start.51 = (f32[3072]{0:T(1024)S(1)}, f32[3072]{0:T(1024)}, u32[]{:S(2)}) copy-start(f32[3072]{0:T(1024)} %add.414) | copy-start | bytes 36868
  159.2 11.2 %copy-start.33 = (bf16[1,750,768]{2,1,0:T(8,128)(2,1)S(1)}, bf16[1,750,768]{2,1,0:T(8,128)(2,1)}, u32[]{:S(2)}) copy-start(bf16[1,750,768]{2,1,0:T(8,128)(2,1)} %param.15) | copy-start | bytes 3456004
  184.6 10.8 %copy-start.11 = (f32[750,768]{1,0:T(8,128)S(1)}, f32[750,768]{1,0:T(8,128)}, u32[]{:S(2)}) copy-start(f32[750,768]{1,0:T(8,128)} %copy-done.10) | copy-start | bytes 6912004
  233.3 30.4 %collective-permute-start.14 = (bf16[2,2,2,2,24,6912]{5,4,0,3,2,1:T(8,128)(2,1)}, bf16[2,2,2,2,24,6912]{5,4,0,3,2,1:T(8,128)(2,1)}, u32[]{:S(2)}, u32[]{:S(2)}) collective-permute-start(bf16[2,2,2,2,24,6912]{5,4,0,3,2,1:T(8,128)(2,1)} %bitcast.323), channel_id=1, source_target_pairs={{0,2},{1,3},{2,0},{3,1},{4,6},{5,7},{6,4},{7,5},{8,10},{9,11},{10,... | collective-permute-start | bytes 15925256 | tf_op jit(solution)/shard_map/ppermute | solution.py:316
  261.1 33.8 %collective-permute-start.19 = (bf16[750,512]{1,0:T(8,128)(2,1)}, bf16[750,512]{1,0:T(8,128)(2,1)}, u32[]{:S(2)}, u32[]{:S(2)}) collective-permute-start(bf16[750,512]{1,0:T(8,128)(2,1)} %fusion.50), channel_id=1, source_target_pairs={{0,1},{1,0},{2,3},{3,2},{4,5},{5,4},{6,7},{7,6},{8,9},{9,8},{10,11... | collective-permute-start | bytes 2304008 | tf_op jit(solution)/shard_map/ppermute | solution.py:504
  277.1 43.4 %collective-permute-start.15 = (bf16[2,2,2,24,3456]{4,3,0,2,1:T(8,128)(2,1)}, bf16[2,2,2,24,3456]{4,3,0,2,1:T(8,128)(2,1)}, u32[]{:S(2)}, u32[]{:S(2)}) collective-permute-start(bf16[2,2,2,24,3456]{4,3,0,2,1:T(8,128)(2,1)} %fusion.52), channel_id=1, source_target_pairs={{0,4},{1,5},{2,6},{3,7},{4,0},{5,1},{6,2},{7,3},{8,12},{9,13},{10,... | collective-permute-start | bytes 3981320 | tf_op jit(solution)/shard_map/ppermute | solution.py:316
  280.1 42.0 %collective-permute-start.16 = (bf16[2,2,2,24,3456]{4,3,0,2,1:T(8,128)(2,1)}, bf16[2,2,2,24,3456]{4,3,0,2,1:T(8,128)(2,1)}, u32[]{:S(2)}, u32[]{:S(2)}) collective-permute-start(bf16[2,2,2,24,3456]{4,3,0,2,1:T(8,128)(2,1)} %fusion.53), channel_id=1, source_target_pairs={{0,8},{1,9},{2,10},{3,11},{4,12},{5,13},{6,14},{7,15},{8,0},{9,1},... | collective-permute-start | bytes 3981320 | tf_op jit(solution)/shard_map/ppermute | solution.py:316
  280.1 8.5 %copy-start.50 = (f32[3072]{0:T(1024)S(1)}, f32[3072]{0:T(1024)}, u32[]{:S(2)}) copy-start(f32[3072]{0:T(1024)} %get-tuple-element.219) | copy-start | bytes 36868
  280.1 9.7 %copy-start.46 = (f32[768]{0:T(1024)S(1)}, f32[768]{0:T(1024)}, u32[]{:S(2)}) copy-start(f32[768]{0:T(1024)} %get-tuple-element.170) | copy-start | bytes 9220
  280.1 10.7 %copy-start.55 = (f32[768]{0:T(1024)S(1)}, f32[768]{0:T(1024)}, u32[]{:S(2)}) copy-start(f32[768]{0:T(1024)} %get-tuple-element.148) | copy-start | bytes 9220
  280.1 12.8 %copy-start.54 = (f32[768]{0:T(1024)S(1)}, f32[768]{0:T(1024)}, u32[]{:S(2)}) copy-start(f32[768]{0:T(1024)} %get-tuple-element.154) | copy-start | bytes 9220
  298.1 22.4 %slice-start.4 = ((s8[5308416]{0:T(1024)(128)(4,1)}), s8[4194304]{0:T(1024)(128)(4,1)S(1)}, s32[]{:S(2)}) async-start(s8[5308416]{0:T(1024)(128)(4,1)} %bitcast.328), calls=%async_computation.5 | async-start | bytes 8388608
  298.2 22.3 %slice-start.5 = ((s8[5308416]{0:T(1024)(128)(4,1)}), s8[1114112]{0:T(1024)(128)(4,1)S(1)}, s32[]{:S(2)}) async-start(s8[5308416]{0:T(1024)(128)(4,1)} %bitcast.328), calls=%async_computation.6 | async-start | bytes 2228224
  324.6 27.2 %collective-permute-start.18 = (bf16[2,2,24,3456]{3,2,0,1:T(8,128)(2,1)}, bf16[2,2,24,3456]{3,2,0,1:T(8,128)(2,1)}, u32[]{:S(2)}, u32[]{:S(2)}) collective-permute-start(bf16[2,2,24,3456]{3,2,0,1:T(8,128)(2,1)} %fusion.68), channel_id=1, source_target_pairs={{0,4},{1,5},{2,6},{3,7},{4,0},{5,1},{6,2},{7,3},{8,12},{9,13},{10,... | collective-permute-start | bytes 1990664 | tf_op jit(solution)/shard_map/ppermute | solution.py:316
  326.8 26.3 %collective-permute-start.17 = (bf16[2,2,24,3456]{3,2,0,1:T(8,128)(2,1)S(1)}, bf16[2,2,24,3456]{3,2,0,1:T(8,128)(2,1)}, u32[]{:S(2)}, u32[]{:S(2)}) collective-permute-start(bf16[2,2,24,3456]{3,2,0,1:T(8,128)(2,1)S(1)} %fusion.67), channel_id=1, source_target_pairs={{0,8},{1,9},{2,10},{3,11},{4,12},{5,13},{6,14},{7,15},{8,0},{9,1},... | collective-permute-start | bytes 1990664 | tf_op jit(solution)/shard_map/ppermute | solution.py:316
  351.6 20.2 %collective-permute-start.20 = (bf16[750,512]{1,0:T(8,128)(2,1)S(1)}, bf16[750,512]{1,0:T(8,128)(2,1)S(1)}, u32[]{:S(2)}, u32[]{:S(2)}) collective-permute-start(bf16[750,512]{1,0:T(8,128)(2,1)S(1)} %slice.460), channel_id=1, source_target_pairs={{0,1},{1,0},{2,3},{3,2},{4,5},{5,4},{6,7},{7,6},{8,9},{9,8},{10,11... | collective-permute-start | bytes 2304008 | tf_op jit(solution)/shard_map/ppermute | solution.py:504
  354.4 24.5 %collective-permute-start.37 = (bf16[2,24,3456]{2,1,0:T(8,128)(2,1)S(1)}, bf16[2,24,3456]{2,1,0:T(8,128)(2,1)S(1)}, u32[]{:S(2)}, u32[]{:S(2)}) collective-permute-start(bf16[2,24,3456]{2,1,0:T(8,128)(2,1)S(1)} %fusion.71), channel_id=1, source_target_pairs={{0,1},{1,0},{2,3},{3,2},{4,5},{5,4},{6,7},{7,6},{8,9},{9,8},{10,11... | collective-permute-start | bytes 995336 | tf_op jit(solution)/shard_map/ppermute | solution.py:316
  356.3 29.7 %collective-permute-start.35 = (bf16[2,24,3456]{2,1,0:T(8,128)(2,1)S(1)}, bf16[2,24,3456]{2,1,0:T(8,128)(2,1)S(1)}, u32[]{:S(2)}, u32[]{:S(2)}) collective-permute-start(bf16[2,24,3456]{2,1,0:T(8,128)(2,1)S(1)} %fusion.70), channel_id=1, source_target_pairs={{0,1},{1,0},{2,3},{3,2},{4,5},{5,4},{6,7},{7,6},{8,9},{9,8},{10,11... | collective-permute-start | bytes 995336 | tf_op jit(solution)/shard_map/ppermute | solution.py:316
  358.1 42.1 %collective-permute-start.21 = (bf16[750,512]{1,0:T(8,128)(2,1)}, bf16[750,512]{1,0:T(8,128)(2,1)}, u32[]{:S(2)}, u32[]{:S(2)}) collective-permute-start(bf16[750,512]{1,0:T(8,128)(2,1)} %slice.459), channel_id=1, source_target_pairs={{0,1},{1,0},{2,3},{3,2},{4,5},{5,4},{6,7},{7,6},{8,9},{9,8},{10,11... | collective-permute-start | bytes 2304008 | tf_op jit(solution)/shard_map/ppermute | solution.py:504
  372.1 14.1 %copy-start.25 = (bf16[750,512]{1,0:T(8,128)(2,1)}, bf16[750,512]{1,0:T(8,128)(2,1)S(1)}, u32[]{:S(2)}) copy-start(bf16[750,512]{1,0:T(8,128)(2,1)S(1)} %fusion.49) | copy-start | bytes 2304004
  372.1 17.9 %copy-start.14 = (bf16[750,2304]{1,0:T(8,128)(2,1)}, bf16[750,2304]{1,0:T(8,128)(2,1)S(1)}, u32[]{:S(2)}) copy-start(bf16[750,2304]{1,0:T(8,128)(2,1)S(1)} %slice_dynamic-update-slice_fusion.4) | copy-start | bytes 10368004
  379.0 14.7 %copy-start.32 = (f32[2,24,3072]{2,1,0:T(8,128)S(1)}, f32[2,24,3072]{2,1,0:T(8,128)}, u32[]{:S(2)}) copy-start(f32[2,24,3072]{2,1,0:T(8,128)} %param.24) | copy-start | bytes 1769476
  379.1 11.0 %collective-permute-start.38 = (bf16[24,3456]{1,0:T(8,128)(2,1)S(1)}, bf16[24,3456]{1,0:T(8,128)(2,1)S(1)}, u32[]{:S(2)}, u32[]{:S(2)}) collective-permute-start(bf16[24,3456]{1,0:T(8,128)(2,1)S(1)} %fusion.87), channel_id=1, source_target_pairs={{0,16},{1,17},{2,18},{3,19},{4,20},{5,21},{6,22},{7,23},{8,24},{9,... | collective-permute-start | bytes 497672 | tf_op jit(solution)/shard_map/ppermute | solution.py:316
  386.2 9.4 %copy-start.27 = (f32[2,96,768]{2,1,0:T(8,128)S(1)}, f32[2,96,768]{2,1,0:T(8,128)}, u32[]{:S(2)}) copy-start(f32[2,96,768]{2,1,0:T(8,128)} %param.25) | copy-start | bytes 1769476
  386.2 7.6 %collective-permute-start.36 = (bf16[24,3456]{1,0:T(8,128)(2,1)S(1)}, bf16[24,3456]{1,0:T(8,128)(2,1)S(1)}, u32[]{:S(2)}, u32[]{:S(2)}) collective-permute-start(bf16[24,3456]{1,0:T(8,128)(2,1)S(1)} %fusion.86), channel_id=1, source_target_pairs={{0,16},{1,17},{2,18},{3,19},{4,20},{5,21},{6,22},{7,23},{8,24},{9,... | collective-permute-start | bytes 497672 | tf_op jit(solution)/shard_map/ppermute | solution.py:316
  434.5 10.6 %copy-start.1 = (f32[2,2,2,2,2,24,2432]{6,5,4,3,2,1,0:T(8,128)S(1)}, f32[2,2,2,2,2,24,2432]{6,5,4,3,2,1,0:T(8,128)}, u32[]{:S(2)}) copy-start(f32[2,2,2,2,2,24,2432]{6,5,4,3,2,1,0:T(8,128)} %concatenate.334) | copy-start | bytes 22413316
  436.9 8.2 %collective-permute-start.22 = (bf16[2,2,2,2,24,2432]{5,4,3,2,1,0:T(8,128)(2,1)S(1)}, bf16[2,2,2,2,24,2432]{5,4,3,2,1,0:T(8,128)(2,1)S(1)}, u32[]{:S(2)}, u32[]{:S(2)}) collective-permute-start(bf16[2,2,2,2,24,2432]{5,4,3,2,1,0:T(8,128)(2,1)S(1)} %fusion.44), channel_id=1, source_target_pairs={{0,2},{1,3},{2,0},{3,1},{4,6},{5,7},{6,4},{7,5},{8,10},{9,11},{10,... | collective-permute-start | bytes 5603336 | tf_op jit(solution)/shard_map/ppermute | solution.py:316
  445.8 9.2 %collective-permute-start.31 = (bf16[2,2,2,24,768]{4,3,2,1,0:T(8,128)(2,1)S(1)}, bf16[2,2,2,24,768]{4,3,2,1,0:T(8,128)(2,1)S(1)}, u32[]{:S(2)}, u32[]{:S(2)}) collective-permute-start(bf16[2,2,2,24,768]{4,3,2,1,0:T(8,128)(2,1)S(1)} %fusion.81), channel_id=1, source_target_pairs={{0,8},{1,9},{2,10},{3,11},{4,12},{5,13},{6,14},{7,15},{8,0},{9,1},... | collective-permute-start | bytes 884744 | tf_op jit(solution)/shard_map/ppermute | solution.py:316
  449.0 9.2 %collective-permute-start.27 = (bf16[2,2,2,24,768]{4,3,2,1,0:T(8,128)(2,1)S(1)}, bf16[2,2,2,24,768]{4,3,2,1,0:T(8,128)(2,1)S(1)}, u32[]{:S(2)}, u32[]{:S(2)}) collective-permute-start(bf16[2,2,2,24,768]{4,3,2,1,0:T(8,128)(2,1)S(1)} %fusion.80), channel_id=1, source_target_pairs={{0,4},{1,5},{2,6},{3,7},{4,0},{5,1},{6,2},{7,3},{8,12},{9,13},{10,... | collective-permute-start | bytes 884744 | tf_op jit(solution)/shard_map/ppermute | solution.py:316
  449.2 11.0 %collective-permute-start.23 = (bf16[2,2,2,24,896]{4,3,2,1,0:T(8,128)(2,1)S(1)}, bf16[2,2,2,24,896]{4,3,2,1,0:T(8,128)(2,1)S(1)}, u32[]{:S(2)}, u32[]{:S(2)}) collective-permute-start(bf16[2,2,2,24,896]{4,3,2,1,0:T(8,128)(2,1)S(1)} %fusion.69), channel_id=1, source_target_pairs={{0,1},{1,0},{2,3},{3,2},{4,5},{5,4},{6,7},{7,6},{8,9},{9,8},{10,11... | collective-permute-start | bytes 1032200 | tf_op jit(solution)/shard_map/ppermute | solution.py:316
  455.1 7.5 %collective-permute-start.32 = (bf16[2,2,24,768]{3,2,1,0:T(8,128)(2,1)S(1)}, bf16[2,2,24,768]{3,2,1,0:T(8,128)(2,1)S(1)}, u32[]{:S(2)}, u32[]{:S(2)}) collective-permute-start(bf16[2,2,24,768]{3,2,1,0:T(8,128)(2,1)S(1)} %fusion.89), channel_id=1, source_target_pairs={{0,1},{1,0},{2,3},{3,2},{4,5},{5,4},{6,7},{7,6},{8,9},{9,8},{10,11... | collective-permute-start | bytes 442376 | tf_op jit(solution)/shard_map/ppermute | solution.py:316
  458.3 6.1 %collective-permute-start.28 = (bf16[2,2,24,768]{3,2,1,0:T(8,128)(2,1)S(1)}, bf16[2,2,24,768]{3,2,1,0:T(8,128)(2,1)S(1)}, u32[]{:S(2)}, u32[]{:S(2)}) collective-permute-start(bf16[2,2,24,768]{3,2,1,0:T(8,128)(2,1)S(1)} %fusion.88), channel_id=1, source_target_pairs={{0,8},{1,9},{2,10},{3,11},{4,12},{5,13},{6,14},{7,15},{8,0},{9,1},... | collective-permute-start | bytes 442376 | tf_op jit(solution)/shard_map/ppermute | solution.py:316
  460.2 12.6 %copy-start.57 = (f32[2,96]{1,0:T(2,128)S(1)}, f32[2,96]{1,0:T(2,128)}, u32[]{:S(2)}) copy-start(f32[2,96]{1,0:T(2,128)} %param.26) | copy-start | bytes 2308
  460.2 12.6 %copy-start.59 = (f32[96]{0:T(128)S(1)}, f32[96]{0:T(128)}, u32[]{:S(2)}) copy-start(f32[96]{0:T(128)} %param.20) | copy-start | bytes 1156
  460.2 13.2 %copy-start.43 = (f32[1,24,8]{2,1,0:T(8,128)S(1)}, f32[1,24,8]{2,1,0:T(8,128)}, u32[]{:S(2)}) copy-start(f32[1,24,8]{2,1,0:T(8,128)} %copy.133) | copy-start | bytes 2308
  460.3 10.2 %collective-permute-start.24 = (bf16[2,2,24,896]{3,2,1,0:T(8,128)(2,1)S(1)}, bf16[2,2,24,896]{3,2,1,0:T(8,128)(2,1)S(1)}, u32[]{:S(2)}, u32[]{:S(2)}) collective-permute-start(bf16[2,2,24,896]{3,2,1,0:T(8,128)(2,1)S(1)} %fusion.85), channel_id=1, source_target_pairs={{0,4},{1,5},{2,6},{3,7},{4,0},{5,1},{6,2},{7,3},{8,12},{9,13},{10,... | collective-permute-start | bytes 516104 | tf_op jit(solution)/shard_map/ppermute | solution.py:316
  462.6 18.0 %copy-start.35 = (f32[2,24,2304]{2,1,0:T(8,128)S(1)}, f32[2,24,2304]{2,1,0:T(8,128)}, u32[]{:S(2)}) copy-start(f32[2,24,2304]{2,1,0:T(8,128)} %param.22) | copy-start | bytes 1327108
  462.7 4.7 collective-permute-start.33
  464.5 16.2 %copy-start.38 = (f32[24,2304]{1,0:T(8,128)S(1)}, f32[24,2304]{1,0:T(8,128)}, u32[]{:S(2)}) copy-start(f32[24,2304]{1,0:T(8,128)} %param.16) | copy-start | bytes 663556
  464.5 4.4 collective-permute-start.29
  467.4 5.2 %collective-permute-start.34 = (bf16[24,768]{1,0:T(8,128)(2,1)S(1)}, bf16[24,768]{1,0:T(8,128)(2,1)S(1)}, u32[]{:S(2)}, u32[]{:S(2)}) collective-permute-start(bf16[24,768]{1,0:T(8,128)(2,1)S(1)} %fusion.100), channel_id=1, source_target_pairs={{0,16},{1,17},{2,18},{3,19},{4,20},{5,21},{6,22},{7,23},{8,24},{9,... | collective-permute-start | bytes 110600 | tf_op jit(solution)/shard_map/ppermute | solution.py:316
  469.0 5.2 %collective-permute-start.30 = (bf16[24,768]{1,0:T(8,128)(2,1)S(1)}, bf16[24,768]{1,0:T(8,128)(2,1)S(1)}, u32[]{:S(2)}, u32[]{:S(2)}) collective-permute-start(bf16[24,768]{1,0:T(8,128)(2,1)S(1)} %fusion.99), channel_id=1, source_target_pairs={{0,16},{1,17},{2,18},{3,19},{4,20},{5,21},{6,22},{7,23},{8,24},{9,... | collective-permute-start | bytes 110600 | tf_op jit(solution)/shard_map/ppermute | solution.py:316
  470.6 4.6 collective-permute-start.25
  472.7 9.6 %copy-start.58 = (f32[96]{0:T(128)}, f32[96]{0:T(128)S(1)}, u32[]{:S(2)}) copy-start(f32[96]{0:T(128)S(1)} %reshape.1182) | copy-start | bytes 1156
  475.2 5.4 %collective-permute-start.26 = (bf16[24,896]{1,0:T(8,128)(2,1)S(1)}, bf16[24,896]{1,0:T(8,128)(2,1)S(1)}, u32[]{:S(2)}, u32[]{:S(2)}) collective-permute-start(bf16[24,896]{1,0:T(8,128)(2,1)S(1)} %fusion.98), channel_id=1, source_target_pairs={{0,16},{1,17},{2,18},{3,19},{4,20},{5,21},{6,22},{7,23},{8,24},{9,... | collective-permute-start | bytes 129032 | tf_op jit(solution)/shard_map/ppermute | solution.py:316
  (44 other events, 142.6 us)
Sparse Core Ops, SparseCore 0:
  11.5 97.3 all-gather.1

commit v11 on v10

--- a/solution.py
+++ b/solution.py
@@ -284,44 +284,37 @@
     return bit_count, core_bit, rotated, late
 
 
-def tree_reduce_scatter(terms, part_columns, orders, plan_bits, hooks=None):
+def tree_reduce_scatter(terms, orders, plan_bits, hooks=None):
     hooks = dict(hooks or {})
     tied = {}
     bit_count, core_bit = plan_bits
     device = lax.axis_index("clip") * lax.axis_size("frame") + lax.axis_index("frame")
     blocks = 1 << bit_count
-    block_rows = terms.shape[0] // blocks
-    data = terms.reshape((2,) * bit_count + (block_rows, terms.shape[1]))
-    parts = [(data, list(range(bit_count - 1, -1, -1)))]
-    plan = [(core_bit,)] + [tuple(order[stage] for order in orders) for stage in range(len(orders[0]))]
-    for stage, stage_bits in enumerate(plan):
-        if stage == 1:
-            whole, bits = parts[0]
-            parts = []
-            offset = 0
-            for width in part_columns:
-                parts.append((whole[..., offset : offset + width], bits))
-                offset += width
-        keeps, sends = [], []
-        for (part, part_bits), bit in zip(parts, stage_bits):
+    parts = []
+    for term in terms:
+        shape = (2,) * bit_count + (term.shape[0] // blocks, term.shape[1])
+        parts.append((term.reshape(shape), list(range(bit_count - 1, -1, -1))))
+    plans = [(core_bit,) + tuple(order) for order in orders]
+    for stage in range(len(plans[0])):
+        new_parts = []
+        for (part, part_bits), plan in zip(parts, plans):
+            bit = plan[stage]
             axis = part_bits.index(bit)
             mine = (device >> bit) & 1
-            keeps.append(lax.dynamic_index_in_dim(part, mine, axis=axis, keepdims=False))
-            sends.append(
-                lax.dynamic_index_in_dim(part, 1 - mine, axis=axis, keepdims=False).astype(jnp.bfloat16)
+            keep = lax.dynamic_index_in_dim(part, mine, axis=axis, keepdims=False)
+            send = lax.dynamic_index_in_dim(part, 1 - mine, axis=axis, keepdims=False)
+            pairs = [(index, index ^ (1 << bit)) for index in range(blocks)]
+            got = lax.ppermute(send.astype(jnp.bfloat16), ("clip", "frame"), pairs)
+            new_parts.append(
+                (keep.astype(jnp.float32) + got.astype(jnp.float32), [b for b in part_bits if b != bit])
             )
-        new_parts = []
-        for keep, send, (part, part_bits), bit in zip(keeps, sends, parts, stage_bits):
-            pairs = [(index, index ^ (1 << bit)) for index in range(blocks)]
-            got = lax.ppermute(send, ("clip", "frame"), pairs)
-            new_parts.append((keep + got.astype(jnp.float32), [b for b in part_bits if b != bit]))
         if stage in hooks:
             values, tied[stage] = lax.optimization_barrier(
                 ([part for part, _ in new_parts], hooks[stage](tied))
             )
             new_parts = [(value, part_bits) for value, (_, part_bits) in zip(values, new_parts)]
         parts = new_parts
-    return jnp.concatenate([part for part, _ in parts], axis=-1).astype(jnp.float32), tied
+    return [part for part, _ in parts], tied
 
 
 def tree_all_gather(local, part_columns, orders, plan_bits):
@@ -474,9 +467,7 @@
         mixed_low.T, grad_attended, preferred_element_type=jnp.float32
     ).astype(jnp.bfloat16)
     grad_out_bias = jnp.sum(grad_attended.astype(jnp.float32), axis=0)
-    late_terms = jnp.concatenate(
-        [grad_shrink_term.reshape(model_width, -1), grad_expand_term, grad_out_term], axis=1
-    )
+    late_terms = [grad_shrink_term.reshape(model_width, -1), grad_expand_term, grad_out_term]
     grad_mixed = jnp.dot(grad_attended, full_out.T, preferred_element_type=jnp.float32).astype(
         jnp.bfloat16
     )
@@ -495,7 +486,7 @@
     hooks.update({index: piece_hook(index) for index in range(1, piece_count)})
     pieces = [run_piece(0, grad_mixed)]
     owned_late, tied = tree_reduce_scatter(
-        late_terms, (3456, 3456), late_orders, (bit_count, core_bit), hooks
+        late_terms, [late_orders[index % len(late_orders)] for index in range(3)], (bit_count, core_bit), hooks
     )
     pieces += [tied[index][0] for index in range(1, piece_count)]
     finished = []
@@ -504,24 +495,30 @@
         returned = lax.ppermute(terms[row_count:].astype(jnp.bfloat16), "frame", swap)
         finished.append((grad_query, terms[:row_count] + returned.astype(jnp.float32)))
     piece_width = finished[0][0].shape[1]
-    grad_projected = jnp.concatenate(
-        [
-            (jnp.concatenate([query for query, _ in finished], axis=1) * score_scale).astype(
-                jnp.bfloat16
-            ),
-            jnp.concatenate(
-                [pair[:, :piece_width] for _, pair in finished]
-                + [pair[:, piece_width:] for _, pair in finished],
-                axis=1,
-            ).astype(jnp.bfloat16),
-        ],
-        axis=1,
-    )
-    grad_in_term = jnp.dot(hidden_first.T, grad_projected, preferred_element_type=jnp.float32)
-    projected_sums = jnp.sum(grad_projected.astype(jnp.float32), axis=0)
-    grad_query_bias = projected_sums[:model_width]
-    grad_value_bias = projected_sums[2 * model_width :]
-    grad_hidden_first = jnp.dot(grad_projected, full_in.T, preferred_element_type=jnp.float32)
+    grad_query_all = (jnp.concatenate([query for query, _ in finished], axis=1) * score_scale).astype(
+        jnp.bfloat16
+    )
+    grad_key_all = jnp.concatenate([pair[:, :piece_width] for _, pair in finished], axis=1).astype(
+        jnp.bfloat16
+    )
+    grad_value_all = jnp.concatenate([pair[:, piece_width:] for _, pair in finished], axis=1).astype(
+        jnp.bfloat16
+    )
+    grad_blocks = (grad_query_all, grad_key_all, grad_value_all)
+    grad_in_terms = [
+        jnp.dot(hidden_first.T, block, preferred_element_type=jnp.float32).astype(jnp.bfloat16)
+        for block in grad_blocks
+    ]
+    grad_query_bias = jnp.sum(grad_query_all.astype(jnp.float32), axis=0)
+    grad_value_bias = jnp.sum(grad_value_all.astype(jnp.float32), axis=0)
+    grad_hidden_first = sum(
+        jnp.dot(
+            block,
+            full_in[:, index * model_width : (index + 1) * model_width].T,
+            preferred_element_type=jnp.float32,
+        )
+        for index, block in enumerate(grad_blocks)
+    )
     norm_term_first, gain_first, shift_first = norm_backward(
         grad_hidden_first, plain_first, inv_first, column_set[:, 0]
     )
@@ -548,17 +545,16 @@
         axis=1,
     )
     owned_first = tree_reduce_scatter(
-        jnp.concatenate([grad_in_term, small_grads], axis=1),
-        (896, 768, 768),
-        rotated_orders,
+        grad_in_terms + [small_grads],
+        [rotated_orders[index % len(rotated_orders)] for index in range(4)],
         (bit_count, core_bit),
     )[0]
-    owned_in = owned_first[:, :wide_in]
-    owned_vectors = owned_first[:, wide_in : wide_in + vectors.shape[1]]
-    owned_bias = owned_first[:, wide_in + vectors.shape[1] : wide_in + 12].reshape(-1)
-    owned_shrink = owned_late[:, :ff_width].reshape(shrink_weight.shape)
-    owned_expand = owned_late[:, ff_width : 2 * ff_width]
-    owned_out = owned_late[:, 2 * ff_width :]
+    owned_in = jnp.concatenate(owned_first[:3], axis=1)
+    owned_vectors = owned_first[3][:, : vectors.shape[1]]
+    owned_bias = owned_first[3][:, vectors.shape[1] : 12].reshape(-1)
+    owned_shrink = owned_late[0].reshape(shrink_weight.shape)
+    owned_expand = owned_late[1]
+    owned_out = owned_late[2]
     new_in, mom_in = adam_step(project_in, moments_in, owned_in)
     new_out, mom_out = adam_step(project_out, moments_out, owned_out)
     new_expand, mom_expand = adam_step(expand_weight, moments_expand, owned_expand)

time: 495 us -> 509 us (1.028)
  waiting for transfers between devices: 92.7 us -> 132 us
  local copies, waits for them, and re-layouts: 105 us -> 83.3 us
  other arithmetic: 67.2 us -> 55.1 us
  starting transfers between devices: 42.2 us -> 48.1 us
    ppermute x22 -> x35, waiting for transfers between devices: 39 us -> 87.9 us  [tree_reduce_scatter(): got = lax.ppermute(send.astype(jnp.bfloat16), ('clip', 'frame'), pairs)]
    concatenate x12 -> x10, local copies, waits for them, and re-layouts: 28.2 us -> 13.3 us  [body(): jnp.concatenate([grad_columns, grad_bias_term.reshape(model_width, -1), j...]
    ppermute x3, waiting for transfers between devices: 11.6 us -> 0.01 us  [body(): lax.ppermute(terms[row_count:].astype(jnp.bfloat16), 'frame', swap)]
    dot_general x2 -> x6, matrix products: 11.1 us -> 21.5 us  [the longest x3 14 us: body(): jnp.dot(block, full_in[:, index * model_width:(index + 1) * model_width]....]
    unnamed x147 -> x173, local copies, waits for them, and re-layouts: 26.5 us -> 16.4 us
    another operation x1 -> x2, local copies, waits for them, and re-layouts: 0.09 us -> 8.54 us  [the longest x1 8.46 us: tree_reduce_scatter(): parts.append((term.reshape(shape), list(range(bit_count - 1, -1, -1))))]
    concatenate x1 -> x0, other arithmetic: 8.01 us -> none  [body(): jnp.concatenate([grad_shrink_term.reshape(model_width, -1), grad_expand_t...]
    ppermute x22 -> x35, starting transfers between devices: 16.5 us -> 24.3 us  [tree_reduce_scatter(): got = lax.ppermute(send.astype(jnp.bfloat16), ('clip', 'frame'), pairs)]
  transfers between devices with their start and end apart: 40 -> 53, of which waited for: 21 -> 26; matrix products, arithmetic and copies ran while one was open for 19% -> 29% of each run, Pallas kernels for 19% -> 14%
where the time goes in v11:
time: 509 us; the launch traced here: 504 us
  waiting for transfers between devices  132 us (26%)
  Pallas kernels  92.3 us (18%)
  local copies, waits for them, and re-layouts  83.3 us (16%)
  matrix products  77.7 us (15%)
  other arithmetic  55.1 us (11%)
  starting transfers between devices  48.1 us (9%)
  between operations  16.3 us (3%)
    ppermute x35, waiting for transfers between devices, tree_reduce_scatter(): got = lax.ppermute(send.astype(jnp.bfloat16), ('clip', 'frame'), pairs)  87.9 us
    pallas_call x3, Pallas kernels, attention_pallas(): pl.pallas_call(attention_backward_kernel, grid=(span,), in_specs=[qi_spec...  57.6 us
    ppermute x13, waiting for transfers between devices, double(): got = lax.ppermute(data, ('clip', 'frame'), pairs)  43.8 us
    pallas_call x1, Pallas kernels, attention_pallas(): pl.pallas_call(attention_forward_kernel, grid=(pair_count,), in_specs=[q_...  34.7 us
    ppermute x35, starting transfers between devices, tree_reduce_scatter(): got = lax.ppermute(send.astype(jnp.bfloat16), ('clip', 'frame'), pairs)  24.3 us
    ppermute x13, starting transfers between devices, double(): got = lax.ppermute(data, ('clip', 'frame'), pairs)  18.3 us
    add x33, other arithmetic, tree_reduce_scatter(): keep.astype(jnp.float32) + got.astype(jnp.float32)  18.2 us
    unnamed x173, local copies, waits for them, and re-layouts  16.4 us
  transfers between devices with their start and end apart: 53, of which 26 were waited for; matrix products, arithmetic and copies ran while one was open for 29% of the time, Pallas kernels for 14%

profile of v11, /device:TPU:0, one launch (start us, length us, event | category | flops | bytes accessed | tf_op | source)
XLA Modules:
  0.0 504.4 jit_solution(13818489839785445901)
XLA Ops:
  11.5 4.1 collective-permute-start.8
  15.7 3.0 collective-permute-start
  25.8 29.5 %collective-permute-done.5 = bf16[2,24,768]{2,1,0:T(8,128)(2,1)S(1)} collective-permute-done((bf16[2,24,768]{2,1,0:T(8,128)(2,1)S(1)}, bf16[2,24,768]{2,1,0:T(8,128)(2,1)S(1)}, u32[]{:S(2)}, u32[]{:S(2)}) %collective-permute-start.5) | collective-permute-done | bytes 73760 | tf_op jit(solution)/shard_map/ppermute | solution.py:328
  55.3 1.6 collective-permute-start.6
  59.3 7.7 %collective-permute-done.6 = bf16[2,2,24,768]{3,2,0,1:T(8,128)(2,1)S(1)} collective-permute-done((bf16[2,2,24,768]{3,2,0,1:T(8,128)(2,1)S(1)}, bf16[2,2,24,768]{3,2,0,1:T(8,128)(2,1)S(1)}, u32[]{:S(2)}, u32[]{:S(2)}) %collective-permute-start.6) | collective-permute-done | bytes 147488 | tf_op jit(solution)/shard_map/ppermute | solution.py:328
  71.4 2.4 collective-permute-done.7
  73.9 2.1 collective-permute-done.3
  76.0 1.7 fusion.131
  82.0 1.7 fusion.35
  83.7 3.1 maximum_select_fusion
  87.1 1.8 slice_reduce_fusion
  88.9 3.5 add_convert_fusion
  92.6 1.6 copy-done.15
  95.1 4.5 add_convert_fusion.1
  99.7 2.8 fusion.8.k_ref.v_ref
  102.5 34.7 %shard_map.293 = (bf16[768,768]{1,0:T(8,128)(2,1)S(1)}, f32[768,768]{1,0:T(8,128)S(1)}) custom-call(bf16[768,768]{1,0:T(8,128)(2,1)S(1)} %pad.24.q_ref, bf16[1536,1536]{1,0:T(8,128)(2,1)} %fusion.8.k_ref.v_ref, bf16[1536,1536]{1,0:T(8,128)(2,1)} %fusion.8.k_ref.v_ref, f32[1,1536]{1,0:T(1,128)S(1)} %compare_select_fusion.kbias_ref), custom_call_target="tpu_custom_call" | custom-call | tf_op jit(solution)/shard_map/pallas_call | solution.py:157
  138.5 2.5 fusion.141
  142.8 4.8 slice.284
  147.6 8.5 %reshape.1313 = bf16[3072,768]{1,0:T(8,128)(2,1)} reshape(bf16[768,3072]{1,0:T(8,128)(2,1)} %slice.284) | data formatting | bytes 9437184 | tf_op jit(solution)/shard_map/reshape | solution.py:405
  156.1 9.9 %multiply_convert_fusion = (bf16[750,3072]{1,0:T(8,128)(2,1)}, f32[750,3072]{1,0:T(8,128)}) fusion(f32[3072]{0:T(1024)S(1)} %copy-done.66, bf16[768,6912]{1,0:T(8,128)(2,1)} %all-gather.2.cloned.1.call-done, f32[750,768]{1,0:T(8,128)} %copy-done.13, f32[768]{0:T(1024)S(1)} %copy-done.72, f32[768]{0:T(1024)S(1)} %get-tuple-element.146, ...), kind=kOutput, calls=%fused_computation.11 | convolution fusion | flops 3555648000 | bytes 20877168 | tf_op jit(solution)/shard_map/dot_general | solution.py:440
  166.1 8.9 %convert_reduce_fusion = (f32[3072]{0:T(1024)S(1)}, bf16[750,3072]{1,0:T(8,128)(2,1)S(1)}) fusion(f32[750,3072]{1,0:T(8,128)} %get-tuple-element.213, f32[3072]{0:T(1024)S(1)} %copy-done.66, bf16[3072,768]{1,0:T(8,128)(2,1)S(1)} %copy-done.20, bf16[1,750,768]{2,1,0:T(8,128)(2,1)S(1)} %copy-done.45), kind=kOutput, calls=%fused_computation.10 | convolution fusion | flops 3568892928 | bytes 19719168 | tf_op jit(solution)/shard_map/dot_general | solution.py:454
  175.0 5.0 convolution_convert_fusion
  180.0 4.3 multiply_reduce_fusion
  187.3 19.2 %shard_map.294 = (f32[768,256]{1,0:T(8,128)S(1)}, f32[1536,256]{1,0:T(8,128)S(1)}, f32[1536,256]{1,0:T(8,128)}) custom-call(bf16[768,768]{1,0:T(8,128)(2,1)S(1)} %pad.24.q_ref, bf16[1536,1536]{1,0:T(8,128)(2,1)} %fusion.8.k_ref.v_ref, bf16[1536,1536]{1,0:T(8,128)(2,1)} %fusion.8.k_ref.v_ref, bf16[768,768]{1,0:T(8,128)(2,1)S(1)} %pad.26.do_ref, ...), custom_call_target="tpu_custom_call" | custom-call | tf_op jit(solution)/shard_map/pallas_call | solution.py:176
  206.6 1.8 copy-done.35
  209.6 1.9 collective-permute-start.23
  211.5 1.9 constant_dynamic-slice_fusion.11
  215.1 6.1 %convolution_convert_fusion.1 = bf16[3072,768]{1,0:T(8,128)(2,1)} fusion(bf16[750,3072]{1,0:T(8,128)(2,1)S(1)} %bitcast.439, bf16[1,750,768]{2,1,0:T(8,128)(2,1)S(1)} %copy-done.46), kind=kOutput, calls=%fused_computation.15 | convolution fusion | flops 3541303296 | bytes 10478592 | tf_op jit(solution)/shard_map/dot_general | solution.py:450
  221.2 8.5 %reshape_reshape.3 = bf16[2,2,2,2,2,24,3072]{6,5,4,3,2,1,0:T(8,128)(2,1)} reshape(bf16[3072,768]{1,0:T(8,128)(2,1)} %convolution_convert_fusion.1) | data formatting | bytes 9437184 | tf_op jit(solution)/shard_map/reshape;reshape | solution.py:296
  229.6 3.5 dynamic-slice_bitcast_fusion
  242.0 9.2 %fusion.46 = bf16[1,750,768]{2,1,0:T(8,128)(2,1)} fusion(f32[750,768]{1,0:T(8,128)} %copy-done.13, bf16[750,3072]{1,0:T(8,128)(2,1)} %get-tuple-element.212, bf16[3072,768]{1,0:T(8,128)(2,1)} %reshape.1313, f32[768]{0:T(1024)S(1)} %copy-done.71), kind=kOutput, calls=%fused_computation.97 | convolution fusion | flops 3540672000 | bytes 12785664 | tf_op jit(solution)/shard_map/dot_general | solution.py:444
  253.4 2.6 convert_add_fusion
  256.1 2.7 convert_add_fusion.1
  266.3 19.1 %shard_map.295 = (f32[768,256]{1,0:T(8,128)S(1)}, f32[1536,256]{1,0:T(8,128)S(1)}, f32[1536,256]{1,0:T(8,128)}) custom-call(bf16[768,768]{1,0:T(8,128)(2,1)S(1)} %pad.24.q_ref, bf16[1536,1536]{1,0:T(8,128)(2,1)} %fusion.8.k_ref.v_ref, bf16[1536,1536]{1,0:T(8,128)(2,1)} %fusion.8.k_ref.v_ref, bf16[768,768]{1,0:T(8,128)(2,1)S(1)} %pad.27.do_ref, ...), custom_call_target="tpu_custom_call" | custom-call | tf_op jit(solution)/shard_map/pallas_call | solution.py:176
  287.0 7.8 %collective-permute-done.19 = bf16[2,2,2,24,768]{4,3,0,2,1:T(8,128)(2,1)} collective-permute-done((bf16[2,2,2,24,768]{4,3,0,2,1:T(8,128)(2,1)}, bf16[2,2,2,24,768]{4,3,0,2,1:T(8,128)(2,1)}, u32[]{:S(2)}, u32[]{:S(2)}) %collective-permute-start.19) | collective-permute-done | bytes 294944 | tf_op jit(solution)/shard_map/ppermute | solution.py:307
  295.9 1.6 bitcast_add_fusion.1
  302.2 19.3 %shard_map.296 = (f32[768,256]{1,0:T(8,128)S(1)}, f32[1536,256]{1,0:T(8,128)S(1)}, f32[1536,256]{1,0:T(8,128)}) custom-call(bf16[768,768]{1,0:T(8,128)(2,1)S(1)} %pad.24.q_ref, bf16[1536,1536]{1,0:T(8,128)(2,1)} %fusion.8.k_ref.v_ref, bf16[1536,1536]{1,0:T(8,128)(2,1)} %fusion.8.k_ref.v_ref, bf16[768,768]{1,0:T(8,128)(2,1)S(1)} %pad.28.do_ref, ...), custom_call_target="tpu_custom_call" | custom-call | tf_op jit(solution)/shard_map/pallas_call | solution.py:176
  323.1 2.1 collective-permute-start.20
  326.0 11.5 %collective-permute-done.20 = bf16[2,2,24,3072]{3,2,1,0:T(8,128)(2,1)S(1)} collective-permute-done((bf16[2,2,24,3072]{3,2,1,0:T(8,128)(2,1)S(1)}, bf16[2,2,24,3072]{3,2,1,0:T(8,128)(2,1)S(1)}, u32[]{:S(2)}, u32[]{:S(2)}) %collective-permute-start.20) | collective-permute-done | bytes 589856 | tf_op jit(solution)/shard_map/ppermute | solution.py:307
  338.2 3.8 fusion.52
  342.0 2.5 convolution_convert_fusion.4
  345.0 1.6 copy-done.18
  354.0 22.0 %collective-permute-done.41 = bf16[2,24,768]{2,1,0:T(8,128)(2,1)S(1)} collective-permute-done((bf16[2,24,768]{2,1,0:T(8,128)(2,1)S(1)}, bf16[2,24,768]{2,1,0:T(8,128)(2,1)S(1)}, u32[]{:S(2)}, u32[]{:S(2)}) %collective-permute-start.41) | collective-permute-done | bytes 73760 | tf_op jit(solution)/shard_map/ppermute | solution.py:307
  380.0 1.9 collective-permute-done.42
  387.2 1.8 collective-permute-start.44
  389.0 10.8 %collective-permute-done.46 = bf16[24,3072]{1,0:T(8,128)(2,1)S(1)} collective-permute-done((bf16[24,3072]{1,0:T(8,128)(2,1)S(1)}, bf16[24,3072]{1,0:T(8,128)(2,1)S(1)}, u32[]{:S(2)}, u32[]{:S(2)}) %collective-permute-start.46) | collective-permute-done | bytes 147488 | tf_op jit(solution)/shard_map/ppermute | solution.py:307
  402.6 2.0 fusion.106
  412.7 3.8 fusion.50
  416.6 2.5 convolution_convert_fusion.3
  419.3 2.5 convolution_convert_fusion.2
  422.9 6.4 %fusion.30 = (f32[768]{0:T(1024)S(1)}, f32[750]{0:T(1024)S(1)}, f32[750]{0:T(1024)S(1)}, f32[768]{0:T(1024)S(1)}, f32[750,768]{1,0:T(8,128)}) fusion(bf16[1,750,768]{2,1,0:T(8,128)(2,1)S(1)} %copy-done.8, f32[750]{0:T(1024)S(1)} %copy-done.63, f32[750]{0:T(1024)S(1)} %broadcast_multiply_fusion.6, f32[768]{0:T(1024)S(1)} %copy-done.59, ...), kind=kOutput, calls=%fused_computation.57 | convolution fusion | flops 895100928 | bytes 10432224 | tf_op jit(solution)/shard_map/dot_general | solution.py:515
  432.1 3.9 concatenate.349
  441.5 3.6 collective-permute-done.48
  446.7 1.8 fusion.55
  450.1 2.6 collective-permute-done.50
  454.5 2.9 collective-permute-done.51
  460.8 4.0 collective-permute-done.29
  467.5 2.3 collective-permute-done.30
  473.9 3.9 collective-permute-done.32
  478.2 2.4 collective-permute-done.37
  481.5 2.1 collective-permute-done.33
  484.2 1.6 collective-permute-done.38
  491.2 1.8 collective-permute-done.35
  493.0 2.3 collective-permute-done.40
  (450 shorter events, 123.0 us)
Async XLA Ops:
  7.2 131.3 %all-gather.2.cloned.1.call-start = ((), (), s32[]{:S(2)}) async-start(), calls=%async_computation | async-start | bytes 10948608 | tf_op jit(solution)/shard_map/all_gather | solution.py:398
  11.5 8.7 %collective-permute-start.8 = (bf16[24,768]{1,0:T(8,128)(2,1)S(1)}, bf16[24,768]{1,0:T(8,128)(2,1)S(1)}, u32[]{:S(2)}, u32[]{:S(2)}) collective-permute-start(bf16[24,768]{1,0:T(8,128)(2,1)S(1)} %get-tuple-element.195), channel_id=1, source_target_pairs={{0,16},{1,17},{2,18},{3,19},{4,20},{5,21},{6,22},{7,23},{8,24},{9,... | collective-permute-start | bytes 110600 | tf_op jit(solution)/shard_map/ppermute | solution.py:328
  15.6 6.2 %collective-permute-start.4 = (bf16[24,768]{1,0:T(8,128)(2,1)S(1)}, bf16[24,768]{1,0:T(8,128)(2,1)S(1)}, u32[]{:S(2)}, u32[]{:S(2)}) collective-permute-start(bf16[24,768]{1,0:T(8,128)(2,1)S(1)} %get-tuple-element.201), channel_id=1, source_target_pairs={{0,16},{1,17},{2,18},{3,19},{4,20},{5,21},{6,22},{7,23},{8,24},{9,... | collective-permute-start | bytes 110600 | tf_op jit(solution)/shard_map/ppermute | solution.py:328
  15.7 6.9 %collective-permute-start = (bf16[24,896]{1,0:T(8,128)(2,1)S(1)}, bf16[24,896]{1,0:T(8,128)(2,1)S(1)}, u32[]{:S(2)}, u32[]{:S(2)}) collective-permute-start(bf16[24,896]{1,0:T(8,128)(2,1)S(1)} %get-tuple-element.198), channel_id=1, source_target_pairs={{0,16},{1,17},{2,18},{3,19},{4,20},{5,21},{6,22},{7,23},{8,24},{9,... | collective-permute-start | bytes 129032 | tf_op jit(solution)/shard_map/ppermute | solution.py:328
  18.7 61.7 %collective-permute-start.13 = (bf16[1,750,768]{2,1,0:T(8,128)(2,1)S(1)}, bf16[1,750,768]{2,1,0:T(8,128)(2,1)}, u32[]{:S(2)}, u32[]{:S(2)}) collective-permute-start(bf16[1,750,768]{2,1,0:T(8,128)(2,1)S(1)} %copy-done.7), channel_id=1, source_target_pairs={{0,1},{1,0},{2,3},{3,2},{4,5},{5,4},{6,7},{7,6},{8,9},{9,8},{10,11... | collective-permute-start | bytes 3456008 | tf_op jit(solution)/shard_map/ppermute | solution.py:412
  20.3 4.4 collective-permute-start.9
  21.9 33.4 %collective-permute-start.5 = (bf16[2,24,768]{2,1,0:T(8,128)(2,1)S(1)}, bf16[2,24,768]{2,1,0:T(8,128)(2,1)S(1)}, u32[]{:S(2)}, u32[]{:S(2)}) collective-permute-start(bf16[2,24,768]{2,1,0:T(8,128)(2,1)S(1)} %maximum_select_fusion.17), channel_id=1, source_target_pairs={{0,1},{1,0},{2,3},{3,2},{4,5},{5,4},{6,7},{7,6},{8,9},{9,8},{10,11... | collective-permute-start | bytes 221192 | tf_op jit(solution)/shard_map/ppermute | solution.py:328
  22.7 34.4 %collective-permute-start.1 = (bf16[2,24,896]{2,1,0:T(8,128)(2,1)S(1)}, bf16[2,24,896]{2,1,0:T(8,128)(2,1)S(1)}, u32[]{:S(2)}, u32[]{:S(2)}) collective-permute-start(bf16[2,24,896]{2,1,0:T(8,128)(2,1)S(1)} %maximum_select_fusion.15), channel_id=1, source_target_pairs={{0,8},{1,9},{2,10},{3,11},{4,12},{5,13},{6,14},{7,15},{8,0},{9,1},... | collective-permute-start | bytes 258056 | tf_op jit(solution)/shard_map/ppermute | solution.py:328
  24.7 34.0 %collective-permute-start.10 = (bf16[2,2,24,768]{3,2,1,0:T(8,128)(2,1)S(1)}, bf16[2,2,24,768]{3,2,1,0:T(8,128)(2,1)S(1)}, u32[]{:S(2)}, u32[]{:S(2)}) collective-permute-start(bf16[2,2,24,768]{3,2,1,0:T(8,128)(2,1)S(1)} %maximum_select_fusion.13), channel_id=1, source_target_pairs={{0,1},{1,0},{2,3},{3,2},{4,5},{5,4},{6,7},{7,6},{8,9},{9,8},{10,11... | collective-permute-start | bytes 442376 | tf_op jit(solution)/shard_map/ppermute | solution.py:328
  55.3 11.7 %collective-permute-start.6 = (bf16[2,2,24,768]{3,2,0,1:T(8,128)(2,1)S(1)}, bf16[2,2,24,768]{3,2,0,1:T(8,128)(2,1)S(1)}, u32[]{:S(2)}, u32[]{:S(2)}) collective-permute-start(bf16[2,2,24,768]{3,2,0,1:T(8,128)(2,1)S(1)} %maximum_select_fusion.12), channel_id=1, source_target_pairs={{0,8},{1,9},{2,10},{3,11},{4,12},{5,13},{6,14},{7,15},{8,0},{9,1},... | collective-permute-start | bytes 442376 | tf_op jit(solution)/shard_map/ppermute | solution.py:328
  57.2 11.4 %collective-permute-start.2 = (bf16[2,2,24,896]{3,2,0,1:T(8,128)(2,1)S(1)}, bf16[2,2,24,896]{3,2,0,1:T(8,128)(2,1)S(1)}, u32[]{:S(2)}, u32[]{:S(2)}) collective-permute-start(bf16[2,2,24,896]{3,2,0,1:T(8,128)(2,1)S(1)} %maximum_select_fusion.10), channel_id=1, source_target_pairs={{0,4},{1,5},{2,6},{3,7},{4,0},{5,1},{6,2},{7,3},{8,12},{9,13},{10,... | collective-permute-start | bytes 516104 | tf_op jit(solution)/shard_map/ppermute | solution.py:328
  58.8 12.6 %collective-permute-start.11 = (bf16[2,2,2,24,768]{4,3,2,1,0:T(8,128)(2,1)S(1)}, bf16[2,2,2,24,768]{4,3,2,1,0:T(8,128)(2,1)S(1)}, u32[]{:S(2)}, u32[]{:S(2)}) collective-permute-start(bf16[2,2,2,24,768]{4,3,2,1,0:T(8,128)(2,1)S(1)} %maximum_select_fusion.8), channel_id=1, source_target_pairs={{0,8},{1,9},{2,10},{3,11},{4,12},{5,13},{6,14},{7,15},{8,0},{9,1},... | collective-permute-start | bytes 884744 | tf_op jit(solution)/shard_map/ppermute | solution.py:328
  67.1 6.8 %collective-permute-start.7 = (bf16[2,2,2,24,768]{4,3,0,2,1:T(8,128)(2,1)S(1)}, bf16[2,2,2,24,768]{4,3,0,2,1:T(8,128)(2,1)S(1)}, u32[]{:S(2)}, u32[]{:S(2)}) collective-permute-start(bf16[2,2,2,24,768]{4,3,0,2,1:T(8,128)(2,1)S(1)} %maximum_select_fusion.7), channel_id=1, source_target_pairs={{0,4},{1,5},{2,6},{3,7},{4,0},{5,1},{6,2},{7,3},{8,12},{9,13},{10,... | collective-permute-start | bytes 884744 | tf_op jit(solution)/shard_map/ppermute | solution.py:328
  68.7 7.3 %collective-permute-start.3 = (bf16[2,2,2,24,896]{4,3,0,1,2:T(8,128)(2,1)S(1)}, bf16[2,2,2,24,896]{4,3,0,1,2:T(8,128)(2,1)S(1)}, u32[]{:S(2)}, u32[]{:S(2)}) collective-permute-start(bf16[2,2,2,24,896]{4,3,0,1,2:T(8,128)(2,1)S(1)} %maximum_select_fusion.5), channel_id=1, source_target_pairs={{0,1},{1,0},{2,3},{3,2},{4,5},{5,4},{6,7},{7,6},{8,9},{9,8},{10,11... | collective-permute-start | bytes 1032200 | tf_op jit(solution)/shard_map/ppermute | solution.py:328
  77.7 6.1 %collective-permute-start.12 = (bf16[2,2,2,2,24,2432]{5,4,3,2,1,0:T(8,128)(2,1)}, bf16[2,2,2,2,24,2432]{5,4,3,2,1,0:T(8,128)(2,1)}, u32[]{:S(2)}, u32[]{:S(2)}) collective-permute-start(bf16[2,2,2,2,24,2432]{5,4,3,2,1,0:T(8,128)(2,1)} %get-tuple-element.165), channel_id=1, source_target_pairs={{0,2},{1,3},{2,0},{3,1},{4,6},{5,7},{6,4},{7,5},{8,10},{9,11},{10,... | collective-permute-start | bytes 5603336 | tf_op jit(solution)/shard_map/ppermute | solution.py:328
  88.9 253.1 %copy-start.58 = (f32[768]{0:T(1024)}, f32[768]{0:T(1024)S(1)}, u32[]{:S(2)}) copy-start(f32[768]{0:T(1024)S(1)} %get-tuple-element.151) | copy-start | bytes 9220
  102.5 36.1 %copy-start.73 = (f32[768]{0:T(1024)S(1)}, f32[768]{0:T(1024)}, u32[]{:S(2)}) copy-start(f32[768]{0:T(1024)} %get-tuple-element.147) | copy-start | bytes 9220
  156.1 23.9 %slice-start.3 = ((s8[10616832]{0:T(1024)(128)(4,1)}), s8[4194304]{0:T(1024)(128)(4,1)S(1)}, s32[]{:S(2)}) async-start(s8[10616832]{0:T(1024)(128)(4,1)} %bitcast.401), calls=%async_computation.4 | async-start | bytes 8388608
  166.0 13.9 %slice-start.4 = ((s8[10616832]{0:T(1024)(128)(4,1)}), s8[4194304]{0:T(1024)(128)(4,1)S(1)}, s32[]{:S(2)}) async-start(s8[10616832]{0:T(1024)(128)(4,1)} %bitcast.401), calls=%async_computation.5 | async-start | bytes 8388608
  187.2 19.3 %copy-start.5 = (bf16[750,768]{1,0:T(8,128)(2,1)}, bf16[750,768]{1,0:T(8,128)(2,1)S(1)}, u32[]{:S(2)}) copy-start(bf16[750,768]{1,0:T(8,128)(2,1)S(1)} %convolution_convert_fusion.6) | copy-start | bytes 3456004
  209.6 50.4 %collective-permute-start.23 = (bf16[750,512]{1,0:T(8,128)(2,1)}, bf16[750,512]{1,0:T(8,128)(2,1)}, u32[]{:S(2)}, u32[]{:S(2)}) collective-permute-start(bf16[750,512]{1,0:T(8,128)(2,1)} %fusion.45), channel_id=1, source_target_pairs={{0,1},{1,0},{2,3},{3,2},{4,5},{5,4},{6,7},{7,6},{8,9},{9,8},{10,11... | collective-permute-start | bytes 2304008 | tf_op jit(solution)/shard_map/ppermute | solution.py:495
  214.9 38.5 %collective-permute-start.15 = (bf16[2,2,2,2,24,3072]{5,4,0,3,2,1:T(8,128)(2,1)}, bf16[2,2,2,2,24,3072]{5,4,0,3,2,1:T(8,128)(2,1)}, u32[]{:S(2)}, u32[]{:S(2)}) collective-permute-start(bf16[2,2,2,2,24,3072]{5,4,0,3,2,1:T(8,128)(2,1)} %bitcast.387), channel_id=1, source_target_pairs={{0,2},{1,3},{2,0},{3,1},{4,6},{5,7},{6,4},{7,5},{8,10},{9,11},{10,... | collective-permute-start | bytes 7077896 | tf_op jit(solution)/shard_map/ppermute | solution.py:307
  233.1 23.0 %collective-permute-start.14 = (bf16[2,2,2,2,24,3072]{5,4,3,2,1,0:T(8,128)(2,1)}, bf16[2,2,2,2,24,3072]{5,4,3,2,1,0:T(8,128)(2,1)}, u32[]{:S(2)}, u32[]{:S(2)}) collective-permute-start(bf16[2,2,2,2,24,3072]{5,4,3,2,1,0:T(8,128)(2,1)} %dynamic-slice_bitcast_fusion), channel_id=1, source_target_pairs={{0,2},{1,3},{2,0},{3,1},{4,6},{5,7},{6,4},{7,5},{8,10},{9,11},{10,... | collective-permute-start | bytes 7077896 | tf_op jit(solution)/shard_map/ppermute | solution.py:307
  235.6 15.6 %collective-permute-start.16 = (bf16[2,2,2,2,24,768]{5,4,0,3,1,2:T(8,128)(2,1)S(1)}, bf16[2,2,2,2,24,768]{5,4,0,3,1,2:T(8,128)(2,1)S(1)}, u32[]{:S(2)}, u32[]{:S(2)}) collective-permute-start(bf16[2,2,2,2,24,768]{5,4,0,3,1,2:T(8,128)(2,1)S(1)} %bitcast.419), channel_id=1, source_target_pairs={{0,2},{1,3},{2,0},{3,1},{4,6},{5,7},{6,4},{7,5},{8,10},{9,11},{10,... | collective-permute-start | bytes 1769480 | tf_op jit(solution)/shard_map/ppermute | solution.py:307
  260.0 35.9 %collective-permute-start.17 = (bf16[2,2,2,24,3072]{4,3,2,1,0:T(8,128)(2,1)}, bf16[2,2,2,24,3072]{4,3,2,1,0:T(8,128)(2,1)}, u32[]{:S(2)}, u32[]{:S(2)}) collective-permute-start(bf16[2,2,2,24,3072]{4,3,2,1,0:T(8,128)(2,1)} %fusion.47), channel_id=1, source_target_pairs={{0,4},{1,5},{2,6},{3,7},{4,0},{5,1},{6,2},{7,3},{8,12},{9,13},{10,... | collective-permute-start | bytes 3538952 | tf_op jit(solution)/shard_map/ppermute | solution.py:307
  262.7 32.2 %collective-permute-start.19 = (bf16[2,2,2,24,768]{4,3,0,2,1:T(8,128)(2,1)}, bf16[2,2,2,24,768]{4,3,0,2,1:T(8,128)(2,1)}, u32[]{:S(2)}, u32[]{:S(2)}) collective-permute-start(bf16[2,2,2,24,768]{4,3,0,2,1:T(8,128)(2,1)} %fusion.76), channel_id=1, source_target_pairs={{0,4},{1,5},{2,6},{3,7},{4,0},{5,1},{6,2},{7,3},{8,12},{9,13},{10,... | collective-permute-start | bytes 884744 | tf_op jit(solution)/shard_map/ppermute | solution.py:307
  265.3 32.2 %collective-permute-start.18 = (bf16[2,2,2,24,3072]{4,3,0,2,1:T(8,128)(2,1)}, bf16[2,2,2,24,3072]{4,3,0,2,1:T(8,128)(2,1)}, u32[]{:S(2)}, u32[]{:S(2)}) collective-permute-start(bf16[2,2,2,24,3072]{4,3,0,2,1:T(8,128)(2,1)} %fusion.48), channel_id=1, source_target_pairs={{0,8},{1,9},{2,10},{3,11},{4,12},{5,13},{6,14},{7,15},{8,0},{9,1},... | collective-permute-start | bytes 3538952 | tf_op jit(solution)/shard_map/ppermute | solution.py:307
  300.9 82.4 %collective-permute-start.24 = (bf16[750,512]{1,0:T(8,128)(2,1)}, bf16[750,512]{1,0:T(8,128)(2,1)}, u32[]{:S(2)}, u32[]{:S(2)}) collective-permute-start(bf16[750,512]{1,0:T(8,128)(2,1)} %slice.413), channel_id=1, source_target_pairs={{0,1},{1,0},{2,3},{3,2},{4,5},{5,4},{6,7},{7,6},{8,9},{9,8},{10,11... | collective-permute-start | bytes 2304008 | tf_op jit(solution)/shard_map/ppermute | solution.py:495
  301.6 24.3 %collective-permute-start.21 = (bf16[2,2,24,3072]{3,2,0,1:T(8,128)(2,1)S(1)}, bf16[2,2,24,3072]{3,2,0,1:T(8,128)(2,1)S(1)}, u32[]{:S(2)}, u32[]{:S(2)}) collective-permute-start(bf16[2,2,24,3072]{3,2,0,1:T(8,128)(2,1)S(1)} %fusion.67), channel_id=1, source_target_pairs={{0,4},{1,5},{2,6},{3,7},{4,0},{5,1},{6,2},{7,3},{8,12},{9,13},{10,... | collective-permute-start | bytes 1769480 | tf_op jit(solution)/shard_map/ppermute | solution.py:307
  301.9 23.2 %collective-permute-start.22 = (bf16[2,2,24,768]{3,2,0,1:T(8,128)(2,1)S(1)}, bf16[2,2,24,768]{3,2,0,1:T(8,128)(2,1)S(1)}, u32[]{:S(2)}, u32[]{:S(2)}) collective-permute-start(bf16[2,2,24,768]{3,2,0,1:T(8,128)(2,1)S(1)} %fusion.93), channel_id=1, source_target_pairs={{0,8},{1,9},{2,10},{3,11},{4,12},{5,13},{6,14},{7,15},{8,0},{9,1},... | collective-permute-start | bytes 442376 | tf_op jit(solution)/shard_map/ppermute | solution.py:307
  323.1 14.5 %collective-permute-start.20 = (bf16[2,2,24,3072]{3,2,1,0:T(8,128)(2,1)S(1)}, bf16[2,2,24,3072]{3,2,1,0:T(8,128)(2,1)S(1)}, u32[]{:S(2)}, u32[]{:S(2)}) collective-permute-start(bf16[2,2,24,3072]{3,2,1,0:T(8,128)(2,1)S(1)} %fusion.66), channel_id=1, source_target_pairs={{0,8},{1,9},{2,10},{3,11},{4,12},{5,13},{6,14},{7,15},{8,0},{9,1},... | collective-permute-start | bytes 1769480 | tf_op jit(solution)/shard_map/ppermute | solution.py:307
  347.7 63.4 %collective-permute-start.25 = (bf16[750,512]{1,0:T(8,128)(2,1)}, bf16[750,512]{1,0:T(8,128)(2,1)}, u32[]{:S(2)}, u32[]{:S(2)}) collective-permute-start(bf16[750,512]{1,0:T(8,128)(2,1)} %slice.412), channel_id=1, source_target_pairs={{0,1},{1,0},{2,3},{3,2},{4,5},{5,4},{6,7},{7,6},{8,9},{9,8},{10,11... | collective-permute-start | bytes 2304008 | tf_op jit(solution)/shard_map/ppermute | solution.py:495
  350.2 28.0 %copy-start.40 = (bf16[768,768]{1,0:T(8,128)(2,1)S(1)}, bf16[768,768]{1,0:T(8,128)(2,1)}, u32[]{:S(2)}) copy-start(bf16[768,768]{1,0:T(8,128)(2,1)} %convolution_convert_fusion.4) | copy-start | bytes 3538948
  350.3 35.4 %collective-permute-start.45 = (bf16[2,24,3072]{2,1,0:T(8,128)(2,1)S(1)}, bf16[2,24,3072]{2,1,0:T(8,128)(2,1)S(1)}, u32[]{:S(2)}, u32[]{:S(2)}) collective-permute-start(bf16[2,24,3072]{2,1,0:T(8,128)(2,1)S(1)} %fusion.81), channel_id=1, source_target_pairs={{0,1},{1,0},{2,3},{3,2},{4,5},{5,4},{6,7},{7,6},{8,9},{9,8},{10,11... | collective-permute-start | bytes 884744 | tf_op jit(solution)/shard_map/ppermute | solution.py:307
  351.8 30.1 %copy-start.52 = (f32[2,24,768]{2,1,0:T(8,128)S(1)}, f32[2,24,768]{2,1,0:T(8,128)}, u32[]{:S(2)}) copy-start(f32[2,24,768]{2,1,0:T(8,128)} %param.23) | copy-start | bytes 442372
  351.8 30.1 %copy-start.53 = (f32[24,768]{1,0:T(8,128)S(1)}, f32[24,768]{1,0:T(8,128)}, u32[]{:S(2)}) copy-start(f32[24,768]{1,0:T(8,128)} %param.17) | copy-start | bytes 221188
  351.8 24.1 %collective-permute-start.41 = (bf16[2,24,768]{2,1,0:T(8,128)(2,1)S(1)}, bf16[2,24,768]{2,1,0:T(8,128)(2,1)S(1)}, u32[]{:S(2)}, u32[]{:S(2)}) collective-permute-start(bf16[2,24,768]{2,1,0:T(8,128)(2,1)S(1)} %fusion.105), channel_id=1, source_target_pairs={{0,1},{1,0},{2,3},{3,2},{4,5},{5,4},{6,7},{7,6},{8,9},{9,8},{10,11... | collective-permute-start | bytes 221192 | tf_op jit(solution)/shard_map/ppermute | solution.py:307
  353.4 33.7 %collective-permute-start.43 = (bf16[2,24,3072]{2,1,0:T(8,128)(2,1)S(1)}, bf16[2,24,3072]{2,1,0:T(8,128)(2,1)S(1)}, u32[]{:S(2)}, u32[]{:S(2)}) collective-permute-start(bf16[2,24,3072]{2,1,0:T(8,128)(2,1)S(1)} %fusion.80), channel_id=1, source_target_pairs={{0,1},{1,0},{2,3},{3,2},{4,5},{5,4},{6,7},{7,6},{8,9},{9,8},{10,11... | collective-permute-start | bytes 884744 | tf_op jit(solution)/shard_map/ppermute | solution.py:307
  376.9 4.9 collective-permute-start.42
  381.8 25.6 %collective-permute-start.26 = (bf16[2,2,2,2,24,768]{5,4,0,1,2,3:T(8,128)(2,1)}, bf16[2,2,2,2,24,768]{5,4,0,1,2,3:T(8,128)(2,1)}, u32[]{:S(2)}, u32[]{:S(2)}) collective-permute-start(bf16[2,2,2,2,24,768]{5,4,0,1,2,3:T(8,128)(2,1)} %bitcast.390), channel_id=1, source_target_pairs={{0,2},{1,3},{2,0},{3,1},{4,6},{5,7},{6,4},{7,5},{8,10},{9,11},{10,... | collective-permute-start | bytes 1769480 | tf_op jit(solution)/shard_map/ppermute | solution.py:307
  385.8 16.8 %copy-start.37 = (f32[2,24,3072]{2,1,0:T(8,128)S(1)}, f32[2,24,3072]{2,1,0:T(8,128)}, u32[]{:S(2)}) copy-start(f32[2,24,3072]{2,1,0:T(8,128)} %param.24) | copy-start | bytes 1769476
  385.8 13.9 %collective-permute-start.46 = (bf16[24,3072]{1,0:T(8,128)(2,1)S(1)}, bf16[24,3072]{1,0:T(8,128)(2,1)S(1)}, u32[]{:S(2)}, u32[]{:S(2)}) collective-permute-start(bf16[24,3072]{1,0:T(8,128)(2,1)S(1)} %fusion.98), channel_id=1, source_target_pairs={{0,16},{1,17},{2,18},{3,19},{4,20},{5,21},{6,22},{7,23},{8,24},{9,... | collective-permute-start | bytes 442376 | tf_op jit(solution)/shard_map/ppermute | solution.py:307
  387.2 15.3 %collective-permute-start.44 = (bf16[24,3072]{1,0:T(8,128)(2,1)S(1)}, bf16[24,3072]{1,0:T(8,128)(2,1)S(1)}, u32[]{:S(2)}, u32[]{:S(2)}) collective-permute-start(bf16[24,3072]{1,0:T(8,128)(2,1)S(1)} %fusion.97), channel_id=1, source_target_pairs={{0,16},{1,17},{2,18},{3,19},{4,20},{5,21},{6,22},{7,23},{8,24},{9,... | collective-permute-start | bytes 442376 | tf_op jit(solution)/shard_map/ppermute | solution.py:307
  409.7 39.4 %collective-permute-start.27 = (bf16[2,2,2,24,768]{4,3,0,1,2:T(8,128)(2,1)}, bf16[2,2,2,24,768]{4,3,0,1,2:T(8,128)(2,1)}, u32[]{:S(2)}, u32[]{:S(2)}) collective-permute-start(bf16[2,2,2,24,768]{4,3,0,1,2:T(8,128)(2,1)} %fusion.77), channel_id=1, source_target_pairs={{0,1},{1,0},{2,3},{3,2},{4,5},{5,4},{6,7},{7,6},{8,9},{9,8},{10,11... | collective-permute-start | bytes 884744 | tf_op jit(solution)/shard_map/ppermute | solution.py:307
  437.0 3.8 collective-permute-start.47
  439.3 30.4 %collective-permute-start.31 = (bf16[2,2,2,2,24,768]{5,4,0,3,1,2:T(8,128)(2,1)}, bf16[2,2,2,2,24,768]{5,4,0,3,1,2:T(8,128)(2,1)}, u32[]{:S(2)}, u32[]{:S(2)}) collective-permute-start(bf16[2,2,2,2,24,768]{5,4,0,3,1,2:T(8,128)(2,1)} %bitcast.389), channel_id=1, source_target_pairs={{0,2},{1,3},{2,0},{3,1},{4,6},{5,7},{6,4},{7,5},{8,10},{9,11},{10,... | collective-permute-start | bytes 1769480 | tf_op jit(solution)/shard_map/ppermute | solution.py:307
  440.8 31.8 %collective-permute-start.36 = (bf16[2,2,2,2,24,768]{5,4,0,2,3,1:T(8,128)(2,1)}, bf16[2,2,2,2,24,768]{5,4,0,2,3,1:T(8,128)(2,1)}, u32[]{:S(2)}, u32[]{:S(2)}) collective-permute-start(bf16[2,2,2,2,24,768]{5,4,0,2,3,1:T(8,128)(2,1)} %bitcast.388), channel_id=1, source_target_pairs={{0,2},{1,3},{2,0},{3,1},{4,6},{5,7},{6,4},{7,5},{8,10},{9,11},{10,... | collective-permute-start | bytes 1769480 | tf_op jit(solution)/shard_map/ppermute | solution.py:307
  440.8 4.2 collective-permute-start.48
  445.1 3.9 collective-permute-start.49
  449.0 3.8 collective-permute-start.50
  452.8 4.6 collective-permute-start.51
  452.9 7.0 %collective-permute-start.28 = (bf16[2,2,24,768]{3,2,0,1:T(8,128)(2,1)S(1)}, bf16[2,2,24,768]{3,2,0,1:T(8,128)(2,1)S(1)}, u32[]{:S(2)}, u32[]{:S(2)}) collective-permute-start(bf16[2,2,24,768]{3,2,0,1:T(8,128)(2,1)S(1)} %fusion.94), channel_id=1, source_target_pairs={{0,4},{1,5},{2,6},{3,7},{4,0},{5,1},{6,2},{7,3},{8,12},{9,13},{10,... | collective-permute-start | bytes 442376 | tf_op jit(solution)/shard_map/ppermute | solution.py:307
  460.0 4.8 collective-permute-start.29
  464.8 4.9 collective-permute-start.30
  471.0 6.8 %collective-permute-start.32 = (bf16[2,2,2,24,768]{4,3,0,2,1:T(8,128)(2,1)S(1)}, bf16[2,2,2,24,768]{4,3,0,2,1:T(8,128)(2,1)S(1)}, u32[]{:S(2)}, u32[]{:S(2)}) collective-permute-start(bf16[2,2,2,24,768]{4,3,0,2,1:T(8,128)(2,1)S(1)} %fusion.78), channel_id=1, source_target_pairs={{0,4},{1,5},{2,6},{3,7},{4,0},{5,1},{6,2},{7,3},{8,12},{9,13},{10,... | collective-permute-start | bytes 884744 | tf_op jit(solution)/shard_map/ppermute | solution.py:307
  473.8 6.8 %collective-permute-start.37 = (bf16[2,2,2,24,768]{4,3,0,1,2:T(8,128)(2,1)S(1)}, bf16[2,2,2,24,768]{4,3,0,1,2:T(8,128)(2,1)S(1)}, u32[]{:S(2)}, u32[]{:S(2)}) collective-permute-start(bf16[2,2,2,24,768]{4,3,0,1,2:T(8,128)(2,1)S(1)} %fusion.79), channel_id=1, source_target_pairs={{0,8},{1,9},{2,10},{3,11},{4,12},{5,13},{6,14},{7,15},{8,0},{9,1},... | collective-permute-start | bytes 884744 | tf_op jit(solution)/shard_map/ppermute | solution.py:307
  477.9 17.4 %copy-start.27 = (f32[2,24,2304]{2,1,0:T(8,128)S(1)}, f32[2,24,2304]{2,1,0:T(8,128)}, u32[]{:S(2)}) copy-start(f32[2,24,2304]{2,1,0:T(8,128)} %param.22) | copy-start | bytes 1327108
  477.9 17.4 %copy-start.48 = (f32[24,2304]{1,0:T(8,128)S(1)}, f32[24,2304]{1,0:T(8,128)}, u32[]{:S(2)}) copy-start(f32[24,2304]{1,0:T(8,128)} %param.16) | copy-start | bytes 663556
  477.9 5.6 %collective-permute-start.33 = (bf16[2,2,24,768]{3,2,0,1:T(8,128)(2,1)S(1)}, bf16[2,2,24,768]{3,2,0,1:T(8,128)(2,1)S(1)}, u32[]{:S(2)}, u32[]{:S(2)}) collective-permute-start(bf16[2,2,24,768]{3,2,0,1:T(8,128)(2,1)S(1)} %fusion.95), channel_id=1, source_target_pairs={{0,8},{1,9},{2,10},{3,11},{4,12},{5,13},{6,14},{7,15},{8,0},{9,1},... | collective-permute-start | bytes 442376 | tf_op jit(solution)/shard_map/ppermute | solution.py:307
  480.7 5.2 %collective-permute-start.38 = (bf16[2,2,24,768]{3,2,0,1:T(8,128)(2,1)S(1)}, bf16[2,2,24,768]{3,2,0,1:T(8,128)(2,1)S(1)}, u32[]{:S(2)}, u32[]{:S(2)}) collective-permute-start(bf16[2,2,24,768]{3,2,0,1:T(8,128)(2,1)S(1)} %fusion.96), channel_id=1, source_target_pairs={{0,1},{1,0},{2,3},{3,2},{4,5},{5,4},{6,7},{7,6},{8,9},{9,8},{10,11... | collective-permute-start | bytes 442376 | tf_op jit(solution)/shard_map/ppermute | solution.py:307
  483.6 4.4 collective-permute-start.34
  485.9 4.4 collective-permute-start.39
  488.1 4.9 collective-permute-start.35
  490.4 4.9 collective-permute-start.40
  (73 other events, 380.3 us)
Sparse Core Ops, SparseCore 0:
  11.6 98.4 all-gather.1

commit v12 on v11

--- a/solution.py
+++ b/solution.py
@@ -284,7 +284,47 @@
     return bit_count, core_bit, rotated, late
 
 
-def tree_reduce_scatter(terms, orders, plan_bits, hooks=None):
+def tree_reduce_scatter(terms, part_columns, orders, plan_bits, hooks=None):
+    hooks = dict(hooks or {})
+    tied = {}
+    bit_count, core_bit = plan_bits
+    device = lax.axis_index("clip") * lax.axis_size("frame") + lax.axis_index("frame")
+    blocks = 1 << bit_count
+    block_rows = terms.shape[0] // blocks
+    data = terms.reshape((2,) * bit_count + (block_rows, terms.shape[1]))
+    parts = [(data, list(range(bit_count - 1, -1, -1)))]
+    plan = [(core_bit,)] + [tuple(order[stage] for order in orders) for stage in range(len(orders[0]))]
+    for stage, stage_bits in enumerate(plan):
+        if stage == 1:
+            whole, bits = parts[0]
+            parts = []
+            offset = 0
+            for width in part_columns:
+                parts.append((whole[..., offset : offset + width], bits))
+                offset += width
+        keeps, sends = [], []
+        for (part, part_bits), bit in zip(parts, stage_bits):
+            axis = part_bits.index(bit)
+            mine = (device >> bit) & 1
+            keeps.append(lax.dynamic_index_in_dim(part, mine, axis=axis, keepdims=False))
+            sends.append(
+                lax.dynamic_index_in_dim(part, 1 - mine, axis=axis, keepdims=False).astype(jnp.bfloat16)
+            )
+        new_parts = []
+        for keep, send, (part, part_bits), bit in zip(keeps, sends, parts, stage_bits):
+            pairs = [(index, index ^ (1 << bit)) for index in range(blocks)]
+            got = lax.ppermute(send, ("clip", "frame"), pairs)
+            new_parts.append((keep + got.astype(jnp.float32), [b for b in part_bits if b != bit]))
+        if stage in hooks:
+            values, tied[stage] = lax.optimization_barrier(
+                ([part for part, _ in new_parts], hooks[stage](tied))
+            )
+            new_parts = [(value, part_bits) for value, (_, part_bits) in zip(values, new_parts)]
+        parts = new_parts
+    return jnp.concatenate([part for part, _ in parts], axis=-1).astype(jnp.float32), tied
+
+
+def tree_reduce_scatter_parts(terms, orders, plan_bits, hooks=None):
     hooks = dict(hooks or {})
     tied = {}
     bit_count, core_bit = plan_bits
@@ -467,7 +507,9 @@
         mixed_low.T, grad_attended, preferred_element_type=jnp.float32
     ).astype(jnp.bfloat16)
     grad_out_bias = jnp.sum(grad_attended.astype(jnp.float32), axis=0)
-    late_terms = [grad_shrink_term.reshape(model_width, -1), grad_expand_term, grad_out_term]
+    late_terms = jnp.concatenate(
+        [grad_shrink_term.reshape(model_width, -1), grad_expand_term, grad_out_term], axis=1
+    )
     grad_mixed = jnp.dot(grad_attended, full_out.T, preferred_element_type=jnp.float32).astype(
         jnp.bfloat16
     )
@@ -486,7 +528,7 @@
     hooks.update({index: piece_hook(index) for index in range(1, piece_count)})
     pieces = [run_piece(0, grad_mixed)]
     owned_late, tied = tree_reduce_scatter(
-        late_terms, [late_orders[index % len(late_orders)] for index in range(3)], (bit_count, core_bit), hooks
+        late_terms, (3456, 3456), late_orders, (bit_count, core_bit), hooks
     )
     pieces += [tied[index][0] for index in range(1, piece_count)]
     finished = []
@@ -544,7 +586,7 @@
         ],
         axis=1,
     )
-    owned_first = tree_reduce_scatter(
+    owned_first = tree_reduce_scatter_parts(
         grad_in_terms + [small_grads],
         [rotated_orders[index % len(rotated_orders)] for index in range(4)],
         (bit_count, core_bit),
@@ -552,9 +594,9 @@
     owned_in = jnp.concatenate(owned_first[:3], axis=1)
     owned_vectors = owned_first[3][:, : vectors.shape[1]]
     owned_bias = owned_first[3][:, vectors.shape[1] : 12].reshape(-1)
-    owned_shrink = owned_late[0].reshape(shrink_weight.shape)
-    owned_expand = owned_late[1]
-    owned_out = owned_late[2]
+    owned_shrink = owned_late[:, :ff_width].reshape(shrink_weight.shape)
+    owned_expand = owned_late[:, ff_width : 2 * ff_width]
+    owned_out = owned_late[:, 2 * ff_width :]
     new_in, mom_in = adam_step(project_in, moments_in, owned_in)
     new_out, mom_out = adam_step(project_out, moments_out, owned_out)
     new_expand, mom_expand = adam_step(expand_weight, moments_expand, owned_expand)

time: 509 us -> 513 us (level)
  waiting for transfers between devices: 132 us -> 93.2 us
  local copies, waits for them, and re-layouts: 83.3 us -> 112 us
  other arithmetic: 55.1 us -> 69.6 us
  starting transfers between devices: 48.1 us -> 42.6 us
    ppermute x35 -> x29, waiting for transfers between devices: 87.9 us -> 51.1 us  [the longest x20 30.3 us: tree_reduce_scatter_parts(): got = lax.ppermute(send.astype(jnp.bfloat16), ('clip', 'frame'), pairs)]
    unnamed x173 -> x168, local copies, waits for them, and re-layouts: 16.4 us -> 26.2 us
    concatenate x0 -> x1, local copies, waits for them, and re-layouts: none -> 8.51 us  [body(): jnp.concatenate([grad_shrink_term.reshape(model_width, -1), grad_expand_t...]
    another operation x2 -> x1, local copies, waits for them, and re-layouts: 8.54 us -> 0.09 us  [the longest x1 8.46 us: tree_reduce_scatter(): parts.append((term.reshape(shape), list(range(bit_count - 1, -1, -1))))]
    concatenate x0 -> x1, other arithmetic: none -> 7.94 us  [body(): jnp.concatenate([grad_shrink_term.reshape(model_width, -1), grad_expand_t...]
    ppermute x35 -> x29, starting transfers between devices: 24.3 us -> 17.2 us  [the longest x20 12.3 us: tree_reduce_scatter_parts(): got = lax.ppermute(send.astype(jnp.bfloat16), ('clip', 'frame'), pairs)]
    convert_element_type x29 -> x25, local copies, waits for them, and re-layouts: 6.48 us -> 11.7 us  [the longest x8 9.55 us: tree_reduce_scatter(): lax.dynamic_index_in_dim(part, 1 - mine, axis=axis, keepdims=False)]
    dynamic_slice x10 -> x7, local copies, waits for them, and re-layouts: 9.28 us -> 14.1 us  [the longest x1 8.68 us: tree_reduce_scatter(): lax.dynamic_index_in_dim(part, mine, axis=axis, keepdims=False)]
  transfers between devices with their start and end apart: 53 -> 47, of which waited for: 26 -> 25; matrix products, arithmetic and copies ran while one was open for 29% -> 29% of each run, Pallas kernels for 14% -> 18%
where the time goes in v12:
time: 513 us; the launch traced here: 507 us
  local copies, waits for them, and re-layouts  112 us (22%)
  waiting for transfers between devices  93.2 us (18%)
  Pallas kernels  92.6 us (18%)
  matrix products  81.3 us (16%)
  other arithmetic  69.6 us (14%)
  starting transfers between devices  42.6 us (8%)
  between operations  15.7 us (3%)
    pallas_call x3, Pallas kernels, attention_pallas(): pl.pallas_call(attention_backward_kernel, grid=(span,), in_specs=[qi_spec...  58.1 us
    ppermute x13, waiting for transfers between devices, double(): got = lax.ppermute(data, ('clip', 'frame'), pairs)  42.1 us
    pallas_call x1, Pallas kernels, attention_pallas(): pl.pallas_call(attention_forward_kernel, grid=(pair_count,), in_specs=[q_...  34.5 us
    ppermute x20, waiting for transfers between devices, tree_reduce_scatter_parts(): got = lax.ppermute(send.astype(jnp.bfloat16), ('clip', 'frame'), pairs)  30.3 us
    unnamed x168, local copies, waits for them, and re-layouts  26.2 us
    ppermute x9, waiting for transfers between devices, tree_reduce_scatter(): got = lax.ppermute(send, ('clip', 'frame'), pairs)  20.8 us
    ppermute x13, starting transfers between devices, double(): got = lax.ppermute(data, ('clip', 'frame'), pairs)  19.5 us
    concatenate x10, local copies, waits for them, and re-layouts, body(): jnp.concatenate([grad_columns, grad_bias_term.reshape(model_width, -1), j...  16.9 us
  transfers between devices with their start and end apart: 47, of which 25 were waited for; matrix products, arithmetic and copies ran while one was open for 29% of the time, Pallas kernels for 18%

profile of v12, /device:TPU:0, one launch (start us, length us, event | category | flops | bytes accessed | tf_op | source)
XLA Modules:
  0.0 506.6 jit_solution(12610756973372514302)
XLA Ops:
  12.8 4.1 collective-permute-start.8
  17.0 3.0 collective-permute-start
  25.5 29.5 %collective-permute-done.5 = bf16[2,24,768]{2,1,0:T(8,128)(2,1)S(1)} collective-permute-done((bf16[2,24,768]{2,1,0:T(8,128)(2,1)S(1)}, bf16[2,24,768]{2,1,0:T(8,128)(2,1)S(1)}, u32[]{:S(2)}, u32[]{:S(2)}) %collective-permute-start.5) | collective-permute-done | bytes 73760 | tf_op jit(solution)/shard_map/ppermute | solution.py:368
  60.1 1.8 collective-permute-done.10
  62.4 3.4 collective-permute-done.6
  69.4 3.2 collective-permute-done.7
  72.8 4.0 collective-permute-done.3
  80.8 1.8 fusion.35
  82.6 3.0 maximum_select_fusion
  85.7 1.8 copy-done.21
  88.5 1.8 slice_reduce_fusion
  90.4 5.5 %add_convert_fusion = bf16[750,2304]{1,0:T(8,128)(2,1)S(1)} fusion(bf16[768,2432]{1,0:T(8,128)(2,1)} %bitcast.369, f32[2304]{0:T(1024)S(1)} %pad_maximum_fusion.19, bf16[1,750,768]{2,1,0:T(8,128)(2,1)S(1)} %copy-done.5, f32[768]{0:T(1024)S(1)} %get-tuple-element.142, f32[768]{0:T(1024)S(1)} %get-tuple-element.143, f32[750]{0:T(1024)S(1)} %add_rsqrt_fusion.2, ...), kind=kOutput, calls=%fused_computation.15 | convolution fusion | flops 2661120000 | bytes 8168304 | tf_op jit(solution)/shard_map/dot_general | solution.py:460
  99.2 3.5 add_convert_fusion.1
  102.7 2.7 fusion.8.k_ref.v_ref
  105.5 34.5 %shard_map.293 = (bf16[768,768]{1,0:T(8,128)(2,1)S(1)}, f32[768,768]{1,0:T(8,128)S(1)}) custom-call(bf16[768,768]{1,0:T(8,128)(2,1)S(1)} %pad.24.q_ref, bf16[1536,1536]{1,0:T(8,128)(2,1)} %fusion.8.k_ref.v_ref, bf16[1536,1536]{1,0:T(8,128)(2,1)} %fusion.8.k_ref.v_ref, f32[1,1536]{1,0:T(1,128)S(1)} %compare_select_fusion.kbias_ref), custom_call_target="tpu_custom_call" | custom-call | tf_op jit(solution)/shard_map/pallas_call | solution.py:157
  141.4 2.5 fusion.138
  145.7 4.8 slice.304
  150.4 8.5 %reshape.1305 = bf16[3072,768]{1,0:T(8,128)(2,1)} reshape(bf16[768,3072]{1,0:T(8,128)(2,1)} %slice.304) | data formatting | bytes 9437184 | tf_op jit(solution)/shard_map/reshape | solution.py:445
  158.9 9.0 %multiply_convert_fusion = (bf16[750,3072]{1,0:T(8,128)(2,1)S(1)}, f32[750,3072]{1,0:T(8,128)}) fusion(f32[3072]{0:T(1024)S(1)} %copy-done.63, bf16[768,6912]{1,0:T(8,128)(2,1)} %all-gather.2.cloned.1.call-done, f32[750,768]{1,0:T(8,128)} %copy-done.10, f32[768]{0:T(1024)S(1)} %copy-done.69, f32[768]{0:T(1024)S(1)} %get-tuple-element.138, ...), kind=kOutput, calls=%fused_computation.13 | convolution fusion | flops 3555648000 | bytes 20877168 | tf_op jit(solution)/shard_map/dot_general | solution.py:480
  167.9 2.2 copy-done.73
  170.1 5.8 %convolution_convert_fusion.1 = bf16[3072,768]{1,0:T(8,128)(2,1)} fusion(bf16[750,3072]{1,0:T(8,128)(2,1)S(1)} %get-tuple-element.206, bf16[1,750,768]{2,1,0:T(8,128)(2,1)S(1)} %copy-done.45), kind=kOutput, calls=%fused_computation.19 | convolution fusion | flops 3541303296 | bytes 10478592 | tf_op jit(solution)/shard_map/dot_general | solution.py:490
  175.9 8.5 %concatenate.346 = bf16[2,2,2,2,2,24,3072]{6,5,4,3,2,1,0:T(8,128)(2,1)} reshape(bf16[3072,768]{1,0:T(8,128)(2,1)} %convolution_convert_fusion.1) | data formatting | bytes 9437184 | tf_op jit(solution)/shard_map/concatenate | solution.py:510
  184.4 10.0 %convert_reduce_fusion = (f32[3072]{0:T(1024)}, bf16[750,3072]{1,0:T(8,128)(2,1)S(1)}) fusion(f32[750,3072]{1,0:T(8,128)} %get-tuple-element.207, f32[3072]{0:T(1024)S(1)} %copy-done.63, bf16[3072,768]{1,0:T(8,128)(2,1)} %reshape.1305, bf16[1,750,768]{2,1,0:T(8,128)(2,1)S(1)} %copy-done.45), kind=kOutput, calls=%fused_computation.12 | convolution fusion | flops 3568892928 | bytes 19719168 | tf_op jit(solution)/shard_map/dot_general | solution.py:494
  194.4 5.4 %convolution_convert_fusion = bf16[768,3072]{1,0:T(8,128)(2,1)S(1)} fusion(bf16[750,3072]{1,0:T(8,128)(2,1)S(1)} %get-tuple-element.210, f32[750,768]{1,0:T(8,128)S(1)} %copy-done.11, f32[768]{0:T(1024)S(1)} %copy-done.69, f32[768]{0:T(1024)S(1)} %get-tuple-element.138, f32[750]{0:T(1024)S(1)} %add_rsqrt_fusion, f32[750]{0:T(1024)S(1)} %broadcast_multiply_fusion.4), kind=kOutput, calls=%fused_computation.18 | convolution fusion | flops 3544183296 | bytes 11642736 | tf_op jit(solution)/shard_map/dot_general | solution.py:496
  199.8 7.3 %multiply_reduce_fusion = (f32[768]{0:T(1024)}, f32[750]{0:T(1024)S(1)}, f32[750]{0:T(1024)S(1)}, f32[768]{0:T(1024)}, f32[750,768]{1,0:T(8,128)S(1)}) fusion(f32[750,768]{1,0:T(8,128)S(1)} %copy-done.11, f32[750]{0:T(1024)S(1)} %add_rsqrt_fusion, f32[750]{0:T(1024)S(1)} %broadcast_multiply_fusion.4, f32[768]{0:T(1024)S(1)} %get-tuple-element.138, ...), kind=kOutput, calls=%fused_computation.67 | convolution fusion | flops 3544124928 | bytes 13955808 | tf_op jit(solution)/shard_map/dot_general | solution.py:500
  207.2 1.8 convert_reduce_fusion.4
  210.4 7.9 %pad_maximum_fusion = bf16[2,2,2,2,2,24,6912]{6,5,4,3,2,1,0:T(8,128)(2,1)} fusion(bf16[2,2,2,2,2,24,768]{6,5,4,3,2,1,0:T(8,128)(2,1)S(1)} %bitcast.378, bf16[2,2,2,2,2,24,3072]{6,5,4,3,2,1,0:T(8,128)(2,1)S(1)} %bitcast.367, bf16[2,2,2,2,2,24,3072]{6,5,4,3,2,1,0:T(8,128)(2,1)S(1)} %bitcast.362), kind=kLoop, calls=%fused_computation.1 | loop fusion | flops 31850496 | bytes 21233664 | tf_op jit(solution)/shard_map/concatenate | solution.py:510
  218.3 8.7 %constant_dynamic-slice_fusion.9 = (bf16[2,2,2,1,2,24,6912]{6,5,4,3,2,1,0:T(8,128)(2,1)}, bf16[2,2,2,1,2,24,6912]{6,5,4,3,2,1,0:T(8,128)(2,1)}) fusion(bf16[2,2,2,2,2,24,6912]{6,5,4,3,2,1,0:T(8,128)(2,1)} %pad_maximum_fusion, s32[]{:T(128)S(6)} %select_n.410, s32[]{:T(128)S(6)} %select_n.411), kind=kLoop, calls=%fused_computation.287 | loop fusion | bytes 21233672 | tf_op jit(solution)/shard_map/jit(dynamic_index_in_dim)/dynamic_slice | solution.py:309
  227.0 5.3 %copy.205 = bf16[2,2,2,1,2,24,6912]{6,5,0,4,2,1,3:T(8,128)(2,1)} copy(bf16[2,2,2,1,2,24,6912]{6,5,4,3,2,1,0:T(8,128)(2,1)} %get-tuple-element.157) | data formatting | bytes 10616832
  233.2 2.4 convolution_convert_fusion.6
  235.7 19.3 %shard_map.294 = (f32[768,256]{1,0:T(8,128)S(1)}, f32[1536,256]{1,0:T(8,128)S(1)}, f32[1536,256]{1,0:T(8,128)}) custom-call(bf16[768,768]{1,0:T(8,128)(2,1)S(1)} %pad.24.q_ref, bf16[1536,1536]{1,0:T(8,128)(2,1)} %fusion.8.k_ref.v_ref, bf16[1536,1536]{1,0:T(8,128)(2,1)} %fusion.8.k_ref.v_ref, bf16[768,768]{1,0:T(8,128)(2,1)S(1)} %pad.26.do_ref, ...), custom_call_target="tpu_custom_call" | custom-call | tf_op jit(solution)/shard_map/pallas_call | solution.py:176
  257.7 2.2 collective-permute-start.19
  260.0 5.3 %convert_add_fusion = f32[2,2,2,2,24,6912]{5,4,0,3,2,1:T(8,128)S(1)} fusion(bf16[2,2,2,2,24,6912]{5,4,0,3,2,1:T(8,128)(2,1)} %collective-permute-done.14, bf16[2,2,2,1,2,24,6912]{6,5,4,3,2,1,0:T(8,128)(2,1)} %get-tuple-element.156), kind=kLoop, calls=%fused_computation.2 | loop fusion | flops 7962624 | bytes 21233664 | tf_op jit(solution)/shard_map/add | solution.py:317
  265.3 4.9 fusion.133
  270.2 3.1 fusion.47
  273.3 8.5 %fusion.46 = bf16[1,750,768]{2,1,0:T(8,128)(2,1)} fusion(f32[750,768]{1,0:T(8,128)S(1)} %copy-done.12, bf16[750,3072]{1,0:T(8,128)(2,1)} %copy-done.73, bf16[3072,768]{1,0:T(8,128)(2,1)} %reshape.1305, f32[768]{0:T(1024)S(1)} %copy-done.68), kind=kOutput, calls=%fused_computation.96 | convolution fusion | flops 3540672000 | bytes 12785664 | tf_op jit(solution)/shard_map/dot_general | solution.py:484
  281.8 1.9 concatenate.366
  291.4 2.9 fusion.48
  296.8 19.3 %shard_map.295 = (f32[768,256]{1,0:T(8,128)S(1)}, f32[1536,256]{1,0:T(8,128)S(1)}, f32[1536,256]{1,0:T(8,128)}) custom-call(bf16[768,768]{1,0:T(8,128)(2,1)S(1)} %pad.24.q_ref, bf16[1536,1536]{1,0:T(8,128)(2,1)} %fusion.8.k_ref.v_ref, bf16[1536,1536]{1,0:T(8,128)(2,1)} %fusion.8.k_ref.v_ref, bf16[768,768]{1,0:T(8,128)(2,1)S(1)} %pad.27.do_ref, ...), custom_call_target="tpu_custom_call" | custom-call | tf_op jit(solution)/shard_map/pallas_call | solution.py:176
  320.9 4.5 collective-permute-done.16
  331.0 19.5 %shard_map.296 = (f32[768,256]{1,0:T(8,128)S(1)}, f32[1536,256]{1,0:T(8,128)S(1)}, f32[1536,256]{1,0:T(8,128)}) custom-call(bf16[768,768]{1,0:T(8,128)(2,1)S(1)} %pad.24.q_ref, bf16[1536,1536]{1,0:T(8,128)(2,1)} %fusion.8.k_ref.v_ref, bf16[1536,1536]{1,0:T(8,128)(2,1)} %fusion.8.k_ref.v_ref, bf16[768,768]{1,0:T(8,128)(2,1)S(1)} %pad.28.do_ref, ...), custom_call_target="tpu_custom_call" | custom-call | tf_op jit(solution)/shard_map/pallas_call | solution.py:176
  366.8 2.7 convolution_convert_fusion.4
  375.8 3.7 fusion.52
  382.0 2.4 collective-permute-done.39
  385.6 5.9 %collective-permute-done.37 = bf16[2,24,3456]{2,1,0:T(8,128)(2,1)} collective-permute-done((bf16[2,24,3456]{2,1,0:T(8,128)(2,1)}, bf16[2,24,3456]{2,1,0:T(8,128)(2,1)}, u32[]{:S(2)}, u32[]{:S(2)}) %collective-permute-start.37) | collective-permute-done | bytes 331808 | tf_op jit(solution)/shard_map/ppermute | solution.py:316
  392.7 3.7 collective-permute-done.40
  396.5 4.2 collective-permute-done.38
  404.6 2.0 fusion.82
  406.7 2.1 fusion.103
  415.4 2.5 convolution_convert_fusion.3
  417.8 3.8 fusion.50
  421.9 2.5 convolution_convert_fusion.2
  427.8 5.1 fusion.30
  436.3 4.1 concatenate.367
  448.6 1.8 fusion.55
  453.3 2.6 collective-permute-done.44
  456.4 4.1 collective-permute-done.45
  463.8 4.1 collective-permute-done.25
  470.6 2.2 collective-permute-done.26
  476.1 4.9 collective-permute-done.28
  484.2 2.5 collective-permute-done.29
  488.0 1.7 collective-permute-start.35
  492.4 1.9 collective-permute-start.36
  494.3 1.8 collective-permute-done.31
  (423 shorter events, 133.2 us)
Async XLA Ops:
  7.2 12.8 %copy-start.5 = (bf16[1,750,768]{2,1,0:T(8,128)(2,1)S(1)}, bf16[1,750,768]{2,1,0:T(8,128)(2,1)}, u32[]{:S(2)}) copy-start(bf16[1,750,768]{2,1,0:T(8,128)(2,1)} %param.14) | copy-start | bytes 3456004
  7.2 134.2 %all-gather.2.cloned.1.call-start = ((), (), s32[]{:S(2)}) async-start(), calls=%async_computation | async-start | bytes 10948608 | tf_op jit(solution)/shard_map/all_gather | solution.py:438
  12.8 8.7 %collective-permute-start.8 = (bf16[24,768]{1,0:T(8,128)(2,1)S(1)}, bf16[24,768]{1,0:T(8,128)(2,1)S(1)}, u32[]{:S(2)}, u32[]{:S(2)}) collective-permute-start(bf16[24,768]{1,0:T(8,128)(2,1)S(1)} %get-tuple-element.188), channel_id=1, source_target_pairs={{0,16},{1,17},{2,18},{3,19},{4,20},{5,21},{6,22},{7,23},{8,24},{9,... | collective-permute-start | bytes 110600 | tf_op jit(solution)/shard_map/ppermute | solution.py:368
  16.9 6.2 %collective-permute-start.4 = (bf16[24,768]{1,0:T(8,128)(2,1)S(1)}, bf16[24,768]{1,0:T(8,128)(2,1)S(1)}, u32[]{:S(2)}, u32[]{:S(2)}) collective-permute-start(bf16[24,768]{1,0:T(8,128)(2,1)S(1)} %get-tuple-element.194), channel_id=1, source_target_pairs={{0,16},{1,17},{2,18},{3,19},{4,20},{5,21},{6,22},{7,23},{8,24},{9,... | collective-permute-start | bytes 110600 | tf_op jit(solution)/shard_map/ppermute | solution.py:368
  17.0 6.9 %collective-permute-start = (bf16[24,896]{1,0:T(8,128)(2,1)S(1)}, bf16[24,896]{1,0:T(8,128)(2,1)S(1)}, u32[]{:S(2)}, u32[]{:S(2)}) collective-permute-start(bf16[24,896]{1,0:T(8,128)(2,1)S(1)} %get-tuple-element.191), channel_id=1, source_target_pairs={{0,16},{1,17},{2,18},{3,19},{4,20},{5,21},{6,22},{7,23},{8,24},{9,... | collective-permute-start | bytes 129032 | tf_op jit(solution)/shard_map/ppermute | solution.py:368
  20.0 59.3 %collective-permute-start.13 = (bf16[1,750,768]{2,1,0:T(8,128)(2,1)S(1)}, bf16[1,750,768]{2,1,0:T(8,128)(2,1)}, u32[]{:S(2)}, u32[]{:S(2)}) collective-permute-start(bf16[1,750,768]{2,1,0:T(8,128)(2,1)S(1)} %copy-done.5), channel_id=1, source_target_pairs={{0,1},{1,0},{2,3},{3,2},{4,5},{5,4},{6,7},{7,6},{8,9},{9,8},{10,11... | collective-permute-start | bytes 3456008 | tf_op jit(solution)/shard_map/ppermute | solution.py:452
  21.6 35.1 %collective-permute-start.9 = (bf16[2,24,768]{2,1,0:T(8,128)(2,1)S(1)}, bf16[2,24,768]{2,1,0:T(8,128)(2,1)S(1)}, u32[]{:S(2)}, u32[]{:S(2)}) collective-permute-start(bf16[2,24,768]{2,1,0:T(8,128)(2,1)S(1)} %maximum_select_fusion.18), channel_id=1, source_target_pairs={{0,4},{1,5},{2,6},{3,7},{4,0},{5,1},{6,2},{7,3},{8,12},{9,13},{10,... | collective-permute-start | bytes 221192 | tf_op jit(solution)/shard_map/ppermute | solution.py:368
  23.2 31.8 %collective-permute-start.5 = (bf16[2,24,768]{2,1,0:T(8,128)(2,1)S(1)}, bf16[2,24,768]{2,1,0:T(8,128)(2,1)S(1)}, u32[]{:S(2)}, u32[]{:S(2)}) collective-permute-start(bf16[2,24,768]{2,1,0:T(8,128)(2,1)S(1)} %maximum_select_fusion.17), channel_id=1, source_target_pairs={{0,1},{1,0},{2,3},{3,2},{4,5},{5,4},{6,7},{7,6},{8,9},{9,8},{10,11... | collective-permute-start | bytes 221192 | tf_op jit(solution)/shard_map/ppermute | solution.py:368
  23.9 34.4 %collective-permute-start.1 = (bf16[2,24,896]{2,1,0:T(8,128)(2,1)S(1)}, bf16[2,24,896]{2,1,0:T(8,128)(2,1)S(1)}, u32[]{:S(2)}, u32[]{:S(2)}) collective-permute-start(bf16[2,24,896]{2,1,0:T(8,128)(2,1)S(1)} %maximum_select_fusion.15), channel_id=1, source_target_pairs={{0,8},{1,9},{2,10},{3,11},{4,12},{5,13},{6,14},{7,15},{8,0},{9,1},... | collective-permute-start | bytes 258056 | tf_op jit(solution)/shard_map/ppermute | solution.py:368
  55.0 10.8 %collective-permute-start.6 = (bf16[2,2,24,768]{3,2,0,1:T(8,128)(2,1)S(1)}, bf16[2,2,24,768]{3,2,0,1:T(8,128)(2,1)S(1)}, u32[]{:S(2)}, u32[]{:S(2)}) collective-permute-start(bf16[2,2,24,768]{3,2,0,1:T(8,128)(2,1)S(1)} %maximum_select_fusion.12), channel_id=1, source_target_pairs={{0,8},{1,9},{2,10},{3,11},{4,12},{5,13},{6,14},{7,15},{8,0},{9,1},... | collective-permute-start | bytes 442376 | tf_op jit(solution)/shard_map/ppermute | solution.py:368
  56.7 5.2 %collective-permute-start.10 = (bf16[2,2,24,768]{3,2,1,0:T(8,128)(2,1)S(1)}, bf16[2,2,24,768]{3,2,1,0:T(8,128)(2,1)S(1)}, u32[]{:S(2)}, u32[]{:S(2)}) collective-permute-start(bf16[2,2,24,768]{3,2,1,0:T(8,128)(2,1)S(1)} %maximum_select_fusion.13), channel_id=1, source_target_pairs={{0,1},{1,0},{2,3},{3,2},{4,5},{5,4},{6,7},{7,6},{8,9},{9,8},{10,11... | collective-permute-start | bytes 442376 | tf_op jit(solution)/shard_map/ppermute | solution.py:368
  58.5 9.1 %collective-permute-start.2 = (bf16[2,2,24,896]{3,2,0,1:T(8,128)(2,1)S(1)}, bf16[2,2,24,896]{3,2,0,1:T(8,128)(2,1)S(1)}, u32[]{:S(2)}, u32[]{:S(2)}) collective-permute-start(bf16[2,2,24,896]{3,2,0,1:T(8,128)(2,1)S(1)} %maximum_select_fusion.10), channel_id=1, source_target_pairs={{0,4},{1,5},{2,6},{3,7},{4,0},{5,1},{6,2},{7,3},{8,12},{9,13},{10,... | collective-permute-start | bytes 516104 | tf_op jit(solution)/shard_map/ppermute | solution.py:368
  61.9 10.8 %collective-permute-start.11 = (bf16[2,2,2,24,768]{4,3,2,1,0:T(8,128)(2,1)S(1)}, bf16[2,2,2,24,768]{4,3,2,1,0:T(8,128)(2,1)S(1)}, u32[]{:S(2)}, u32[]{:S(2)}) collective-permute-start(bf16[2,2,2,24,768]{4,3,2,1,0:T(8,128)(2,1)S(1)} %maximum_select_fusion.8), channel_id=1, source_target_pairs={{0,8},{1,9},{2,10},{3,11},{4,12},{5,13},{6,14},{7,15},{8,0},{9,1},... | collective-permute-start | bytes 884744 | tf_op jit(solution)/shard_map/ppermute | solution.py:368
  65.9 6.8 %collective-permute-start.7 = (bf16[2,2,2,24,768]{4,3,0,2,1:T(8,128)(2,1)S(1)}, bf16[2,2,2,24,768]{4,3,0,2,1:T(8,128)(2,1)S(1)}, u32[]{:S(2)}, u32[]{:S(2)}) collective-permute-start(bf16[2,2,2,24,768]{4,3,0,2,1:T(8,128)(2,1)S(1)} %maximum_select_fusion.7), channel_id=1, source_target_pairs={{0,4},{1,5},{2,6},{3,7},{4,0},{5,1},{6,2},{7,3},{8,12},{9,13},{10,... | collective-permute-start | bytes 884744 | tf_op jit(solution)/shard_map/ppermute | solution.py:368
  67.7 9.1 %collective-permute-start.3 = (bf16[2,2,2,24,896]{4,3,0,1,2:T(8,128)(2,1)S(1)}, bf16[2,2,2,24,896]{4,3,0,1,2:T(8,128)(2,1)S(1)}, u32[]{:S(2)}, u32[]{:S(2)}) collective-permute-start(bf16[2,2,2,24,896]{4,3,0,1,2:T(8,128)(2,1)S(1)} %maximum_select_fusion.5), channel_id=1, source_target_pairs={{0,1},{1,0},{2,3},{3,2},{4,5},{5,4},{6,7},{7,6},{8,9},{9,8},{10,11... | collective-permute-start | bytes 1032200 | tf_op jit(solution)/shard_map/ppermute | solution.py:368
  78.5 4.2 collective-permute-start.12
  79.2 11.1 %copy-start.57 = (f32[750]{0:T(1024)}, f32[750]{0:T(1024)S(1)}, u32[]{:S(2)}) copy-start(f32[750]{0:T(1024)S(1)} %add_rsqrt_fusion.2) | copy-start | bytes 9004
  105.5 35.9 %copy-start.70 = (f32[768]{0:T(1024)S(1)}, f32[768]{0:T(1024)}, u32[]{:S(2)}) copy-start(f32[768]{0:T(1024)} %get-tuple-element.139) | copy-start | bytes 9220
  150.4 8.5 %copy-start.69 = (f32[768]{0:T(1024)S(1)}, f32[768]{0:T(1024)}, u32[]{:S(2)}) copy-start(f32[768]{0:T(1024)} %get-tuple-element.137) | copy-start | bytes 9220
  158.9 11.2 %copy-start.45 = (bf16[1,750,768]{2,1,0:T(8,128)(2,1)S(1)}, bf16[1,750,768]{2,1,0:T(8,128)(2,1)}, u32[]{:S(2)}) copy-start(bf16[1,750,768]{2,1,0:T(8,128)(2,1)} %param.15) | copy-start | bytes 3456004
  184.4 10.0 %copy-start.11 = (f32[750,768]{1,0:T(8,128)S(1)}, f32[750,768]{1,0:T(8,128)}, u32[]{:S(2)}) copy-start(f32[750,768]{1,0:T(8,128)} %copy-done.10) | copy-start | bytes 6912004
  232.3 27.7 %collective-permute-start.14 = (bf16[2,2,2,2,24,6912]{5,4,0,3,2,1:T(8,128)(2,1)}, bf16[2,2,2,2,24,6912]{5,4,0,3,2,1:T(8,128)(2,1)}, u32[]{:S(2)}, u32[]{:S(2)}) collective-permute-start(bf16[2,2,2,2,24,6912]{5,4,0,3,2,1:T(8,128)(2,1)} %bitcast.357), channel_id=1, source_target_pairs={{0,2},{1,3},{2,0},{3,1},{4,6},{5,7},{6,4},{7,5},{8,10},{9,11},{10,... | collective-permute-start | bytes 15925256 | tf_op jit(solution)/shard_map/ppermute | solution.py:316
  235.6 19.4 %copy-start.3 = (bf16[750,768]{1,0:T(8,128)(2,1)}, bf16[750,768]{1,0:T(8,128)(2,1)S(1)}, u32[]{:S(2)}) copy-start(bf16[750,768]{1,0:T(8,128)(2,1)S(1)} %convolution_convert_fusion.6) | copy-start | bytes 3456004
  257.7 36.6 %collective-permute-start.19 = (bf16[750,512]{1,0:T(8,128)(2,1)}, bf16[750,512]{1,0:T(8,128)(2,1)}, u32[]{:S(2)}, u32[]{:S(2)}) collective-permute-start(bf16[750,512]{1,0:T(8,128)(2,1)} %fusion.45), channel_id=1, source_target_pairs={{0,1},{1,0},{2,3},{3,2},{4,5},{5,4},{6,7},{7,6},{8,9},{9,8},{10,11... | collective-permute-start | bytes 2304008 | tf_op jit(solution)/shard_map/ppermute | solution.py:537
  273.3 46.1 %collective-permute-start.15 = (bf16[2,2,2,24,3456]{4,3,0,2,1:T(8,128)(2,1)}, bf16[2,2,2,24,3456]{4,3,0,2,1:T(8,128)(2,1)}, u32[]{:S(2)}, u32[]{:S(2)}) collective-permute-start(bf16[2,2,2,24,3456]{4,3,0,2,1:T(8,128)(2,1)} %fusion.47), channel_id=1, source_target_pairs={{0,4},{1,5},{2,6},{3,7},{4,0},{5,1},{6,2},{7,3},{8,12},{9,13},{10,... | collective-permute-start | bytes 3981320 | tf_op jit(solution)/shard_map/ppermute | solution.py:316
  294.4 31.1 %collective-permute-start.16 = (bf16[2,2,2,24,3456]{4,3,0,2,1:T(8,128)(2,1)}, bf16[2,2,2,24,3456]{4,3,0,2,1:T(8,128)(2,1)}, u32[]{:S(2)}, u32[]{:S(2)}) collective-permute-start(bf16[2,2,2,24,3456]{4,3,0,2,1:T(8,128)(2,1)} %fusion.48), channel_id=1, source_target_pairs={{0,8},{1,9},{2,10},{3,11},{4,12},{5,13},{6,14},{7,15},{8,0},{9,1},... | collective-permute-start | bytes 3981320 | tf_op jit(solution)/shard_map/ppermute | solution.py:316
  296.7 22.7 %slice-start.4 = ((s8[5308416]{0:T(1024)(128)(4,1)}), s8[4194304]{0:T(1024)(128)(4,1)S(1)}, s32[]{:S(2)}) async-start(s8[5308416]{0:T(1024)(128)(4,1)} %bitcast.365), calls=%async_computation.5 | async-start | bytes 8388608
  296.8 22.6 %slice-start.5 = ((s8[5308416]{0:T(1024)(128)(4,1)}), s8[1114112]{0:T(1024)(128)(4,1)S(1)}, s32[]{:S(2)}) async-start(s8[5308416]{0:T(1024)(128)(4,1)} %bitcast.365), calls=%async_computation.6 | async-start | bytes 2228224
  316.1 9.3 %slice-start.2 = ((s8[5308416]{0:T(1024)(128)(4,1)}), s8[4194304]{0:T(1024)(128)(4,1)S(1)}, s32[]{:S(2)}) async-start(s8[5308416]{0:T(1024)(128)(4,1)} %bitcast.363), calls=%async_computation.3 | async-start | bytes 8388608
  328.0 29.4 %collective-permute-start.18 = (bf16[2,2,24,3456]{3,2,0,1:T(8,128)(2,1)}, bf16[2,2,24,3456]{3,2,0,1:T(8,128)(2,1)}, u32[]{:S(2)}, u32[]{:S(2)}) collective-permute-start(bf16[2,2,24,3456]{3,2,0,1:T(8,128)(2,1)} %fusion.67), channel_id=1, source_target_pairs={{0,4},{1,5},{2,6},{3,7},{4,0},{5,1},{6,2},{7,3},{8,12},{9,13},{10,... | collective-permute-start | bytes 1990664 | tf_op jit(solution)/shard_map/ppermute | solution.py:316
  330.6 28.0 %collective-permute-start.17 = (bf16[2,2,24,3456]{3,2,0,1:T(8,128)(2,1)}, bf16[2,2,24,3456]{3,2,0,1:T(8,128)(2,1)}, u32[]{:S(2)}, u32[]{:S(2)}) collective-permute-start(bf16[2,2,24,3456]{3,2,0,1:T(8,128)(2,1)} %fusion.66), channel_id=1, source_target_pairs={{0,8},{1,9},{2,10},{3,11},{4,12},{5,13},{6,14},{7,15},{8,0},{9,1},... | collective-permute-start | bytes 1990664 | tf_op jit(solution)/shard_map/ppermute | solution.py:316
  356.9 22.6 %collective-permute-start.20 = (bf16[750,512]{1,0:T(8,128)(2,1)}, bf16[750,512]{1,0:T(8,128)(2,1)}, u32[]{:S(2)}, u32[]{:S(2)}) collective-permute-start(bf16[750,512]{1,0:T(8,128)(2,1)} %slice.435), channel_id=1, source_target_pairs={{0,1},{1,0},{2,3},{3,2},{4,5},{5,4},{6,7},{7,6},{8,9},{9,8},{10,11... | collective-permute-start | bytes 2304008 | tf_op jit(solution)/shard_map/ppermute | solution.py:537
  362.4 22.1 %collective-permute-start.39 = (bf16[2,24,3456]{2,1,0:T(8,128)(2,1)}, bf16[2,24,3456]{2,1,0:T(8,128)(2,1)}, u32[]{:S(2)}, u32[]{:S(2)}) collective-permute-start(bf16[2,24,3456]{2,1,0:T(8,128)(2,1)} %fusion.69), channel_id=1, source_target_pairs={{0,1},{1,0},{2,3},{3,2},{4,5},{5,4},{6,7},{7,6},{8,9},{9,8},{10,11... | collective-permute-start | bytes 995336 | tf_op jit(solution)/shard_map/ppermute | solution.py:316
  363.9 27.7 %collective-permute-start.37 = (bf16[2,24,3456]{2,1,0:T(8,128)(2,1)}, bf16[2,24,3456]{2,1,0:T(8,128)(2,1)}, u32[]{:S(2)}, u32[]{:S(2)}) collective-permute-start(bf16[2,24,3456]{2,1,0:T(8,128)(2,1)} %fusion.68), channel_id=1, source_target_pairs={{0,1},{1,0},{2,3},{3,2},{4,5},{5,4},{6,7},{7,6},{8,9},{9,8},{10,11... | collective-permute-start | bytes 995336 | tf_op jit(solution)/shard_map/ppermute | solution.py:316
  370.5 40.7 %collective-permute-start.22 = (bf16[2,2,2,2,24,768]{5,4,0,1,2,3:T(8,128)(2,1)}, bf16[2,2,2,2,24,768]{5,4,0,1,2,3:T(8,128)(2,1)}, u32[]{:S(2)}, u32[]{:S(2)}) collective-permute-start(bf16[2,2,2,2,24,768]{5,4,0,1,2,3:T(8,128)(2,1)} %bitcast.360), channel_id=1, source_target_pairs={{0,2},{1,3},{2,0},{3,1},{4,6},{5,7},{6,4},{7,5},{8,10},{9,11},{10,... | collective-permute-start | bytes 1769480 | tf_op jit(solution)/shard_map/ppermute | solution.py:347
  374.2 39.6 %collective-permute-start.21 = (bf16[750,512]{1,0:T(8,128)(2,1)}, bf16[750,512]{1,0:T(8,128)(2,1)}, u32[]{:S(2)}, u32[]{:S(2)}) collective-permute-start(bf16[750,512]{1,0:T(8,128)(2,1)} %slice.434), channel_id=1, source_target_pairs={{0,1},{1,0},{2,3},{3,2},{4,5},{5,4},{6,7},{7,6},{8,9},{9,8},{10,11... | collective-permute-start | bytes 2304008 | tf_op jit(solution)/shard_map/ppermute | solution.py:537
  381.1 10.5 %copy-start.24 = (f32[2,2,24,3456]{3,2,0,1:T(8,128)S(1)}, f32[2,2,24,3456]{3,2,0,1:T(8,128)}, u32[]{:S(2)}) copy-start(f32[2,2,24,3456]{3,2,0,1:T(8,128)} %copy-done.23) | copy-start | bytes 3981316
  385.5 15.3 %copy-start.41 = (f32[2,24,3072]{2,1,0:T(8,128)S(1)}, f32[2,24,3072]{2,1,0:T(8,128)}, u32[]{:S(2)}) copy-start(f32[2,24,3072]{2,1,0:T(8,128)} %param.24) | copy-start | bytes 1769476
  385.5 10.9 %collective-permute-start.40 = (bf16[24,3456]{1,0:T(8,128)(2,1)S(1)}, bf16[24,3456]{1,0:T(8,128)(2,1)S(1)}, u32[]{:S(2)}, u32[]{:S(2)}) collective-permute-start(bf16[24,3456]{1,0:T(8,128)(2,1)S(1)} %fusion.93), channel_id=1, source_target_pairs={{0,16},{1,17},{2,18},{3,19},{4,20},{5,21},{6,22},{7,23},{8,24},{9,... | collective-permute-start | bytes 497672 | tf_op jit(solution)/shard_map/ppermute | solution.py:316
  392.6 10.6 %copy-start.51 = (f32[2,24,768]{2,1,0:T(8,128)S(1)}, f32[2,24,768]{2,1,0:T(8,128)}, u32[]{:S(2)}) copy-start(f32[2,24,768]{2,1,0:T(8,128)} %param.23) | copy-start | bytes 442372
  392.6 8.1 %collective-permute-start.38 = (bf16[24,3456]{1,0:T(8,128)(2,1)S(1)}, bf16[24,3456]{1,0:T(8,128)(2,1)S(1)}, u32[]{:S(2)}, u32[]{:S(2)}) collective-permute-start(bf16[24,3456]{1,0:T(8,128)(2,1)S(1)} %fusion.92), channel_id=1, source_target_pairs={{0,16},{1,17},{2,18},{3,19},{4,20},{5,21},{6,22},{7,23},{8,24},{9,... | collective-permute-start | bytes 497672 | tf_op jit(solution)/shard_map/ppermute | solution.py:316
  413.2 39.1 %collective-permute-start.23 = (bf16[2,2,2,24,768]{4,3,0,1,2:T(8,128)(2,1)}, bf16[2,2,2,24,768]{4,3,0,1,2:T(8,128)(2,1)}, u32[]{:S(2)}, u32[]{:S(2)}) collective-permute-start(bf16[2,2,2,24,768]{4,3,0,1,2:T(8,128)(2,1)} %fusion.78), channel_id=1, source_target_pairs={{0,1},{1,0},{2,3},{3,2},{4,5},{5,4},{6,7},{7,6},{8,9},{9,8},{10,11... | collective-permute-start | bytes 884744 | tf_op jit(solution)/shard_map/ppermute | solution.py:347
  427.8 8.5 %copy-start.31 = (f32[2,2,2,2,2,24,4]{6,5,4,3,2,1,0:T(8,128)S(1)}, f32[2,2,2,2,2,24,4]{6,5,4,3,2,1,0:T(8,128)}, u32[]{:S(2)}) copy-start(f32[2,2,2,2,2,24,4]{6,5,4,3,2,1,0:T(8,128)} %concatenate.366) | copy-start | bytes 36868
  427.8 45.1 %collective-permute-start.27 = (bf16[2,2,2,2,24,768]{5,4,0,3,1,2:T(8,128)(2,1)}, bf16[2,2,2,2,24,768]{5,4,0,3,1,2:T(8,128)(2,1)}, u32[]{:S(2)}, u32[]{:S(2)}) collective-permute-start(bf16[2,2,2,2,24,768]{5,4,0,3,1,2:T(8,128)(2,1)} %bitcast.359), channel_id=1, source_target_pairs={{0,2},{1,3},{2,0},{3,1},{4,6},{5,7},{6,4},{7,5},{8,10},{9,11},{10,... | collective-permute-start | bytes 1769480 | tf_op jit(solution)/shard_map/ppermute | solution.py:347
  441.6 1.5 collective-permute-start.41
  444.0 4.2 collective-permute-start.42
  447.8 26.8 %collective-permute-start.32 = (bf16[2,2,2,2,24,768]{5,4,0,2,3,1:T(8,128)(2,1)}, bf16[2,2,2,2,24,768]{5,4,0,2,3,1:T(8,128)(2,1)}, u32[]{:S(2)}, u32[]{:S(2)}) collective-permute-start(bf16[2,2,2,2,24,768]{5,4,0,2,3,1:T(8,128)(2,1)} %bitcast.358), channel_id=1, source_target_pairs={{0,2},{1,3},{2,0},{3,1},{4,6},{5,7},{6,4},{7,5},{8,10},{9,11},{10,... | collective-permute-start | bytes 1769480 | tf_op jit(solution)/shard_map/ppermute | solution.py:347
  448.2 3.9 collective-permute-start.43
  452.2 3.8 collective-permute-start.44
  455.9 4.6 collective-permute-start.45
  456.1 7.0 %collective-permute-start.24 = (bf16[2,2,24,768]{3,2,0,1:T(8,128)(2,1)S(1)}, bf16[2,2,24,768]{3,2,0,1:T(8,128)(2,1)S(1)}, u32[]{:S(2)}, u32[]{:S(2)}) collective-permute-start(bf16[2,2,24,768]{3,2,0,1:T(8,128)(2,1)S(1)} %fusion.94), channel_id=1, source_target_pairs={{0,4},{1,5},{2,6},{3,7},{4,0},{5,1},{6,2},{7,3},{8,12},{9,13},{10,... | collective-permute-start | bytes 442376 | tf_op jit(solution)/shard_map/ppermute | solution.py:347
  460.7 13.4 %copy-start.71 = (f32[96]{0:T(128)}, f32[96]{0:T(128)S(1)}, u32[]{:S(2)}) copy-start(f32[96]{0:T(128)S(1)} %reshape.1313) | copy-start | bytes 1156
  463.1 4.8 collective-permute-start.25
  468.0 4.9 collective-permute-start.26
  474.2 6.8 %collective-permute-start.28 = (bf16[2,2,2,24,768]{4,3,0,2,1:T(8,128)(2,1)S(1)}, bf16[2,2,2,24,768]{4,3,0,2,1:T(8,128)(2,1)S(1)}, u32[]{:S(2)}, u32[]{:S(2)}) collective-permute-start(bf16[2,2,2,24,768]{4,3,0,2,1:T(8,128)(2,1)S(1)} %fusion.79), channel_id=1, source_target_pairs={{0,4},{1,5},{2,6},{3,7},{4,0},{5,1},{6,2},{7,3},{8,12},{9,13},{10,... | collective-permute-start | bytes 884744 | tf_op jit(solution)/shard_map/ppermute | solution.py:347
  475.8 6.8 %collective-permute-start.33 = (bf16[2,2,2,24,768]{4,3,0,1,2:T(8,128)(2,1)S(1)}, bf16[2,2,2,24,768]{4,3,0,1,2:T(8,128)(2,1)S(1)}, u32[]{:S(2)}, u32[]{:S(2)}) collective-permute-start(bf16[2,2,2,24,768]{4,3,0,1,2:T(8,128)(2,1)S(1)} %fusion.80), channel_id=1, source_target_pairs={{0,8},{1,9},{2,10},{3,11},{4,12},{5,13},{6,14},{7,15},{8,0},{9,1},... | collective-permute-start | bytes 884744 | tf_op jit(solution)/shard_map/ppermute | solution.py:347
  481.1 16.7 %copy-start.30 = (f32[2,24,2304]{2,1,0:T(8,128)S(1)}, f32[2,24,2304]{2,1,0:T(8,128)}, u32[]{:S(2)}) copy-start(f32[2,24,2304]{2,1,0:T(8,128)} %param.22) | copy-start | bytes 1327108
  481.1 16.7 %copy-start.48 = (f32[24,2304]{1,0:T(8,128)S(1)}, f32[24,2304]{1,0:T(8,128)}, u32[]{:S(2)}) copy-start(f32[24,2304]{1,0:T(8,128)} %param.16) | copy-start | bytes 663556
  481.1 5.6 %collective-permute-start.29 = (bf16[2,2,24,768]{3,2,0,1:T(8,128)(2,1)S(1)}, bf16[2,2,24,768]{3,2,0,1:T(8,128)(2,1)S(1)}, u32[]{:S(2)}, u32[]{:S(2)}) collective-permute-start(bf16[2,2,24,768]{3,2,0,1:T(8,128)(2,1)S(1)} %fusion.95), channel_id=1, source_target_pairs={{0,8},{1,9},{2,10},{3,11},{4,12},{5,13},{6,14},{7,15},{8,0},{9,1},... | collective-permute-start | bytes 442376 | tf_op jit(solution)/shard_map/ppermute | solution.py:347
  482.7 5.2 %collective-permute-start.34 = (bf16[2,2,24,768]{3,2,0,1:T(8,128)(2,1)S(1)}, bf16[2,2,24,768]{3,2,0,1:T(8,128)(2,1)S(1)}, u32[]{:S(2)}, u32[]{:S(2)}) collective-permute-start(bf16[2,2,24,768]{3,2,0,1:T(8,128)(2,1)S(1)} %fusion.96), channel_id=1, source_target_pairs={{0,1},{1,0},{2,3},{3,2},{4,5},{5,4},{6,7},{7,6},{8,9},{9,8},{10,11... | collective-permute-start | bytes 442376 | tf_op jit(solution)/shard_map/ppermute | solution.py:347
  486.7 4.4 collective-permute-start.30
  488.0 4.4 collective-permute-start.35
  491.2 4.9 collective-permute-start.31
  492.4 5.3 %collective-permute-start.36 = (bf16[24,768]{1,0:T(8,128)(2,1)S(1)}, bf16[24,768]{1,0:T(8,128)(2,1)S(1)}, u32[]{:S(2)}, u32[]{:S(2)}) collective-permute-start(bf16[24,768]{1,0:T(8,128)(2,1)S(1)} %fusion.107), channel_id=1, source_target_pairs={{0,16},{1,17},{2,18},{3,19},{4,20},{5,21},{6,22},{7,23},{8,24},{9,... | collective-permute-start | bytes 110600 | tf_op jit(solution)/shard_map/ppermute | solution.py:347
  (64 other events, 258.1 us)
Sparse Core Ops, SparseCore 0:
  11.5 97.3 all-gather.1

commit v13 on v10

--- a/solution.py
+++ b/solution.py
@@ -63,8 +63,9 @@
     rows = q_ref.shape[0]
     kbias = kbias_ref[...]
     lane = lax.broadcasted_iota(jnp.int32, (QUERY_CHUNK, 2 * head_size), 1)
-    for chunk in range(rows // QUERY_CHUNK):
-        span = pl.ds(chunk * QUERY_CHUNK, QUERY_CHUNK)
+
+    def chunk_body(chunk, carry):
+        span = pl.ds(pl.multiple_of(chunk * QUERY_CHUNK, QUERY_CHUNK), QUERY_CHUNK)
         mixed_parts = []
         totals = []
         for half in range(2):
@@ -86,6 +87,9 @@
             totals.append(highest + jnp.log(denominator))
         o_ref[span, :] = jnp.concatenate(mixed_parts, axis=1).astype(o_ref.dtype)
         l_ref[span, :] = jnp.where(lane < head_size, totals[0], totals[1])
+        return carry
+
+    lax.fori_loop(0, rows // QUERY_CHUNK, chunk_body, 0)
 
 
 def attention_backward_kernel(
@@ -94,14 +98,15 @@
     head_size = q_ref.shape[1] // 2
     rows = q_ref.shape[0]
     kbias = kbias_ref[...]
+    dk_ref[...] = jnp.zeros_like(dk_ref)
+    dv_ref[...] = jnp.zeros_like(dv_ref)
     for half in range(2):
         cols = pl.ds(half * head_size, head_size)
-        key = k_ref[:, cols]
-        value = v_ref[:, cols]
-        grad_key = None
-        grad_value = None
-        for chunk in range(rows // QUERY_CHUNK):
-            span = pl.ds(chunk * QUERY_CHUNK, QUERY_CHUNK)
+
+        def chunk_body(chunk, carry, cols=cols, half=half):
+            span = pl.ds(pl.multiple_of(chunk * QUERY_CHUNK, QUERY_CHUNK), QUERY_CHUNK)
+            key = k_ref[:, cols]
+            value = v_ref[:, cols]
             query = q_ref[span, cols]
             grad_out = do_ref[span, cols]
             total = l_ref[span, pl.ds(half * head_size, 1)]
@@ -120,19 +125,18 @@
             dq_ref[span, cols] = jnp.dot(
                 grad_scores, key, preferred_element_type=jnp.float32
             ).astype(dq_ref.dtype)
-            key_part = lax.dot_general(
+            dk_ref[:, cols] += lax.dot_general(
                 grad_scores, query, (((0,), (0,)), ((), ())), preferred_element_type=jnp.float32
             )
-            value_part = lax.dot_general(
+            dv_ref[:, cols] += lax.dot_general(
                 weights.astype(jnp.bfloat16),
                 grad_out,
                 (((0,), (0,)), ((), ())),
                 preferred_element_type=jnp.float32,
             )
-            grad_key = key_part if grad_key is None else grad_key + key_part
-            grad_value = value_part if grad_value is None else grad_value + value_part
-        dk_ref[:, cols] = grad_key
-        dv_ref[:, cols] = grad_value
+            return carry
+
+        lax.fori_loop(0, rows // QUERY_CHUNK, chunk_body, 0)
 
 
 def pad_rows(values, rows):
@@ -517,7 +521,9 @@
         ],
         axis=1,
     )
-    grad_in_term = jnp.dot(hidden_first.T, grad_projected, preferred_element_type=jnp.float32)
+    grad_in_term = jnp.dot(
+        hidden_first.T, grad_projected, preferred_element_type=jnp.float32
+    ).astype(jnp.bfloat16)
     projected_sums = jnp.sum(grad_projected.astype(jnp.float32), axis=0)
     grad_query_bias = projected_sums[:model_width]
     grad_value_bias = projected_sums[2 * model_width :]
@@ -546,7 +552,7 @@
             jnp.zeros((model_width, 128 - 12), jnp.float32),
         ],
         axis=1,
-    )
+    ).astype(jnp.bfloat16)
     owned_first = tree_reduce_scatter(
         jnp.concatenate([grad_in_term, small_grads], axis=1),
         (896, 768, 768),

time: 495 us -> 494 us (level)
  Pallas kernels: 92.6 us -> 102 us
  local copies, waits for them, and re-layouts: 105 us -> 99.9 us
    concatenate x10 -> x1, local copies, waits for them, and re-layouts: 19.7 us -> 7.69 us  [body(): jnp.concatenate([grad_in_term, small_grads], axis=1)]
    pallas_call x3, Pallas kernels: 58 us -> 64.4 us  [attention_pallas(): pl.pallas_call(attention_backward_kernel, grid=(span,), in_specs=[qi_spec...]
    another operation x13, other arithmetic: 14.2 us -> 8.47 us  [adam_step(): return (change, jnp.stack([first, second]))]
    unnamed x147 -> x173, local copies, waits for them, and re-layouts: 26.5 us -> 30.5 us
    convert_element_type x21 -> x20, local copies, waits for them, and re-layouts: 10 us -> 8.36 us  [tree_reduce_scatter(): lax.dynamic_index_in_dim(part, 1 - mine, axis=axis, keepdims=False)]
  transfers between devices with their start and end apart: 40 -> 40, of which waited for: 21 -> 22; matrix products, arithmetic and copies ran while one was open for 19% -> 19% of each run, Pallas kernels for 19% -> 21%
where the time goes in v13:
time: 494 us; the launch traced here: 489 us
  Pallas kernels  102 us (21%)
  local copies, waits for them, and re-layouts  99.9 us (20%)
  waiting for transfers between devices  92.8 us (19%)
  matrix products  73.9 us (15%)
  other arithmetic  62.5 us (13%)
  starting transfers between devices  42.3 us (9%)
  between operations  15.9 us (3%)
    pallas_call x3, Pallas kernels, attention_pallas(): pl.pallas_call(attention_backward_kernel, grid=(span,), in_specs=[qi_spec...  64.4 us
    ppermute x13, waiting for transfers between devices, double(): got = lax.ppermute(data, ('clip', 'frame'), pairs)  42 us
    ppermute x22, waiting for transfers between devices, tree_reduce_scatter(): got = lax.ppermute(send, ('clip', 'frame'), pairs)  38.6 us
    pallas_call x1, Pallas kernels, attention_pallas(): pl.pallas_call(attention_forward_kernel, grid=(pair_count,), in_specs=[q_...  37.4 us
    unnamed x173, local copies, waits for them, and re-layouts  30.5 us
    ppermute x13, starting transfers between devices, double(): got = lax.ppermute(data, ('clip', 'frame'), pairs)  19.5 us
    ppermute x22, starting transfers between devices, tree_reduce_scatter(): got = lax.ppermute(send, ('clip', 'frame'), pairs)  16.9 us
    ppermute x3, waiting for transfers between devices, body(): lax.ppermute(terms[row_count:].astype(jnp.bfloat16), 'frame', swap)  12.2 us
  transfers between devices with their start and end apart: 40, of which 22 were waited for; matrix products, arithmetic and copies ran while one was open for 19% of the time, Pallas kernels for 21%

profile of v13, /device:TPU:0, one launch (start us, length us, event | category | flops | bytes accessed | tf_op | source)
XLA Modules:
  0.0 489.1 jit_solution(7047662111554911718)
XLA Ops:
  12.8 4.1 collective-permute-start.8
  17.0 3.0 collective-permute-start
  25.5 29.5 %collective-permute-done.5 = bf16[2,24,768]{2,1,0:T(8,128)(2,1)S(1)} collective-permute-done((bf16[2,24,768]{2,1,0:T(8,128)(2,1)S(1)}, bf16[2,24,768]{2,1,0:T(8,128)(2,1)S(1)}, u32[]{:S(2)}, u32[]{:S(2)}) %collective-permute-start.5) | collective-permute-done | bytes 73760 | tf_op jit(solution)/shard_map/ppermute | solution.py:339
  60.1 1.8 collective-permute-done.10
  62.4 3.4 collective-permute-done.6
  69.4 3.2 collective-permute-done.7
  72.8 4.0 collective-permute-done.3
  76.8 1.7 fusion.111
  80.8 1.7 fusion.37
  83.2 3.1 maximum_select_fusion
  86.2 1.9 copy-done.18
  90.2 5.5 %add_convert_fusion = bf16[750,2304]{1,0:T(8,128)(2,1)S(1)} fusion(f32[2304]{0:T(1024)S(1)} %pad_maximum_fusion.15, bf16[768,2432]{1,0:T(8,128)(2,1)} %bitcast.328, bf16[1,750,768]{2,1,0:T(8,128)(2,1)S(1)} %copy-done.6, f32[768]{0:T(1024)S(1)} %get-tuple-element.182, f32[768]{0:T(1024)S(1)} %get-tuple-element.183, f32[750]{0:T(1024)S(1)} %add_rsqrt_fusion.2, ...), kind=kOutput, calls=%fused_computation.14 | convolution fusion | flops 2661120000 | bytes 8168304 | tf_op jit(solution)/shard_map/dot_general | solution.py:431
  99.1 3.5 add_convert_fusion.1
  102.6 2.7 fusion.8.k_ref.v_ref
  105.3 37.4 %shard_map.293 = (bf16[768,768]{1,0:T(8,128)(2,1)S(1)}, f32[768,768]{1,0:T(8,128)S(1)}) custom-call(bf16[768,768]{1,0:T(8,128)(2,1)S(1)} %pad.24.q_ref, bf16[1536,1536]{1,0:T(8,128)(2,1)} %fusion.8.k_ref.v_ref, bf16[1536,1536]{1,0:T(8,128)(2,1)} %fusion.8.k_ref.v_ref, f32[1,1536]{1,0:T(1,128)S(1)} %compare_select_fusion.kbias_ref), custom_call_target="tpu_custom_call" | custom-call | tf_op jit(solution)/shard_map/pallas_call | solution.py:161
  144.1 2.5 fusion.116
  148.4 4.8 slice.315
  153.2 8.5 %reshape.1150 = bf16[3072,768]{1,0:T(8,128)(2,1)} reshape(bf16[768,3072]{1,0:T(8,128)(2,1)} %slice.315) | data formatting | bytes 9437184 | tf_op jit(solution)/shard_map/reshape | solution.py:416
  161.7 9.1 %multiply_convert_fusion = (bf16[750,3072]{1,0:T(8,128)(2,1)S(1)}, f32[750,3072]{1,0:T(8,128)}) fusion(f32[3072]{0:T(1024)S(1)} %add.414, bf16[768,6912]{1,0:T(8,128)(2,1)} %all-gather.2.cloned.1.call-done, f32[750,768]{1,0:T(8,128)} %copy-done.11, f32[768]{0:T(1024)S(1)} %get-tuple-element.177, f32[768]{0:T(1024)S(1)} %get-tuple-element.178, ...), kind=kOutput, calls=%fused_computation.12 | convolution fusion | flops 3555648000 | bytes 20877168 | tf_op jit(solution)/shard_map/dot_general | solution.py:451
  170.7 2.2 copy-done.73
  172.9 6.0 %convolution_convert_fusion.2 = bf16[3072,768]{1,0:T(8,128)(2,1)} fusion(bf16[750,3072]{1,0:T(8,128)(2,1)S(1)} %get-tuple-element.235, bf16[1,750,768]{2,1,0:T(8,128)(2,1)S(1)} %copy-done.17), kind=kOutput, calls=%fused_computation.19 | convolution fusion | flops 3541303296 | bytes 10478592 | tf_op jit(solution)/shard_map/dot_general | solution.py:461
  178.8 8.5 %concatenate.300 = bf16[2,2,2,2,2,24,3072]{6,5,4,3,2,1,0:T(8,128)(2,1)} reshape(bf16[3072,768]{1,0:T(8,128)(2,1)} %convolution_convert_fusion.2) | data formatting | bytes 9437184 | tf_op jit(solution)/shard_map/concatenate | solution.py:481
  187.4 9.4 %fusion.117 = (bf16[3072]{0:T(1024)(128)(2,1)S(1)}, bf16[750,3072]{1,0:T(8,128)(2,1)S(1)}) fusion(f32[750,3072]{1,0:T(8,128)} %get-tuple-element.236, f32[3072]{0:T(1024)S(1)} %add.414, bf16[3072,768]{1,0:T(8,128)(2,1)} %reshape.1150, bf16[1,750,768]{2,1,0:T(8,128)(2,1)S(1)} %copy-done.17), kind=kOutput, calls=%fused_computation.295 | convolution fusion | flops 3566588928 | bytes 19713024 | tf_op jit(solution)/shard_map/dot_general | solution.py:465
  196.8 5.0 %convolution_convert_fusion.1 = bf16[768,3072]{1,0:T(8,128)(2,1)S(1)} fusion(bf16[750,3072]{1,0:T(8,128)(2,1)S(1)} %get-tuple-element.239, f32[750,768]{1,0:T(8,128)S(1)} %copy-done.12, f32[768]{0:T(1024)S(1)} %copy-done.67, f32[768]{0:T(1024)S(1)} %get-tuple-element.178, f32[750]{0:T(1024)S(1)} %add_rsqrt_fusion, f32[750]{0:T(1024)S(1)} %broadcast_multiply_fusion.4), kind=kOutput, calls=%fused_computation.18 | convolution fusion | flops 3544183296 | bytes 11642736 | tf_op jit(solution)/shard_map/dot_general | solution.py:467
  201.8 7.3 %multiply_reduce_fusion = (bf16[768]{0:T(1024)(128)(2,1)}, f32[750]{0:T(1024)S(1)}, f32[750]{0:T(1024)S(1)}, bf16[768]{0:T(1024)(128)(2,1)S(1)}, f32[750,768]{1,0:T(8,128)S(1)}) fusion(f32[750,768]{1,0:T(8,128)S(1)} %copy-done.12, f32[750]{0:T(1024)S(1)} %add_rsqrt_fusion, f32[750]{0:T(1024)S(1)} %broadcast_multiply_fusion.4, ...), kind=kOutput, calls=%fused_computation.68 | convolution fusion | flops 3544124928 | bytes 13952736 | tf_op jit(solution)/shard_map/dot_general | solution.py:471
  212.2 8.3 %pad_maximum_fusion = bf16[2,2,2,2,2,24,6912]{6,5,4,3,2,1,0:T(8,128)(2,1)} fusion(bf16[2,2,2,2,2,24,768]{6,5,4,3,2,1,0:T(8,128)(2,1)S(1)} %bitcast.332, bf16[2,2,2,2,2,24,3072]{6,5,4,3,2,1,0:T(8,128)(2,1)S(1)} %bitcast.326, bf16[2,2,2,2,2,24,3072]{6,5,4,3,2,1,0:T(8,128)(2,1)S(1)} %bitcast.319), kind=kLoop, calls=%fused_computation.1 | loop fusion | flops 31850496 | bytes 21233664 | tf_op jit(solution)/shard_map/concatenate | solution.py:481
  220.6 8.7 %constant_dynamic-slice_fusion.1 = (bf16[2,2,2,1,2,24,6912]{6,5,4,3,2,1,0:T(8,128)(2,1)}, bf16[2,2,2,1,2,24,6912]{6,5,4,3,2,1,0:T(8,128)(2,1)}) fusion(bf16[2,2,2,2,2,24,6912]{6,5,4,3,2,1,0:T(8,128)(2,1)} %pad_maximum_fusion, s32[]{:T(128)S(6)} %select_n.394, s32[]{:T(128)S(6)} %select_n.395), kind=kLoop, calls=%fused_computation.254 | loop fusion | bytes 21233672 | tf_op jit(solution)/shard_map/jit(dynamic_index_in_dim)/dynamic_slice | solution.py:313
  229.2 5.3 %copy.175 = bf16[2,2,2,1,2,24,6912]{6,5,0,4,2,1,3:T(8,128)(2,1)} copy(bf16[2,2,2,1,2,24,6912]{6,5,4,3,2,1,0:T(8,128)(2,1)} %get-tuple-element.195) | data formatting | bytes 10616832
  239.7 2.4 convolution_convert_fusion.4
  242.2 21.6 %shard_map.294 = (f32[768,256]{1,0:T(8,128)S(1)}, f32[1536,256]{1,0:T(8,128)S(1)}, f32[1536,256]{1,0:T(8,128)}) custom-call(bf16[768,768]{1,0:T(8,128)(2,1)S(1)} %pad.24.q_ref, bf16[1536,1536]{1,0:T(8,128)(2,1)} %fusion.8.k_ref.v_ref, bf16[1536,1536]{1,0:T(8,128)(2,1)} %fusion.8.k_ref.v_ref, bf16[768,768]{1,0:T(8,128)(2,1)S(1)} %pad.26.do_ref, ...), custom_call_target="tpu_custom_call" | custom-call | tf_op jit(solution)/shard_map/pallas_call | solution.py:180
  266.5 2.2 collective-permute-start.19
  268.7 5.3 %convert_add_fusion = f32[2,2,2,2,24,6912]{5,4,0,3,2,1:T(8,128)S(1)} fusion(bf16[2,2,2,2,24,6912]{5,4,0,3,2,1:T(8,128)(2,1)} %collective-permute-done.14, bf16[2,2,2,1,2,24,6912]{6,5,4,3,2,1,0:T(8,128)(2,1)} %get-tuple-element.194), kind=kLoop, calls=%fused_computation.2 | loop fusion | flops 7962624 | bytes 21233664 | tf_op jit(solution)/shard_map/add | solution.py:321
  274.1 4.9 %fusion.112 = (f32[2,2,2,2,24,3456]{5,4,0,3,2,1:T(8,128)}, f32[2,2,2,2,24,3456]{5,4,0,3,2,1:T(8,128)}) fusion(f32[2,2,2,2,24,6912]{5,4,0,3,2,1:T(8,128)S(1)} %convert_add_fusion), kind=kLoop, calls=%fused_computation.290 | loop fusion | bytes 21233664 | tf_op jit(solution)/shard_map/slice | solution.py:307
  279.0 3.1 fusion.49
  282.0 3.0 fusion.50
  285.0 8.5 %fusion.48 = bf16[1,750,768]{2,1,0:T(8,128)(2,1)} fusion(f32[750,768]{1,0:T(8,128)S(1)} %copy-done.13, bf16[750,3072]{1,0:T(8,128)(2,1)} %copy-done.73, bf16[3072,768]{1,0:T(8,128)(2,1)} %reshape.1150, f32[768]{0:T(1024)S(1)} %copy-done.65), kind=kOutput, calls=%fused_computation.92 | convolution fusion | flops 3540672000 | bytes 12785664 | tf_op jit(solution)/shard_map/dot_general | solution.py:455
  298.1 2.3 fusion.44
  300.5 21.4 %shard_map.295 = (f32[768,256]{1,0:T(8,128)S(1)}, f32[1536,256]{1,0:T(8,128)S(1)}, f32[1536,256]{1,0:T(8,128)}) custom-call(bf16[768,768]{1,0:T(8,128)(2,1)S(1)} %pad.24.q_ref, bf16[1536,1536]{1,0:T(8,128)(2,1)} %fusion.8.k_ref.v_ref, bf16[1536,1536]{1,0:T(8,128)(2,1)} %fusion.8.k_ref.v_ref, bf16[768,768]{1,0:T(8,128)(2,1)S(1)} %pad.27.do_ref, ...), custom_call_target="tpu_custom_call" | custom-call | tf_op jit(solution)/shard_map/pallas_call | solution.py:180
  328.7 2.0 collective-permute-start.18
  331.6 2.0 collective-permute-start.17
  333.7 21.4 %shard_map.296 = (f32[768,256]{1,0:T(8,128)S(1)}, f32[1536,256]{1,0:T(8,128)S(1)}, f32[1536,256]{1,0:T(8,128)}) custom-call(bf16[768,768]{1,0:T(8,128)(2,1)S(1)} %pad.24.q_ref, bf16[1536,1536]{1,0:T(8,128)(2,1)} %fusion.8.k_ref.v_ref, bf16[1536,1536]{1,0:T(8,128)(2,1)} %fusion.8.k_ref.v_ref, bf16[768,768]{1,0:T(8,128)(2,1)S(1)} %pad.28.do_ref, ...), custom_call_target="tpu_custom_call" | custom-call | tf_op jit(solution)/shard_map/pallas_call | solution.py:180
  361.2 1.9 collective-permute-start.37
  364.9 1.8 collective-permute-start.21
  368.8 9.8 %collective-permute-done.20 = bf16[750,512]{1,0:T(8,128)(2,1)S(1)} collective-permute-done((bf16[750,512]{1,0:T(8,128)(2,1)S(1)}, bf16[750,512]{1,0:T(8,128)(2,1)S(1)}, u32[]{:S(2)}, u32[]{:S(2)}) %collective-permute-start.20) | collective-permute-done | bytes 768032 | tf_op jit(solution)/shard_map/ppermute | solution.py:508
  379.7 6.0 %collective-permute-done.37 = bf16[2,24,3456]{2,1,0:T(8,128)(2,1)S(1)} collective-permute-done((bf16[2,24,3456]{2,1,0:T(8,128)(2,1)S(1)}, bf16[2,24,3456]{2,1,0:T(8,128)(2,1)S(1)}, u32[]{:S(2)}, u32[]{:S(2)}) %collective-permute-start.37) | collective-permute-done | bytes 331808 | tf_op jit(solution)/shard_map/ppermute | solution.py:320
  385.9 6.9 %collective-permute-done.35 = bf16[2,24,3456]{2,1,0:T(8,128)(2,1)S(1)} collective-permute-done((bf16[2,24,3456]{2,1,0:T(8,128)(2,1)S(1)}, bf16[2,24,3456]{2,1,0:T(8,128)(2,1)S(1)}, u32[]{:S(2)}, u32[]{:S(2)}) %collective-permute-start.35) | collective-permute-done | bytes 331808 | tf_op jit(solution)/shard_map/ppermute | solution.py:320
  393.0 3.7 collective-permute-done.38
  396.7 3.7 collective-permute-done.36
  404.6 2.3 collective-permute-done.21
  407.0 1.8 fusion.45
  412.0 6.6 %fusion.32 = (bf16[768]{0:T(1024)(128)(2,1)S(1)}, f32[750]{0:T(1024)S(1)}, f32[750]{0:T(1024)S(1)}, bf16[768]{0:T(1024)(128)(2,1)S(1)}, f32[750,768]{1,0:T(8,128)}) fusion(bf16[1,750,768]{2,1,0:T(8,128)(2,1)S(1)} %copy-done.7, f32[750]{0:T(1024)S(1)} %copy-done.59, f32[750]{0:T(1024)S(1)} %copy-done.53, f32[768]{0:T(1024)S(1)} %copy-done.56, ...), kind=kOutput, calls=%fused_computation.57 | convolution fusion | flops 2659964928 | bytes 10475376 | tf_op jit(solution)/shard_map/dot_general | solution.py:530
  418.7 2.5 reduce.2
  421.3 7.0 %convolution_convert_fusion = bf16[768,2304]{1,0:T(8,128)(2,1)} fusion(bf16[750,2304]{1,0:T(8,128)(2,1)} %slice_dynamic-update-slice_fusion, bf16[1,750,768]{2,1,0:T(8,128)(2,1)S(1)} %copy-done.7, f32[768]{0:T(1024)S(1)} %copy-done.64, f32[768]{0:T(1024)S(1)} %copy-done.56, f32[750]{0:T(1024)S(1)} %copy-done.59, f32[750]{0:T(1024)S(1)} %copy-done.53), kind=kOutput, calls=%fused_computation.17 | convolution fusion | flops 2659433472 | bytes 8159088 | tf_op jit(solution)/shard_map/dot_general | solution.py:524
  430.4 7.7 %concatenate.309 = bf16[768,2432]{1,0:T(8,128)(2,1)} concatenate(bf16[768,2304]{1,0:T(8,128)(2,1)} %convolution_convert_fusion, bf16[768,1]{1,0:T(8,128)(2,1)S(1)} %stack.415, bf16[768,1]{1,0:T(8,128)(2,1)} %stack.416, bf16[768,1]{1,0:T(8,128)(2,1)S(1)} %stack.417, bf16[768,1]{1,0:T(8,128)(2,1)S(1)} %stack.418, bf16[768,1]{1,0:T(8,128)(2,1)S(1)} %copy-done.41, ...), dimensions={1} | concatenate | bytes 7471104 | tf_op jit(solution)/shard_map/concatenate | solution.py:557
  438.2 1.8 dynamic-slice_bitcast_fusion
  446.6 1.8 fusion.53
  449.6 4.3 collective-permute-done.31
  454.4 3.3 collective-permute-done.27
  458.2 1.8 collective-permute-done.23
  460.2 1.8 collective-permute-start.24
  462.2 1.8 collective-permute-start.33
  464.6 2.6 collective-permute-done.33
  468.5 1.9 collective-permute-start.30
  478.1 2.1 collective-permute-done.26
  (395 shorter events, 96.0 us)
Async XLA Ops:
  7.2 12.8 %copy-start.6 = (bf16[1,750,768]{2,1,0:T(8,128)(2,1)S(1)}, bf16[1,750,768]{2,1,0:T(8,128)(2,1)}, u32[]{:S(2)}) copy-start(bf16[1,750,768]{2,1,0:T(8,128)(2,1)} %param.14) | copy-start | bytes 3456004
  7.2 136.9 %all-gather.2.cloned.1.call-start = ((), (), s32[]{:S(2)}) async-start(), calls=%async_computation | async-start | bytes 10948608 | tf_op jit(solution)/shard_map/all_gather | solution.py:409
  12.8 8.7 %collective-permute-start.8 = (bf16[24,768]{1,0:T(8,128)(2,1)S(1)}, bf16[24,768]{1,0:T(8,128)(2,1)S(1)}, u32[]{:S(2)}, u32[]{:S(2)}) collective-permute-start(bf16[24,768]{1,0:T(8,128)(2,1)S(1)} %get-tuple-element.215), channel_id=1, source_target_pairs={{0,16},{1,17},{2,18},{3,19},{4,20},{5,21},{6,22},{7,23},{8,24},{9,... | collective-permute-start | bytes 110600 | tf_op jit(solution)/shard_map/ppermute | solution.py:339
  16.9 6.2 %collective-permute-start.4 = (bf16[24,768]{1,0:T(8,128)(2,1)S(1)}, bf16[24,768]{1,0:T(8,128)(2,1)S(1)}, u32[]{:S(2)}, u32[]{:S(2)}) collective-permute-start(bf16[24,768]{1,0:T(8,128)(2,1)S(1)} %get-tuple-element.221), channel_id=1, source_target_pairs={{0,16},{1,17},{2,18},{3,19},{4,20},{5,21},{6,22},{7,23},{8,24},{9,... | collective-permute-start | bytes 110600 | tf_op jit(solution)/shard_map/ppermute | solution.py:339
  17.0 6.9 %collective-permute-start = (bf16[24,896]{1,0:T(8,128)(2,1)S(1)}, bf16[24,896]{1,0:T(8,128)(2,1)S(1)}, u32[]{:S(2)}, u32[]{:S(2)}) collective-permute-start(bf16[24,896]{1,0:T(8,128)(2,1)S(1)} %get-tuple-element.218), channel_id=1, source_target_pairs={{0,16},{1,17},{2,18},{3,19},{4,20},{5,21},{6,22},{7,23},{8,24},{9,... | collective-permute-start | bytes 129032 | tf_op jit(solution)/shard_map/ppermute | solution.py:339
  20.0 59.3 %collective-permute-start.13 = (bf16[1,750,768]{2,1,0:T(8,128)(2,1)S(1)}, bf16[1,750,768]{2,1,0:T(8,128)(2,1)}, u32[]{:S(2)}, u32[]{:S(2)}) collective-permute-start(bf16[1,750,768]{2,1,0:T(8,128)(2,1)S(1)} %copy-done.6), channel_id=1, source_target_pairs={{0,1},{1,0},{2,3},{3,2},{4,5},{5,4},{6,7},{7,6},{8,9},{9,8},{10,11... | collective-permute-start | bytes 3456008 | tf_op jit(solution)/shard_map/ppermute | solution.py:423
  21.6 35.1 %collective-permute-start.9 = (bf16[2,24,768]{2,1,0:T(8,128)(2,1)S(1)}, bf16[2,24,768]{2,1,0:T(8,128)(2,1)S(1)}, u32[]{:S(2)}, u32[]{:S(2)}) collective-permute-start(bf16[2,24,768]{2,1,0:T(8,128)(2,1)S(1)} %maximum_select_fusion.18), channel_id=1, source_target_pairs={{0,4},{1,5},{2,6},{3,7},{4,0},{5,1},{6,2},{7,3},{8,12},{9,13},{10,... | collective-permute-start | bytes 221192 | tf_op jit(solution)/shard_map/ppermute | solution.py:339
  23.2 31.8 %collective-permute-start.5 = (bf16[2,24,768]{2,1,0:T(8,128)(2,1)S(1)}, bf16[2,24,768]{2,1,0:T(8,128)(2,1)S(1)}, u32[]{:S(2)}, u32[]{:S(2)}) collective-permute-start(bf16[2,24,768]{2,1,0:T(8,128)(2,1)S(1)} %maximum_select_fusion.17), channel_id=1, source_target_pairs={{0,1},{1,0},{2,3},{3,2},{4,5},{5,4},{6,7},{7,6},{8,9},{9,8},{10,11... | collective-permute-start | bytes 221192 | tf_op jit(solution)/shard_map/ppermute | solution.py:339
  23.9 34.4 %collective-permute-start.1 = (bf16[2,24,896]{2,1,0:T(8,128)(2,1)S(1)}, bf16[2,24,896]{2,1,0:T(8,128)(2,1)S(1)}, u32[]{:S(2)}, u32[]{:S(2)}) collective-permute-start(bf16[2,24,896]{2,1,0:T(8,128)(2,1)S(1)} %maximum_select_fusion.15), channel_id=1, source_target_pairs={{0,8},{1,9},{2,10},{3,11},{4,12},{5,13},{6,14},{7,15},{8,0},{9,1},... | collective-permute-start | bytes 258056 | tf_op jit(solution)/shard_map/ppermute | solution.py:339
  55.0 10.8 %collective-permute-start.6 = (bf16[2,2,24,768]{3,2,0,1:T(8,128)(2,1)S(1)}, bf16[2,2,24,768]{3,2,0,1:T(8,128)(2,1)S(1)}, u32[]{:S(2)}, u32[]{:S(2)}) collective-permute-start(bf16[2,2,24,768]{3,2,0,1:T(8,128)(2,1)S(1)} %maximum_select_fusion.12), channel_id=1, source_target_pairs={{0,8},{1,9},{2,10},{3,11},{4,12},{5,13},{6,14},{7,15},{8,0},{9,1},... | collective-permute-start | bytes 442376 | tf_op jit(solution)/shard_map/ppermute | solution.py:339
  56.7 5.2 %collective-permute-start.10 = (bf16[2,2,24,768]{3,2,1,0:T(8,128)(2,1)S(1)}, bf16[2,2,24,768]{3,2,1,0:T(8,128)(2,1)S(1)}, u32[]{:S(2)}, u32[]{:S(2)}) collective-permute-start(bf16[2,2,24,768]{3,2,1,0:T(8,128)(2,1)S(1)} %maximum_select_fusion.13), channel_id=1, source_target_pairs={{0,1},{1,0},{2,3},{3,2},{4,5},{5,4},{6,7},{7,6},{8,9},{9,8},{10,11... | collective-permute-start | bytes 442376 | tf_op jit(solution)/shard_map/ppermute | solution.py:339
  58.5 9.1 %collective-permute-start.2 = (bf16[2,2,24,896]{3,2,0,1:T(8,128)(2,1)S(1)}, bf16[2,2,24,896]{3,2,0,1:T(8,128)(2,1)S(1)}, u32[]{:S(2)}, u32[]{:S(2)}) collective-permute-start(bf16[2,2,24,896]{3,2,0,1:T(8,128)(2,1)S(1)} %maximum_select_fusion.10), channel_id=1, source_target_pairs={{0,4},{1,5},{2,6},{3,7},{4,0},{5,1},{6,2},{7,3},{8,12},{9,13},{10,... | collective-permute-start | bytes 516104 | tf_op jit(solution)/shard_map/ppermute | solution.py:339
  61.9 10.8 %collective-permute-start.11 = (bf16[2,2,2,24,768]{4,3,2,1,0:T(8,128)(2,1)S(1)}, bf16[2,2,2,24,768]{4,3,2,1,0:T(8,128)(2,1)S(1)}, u32[]{:S(2)}, u32[]{:S(2)}) collective-permute-start(bf16[2,2,2,24,768]{4,3,2,1,0:T(8,128)(2,1)S(1)} %maximum_select_fusion.8), channel_id=1, source_target_pairs={{0,8},{1,9},{2,10},{3,11},{4,12},{5,13},{6,14},{7,15},{8,0},{9,1},... | collective-permute-start | bytes 884744 | tf_op jit(solution)/shard_map/ppermute | solution.py:339
  65.9 6.8 %collective-permute-start.7 = (bf16[2,2,2,24,768]{4,3,0,2,1:T(8,128)(2,1)S(1)}, bf16[2,2,2,24,768]{4,3,0,2,1:T(8,128)(2,1)S(1)}, u32[]{:S(2)}, u32[]{:S(2)}) collective-permute-start(bf16[2,2,2,24,768]{4,3,0,2,1:T(8,128)(2,1)S(1)} %maximum_select_fusion.7), channel_id=1, source_target_pairs={{0,4},{1,5},{2,6},{3,7},{4,0},{5,1},{6,2},{7,3},{8,12},{9,13},{10,... | collective-permute-start | bytes 884744 | tf_op jit(solution)/shard_map/ppermute | solution.py:339
  67.7 9.1 %collective-permute-start.3 = (bf16[2,2,2,24,896]{4,3,0,1,2:T(8,128)(2,1)S(1)}, bf16[2,2,2,24,896]{4,3,0,1,2:T(8,128)(2,1)S(1)}, u32[]{:S(2)}, u32[]{:S(2)}) collective-permute-start(bf16[2,2,2,24,896]{4,3,0,1,2:T(8,128)(2,1)S(1)} %maximum_select_fusion.5), channel_id=1, source_target_pairs={{0,1},{1,0},{2,3},{3,2},{4,5},{5,4},{6,7},{7,6},{8,9},{9,8},{10,11... | collective-permute-start | bytes 1032200 | tf_op jit(solution)/shard_map/ppermute | solution.py:339
  78.5 4.7 collective-permute-start.12
  78.7 11.5 %copy-start.52 = (f32[750]{0:T(1024)}, f32[750]{0:T(1024)S(1)}, u32[]{:S(2)}) copy-start(f32[750]{0:T(1024)S(1)} %broadcast_multiply_fusion.6) | copy-start | bytes 9004
  79.3 10.9 %copy-start.58 = (f32[750]{0:T(1024)}, f32[750]{0:T(1024)S(1)}, u32[]{:S(2)}) copy-start(f32[750]{0:T(1024)S(1)} %add_rsqrt_fusion.2) | copy-start | bytes 9004
  90.2 71.5 %copy-start.66 = (f32[768]{0:T(1024)}, f32[768]{0:T(1024)S(1)}, u32[]{:S(2)}) copy-start(f32[768]{0:T(1024)S(1)} %get-tuple-element.177) | copy-start | bytes 9220
  161.7 11.2 %copy-start.17 = (bf16[1,750,768]{2,1,0:T(8,128)(2,1)S(1)}, bf16[1,750,768]{2,1,0:T(8,128)(2,1)}, u32[]{:S(2)}) copy-start(bf16[1,750,768]{2,1,0:T(8,128)(2,1)} %param.15) | copy-start | bytes 3456004
  187.3 9.5 %copy-start.12 = (f32[750,768]{1,0:T(8,128)S(1)}, f32[750,768]{1,0:T(8,128)}, u32[]{:S(2)}) copy-start(f32[750,768]{1,0:T(8,128)} %copy-done.11) | copy-start | bytes 6912004
  187.3 9.5 %copy-start.67 = (f32[768]{0:T(1024)S(1)}, f32[768]{0:T(1024)}, u32[]{:S(2)}) copy-start(f32[768]{0:T(1024)} %copy-done.66) | copy-start | bytes 9220
  229.2 10.5 %copy-start.9 = (f32[750,768]{1,0:T(8,128)S(1)}, f32[750,768]{1,0:T(8,128)}, u32[]{:S(2)}) copy-start(f32[750,768]{1,0:T(8,128)} %copy-done.8) | copy-start | bytes 6912004
  234.5 34.2 %collective-permute-start.14 = (bf16[2,2,2,2,24,6912]{5,4,0,3,2,1:T(8,128)(2,1)}, bf16[2,2,2,2,24,6912]{5,4,0,3,2,1:T(8,128)(2,1)}, u32[]{:S(2)}, u32[]{:S(2)}) collective-permute-start(bf16[2,2,2,2,24,6912]{5,4,0,3,2,1:T(8,128)(2,1)} %bitcast.317), channel_id=1, source_target_pairs={{0,2},{1,3},{2,0},{3,1},{4,6},{5,7},{6,4},{7,5},{8,10},{9,11},{10,... | collective-permute-start | bytes 15925256 | tf_op jit(solution)/shard_map/ppermute | solution.py:320
  242.1 21.7 %copy-start.4 = (bf16[750,768]{1,0:T(8,128)(2,1)}, bf16[750,768]{1,0:T(8,128)(2,1)S(1)}, u32[]{:S(2)}) copy-start(bf16[750,768]{1,0:T(8,128)(2,1)S(1)} %convolution_convert_fusion.4) | copy-start | bytes 3456004
  266.5 31.6 %collective-permute-start.19 = (bf16[750,512]{1,0:T(8,128)(2,1)}, bf16[750,512]{1,0:T(8,128)(2,1)}, u32[]{:S(2)}, u32[]{:S(2)}) collective-permute-start(bf16[750,512]{1,0:T(8,128)(2,1)} %fusion.47), channel_id=1, source_target_pairs={{0,1},{1,0},{2,3},{3,2},{4,5},{5,4},{6,7},{7,6},{8,9},{9,8},{10,11... | collective-permute-start | bytes 2304008 | tf_op jit(solution)/shard_map/ppermute | solution.py:508
  282.0 42.5 %collective-permute-start.15 = (bf16[2,2,2,24,3456]{4,3,0,2,1:T(8,128)(2,1)}, bf16[2,2,2,24,3456]{4,3,0,2,1:T(8,128)(2,1)}, u32[]{:S(2)}, u32[]{:S(2)}) collective-permute-start(bf16[2,2,2,24,3456]{4,3,0,2,1:T(8,128)(2,1)} %fusion.49), channel_id=1, source_target_pairs={{0,4},{1,5},{2,6},{3,7},{4,0},{5,1},{6,2},{7,3},{8,12},{9,13},{10,... | collective-permute-start | bytes 3981320 | tf_op jit(solution)/shard_map/ppermute | solution.py:320
  285.0 41.1 %collective-permute-start.16 = (bf16[2,2,2,24,3456]{4,3,0,2,1:T(8,128)(2,1)}, bf16[2,2,2,24,3456]{4,3,0,2,1:T(8,128)(2,1)}, u32[]{:S(2)}, u32[]{:S(2)}) collective-permute-start(bf16[2,2,2,24,3456]{4,3,0,2,1:T(8,128)(2,1)} %fusion.50), channel_id=1, source_target_pairs={{0,8},{1,9},{2,10},{3,11},{4,12},{5,13},{6,14},{7,15},{8,0},{9,1},... | collective-permute-start | bytes 3981320 | tf_op jit(solution)/shard_map/ppermute | solution.py:320
  285.0 10.5 %copy-start.70 = (bf16[768]{0:T(1024)(128)(2,1)S(1)}, bf16[768]{0:T(1024)(128)(2,1)}, u32[]{:S(2)}) copy-start(bf16[768]{0:T(1024)(128)(2,1)} %get-tuple-element.168) | copy-start | bytes 4612
  300.4 24.1 %slice-start.4 = ((s8[5308416]{0:T(1024)(128)(4,1)}), s8[4194304]{0:T(1024)(128)(4,1)S(1)}, s32[]{:S(2)}) async-start(s8[5308416]{0:T(1024)(128)(4,1)} %bitcast.322), calls=%async_computation.5 | async-start | bytes 8388608
  300.5 24.0 %slice-start.5 = ((s8[5308416]{0:T(1024)(128)(4,1)}), s8[1114112]{0:T(1024)(128)(4,1)S(1)}, s32[]{:S(2)}) async-start(s8[5308416]{0:T(1024)(128)(4,1)} %bitcast.322), calls=%async_computation.6 | async-start | bytes 2228224
  328.7 30.0 %collective-permute-start.18 = (bf16[2,2,24,3456]{3,2,0,1:T(8,128)(2,1)}, bf16[2,2,24,3456]{3,2,0,1:T(8,128)(2,1)}, u32[]{:S(2)}, u32[]{:S(2)}) collective-permute-start(bf16[2,2,24,3456]{3,2,0,1:T(8,128)(2,1)} %fusion.65), channel_id=1, source_target_pairs={{0,4},{1,5},{2,6},{3,7},{4,0},{5,1},{6,2},{7,3},{8,12},{9,13},{10,... | collective-permute-start | bytes 1990664 | tf_op jit(solution)/shard_map/ppermute | solution.py:320
  331.6 28.2 %collective-permute-start.17 = (bf16[2,2,24,3456]{3,2,0,1:T(8,128)(2,1)}, bf16[2,2,24,3456]{3,2,0,1:T(8,128)(2,1)}, u32[]{:S(2)}, u32[]{:S(2)}) collective-permute-start(bf16[2,2,24,3456]{3,2,0,1:T(8,128)(2,1)} %fusion.64), channel_id=1, source_target_pairs={{0,8},{1,9},{2,10},{3,11},{4,12},{5,13},{6,14},{7,15},{8,0},{9,1},... | collective-permute-start | bytes 1990664 | tf_op jit(solution)/shard_map/ppermute | solution.py:320
  358.4 20.2 %collective-permute-start.20 = (bf16[750,512]{1,0:T(8,128)(2,1)S(1)}, bf16[750,512]{1,0:T(8,128)(2,1)S(1)}, u32[]{:S(2)}, u32[]{:S(2)}) collective-permute-start(bf16[750,512]{1,0:T(8,128)(2,1)S(1)} %slice.450), channel_id=1, source_target_pairs={{0,1},{1,0},{2,3},{3,2},{4,5},{5,4},{6,7},{7,6},{8,9},{9,8},{10,11... | collective-permute-start | bytes 2304008 | tf_op jit(solution)/shard_map/ppermute | solution.py:508
  361.2 24.5 %collective-permute-start.37 = (bf16[2,24,3456]{2,1,0:T(8,128)(2,1)S(1)}, bf16[2,24,3456]{2,1,0:T(8,128)(2,1)S(1)}, u32[]{:S(2)}, u32[]{:S(2)}) collective-permute-start(bf16[2,24,3456]{2,1,0:T(8,128)(2,1)S(1)} %fusion.68), channel_id=1, source_target_pairs={{0,1},{1,0},{2,3},{3,2},{4,5},{5,4},{6,7},{7,6},{8,9},{9,8},{10,11... | collective-permute-start | bytes 995336 | tf_op jit(solution)/shard_map/ppermute | solution.py:320
  363.1 29.7 %collective-permute-start.35 = (bf16[2,24,3456]{2,1,0:T(8,128)(2,1)S(1)}, bf16[2,24,3456]{2,1,0:T(8,128)(2,1)S(1)}, u32[]{:S(2)}, u32[]{:S(2)}) collective-permute-start(bf16[2,24,3456]{2,1,0:T(8,128)(2,1)S(1)} %fusion.67), channel_id=1, source_target_pairs={{0,1},{1,0},{2,3},{3,2},{4,5},{5,4},{6,7},{7,6},{8,9},{9,8},{10,11... | collective-permute-start | bytes 995336 | tf_op jit(solution)/shard_map/ppermute | solution.py:320
  364.9 42.1 %collective-permute-start.21 = (bf16[750,512]{1,0:T(8,128)(2,1)}, bf16[750,512]{1,0:T(8,128)(2,1)}, u32[]{:S(2)}, u32[]{:S(2)}) collective-permute-start(bf16[750,512]{1,0:T(8,128)(2,1)} %slice.449), channel_id=1, source_target_pairs={{0,1},{1,0},{2,3},{3,2},{4,5},{5,4},{6,7},{7,6},{8,9},{9,8},{10,11... | collective-permute-start | bytes 2304008 | tf_op jit(solution)/shard_map/ppermute | solution.py:508
  385.8 14.7 %copy-start.28 = (f32[2,24,3072]{2,1,0:T(8,128)S(1)}, f32[2,24,3072]{2,1,0:T(8,128)}, u32[]{:S(2)}) copy-start(f32[2,24,3072]{2,1,0:T(8,128)} %param.24) | copy-start | bytes 1769476
  385.8 10.9 %collective-permute-start.38 = (bf16[24,3456]{1,0:T(8,128)(2,1)S(1)}, bf16[24,3456]{1,0:T(8,128)(2,1)S(1)}, u32[]{:S(2)}, u32[]{:S(2)}) collective-permute-start(bf16[24,3456]{1,0:T(8,128)(2,1)S(1)} %fusion.84), channel_id=1, source_target_pairs={{0,16},{1,17},{2,18},{3,19},{4,20},{5,21},{6,22},{7,23},{8,24},{9,... | collective-permute-start | bytes 497672 | tf_op jit(solution)/shard_map/ppermute | solution.py:320
  392.9 9.4 %copy-start.23 = (f32[2,96,768]{2,1,0:T(8,128)S(1)}, f32[2,96,768]{2,1,0:T(8,128)}, u32[]{:S(2)}) copy-start(f32[2,96,768]{2,1,0:T(8,128)} %param.25) | copy-start | bytes 1769476
  392.9 7.5 %collective-permute-start.36 = (bf16[24,3456]{1,0:T(8,128)(2,1)S(1)}, bf16[24,3456]{1,0:T(8,128)(2,1)S(1)}, u32[]{:S(2)}, u32[]{:S(2)}) collective-permute-start(bf16[24,3456]{1,0:T(8,128)(2,1)S(1)} %fusion.83), channel_id=1, source_target_pairs={{0,16},{1,17},{2,18},{3,19},{4,20},{5,21},{6,22},{7,23},{8,24},{9,... | collective-permute-start | bytes 497672 | tf_op jit(solution)/shard_map/ppermute | solution.py:320
  421.2 9.2 %copy-start.39 = (bf16[768,1]{1,0:T(8,128)(2,1)S(1)}, bf16[768,1]{1,0:T(8,128)(2,1)}, u32[]{:S(2)}) copy-start(bf16[768,1]{1,0:T(8,128)(2,1)} %stack.422) | copy-start | bytes 4612
  421.2 9.2 %copy-start.40 = (bf16[768,4]{1,0:T(8,128)(2,1)S(1)}, bf16[768,4]{1,0:T(8,128)(2,1)}, u32[]{:S(2)}) copy-start(bf16[768,4]{1,0:T(8,128)(2,1)} %reshape.1154) | copy-start | bytes 18436
  440.0 3.9 collective-permute-start.22
  444.7 9.1 %collective-permute-start.31 = (bf16[2,2,2,24,768]{4,3,2,1,0:T(8,128)(2,1)S(1)}, bf16[2,2,2,24,768]{4,3,2,1,0:T(8,128)(2,1)S(1)}, u32[]{:S(2)}, u32[]{:S(2)}) collective-permute-start(bf16[2,2,2,24,768]{4,3,2,1,0:T(8,128)(2,1)S(1)} %fusion.78), channel_id=1, source_target_pairs={{0,8},{1,9},{2,10},{3,11},{4,12},{5,13},{6,14},{7,15},{8,0},{9,1},... | collective-permute-start | bytes 884744 | tf_op jit(solution)/shard_map/ppermute | solution.py:320
  448.6 9.1 %collective-permute-start.27 = (bf16[2,2,2,24,768]{4,3,2,1,0:T(8,128)(2,1)S(1)}, bf16[2,2,2,24,768]{4,3,2,1,0:T(8,128)(2,1)S(1)}, u32[]{:S(2)}, u32[]{:S(2)}) collective-permute-start(bf16[2,2,2,24,768]{4,3,2,1,0:T(8,128)(2,1)S(1)} %fusion.77), channel_id=1, source_target_pairs={{0,4},{1,5},{2,6},{3,7},{4,0},{5,1},{6,2},{7,3},{8,12},{9,13},{10,... | collective-permute-start | bytes 884744 | tf_op jit(solution)/shard_map/ppermute | solution.py:320
  449.0 11.0 %collective-permute-start.23 = (bf16[2,2,2,24,896]{4,3,2,1,0:T(8,128)(2,1)S(1)}, bf16[2,2,2,24,896]{4,3,2,1,0:T(8,128)(2,1)S(1)}, u32[]{:S(2)}, u32[]{:S(2)}) collective-permute-start(bf16[2,2,2,24,896]{4,3,2,1,0:T(8,128)(2,1)S(1)} %fusion.66), channel_id=1, source_target_pairs={{0,1},{1,0},{2,3},{3,2},{4,5},{5,4},{6,7},{7,6},{8,9},{9,8},{10,11... | collective-permute-start | bytes 1032200 | tf_op jit(solution)/shard_map/ppermute | solution.py:320
  453.9 8.2 %collective-permute-start.32 = (bf16[2,2,24,768]{3,2,1,0:T(8,128)(2,1)S(1)}, bf16[2,2,24,768]{3,2,1,0:T(8,128)(2,1)S(1)}, u32[]{:S(2)}, u32[]{:S(2)}) collective-permute-start(bf16[2,2,24,768]{3,2,1,0:T(8,128)(2,1)S(1)} %fusion.86), channel_id=1, source_target_pairs={{0,1},{1,0},{2,3},{3,2},{4,5},{5,4},{6,7},{7,6},{8,9},{9,8},{10,11... | collective-permute-start | bytes 442376 | tf_op jit(solution)/shard_map/ppermute | solution.py:320
  457.9 6.1 %collective-permute-start.28 = (bf16[2,2,24,768]{3,2,1,0:T(8,128)(2,1)S(1)}, bf16[2,2,24,768]{3,2,1,0:T(8,128)(2,1)S(1)}, u32[]{:S(2)}, u32[]{:S(2)}) collective-permute-start(bf16[2,2,24,768]{3,2,1,0:T(8,128)(2,1)S(1)} %fusion.85), channel_id=1, source_target_pairs={{0,8},{1,9},{2,10},{3,11},{4,12},{5,13},{6,14},{7,15},{8,0},{9,1},... | collective-permute-start | bytes 442376 | tf_op jit(solution)/shard_map/ppermute | solution.py:320
  460.1 12.7 %copy-start.69 = (f32[2,96]{1,0:T(2,128)S(1)}, f32[2,96]{1,0:T(2,128)}, u32[]{:S(2)}) copy-start(f32[2,96]{1,0:T(2,128)} %param.26) | copy-start | bytes 2308
  460.1 12.7 %copy-start.72 = (f32[96]{0:T(128)S(1)}, f32[96]{0:T(128)}, u32[]{:S(2)}) copy-start(f32[96]{0:T(128)} %param.20) | copy-start | bytes 1156
  460.1 13.2 %copy-start.49 = (f32[24,8]{1,0:T(8,128)S(1)}, f32[24,8]{1,0:T(8,128)}, u32[]{:S(2)}) copy-start(f32[24,8]{1,0:T(8,128)} %copy.152) | copy-start | bytes 2308
  460.1 13.2 %copy-start.50 = (f32[1,24,8]{2,1,0:T(8,128)S(1)}, f32[1,24,8]{2,1,0:T(8,128)}, u32[]{:S(2)}) copy-start(f32[1,24,8]{2,1,0:T(8,128)} %copy.162) | copy-start | bytes 2308
  460.1 13.2 %copy-start.51 = (f32[1,24,8]{2,1,0:T(8,128)S(1)}, f32[1,24,8]{2,1,0:T(8,128)}, u32[]{:S(2)}) copy-start(f32[1,24,8]{2,1,0:T(8,128)} %copy.161) | copy-start | bytes 2308
  460.2 10.2 %collective-permute-start.24 = (bf16[2,2,24,896]{3,2,1,0:T(8,128)(2,1)S(1)}, bf16[2,2,24,896]{3,2,1,0:T(8,128)(2,1)S(1)}, u32[]{:S(2)}, u32[]{:S(2)}) collective-permute-start(bf16[2,2,24,896]{3,2,1,0:T(8,128)(2,1)S(1)} %fusion.82), channel_id=1, source_target_pairs={{0,4},{1,5},{2,6},{3,7},{4,0},{5,1},{6,2},{7,3},{8,12},{9,13},{10,... | collective-permute-start | bytes 516104 | tf_op jit(solution)/shard_map/ppermute | solution.py:320
  462.1 18.1 %copy-start.35 = (f32[2,24,2304]{2,1,0:T(8,128)S(1)}, f32[2,24,2304]{2,1,0:T(8,128)}, u32[]{:S(2)}) copy-start(f32[2,24,2304]{2,1,0:T(8,128)} %param.22) | copy-start | bytes 1327108
  462.2 5.0 %collective-permute-start.33 = (bf16[2,24,768]{2,1,0:T(8,128)(2,1)S(1)}, bf16[2,24,768]{2,1,0:T(8,128)(2,1)S(1)}, u32[]{:S(2)}, u32[]{:S(2)}) collective-permute-start(bf16[2,24,768]{2,1,0:T(8,128)(2,1)S(1)} %fusion.91), channel_id=1, source_target_pairs={{0,4},{1,5},{2,6},{3,7},{4,0},{5,1},{6,2},{7,3},{8,12},{9,13},{10,... | collective-permute-start | bytes 221192 | tf_op jit(solution)/shard_map/ppermute | solution.py:320
  464.0 16.3 %copy-start.38 = (f32[24,2304]{1,0:T(8,128)S(1)}, f32[24,2304]{1,0:T(8,128)}, u32[]{:S(2)}) copy-start(f32[24,2304]{1,0:T(8,128)} %param.16) | copy-start | bytes 663556
  464.0 4.4 collective-permute-start.29
  467.3 5.2 %collective-permute-start.34 = (bf16[24,768]{1,0:T(8,128)(2,1)S(1)}, bf16[24,768]{1,0:T(8,128)(2,1)S(1)}, u32[]{:S(2)}, u32[]{:S(2)}) collective-permute-start(bf16[24,768]{1,0:T(8,128)(2,1)S(1)} %fusion.97), channel_id=1, source_target_pairs={{0,16},{1,17},{2,18},{3,19},{4,20},{5,21},{6,22},{7,23},{8,24},{9,... | collective-permute-start | bytes 110600 | tf_op jit(solution)/shard_map/ppermute | solution.py:320
  468.5 5.0 %collective-permute-start.30 = (bf16[24,768]{1,0:T(8,128)(2,1)S(1)}, bf16[24,768]{1,0:T(8,128)(2,1)S(1)}, u32[]{:S(2)}, u32[]{:S(2)}) collective-permute-start(bf16[24,768]{1,0:T(8,128)(2,1)S(1)} %fusion.96), channel_id=1, source_target_pairs={{0,16},{1,17},{2,18},{3,19},{4,20},{5,21},{6,22},{7,23},{8,24},{9,... | collective-permute-start | bytes 110600 | tf_op jit(solution)/shard_map/ppermute | solution.py:320
  470.4 4.6 collective-permute-start.25
  472.6 9.3 %copy-start.71 = (f32[96]{0:T(128)}, f32[96]{0:T(128)S(1)}, u32[]{:S(2)}) copy-start(f32[96]{0:T(128)S(1)} %reshape.1157) | copy-start | bytes 1156
  475.0 5.2 %collective-permute-start.26 = (bf16[24,896]{1,0:T(8,128)(2,1)S(1)}, bf16[24,896]{1,0:T(8,128)(2,1)S(1)}, u32[]{:S(2)}, u32[]{:S(2)}) collective-permute-start(bf16[24,896]{1,0:T(8,128)(2,1)S(1)} %fusion.95), channel_id=1, source_target_pairs={{0,16},{1,17},{2,18},{3,19},{4,20},{5,21},{6,22},{7,23},{8,24},{9,... | collective-permute-start | bytes 129032 | tf_op jit(solution)/shard_map/ppermute | solution.py:320
  (57 other events, 224.7 us)
Sparse Core Ops, SparseCore 0:
  11.5 97.3 all-gather.1

commit v14 on v13

--- a/solution.py
+++ b/solution.py
@@ -484,8 +484,10 @@
     grad_mixed = jnp.dot(grad_attended, full_out.T, preferred_element_type=jnp.float32).astype(
         jnp.bfloat16
     )
-    piece_pairs = 2
+    piece_pairs = 1
     piece_count = model_width // 128 // piece_pairs
+    stage_count = 1 + len(late_orders[0])
+    hooked = list(range(1, min(piece_count, stage_count)))
 
     def run_piece(index, mixed_grads):
         return attention_pallas(
@@ -496,12 +498,14 @@
         return lambda tied: (run_piece(index, tied[index - 1][1]), tied[index - 1][1])
 
     hooks = {0: lambda tied: ((), grad_mixed)}
-    hooks.update({index: piece_hook(index) for index in range(1, piece_count)})
+    hooks.update({index: piece_hook(index) for index in hooked})
     pieces = [run_piece(0, grad_mixed)]
     owned_late, tied = tree_reduce_scatter(
         late_terms, (3456, 3456), late_orders, (bit_count, core_bit), hooks
     )
-    pieces += [tied[index][0] for index in range(1, piece_count)]
+    pieces += [tied[index][0] for index in hooked]
+    last_mixed = tied[hooked[-1]][1] if hooked else grad_mixed
+    pieces += [run_piece(index, last_mixed) for index in range(len(hooked) + 1, piece_count)]
     finished = []
     for grad_query, grad_keys, grad_values in pieces:
         terms = jnp.concatenate([grad_keys, grad_values], axis=1)

time: 494 us -> 486 us (0.984)
  waiting for transfers between devices: 92.8 us -> 84.2 us
  starting transfers between devices: 42.3 us -> 49.4 us
    ppermute x22, waiting for transfers between devices: 38.6 us -> 31.4 us  [tree_reduce_scatter(): got = lax.ppermute(send, ('clip', 'frame'), pairs)]
    unnamed x173 -> x178, local copies, waits for them, and re-layouts: 30.5 us -> 29 us
    ppermute x3 -> x6, waiting for transfers between devices: 12.2 us -> 10.7 us  [body(): lax.ppermute(terms[row_count:].astype(jnp.bfloat16), 'frame', swap)]
    pallas_call x3 -> x6, Pallas kernels: 64.4 us -> 64.8 us  [attention_pallas(): pl.pallas_call(attention_backward_kernel, grid=(span,), in_specs=[qi_spec...]
    another operation x10 -> x14, other arithmetic: 9.95 us -> 9.97 us
  transfers between devices with their start and end apart: 40 -> 43, of which waited for: 22 -> 22; matrix products, arithmetic and copies ran while one was open for 19% -> 17% of each run, Pallas kernels for 21% -> 21%
where the time goes in v14:
time: 486 us; the launch traced here: 480 us
  Pallas kernels  102 us (21%)
  local copies, waits for them, and re-layouts  95.3 us (20%)
  waiting for transfers between devices  84.2 us (17%)
  matrix products  72.4 us (15%)
  other arithmetic  60.6 us (12%)
  starting transfers between devices  49.4 us (10%)
  between operations  16.4 us (3%)
    pallas_call x6, Pallas kernels, attention_pallas(): pl.pallas_call(attention_backward_kernel, grid=(span,), in_specs=[qi_spec...  64.8 us
    ppermute x13, waiting for transfers between devices, double(): got = lax.ppermute(data, ('clip', 'frame'), pairs)  42 us
    pallas_call x1, Pallas kernels, attention_pallas(): pl.pallas_call(attention_forward_kernel, grid=(pair_count,), in_specs=[q_...  37.4 us
    ppermute x22, waiting for transfers between devices, tree_reduce_scatter(): got = lax.ppermute(send, ('clip', 'frame'), pairs)  31.4 us
    unnamed x178, local copies, waits for them, and re-layouts  29 us
    ppermute x22, starting transfers between devices, tree_reduce_scatter(): got = lax.ppermute(send, ('clip', 'frame'), pairs)  21.2 us
    ppermute x13, starting transfers between devices, double(): got = lax.ppermute(data, ('clip', 'frame'), pairs)  19.5 us
    ppermute x6, waiting for transfers between devices, body(): lax.ppermute(terms[row_count:].astype(jnp.bfloat16), 'frame', swap)  10.7 us
  transfers between devices with their start and end apart: 43, of which 22 were waited for; matrix products, arithmetic and copies ran while one was open for 17% of the time, Pallas kernels for 21%

profile of v14, /device:TPU:0, one launch (start us, length us, event | category | flops | bytes accessed | tf_op | source)
XLA Modules:
  0.0 480.4 jit_solution(13061196638288750213)
XLA Ops:
  12.8 4.1 collective-permute-start.8
  17.0 3.0 collective-permute-start
  25.5 29.5 %collective-permute-done.5 = bf16[2,24,768]{2,1,0:T(8,128)(2,1)S(1)} collective-permute-done((bf16[2,24,768]{2,1,0:T(8,128)(2,1)S(1)}, bf16[2,24,768]{2,1,0:T(8,128)(2,1)S(1)}, u32[]{:S(2)}, u32[]{:S(2)}) %collective-permute-start.5) | collective-permute-done | bytes 73760 | tf_op jit(solution)/shard_map/ppermute | solution.py:339
  60.1 1.8 collective-permute-done.10
  62.4 3.4 collective-permute-done.6
  69.4 3.2 collective-permute-done.7
  72.8 4.0 collective-permute-done.3
  76.8 1.7 fusion.116
  80.8 1.7 fusion.37
  83.2 3.1 maximum_select_fusion
  86.2 1.9 copy-done.15
  90.2 5.5 %add_convert_fusion = bf16[750,2304]{1,0:T(8,128)(2,1)S(1)} fusion(f32[2304]{0:T(1024)S(1)} %pad_maximum_fusion.16, bf16[768,2432]{1,0:T(8,128)(2,1)} %bitcast.326, bf16[1,750,768]{2,1,0:T(8,128)(2,1)S(1)} %copy-done.2, f32[768]{0:T(1024)S(1)} %get-tuple-element.226, f32[768]{0:T(1024)S(1)} %get-tuple-element.227, f32[750]{0:T(1024)S(1)} %add_rsqrt_fusion.2, ...), kind=kOutput, calls=%fused_computation.14 | convolution fusion | flops 2661120000 | bytes 8168304 | tf_op jit(solution)/shard_map/dot_general | solution.py:431
  99.1 3.5 add_convert_fusion.1
  102.6 2.7 fusion.8.k_ref.v_ref
  105.3 37.4 %shard_map.293 = (bf16[768,768]{1,0:T(8,128)(2,1)S(1)}, f32[768,768]{1,0:T(8,128)S(1)}) custom-call(bf16[768,768]{1,0:T(8,128)(2,1)S(1)} %pad.39.q_ref, bf16[1536,1536]{1,0:T(8,128)(2,1)} %fusion.8.k_ref.v_ref, bf16[1536,1536]{1,0:T(8,128)(2,1)} %fusion.8.k_ref.v_ref, f32[1,1536]{1,0:T(1,128)S(1)} %compare_select_fusion.kbias_ref), custom_call_target="tpu_custom_call" | custom-call | tf_op jit(solution)/shard_map/pallas_call | solution.py:161
  144.1 2.5 fusion.121
  148.4 4.8 slice.408
  153.2 8.5 %reshape.1150 = bf16[3072,768]{1,0:T(8,128)(2,1)} reshape(bf16[768,3072]{1,0:T(8,128)(2,1)} %slice.408) | data formatting | bytes 9437184 | tf_op jit(solution)/shard_map/reshape | solution.py:416
  161.7 9.1 %multiply_convert_fusion = (bf16[750,3072]{1,0:T(8,128)(2,1)S(1)}, f32[750,3072]{1,0:T(8,128)}) fusion(f32[3072]{0:T(1024)S(1)} %add.429, bf16[768,6912]{1,0:T(8,128)(2,1)} %all-gather.2.cloned.1.call-done, f32[750,768]{1,0:T(8,128)} %copy-done.6, f32[768]{0:T(1024)S(1)} %get-tuple-element.221, f32[768]{0:T(1024)S(1)} %get-tuple-element.222, ...), kind=kOutput, calls=%fused_computation.12 | convolution fusion | flops 3555648000 | bytes 20877168 | tf_op jit(solution)/shard_map/dot_general | solution.py:451
  170.7 2.2 copy-done.71
  172.9 6.0 %convolution_convert_fusion.2 = bf16[3072,768]{1,0:T(8,128)(2,1)} fusion(bf16[750,3072]{1,0:T(8,128)(2,1)S(1)} %get-tuple-element.279, bf16[1,750,768]{2,1,0:T(8,128)(2,1)S(1)} %copy-done.14), kind=kOutput, calls=%fused_computation.19 | convolution fusion | flops 3541303296 | bytes 10478592 | tf_op jit(solution)/shard_map/dot_general | solution.py:461
  178.9 8.5 %concatenate.309 = bf16[2,2,2,2,2,24,3072]{6,5,4,3,2,1,0:T(8,128)(2,1)} reshape(bf16[3072,768]{1,0:T(8,128)(2,1)} %convolution_convert_fusion.2) | data formatting | bytes 9437184 | tf_op jit(solution)/shard_map/concatenate | solution.py:481
  187.4 9.4 %fusion.122 = (bf16[3072]{0:T(1024)(128)(2,1)S(1)}, bf16[750,3072]{1,0:T(8,128)(2,1)S(1)}) fusion(f32[750,3072]{1,0:T(8,128)} %get-tuple-element.280, f32[3072]{0:T(1024)S(1)} %add.429, bf16[3072,768]{1,0:T(8,128)(2,1)} %reshape.1150, bf16[1,750,768]{2,1,0:T(8,128)(2,1)S(1)} %copy-done.14), kind=kOutput, calls=%fused_computation.323 | convolution fusion | flops 3566588928 | bytes 19713024 | tf_op jit(solution)/shard_map/dot_general | solution.py:465
  196.8 5.0 %convolution_convert_fusion.1 = bf16[768,3072]{1,0:T(8,128)(2,1)S(1)} fusion(bf16[750,3072]{1,0:T(8,128)(2,1)S(1)} %get-tuple-element.283, f32[750,768]{1,0:T(8,128)S(1)} %copy-done.7, f32[768]{0:T(1024)S(1)} %copy-done.65, f32[768]{0:T(1024)S(1)} %get-tuple-element.222, f32[750]{0:T(1024)S(1)} %add_rsqrt_fusion, f32[750]{0:T(1024)S(1)} %broadcast_multiply_fusion.4), kind=kOutput, calls=%fused_computation.18 | convolution fusion | flops 3544183296 | bytes 11642736 | tf_op jit(solution)/shard_map/dot_general | solution.py:467
  201.8 7.3 %multiply_reduce_fusion = (bf16[768]{0:T(1024)(128)(2,1)}, f32[750]{0:T(1024)S(1)}, f32[750]{0:T(1024)S(1)}, bf16[768]{0:T(1024)(128)(2,1)S(1)}, f32[750,768]{1,0:T(8,128)S(1)}) fusion(f32[750,768]{1,0:T(8,128)S(1)} %copy-done.7, f32[750]{0:T(1024)S(1)} %add_rsqrt_fusion, f32[750]{0:T(1024)S(1)} %broadcast_multiply_fusion.4, ...), kind=kOutput, calls=%fused_computation.64 | convolution fusion | flops 3544124928 | bytes 13952736 | tf_op jit(solution)/shard_map/dot_general | solution.py:471
  212.2 8.3 %pad_maximum_fusion = bf16[2,2,2,2,2,24,6912]{6,5,4,3,2,1,0:T(8,128)(2,1)} fusion(bf16[2,2,2,2,2,24,768]{6,5,4,3,2,1,0:T(8,128)(2,1)S(1)} %bitcast.330, bf16[2,2,2,2,2,24,3072]{6,5,4,3,2,1,0:T(8,128)(2,1)S(1)} %bitcast.324, bf16[2,2,2,2,2,24,3072]{6,5,4,3,2,1,0:T(8,128)(2,1)S(1)} %bitcast.319), kind=kLoop, calls=%fused_computation.1 | loop fusion | flops 31850496 | bytes 21233664 | tf_op jit(solution)/shard_map/concatenate | solution.py:481
  220.6 8.7 %constant_dynamic-slice_fusion.1 = (bf16[2,2,2,1,2,24,6912]{6,5,4,3,2,1,0:T(8,128)(2,1)}, bf16[2,2,2,1,2,24,6912]{6,5,4,3,2,1,0:T(8,128)(2,1)}) fusion(bf16[2,2,2,2,2,24,6912]{6,5,4,3,2,1,0:T(8,128)(2,1)} %pad_maximum_fusion, s32[]{:T(128)S(6)} %select_n.403, s32[]{:T(128)S(6)} %select_n.404), kind=kLoop, calls=%fused_computation.282 | loop fusion | bytes 21233672 | tf_op jit(solution)/shard_map/jit(dynamic_index_in_dim)/dynamic_slice | solution.py:313
  229.3 5.2 %copy.175 = bf16[2,2,2,1,2,24,6912]{6,5,0,4,2,1,3:T(8,128)(2,1)} copy(bf16[2,2,2,1,2,24,6912]{6,5,4,3,2,1,0:T(8,128)(2,1)} %get-tuple-element.239) | data formatting | bytes 10616832
  238.3 3.1 convolution_convert_fusion.4
  241.4 2.6 collective-permute-done.14
  243.9 5.3 %convert_add_fusion = f32[2,2,2,2,24,6912]{5,4,0,3,2,1:T(8,128)S(1)} fusion(bf16[2,2,2,2,24,6912]{5,4,0,3,2,1:T(8,128)(2,1)} %collective-permute-done.14, bf16[2,2,2,1,2,24,6912]{6,5,4,3,2,1,0:T(8,128)(2,1)} %get-tuple-element.238), kind=kLoop, calls=%fused_computation.2 | loop fusion | flops 7962624 | bytes 21233664 | tf_op jit(solution)/shard_map/add | solution.py:321
  249.3 4.9 %fusion.117 = (f32[2,2,2,2,24,3456]{5,4,0,3,2,1:T(8,128)}, f32[2,2,2,2,24,3456]{5,4,0,3,2,1:T(8,128)}) fusion(f32[2,2,2,2,24,6912]{5,4,0,3,2,1:T(8,128)S(1)} %convert_add_fusion), kind=kLoop, calls=%fused_computation.318 | loop fusion | bytes 21233664 | tf_op jit(solution)/shard_map/slice | solution.py:307
  254.2 3.1 fusion.42
  257.3 8.5 %fusion.41 = bf16[1,750,768]{2,1,0:T(8,128)(2,1)} fusion(f32[750,768]{1,0:T(8,128)S(1)} %copy-done.8, bf16[750,3072]{1,0:T(8,128)(2,1)} %copy-done.71, bf16[3072,768]{1,0:T(8,128)(2,1)} %reshape.1150, f32[768]{0:T(1024)S(1)} %copy-done.63), kind=kOutput, calls=%fused_computation.82 | convolution fusion | flops 3540672000 | bytes 12785664 | tf_op jit(solution)/shard_map/dot_general | solution.py:455
  265.8 10.8 %shard_map.294 = (f32[768,128]{1,0:T(8,128)S(1)}, f32[1536,128]{1,0:T(8,128)S(1)}, f32[1536,128]{1,0:T(8,128)S(1)}) custom-call(bf16[768,768]{1,0:T(8,128)(2,1)S(1)} %pad.39.q_ref, bf16[1536,1536]{1,0:T(8,128)(2,1)} %fusion.8.k_ref.v_ref, bf16[1536,1536]{1,0:T(8,128)(2,1)} %fusion.8.k_ref.v_ref, bf16[768,768]{1,0:T(8,128)(2,1)S(1)} %pad.41.do_ref, ...), custom_call_target="tpu_custom_call" | custom-call | tf_op jit(solution)/shard_map/pallas_call | solution.py:180
  277.7 2.2 collective-permute-start.23
  279.9 3.0 fusion.43
  287.4 2.2 collective-permute-done.23
  289.6 1.8 fusion.62
  291.5 10.8 %shard_map.295 = (f32[768,128]{1,0:T(8,128)S(1)}, f32[1536,128]{1,0:T(8,128)S(1)}, f32[1536,128]{1,0:T(8,128)S(1)}) custom-call(bf16[768,768]{1,0:T(8,128)(2,1)S(1)} %pad.39.q_ref, bf16[1536,1536]{1,0:T(8,128)(2,1)} %fusion.8.k_ref.v_ref, bf16[1536,1536]{1,0:T(8,128)(2,1)} %fusion.8.k_ref.v_ref, bf16[768,768]{1,0:T(8,128)(2,1)S(1)} %pad.42.do_ref, ...), custom_call_target="tpu_custom_call" | custom-call | tf_op jit(solution)/shard_map/pallas_call | solution.py:180
  302.5 2.4 bitcast_add_fusion.1
  304.9 9.5 %collective-permute-done.16 = bf16[2,2,2,24,3456]{4,3,0,2,1:T(8,128)(2,1)} collective-permute-done((bf16[2,2,2,24,3456]{4,3,0,2,1:T(8,128)(2,1)}, bf16[2,2,2,24,3456]{4,3,0,2,1:T(8,128)(2,1)}, u32[]{:S(2)}, u32[]{:S(2)}) %collective-permute-start.16) | collective-permute-done | bytes 1327136 | tf_op jit(solution)/shard_map/ppermute | solution.py:320
  316.0 1.8 collective-permute-start.18
  318.9 10.7 %shard_map.296 = (f32[768,128]{1,0:T(8,128)S(1)}, f32[1536,128]{1,0:T(8,128)S(1)}, f32[1536,128]{1,0:T(8,128)S(1)}) custom-call(bf16[768,768]{1,0:T(8,128)(2,1)S(1)} %pad.39.q_ref, bf16[1536,1536]{1,0:T(8,128)(2,1)} %fusion.8.k_ref.v_ref, bf16[1536,1536]{1,0:T(8,128)(2,1)} %fusion.8.k_ref.v_ref, bf16[768,768]{1,0:T(8,128)(2,1)S(1)} %pad.43.do_ref, ...), custom_call_target="tpu_custom_call" | custom-call | tf_op jit(solution)/shard_map/pallas_call | solution.py:180
  332.2 1.8 collective-permute-done.17
  336.4 10.9 %shard_map.297 = (f32[768,128]{1,0:T(8,128)S(1)}, f32[1536,128]{1,0:T(8,128)S(1)}, f32[1536,128]{1,0:T(8,128)S(1)}) custom-call(bf16[768,768]{1,0:T(8,128)(2,1)S(1)} %pad.39.q_ref, bf16[1536,1536]{1,0:T(8,128)(2,1)} %fusion.8.k_ref.v_ref, bf16[1536,1536]{1,0:T(8,128)(2,1)} %fusion.8.k_ref.v_ref, bf16[768,768]{1,0:T(8,128)(2,1)S(1)} %pad.44.do_ref, ...), custom_call_target="tpu_custom_call" | custom-call | tf_op jit(solution)/shard_map/pallas_call | solution.py:180
  350.4 2.9 collective-permute-start.21
  353.4 10.7 %shard_map.298 = (f32[768,128]{1,0:T(8,128)S(1)}, f32[1536,128]{1,0:T(8,128)S(1)}, f32[1536,128]{1,0:T(8,128)S(1)}) custom-call(bf16[768,768]{1,0:T(8,128)(2,1)S(1)} %pad.39.q_ref, bf16[1536,1536]{1,0:T(8,128)(2,1)} %fusion.8.k_ref.v_ref, bf16[1536,1536]{1,0:T(8,128)(2,1)} %fusion.8.k_ref.v_ref, bf16[768,768]{1,0:T(8,128)(2,1)S(1)} %pad.45.do_ref, ...), custom_call_target="tpu_custom_call" | custom-call | tf_op jit(solution)/shard_map/pallas_call | solution.py:180
  375.4 10.9 %shard_map.299 = (f32[768,128]{1,0:T(8,128)S(1)}, f32[1536,128]{1,0:T(8,128)S(1)}, f32[1536,128]{1,0:T(8,128)S(1)}) custom-call(bf16[768,768]{1,0:T(8,128)(2,1)S(1)} %pad.39.q_ref, bf16[1536,1536]{1,0:T(8,128)(2,1)} %fusion.8.k_ref.v_ref, bf16[1536,1536]{1,0:T(8,128)(2,1)} %fusion.8.k_ref.v_ref, bf16[768,768]{1,0:T(8,128)(2,1)S(1)} %pad.46.do_ref, ...), custom_call_target="tpu_custom_call" | custom-call | tf_op jit(solution)/shard_map/pallas_call | solution.py:180
  392.7 8.5 %collective-permute-done.27 = bf16[750,256]{1,0:T(8,128)(2,1)S(1)} collective-permute-done((bf16[750,256]{1,0:T(8,128)(2,1)S(1)}, bf16[750,256]{1,0:T(8,128)(2,1)S(1)}, u32[]{:S(2)}, u32[]{:S(2)}) %collective-permute-start.27) | collective-permute-done | bytes 384032 | tf_op jit(solution)/shard_map/ppermute | solution.py:512
  401.9 1.8 copy-done.13
  405.0 4.6 fusion.32
  409.6 2.5 reduce.2
  412.2 6.8 %convolution_convert_fusion = bf16[768,2304]{1,0:T(8,128)(2,1)} fusion(bf16[750,2304]{1,0:T(8,128)(2,1)} %copy-done.13, bf16[1,750,768]{2,1,0:T(8,128)(2,1)S(1)} %copy-done.3, f32[768]{0:T(1024)S(1)} %copy-done.62, f32[768]{0:T(1024)S(1)} %copy-done.56, f32[750]{0:T(1024)S(1)} %copy-done.58, f32[750]{0:T(1024)S(1)} %copy-done.54), kind=kOutput, calls=%fused_computation.17 | convolution fusion | flops 2659433472 | bytes 8159088 | tf_op jit(solution)/shard_map/dot_general | solution.py:528
  420.5 7.7 %concatenate.321 = bf16[768,2432]{1,0:T(8,128)(2,1)} concatenate(bf16[768,2304]{1,0:T(8,128)(2,1)} %convolution_convert_fusion, bf16[768,1]{1,0:T(8,128)(2,1)S(1)} %stack.415, bf16[768,1]{1,0:T(8,128)(2,1)S(1)} %stack.416, bf16[768,1]{1,0:T(8,128)(2,1)S(1)} %stack.417, bf16[768,1]{1,0:T(8,128)(2,1)S(1)} %stack.418, bf16[768,1]{1,0:T(8,128)(2,1)S(1)} %copy-done.43, ...), dimensions={1} | concatenate | bytes 7471104 | tf_op jit(solution)/shard_map/concatenate | solution.py:561
  428.3 1.8 dynamic-slice_bitcast_fusion
  436.7 1.8 fusion.46
  438.7 1.7 collective-permute-start.34
  441.5 2.3 collective-permute-done.38
  445.1 2.7 collective-permute-done.34
  448.9 2.5 collective-permute-done.30
  455.2 3.3 collective-permute-done.40
  459.1 2.6 collective-permute-start.37
  469.2 2.2 collective-permute-done.33
  (427 shorter events, 99.5 us)
Async XLA Ops:
  7.2 12.8 %copy-start.2 = (bf16[1,750,768]{2,1,0:T(8,128)(2,1)S(1)}, bf16[1,750,768]{2,1,0:T(8,128)(2,1)}, u32[]{:S(2)}) copy-start(bf16[1,750,768]{2,1,0:T(8,128)(2,1)} %param.14) | copy-start | bytes 3456004
  7.2 136.9 %all-gather.2.cloned.1.call-start = ((), (), s32[]{:S(2)}) async-start(), calls=%async_computation | async-start | bytes 10948608 | tf_op jit(solution)/shard_map/all_gather | solution.py:409
  12.8 8.7 %collective-permute-start.8 = (bf16[24,768]{1,0:T(8,128)(2,1)S(1)}, bf16[24,768]{1,0:T(8,128)(2,1)S(1)}, u32[]{:S(2)}, u32[]{:S(2)}) collective-permute-start(bf16[24,768]{1,0:T(8,128)(2,1)S(1)} %get-tuple-element.259), channel_id=1, source_target_pairs={{0,16},{1,17},{2,18},{3,19},{4,20},{5,21},{6,22},{7,23},{8,24},{9,... | collective-permute-start | bytes 110600 | tf_op jit(solution)/shard_map/ppermute | solution.py:339
  16.9 6.2 %collective-permute-start.4 = (bf16[24,768]{1,0:T(8,128)(2,1)S(1)}, bf16[24,768]{1,0:T(8,128)(2,1)S(1)}, u32[]{:S(2)}, u32[]{:S(2)}) collective-permute-start(bf16[24,768]{1,0:T(8,128)(2,1)S(1)} %get-tuple-element.265), channel_id=1, source_target_pairs={{0,16},{1,17},{2,18},{3,19},{4,20},{5,21},{6,22},{7,23},{8,24},{9,... | collective-permute-start | bytes 110600 | tf_op jit(solution)/shard_map/ppermute | solution.py:339
  17.0 6.9 %collective-permute-start = (bf16[24,896]{1,0:T(8,128)(2,1)S(1)}, bf16[24,896]{1,0:T(8,128)(2,1)S(1)}, u32[]{:S(2)}, u32[]{:S(2)}) collective-permute-start(bf16[24,896]{1,0:T(8,128)(2,1)S(1)} %get-tuple-element.262), channel_id=1, source_target_pairs={{0,16},{1,17},{2,18},{3,19},{4,20},{5,21},{6,22},{7,23},{8,24},{9,... | collective-permute-start | bytes 129032 | tf_op jit(solution)/shard_map/ppermute | solution.py:339
  20.0 59.3 %collective-permute-start.13 = (bf16[1,750,768]{2,1,0:T(8,128)(2,1)S(1)}, bf16[1,750,768]{2,1,0:T(8,128)(2,1)}, u32[]{:S(2)}, u32[]{:S(2)}) collective-permute-start(bf16[1,750,768]{2,1,0:T(8,128)(2,1)S(1)} %copy-done.2), channel_id=1, source_target_pairs={{0,1},{1,0},{2,3},{3,2},{4,5},{5,4},{6,7},{7,6},{8,9},{9,8},{10,11... | collective-permute-start | bytes 3456008 | tf_op jit(solution)/shard_map/ppermute | solution.py:423
  21.6 35.1 %collective-permute-start.9 = (bf16[2,24,768]{2,1,0:T(8,128)(2,1)S(1)}, bf16[2,24,768]{2,1,0:T(8,128)(2,1)S(1)}, u32[]{:S(2)}, u32[]{:S(2)}) collective-permute-start(bf16[2,24,768]{2,1,0:T(8,128)(2,1)S(1)} %maximum_select_fusion.18), channel_id=1, source_target_pairs={{0,4},{1,5},{2,6},{3,7},{4,0},{5,1},{6,2},{7,3},{8,12},{9,13},{10,... | collective-permute-start | bytes 221192 | tf_op jit(solution)/shard_map/ppermute | solution.py:339
  23.2 31.8 %collective-permute-start.5 = (bf16[2,24,768]{2,1,0:T(8,128)(2,1)S(1)}, bf16[2,24,768]{2,1,0:T(8,128)(2,1)S(1)}, u32[]{:S(2)}, u32[]{:S(2)}) collective-permute-start(bf16[2,24,768]{2,1,0:T(8,128)(2,1)S(1)} %maximum_select_fusion.17), channel_id=1, source_target_pairs={{0,1},{1,0},{2,3},{3,2},{4,5},{5,4},{6,7},{7,6},{8,9},{9,8},{10,11... | collective-permute-start | bytes 221192 | tf_op jit(solution)/shard_map/ppermute | solution.py:339
  23.9 34.4 %collective-permute-start.1 = (bf16[2,24,896]{2,1,0:T(8,128)(2,1)S(1)}, bf16[2,24,896]{2,1,0:T(8,128)(2,1)S(1)}, u32[]{:S(2)}, u32[]{:S(2)}) collective-permute-start(bf16[2,24,896]{2,1,0:T(8,128)(2,1)S(1)} %maximum_select_fusion.15), channel_id=1, source_target_pairs={{0,8},{1,9},{2,10},{3,11},{4,12},{5,13},{6,14},{7,15},{8,0},{9,1},... | collective-permute-start | bytes 258056 | tf_op jit(solution)/shard_map/ppermute | solution.py:339
  55.0 10.8 %collective-permute-start.6 = (bf16[2,2,24,768]{3,2,0,1:T(8,128)(2,1)S(1)}, bf16[2,2,24,768]{3,2,0,1:T(8,128)(2,1)S(1)}, u32[]{:S(2)}, u32[]{:S(2)}) collective-permute-start(bf16[2,2,24,768]{3,2,0,1:T(8,128)(2,1)S(1)} %maximum_select_fusion.12), channel_id=1, source_target_pairs={{0,8},{1,9},{2,10},{3,11},{4,12},{5,13},{6,14},{7,15},{8,0},{9,1},... | collective-permute-start | bytes 442376 | tf_op jit(solution)/shard_map/ppermute | solution.py:339
  56.7 5.2 %collective-permute-start.10 = (bf16[2,2,24,768]{3,2,1,0:T(8,128)(2,1)S(1)}, bf16[2,2,24,768]{3,2,1,0:T(8,128)(2,1)S(1)}, u32[]{:S(2)}, u32[]{:S(2)}) collective-permute-start(bf16[2,2,24,768]{3,2,1,0:T(8,128)(2,1)S(1)} %maximum_select_fusion.13), channel_id=1, source_target_pairs={{0,1},{1,0},{2,3},{3,2},{4,5},{5,4},{6,7},{7,6},{8,9},{9,8},{10,11... | collective-permute-start | bytes 442376 | tf_op jit(solution)/shard_map/ppermute | solution.py:339
  58.5 9.1 %collective-permute-start.2 = (bf16[2,2,24,896]{3,2,0,1:T(8,128)(2,1)S(1)}, bf16[2,2,24,896]{3,2,0,1:T(8,128)(2,1)S(1)}, u32[]{:S(2)}, u32[]{:S(2)}) collective-permute-start(bf16[2,2,24,896]{3,2,0,1:T(8,128)(2,1)S(1)} %maximum_select_fusion.10), channel_id=1, source_target_pairs={{0,4},{1,5},{2,6},{3,7},{4,0},{5,1},{6,2},{7,3},{8,12},{9,13},{10,... | collective-permute-start | bytes 516104 | tf_op jit(solution)/shard_map/ppermute | solution.py:339
  61.9 10.8 %collective-permute-start.11 = (bf16[2,2,2,24,768]{4,3,2,1,0:T(8,128)(2,1)S(1)}, bf16[2,2,2,24,768]{4,3,2,1,0:T(8,128)(2,1)S(1)}, u32[]{:S(2)}, u32[]{:S(2)}) collective-permute-start(bf16[2,2,2,24,768]{4,3,2,1,0:T(8,128)(2,1)S(1)} %maximum_select_fusion.8), channel_id=1, source_target_pairs={{0,8},{1,9},{2,10},{3,11},{4,12},{5,13},{6,14},{7,15},{8,0},{9,1},... | collective-permute-start | bytes 884744 | tf_op jit(solution)/shard_map/ppermute | solution.py:339
  65.9 6.8 %collective-permute-start.7 = (bf16[2,2,2,24,768]{4,3,0,2,1:T(8,128)(2,1)S(1)}, bf16[2,2,2,24,768]{4,3,0,2,1:T(8,128)(2,1)S(1)}, u32[]{:S(2)}, u32[]{:S(2)}) collective-permute-start(bf16[2,2,2,24,768]{4,3,0,2,1:T(8,128)(2,1)S(1)} %maximum_select_fusion.7), channel_id=1, source_target_pairs={{0,4},{1,5},{2,6},{3,7},{4,0},{5,1},{6,2},{7,3},{8,12},{9,13},{10,... | collective-permute-start | bytes 884744 | tf_op jit(solution)/shard_map/ppermute | solution.py:339
  67.7 9.1 %collective-permute-start.3 = (bf16[2,2,2,24,896]{4,3,0,1,2:T(8,128)(2,1)S(1)}, bf16[2,2,2,24,896]{4,3,0,1,2:T(8,128)(2,1)S(1)}, u32[]{:S(2)}, u32[]{:S(2)}) collective-permute-start(bf16[2,2,2,24,896]{4,3,0,1,2:T(8,128)(2,1)S(1)} %maximum_select_fusion.5), channel_id=1, source_target_pairs={{0,1},{1,0},{2,3},{3,2},{4,5},{5,4},{6,7},{7,6},{8,9},{9,8},{10,11... | collective-permute-start | bytes 1032200 | tf_op jit(solution)/shard_map/ppermute | solution.py:339
  78.5 4.7 collective-permute-start.12
  78.7 11.5 %copy-start.53 = (f32[750]{0:T(1024)}, f32[750]{0:T(1024)S(1)}, u32[]{:S(2)}) copy-start(f32[750]{0:T(1024)S(1)} %broadcast_multiply_fusion.6) | copy-start | bytes 9004
  79.3 10.9 %copy-start.57 = (f32[750]{0:T(1024)}, f32[750]{0:T(1024)S(1)}, u32[]{:S(2)}) copy-start(f32[750]{0:T(1024)S(1)} %add_rsqrt_fusion.2) | copy-start | bytes 9004
  90.2 71.5 %copy-start.64 = (f32[768]{0:T(1024)}, f32[768]{0:T(1024)S(1)}, u32[]{:S(2)}) copy-start(f32[768]{0:T(1024)S(1)} %get-tuple-element.221) | copy-start | bytes 9220
  161.7 11.2 %copy-start.14 = (bf16[1,750,768]{2,1,0:T(8,128)(2,1)S(1)}, bf16[1,750,768]{2,1,0:T(8,128)(2,1)}, u32[]{:S(2)}) copy-start(bf16[1,750,768]{2,1,0:T(8,128)(2,1)} %param.15) | copy-start | bytes 3456004
  187.4 9.5 %copy-start.7 = (f32[750,768]{1,0:T(8,128)S(1)}, f32[750,768]{1,0:T(8,128)}, u32[]{:S(2)}) copy-start(f32[750,768]{1,0:T(8,128)} %copy-done.6) | copy-start | bytes 6912004
  187.4 9.5 %copy-start.65 = (f32[768]{0:T(1024)S(1)}, f32[768]{0:T(1024)}, u32[]{:S(2)}) copy-start(f32[768]{0:T(1024)} %copy-done.64) | copy-start | bytes 9220
  234.4 9.5 %collective-permute-start.14 = (bf16[2,2,2,2,24,6912]{5,4,0,3,2,1:T(8,128)(2,1)}, bf16[2,2,2,2,24,6912]{5,4,0,3,2,1:T(8,128)(2,1)}, u32[]{:S(2)}, u32[]{:S(2)}) collective-permute-start(bf16[2,2,2,2,24,6912]{5,4,0,3,2,1:T(8,128)(2,1)} %bitcast.317), channel_id=1, source_target_pairs={{0,2},{1,3},{2,0},{3,1},{4,6},{5,7},{6,4},{7,5},{8,10},{9,11},{10,... | collective-permute-start | bytes 15925256 | tf_op jit(solution)/shard_map/ppermute | solution.py:320
  257.3 45.2 %collective-permute-start.15 = (bf16[2,2,2,24,3456]{4,3,0,2,1:T(8,128)(2,1)}, bf16[2,2,2,24,3456]{4,3,0,2,1:T(8,128)(2,1)}, u32[]{:S(2)}, u32[]{:S(2)}) collective-permute-start(bf16[2,2,2,24,3456]{4,3,0,2,1:T(8,128)(2,1)} %fusion.42), channel_id=1, source_target_pairs={{0,4},{1,5},{2,6},{3,7},{4,0},{5,1},{6,2},{7,3},{8,12},{9,13},{10,... | collective-permute-start | bytes 3981320 | tf_op jit(solution)/shard_map/ppermute | solution.py:320
  277.7 11.9 %collective-permute-start.23 = (bf16[750,256]{1,0:T(8,128)(2,1)}, bf16[750,256]{1,0:T(8,128)(2,1)S(1)}, u32[]{:S(2)}, u32[]{:S(2)}) collective-permute-start(bf16[750,256]{1,0:T(8,128)(2,1)} %fusion.68), channel_id=1, source_target_pairs={{0,1},{1,0},{2,3},{3,2},{4,5},{5,4},{6,7},{7,6},{8,9},{9,8},{10,11... | collective-permute-start | bytes 1152008 | tf_op jit(solution)/shard_map/ppermute | solution.py:512
  282.9 31.4 %collective-permute-start.16 = (bf16[2,2,2,24,3456]{4,3,0,2,1:T(8,128)(2,1)}, bf16[2,2,2,24,3456]{4,3,0,2,1:T(8,128)(2,1)}, u32[]{:S(2)}, u32[]{:S(2)}) collective-permute-start(bf16[2,2,2,24,3456]{4,3,0,2,1:T(8,128)(2,1)} %fusion.43), channel_id=1, source_target_pairs={{0,8},{1,9},{2,10},{3,11},{4,12},{5,13},{6,14},{7,15},{8,0},{9,1},... | collective-permute-start | bytes 3981320 | tf_op jit(solution)/shard_map/ppermute | solution.py:320
  291.4 22.9 %slice-start.2 = ((s8[5308416]{0:T(1024)(128)(4,1)}), s8[4194304]{0:T(1024)(128)(4,1)S(1)}, s32[]{:S(2)}) async-start(s8[5308416]{0:T(1024)(128)(4,1)} %bitcast.320), calls=%async_computation.3 | async-start | bytes 8388608
  291.5 22.8 %slice-start.3 = ((s8[5308416]{0:T(1024)(128)(4,1)}), s8[1114112]{0:T(1024)(128)(4,1)S(1)}, s32[]{:S(2)}) async-start(s8[5308416]{0:T(1024)(128)(4,1)} %bitcast.320), calls=%async_computation.4 | async-start | bytes 2228224
  316.0 16.1 %collective-permute-start.18 = (bf16[2,2,24,3456]{3,2,0,1:T(8,128)(2,1)S(1)}, bf16[2,2,24,3456]{3,2,0,1:T(8,128)(2,1)S(1)}, u32[]{:S(2)}, u32[]{:S(2)}) collective-permute-start(bf16[2,2,24,3456]{3,2,0,1:T(8,128)(2,1)S(1)} %fusion.70), channel_id=1, source_target_pairs={{0,4},{1,5},{2,6},{3,7},{4,0},{5,1},{6,2},{7,3},{8,12},{9,13},{10,... | collective-permute-start | bytes 1990664 | tf_op jit(solution)/shard_map/ppermute | solution.py:320
  318.0 12.5 %collective-permute-start.24 = (bf16[750,256]{1,0:T(8,128)(2,1)S(1)}, bf16[750,256]{1,0:T(8,128)(2,1)S(1)}, u32[]{:S(2)}, u32[]{:S(2)}) collective-permute-start(bf16[750,256]{1,0:T(8,128)(2,1)S(1)} %slice.581), channel_id=1, source_target_pairs={{0,1},{1,0},{2,3},{3,2},{4,5},{5,4},{6,7},{7,6},{8,9},{9,8},{10,11... | collective-permute-start | bytes 1152008 | tf_op jit(solution)/shard_map/ppermute | solution.py:512
  318.4 15.6 %collective-permute-start.17 = (bf16[2,2,24,3456]{3,2,0,1:T(8,128)(2,1)S(1)}, bf16[2,2,24,3456]{3,2,0,1:T(8,128)(2,1)S(1)}, u32[]{:S(2)}, u32[]{:S(2)}) collective-permute-start(bf16[2,2,24,3456]{3,2,0,1:T(8,128)(2,1)S(1)} %fusion.69), channel_id=1, source_target_pairs={{0,8},{1,9},{2,10},{3,11},{4,12},{5,13},{6,14},{7,15},{8,0},{9,1},... | collective-permute-start | bytes 1990664 | tf_op jit(solution)/shard_map/ppermute | solution.py:320
  334.2 15.7 %collective-permute-start.20 = (bf16[2,24,3456]{2,1,0:T(8,128)(2,1)S(1)}, bf16[2,24,3456]{2,1,0:T(8,128)(2,1)S(1)}, u32[]{:S(2)}, u32[]{:S(2)}) collective-permute-start(bf16[2,24,3456]{2,1,0:T(8,128)(2,1)S(1)} %fusion.73), channel_id=1, source_target_pairs={{0,1},{1,0},{2,3},{3,2},{4,5},{5,4},{6,7},{7,6},{8,9},{9,8},{10,11... | collective-permute-start | bytes 995336 | tf_op jit(solution)/shard_map/ppermute | solution.py:320
  335.7 14.4 %collective-permute-start.19 = (bf16[2,24,3456]{2,1,0:T(8,128)(2,1)S(1)}, bf16[2,24,3456]{2,1,0:T(8,128)(2,1)S(1)}, u32[]{:S(2)}, u32[]{:S(2)}) collective-permute-start(bf16[2,24,3456]{2,1,0:T(8,128)(2,1)S(1)} %fusion.72), channel_id=1, source_target_pairs={{0,1},{1,0},{2,3},{3,2},{4,5},{5,4},{6,7},{7,6},{8,9},{9,8},{10,11... | collective-permute-start | bytes 995336 | tf_op jit(solution)/shard_map/ppermute | solution.py:320
  347.6 21.1 %collective-permute-start.25 = (bf16[750,256]{1,0:T(8,128)(2,1)S(1)}, bf16[750,256]{1,0:T(8,128)(2,1)S(1)}, u32[]{:S(2)}, u32[]{:S(2)}) collective-permute-start(bf16[750,256]{1,0:T(8,128)(2,1)S(1)} %slice.580), channel_id=1, source_target_pairs={{0,1},{1,0},{2,3},{3,2},{4,5},{5,4},{6,7},{7,6},{8,9},{9,8},{10,11... | collective-permute-start | bytes 1152008 | tf_op jit(solution)/shard_map/ppermute | solution.py:512
  350.3 19.2 %collective-permute-start.22 = (bf16[24,3456]{1,0:T(8,128)(2,1)S(1)}, bf16[24,3456]{1,0:T(8,128)(2,1)S(1)}, u32[]{:S(2)}, u32[]{:S(2)}) collective-permute-start(bf16[24,3456]{1,0:T(8,128)(2,1)S(1)} %fusion.89), channel_id=1, source_target_pairs={{0,16},{1,17},{2,18},{3,19},{4,20},{5,21},{6,22},{7,23},{8,24},{9,... | collective-permute-start | bytes 497672 | tf_op jit(solution)/shard_map/ppermute | solution.py:320
  350.4 19.2 %collective-permute-start.21 = (bf16[24,3456]{1,0:T(8,128)(2,1)S(1)}, bf16[24,3456]{1,0:T(8,128)(2,1)S(1)}, u32[]{:S(2)}, u32[]{:S(2)}) collective-permute-start(bf16[24,3456]{1,0:T(8,128)(2,1)S(1)} %fusion.88), channel_id=1, source_target_pairs={{0,16},{1,17},{2,18},{3,19},{4,20},{5,21},{6,22},{7,23},{8,24},{9,... | collective-permute-start | bytes 497672 | tf_op jit(solution)/shard_map/ppermute | solution.py:320
  366.7 24.8 %collective-permute-start.26 = (bf16[750,256]{1,0:T(8,128)(2,1)}, bf16[750,256]{1,0:T(8,128)(2,1)}, u32[]{:S(2)}, u32[]{:S(2)}) collective-permute-start(bf16[750,256]{1,0:T(8,128)(2,1)} %slice.579), channel_id=1, source_target_pairs={{0,1},{1,0},{2,3},{3,2},{4,5},{5,4},{6,7},{7,6},{8,9},{9,8},{10,11... | collective-permute-start | bytes 1152008 | tf_op jit(solution)/shard_map/ppermute | solution.py:512
  373.7 12.6 %copy-start.47 = (f32[24,768]{1,0:T(8,128)}, f32[24,768]{1,0:T(8,128)S(1)}, u32[]{:S(2)}) copy-start(f32[24,768]{1,0:T(8,128)S(1)} %get-tuple-element.231) | copy-start | bytes 221188
  386.5 14.8 %collective-permute-start.28 = (bf16[750,256]{1,0:T(8,128)(2,1)S(1)}, bf16[750,256]{1,0:T(8,128)(2,1)S(1)}, u32[]{:S(2)}, u32[]{:S(2)}) collective-permute-start(bf16[750,256]{1,0:T(8,128)(2,1)S(1)} %fusion.63), channel_id=1, source_target_pairs={{0,1},{1,0},{2,3},{3,2},{4,5},{5,4},{6,7},{7,6},{8,9},{9,8},{10,11... | collective-permute-start | bytes 1152008 | tf_op jit(solution)/shard_map/ppermute | solution.py:512
  389.4 11.8 %collective-permute-start.27 = (bf16[750,256]{1,0:T(8,128)(2,1)S(1)}, bf16[750,256]{1,0:T(8,128)(2,1)S(1)}, u32[]{:S(2)}, u32[]{:S(2)}) collective-permute-start(bf16[750,256]{1,0:T(8,128)(2,1)S(1)} %slice.578), channel_id=1, source_target_pairs={{0,1},{1,0},{2,3},{3,2},{4,5},{5,4},{6,7},{7,6},{8,9},{9,8},{10,11... | collective-permute-start | bytes 1152008 | tf_op jit(solution)/shard_map/ppermute | solution.py:512
  412.2 8.3 %copy-start.41 = (bf16[768,1]{1,0:T(8,128)(2,1)S(1)}, bf16[768,1]{1,0:T(8,128)(2,1)}, u32[]{:S(2)}) copy-start(bf16[768,1]{1,0:T(8,128)(2,1)} %stack.422) | copy-start | bytes 4612
  412.2 8.3 %copy-start.42 = (bf16[768,4]{1,0:T(8,128)(2,1)S(1)}, bf16[768,4]{1,0:T(8,128)(2,1)}, u32[]{:S(2)}) copy-start(bf16[768,4]{1,0:T(8,128)(2,1)} %reshape.1154) | copy-start | bytes 18436
  412.2 8.3 %copy-start.43 = (bf16[768,1]{1,0:T(8,128)(2,1)S(1)}, bf16[768,1]{1,0:T(8,128)(2,1)}, u32[]{:S(2)}) copy-start(bf16[768,1]{1,0:T(8,128)(2,1)} %stack.419) | copy-start | bytes 4612
  430.1 3.9 collective-permute-start.29
  434.7 9.1 %collective-permute-start.38 = (bf16[2,2,2,24,768]{4,3,2,1,0:T(8,128)(2,1)S(1)}, bf16[2,2,2,24,768]{4,3,2,1,0:T(8,128)(2,1)S(1)}, u32[]{:S(2)}, u32[]{:S(2)}) collective-permute-start(bf16[2,2,2,24,768]{4,3,2,1,0:T(8,128)(2,1)S(1)} %fusion.83), channel_id=1, source_target_pairs={{0,8},{1,9},{2,10},{3,11},{4,12},{5,13},{6,14},{7,15},{8,0},{9,1},... | collective-permute-start | bytes 884744 | tf_op jit(solution)/shard_map/ppermute | solution.py:320
  438.7 9.1 %collective-permute-start.34 = (bf16[2,2,2,24,768]{4,3,2,1,0:T(8,128)(2,1)S(1)}, bf16[2,2,2,24,768]{4,3,2,1,0:T(8,128)(2,1)S(1)}, u32[]{:S(2)}, u32[]{:S(2)}) collective-permute-start(bf16[2,2,2,24,768]{4,3,2,1,0:T(8,128)(2,1)S(1)} %fusion.82), channel_id=1, source_target_pairs={{0,4},{1,5},{2,6},{3,7},{4,0},{5,1},{6,2},{7,3},{8,12},{9,13},{10,... | collective-permute-start | bytes 884744 | tf_op jit(solution)/shard_map/ppermute | solution.py:320
  440.4 11.0 %collective-permute-start.30 = (bf16[2,2,2,24,896]{4,3,2,1,0:T(8,128)(2,1)S(1)}, bf16[2,2,2,24,896]{4,3,2,1,0:T(8,128)(2,1)S(1)}, u32[]{:S(2)}, u32[]{:S(2)}) collective-permute-start(bf16[2,2,2,24,896]{4,3,2,1,0:T(8,128)(2,1)S(1)} %fusion.71), channel_id=1, source_target_pairs={{0,1},{1,0},{2,3},{3,2},{4,5},{5,4},{6,7},{7,6},{8,9},{9,8},{10,11... | collective-permute-start | bytes 1032200 | tf_op jit(solution)/shard_map/ppermute | solution.py:320
  443.9 9.5 %collective-permute-start.39 = (bf16[2,2,24,768]{3,2,1,0:T(8,128)(2,1)S(1)}, bf16[2,2,24,768]{3,2,1,0:T(8,128)(2,1)S(1)}, u32[]{:S(2)}, u32[]{:S(2)}) collective-permute-start(bf16[2,2,24,768]{3,2,1,0:T(8,128)(2,1)S(1)} %fusion.91), channel_id=1, source_target_pairs={{0,1},{1,0},{2,3},{3,2},{4,5},{5,4},{6,7},{7,6},{8,9},{9,8},{10,11... | collective-permute-start | bytes 442376 | tf_op jit(solution)/shard_map/ppermute | solution.py:320
  447.9 6.1 %collective-permute-start.35 = (bf16[2,2,24,768]{3,2,1,0:T(8,128)(2,1)S(1)}, bf16[2,2,24,768]{3,2,1,0:T(8,128)(2,1)S(1)}, u32[]{:S(2)}, u32[]{:S(2)}) collective-permute-start(bf16[2,2,24,768]{3,2,1,0:T(8,128)(2,1)S(1)} %fusion.90), channel_id=1, source_target_pairs={{0,8},{1,9},{2,10},{3,11},{4,12},{5,13},{6,14},{7,15},{8,0},{9,1},... | collective-permute-start | bytes 442376 | tf_op jit(solution)/shard_map/ppermute | solution.py:320
  451.4 12.4 %copy-start.67 = (f32[2,96]{1,0:T(2,128)S(1)}, f32[2,96]{1,0:T(2,128)}, u32[]{:S(2)}) copy-start(f32[2,96]{1,0:T(2,128)} %param.26) | copy-start | bytes 2308
  451.4 12.4 %copy-start.70 = (f32[96]{0:T(128)S(1)}, f32[96]{0:T(128)}, u32[]{:S(2)}) copy-start(f32[96]{0:T(128)} %param.20) | copy-start | bytes 1156
  451.5 12.9 %copy-start.50 = (f32[24,8]{1,0:T(8,128)S(1)}, f32[24,8]{1,0:T(8,128)}, u32[]{:S(2)}) copy-start(f32[24,8]{1,0:T(8,128)} %copy.152) | copy-start | bytes 2308
  451.5 12.9 %copy-start.51 = (f32[1,24,8]{2,1,0:T(8,128)S(1)}, f32[1,24,8]{2,1,0:T(8,128)}, u32[]{:S(2)}) copy-start(f32[1,24,8]{2,1,0:T(8,128)} %copy.162) | copy-start | bytes 2308
  451.5 12.9 %copy-start.52 = (f32[1,24,8]{2,1,0:T(8,128)S(1)}, f32[1,24,8]{2,1,0:T(8,128)}, u32[]{:S(2)}) copy-start(f32[1,24,8]{2,1,0:T(8,128)} %copy.161) | copy-start | bytes 2308
  451.5 10.2 %collective-permute-start.31 = (bf16[2,2,24,896]{3,2,1,0:T(8,128)(2,1)S(1)}, bf16[2,2,24,896]{3,2,1,0:T(8,128)(2,1)S(1)}, u32[]{:S(2)}, u32[]{:S(2)}) collective-permute-start(bf16[2,2,24,896]{3,2,1,0:T(8,128)(2,1)S(1)} %fusion.87), channel_id=1, source_target_pairs={{0,4},{1,5},{2,6},{3,7},{4,0},{5,1},{6,2},{7,3},{8,12},{9,13},{10,... | collective-permute-start | bytes 516104 | tf_op jit(solution)/shard_map/ppermute | solution.py:320
  453.5 17.9 %copy-start.37 = (f32[2,24,2304]{2,1,0:T(8,128)S(1)}, f32[2,24,2304]{2,1,0:T(8,128)}, u32[]{:S(2)}) copy-start(f32[2,24,2304]{2,1,0:T(8,128)} %param.22) | copy-start | bytes 1327108
  453.5 5.1 %collective-permute-start.40 = (bf16[2,24,768]{2,1,0:T(8,128)(2,1)S(1)}, bf16[2,24,768]{2,1,0:T(8,128)(2,1)S(1)}, u32[]{:S(2)}, u32[]{:S(2)}) collective-permute-start(bf16[2,24,768]{2,1,0:T(8,128)(2,1)S(1)} %fusion.96), channel_id=1, source_target_pairs={{0,4},{1,5},{2,6},{3,7},{4,0},{5,1},{6,2},{7,3},{8,12},{9,13},{10,... | collective-permute-start | bytes 221192 | tf_op jit(solution)/shard_map/ppermute | solution.py:320
  454.0 17.4 %copy-start.40 = (f32[24,2304]{1,0:T(8,128)S(1)}, f32[24,2304]{1,0:T(8,128)}, u32[]{:S(2)}) copy-start(f32[24,2304]{1,0:T(8,128)} %param.16) | copy-start | bytes 663556
  454.1 5.0 %collective-permute-start.36 = (bf16[2,24,768]{2,1,0:T(8,128)(2,1)S(1)}, bf16[2,24,768]{2,1,0:T(8,128)(2,1)S(1)}, u32[]{:S(2)}, u32[]{:S(2)}) collective-permute-start(bf16[2,24,768]{2,1,0:T(8,128)(2,1)S(1)} %fusion.95), channel_id=1, source_target_pairs={{0,1},{1,0},{2,3},{3,2},{4,5},{5,4},{6,7},{7,6},{8,9},{9,8},{10,11... | collective-permute-start | bytes 221192 | tf_op jit(solution)/shard_map/ppermute | solution.py:320
  458.6 4.9 %collective-permute-start.41 = (bf16[24,768]{1,0:T(8,128)(2,1)S(1)}, bf16[24,768]{1,0:T(8,128)(2,1)S(1)}, u32[]{:S(2)}, u32[]{:S(2)}) collective-permute-start(bf16[24,768]{1,0:T(8,128)(2,1)S(1)} %fusion.102), channel_id=1, source_target_pairs={{0,16},{1,17},{2,18},{3,19},{4,20},{5,21},{6,22},{7,23},{8,24},{9,... | collective-permute-start | bytes 110600 | tf_op jit(solution)/shard_map/ppermute | solution.py:320
  459.1 5.6 %collective-permute-start.37 = (bf16[24,768]{1,0:T(8,128)(2,1)S(1)}, bf16[24,768]{1,0:T(8,128)(2,1)S(1)}, u32[]{:S(2)}, u32[]{:S(2)}) collective-permute-start(bf16[24,768]{1,0:T(8,128)(2,1)S(1)} %fusion.101), channel_id=1, source_target_pairs={{0,16},{1,17},{2,18},{3,19},{4,20},{5,21},{6,22},{7,23},{8,24},{9,... | collective-permute-start | bytes 110600 | tf_op jit(solution)/shard_map/ppermute | solution.py:320
  461.8 4.6 collective-permute-start.32
  463.7 9.4 %copy-start.69 = (f32[96]{0:T(128)}, f32[96]{0:T(128)S(1)}, u32[]{:S(2)}) copy-start(f32[96]{0:T(128)S(1)} %reshape.1157) | copy-start | bytes 1156
  466.4 5.0 %collective-permute-start.33 = (bf16[24,896]{1,0:T(8,128)(2,1)S(1)}, bf16[24,896]{1,0:T(8,128)(2,1)S(1)}, u32[]{:S(2)}, u32[]{:S(2)}) collective-permute-start(bf16[24,896]{1,0:T(8,128)(2,1)S(1)} %fusion.100), channel_id=1, source_target_pairs={{0,16},{1,17},{2,18},{3,19},{4,20},{5,21},{6,22},{7,23},{8,24},{9,... | collective-permute-start | bytes 129032 | tf_op jit(solution)/shard_map/ppermute | solution.py:320
  (56 other events, 183.1 us)
Sparse Core Ops, SparseCore 0:
  11.5 97.3 all-gather.1

commit v15 on v14

--- a/solution.py
+++ b/solution.py
@@ -557,15 +557,14 @@
         ],
         axis=1,
     ).astype(jnp.bfloat16)
-    owned_first = tree_reduce_scatter(
-        jnp.concatenate([grad_in_term, small_grads], axis=1),
-        (896, 768, 768),
-        rotated_orders,
-        (bit_count, core_bit),
+    owned_in = tree_reduce_scatter(
+        grad_in_term, (768, 768, 768), rotated_orders, (bit_count, core_bit)
     )[0]
-    owned_in = owned_first[:, :wide_in]
-    owned_vectors = owned_first[:, wide_in : wide_in + vectors.shape[1]]
-    owned_bias = owned_first[:, wide_in + vectors.shape[1] : wide_in + 12].reshape(-1)
+    owned_small = tree_reduce_scatter(
+        small_grads, (small_grads.shape[1],), rotated_orders[:1], (bit_count, core_bit)
+    )[0]
+    owned_vectors = owned_small[:, : vectors.shape[1]]
+    owned_bias = owned_small[:, vectors.shape[1] : 12].reshape(-1)
     owned_shrink = owned_late[:, :ff_width].reshape(shrink_weight.shape)
     owned_expand = owned_late[:, ff_width : 2 * ff_width]
     owned_out = owned_late[:, 2 * ff_width :]

time: 486 us -> 488 us (level)
  local copies, waits for them, and re-layouts: 95.3 us -> 89.5 us
    ppermute x22 -> x27, waiting for transfers between devices: 31.4 us -> 36.2 us  [tree_reduce_scatter(): got = lax.ppermute(send, ('clip', 'frame'), pairs)]
    ppermute x22 -> x27, starting transfers between devices: 21.2 us -> 24.3 us  [tree_reduce_scatter(): got = lax.ppermute(send, ('clip', 'frame'), pairs)]
    add x22 -> x27, other arithmetic: 10.4 us -> 12.9 us  [tree_reduce_scatter(): keep + got.astype(jnp.float32)]
    another operation x13 -> x11, other arithmetic: 10.3 us -> 9.51 us  [adam_step(): return (change, jnp.stack([first, second]))]
    unnamed x178 -> x166, local copies, waits for them, and re-layouts: 29 us -> 28.7 us
  transfers between devices with their start and end apart: 43 -> 48, of which waited for: 22 -> 26; matrix products, arithmetic and copies ran while one was open for 17% -> 19% of each run, Pallas kernels for 21% -> 21%
where the time goes in v15:
time: 488 us; the launch traced here: 483 us
  Pallas kernels  102 us (21%)
  local copies, waits for them, and re-layouts  89.5 us (18%)
  waiting for transfers between devices  86.6 us (18%)
  matrix products  71 us (15%)
  other arithmetic  64.7 us (13%)
  starting transfers between devices  52.5 us (11%)
  between operations  16.1 us (3%)
    pallas_call x6, Pallas kernels, attention_pallas(): pl.pallas_call(attention_backward_kernel, grid=(span,), in_specs=[qi_spec...  65 us
    ppermute x13, waiting for transfers between devices, double(): got = lax.ppermute(data, ('clip', 'frame'), pairs)  42 us
    pallas_call x1, Pallas kernels, attention_pallas(): pl.pallas_call(attention_forward_kernel, grid=(pair_count,), in_specs=[q_...  37.4 us
    ppermute x27, waiting for transfers between devices, tree_reduce_scatter(): got = lax.ppermute(send, ('clip', 'frame'), pairs)  36.2 us
    unnamed x166, local copies, waits for them, and re-layouts  28.7 us
    ppermute x27, starting transfers between devices, tree_reduce_scatter(): got = lax.ppermute(send, ('clip', 'frame'), pairs)  24.3 us
    ppermute x13, starting transfers between devices, double(): got = lax.ppermute(data, ('clip', 'frame'), pairs)  19.5 us
    add x27, other arithmetic, tree_reduce_scatter(): keep + got.astype(jnp.float32)  12.9 us
  transfers between devices with their start and end apart: 48, of which 26 were waited for; matrix products, arithmetic and copies ran while one was open for 19% of the time, Pallas kernels for 21%

profile of v15, /device:TPU:0, one launch (start us, length us, event | category | flops | bytes accessed | tf_op | source)
XLA Modules:
  0.0 482.9 jit_solution(10724942693975393497)
XLA Ops:
  12.8 4.1 collective-permute-start.8
  17.0 3.0 collective-permute-start
  25.5 29.5 %collective-permute-done.5 = bf16[2,24,768]{2,1,0:T(8,128)(2,1)S(1)} collective-permute-done((bf16[2,24,768]{2,1,0:T(8,128)(2,1)S(1)}, bf16[2,24,768]{2,1,0:T(8,128)(2,1)S(1)}, u32[]{:S(2)}, u32[]{:S(2)}) %collective-permute-start.5) | collective-permute-done | bytes 73760 | tf_op jit(solution)/shard_map/ppermute | solution.py:339
  60.1 1.8 collective-permute-done.10
  62.4 3.4 collective-permute-done.6
  69.4 3.2 collective-permute-done.7
  72.8 4.0 collective-permute-done.3
  76.8 1.7 fusion.129
  80.8 1.7 fusion.37
  83.2 3.1 maximum_select_fusion
  86.2 1.9 copy-done.14
  90.2 5.5 %add_convert_fusion = bf16[750,2304]{1,0:T(8,128)(2,1)S(1)} fusion(f32[2304]{0:T(1024)S(1)} %pad_maximum_fusion.16, bf16[768,2432]{1,0:T(8,128)(2,1)} %bitcast.347, bf16[1,750,768]{2,1,0:T(8,128)(2,1)S(1)} %copy-done.1, f32[768]{0:T(1024)S(1)} %get-tuple-element.186, f32[768]{0:T(1024)S(1)} %get-tuple-element.187, f32[750]{0:T(1024)S(1)} %add_rsqrt_fusion.2, ...), kind=kOutput, calls=%fused_computation.14 | convolution fusion | flops 2661120000 | bytes 8168304 | tf_op jit(solution)/shard_map/dot_general | solution.py:431
  99.1 3.5 add_convert_fusion.1
  102.6 2.7 fusion.8.k_ref.v_ref
  105.3 37.4 %shard_map.293 = (bf16[768,768]{1,0:T(8,128)(2,1)S(1)}, f32[768,768]{1,0:T(8,128)S(1)}) custom-call(bf16[768,768]{1,0:T(8,128)(2,1)S(1)} %pad.39.q_ref, bf16[1536,1536]{1,0:T(8,128)(2,1)} %fusion.8.k_ref.v_ref, bf16[1536,1536]{1,0:T(8,128)(2,1)} %fusion.8.k_ref.v_ref, f32[1,1536]{1,0:T(1,128)S(1)} %compare_select_fusion.kbias_ref), custom_call_target="tpu_custom_call" | custom-call | tf_op jit(solution)/shard_map/pallas_call | solution.py:161
  144.1 2.5 fusion.134
  148.4 4.8 slice.416
  153.2 8.5 %reshape.1317 = bf16[3072,768]{1,0:T(8,128)(2,1)} reshape(bf16[768,3072]{1,0:T(8,128)(2,1)} %slice.416) | data formatting | bytes 9437184 | tf_op jit(solution)/shard_map/reshape | solution.py:416
  161.7 9.1 %multiply_convert_fusion = (bf16[750,3072]{1,0:T(8,128)(2,1)S(1)}, f32[750,3072]{1,0:T(8,128)}) fusion(f32[3072]{0:T(1024)S(1)} %add.463, bf16[768,6912]{1,0:T(8,128)(2,1)} %all-gather.2.cloned.1.call-done, f32[750,768]{1,0:T(8,128)} %copy-done.5, f32[768]{0:T(1024)S(1)} %get-tuple-element.181, f32[768]{0:T(1024)S(1)} %get-tuple-element.182, ...), kind=kOutput, calls=%fused_computation.12 | convolution fusion | flops 3555648000 | bytes 20877168 | tf_op jit(solution)/shard_map/dot_general | solution.py:451
  170.7 2.2 copy-done.65
  172.9 6.0 %convolution_convert_fusion.2 = bf16[3072,768]{1,0:T(8,128)(2,1)} fusion(bf16[750,3072]{1,0:T(8,128)(2,1)S(1)} %get-tuple-element.242, bf16[1,750,768]{2,1,0:T(8,128)(2,1)S(1)} %copy-done.13), kind=kOutput, calls=%fused_computation.19 | convolution fusion | flops 3541303296 | bytes 10478592 | tf_op jit(solution)/shard_map/dot_general | solution.py:461
  178.9 8.5 %concatenate.354 = bf16[2,2,2,2,2,24,3072]{6,5,4,3,2,1,0:T(8,128)(2,1)} reshape(bf16[3072,768]{1,0:T(8,128)(2,1)} %convolution_convert_fusion.2) | data formatting | bytes 9437184 | tf_op jit(solution)/shard_map/concatenate | solution.py:481
  187.4 9.4 %fusion.135 = (bf16[3072]{0:T(1024)(128)(2,1)S(1)}, bf16[750,3072]{1,0:T(8,128)(2,1)S(1)}) fusion(f32[750,3072]{1,0:T(8,128)} %get-tuple-element.243, f32[3072]{0:T(1024)S(1)} %add.463, bf16[3072,768]{1,0:T(8,128)(2,1)} %reshape.1317, bf16[1,750,768]{2,1,0:T(8,128)(2,1)S(1)} %copy-done.13), kind=kOutput, calls=%fused_computation.352 | convolution fusion | flops 3566588928 | bytes 19713024 | tf_op jit(solution)/shard_map/dot_general | solution.py:465
  196.8 5.0 %convolution_convert_fusion.1 = bf16[768,3072]{1,0:T(8,128)(2,1)S(1)} fusion(bf16[750,3072]{1,0:T(8,128)(2,1)S(1)} %get-tuple-element.246, f32[750,768]{1,0:T(8,128)S(1)} %copy-done.6, f32[768]{0:T(1024)S(1)} %copy-done.59, f32[768]{0:T(1024)S(1)} %get-tuple-element.182, f32[750]{0:T(1024)S(1)} %add_rsqrt_fusion, f32[750]{0:T(1024)S(1)} %broadcast_multiply_fusion.4), kind=kOutput, calls=%fused_computation.18 | convolution fusion | flops 3544183296 | bytes 11642736 | tf_op jit(solution)/shard_map/dot_general | solution.py:467
  201.8 7.3 %multiply_reduce_fusion = (bf16[768]{0:T(1024)(128)(2,1)}, f32[750]{0:T(1024)S(1)}, f32[750]{0:T(1024)S(1)}, bf16[768]{0:T(1024)(128)(2,1)S(1)}, f32[750,768]{1,0:T(8,128)S(1)}) fusion(f32[750,768]{1,0:T(8,128)S(1)} %copy-done.6, f32[750]{0:T(1024)S(1)} %add_rsqrt_fusion, f32[750]{0:T(1024)S(1)} %broadcast_multiply_fusion.4, ...), kind=kOutput, calls=%fused_computation.64 | convolution fusion | flops 3544124928 | bytes 13952736 | tf_op jit(solution)/shard_map/dot_general | solution.py:471
  212.2 8.3 %pad_maximum_fusion = bf16[2,2,2,2,2,24,6912]{6,5,4,3,2,1,0:T(8,128)(2,1)} fusion(bf16[2,2,2,2,2,24,768]{6,5,4,3,2,1,0:T(8,128)(2,1)S(1)} %bitcast.352, bf16[2,2,2,2,2,24,3072]{6,5,4,3,2,1,0:T(8,128)(2,1)S(1)} %bitcast.345, bf16[2,2,2,2,2,24,3072]{6,5,4,3,2,1,0:T(8,128)(2,1)S(1)} %bitcast.342), kind=kLoop, calls=%fused_computation.1 | loop fusion | flops 31850496 | bytes 21233664 | tf_op jit(solution)/shard_map/concatenate | solution.py:481
  220.6 8.7 %constant_dynamic-slice_fusion.5 = (bf16[2,2,2,1,2,24,6912]{6,5,4,3,2,1,0:T(8,128)(2,1)}, bf16[2,2,2,1,2,24,6912]{6,5,4,3,2,1,0:T(8,128)(2,1)}) fusion(bf16[2,2,2,2,2,24,6912]{6,5,4,3,2,1,0:T(8,128)(2,1)} %pad_maximum_fusion, s32[]{:T(128)S(6)} %select_n.415, s32[]{:T(128)S(6)} %select_n.416), kind=kLoop, calls=%fused_computation.302 | loop fusion | bytes 21233672 | tf_op jit(solution)/shard_map/jit(dynamic_index_in_dim)/dynamic_slice | solution.py:313
  229.3 5.2 %copy.175 = bf16[2,2,2,1,2,24,6912]{6,5,0,4,2,1,3:T(8,128)(2,1)} copy(bf16[2,2,2,1,2,24,6912]{6,5,4,3,2,1,0:T(8,128)(2,1)} %get-tuple-element.199) | data formatting | bytes 10616832
  238.5 3.1 convolution_convert_fusion.4
  241.5 2.4 collective-permute-done.14
  243.9 5.3 %convert_add_fusion = f32[2,2,2,2,24,6912]{5,4,0,3,2,1:T(8,128)S(1)} fusion(bf16[2,2,2,2,24,6912]{5,4,0,3,2,1:T(8,128)(2,1)} %collective-permute-done.14, bf16[2,2,2,1,2,24,6912]{6,5,4,3,2,1,0:T(8,128)(2,1)} %get-tuple-element.198), kind=kLoop, calls=%fused_computation.2 | loop fusion | flops 7962624 | bytes 21233664 | tf_op jit(solution)/shard_map/add | solution.py:321
  249.3 4.9 %fusion.130 = (f32[2,2,2,2,24,3456]{5,4,0,3,2,1:T(8,128)}, f32[2,2,2,2,24,3456]{5,4,0,3,2,1:T(8,128)}) fusion(f32[2,2,2,2,24,6912]{5,4,0,3,2,1:T(8,128)S(1)} %convert_add_fusion), kind=kLoop, calls=%fused_computation.347 | loop fusion | bytes 21233664 | tf_op jit(solution)/shard_map/slice | solution.py:307
  254.2 3.1 fusion.42
  257.3 8.5 %fusion.41 = bf16[1,750,768]{2,1,0:T(8,128)(2,1)} fusion(f32[750,768]{1,0:T(8,128)S(1)} %copy-done.7, bf16[750,3072]{1,0:T(8,128)(2,1)} %copy-done.65, bf16[3072,768]{1,0:T(8,128)(2,1)} %reshape.1317, f32[768]{0:T(1024)S(1)} %copy-done.57), kind=kOutput, calls=%fused_computation.83 | convolution fusion | flops 3540672000 | bytes 12785664 | tf_op jit(solution)/shard_map/dot_general | solution.py:455
  265.8 10.8 %shard_map.294 = (f32[768,128]{1,0:T(8,128)S(1)}, f32[1536,128]{1,0:T(8,128)S(1)}, f32[1536,128]{1,0:T(8,128)S(1)}) custom-call(bf16[768,768]{1,0:T(8,128)(2,1)S(1)} %pad.39.q_ref, bf16[1536,1536]{1,0:T(8,128)(2,1)} %fusion.8.k_ref.v_ref, bf16[1536,1536]{1,0:T(8,128)(2,1)} %fusion.8.k_ref.v_ref, bf16[768,768]{1,0:T(8,128)(2,1)S(1)} %pad.41.do_ref, ...), custom_call_target="tpu_custom_call" | custom-call | tf_op jit(solution)/shard_map/pallas_call | solution.py:180
  277.7 2.2 collective-permute-start.23
  279.9 3.0 fusion.43
  287.9 1.7 collective-permute-done.23
  289.6 1.8 fusion.62
  291.5 10.8 %shard_map.295 = (f32[768,128]{1,0:T(8,128)S(1)}, f32[1536,128]{1,0:T(8,128)S(1)}, f32[1536,128]{1,0:T(8,128)S(1)}) custom-call(bf16[768,768]{1,0:T(8,128)(2,1)S(1)} %pad.39.q_ref, bf16[1536,1536]{1,0:T(8,128)(2,1)} %fusion.8.k_ref.v_ref, bf16[1536,1536]{1,0:T(8,128)(2,1)} %fusion.8.k_ref.v_ref, bf16[768,768]{1,0:T(8,128)(2,1)S(1)} %pad.42.do_ref, ...), custom_call_target="tpu_custom_call" | custom-call | tf_op jit(solution)/shard_map/pallas_call | solution.py:180
  302.5 2.4 bitcast_add_fusion.1
  304.8 9.5 %collective-permute-done.16 = bf16[2,2,2,24,3456]{4,3,0,2,1:T(8,128)(2,1)} collective-permute-done((bf16[2,2,2,24,3456]{4,3,0,2,1:T(8,128)(2,1)}, bf16[2,2,2,24,3456]{4,3,0,2,1:T(8,128)(2,1)}, u32[]{:S(2)}, u32[]{:S(2)}) %collective-permute-start.16) | collective-permute-done | bytes 1327136 | tf_op jit(solution)/shard_map/ppermute | solution.py:320
  316.0 1.8 collective-permute-start.18
  318.9 10.9 %shard_map.296 = (f32[768,128]{1,0:T(8,128)S(1)}, f32[1536,128]{1,0:T(8,128)S(1)}, f32[1536,128]{1,0:T(8,128)S(1)}) custom-call(bf16[768,768]{1,0:T(8,128)(2,1)S(1)} %pad.39.q_ref, bf16[1536,1536]{1,0:T(8,128)(2,1)} %fusion.8.k_ref.v_ref, bf16[1536,1536]{1,0:T(8,128)(2,1)} %fusion.8.k_ref.v_ref, bf16[768,768]{1,0:T(8,128)(2,1)S(1)} %pad.43.do_ref, ...), custom_call_target="tpu_custom_call" | custom-call | tf_op jit(solution)/shard_map/pallas_call | solution.py:180
  332.2 1.8 collective-permute-done.17
  336.4 10.7 %shard_map.297 = (f32[768,128]{1,0:T(8,128)S(1)}, f32[1536,128]{1,0:T(8,128)S(1)}, f32[1536,128]{1,0:T(8,128)S(1)}) custom-call(bf16[768,768]{1,0:T(8,128)(2,1)S(1)} %pad.39.q_ref, bf16[1536,1536]{1,0:T(8,128)(2,1)} %fusion.8.k_ref.v_ref, bf16[1536,1536]{1,0:T(8,128)(2,1)} %fusion.8.k_ref.v_ref, bf16[768,768]{1,0:T(8,128)(2,1)S(1)} %pad.44.do_ref, ...), custom_call_target="tpu_custom_call" | custom-call | tf_op jit(solution)/shard_map/pallas_call | solution.py:180
  350.6 2.9 collective-permute-start.21
  353.6 10.7 %shard_map.298 = (f32[768,128]{1,0:T(8,128)S(1)}, f32[1536,128]{1,0:T(8,128)S(1)}, f32[1536,128]{1,0:T(8,128)S(1)}) custom-call(bf16[768,768]{1,0:T(8,128)(2,1)S(1)} %pad.39.q_ref, bf16[1536,1536]{1,0:T(8,128)(2,1)} %fusion.8.k_ref.v_ref, bf16[1536,1536]{1,0:T(8,128)(2,1)} %fusion.8.k_ref.v_ref, bf16[768,768]{1,0:T(8,128)(2,1)S(1)} %pad.45.do_ref, ...), custom_call_target="tpu_custom_call" | custom-call | tf_op jit(solution)/shard_map/pallas_call | solution.py:180
  375.1 2.2 fusion.85
  378.4 11.1 %shard_map.299 = (f32[768,128]{1,0:T(8,128)S(1)}, f32[1536,128]{1,0:T(8,128)S(1)}, f32[1536,128]{1,0:T(8,128)S(1)}) custom-call(bf16[768,768]{1,0:T(8,128)(2,1)S(1)} %pad.39.q_ref, bf16[1536,1536]{1,0:T(8,128)(2,1)} %fusion.8.k_ref.v_ref, bf16[1536,1536]{1,0:T(8,128)(2,1)} %fusion.8.k_ref.v_ref, bf16[768,768]{1,0:T(8,128)(2,1)S(1)} %pad.46.do_ref, ...), custom_call_target="tpu_custom_call" | custom-call | tf_op jit(solution)/shard_map/pallas_call | solution.py:180
  397.2 6.7 %collective-permute-done.27 = bf16[750,256]{1,0:T(8,128)(2,1)S(1)} collective-permute-done((bf16[750,256]{1,0:T(8,128)(2,1)S(1)}, bf16[750,256]{1,0:T(8,128)(2,1)S(1)}, u32[]{:S(2)}, u32[]{:S(2)}) %collective-permute-start.27) | collective-permute-done | bytes 384032 | tf_op jit(solution)/shard_map/ppermute | solution.py:512
  404.6 1.8 copy-done.12
  407.7 4.6 fusion.32
  412.4 2.6 reduce.2
  417.5 5.5 %convolution_convert_fusion = bf16[768,2304]{1,0:T(8,128)(2,1)S(1)} fusion(bf16[750,2304]{1,0:T(8,128)(2,1)} %copy-done.12, bf16[1,750,768]{2,1,0:T(8,128)(2,1)S(1)} %copy-done.2, f32[768]{0:T(1024)S(1)} %copy-done.56, f32[768]{0:T(1024)S(1)} %copy-done.50, f32[750]{0:T(1024)S(1)} %copy-done.52, f32[750]{0:T(1024)S(1)} %copy-done.48), kind=kOutput, calls=%fused_computation.17 | convolution fusion | flops 2659433472 | bytes 8159088 | tf_op jit(solution)/shard_map/dot_general | solution.py:528
  424.5 2.8 collective-permute-done.43
  432.2 2.8 collective-permute-done.45
  435.5 2.0 fusion.46
  437.5 2.1 collective-permute-done.46
  441.8 1.9 convert_add_fusion.1
  453.9 2.6 collective-permute-done.38
  462.8 1.8 collective-permute-done.31
  466.3 2.5 collective-permute-start.41
  472.0 2.1 collective-permute-done.33
  (435 shorter events, 111.8 us)
Async XLA Ops:
  7.2 12.8 %copy-start.1 = (bf16[1,750,768]{2,1,0:T(8,128)(2,1)S(1)}, bf16[1,750,768]{2,1,0:T(8,128)(2,1)}, u32[]{:S(2)}) copy-start(bf16[1,750,768]{2,1,0:T(8,128)(2,1)} %param.14) | copy-start | bytes 3456004
  7.2 136.9 %all-gather.2.cloned.1.call-start = ((), (), s32[]{:S(2)}) async-start(), calls=%async_computation | async-start | bytes 10948608 | tf_op jit(solution)/shard_map/all_gather | solution.py:409
  12.8 8.7 %collective-permute-start.8 = (bf16[24,768]{1,0:T(8,128)(2,1)S(1)}, bf16[24,768]{1,0:T(8,128)(2,1)S(1)}, u32[]{:S(2)}, u32[]{:S(2)}) collective-permute-start(bf16[24,768]{1,0:T(8,128)(2,1)S(1)} %get-tuple-element.222), channel_id=1, source_target_pairs={{0,16},{1,17},{2,18},{3,19},{4,20},{5,21},{6,22},{7,23},{8,24},{9,... | collective-permute-start | bytes 110600 | tf_op jit(solution)/shard_map/ppermute | solution.py:339
  16.9 6.2 %collective-permute-start.4 = (bf16[24,768]{1,0:T(8,128)(2,1)S(1)}, bf16[24,768]{1,0:T(8,128)(2,1)S(1)}, u32[]{:S(2)}, u32[]{:S(2)}) collective-permute-start(bf16[24,768]{1,0:T(8,128)(2,1)S(1)} %get-tuple-element.228), channel_id=1, source_target_pairs={{0,16},{1,17},{2,18},{3,19},{4,20},{5,21},{6,22},{7,23},{8,24},{9,... | collective-permute-start | bytes 110600 | tf_op jit(solution)/shard_map/ppermute | solution.py:339
  17.0 6.9 %collective-permute-start = (bf16[24,896]{1,0:T(8,128)(2,1)S(1)}, bf16[24,896]{1,0:T(8,128)(2,1)S(1)}, u32[]{:S(2)}, u32[]{:S(2)}) collective-permute-start(bf16[24,896]{1,0:T(8,128)(2,1)S(1)} %get-tuple-element.225), channel_id=1, source_target_pairs={{0,16},{1,17},{2,18},{3,19},{4,20},{5,21},{6,22},{7,23},{8,24},{9,... | collective-permute-start | bytes 129032 | tf_op jit(solution)/shard_map/ppermute | solution.py:339
  20.0 59.3 %collective-permute-start.13 = (bf16[1,750,768]{2,1,0:T(8,128)(2,1)S(1)}, bf16[1,750,768]{2,1,0:T(8,128)(2,1)}, u32[]{:S(2)}, u32[]{:S(2)}) collective-permute-start(bf16[1,750,768]{2,1,0:T(8,128)(2,1)S(1)} %copy-done.1), channel_id=1, source_target_pairs={{0,1},{1,0},{2,3},{3,2},{4,5},{5,4},{6,7},{7,6},{8,9},{9,8},{10,11... | collective-permute-start | bytes 3456008 | tf_op jit(solution)/shard_map/ppermute | solution.py:423
  21.6 35.1 %collective-permute-start.9 = (bf16[2,24,768]{2,1,0:T(8,128)(2,1)S(1)}, bf16[2,24,768]{2,1,0:T(8,128)(2,1)S(1)}, u32[]{:S(2)}, u32[]{:S(2)}) collective-permute-start(bf16[2,24,768]{2,1,0:T(8,128)(2,1)S(1)} %maximum_select_fusion.18), channel_id=1, source_target_pairs={{0,4},{1,5},{2,6},{3,7},{4,0},{5,1},{6,2},{7,3},{8,12},{9,13},{10,... | collective-permute-start | bytes 221192 | tf_op jit(solution)/shard_map/ppermute | solution.py:339
  23.2 31.8 %collective-permute-start.5 = (bf16[2,24,768]{2,1,0:T(8,128)(2,1)S(1)}, bf16[2,24,768]{2,1,0:T(8,128)(2,1)S(1)}, u32[]{:S(2)}, u32[]{:S(2)}) collective-permute-start(bf16[2,24,768]{2,1,0:T(8,128)(2,1)S(1)} %maximum_select_fusion.17), channel_id=1, source_target_pairs={{0,1},{1,0},{2,3},{3,2},{4,5},{5,4},{6,7},{7,6},{8,9},{9,8},{10,11... | collective-permute-start | bytes 221192 | tf_op jit(solution)/shard_map/ppermute | solution.py:339
  23.9 34.4 %collective-permute-start.1 = (bf16[2,24,896]{2,1,0:T(8,128)(2,1)S(1)}, bf16[2,24,896]{2,1,0:T(8,128)(2,1)S(1)}, u32[]{:S(2)}, u32[]{:S(2)}) collective-permute-start(bf16[2,24,896]{2,1,0:T(8,128)(2,1)S(1)} %maximum_select_fusion.15), channel_id=1, source_target_pairs={{0,8},{1,9},{2,10},{3,11},{4,12},{5,13},{6,14},{7,15},{8,0},{9,1},... | collective-permute-start | bytes 258056 | tf_op jit(solution)/shard_map/ppermute | solution.py:339
  55.0 10.8 %collective-permute-start.6 = (bf16[2,2,24,768]{3,2,0,1:T(8,128)(2,1)S(1)}, bf16[2,2,24,768]{3,2,0,1:T(8,128)(2,1)S(1)}, u32[]{:S(2)}, u32[]{:S(2)}) collective-permute-start(bf16[2,2,24,768]{3,2,0,1:T(8,128)(2,1)S(1)} %maximum_select_fusion.12), channel_id=1, source_target_pairs={{0,8},{1,9},{2,10},{3,11},{4,12},{5,13},{6,14},{7,15},{8,0},{9,1},... | collective-permute-start | bytes 442376 | tf_op jit(solution)/shard_map/ppermute | solution.py:339
  56.7 5.2 %collective-permute-start.10 = (bf16[2,2,24,768]{3,2,1,0:T(8,128)(2,1)S(1)}, bf16[2,2,24,768]{3,2,1,0:T(8,128)(2,1)S(1)}, u32[]{:S(2)}, u32[]{:S(2)}) collective-permute-start(bf16[2,2,24,768]{3,2,1,0:T(8,128)(2,1)S(1)} %maximum_select_fusion.13), channel_id=1, source_target_pairs={{0,1},{1,0},{2,3},{3,2},{4,5},{5,4},{6,7},{7,6},{8,9},{9,8},{10,11... | collective-permute-start | bytes 442376 | tf_op jit(solution)/shard_map/ppermute | solution.py:339
  58.5 9.1 %collective-permute-start.2 = (bf16[2,2,24,896]{3,2,0,1:T(8,128)(2,1)S(1)}, bf16[2,2,24,896]{3,2,0,1:T(8,128)(2,1)S(1)}, u32[]{:S(2)}, u32[]{:S(2)}) collective-permute-start(bf16[2,2,24,896]{3,2,0,1:T(8,128)(2,1)S(1)} %maximum_select_fusion.10), channel_id=1, source_target_pairs={{0,4},{1,5},{2,6},{3,7},{4,0},{5,1},{6,2},{7,3},{8,12},{9,13},{10,... | collective-permute-start | bytes 516104 | tf_op jit(solution)/shard_map/ppermute | solution.py:339
  61.9 10.8 %collective-permute-start.11 = (bf16[2,2,2,24,768]{4,3,2,1,0:T(8,128)(2,1)S(1)}, bf16[2,2,2,24,768]{4,3,2,1,0:T(8,128)(2,1)S(1)}, u32[]{:S(2)}, u32[]{:S(2)}) collective-permute-start(bf16[2,2,2,24,768]{4,3,2,1,0:T(8,128)(2,1)S(1)} %maximum_select_fusion.8), channel_id=1, source_target_pairs={{0,8},{1,9},{2,10},{3,11},{4,12},{5,13},{6,14},{7,15},{8,0},{9,1},... | collective-permute-start | bytes 884744 | tf_op jit(solution)/shard_map/ppermute | solution.py:339
  65.9 6.8 %collective-permute-start.7 = (bf16[2,2,2,24,768]{4,3,0,2,1:T(8,128)(2,1)S(1)}, bf16[2,2,2,24,768]{4,3,0,2,1:T(8,128)(2,1)S(1)}, u32[]{:S(2)}, u32[]{:S(2)}) collective-permute-start(bf16[2,2,2,24,768]{4,3,0,2,1:T(8,128)(2,1)S(1)} %maximum_select_fusion.7), channel_id=1, source_target_pairs={{0,4},{1,5},{2,6},{3,7},{4,0},{5,1},{6,2},{7,3},{8,12},{9,13},{10,... | collective-permute-start | bytes 884744 | tf_op jit(solution)/shard_map/ppermute | solution.py:339
  67.7 9.1 %collective-permute-start.3 = (bf16[2,2,2,24,896]{4,3,0,1,2:T(8,128)(2,1)S(1)}, bf16[2,2,2,24,896]{4,3,0,1,2:T(8,128)(2,1)S(1)}, u32[]{:S(2)}, u32[]{:S(2)}) collective-permute-start(bf16[2,2,2,24,896]{4,3,0,1,2:T(8,128)(2,1)S(1)} %maximum_select_fusion.5), channel_id=1, source_target_pairs={{0,1},{1,0},{2,3},{3,2},{4,5},{5,4},{6,7},{7,6},{8,9},{9,8},{10,11... | collective-permute-start | bytes 1032200 | tf_op jit(solution)/shard_map/ppermute | solution.py:339
  78.5 4.7 collective-permute-start.12
  78.7 11.5 %copy-start.47 = (f32[750]{0:T(1024)}, f32[750]{0:T(1024)S(1)}, u32[]{:S(2)}) copy-start(f32[750]{0:T(1024)S(1)} %broadcast_multiply_fusion.6) | copy-start | bytes 9004
  79.3 10.9 %copy-start.51 = (f32[750]{0:T(1024)}, f32[750]{0:T(1024)S(1)}, u32[]{:S(2)}) copy-start(f32[750]{0:T(1024)S(1)} %add_rsqrt_fusion.2) | copy-start | bytes 9004
  90.1 7.5 %copy-start.49 = (f32[768]{0:T(1024)}, f32[768]{0:T(1024)S(1)}, u32[]{:S(2)}) copy-start(f32[768]{0:T(1024)S(1)} %get-tuple-element.187) | copy-start | bytes 9220
  90.1 7.5 %copy-start.55 = (f32[768]{0:T(1024)}, f32[768]{0:T(1024)S(1)}, u32[]{:S(2)}) copy-start(f32[768]{0:T(1024)S(1)} %get-tuple-element.186) | copy-start | bytes 9220
  90.2 71.5 %copy-start.58 = (f32[768]{0:T(1024)}, f32[768]{0:T(1024)S(1)}, u32[]{:S(2)}) copy-start(f32[768]{0:T(1024)S(1)} %get-tuple-element.181) | copy-start | bytes 9220
  161.7 11.2 %copy-start.13 = (bf16[1,750,768]{2,1,0:T(8,128)(2,1)S(1)}, bf16[1,750,768]{2,1,0:T(8,128)(2,1)}, u32[]{:S(2)}) copy-start(bf16[1,750,768]{2,1,0:T(8,128)(2,1)} %param.15) | copy-start | bytes 3456004
  187.4 9.5 %copy-start.6 = (f32[750,768]{1,0:T(8,128)S(1)}, f32[750,768]{1,0:T(8,128)}, u32[]{:S(2)}) copy-start(f32[750,768]{1,0:T(8,128)} %copy-done.5) | copy-start | bytes 6912004
  187.4 9.5 %copy-start.59 = (f32[768]{0:T(1024)S(1)}, f32[768]{0:T(1024)}, u32[]{:S(2)}) copy-start(f32[768]{0:T(1024)} %copy-done.58) | copy-start | bytes 9220
  234.4 9.5 %collective-permute-start.14 = (bf16[2,2,2,2,24,6912]{5,4,0,3,2,1:T(8,128)(2,1)}, bf16[2,2,2,2,24,6912]{5,4,0,3,2,1:T(8,128)(2,1)}, u32[]{:S(2)}, u32[]{:S(2)}) collective-permute-start(bf16[2,2,2,2,24,6912]{5,4,0,3,2,1:T(8,128)(2,1)} %bitcast.339), channel_id=1, source_target_pairs={{0,2},{1,3},{2,0},{3,1},{4,6},{5,7},{6,4},{7,5},{8,10},{9,11},{10,... | collective-permute-start | bytes 15925256 | tf_op jit(solution)/shard_map/ppermute | solution.py:320
  257.2 45.2 %collective-permute-start.15 = (bf16[2,2,2,24,3456]{4,3,0,2,1:T(8,128)(2,1)}, bf16[2,2,2,24,3456]{4,3,0,2,1:T(8,128)(2,1)}, u32[]{:S(2)}, u32[]{:S(2)}) collective-permute-start(bf16[2,2,2,24,3456]{4,3,0,2,1:T(8,128)(2,1)} %fusion.42), channel_id=1, source_target_pairs={{0,4},{1,5},{2,6},{3,7},{4,0},{5,1},{6,2},{7,3},{8,12},{9,13},{10,... | collective-permute-start | bytes 3981320 | tf_op jit(solution)/shard_map/ppermute | solution.py:320
  277.7 8.2 %copy-start.62 = (bf16[768]{0:T(1024)(128)(2,1)S(1)}, bf16[768]{0:T(1024)(128)(2,1)}, u32[]{:S(2)}) copy-start(bf16[768]{0:T(1024)(128)(2,1)} %get-tuple-element.172) | copy-start | bytes 4612
  277.7 11.9 %collective-permute-start.23 = (bf16[750,256]{1,0:T(8,128)(2,1)}, bf16[750,256]{1,0:T(8,128)(2,1)S(1)}, u32[]{:S(2)}, u32[]{:S(2)}) collective-permute-start(bf16[750,256]{1,0:T(8,128)(2,1)} %fusion.68), channel_id=1, source_target_pairs={{0,1},{1,0},{2,3},{3,2},{4,5},{5,4},{6,7},{7,6},{8,9},{9,8},{10,11... | collective-permute-start | bytes 1152008 | tf_op jit(solution)/shard_map/ppermute | solution.py:512
  282.9 31.4 %collective-permute-start.16 = (bf16[2,2,2,24,3456]{4,3,0,2,1:T(8,128)(2,1)}, bf16[2,2,2,24,3456]{4,3,0,2,1:T(8,128)(2,1)}, u32[]{:S(2)}, u32[]{:S(2)}) collective-permute-start(bf16[2,2,2,24,3456]{4,3,0,2,1:T(8,128)(2,1)} %fusion.43), channel_id=1, source_target_pairs={{0,8},{1,9},{2,10},{3,11},{4,12},{5,13},{6,14},{7,15},{8,0},{9,1},... | collective-permute-start | bytes 3981320 | tf_op jit(solution)/shard_map/ppermute | solution.py:320
  291.4 22.9 %slice-start.2 = ((s8[5308416]{0:T(1024)(128)(4,1)}), s8[4194304]{0:T(1024)(128)(4,1)S(1)}, s32[]{:S(2)}) async-start(s8[5308416]{0:T(1024)(128)(4,1)} %bitcast.343), calls=%async_computation.3 | async-start | bytes 8388608
  291.5 22.8 %slice-start.3 = ((s8[5308416]{0:T(1024)(128)(4,1)}), s8[1114112]{0:T(1024)(128)(4,1)S(1)}, s32[]{:S(2)}) async-start(s8[5308416]{0:T(1024)(128)(4,1)} %bitcast.343), calls=%async_computation.4 | async-start | bytes 2228224
  316.0 16.1 %collective-permute-start.18 = (bf16[2,2,24,3456]{3,2,0,1:T(8,128)(2,1)S(1)}, bf16[2,2,24,3456]{3,2,0,1:T(8,128)(2,1)S(1)}, u32[]{:S(2)}, u32[]{:S(2)}) collective-permute-start(bf16[2,2,24,3456]{3,2,0,1:T(8,128)(2,1)S(1)} %fusion.70), channel_id=1, source_target_pairs={{0,4},{1,5},{2,6},{3,7},{4,0},{5,1},{6,2},{7,3},{8,12},{9,13},{10,... | collective-permute-start | bytes 1990664 | tf_op jit(solution)/shard_map/ppermute | solution.py:320
  318.0 12.7 %collective-permute-start.24 = (bf16[750,256]{1,0:T(8,128)(2,1)S(1)}, bf16[750,256]{1,0:T(8,128)(2,1)S(1)}, u32[]{:S(2)}, u32[]{:S(2)}) collective-permute-start(bf16[750,256]{1,0:T(8,128)(2,1)S(1)} %slice.589), channel_id=1, source_target_pairs={{0,1},{1,0},{2,3},{3,2},{4,5},{5,4},{6,7},{7,6},{8,9},{9,8},{10,11... | collective-permute-start | bytes 1152008 | tf_op jit(solution)/shard_map/ppermute | solution.py:512
  318.4 15.6 %collective-permute-start.17 = (bf16[2,2,24,3456]{3,2,0,1:T(8,128)(2,1)S(1)}, bf16[2,2,24,3456]{3,2,0,1:T(8,128)(2,1)S(1)}, u32[]{:S(2)}, u32[]{:S(2)}) collective-permute-start(bf16[2,2,24,3456]{3,2,0,1:T(8,128)(2,1)S(1)} %fusion.69), channel_id=1, source_target_pairs={{0,8},{1,9},{2,10},{3,11},{4,12},{5,13},{6,14},{7,15},{8,0},{9,1},... | collective-permute-start | bytes 1990664 | tf_op jit(solution)/shard_map/ppermute | solution.py:320
  334.2 15.5 %collective-permute-start.20 = (bf16[2,24,3456]{2,1,0:T(8,128)(2,1)S(1)}, bf16[2,24,3456]{2,1,0:T(8,128)(2,1)S(1)}, u32[]{:S(2)}, u32[]{:S(2)}) collective-permute-start(bf16[2,24,3456]{2,1,0:T(8,128)(2,1)S(1)} %fusion.72), channel_id=1, source_target_pairs={{0,1},{1,0},{2,3},{3,2},{4,5},{5,4},{6,7},{7,6},{8,9},{9,8},{10,11... | collective-permute-start | bytes 995336 | tf_op jit(solution)/shard_map/ppermute | solution.py:320
  335.7 14.7 %collective-permute-start.19 = (bf16[2,24,3456]{2,1,0:T(8,128)(2,1)S(1)}, bf16[2,24,3456]{2,1,0:T(8,128)(2,1)S(1)}, u32[]{:S(2)}, u32[]{:S(2)}) collective-permute-start(bf16[2,24,3456]{2,1,0:T(8,128)(2,1)S(1)} %fusion.71), channel_id=1, source_target_pairs={{0,1},{1,0},{2,3},{3,2},{4,5},{5,4},{6,7},{7,6},{8,9},{9,8},{10,11... | collective-permute-start | bytes 995336 | tf_op jit(solution)/shard_map/ppermute | solution.py:320
  347.4 21.5 %collective-permute-start.25 = (bf16[750,256]{1,0:T(8,128)(2,1)S(1)}, bf16[750,256]{1,0:T(8,128)(2,1)S(1)}, u32[]{:S(2)}, u32[]{:S(2)}) collective-permute-start(bf16[750,256]{1,0:T(8,128)(2,1)S(1)} %slice.588), channel_id=1, source_target_pairs={{0,1},{1,0},{2,3},{3,2},{4,5},{5,4},{6,7},{7,6},{8,9},{9,8},{10,11... | collective-permute-start | bytes 1152008 | tf_op jit(solution)/shard_map/ppermute | solution.py:512
  350.5 19.3 %collective-permute-start.22 = (bf16[24,3456]{1,0:T(8,128)(2,1)S(1)}, bf16[24,3456]{1,0:T(8,128)(2,1)S(1)}, u32[]{:S(2)}, u32[]{:S(2)}) collective-permute-start(bf16[24,3456]{1,0:T(8,128)(2,1)S(1)} %fusion.96), channel_id=1, source_target_pairs={{0,16},{1,17},{2,18},{3,19},{4,20},{5,21},{6,22},{7,23},{8,24},{9,... | collective-permute-start | bytes 497672 | tf_op jit(solution)/shard_map/ppermute | solution.py:320
  350.6 19.3 %collective-permute-start.21 = (bf16[24,3456]{1,0:T(8,128)(2,1)S(1)}, bf16[24,3456]{1,0:T(8,128)(2,1)S(1)}, u32[]{:S(2)}, u32[]{:S(2)}) collective-permute-start(bf16[24,3456]{1,0:T(8,128)(2,1)S(1)} %fusion.95), channel_id=1, source_target_pairs={{0,16},{1,17},{2,18},{3,19},{4,20},{5,21},{6,22},{7,23},{8,24},{9,... | collective-permute-start | bytes 497672 | tf_op jit(solution)/shard_map/ppermute | solution.py:320
  366.9 29.1 %collective-permute-start.26 = (bf16[750,256]{1,0:T(8,128)(2,1)}, bf16[750,256]{1,0:T(8,128)(2,1)}, u32[]{:S(2)}, u32[]{:S(2)}) collective-permute-start(bf16[750,256]{1,0:T(8,128)(2,1)} %slice.587), channel_id=1, source_target_pairs={{0,1},{1,0},{2,3},{3,2},{4,5},{5,4},{6,7},{7,6},{8,9},{9,8},{10,11... | collective-permute-start | bytes 1152008 | tf_op jit(solution)/shard_map/ppermute | solution.py:512
  389.7 14.4 %collective-permute-start.28 = (bf16[750,256]{1,0:T(8,128)(2,1)S(1)}, bf16[750,256]{1,0:T(8,128)(2,1)S(1)}, u32[]{:S(2)}, u32[]{:S(2)}) collective-permute-start(bf16[750,256]{1,0:T(8,128)(2,1)S(1)} %fusion.63), channel_id=1, source_target_pairs={{0,1},{1,0},{2,3},{3,2},{4,5},{5,4},{6,7},{7,6},{8,9},{9,8},{10,11... | collective-permute-start | bytes 1152008 | tf_op jit(solution)/shard_map/ppermute | solution.py:512
  392.5 11.4 %collective-permute-start.27 = (bf16[750,256]{1,0:T(8,128)(2,1)S(1)}, bf16[750,256]{1,0:T(8,128)(2,1)S(1)}, u32[]{:S(2)}, u32[]{:S(2)}) collective-permute-start(bf16[750,256]{1,0:T(8,128)(2,1)S(1)} %slice.586), channel_id=1, source_target_pairs={{0,1},{1,0},{2,3},{3,2},{4,5},{5,4},{6,7},{7,6},{8,9},{9,8},{10,11... | collective-permute-start | bytes 1152008 | tf_op jit(solution)/shard_map/ppermute | solution.py:512
  417.5 5.6 %collective-permute-start.42 = (bf16[2,2,2,2,24,128]{5,4,3,2,1,0:T(8,128)(2,1)S(1)}, bf16[2,2,2,2,24,128]{5,4,3,2,1,0:T(8,128)(2,1)S(1)}, u32[]{:S(2)}, u32[]{:S(2)}) collective-permute-start(bf16[2,2,2,2,24,128]{5,4,3,2,1,0:T(8,128)(2,1)S(1)} %dynamic-slice_bitcast_fusion), channel_id=1, source_target_pairs={{0,2},{1,3},{2,0},{3,1},{4,6},{5,7},{6,4},{7,5},{8,10},{9,11},{10,... | collective-permute-start | bytes 294920 | tf_op jit(solution)/shard_map/ppermute | solution.py:320
  423.1 4.2 collective-permute-start.43
  424.2 11.2 %copy-start.22 = (f32[750,768]{1,0:T(8,128)S(1)}, f32[750,768]{1,0:T(8,128)}, u32[]{:S(2)}) copy-start(f32[750,768]{1,0:T(8,128)} %get-tuple-element.244) | copy-start | bytes 6912004
  424.4 11.0 %copy-start.4 = (f32[750,768]{1,0:T(8,128)S(1)}, f32[750,768]{1,0:T(8,128)}, u32[]{:S(2)}) copy-start(f32[750,768]{1,0:T(8,128)} %copy-done.3) | copy-start | bytes 6912004
  427.3 3.9 collective-permute-start.44
  430.3 11.5 %collective-permute-start.29 = (bf16[2,2,2,2,24,2304]{5,4,0,3,1,2:T(8,128)(2,1)}, bf16[2,2,2,2,24,2304]{5,4,0,3,1,2:T(8,128)(2,1)}, u32[]{:S(2)}, u32[]{:S(2)}) collective-permute-start(bf16[2,2,2,2,24,2304]{5,4,0,3,1,2:T(8,128)(2,1)} %bitcast.340), channel_id=1, source_target_pairs={{0,2},{1,3},{2,0},{3,1},{4,6},{5,7},{6,4},{7,5},{8,10},{9,11},{10,... | collective-permute-start | bytes 5308424 | tf_op jit(solution)/shard_map/ppermute | solution.py:320
  431.2 3.8 collective-permute-start.45
  435.0 4.6 collective-permute-start.46
  444.9 7.0 %collective-permute-start.34 = (bf16[2,2,2,24,768]{4,3,0,2,1:T(8,128)(2,1)}, bf16[2,2,2,24,768]{4,3,0,2,1:T(8,128)(2,1)}, u32[]{:S(2)}, u32[]{:S(2)}) collective-permute-start(bf16[2,2,2,24,768]{4,3,0,2,1:T(8,128)(2,1)} %fusion.82), channel_id=1, source_target_pairs={{0,4},{1,5},{2,6},{3,7},{4,0},{5,1},{6,2},{7,3},{8,12},{9,13},{10,... | collective-permute-start | bytes 884744 | tf_op jit(solution)/shard_map/ppermute | solution.py:320
  449.1 7.4 %collective-permute-start.38 = (bf16[2,2,2,24,768]{4,3,0,2,1:T(8,128)(2,1)S(1)}, bf16[2,2,2,24,768]{4,3,0,2,1:T(8,128)(2,1)S(1)}, u32[]{:S(2)}, u32[]{:S(2)}) collective-permute-start(bf16[2,2,2,24,768]{4,3,0,2,1:T(8,128)(2,1)S(1)} %fusion.83), channel_id=1, source_target_pairs={{0,8},{1,9},{2,10},{3,11},{4,12},{5,13},{6,14},{7,15},{8,0},{9,1},... | collective-permute-start | bytes 884744 | tf_op jit(solution)/shard_map/ppermute | solution.py:320
  450.1 9.2 %collective-permute-start.30 = (bf16[2,2,2,24,768]{4,3,0,1,2:T(8,128)(2,1)S(1)}, bf16[2,2,2,24,768]{4,3,0,1,2:T(8,128)(2,1)S(1)}, u32[]{:S(2)}, u32[]{:S(2)}) collective-permute-start(bf16[2,2,2,24,768]{4,3,0,1,2:T(8,128)(2,1)S(1)} %fusion.81), channel_id=1, source_target_pairs={{0,1},{1,0},{2,3},{3,2},{4,5},{5,4},{6,7},{7,6},{8,9},{9,8},{10,11... | collective-permute-start | bytes 884744 | tf_op jit(solution)/shard_map/ppermute | solution.py:320
  452.9 6.5 %collective-permute-start.35 = (bf16[2,2,24,768]{3,2,0,1:T(8,128)(2,1)S(1)}, bf16[2,2,24,768]{3,2,0,1:T(8,128)(2,1)S(1)}, u32[]{:S(2)}, u32[]{:S(2)}) collective-permute-start(bf16[2,2,24,768]{3,2,0,1:T(8,128)(2,1)S(1)} %fusion.98), channel_id=1, source_target_pairs={{0,8},{1,9},{2,10},{3,11},{4,12},{5,13},{6,14},{7,15},{8,0},{9,1},... | collective-permute-start | bytes 442376 | tf_op jit(solution)/shard_map/ppermute | solution.py:320
  456.6 5.2 %collective-permute-start.39 = (bf16[2,2,24,768]{3,2,0,1:T(8,128)(2,1)S(1)}, bf16[2,2,24,768]{3,2,0,1:T(8,128)(2,1)S(1)}, u32[]{:S(2)}, u32[]{:S(2)}) collective-permute-start(bf16[2,2,24,768]{3,2,0,1:T(8,128)(2,1)S(1)} %fusion.99), channel_id=1, source_target_pairs={{0,1},{1,0},{2,3},{3,2},{4,5},{5,4},{6,7},{7,6},{8,9},{9,8},{10,11... | collective-permute-start | bytes 442376 | tf_op jit(solution)/shard_map/ppermute | solution.py:320
  459.4 14.7 %copy-start.23 = (f32[2,24,2304]{2,1,0:T(8,128)S(1)}, f32[2,24,2304]{2,1,0:T(8,128)}, u32[]{:S(2)}) copy-start(f32[2,24,2304]{2,1,0:T(8,128)} %param.22) | copy-start | bytes 1327108
  459.4 14.7 %copy-start.36 = (f32[24,2304]{1,0:T(8,128)S(1)}, f32[24,2304]{1,0:T(8,128)}, u32[]{:S(2)}) copy-start(f32[24,2304]{1,0:T(8,128)} %param.16) | copy-start | bytes 663556
  459.4 5.2 %collective-permute-start.31 = (bf16[2,2,24,768]{3,2,0,1:T(8,128)(2,1)S(1)}, bf16[2,2,24,768]{3,2,0,1:T(8,128)(2,1)S(1)}, u32[]{:S(2)}, u32[]{:S(2)}) collective-permute-start(bf16[2,2,24,768]{3,2,0,1:T(8,128)(2,1)S(1)} %fusion.97), channel_id=1, source_target_pairs={{0,4},{1,5},{2,6},{3,7},{4,0},{5,1},{6,2},{7,3},{8,12},{9,13},{10,... | collective-permute-start | bytes 442376 | tf_op jit(solution)/shard_map/ppermute | solution.py:320
  459.5 6.2 %collective-permute-start.36 = (bf16[2,24,768]{2,1,0:T(8,128)(2,1)S(1)}, bf16[2,24,768]{2,1,0:T(8,128)(2,1)S(1)}, u32[]{:S(2)}, u32[]{:S(2)}) collective-permute-start(bf16[2,24,768]{2,1,0:T(8,128)(2,1)S(1)} %fusion.103), channel_id=1, source_target_pairs={{0,1},{1,0},{2,3},{3,2},{4,5},{5,4},{6,7},{7,6},{8,9},{9,8},{10,11... | collective-permute-start | bytes 221192 | tf_op jit(solution)/shard_map/ppermute | solution.py:320
  461.9 4.4 collective-permute-start.40
  464.7 4.4 collective-permute-start.32
  465.8 4.9 %collective-permute-start.37 = (bf16[24,768]{1,0:T(8,128)(2,1)S(1)}, bf16[24,768]{1,0:T(8,128)(2,1)S(1)}, u32[]{:S(2)}, u32[]{:S(2)}) collective-permute-start(bf16[24,768]{1,0:T(8,128)(2,1)S(1)} %fusion.108), channel_id=1, source_target_pairs={{0,16},{1,17},{2,18},{3,19},{4,20},{5,21},{6,22},{7,23},{8,24},{9,... | collective-permute-start | bytes 110600 | tf_op jit(solution)/shard_map/ppermute | solution.py:320
  466.3 5.6 %collective-permute-start.41 = (bf16[24,768]{1,0:T(8,128)(2,1)S(1)}, bf16[24,768]{1,0:T(8,128)(2,1)S(1)}, u32[]{:S(2)}, u32[]{:S(2)}) collective-permute-start(bf16[24,768]{1,0:T(8,128)(2,1)S(1)} %fusion.109), channel_id=1, source_target_pairs={{0,16},{1,17},{2,18},{3,19},{4,20},{5,21},{6,22},{7,23},{8,24},{9,... | collective-permute-start | bytes 110600 | tf_op jit(solution)/shard_map/ppermute | solution.py:320
  469.1 4.9 %collective-permute-start.33 = (bf16[24,768]{1,0:T(8,128)(2,1)S(1)}, bf16[24,768]{1,0:T(8,128)(2,1)S(1)}, u32[]{:S(2)}, u32[]{:S(2)}) collective-permute-start(bf16[24,768]{1,0:T(8,128)(2,1)S(1)} %fusion.107), channel_id=1, source_target_pairs={{0,16},{1,17},{2,18},{3,19},{4,20},{5,21},{6,22},{7,23},{8,24},{9,... | collective-permute-start | bytes 110600 | tf_op jit(solution)/shard_map/ppermute | solution.py:320
  (55 other events, 191.3 us)
Sparse Core Ops, SparseCore 0:
  11.5 97.3 all-gather.1

commit v16 on v14

--- a/solution.py
+++ b/solution.py
@@ -406,6 +406,7 @@
     ).astype(jnp.bfloat16)
     bit_count, core_bit, rotated_orders, late_orders = plan
     first_full = tree_all_gather(first_pack, (896, 768, 768), rotated_orders, (bit_count, core_bit))
+    partner_send, first_full = lax.optimization_barrier((inputs, first_full))
     second_full = lax.all_gather(second_pack, everyone, axis=0, tiled=True)
     full_in = first_full[:, :wide_in]
     small_full = first_full[:, wide_in:].astype(jnp.float32)
@@ -420,7 +421,7 @@
         frames_rows, column_set[:, 0], column_set[:, 1]
     )
     hidden_first = normed_first.astype(jnp.bfloat16)
-    partner_rows = lax.ppermute(inputs, "frame", swap).reshape(row_count, model_width)
+    partner_rows = lax.ppermute(partner_send, "frame", swap).reshape(row_count, model_width)
     hidden_partner = norm_parts(
         partner_rows.astype(jnp.float32), column_set[:, 0], column_set[:, 1]
     )[0].astype(jnp.bfloat16)

time: 486 us -> 492 us (1.012)
  waiting for transfers between devices: 84.2 us -> 95.2 us
    ppermute x1, waiting for transfers between devices: 0.01 us -> 34.9 us  [body(): lax.ppermute(partner_send, 'frame', swap).reshape(row_count, model_width)]
    ppermute x13, waiting for transfers between devices: 42 us -> 18.8 us  [double(): got = lax.ppermute(data, ('clip', 'frame'), pairs)]
    unnamed x178 -> x176, local copies, waits for them, and re-layouts: 29 us -> 27.3 us
  transfers between devices with their start and end apart: 43 -> 43, of which waited for: 22 -> 23; matrix products, arithmetic and copies ran while one was open for 17% -> 15% of each run, Pallas kernels for 21% -> 21%
where the time goes in v16:
time: 492 us; the launch traced here: 488 us
  Pallas kernels  102 us (21%)
  waiting for transfers between devices  95.2 us (19%)
  local copies, waits for them, and re-layouts  93.6 us (19%)
  matrix products  71.1 us (14%)
  other arithmetic  57.1 us (12%)
  starting transfers between devices  52.3 us (11%)
  between operations  16.1 us (3%)
    pallas_call x6, Pallas kernels, attention_pallas(): pl.pallas_call(attention_backward_kernel, grid=(span,), in_specs=[qi_spec...  65 us
    pallas_call x1, Pallas kernels, attention_pallas(): pl.pallas_call(attention_forward_kernel, grid=(pair_count,), in_specs=[q_...  37.4 us
    ppermute x1, waiting for transfers between devices, body(): lax.ppermute(partner_send, 'frame', swap).reshape(row_count, model_width)  34.9 us
    ppermute x22, waiting for transfers between devices, tree_reduce_scatter(): got = lax.ppermute(send, ('clip', 'frame'), pairs)  30.5 us
    unnamed x176, local copies, waits for them, and re-layouts  27.3 us
    ppermute x22, starting transfers between devices, tree_reduce_scatter(): got = lax.ppermute(send, ('clip', 'frame'), pairs)  22.5 us
    ppermute x13, starting transfers between devices, double(): got = lax.ppermute(data, ('clip', 'frame'), pairs)  19.7 us
    ppermute x13, waiting for transfers between devices, double(): got = lax.ppermute(data, ('clip', 'frame'), pairs)  18.8 us
  transfers between devices with their start and end apart: 43, of which 23 were waited for; matrix products, arithmetic and copies ran while one was open for 15% of the time, Pallas kernels for 21%

profile of v16, /device:TPU:0, one launch (start us, length us, event | category | flops | bytes accessed | tf_op | source)
XLA Modules:
  0.0 487.8 jit_solution(15754615216388525270)
XLA Ops:
  12.7 4.1 collective-permute-start.8
  16.9 3.0 collective-permute-start
  25.2 2.9 collective-permute-done.5
  28.1 1.8 collective-permute-start.6
  32.8 2.4 collective-permute-done.10
  35.5 2.1 collective-permute-done.6
  39.3 1.9 collective-permute-start.3
  41.3 3.2 collective-permute-done.7
  44.6 4.2 collective-permute-done.3
  51.3 3.4 collective-permute-done.12
  54.7 3.1 maximum_select_fusion
  57.8 1.8 copy-done.15
  60.0 2.5 collective-permute-start.13
  64.3 5.5 %add_convert_fusion = bf16[750,2304]{1,0:T(8,128)(2,1)S(1)} fusion(f32[2304]{0:T(1024)S(1)} %pad_maximum_fusion.16, bf16[768,2432]{1,0:T(8,128)(2,1)} %bitcast.326, bf16[1,750,768]{2,1,0:T(8,128)(2,1)S(1)} %copy-done.2, f32[768]{0:T(1024)S(1)} %get-tuple-element.230, f32[768]{0:T(1024)S(1)} %get-tuple-element.231, f32[750]{0:T(1024)S(1)} %add_rsqrt_fusion.2, ...), kind=kOutput, calls=%fused_computation.14 | convolution fusion | flops 2661120000 | bytes 8168304 | tf_op jit(solution)/shard_map/dot_general | solution.py:432
  71.7 34.9 %collective-permute-done.13 = bf16[1,750,768]{2,1,0:T(8,128)(2,1)S(1)} collective-permute-done((bf16[1,750,768]{2,1,0:T(8,128)(2,1)S(1)}, bf16[1,750,768]{2,1,0:T(8,128)(2,1)S(1)}, u32[]{:S(2)}, u32[]{:S(2)}) %collective-permute-start.13) | collective-permute-done | bytes 1152032 | tf_op jit(solution)/shard_map/ppermute | solution.py:424
  107.3 2.1 add_convert_fusion.1
  109.5 2.7 fusion.8.k_ref.v_ref
  112.1 37.4 %shard_map.293 = (bf16[768,768]{1,0:T(8,128)(2,1)S(1)}, f32[768,768]{1,0:T(8,128)S(1)}) custom-call(bf16[768,768]{1,0:T(8,128)(2,1)S(1)} %pad.39.q_ref, bf16[1536,1536]{1,0:T(8,128)(2,1)} %fusion.8.k_ref.v_ref, bf16[1536,1536]{1,0:T(8,128)(2,1)} %fusion.8.k_ref.v_ref, f32[1,1536]{1,0:T(1,128)S(1)} %compare_select_fusion.kbias_ref), custom_call_target="tpu_custom_call" | custom-call | tf_op jit(solution)/shard_map/pallas_call | solution.py:161
  151.0 2.5 fusion.121
  155.3 4.8 slice.405
  160.0 8.5 %reshape.1150 = bf16[3072,768]{1,0:T(8,128)(2,1)} reshape(bf16[768,3072]{1,0:T(8,128)(2,1)} %slice.405) | data formatting | bytes 9437184 | tf_op jit(solution)/shard_map/reshape | solution.py:417
  168.5 9.4 %multiply_convert_fusion = (bf16[750,3072]{1,0:T(8,128)(2,1)S(1)}, f32[750,3072]{1,0:T(8,128)}) fusion(f32[3072]{0:T(1024)S(1)} %add.429, bf16[768,6912]{1,0:T(8,128)(2,1)} %all-gather.2.cloned.1.call-done, f32[750,768]{1,0:T(8,128)} %copy-done.6, f32[768]{0:T(1024)S(1)} %get-tuple-element.225, f32[768]{0:T(1024)S(1)} %get-tuple-element.226, ...), kind=kOutput, calls=%fused_computation.12 | convolution fusion | flops 3555648000 | bytes 20877168 | tf_op jit(solution)/shard_map/dot_general | solution.py:452
  177.9 2.2 copy-done.70
  180.1 5.8 %convolution_convert_fusion.2 = bf16[3072,768]{1,0:T(8,128)(2,1)} fusion(bf16[750,3072]{1,0:T(8,128)(2,1)S(1)} %get-tuple-element.283, bf16[1,750,768]{2,1,0:T(8,128)(2,1)S(1)} %copy-done.14), kind=kOutput, calls=%fused_computation.19 | convolution fusion | flops 3541303296 | bytes 10478592 | tf_op jit(solution)/shard_map/dot_general | solution.py:462
  185.8 8.5 %concatenate.309 = bf16[2,2,2,2,2,24,3072]{6,5,4,3,2,1,0:T(8,128)(2,1)} reshape(bf16[3072,768]{1,0:T(8,128)(2,1)} %convolution_convert_fusion.2) | data formatting | bytes 9437184 | tf_op jit(solution)/shard_map/concatenate | solution.py:482
  194.3 9.4 %fusion.122 = (bf16[3072]{0:T(1024)(128)(2,1)S(1)}, bf16[750,3072]{1,0:T(8,128)(2,1)S(1)}) fusion(f32[750,3072]{1,0:T(8,128)} %get-tuple-element.284, f32[3072]{0:T(1024)S(1)} %add.429, bf16[3072,768]{1,0:T(8,128)(2,1)} %reshape.1150, bf16[1,750,768]{2,1,0:T(8,128)(2,1)S(1)} %copy-done.14), kind=kOutput, calls=%fused_computation.323 | convolution fusion | flops 3566588928 | bytes 19713024 | tf_op jit(solution)/shard_map/dot_general | solution.py:466
  203.8 5.0 %convolution_convert_fusion.1 = bf16[768,3072]{1,0:T(8,128)(2,1)S(1)} fusion(bf16[750,3072]{1,0:T(8,128)(2,1)S(1)} %get-tuple-element.287, f32[750,768]{1,0:T(8,128)S(1)} %copy-done.7, f32[768]{0:T(1024)S(1)} %copy-done.65, f32[768]{0:T(1024)S(1)} %get-tuple-element.226, f32[750]{0:T(1024)S(1)} %add_rsqrt_fusion, f32[750]{0:T(1024)S(1)} %broadcast_multiply_fusion.4), kind=kOutput, calls=%fused_computation.18 | convolution fusion | flops 3544183296 | bytes 11642736 | tf_op jit(solution)/shard_map/dot_general | solution.py:468
  208.8 7.3 %multiply_reduce_fusion = (bf16[768]{0:T(1024)(128)(2,1)}, f32[750]{0:T(1024)S(1)}, f32[750]{0:T(1024)S(1)}, bf16[768]{0:T(1024)(128)(2,1)S(1)}, f32[750,768]{1,0:T(8,128)S(1)}) fusion(f32[750,768]{1,0:T(8,128)S(1)} %copy-done.7, f32[750]{0:T(1024)S(1)} %add_rsqrt_fusion, f32[750]{0:T(1024)S(1)} %broadcast_multiply_fusion.4, ...), kind=kOutput, calls=%fused_computation.64 | convolution fusion | flops 3544124928 | bytes 13952736 | tf_op jit(solution)/shard_map/dot_general | solution.py:472
  219.2 8.0 %pad_maximum_fusion = bf16[2,2,2,2,2,24,6912]{6,5,4,3,2,1,0:T(8,128)(2,1)} fusion(bf16[2,2,2,2,2,24,768]{6,5,4,3,2,1,0:T(8,128)(2,1)S(1)} %bitcast.330, bf16[2,2,2,2,2,24,3072]{6,5,4,3,2,1,0:T(8,128)(2,1)S(1)} %bitcast.324, bf16[2,2,2,2,2,24,3072]{6,5,4,3,2,1,0:T(8,128)(2,1)S(1)} %bitcast.319), kind=kLoop, calls=%fused_computation.1 | loop fusion | flops 31850496 | bytes 21233664 | tf_op jit(solution)/shard_map/concatenate | solution.py:482
  227.2 8.7 %constant_dynamic-slice_fusion.1 = (bf16[2,2,2,1,2,24,6912]{6,5,4,3,2,1,0:T(8,128)(2,1)}, bf16[2,2,2,1,2,24,6912]{6,5,4,3,2,1,0:T(8,128)(2,1)}) fusion(bf16[2,2,2,2,2,24,6912]{6,5,4,3,2,1,0:T(8,128)(2,1)} %pad_maximum_fusion, s32[]{:T(128)S(6)} %select_n.403, s32[]{:T(128)S(6)} %select_n.404), kind=kLoop, calls=%fused_computation.282 | loop fusion | bytes 21233672 | tf_op jit(solution)/shard_map/jit(dynamic_index_in_dim)/dynamic_slice | solution.py:313
  235.9 5.2 %copy.175 = bf16[2,2,2,1,2,24,6912]{6,5,0,4,2,1,3:T(8,128)(2,1)} copy(bf16[2,2,2,1,2,24,6912]{6,5,4,3,2,1,0:T(8,128)(2,1)} %get-tuple-element.243) | data formatting | bytes 10616832
  244.2 3.1 convolution_convert_fusion.4
  247.2 2.9 collective-permute-done.14
  250.2 5.3 %convert_add_fusion = f32[2,2,2,2,24,6912]{5,4,0,3,2,1:T(8,128)S(1)} fusion(bf16[2,2,2,2,24,6912]{5,4,0,3,2,1:T(8,128)(2,1)} %collective-permute-done.14, bf16[2,2,2,1,2,24,6912]{6,5,4,3,2,1,0:T(8,128)(2,1)} %get-tuple-element.242), kind=kLoop, calls=%fused_computation.2 | loop fusion | flops 7962624 | bytes 21233664 | tf_op jit(solution)/shard_map/add | solution.py:321
  255.5 4.9 %fusion.117 = (f32[2,2,2,2,24,3456]{5,4,0,3,2,1:T(8,128)}, f32[2,2,2,2,24,3456]{5,4,0,3,2,1:T(8,128)}) fusion(f32[2,2,2,2,24,6912]{5,4,0,3,2,1:T(8,128)S(1)} %convert_add_fusion), kind=kLoop, calls=%fused_computation.318 | loop fusion | bytes 21233664 | tf_op jit(solution)/shard_map/slice | solution.py:307
  260.4 3.1 fusion.42
  263.5 8.5 %fusion.41 = bf16[1,750,768]{2,1,0:T(8,128)(2,1)} fusion(f32[750,768]{1,0:T(8,128)S(1)} %copy-done.8, bf16[750,3072]{1,0:T(8,128)(2,1)} %copy-done.70, bf16[3072,768]{1,0:T(8,128)(2,1)} %reshape.1150, f32[768]{0:T(1024)S(1)} %copy-done.63), kind=kOutput, calls=%fused_computation.82 | convolution fusion | flops 3540672000 | bytes 12785664 | tf_op jit(solution)/shard_map/dot_general | solution.py:456
  272.1 10.9 %shard_map.294 = (f32[768,128]{1,0:T(8,128)S(1)}, f32[1536,128]{1,0:T(8,128)S(1)}, f32[1536,128]{1,0:T(8,128)S(1)}) custom-call(bf16[768,768]{1,0:T(8,128)(2,1)S(1)} %pad.39.q_ref, bf16[1536,1536]{1,0:T(8,128)(2,1)} %fusion.8.k_ref.v_ref, bf16[1536,1536]{1,0:T(8,128)(2,1)} %fusion.8.k_ref.v_ref, bf16[768,768]{1,0:T(8,128)(2,1)S(1)} %pad.41.do_ref, ...), custom_call_target="tpu_custom_call" | custom-call | tf_op jit(solution)/shard_map/pallas_call | solution.py:180
  284.0 2.5 collective-permute-start.23
  286.5 3.0 fusion.43
  293.9 2.0 collective-permute-done.23
  295.9 1.8 fusion.62
  297.8 10.8 %shard_map.295 = (f32[768,128]{1,0:T(8,128)S(1)}, f32[1536,128]{1,0:T(8,128)S(1)}, f32[1536,128]{1,0:T(8,128)S(1)}) custom-call(bf16[768,768]{1,0:T(8,128)(2,1)S(1)} %pad.39.q_ref, bf16[1536,1536]{1,0:T(8,128)(2,1)} %fusion.8.k_ref.v_ref, bf16[1536,1536]{1,0:T(8,128)(2,1)} %fusion.8.k_ref.v_ref, bf16[768,768]{1,0:T(8,128)(2,1)S(1)} %pad.42.do_ref, ...), custom_call_target="tpu_custom_call" | custom-call | tf_op jit(solution)/shard_map/pallas_call | solution.py:180
  308.8 2.4 bitcast_add_fusion.1
  311.2 9.5 %collective-permute-done.16 = bf16[2,2,2,24,3456]{4,3,0,2,1:T(8,128)(2,1)} collective-permute-done((bf16[2,2,2,24,3456]{4,3,0,2,1:T(8,128)(2,1)}, bf16[2,2,2,24,3456]{4,3,0,2,1:T(8,128)(2,1)}, u32[]{:S(2)}, u32[]{:S(2)}) %collective-permute-start.16) | collective-permute-done | bytes 1327136 | tf_op jit(solution)/shard_map/ppermute | solution.py:320
  322.3 1.8 collective-permute-start.18
  325.2 10.7 %shard_map.296 = (f32[768,128]{1,0:T(8,128)S(1)}, f32[1536,128]{1,0:T(8,128)S(1)}, f32[1536,128]{1,0:T(8,128)S(1)}) custom-call(bf16[768,768]{1,0:T(8,128)(2,1)S(1)} %pad.39.q_ref, bf16[1536,1536]{1,0:T(8,128)(2,1)} %fusion.8.k_ref.v_ref, bf16[1536,1536]{1,0:T(8,128)(2,1)} %fusion.8.k_ref.v_ref, bf16[768,768]{1,0:T(8,128)(2,1)S(1)} %pad.43.do_ref, ...), custom_call_target="tpu_custom_call" | custom-call | tf_op jit(solution)/shard_map/pallas_call | solution.py:180
  342.5 11.1 %shard_map.297 = (f32[768,128]{1,0:T(8,128)S(1)}, f32[1536,128]{1,0:T(8,128)S(1)}, f32[1536,128]{1,0:T(8,128)S(1)}) custom-call(bf16[768,768]{1,0:T(8,128)(2,1)S(1)} %pad.39.q_ref, bf16[1536,1536]{1,0:T(8,128)(2,1)} %fusion.8.k_ref.v_ref, bf16[1536,1536]{1,0:T(8,128)(2,1)} %fusion.8.k_ref.v_ref, bf16[768,768]{1,0:T(8,128)(2,1)S(1)} %pad.44.do_ref, ...), custom_call_target="tpu_custom_call" | custom-call | tf_op jit(solution)/shard_map/pallas_call | solution.py:180
  356.4 3.3 collective-permute-start.22
  360.0 10.7 %shard_map.298 = (f32[768,128]{1,0:T(8,128)S(1)}, f32[1536,128]{1,0:T(8,128)S(1)}, f32[1536,128]{1,0:T(8,128)S(1)}) custom-call(bf16[768,768]{1,0:T(8,128)(2,1)S(1)} %pad.39.q_ref, bf16[1536,1536]{1,0:T(8,128)(2,1)} %fusion.8.k_ref.v_ref, bf16[1536,1536]{1,0:T(8,128)(2,1)} %fusion.8.k_ref.v_ref, bf16[768,768]{1,0:T(8,128)(2,1)S(1)} %pad.45.do_ref, ...), custom_call_target="tpu_custom_call" | custom-call | tf_op jit(solution)/shard_map/pallas_call | solution.py:180
  381.8 10.8 %shard_map.299 = (f32[768,128]{1,0:T(8,128)S(1)}, f32[1536,128]{1,0:T(8,128)S(1)}, f32[1536,128]{1,0:T(8,128)S(1)}) custom-call(bf16[768,768]{1,0:T(8,128)(2,1)S(1)} %pad.39.q_ref, bf16[1536,1536]{1,0:T(8,128)(2,1)} %fusion.8.k_ref.v_ref, bf16[1536,1536]{1,0:T(8,128)(2,1)} %fusion.8.k_ref.v_ref, bf16[768,768]{1,0:T(8,128)(2,1)S(1)} %pad.46.do_ref, ...), custom_call_target="tpu_custom_call" | custom-call | tf_op jit(solution)/shard_map/pallas_call | solution.py:180
  399.2 9.0 %collective-permute-done.27 = bf16[750,256]{1,0:T(8,128)(2,1)S(1)} collective-permute-done((bf16[750,256]{1,0:T(8,128)(2,1)S(1)}, bf16[750,256]{1,0:T(8,128)(2,1)S(1)}, u32[]{:S(2)}, u32[]{:S(2)}) %collective-permute-start.27) | collective-permute-done | bytes 384032 | tf_op jit(solution)/shard_map/ppermute | solution.py:513
  412.0 4.6 fusion.32
  416.6 2.5 reduce.2
  419.2 6.8 %convolution_convert_fusion = bf16[768,2304]{1,0:T(8,128)(2,1)} fusion(bf16[750,2304]{1,0:T(8,128)(2,1)} %copy-done.13, bf16[1,750,768]{2,1,0:T(8,128)(2,1)S(1)} %copy-done.3, f32[768]{0:T(1024)S(1)} %copy-done.62, f32[768]{0:T(1024)S(1)} %copy-done.56, f32[750]{0:T(1024)S(1)} %copy-done.58, f32[750]{0:T(1024)S(1)} %copy-done.54), kind=kOutput, calls=%fused_computation.17 | convolution fusion | flops 2659433472 | bytes 8159088 | tf_op jit(solution)/shard_map/dot_general | solution.py:529
  427.5 7.7 %concatenate.321 = bf16[768,2432]{1,0:T(8,128)(2,1)} concatenate(bf16[768,2304]{1,0:T(8,128)(2,1)} %convolution_convert_fusion, bf16[768,1]{1,0:T(8,128)(2,1)S(1)} %stack.415, bf16[768,1]{1,0:T(8,128)(2,1)S(1)} %stack.416, bf16[768,1]{1,0:T(8,128)(2,1)S(1)} %stack.417, bf16[768,1]{1,0:T(8,128)(2,1)S(1)} %stack.418, bf16[768,1]{1,0:T(8,128)(2,1)S(1)} %copy-done.43, ...), dimensions={1} | concatenate | bytes 7471104 | tf_op jit(solution)/shard_map/concatenate | solution.py:562
  435.2 1.8 dynamic-slice_bitcast_fusion
  443.7 1.8 fusion.46
  448.5 2.3 collective-permute-done.38
  452.1 2.7 collective-permute-done.34
  456.0 2.3 collective-permute-done.30
  462.2 3.4 collective-permute-done.40
  465.6 2.6 collective-permute-start.41
  474.0 2.1 collective-permute-start.33
  (425 shorter events, 98.8 us)
Async XLA Ops:
  7.2 143.8 %all-gather.2.cloned.1.call-start = ((), (), s32[]{:S(2)}) async-start(), calls=%async_computation | async-start | bytes 10948608 | tf_op jit(solution)/shard_map/all_gather | solution.py:410
  12.7 7.2 %collective-permute-start.8 = (bf16[24,768]{1,0:T(8,128)(2,1)S(1)}, bf16[24,768]{1,0:T(8,128)(2,1)S(1)}, u32[]{:S(2)}, u32[]{:S(2)}) collective-permute-start(bf16[24,768]{1,0:T(8,128)(2,1)S(1)} %get-tuple-element.263), channel_id=1, source_target_pairs={{0,16},{1,17},{2,18},{3,19},{4,20},{5,21},{6,22},{7,23},{8,24},{9,... | collective-permute-start | bytes 110600 | tf_op jit(solution)/shard_map/ppermute | solution.py:339
  16.8 5.4 %collective-permute-start.4 = (bf16[24,768]{1,0:T(8,128)(2,1)S(1)}, bf16[24,768]{1,0:T(8,128)(2,1)S(1)}, u32[]{:S(2)}, u32[]{:S(2)}) collective-permute-start(bf16[24,768]{1,0:T(8,128)(2,1)S(1)} %get-tuple-element.269), channel_id=1, source_target_pairs={{0,16},{1,17},{2,18},{3,19},{4,20},{5,21},{6,22},{7,23},{8,24},{9,... | collective-permute-start | bytes 110600 | tf_op jit(solution)/shard_map/ppermute | solution.py:339
  16.9 6.9 %collective-permute-start = (bf16[24,896]{1,0:T(8,128)(2,1)S(1)}, bf16[24,896]{1,0:T(8,128)(2,1)S(1)}, u32[]{:S(2)}, u32[]{:S(2)}) collective-permute-start(bf16[24,896]{1,0:T(8,128)(2,1)S(1)} %get-tuple-element.266), channel_id=1, source_target_pairs={{0,16},{1,17},{2,18},{3,19},{4,20},{5,21},{6,22},{7,23},{8,24},{9,... | collective-permute-start | bytes 129032 | tf_op jit(solution)/shard_map/ppermute | solution.py:339
  20.0 10.0 %collective-permute-start.9 = (bf16[2,24,768]{2,1,0:T(8,128)(2,1)S(1)}, bf16[2,24,768]{2,1,0:T(8,128)(2,1)S(1)}, u32[]{:S(2)}, u32[]{:S(2)}) collective-permute-start(bf16[2,24,768]{2,1,0:T(8,128)(2,1)S(1)} %maximum_select_fusion.18), channel_id=1, source_target_pairs={{0,4},{1,5},{2,6},{3,7},{4,0},{5,1},{6,2},{7,3},{8,12},{9,13},{10,... | collective-permute-start | bytes 221192 | tf_op jit(solution)/shard_map/ppermute | solution.py:339
  22.3 5.8 %collective-permute-start.5 = (bf16[2,24,768]{2,1,0:T(8,128)(2,1)S(1)}, bf16[2,24,768]{2,1,0:T(8,128)(2,1)S(1)}, u32[]{:S(2)}, u32[]{:S(2)}) collective-permute-start(bf16[2,24,768]{2,1,0:T(8,128)(2,1)S(1)} %maximum_select_fusion.17), channel_id=1, source_target_pairs={{0,1},{1,0},{2,3},{3,2},{4,5},{5,4},{6,7},{7,6},{8,9},{9,8},{10,11... | collective-permute-start | bytes 221192 | tf_op jit(solution)/shard_map/ppermute | solution.py:339
  23.9 7.3 %collective-permute-start.1 = (bf16[2,24,896]{2,1,0:T(8,128)(2,1)S(1)}, bf16[2,24,896]{2,1,0:T(8,128)(2,1)S(1)}, u32[]{:S(2)}, u32[]{:S(2)}) collective-permute-start(bf16[2,24,896]{2,1,0:T(8,128)(2,1)S(1)} %maximum_select_fusion.15), channel_id=1, source_target_pairs={{0,8},{1,9},{2,10},{3,11},{4,12},{5,13},{6,14},{7,15},{8,0},{9,1},... | collective-permute-start | bytes 258056 | tf_op jit(solution)/shard_map/ppermute | solution.py:339
  28.1 9.5 %collective-permute-start.6 = (bf16[2,2,24,768]{3,2,0,1:T(8,128)(2,1)S(1)}, bf16[2,2,24,768]{3,2,0,1:T(8,128)(2,1)S(1)}, u32[]{:S(2)}, u32[]{:S(2)}) collective-permute-start(bf16[2,2,24,768]{3,2,0,1:T(8,128)(2,1)S(1)} %maximum_select_fusion.12), channel_id=1, source_target_pairs={{0,8},{1,9},{2,10},{3,11},{4,12},{5,13},{6,14},{7,15},{8,0},{9,1},... | collective-permute-start | bytes 442376 | tf_op jit(solution)/shard_map/ppermute | solution.py:339
  30.0 5.2 %collective-permute-start.10 = (bf16[2,2,24,768]{3,2,1,0:T(8,128)(2,1)S(1)}, bf16[2,2,24,768]{3,2,1,0:T(8,128)(2,1)S(1)}, u32[]{:S(2)}, u32[]{:S(2)}) collective-permute-start(bf16[2,2,24,768]{3,2,1,0:T(8,128)(2,1)S(1)} %maximum_select_fusion.13), channel_id=1, source_target_pairs={{0,1},{1,0},{2,3},{3,2},{4,5},{5,4},{6,7},{7,6},{8,9},{9,8},{10,11... | collective-permute-start | bytes 442376 | tf_op jit(solution)/shard_map/ppermute | solution.py:339
  31.2 8.0 %collective-permute-start.2 = (bf16[2,2,24,896]{3,2,0,1:T(8,128)(2,1)S(1)}, bf16[2,2,24,896]{3,2,0,1:T(8,128)(2,1)S(1)}, u32[]{:S(2)}, u32[]{:S(2)}) collective-permute-start(bf16[2,2,24,896]{3,2,0,1:T(8,128)(2,1)S(1)} %maximum_select_fusion.10), channel_id=1, source_target_pairs={{0,4},{1,5},{2,6},{3,7},{4,0},{5,1},{6,2},{7,3},{8,12},{9,13},{10,... | collective-permute-start | bytes 516104 | tf_op jit(solution)/shard_map/ppermute | solution.py:339
  35.2 9.3 %collective-permute-start.11 = (bf16[2,2,2,24,768]{4,3,2,1,0:T(8,128)(2,1)S(1)}, bf16[2,2,2,24,768]{4,3,2,1,0:T(8,128)(2,1)S(1)}, u32[]{:S(2)}, u32[]{:S(2)}) collective-permute-start(bf16[2,2,2,24,768]{4,3,2,1,0:T(8,128)(2,1)S(1)} %maximum_select_fusion.8), channel_id=1, source_target_pairs={{0,8},{1,9},{2,10},{3,11},{4,12},{5,13},{6,14},{7,15},{8,0},{9,1},... | collective-permute-start | bytes 884744 | tf_op jit(solution)/shard_map/ppermute | solution.py:339
  37.7 6.8 %collective-permute-start.7 = (bf16[2,2,2,24,768]{4,3,0,2,1:T(8,128)(2,1)S(1)}, bf16[2,2,2,24,768]{4,3,0,2,1:T(8,128)(2,1)S(1)}, u32[]{:S(2)}, u32[]{:S(2)}) collective-permute-start(bf16[2,2,2,24,768]{4,3,0,2,1:T(8,128)(2,1)S(1)} %maximum_select_fusion.7), channel_id=1, source_target_pairs={{0,4},{1,5},{2,6},{3,7},{4,0},{5,1},{6,2},{7,3},{8,12},{9,13},{10,... | collective-permute-start | bytes 884744 | tf_op jit(solution)/shard_map/ppermute | solution.py:339
  39.3 9.5 %collective-permute-start.3 = (bf16[2,2,2,24,896]{4,3,0,1,2:T(8,128)(2,1)S(1)}, bf16[2,2,2,24,896]{4,3,0,1,2:T(8,128)(2,1)S(1)}, u32[]{:S(2)}, u32[]{:S(2)}) collective-permute-start(bf16[2,2,2,24,896]{4,3,0,1,2:T(8,128)(2,1)S(1)} %maximum_select_fusion.5), channel_id=1, source_target_pairs={{0,1},{1,0},{2,3},{3,2},{4,5},{5,4},{6,7},{7,6},{8,9},{9,8},{10,11... | collective-permute-start | bytes 1032200 | tf_op jit(solution)/shard_map/ppermute | solution.py:339
  50.5 4.2 collective-permute-start.12
  50.7 13.5 %copy-start.53 = (f32[750]{0:T(1024)}, f32[750]{0:T(1024)S(1)}, u32[]{:S(2)}) copy-start(f32[750]{0:T(1024)S(1)} %broadcast_multiply_fusion.6) | copy-start | bytes 9004
  51.3 13.0 %copy-start.57 = (f32[750]{0:T(1024)}, f32[750]{0:T(1024)S(1)}, u32[]{:S(2)}) copy-start(f32[750]{0:T(1024)S(1)} %add_rsqrt_fusion.2) | copy-start | bytes 9004
  60.0 46.5 %collective-permute-start.13 = (bf16[1,750,768]{2,1,0:T(8,128)(2,1)S(1)}, bf16[1,750,768]{2,1,0:T(8,128)(2,1)S(1)}, u32[]{:S(2)}, u32[]{:S(2)}) collective-permute-start(bf16[1,750,768]{2,1,0:T(8,128)(2,1)S(1)} %copy-done.2), channel_id=1, source_target_pairs={{0,1},{1,0},{2,3},{3,2},{4,5},{5,4},{6,7},{7,6},{8,9},{9,8},{10,11... | collective-permute-start | bytes 3456008 | tf_op jit(solution)/shard_map/ppermute | solution.py:424
  64.2 43.1 %copy-start.55 = (f32[768]{0:T(1024)}, f32[768]{0:T(1024)S(1)}, u32[]{:S(2)}) copy-start(f32[768]{0:T(1024)S(1)} %get-tuple-element.231) | copy-start | bytes 9220
  64.2 43.1 %copy-start.61 = (f32[768]{0:T(1024)}, f32[768]{0:T(1024)S(1)}, u32[]{:S(2)}) copy-start(f32[768]{0:T(1024)S(1)} %get-tuple-element.230) | copy-start | bytes 9220
  64.2 104.3 %copy-start.64 = (f32[768]{0:T(1024)}, f32[768]{0:T(1024)S(1)}, u32[]{:S(2)}) copy-start(f32[768]{0:T(1024)S(1)} %get-tuple-element.225) | copy-start | bytes 9220
  71.6 35.7 %copy-start.16 = (bf16[2,2,2,2,2,24,2432]{6,5,4,3,2,1,0:T(8,128)(2,1)S(1)}, bf16[2,2,2,2,2,24,2432]{6,5,4,3,2,1,0:T(8,128)(2,1)}, u32[]{:S(2)}) copy-start(bf16[2,2,2,2,2,24,2432]{6,5,4,3,2,1,0:T(8,128)(2,1)} %copy-done.15) | copy-start | bytes 11206660
  168.5 11.6 %copy-start.14 = (bf16[1,750,768]{2,1,0:T(8,128)(2,1)S(1)}, bf16[1,750,768]{2,1,0:T(8,128)(2,1)}, u32[]{:S(2)}) copy-start(bf16[1,750,768]{2,1,0:T(8,128)(2,1)} %param.15) | copy-start | bytes 3456004
  194.3 9.5 %copy-start.7 = (f32[750,768]{1,0:T(8,128)S(1)}, f32[750,768]{1,0:T(8,128)}, u32[]{:S(2)}) copy-start(f32[750,768]{1,0:T(8,128)} %copy-done.6) | copy-start | bytes 6912004
  194.3 9.5 %copy-start.65 = (f32[768]{0:T(1024)S(1)}, f32[768]{0:T(1024)}, u32[]{:S(2)}) copy-start(f32[768]{0:T(1024)} %copy-done.64) | copy-start | bytes 9220
  241.1 9.1 %collective-permute-start.14 = (bf16[2,2,2,2,24,6912]{5,4,0,3,2,1:T(8,128)(2,1)}, bf16[2,2,2,2,24,6912]{5,4,0,3,2,1:T(8,128)(2,1)}, u32[]{:S(2)}, u32[]{:S(2)}) collective-permute-start(bf16[2,2,2,2,24,6912]{5,4,0,3,2,1:T(8,128)(2,1)} %bitcast.317), channel_id=1, source_target_pairs={{0,2},{1,3},{2,0},{3,1},{4,6},{5,7},{6,4},{7,5},{8,10},{9,11},{10,... | collective-permute-start | bytes 15925256 | tf_op jit(solution)/shard_map/ppermute | solution.py:320
  263.5 45.3 %collective-permute-start.15 = (bf16[2,2,2,24,3456]{4,3,0,2,1:T(8,128)(2,1)}, bf16[2,2,2,24,3456]{4,3,0,2,1:T(8,128)(2,1)}, u32[]{:S(2)}, u32[]{:S(2)}) collective-permute-start(bf16[2,2,2,24,3456]{4,3,0,2,1:T(8,128)(2,1)} %fusion.42), channel_id=1, source_target_pairs={{0,4},{1,5},{2,6},{3,7},{4,0},{5,1},{6,2},{7,3},{8,12},{9,13},{10,... | collective-permute-start | bytes 3981320 | tf_op jit(solution)/shard_map/ppermute | solution.py:320
  284.0 11.9 %collective-permute-start.23 = (bf16[750,256]{1,0:T(8,128)(2,1)}, bf16[750,256]{1,0:T(8,128)(2,1)S(1)}, u32[]{:S(2)}, u32[]{:S(2)}) collective-permute-start(bf16[750,256]{1,0:T(8,128)(2,1)} %fusion.68), channel_id=1, source_target_pairs={{0,1},{1,0},{2,3},{3,2},{4,5},{5,4},{6,7},{7,6},{8,9},{9,8},{10,11... | collective-permute-start | bytes 1152008 | tf_op jit(solution)/shard_map/ppermute | solution.py:513
  289.5 31.2 %collective-permute-start.16 = (bf16[2,2,2,24,3456]{4,3,0,2,1:T(8,128)(2,1)}, bf16[2,2,2,24,3456]{4,3,0,2,1:T(8,128)(2,1)}, u32[]{:S(2)}, u32[]{:S(2)}) collective-permute-start(bf16[2,2,2,24,3456]{4,3,0,2,1:T(8,128)(2,1)} %fusion.43), channel_id=1, source_target_pairs={{0,8},{1,9},{2,10},{3,11},{4,12},{5,13},{6,14},{7,15},{8,0},{9,1},... | collective-permute-start | bytes 3981320 | tf_op jit(solution)/shard_map/ppermute | solution.py:320
  297.7 22.9 %slice-start.2 = ((s8[5308416]{0:T(1024)(128)(4,1)}), s8[4194304]{0:T(1024)(128)(4,1)S(1)}, s32[]{:S(2)}) async-start(s8[5308416]{0:T(1024)(128)(4,1)} %bitcast.320), calls=%async_computation.3 | async-start | bytes 8388608
  297.8 22.9 %slice-start.3 = ((s8[5308416]{0:T(1024)(128)(4,1)}), s8[1114112]{0:T(1024)(128)(4,1)S(1)}, s32[]{:S(2)}) async-start(s8[5308416]{0:T(1024)(128)(4,1)} %bitcast.320), calls=%async_computation.4 | async-start | bytes 2228224
  322.3 15.9 %collective-permute-start.18 = (bf16[2,2,24,3456]{3,2,0,1:T(8,128)(2,1)S(1)}, bf16[2,2,24,3456]{3,2,0,1:T(8,128)(2,1)S(1)}, u32[]{:S(2)}, u32[]{:S(2)}) collective-permute-start(bf16[2,2,24,3456]{3,2,0,1:T(8,128)(2,1)S(1)} %fusion.70), channel_id=1, source_target_pairs={{0,4},{1,5},{2,6},{3,7},{4,0},{5,1},{6,2},{7,3},{8,12},{9,13},{10,... | collective-permute-start | bytes 1990664 | tf_op jit(solution)/shard_map/ppermute | solution.py:320
  324.3 12.5 %collective-permute-start.24 = (bf16[750,256]{1,0:T(8,128)(2,1)S(1)}, bf16[750,256]{1,0:T(8,128)(2,1)S(1)}, u32[]{:S(2)}, u32[]{:S(2)}) collective-permute-start(bf16[750,256]{1,0:T(8,128)(2,1)S(1)} %slice.578), channel_id=1, source_target_pairs={{0,1},{1,0},{2,3},{3,2},{4,5},{5,4},{6,7},{7,6},{8,9},{9,8},{10,11... | collective-permute-start | bytes 1152008 | tf_op jit(solution)/shard_map/ppermute | solution.py:513
  324.8 15.3 %collective-permute-start.17 = (bf16[2,2,24,3456]{3,2,0,1:T(8,128)(2,1)S(1)}, bf16[2,2,24,3456]{3,2,0,1:T(8,128)(2,1)S(1)}, u32[]{:S(2)}, u32[]{:S(2)}) collective-permute-start(bf16[2,2,24,3456]{3,2,0,1:T(8,128)(2,1)S(1)} %fusion.69), channel_id=1, source_target_pairs={{0,8},{1,9},{2,10},{3,11},{4,12},{5,13},{6,14},{7,15},{8,0},{9,1},... | collective-permute-start | bytes 1990664 | tf_op jit(solution)/shard_map/ppermute | solution.py:320
  340.3 15.9 %collective-permute-start.20 = (bf16[2,24,3456]{2,1,0:T(8,128)(2,1)S(1)}, bf16[2,24,3456]{2,1,0:T(8,128)(2,1)S(1)}, u32[]{:S(2)}, u32[]{:S(2)}) collective-permute-start(bf16[2,24,3456]{2,1,0:T(8,128)(2,1)S(1)} %fusion.73), channel_id=1, source_target_pairs={{0,1},{1,0},{2,3},{3,2},{4,5},{5,4},{6,7},{7,6},{8,9},{9,8},{10,11... | collective-permute-start | bytes 995336 | tf_op jit(solution)/shard_map/ppermute | solution.py:320
  341.8 14.5 %collective-permute-start.19 = (bf16[2,24,3456]{2,1,0:T(8,128)(2,1)S(1)}, bf16[2,24,3456]{2,1,0:T(8,128)(2,1)S(1)}, u32[]{:S(2)}, u32[]{:S(2)}) collective-permute-start(bf16[2,24,3456]{2,1,0:T(8,128)(2,1)S(1)} %fusion.72), channel_id=1, source_target_pairs={{0,1},{1,0},{2,3},{3,2},{4,5},{5,4},{6,7},{7,6},{8,9},{9,8},{10,11... | collective-permute-start | bytes 995336 | tf_op jit(solution)/shard_map/ppermute | solution.py:320
  353.9 21.2 %collective-permute-start.25 = (bf16[750,256]{1,0:T(8,128)(2,1)S(1)}, bf16[750,256]{1,0:T(8,128)(2,1)S(1)}, u32[]{:S(2)}, u32[]{:S(2)}) collective-permute-start(bf16[750,256]{1,0:T(8,128)(2,1)S(1)} %slice.577), channel_id=1, source_target_pairs={{0,1},{1,0},{2,3},{3,2},{4,5},{5,4},{6,7},{7,6},{8,9},{9,8},{10,11... | collective-permute-start | bytes 1152008 | tf_op jit(solution)/shard_map/ppermute | solution.py:513
  356.4 19.5 %collective-permute-start.22 = (bf16[24,3456]{1,0:T(8,128)(2,1)S(1)}, bf16[24,3456]{1,0:T(8,128)(2,1)S(1)}, u32[]{:S(2)}, u32[]{:S(2)}) collective-permute-start(bf16[24,3456]{1,0:T(8,128)(2,1)S(1)} %fusion.89), channel_id=1, source_target_pairs={{0,16},{1,17},{2,18},{3,19},{4,20},{5,21},{6,22},{7,23},{8,24},{9,... | collective-permute-start | bytes 497672 | tf_op jit(solution)/shard_map/ppermute | solution.py:320
  359.7 16.3 %collective-permute-start.21 = (bf16[24,3456]{1,0:T(8,128)(2,1)S(1)}, bf16[24,3456]{1,0:T(8,128)(2,1)S(1)}, u32[]{:S(2)}, u32[]{:S(2)}) collective-permute-start(bf16[24,3456]{1,0:T(8,128)(2,1)S(1)} %fusion.88), channel_id=1, source_target_pairs={{0,16},{1,17},{2,18},{3,19},{4,20},{5,21},{6,22},{7,23},{8,24},{9,... | collective-permute-start | bytes 497672 | tf_op jit(solution)/shard_map/ppermute | solution.py:320
  373.3 24.7 %collective-permute-start.26 = (bf16[750,256]{1,0:T(8,128)(2,1)}, bf16[750,256]{1,0:T(8,128)(2,1)}, u32[]{:S(2)}, u32[]{:S(2)}) collective-permute-start(bf16[750,256]{1,0:T(8,128)(2,1)} %slice.576), channel_id=1, source_target_pairs={{0,1},{1,0},{2,3},{3,2},{4,5},{5,4},{6,7},{7,6},{8,9},{9,8},{10,11... | collective-permute-start | bytes 1152008 | tf_op jit(solution)/shard_map/ppermute | solution.py:513
  380.1 12.6 %copy-start.47 = (f32[24,768]{1,0:T(8,128)}, f32[24,768]{1,0:T(8,128)S(1)}, u32[]{:S(2)}) copy-start(f32[24,768]{1,0:T(8,128)S(1)} %get-tuple-element.235) | copy-start | bytes 221188
  392.9 15.5 %collective-permute-start.28 = (bf16[750,256]{1,0:T(8,128)(2,1)S(1)}, bf16[750,256]{1,0:T(8,128)(2,1)S(1)}, u32[]{:S(2)}, u32[]{:S(2)}) collective-permute-start(bf16[750,256]{1,0:T(8,128)(2,1)S(1)} %fusion.63), channel_id=1, source_target_pairs={{0,1},{1,0},{2,3},{3,2},{4,5},{5,4},{6,7},{7,6},{8,9},{9,8},{10,11... | collective-permute-start | bytes 1152008 | tf_op jit(solution)/shard_map/ppermute | solution.py:513
  395.7 12.4 %collective-permute-start.27 = (bf16[750,256]{1,0:T(8,128)(2,1)S(1)}, bf16[750,256]{1,0:T(8,128)(2,1)S(1)}, u32[]{:S(2)}, u32[]{:S(2)}) collective-permute-start(bf16[750,256]{1,0:T(8,128)(2,1)S(1)} %slice.575), channel_id=1, source_target_pairs={{0,1},{1,0},{2,3},{3,2},{4,5},{5,4},{6,7},{7,6},{8,9},{9,8},{10,11... | collective-permute-start | bytes 1152008 | tf_op jit(solution)/shard_map/ppermute | solution.py:513
  419.2 8.3 %copy-start.41 = (bf16[768,1]{1,0:T(8,128)(2,1)S(1)}, bf16[768,1]{1,0:T(8,128)(2,1)}, u32[]{:S(2)}) copy-start(bf16[768,1]{1,0:T(8,128)(2,1)} %stack.422) | copy-start | bytes 4612
  437.0 3.9 collective-permute-start.29
  441.7 9.1 %collective-permute-start.38 = (bf16[2,2,2,24,768]{4,3,2,1,0:T(8,128)(2,1)S(1)}, bf16[2,2,2,24,768]{4,3,2,1,0:T(8,128)(2,1)S(1)}, u32[]{:S(2)}, u32[]{:S(2)}) collective-permute-start(bf16[2,2,2,24,768]{4,3,2,1,0:T(8,128)(2,1)S(1)} %fusion.83), channel_id=1, source_target_pairs={{0,8},{1,9},{2,10},{3,11},{4,12},{5,13},{6,14},{7,15},{8,0},{9,1},... | collective-permute-start | bytes 884744 | tf_op jit(solution)/shard_map/ppermute | solution.py:320
  445.6 9.1 %collective-permute-start.34 = (bf16[2,2,2,24,768]{4,3,2,1,0:T(8,128)(2,1)S(1)}, bf16[2,2,2,24,768]{4,3,2,1,0:T(8,128)(2,1)S(1)}, u32[]{:S(2)}, u32[]{:S(2)}) collective-permute-start(bf16[2,2,2,24,768]{4,3,2,1,0:T(8,128)(2,1)S(1)} %fusion.82), channel_id=1, source_target_pairs={{0,4},{1,5},{2,6},{3,7},{4,0},{5,1},{6,2},{7,3},{8,12},{9,13},{10,... | collective-permute-start | bytes 884744 | tf_op jit(solution)/shard_map/ppermute | solution.py:320
  447.4 11.0 %collective-permute-start.30 = (bf16[2,2,2,24,896]{4,3,2,1,0:T(8,128)(2,1)S(1)}, bf16[2,2,2,24,896]{4,3,2,1,0:T(8,128)(2,1)S(1)}, u32[]{:S(2)}, u32[]{:S(2)}) collective-permute-start(bf16[2,2,2,24,896]{4,3,2,1,0:T(8,128)(2,1)S(1)} %fusion.71), channel_id=1, source_target_pairs={{0,1},{1,0},{2,3},{3,2},{4,5},{5,4},{6,7},{7,6},{8,9},{9,8},{10,11... | collective-permute-start | bytes 1032200 | tf_op jit(solution)/shard_map/ppermute | solution.py:320
  450.9 9.5 %collective-permute-start.39 = (bf16[2,2,24,768]{3,2,1,0:T(8,128)(2,1)S(1)}, bf16[2,2,24,768]{3,2,1,0:T(8,128)(2,1)S(1)}, u32[]{:S(2)}, u32[]{:S(2)}) collective-permute-start(bf16[2,2,24,768]{3,2,1,0:T(8,128)(2,1)S(1)} %fusion.91), channel_id=1, source_target_pairs={{0,1},{1,0},{2,3},{3,2},{4,5},{5,4},{6,7},{7,6},{8,9},{9,8},{10,11... | collective-permute-start | bytes 442376 | tf_op jit(solution)/shard_map/ppermute | solution.py:320
  454.9 6.1 %collective-permute-start.35 = (bf16[2,2,24,768]{3,2,1,0:T(8,128)(2,1)S(1)}, bf16[2,2,24,768]{3,2,1,0:T(8,128)(2,1)S(1)}, u32[]{:S(2)}, u32[]{:S(2)}) collective-permute-start(bf16[2,2,24,768]{3,2,1,0:T(8,128)(2,1)S(1)} %fusion.90), channel_id=1, source_target_pairs={{0,8},{1,9},{2,10},{3,11},{4,12},{5,13},{6,14},{7,15},{8,0},{9,1},... | collective-permute-start | bytes 442376 | tf_op jit(solution)/shard_map/ppermute | solution.py:320
  458.4 13.3 %copy-start.66 = (f32[2,96]{1,0:T(2,128)S(1)}, f32[2,96]{1,0:T(2,128)}, u32[]{:S(2)}) copy-start(f32[2,96]{1,0:T(2,128)} %param.26) | copy-start | bytes 2308
  458.4 13.3 %copy-start.69 = (f32[96]{0:T(128)S(1)}, f32[96]{0:T(128)}, u32[]{:S(2)}) copy-start(f32[96]{0:T(128)} %param.20) | copy-start | bytes 1156
  458.4 13.8 %copy-start.50 = (f32[24,8]{1,0:T(8,128)S(1)}, f32[24,8]{1,0:T(8,128)}, u32[]{:S(2)}) copy-start(f32[24,8]{1,0:T(8,128)} %copy.152) | copy-start | bytes 2308
  458.5 13.8 %copy-start.51 = (f32[1,24,8]{2,1,0:T(8,128)S(1)}, f32[1,24,8]{2,1,0:T(8,128)}, u32[]{:S(2)}) copy-start(f32[1,24,8]{2,1,0:T(8,128)} %copy.162) | copy-start | bytes 2308
  458.5 13.8 %copy-start.52 = (f32[1,24,8]{2,1,0:T(8,128)S(1)}, f32[1,24,8]{2,1,0:T(8,128)}, u32[]{:S(2)}) copy-start(f32[1,24,8]{2,1,0:T(8,128)} %copy.161) | copy-start | bytes 2308
  458.5 10.2 %collective-permute-start.31 = (bf16[2,2,24,896]{3,2,1,0:T(8,128)(2,1)S(1)}, bf16[2,2,24,896]{3,2,1,0:T(8,128)(2,1)S(1)}, u32[]{:S(2)}, u32[]{:S(2)}) collective-permute-start(bf16[2,2,24,896]{3,2,1,0:T(8,128)(2,1)S(1)} %fusion.87), channel_id=1, source_target_pairs={{0,4},{1,5},{2,6},{3,7},{4,0},{5,1},{6,2},{7,3},{8,12},{9,13},{10,... | collective-permute-start | bytes 516104 | tf_op jit(solution)/shard_map/ppermute | solution.py:320
  460.5 18.5 %copy-start.37 = (f32[2,24,2304]{2,1,0:T(8,128)S(1)}, f32[2,24,2304]{2,1,0:T(8,128)}, u32[]{:S(2)}) copy-start(f32[2,24,2304]{2,1,0:T(8,128)} %param.22) | copy-start | bytes 1327108
  460.5 5.1 %collective-permute-start.40 = (bf16[2,24,768]{2,1,0:T(8,128)(2,1)S(1)}, bf16[2,24,768]{2,1,0:T(8,128)(2,1)S(1)}, u32[]{:S(2)}, u32[]{:S(2)}) collective-permute-start(bf16[2,24,768]{2,1,0:T(8,128)(2,1)S(1)} %fusion.96), channel_id=1, source_target_pairs={{0,4},{1,5},{2,6},{3,7},{4,0},{5,1},{6,2},{7,3},{8,12},{9,13},{10,... | collective-permute-start | bytes 221192 | tf_op jit(solution)/shard_map/ppermute | solution.py:320
  461.0 18.1 %copy-start.40 = (f32[24,2304]{1,0:T(8,128)S(1)}, f32[24,2304]{1,0:T(8,128)}, u32[]{:S(2)}) copy-start(f32[24,2304]{1,0:T(8,128)} %param.16) | copy-start | bytes 663556
  461.1 7.2 %collective-permute-start.36 = (bf16[2,24,768]{2,1,0:T(8,128)(2,1)S(1)}, bf16[2,24,768]{2,1,0:T(8,128)(2,1)S(1)}, u32[]{:S(2)}, u32[]{:S(2)}) collective-permute-start(bf16[2,24,768]{2,1,0:T(8,128)(2,1)S(1)} %fusion.95), channel_id=1, source_target_pairs={{0,1},{1,0},{2,3},{3,2},{4,5},{5,4},{6,7},{7,6},{8,9},{9,8},{10,11... | collective-permute-start | bytes 221192 | tf_op jit(solution)/shard_map/ppermute | solution.py:320
  465.6 5.8 %collective-permute-start.41 = (bf16[24,768]{1,0:T(8,128)(2,1)S(1)}, bf16[24,768]{1,0:T(8,128)(2,1)S(1)}, u32[]{:S(2)}, u32[]{:S(2)}) collective-permute-start(bf16[24,768]{1,0:T(8,128)(2,1)S(1)} %fusion.102), channel_id=1, source_target_pairs={{0,16},{1,17},{2,18},{3,19},{4,20},{5,21},{6,22},{7,23},{8,24},{9,... | collective-permute-start | bytes 110600 | tf_op jit(solution)/shard_map/ppermute | solution.py:320
  468.3 5.0 %collective-permute-start.37 = (bf16[24,768]{1,0:T(8,128)(2,1)S(1)}, bf16[24,768]{1,0:T(8,128)(2,1)S(1)}, u32[]{:S(2)}, u32[]{:S(2)}) collective-permute-start(bf16[24,768]{1,0:T(8,128)(2,1)S(1)} %fusion.101), channel_id=1, source_target_pairs={{0,16},{1,17},{2,18},{3,19},{4,20},{5,21},{6,22},{7,23},{8,24},{9,... | collective-permute-start | bytes 110600 | tf_op jit(solution)/shard_map/ppermute | solution.py:320
  468.8 5.2 %collective-permute-start.32 = (bf16[2,24,896]{2,1,0:T(8,128)(2,1)S(1)}, bf16[2,24,896]{2,1,0:T(8,128)(2,1)S(1)}, u32[]{:S(2)}, u32[]{:S(2)}) collective-permute-start(bf16[2,24,896]{2,1,0:T(8,128)(2,1)S(1)} %fusion.92), channel_id=1, source_target_pairs={{0,8},{1,9},{2,10},{3,11},{4,12},{5,13},{6,14},{7,15},{8,0},{9,1},... | collective-permute-start | bytes 258056 | tf_op jit(solution)/shard_map/ppermute | solution.py:320
  471.6 9.1 %copy-start.68 = (f32[96]{0:T(128)}, f32[96]{0:T(128)S(1)}, u32[]{:S(2)}) copy-start(f32[96]{0:T(128)S(1)} %reshape.1157) | copy-start | bytes 1156
  474.0 5.0 %collective-permute-start.33 = (bf16[24,896]{1,0:T(8,128)(2,1)S(1)}, bf16[24,896]{1,0:T(8,128)(2,1)S(1)}, u32[]{:S(2)}, u32[]{:S(2)}) collective-permute-start(bf16[24,896]{1,0:T(8,128)(2,1)S(1)} %fusion.100), channel_id=1, source_target_pairs={{0,16},{1,17},{2,18},{3,19},{4,20},{5,21},{6,22},{7,23},{8,24},{9,... | collective-permute-start | bytes 129032 | tf_op jit(solution)/shard_map/ppermute | solution.py:320
  (55 other events, 177.6 us)
Sparse Core Ops, SparseCore 0:
  11.5 107.4 all-gather.1

commit v17 on v14

--- a/solution.py
+++ b/solution.py
@@ -54,7 +54,7 @@
     )
 
 
-QUERY_CHUNK = 256
+QUERY_CHUNK = 128
 MASKED = -1e30
 
 

time: 486 us -> 519 us (1.068)
  Pallas kernels: 102 us -> 142 us
  waiting for transfers between devices: 84.2 us -> 75.6 us
    pallas_call x6, Pallas kernels: 64.8 us -> 89.9 us  [attention_pallas(): pl.pallas_call(attention_backward_kernel, grid=(span,), in_specs=[qi_spec...]
    pallas_call x1, Pallas kernels: 37.4 us -> 51.6 us  [attention_pallas(): pl.pallas_call(attention_forward_kernel, grid=(pair_count,), in_specs=[q_...]
    ppermute x22, waiting for transfers between devices: 31.4 us -> 22 us  [tree_reduce_scatter(): got = lax.ppermute(send, ('clip', 'frame'), pairs)]
  transfers between devices with their start and end apart: 43 -> 43, of which waited for: 22 -> 18; matrix products, arithmetic and copies ran while one was open for 17% -> 15% of each run, Pallas kernels for 21% -> 28%
where the time goes in v17:
time: 519 us; the launch traced here: 514 us
  Pallas kernels  142 us (27%)
  local copies, waits for them, and re-layouts  94.6 us (18%)
  waiting for transfers between devices  75.6 us (15%)
  matrix products  72.7 us (14%)
  other arithmetic  60.5 us (12%)
  starting transfers between devices  53 us (10%)
  between operations  16.2 us (3%)
    pallas_call x6, Pallas kernels, attention_pallas(): pl.pallas_call(attention_backward_kernel, grid=(span,), in_specs=[qi_spec...  89.9 us
    pallas_call x1, Pallas kernels, attention_pallas(): pl.pallas_call(attention_forward_kernel, grid=(pair_count,), in_specs=[q_...  51.6 us
    ppermute x13, waiting for transfers between devices, double(): got = lax.ppermute(data, ('clip', 'frame'), pairs)  42 us
    unnamed x178, local copies, waits for them, and re-layouts  28.2 us
    ppermute x22, starting transfers between devices, tree_reduce_scatter(): got = lax.ppermute(send, ('clip', 'frame'), pairs)  23.9 us
    ppermute x22, waiting for transfers between devices, tree_reduce_scatter(): got = lax.ppermute(send, ('clip', 'frame'), pairs)  22 us
    ppermute x13, starting transfers between devices, double(): got = lax.ppermute(data, ('clip', 'frame'), pairs)  19.5 us
    ppermute x6, waiting for transfers between devices, body(): lax.ppermute(terms[row_count:].astype(jnp.bfloat16), 'frame', swap)  11.5 us
  transfers between devices with their start and end apart: 43, of which 18 were waited for; matrix products, arithmetic and copies ran while one was open for 15% of the time, Pallas kernels for 28%

profile of v17, /device:TPU:0, one launch (start us, length us, event | category | flops | bytes accessed | tf_op | source)
XLA Modules:
  0.0 514.0 jit_solution(14087326056758053619)
XLA Ops:
  12.8 4.1 collective-permute-start.8
  17.0 3.0 collective-permute-start
  25.5 29.5 %collective-permute-done.5 = bf16[2,24,768]{2,1,0:T(8,128)(2,1)S(1)} collective-permute-done((bf16[2,24,768]{2,1,0:T(8,128)(2,1)S(1)}, bf16[2,24,768]{2,1,0:T(8,128)(2,1)S(1)}, u32[]{:S(2)}, u32[]{:S(2)}) %collective-permute-start.5) | collective-permute-done | bytes 73760 | tf_op jit(solution)/shard_map/ppermute | solution.py:339
  60.1 1.8 collective-permute-done.10
  62.4 3.4 collective-permute-done.6
  69.4 3.2 collective-permute-done.7
  72.8 4.0 collective-permute-done.3
  80.8 1.7 fusion.37
  83.2 3.2 maximum_select_fusion
  86.4 1.9 copy-done.15
  90.3 5.5 %add_convert_fusion = bf16[750,2304]{1,0:T(8,128)(2,1)S(1)} fusion(f32[2304]{0:T(1024)S(1)} %pad_maximum_fusion.16, bf16[768,2432]{1,0:T(8,128)(2,1)} %bitcast.326, bf16[1,750,768]{2,1,0:T(8,128)(2,1)S(1)} %copy-done.2, f32[768]{0:T(1024)S(1)} %get-tuple-element.226, f32[768]{0:T(1024)S(1)} %get-tuple-element.227, f32[750]{0:T(1024)S(1)} %add_rsqrt_fusion.2, ...), kind=kOutput, calls=%fused_computation.14 | convolution fusion | flops 2661120000 | bytes 8168304 | tf_op jit(solution)/shard_map/dot_general | solution.py:431
  99.2 3.5 add_convert_fusion.1
  102.7 2.7 fusion.8.k_ref.v_ref
  105.4 51.6 %shard_map.293 = (bf16[768,768]{1,0:T(8,128)(2,1)S(1)}, f32[768,768]{1,0:T(8,128)S(1)}) custom-call(bf16[768,768]{1,0:T(8,128)(2,1)S(1)} %pad.39.q_ref, bf16[1536,1536]{1,0:T(8,128)(2,1)} %fusion.8.k_ref.v_ref, bf16[1536,1536]{1,0:T(8,128)(2,1)} %fusion.8.k_ref.v_ref, f32[1,1536]{1,0:T(1,128)S(1)} %compare_select_fusion.kbias_ref), custom_call_target="tpu_custom_call" | custom-call | tf_op jit(solution)/shard_map/pallas_call | solution.py:161
  158.4 2.5 fusion.121
  162.7 4.8 slice.408
  167.5 8.5 %reshape.1150 = bf16[3072,768]{1,0:T(8,128)(2,1)} reshape(bf16[768,3072]{1,0:T(8,128)(2,1)} %slice.408) | data formatting | bytes 9437184 | tf_op jit(solution)/shard_map/reshape | solution.py:416
  176.0 9.1 %multiply_convert_fusion = (bf16[750,3072]{1,0:T(8,128)(2,1)S(1)}, f32[750,3072]{1,0:T(8,128)}) fusion(f32[3072]{0:T(1024)S(1)} %add.429, bf16[768,6912]{1,0:T(8,128)(2,1)} %all-gather.2.cloned.1.call-done, f32[750,768]{1,0:T(8,128)} %copy-done.6, f32[768]{0:T(1024)S(1)} %get-tuple-element.221, f32[768]{0:T(1024)S(1)} %get-tuple-element.222, ...), kind=kOutput, calls=%fused_computation.12 | convolution fusion | flops 3555648000 | bytes 20877168 | tf_op jit(solution)/shard_map/dot_general | solution.py:451
  185.0 2.2 copy-done.71
  187.2 6.3 %convolution_convert_fusion.2 = bf16[3072,768]{1,0:T(8,128)(2,1)} fusion(bf16[750,3072]{1,0:T(8,128)(2,1)S(1)} %get-tuple-element.279, bf16[1,750,768]{2,1,0:T(8,128)(2,1)S(1)} %copy-done.14), kind=kOutput, calls=%fused_computation.19 | convolution fusion | flops 3541303296 | bytes 10478592 | tf_op jit(solution)/shard_map/dot_general | solution.py:461
  193.4 8.5 %concatenate.309 = bf16[2,2,2,2,2,24,3072]{6,5,4,3,2,1,0:T(8,128)(2,1)} reshape(bf16[3072,768]{1,0:T(8,128)(2,1)} %convolution_convert_fusion.2) | data formatting | bytes 9437184 | tf_op jit(solution)/shard_map/concatenate | solution.py:481
  201.9 9.4 %fusion.122 = (bf16[3072]{0:T(1024)(128)(2,1)S(1)}, bf16[750,3072]{1,0:T(8,128)(2,1)S(1)}) fusion(f32[750,3072]{1,0:T(8,128)} %get-tuple-element.280, f32[3072]{0:T(1024)S(1)} %add.429, bf16[3072,768]{1,0:T(8,128)(2,1)} %reshape.1150, bf16[1,750,768]{2,1,0:T(8,128)(2,1)S(1)} %copy-done.14), kind=kOutput, calls=%fused_computation.323 | convolution fusion | flops 3566588928 | bytes 19713024 | tf_op jit(solution)/shard_map/dot_general | solution.py:465
  211.4 5.0 convolution_convert_fusion.1
  216.4 7.3 %multiply_reduce_fusion = (bf16[768]{0:T(1024)(128)(2,1)}, f32[750]{0:T(1024)S(1)}, f32[750]{0:T(1024)S(1)}, bf16[768]{0:T(1024)(128)(2,1)S(1)}, f32[750,768]{1,0:T(8,128)S(1)}) fusion(f32[750,768]{1,0:T(8,128)S(1)} %copy-done.7, f32[750]{0:T(1024)S(1)} %add_rsqrt_fusion, f32[750]{0:T(1024)S(1)} %broadcast_multiply_fusion.4, ...), kind=kOutput, calls=%fused_computation.64 | convolution fusion | flops 3544124928 | bytes 13952736 | tf_op jit(solution)/shard_map/dot_general | solution.py:471
  226.8 8.1 %pad_maximum_fusion = bf16[2,2,2,2,2,24,6912]{6,5,4,3,2,1,0:T(8,128)(2,1)} fusion(bf16[2,2,2,2,2,24,768]{6,5,4,3,2,1,0:T(8,128)(2,1)S(1)} %bitcast.330, bf16[2,2,2,2,2,24,3072]{6,5,4,3,2,1,0:T(8,128)(2,1)S(1)} %bitcast.324, bf16[2,2,2,2,2,24,3072]{6,5,4,3,2,1,0:T(8,128)(2,1)S(1)} %bitcast.319), kind=kLoop, calls=%fused_computation.1 | loop fusion | flops 31850496 | bytes 21233664 | tf_op jit(solution)/shard_map/concatenate | solution.py:481
  234.9 8.7 %constant_dynamic-slice_fusion.1 = (bf16[2,2,2,1,2,24,6912]{6,5,4,3,2,1,0:T(8,128)(2,1)}, bf16[2,2,2,1,2,24,6912]{6,5,4,3,2,1,0:T(8,128)(2,1)}) fusion(bf16[2,2,2,2,2,24,6912]{6,5,4,3,2,1,0:T(8,128)(2,1)} %pad_maximum_fusion, s32[]{:T(128)S(6)} %select_n.403, s32[]{:T(128)S(6)} %select_n.404), kind=kLoop, calls=%fused_computation.282 | loop fusion | bytes 21233672 | tf_op jit(solution)/shard_map/jit(dynamic_index_in_dim)/dynamic_slice | solution.py:313
  243.6 5.2 %copy.175 = bf16[2,2,2,1,2,24,6912]{6,5,0,4,2,1,3:T(8,128)(2,1)} copy(bf16[2,2,2,1,2,24,6912]{6,5,4,3,2,1,0:T(8,128)(2,1)} %get-tuple-element.239) | data formatting | bytes 10616832
  252.6 3.1 convolution_convert_fusion.4
  255.7 2.6 collective-permute-done.14
  258.2 5.3 %convert_add_fusion = f32[2,2,2,2,24,6912]{5,4,0,3,2,1:T(8,128)S(1)} fusion(bf16[2,2,2,2,24,6912]{5,4,0,3,2,1:T(8,128)(2,1)} %collective-permute-done.14, bf16[2,2,2,1,2,24,6912]{6,5,4,3,2,1,0:T(8,128)(2,1)} %get-tuple-element.238), kind=kLoop, calls=%fused_computation.2 | loop fusion | flops 7962624 | bytes 21233664 | tf_op jit(solution)/shard_map/add | solution.py:321
  263.6 4.9 fusion.117
  268.5 3.1 fusion.42
  271.6 8.5 %fusion.41 = bf16[1,750,768]{2,1,0:T(8,128)(2,1)} fusion(f32[750,768]{1,0:T(8,128)S(1)} %copy-done.8, bf16[750,3072]{1,0:T(8,128)(2,1)} %copy-done.71, bf16[3072,768]{1,0:T(8,128)(2,1)} %reshape.1150, f32[768]{0:T(1024)S(1)} %copy-done.63), kind=kOutput, calls=%fused_computation.82 | convolution fusion | flops 3540672000 | bytes 12785664 | tf_op jit(solution)/shard_map/dot_general | solution.py:455
  280.2 15.1 %shard_map.294 = (f32[768,128]{1,0:T(8,128)S(1)}, f32[1536,128]{1,0:T(8,128)S(1)}, f32[1536,128]{1,0:T(8,128)S(1)}) custom-call(bf16[768,768]{1,0:T(8,128)(2,1)S(1)} %pad.39.q_ref, bf16[1536,1536]{1,0:T(8,128)(2,1)} %fusion.8.k_ref.v_ref, bf16[1536,1536]{1,0:T(8,128)(2,1)} %fusion.8.k_ref.v_ref, bf16[768,768]{1,0:T(8,128)(2,1)S(1)} %pad.41.do_ref, ...), custom_call_target="tpu_custom_call" | custom-call | tf_op jit(solution)/shard_map/pallas_call | solution.py:180
  296.2 2.3 collective-permute-start.23
  298.5 3.0 fusion.43
  306.0 2.2 collective-permute-done.23
  308.2 1.8 fusion.62
  310.1 15.0 %shard_map.295 = (f32[768,128]{1,0:T(8,128)S(1)}, f32[1536,128]{1,0:T(8,128)S(1)}, f32[1536,128]{1,0:T(8,128)S(1)}) custom-call(bf16[768,768]{1,0:T(8,128)(2,1)S(1)} %pad.39.q_ref, bf16[1536,1536]{1,0:T(8,128)(2,1)} %fusion.8.k_ref.v_ref, bf16[1536,1536]{1,0:T(8,128)(2,1)} %fusion.8.k_ref.v_ref, bf16[768,768]{1,0:T(8,128)(2,1)S(1)} %pad.42.do_ref, ...), custom_call_target="tpu_custom_call" | custom-call | tf_op jit(solution)/shard_map/pallas_call | solution.py:180
  325.3 2.4 bitcast_add_fusion.1
  327.6 5.3 %collective-permute-done.16 = bf16[2,2,2,24,3456]{4,3,0,2,1:T(8,128)(2,1)} collective-permute-done((bf16[2,2,2,24,3456]{4,3,0,2,1:T(8,128)(2,1)}, bf16[2,2,2,24,3456]{4,3,0,2,1:T(8,128)(2,1)}, u32[]{:S(2)}, u32[]{:S(2)}) %collective-permute-start.16) | collective-permute-done | bytes 1327136 | tf_op jit(solution)/shard_map/ppermute | solution.py:320
  334.6 1.8 collective-permute-start.18
  337.5 14.9 %shard_map.296 = (f32[768,128]{1,0:T(8,128)S(1)}, f32[1536,128]{1,0:T(8,128)S(1)}, f32[1536,128]{1,0:T(8,128)S(1)}) custom-call(bf16[768,768]{1,0:T(8,128)(2,1)S(1)} %pad.39.q_ref, bf16[1536,1536]{1,0:T(8,128)(2,1)} %fusion.8.k_ref.v_ref, bf16[1536,1536]{1,0:T(8,128)(2,1)} %fusion.8.k_ref.v_ref, bf16[768,768]{1,0:T(8,128)(2,1)S(1)} %pad.43.do_ref, ...), custom_call_target="tpu_custom_call" | custom-call | tf_op jit(solution)/shard_map/pallas_call | solution.py:180
  354.7 1.8 collective-permute-start.20
  356.9 14.9 %shard_map.297 = (f32[768,128]{1,0:T(8,128)S(1)}, f32[1536,128]{1,0:T(8,128)S(1)}, f32[1536,128]{1,0:T(8,128)S(1)}) custom-call(bf16[768,768]{1,0:T(8,128)(2,1)S(1)} %pad.39.q_ref, bf16[1536,1536]{1,0:T(8,128)(2,1)} %fusion.8.k_ref.v_ref, bf16[1536,1536]{1,0:T(8,128)(2,1)} %fusion.8.k_ref.v_ref, bf16[768,768]{1,0:T(8,128)(2,1)S(1)} %pad.44.do_ref, ...), custom_call_target="tpu_custom_call" | custom-call | tf_op jit(solution)/shard_map/pallas_call | solution.py:180
  372.1 1.8 collective-permute-start.25
  375.0 2.9 collective-permute-start.21
  378.1 15.3 %shard_map.298 = (f32[768,128]{1,0:T(8,128)S(1)}, f32[1536,128]{1,0:T(8,128)S(1)}, f32[1536,128]{1,0:T(8,128)S(1)}) custom-call(bf16[768,768]{1,0:T(8,128)(2,1)S(1)} %pad.39.q_ref, bf16[1536,1536]{1,0:T(8,128)(2,1)} %fusion.8.k_ref.v_ref, bf16[1536,1536]{1,0:T(8,128)(2,1)} %fusion.8.k_ref.v_ref, bf16[768,768]{1,0:T(8,128)(2,1)S(1)} %pad.45.do_ref, ...), custom_call_target="tpu_custom_call" | custom-call | tf_op jit(solution)/shard_map/pallas_call | solution.py:180
  403.8 14.9 %shard_map.299 = (f32[768,128]{1,0:T(8,128)S(1)}, f32[1536,128]{1,0:T(8,128)S(1)}, f32[1536,128]{1,0:T(8,128)S(1)}) custom-call(bf16[768,768]{1,0:T(8,128)(2,1)S(1)} %pad.39.q_ref, bf16[1536,1536]{1,0:T(8,128)(2,1)} %fusion.8.k_ref.v_ref, bf16[1536,1536]{1,0:T(8,128)(2,1)} %fusion.8.k_ref.v_ref, bf16[768,768]{1,0:T(8,128)(2,1)S(1)} %pad.46.do_ref, ...), custom_call_target="tpu_custom_call" | custom-call | tf_op jit(solution)/shard_map/pallas_call | solution.py:180
  418.9 1.8 collective-permute-start.28
  425.8 9.3 %collective-permute-done.27 = bf16[750,256]{1,0:T(8,128)(2,1)S(1)} collective-permute-done((bf16[750,256]{1,0:T(8,128)(2,1)S(1)}, bf16[750,256]{1,0:T(8,128)(2,1)S(1)}, u32[]{:S(2)}, u32[]{:S(2)}) %collective-permute-start.27) | collective-permute-done | bytes 384032 | tf_op jit(solution)/shard_map/ppermute | solution.py:512
  435.8 1.8 copy-done.13
  439.0 4.6 fusion.32
  443.6 2.5 reduce.2
  446.2 6.8 %convolution_convert_fusion = bf16[768,2304]{1,0:T(8,128)(2,1)} fusion(bf16[750,2304]{1,0:T(8,128)(2,1)} %copy-done.13, bf16[1,750,768]{2,1,0:T(8,128)(2,1)S(1)} %copy-done.3, f32[768]{0:T(1024)S(1)} %copy-done.62, f32[768]{0:T(1024)S(1)} %copy-done.56, f32[750]{0:T(1024)S(1)} %copy-done.58, f32[750]{0:T(1024)S(1)} %copy-done.54), kind=kOutput, calls=%fused_computation.17 | convolution fusion | flops 2659433472 | bytes 8159088 | tf_op jit(solution)/shard_map/dot_general | solution.py:528
  454.4 7.9 %concatenate.321 = bf16[768,2432]{1,0:T(8,128)(2,1)} concatenate(bf16[768,2304]{1,0:T(8,128)(2,1)} %convolution_convert_fusion, bf16[768,1]{1,0:T(8,128)(2,1)S(1)} %stack.415, bf16[768,1]{1,0:T(8,128)(2,1)S(1)} %stack.416, bf16[768,1]{1,0:T(8,128)(2,1)S(1)} %stack.417, bf16[768,1]{1,0:T(8,128)(2,1)S(1)} %stack.418, bf16[768,1]{1,0:T(8,128)(2,1)S(1)} %copy-done.43, ...), dimensions={1} | concatenate | bytes 7471104 | tf_op jit(solution)/shard_map/concatenate | solution.py:561
  462.4 1.8 dynamic-slice_bitcast_fusion
  470.8 1.8 fusion.46
  475.7 2.3 collective-permute-done.38
  479.5 2.4 collective-permute-done.34
  483.5 1.7 collective-permute-done.30
  489.7 2.8 collective-permute-done.40
  493.0 2.6 collective-permute-start.37
  503.2 2.1 collective-permute-done.33
  (427 shorter events, 98.6 us)
Async XLA Ops:
  7.2 12.8 %copy-start.2 = (bf16[1,750,768]{2,1,0:T(8,128)(2,1)S(1)}, bf16[1,750,768]{2,1,0:T(8,128)(2,1)}, u32[]{:S(2)}) copy-start(bf16[1,750,768]{2,1,0:T(8,128)(2,1)} %param.14) | copy-start | bytes 3456004
  7.2 151.2 %all-gather.2.cloned.1.call-start = ((), (), s32[]{:S(2)}) async-start(), calls=%async_computation | async-start | bytes 10948608 | tf_op jit(solution)/shard_map/all_gather | solution.py:409
  12.8 8.7 %collective-permute-start.8 = (bf16[24,768]{1,0:T(8,128)(2,1)S(1)}, bf16[24,768]{1,0:T(8,128)(2,1)S(1)}, u32[]{:S(2)}, u32[]{:S(2)}) collective-permute-start(bf16[24,768]{1,0:T(8,128)(2,1)S(1)} %get-tuple-element.259), channel_id=1, source_target_pairs={{0,16},{1,17},{2,18},{3,19},{4,20},{5,21},{6,22},{7,23},{8,24},{9,... | collective-permute-start | bytes 110600 | tf_op jit(solution)/shard_map/ppermute | solution.py:339
  16.9 6.2 %collective-permute-start.4 = (bf16[24,768]{1,0:T(8,128)(2,1)S(1)}, bf16[24,768]{1,0:T(8,128)(2,1)S(1)}, u32[]{:S(2)}, u32[]{:S(2)}) collective-permute-start(bf16[24,768]{1,0:T(8,128)(2,1)S(1)} %get-tuple-element.265), channel_id=1, source_target_pairs={{0,16},{1,17},{2,18},{3,19},{4,20},{5,21},{6,22},{7,23},{8,24},{9,... | collective-permute-start | bytes 110600 | tf_op jit(solution)/shard_map/ppermute | solution.py:339
  17.0 6.9 %collective-permute-start = (bf16[24,896]{1,0:T(8,128)(2,1)S(1)}, bf16[24,896]{1,0:T(8,128)(2,1)S(1)}, u32[]{:S(2)}, u32[]{:S(2)}) collective-permute-start(bf16[24,896]{1,0:T(8,128)(2,1)S(1)} %get-tuple-element.262), channel_id=1, source_target_pairs={{0,16},{1,17},{2,18},{3,19},{4,20},{5,21},{6,22},{7,23},{8,24},{9,... | collective-permute-start | bytes 129032 | tf_op jit(solution)/shard_map/ppermute | solution.py:339
  20.0 59.3 %collective-permute-start.13 = (bf16[1,750,768]{2,1,0:T(8,128)(2,1)S(1)}, bf16[1,750,768]{2,1,0:T(8,128)(2,1)}, u32[]{:S(2)}, u32[]{:S(2)}) collective-permute-start(bf16[1,750,768]{2,1,0:T(8,128)(2,1)S(1)} %copy-done.2), channel_id=1, source_target_pairs={{0,1},{1,0},{2,3},{3,2},{4,5},{5,4},{6,7},{7,6},{8,9},{9,8},{10,11... | collective-permute-start | bytes 3456008 | tf_op jit(solution)/shard_map/ppermute | solution.py:423
  21.6 35.1 %collective-permute-start.9 = (bf16[2,24,768]{2,1,0:T(8,128)(2,1)S(1)}, bf16[2,24,768]{2,1,0:T(8,128)(2,1)S(1)}, u32[]{:S(2)}, u32[]{:S(2)}) collective-permute-start(bf16[2,24,768]{2,1,0:T(8,128)(2,1)S(1)} %maximum_select_fusion.18), channel_id=1, source_target_pairs={{0,4},{1,5},{2,6},{3,7},{4,0},{5,1},{6,2},{7,3},{8,12},{9,13},{10,... | collective-permute-start | bytes 221192 | tf_op jit(solution)/shard_map/ppermute | solution.py:339
  23.2 31.8 %collective-permute-start.5 = (bf16[2,24,768]{2,1,0:T(8,128)(2,1)S(1)}, bf16[2,24,768]{2,1,0:T(8,128)(2,1)S(1)}, u32[]{:S(2)}, u32[]{:S(2)}) collective-permute-start(bf16[2,24,768]{2,1,0:T(8,128)(2,1)S(1)} %maximum_select_fusion.17), channel_id=1, source_target_pairs={{0,1},{1,0},{2,3},{3,2},{4,5},{5,4},{6,7},{7,6},{8,9},{9,8},{10,11... | collective-permute-start | bytes 221192 | tf_op jit(solution)/shard_map/ppermute | solution.py:339
  23.9 34.4 %collective-permute-start.1 = (bf16[2,24,896]{2,1,0:T(8,128)(2,1)S(1)}, bf16[2,24,896]{2,1,0:T(8,128)(2,1)S(1)}, u32[]{:S(2)}, u32[]{:S(2)}) collective-permute-start(bf16[2,24,896]{2,1,0:T(8,128)(2,1)S(1)} %maximum_select_fusion.15), channel_id=1, source_target_pairs={{0,8},{1,9},{2,10},{3,11},{4,12},{5,13},{6,14},{7,15},{8,0},{9,1},... | collective-permute-start | bytes 258056 | tf_op jit(solution)/shard_map/ppermute | solution.py:339
  55.0 10.8 %collective-permute-start.6 = (bf16[2,2,24,768]{3,2,0,1:T(8,128)(2,1)S(1)}, bf16[2,2,24,768]{3,2,0,1:T(8,128)(2,1)S(1)}, u32[]{:S(2)}, u32[]{:S(2)}) collective-permute-start(bf16[2,2,24,768]{3,2,0,1:T(8,128)(2,1)S(1)} %maximum_select_fusion.12), channel_id=1, source_target_pairs={{0,8},{1,9},{2,10},{3,11},{4,12},{5,13},{6,14},{7,15},{8,0},{9,1},... | collective-permute-start | bytes 442376 | tf_op jit(solution)/shard_map/ppermute | solution.py:339
  56.7 5.2 %collective-permute-start.10 = (bf16[2,2,24,768]{3,2,1,0:T(8,128)(2,1)S(1)}, bf16[2,2,24,768]{3,2,1,0:T(8,128)(2,1)S(1)}, u32[]{:S(2)}, u32[]{:S(2)}) collective-permute-start(bf16[2,2,24,768]{3,2,1,0:T(8,128)(2,1)S(1)} %maximum_select_fusion.13), channel_id=1, source_target_pairs={{0,1},{1,0},{2,3},{3,2},{4,5},{5,4},{6,7},{7,6},{8,9},{9,8},{10,11... | collective-permute-start | bytes 442376 | tf_op jit(solution)/shard_map/ppermute | solution.py:339
  58.5 9.1 %collective-permute-start.2 = (bf16[2,2,24,896]{3,2,0,1:T(8,128)(2,1)S(1)}, bf16[2,2,24,896]{3,2,0,1:T(8,128)(2,1)S(1)}, u32[]{:S(2)}, u32[]{:S(2)}) collective-permute-start(bf16[2,2,24,896]{3,2,0,1:T(8,128)(2,1)S(1)} %maximum_select_fusion.10), channel_id=1, source_target_pairs={{0,4},{1,5},{2,6},{3,7},{4,0},{5,1},{6,2},{7,3},{8,12},{9,13},{10,... | collective-permute-start | bytes 516104 | tf_op jit(solution)/shard_map/ppermute | solution.py:339
  61.9 10.8 %collective-permute-start.11 = (bf16[2,2,2,24,768]{4,3,2,1,0:T(8,128)(2,1)S(1)}, bf16[2,2,2,24,768]{4,3,2,1,0:T(8,128)(2,1)S(1)}, u32[]{:S(2)}, u32[]{:S(2)}) collective-permute-start(bf16[2,2,2,24,768]{4,3,2,1,0:T(8,128)(2,1)S(1)} %maximum_select_fusion.8), channel_id=1, source_target_pairs={{0,8},{1,9},{2,10},{3,11},{4,12},{5,13},{6,14},{7,15},{8,0},{9,1},... | collective-permute-start | bytes 884744 | tf_op jit(solution)/shard_map/ppermute | solution.py:339
  65.9 6.8 %collective-permute-start.7 = (bf16[2,2,2,24,768]{4,3,0,2,1:T(8,128)(2,1)S(1)}, bf16[2,2,2,24,768]{4,3,0,2,1:T(8,128)(2,1)S(1)}, u32[]{:S(2)}, u32[]{:S(2)}) collective-permute-start(bf16[2,2,2,24,768]{4,3,0,2,1:T(8,128)(2,1)S(1)} %maximum_select_fusion.7), channel_id=1, source_target_pairs={{0,4},{1,5},{2,6},{3,7},{4,0},{5,1},{6,2},{7,3},{8,12},{9,13},{10,... | collective-permute-start | bytes 884744 | tf_op jit(solution)/shard_map/ppermute | solution.py:339
  67.7 9.1 %collective-permute-start.3 = (bf16[2,2,2,24,896]{4,3,0,1,2:T(8,128)(2,1)S(1)}, bf16[2,2,2,24,896]{4,3,0,1,2:T(8,128)(2,1)S(1)}, u32[]{:S(2)}, u32[]{:S(2)}) collective-permute-start(bf16[2,2,2,24,896]{4,3,0,1,2:T(8,128)(2,1)S(1)} %maximum_select_fusion.5), channel_id=1, source_target_pairs={{0,1},{1,0},{2,3},{3,2},{4,5},{5,4},{6,7},{7,6},{8,9},{9,8},{10,11... | collective-permute-start | bytes 1032200 | tf_op jit(solution)/shard_map/ppermute | solution.py:339
  78.5 4.7 collective-permute-start.12
  78.7 11.6 %copy-start.53 = (f32[750]{0:T(1024)}, f32[750]{0:T(1024)S(1)}, u32[]{:S(2)}) copy-start(f32[750]{0:T(1024)S(1)} %broadcast_multiply_fusion.6) | copy-start | bytes 9004
  79.3 11.1 %copy-start.57 = (f32[750]{0:T(1024)}, f32[750]{0:T(1024)S(1)}, u32[]{:S(2)}) copy-start(f32[750]{0:T(1024)S(1)} %add_rsqrt_fusion.2) | copy-start | bytes 9004
  90.3 85.7 %copy-start.64 = (f32[768]{0:T(1024)}, f32[768]{0:T(1024)S(1)}, u32[]{:S(2)}) copy-start(f32[768]{0:T(1024)S(1)} %get-tuple-element.221) | copy-start | bytes 9220
  176.0 11.2 %copy-start.14 = (bf16[1,750,768]{2,1,0:T(8,128)(2,1)S(1)}, bf16[1,750,768]{2,1,0:T(8,128)(2,1)}, u32[]{:S(2)}) copy-start(bf16[1,750,768]{2,1,0:T(8,128)(2,1)} %param.15) | copy-start | bytes 3456004
  201.9 9.5 %copy-start.7 = (f32[750,768]{1,0:T(8,128)S(1)}, f32[750,768]{1,0:T(8,128)}, u32[]{:S(2)}) copy-start(f32[750,768]{1,0:T(8,128)} %copy-done.6) | copy-start | bytes 6912004
  201.9 9.5 %copy-start.65 = (f32[768]{0:T(1024)S(1)}, f32[768]{0:T(1024)}, u32[]{:S(2)}) copy-start(f32[768]{0:T(1024)} %copy-done.64) | copy-start | bytes 9220
  248.8 9.5 %collective-permute-start.14 = (bf16[2,2,2,2,24,6912]{5,4,0,3,2,1:T(8,128)(2,1)}, bf16[2,2,2,2,24,6912]{5,4,0,3,2,1:T(8,128)(2,1)}, u32[]{:S(2)}, u32[]{:S(2)}) collective-permute-start(bf16[2,2,2,2,24,6912]{5,4,0,3,2,1:T(8,128)(2,1)} %bitcast.317), channel_id=1, source_target_pairs={{0,2},{1,3},{2,0},{3,1},{4,6},{5,7},{6,4},{7,5},{8,10},{9,11},{10,... | collective-permute-start | bytes 15925256 | tf_op jit(solution)/shard_map/ppermute | solution.py:320
  271.6 53.7 %collective-permute-start.15 = (bf16[2,2,2,24,3456]{4,3,0,2,1:T(8,128)(2,1)}, bf16[2,2,2,24,3456]{4,3,0,2,1:T(8,128)(2,1)}, u32[]{:S(2)}, u32[]{:S(2)}) collective-permute-start(bf16[2,2,2,24,3456]{4,3,0,2,1:T(8,128)(2,1)} %fusion.42), channel_id=1, source_target_pairs={{0,4},{1,5},{2,6},{3,7},{4,0},{5,1},{6,2},{7,3},{8,12},{9,13},{10,... | collective-permute-start | bytes 3981320 | tf_op jit(solution)/shard_map/ppermute | solution.py:320
  296.2 11.9 %collective-permute-start.23 = (bf16[750,256]{1,0:T(8,128)(2,1)}, bf16[750,256]{1,0:T(8,128)(2,1)S(1)}, u32[]{:S(2)}, u32[]{:S(2)}) collective-permute-start(bf16[750,256]{1,0:T(8,128)(2,1)} %fusion.68), channel_id=1, source_target_pairs={{0,1},{1,0},{2,3},{3,2},{4,5},{5,4},{6,7},{7,6},{8,9},{9,8},{10,11... | collective-permute-start | bytes 1152008 | tf_op jit(solution)/shard_map/ppermute | solution.py:512
  301.5 31.4 %collective-permute-start.16 = (bf16[2,2,2,24,3456]{4,3,0,2,1:T(8,128)(2,1)}, bf16[2,2,2,24,3456]{4,3,0,2,1:T(8,128)(2,1)}, u32[]{:S(2)}, u32[]{:S(2)}) collective-permute-start(bf16[2,2,2,24,3456]{4,3,0,2,1:T(8,128)(2,1)} %fusion.43), channel_id=1, source_target_pairs={{0,8},{1,9},{2,10},{3,11},{4,12},{5,13},{6,14},{7,15},{8,0},{9,1},... | collective-permute-start | bytes 3981320 | tf_op jit(solution)/shard_map/ppermute | solution.py:320
  310.0 22.9 %slice-start.2 = ((s8[5308416]{0:T(1024)(128)(4,1)}), s8[4194304]{0:T(1024)(128)(4,1)S(1)}, s32[]{:S(2)}) async-start(s8[5308416]{0:T(1024)(128)(4,1)} %bitcast.320), calls=%async_computation.3 | async-start | bytes 8388608
  310.1 22.8 %slice-start.3 = ((s8[5308416]{0:T(1024)(128)(4,1)}), s8[1114112]{0:T(1024)(128)(4,1)S(1)}, s32[]{:S(2)}) async-start(s8[5308416]{0:T(1024)(128)(4,1)} %bitcast.320), calls=%async_computation.4 | async-start | bytes 2228224
  334.6 19.6 %collective-permute-start.18 = (bf16[2,2,24,3456]{3,2,0,1:T(8,128)(2,1)S(1)}, bf16[2,2,24,3456]{3,2,0,1:T(8,128)(2,1)S(1)}, u32[]{:S(2)}, u32[]{:S(2)}) collective-permute-start(bf16[2,2,24,3456]{3,2,0,1:T(8,128)(2,1)S(1)} %fusion.70), channel_id=1, source_target_pairs={{0,4},{1,5},{2,6},{3,7},{4,0},{5,1},{6,2},{7,3},{8,12},{9,13},{10,... | collective-permute-start | bytes 1990664 | tf_op jit(solution)/shard_map/ppermute | solution.py:320
  336.6 16.7 %collective-permute-start.24 = (bf16[750,256]{1,0:T(8,128)(2,1)S(1)}, bf16[750,256]{1,0:T(8,128)(2,1)S(1)}, u32[]{:S(2)}, u32[]{:S(2)}) collective-permute-start(bf16[750,256]{1,0:T(8,128)(2,1)S(1)} %slice.581), channel_id=1, source_target_pairs={{0,1},{1,0},{2,3},{3,2},{4,5},{5,4},{6,7},{7,6},{8,9},{9,8},{10,11... | collective-permute-start | bytes 1152008 | tf_op jit(solution)/shard_map/ppermute | solution.py:512
  337.0 17.4 %collective-permute-start.17 = (bf16[2,2,24,3456]{3,2,0,1:T(8,128)(2,1)S(1)}, bf16[2,2,24,3456]{3,2,0,1:T(8,128)(2,1)S(1)}, u32[]{:S(2)}, u32[]{:S(2)}) collective-permute-start(bf16[2,2,24,3456]{3,2,0,1:T(8,128)(2,1)S(1)} %fusion.69), channel_id=1, source_target_pairs={{0,8},{1,9},{2,10},{3,11},{4,12},{5,13},{6,14},{7,15},{8,0},{9,1},... | collective-permute-start | bytes 1990664 | tf_op jit(solution)/shard_map/ppermute | solution.py:320
  354.7 20.0 %collective-permute-start.20 = (bf16[2,24,3456]{2,1,0:T(8,128)(2,1)S(1)}, bf16[2,24,3456]{2,1,0:T(8,128)(2,1)S(1)}, u32[]{:S(2)}, u32[]{:S(2)}) collective-permute-start(bf16[2,24,3456]{2,1,0:T(8,128)(2,1)S(1)} %fusion.73), channel_id=1, source_target_pairs={{0,1},{1,0},{2,3},{3,2},{4,5},{5,4},{6,7},{7,6},{8,9},{9,8},{10,11... | collective-permute-start | bytes 995336 | tf_op jit(solution)/shard_map/ppermute | solution.py:320
  356.5 18.3 %collective-permute-start.19 = (bf16[2,24,3456]{2,1,0:T(8,128)(2,1)S(1)}, bf16[2,24,3456]{2,1,0:T(8,128)(2,1)S(1)}, u32[]{:S(2)}, u32[]{:S(2)}) collective-permute-start(bf16[2,24,3456]{2,1,0:T(8,128)(2,1)S(1)} %fusion.72), channel_id=1, source_target_pairs={{0,1},{1,0},{2,3},{3,2},{4,5},{5,4},{6,7},{7,6},{8,9},{9,8},{10,11... | collective-permute-start | bytes 995336 | tf_op jit(solution)/shard_map/ppermute | solution.py:320
  372.1 25.0 %collective-permute-start.25 = (bf16[750,256]{1,0:T(8,128)(2,1)S(1)}, bf16[750,256]{1,0:T(8,128)(2,1)S(1)}, u32[]{:S(2)}, u32[]{:S(2)}) collective-permute-start(bf16[750,256]{1,0:T(8,128)(2,1)S(1)} %slice.580), channel_id=1, source_target_pairs={{0,1},{1,0},{2,3},{3,2},{4,5},{5,4},{6,7},{7,6},{8,9},{9,8},{10,11... | collective-permute-start | bytes 1152008 | tf_op jit(solution)/shard_map/ppermute | solution.py:512
  374.9 23.0 %collective-permute-start.22 = (bf16[24,3456]{1,0:T(8,128)(2,1)S(1)}, bf16[24,3456]{1,0:T(8,128)(2,1)S(1)}, u32[]{:S(2)}, u32[]{:S(2)}) collective-permute-start(bf16[24,3456]{1,0:T(8,128)(2,1)S(1)} %fusion.89), channel_id=1, source_target_pairs={{0,16},{1,17},{2,18},{3,19},{4,20},{5,21},{6,22},{7,23},{8,24},{9,... | collective-permute-start | bytes 497672 | tf_op jit(solution)/shard_map/ppermute | solution.py:320
  375.0 23.0 %collective-permute-start.21 = (bf16[24,3456]{1,0:T(8,128)(2,1)S(1)}, bf16[24,3456]{1,0:T(8,128)(2,1)S(1)}, u32[]{:S(2)}, u32[]{:S(2)}) collective-permute-start(bf16[24,3456]{1,0:T(8,128)(2,1)S(1)} %fusion.88), channel_id=1, source_target_pairs={{0,16},{1,17},{2,18},{3,19},{4,20},{5,21},{6,22},{7,23},{8,24},{9,... | collective-permute-start | bytes 497672 | tf_op jit(solution)/shard_map/ppermute | solution.py:320
  396.0 28.7 %collective-permute-start.26 = (bf16[750,256]{1,0:T(8,128)(2,1)}, bf16[750,256]{1,0:T(8,128)(2,1)}, u32[]{:S(2)}, u32[]{:S(2)}) collective-permute-start(bf16[750,256]{1,0:T(8,128)(2,1)} %slice.579), channel_id=1, source_target_pairs={{0,1},{1,0},{2,3},{3,2},{4,5},{5,4},{6,7},{7,6},{8,9},{9,8},{10,11... | collective-permute-start | bytes 1152008 | tf_op jit(solution)/shard_map/ppermute | solution.py:512
  402.1 16.6 %copy-start.47 = (f32[24,768]{1,0:T(8,128)}, f32[24,768]{1,0:T(8,128)S(1)}, u32[]{:S(2)}) copy-start(f32[24,768]{1,0:T(8,128)S(1)} %get-tuple-element.231) | copy-start | bytes 221188
  418.9 16.4 %collective-permute-start.28 = (bf16[750,256]{1,0:T(8,128)(2,1)S(1)}, bf16[750,256]{1,0:T(8,128)(2,1)S(1)}, u32[]{:S(2)}, u32[]{:S(2)}) collective-permute-start(bf16[750,256]{1,0:T(8,128)(2,1)S(1)} %fusion.63), channel_id=1, source_target_pairs={{0,1},{1,0},{2,3},{3,2},{4,5},{5,4},{6,7},{7,6},{8,9},{9,8},{10,11... | collective-permute-start | bytes 1152008 | tf_op jit(solution)/shard_map/ppermute | solution.py:512
  422.1 13.1 %collective-permute-start.27 = (bf16[750,256]{1,0:T(8,128)(2,1)S(1)}, bf16[750,256]{1,0:T(8,128)(2,1)S(1)}, u32[]{:S(2)}, u32[]{:S(2)}) collective-permute-start(bf16[750,256]{1,0:T(8,128)(2,1)S(1)} %slice.578), channel_id=1, source_target_pairs={{0,1},{1,0},{2,3},{3,2},{4,5},{5,4},{6,7},{7,6},{8,9},{9,8},{10,11... | collective-permute-start | bytes 1152008 | tf_op jit(solution)/shard_map/ppermute | solution.py:512
  446.1 8.3 %copy-start.41 = (bf16[768,1]{1,0:T(8,128)(2,1)S(1)}, bf16[768,1]{1,0:T(8,128)(2,1)}, u32[]{:S(2)}) copy-start(bf16[768,1]{1,0:T(8,128)(2,1)} %stack.422) | copy-start | bytes 4612
  446.2 8.3 %copy-start.42 = (bf16[768,4]{1,0:T(8,128)(2,1)S(1)}, bf16[768,4]{1,0:T(8,128)(2,1)}, u32[]{:S(2)}) copy-start(bf16[768,4]{1,0:T(8,128)(2,1)} %reshape.1154) | copy-start | bytes 18436
  446.2 8.3 %copy-start.43 = (bf16[768,1]{1,0:T(8,128)(2,1)S(1)}, bf16[768,1]{1,0:T(8,128)(2,1)}, u32[]{:S(2)}) copy-start(bf16[768,1]{1,0:T(8,128)(2,1)} %stack.419) | copy-start | bytes 4612
  464.2 3.9 collective-permute-start.29
  468.8 9.1 %collective-permute-start.38 = (bf16[2,2,2,24,768]{4,3,2,1,0:T(8,128)(2,1)S(1)}, bf16[2,2,2,24,768]{4,3,2,1,0:T(8,128)(2,1)S(1)}, u32[]{:S(2)}, u32[]{:S(2)}) collective-permute-start(bf16[2,2,2,24,768]{4,3,2,1,0:T(8,128)(2,1)S(1)} %fusion.83), channel_id=1, source_target_pairs={{0,8},{1,9},{2,10},{3,11},{4,12},{5,13},{6,14},{7,15},{8,0},{9,1},... | collective-permute-start | bytes 884744 | tf_op jit(solution)/shard_map/ppermute | solution.py:320
  472.8 9.1 %collective-permute-start.34 = (bf16[2,2,2,24,768]{4,3,2,1,0:T(8,128)(2,1)S(1)}, bf16[2,2,2,24,768]{4,3,2,1,0:T(8,128)(2,1)S(1)}, u32[]{:S(2)}, u32[]{:S(2)}) collective-permute-start(bf16[2,2,2,24,768]{4,3,2,1,0:T(8,128)(2,1)S(1)} %fusion.82), channel_id=1, source_target_pairs={{0,4},{1,5},{2,6},{3,7},{4,0},{5,1},{6,2},{7,3},{8,12},{9,13},{10,... | collective-permute-start | bytes 884744 | tf_op jit(solution)/shard_map/ppermute | solution.py:320
  474.2 11.0 %collective-permute-start.30 = (bf16[2,2,2,24,896]{4,3,2,1,0:T(8,128)(2,1)S(1)}, bf16[2,2,2,24,896]{4,3,2,1,0:T(8,128)(2,1)S(1)}, u32[]{:S(2)}, u32[]{:S(2)}) collective-permute-start(bf16[2,2,2,24,896]{4,3,2,1,0:T(8,128)(2,1)S(1)} %fusion.71), channel_id=1, source_target_pairs={{0,1},{1,0},{2,3},{3,2},{4,5},{5,4},{6,7},{7,6},{8,9},{9,8},{10,11... | collective-permute-start | bytes 1032200 | tf_op jit(solution)/shard_map/ppermute | solution.py:320
  478.1 9.2 %collective-permute-start.39 = (bf16[2,2,24,768]{3,2,1,0:T(8,128)(2,1)S(1)}, bf16[2,2,24,768]{3,2,1,0:T(8,128)(2,1)S(1)}, u32[]{:S(2)}, u32[]{:S(2)}) collective-permute-start(bf16[2,2,24,768]{3,2,1,0:T(8,128)(2,1)S(1)} %fusion.91), channel_id=1, source_target_pairs={{0,1},{1,0},{2,3},{3,2},{4,5},{5,4},{6,7},{7,6},{8,9},{9,8},{10,11... | collective-permute-start | bytes 442376 | tf_op jit(solution)/shard_map/ppermute | solution.py:320
  482.0 6.1 %collective-permute-start.35 = (bf16[2,2,24,768]{3,2,1,0:T(8,128)(2,1)S(1)}, bf16[2,2,24,768]{3,2,1,0:T(8,128)(2,1)S(1)}, u32[]{:S(2)}, u32[]{:S(2)}) collective-permute-start(bf16[2,2,24,768]{3,2,1,0:T(8,128)(2,1)S(1)} %fusion.90), channel_id=1, source_target_pairs={{0,8},{1,9},{2,10},{3,11},{4,12},{5,13},{6,14},{7,15},{8,0},{9,1},... | collective-permute-start | bytes 442376 | tf_op jit(solution)/shard_map/ppermute | solution.py:320
  485.3 12.4 %copy-start.67 = (f32[2,96]{1,0:T(2,128)S(1)}, f32[2,96]{1,0:T(2,128)}, u32[]{:S(2)}) copy-start(f32[2,96]{1,0:T(2,128)} %param.26) | copy-start | bytes 2308
  485.3 12.4 %copy-start.70 = (f32[96]{0:T(128)S(1)}, f32[96]{0:T(128)}, u32[]{:S(2)}) copy-start(f32[96]{0:T(128)} %param.20) | copy-start | bytes 1156
  485.3 12.9 %copy-start.50 = (f32[24,8]{1,0:T(8,128)S(1)}, f32[24,8]{1,0:T(8,128)}, u32[]{:S(2)}) copy-start(f32[24,8]{1,0:T(8,128)} %copy.152) | copy-start | bytes 2308
  485.3 12.9 %copy-start.51 = (f32[1,24,8]{2,1,0:T(8,128)S(1)}, f32[1,24,8]{2,1,0:T(8,128)}, u32[]{:S(2)}) copy-start(f32[1,24,8]{2,1,0:T(8,128)} %copy.162) | copy-start | bytes 2308
  485.3 12.9 %copy-start.52 = (f32[1,24,8]{2,1,0:T(8,128)S(1)}, f32[1,24,8]{2,1,0:T(8,128)}, u32[]{:S(2)}) copy-start(f32[1,24,8]{2,1,0:T(8,128)} %copy.161) | copy-start | bytes 2308
  485.4 10.2 %collective-permute-start.31 = (bf16[2,2,24,896]{3,2,1,0:T(8,128)(2,1)S(1)}, bf16[2,2,24,896]{3,2,1,0:T(8,128)(2,1)S(1)}, u32[]{:S(2)}, u32[]{:S(2)}) collective-permute-start(bf16[2,2,24,896]{3,2,1,0:T(8,128)(2,1)S(1)} %fusion.87), channel_id=1, source_target_pairs={{0,4},{1,5},{2,6},{3,7},{4,0},{5,1},{6,2},{7,3},{8,12},{9,13},{10,... | collective-permute-start | bytes 516104 | tf_op jit(solution)/shard_map/ppermute | solution.py:320
  487.3 17.9 %copy-start.37 = (f32[2,24,2304]{2,1,0:T(8,128)S(1)}, f32[2,24,2304]{2,1,0:T(8,128)}, u32[]{:S(2)}) copy-start(f32[2,24,2304]{2,1,0:T(8,128)} %param.22) | copy-start | bytes 1327108
  487.4 5.1 collective-permute-start.40
  488.2 17.2 %copy-start.40 = (f32[24,2304]{1,0:T(8,128)S(1)}, f32[24,2304]{1,0:T(8,128)}, u32[]{:S(2)}) copy-start(f32[24,2304]{1,0:T(8,128)} %param.16) | copy-start | bytes 663556
  488.2 4.7 collective-permute-start.36
  492.5 4.9 collective-permute-start.41
  493.0 5.5 %collective-permute-start.37 = (bf16[24,768]{1,0:T(8,128)(2,1)S(1)}, bf16[24,768]{1,0:T(8,128)(2,1)S(1)}, u32[]{:S(2)}, u32[]{:S(2)}) collective-permute-start(bf16[24,768]{1,0:T(8,128)(2,1)S(1)} %fusion.101), channel_id=1, source_target_pairs={{0,16},{1,17},{2,18},{3,19},{4,20},{5,21},{6,22},{7,23},{8,24},{9,... | collective-permute-start | bytes 110600 | tf_op jit(solution)/shard_map/ppermute | solution.py:320
  495.7 4.6 collective-permute-start.32
  497.6 9.4 %copy-start.69 = (f32[96]{0:T(128)}, f32[96]{0:T(128)S(1)}, u32[]{:S(2)}) copy-start(f32[96]{0:T(128)S(1)} %reshape.1157) | copy-start | bytes 1156
  500.3 5.0 collective-permute-start.33
  (56 other events, 184.8 us)
Sparse Core Ops, SparseCore 0:
  11.5 97.3 all-gather.1

commit v18 on v17

--- a/solution.py
+++ b/solution.py
@@ -54,7 +54,7 @@
     )
 
 
-QUERY_CHUNK = 128
+QUERY_CHUNK = 384
 MASKED = -1e30
 
 

time: 519 us -> 489 us (0.942); the launches traced: 514 us -> 489 us
  Pallas kernels: 142 us -> 100 us
  matrix products: 72.7 us -> 83 us
  waiting for transfers between devices: 75.6 us -> 84.7 us
    pallas_call x6, Pallas kernels: 89.9 us -> 62.7 us  [attention_pallas(): pl.pallas_call(attention_backward_kernel, grid=(span,), in_specs=[qi_spec...]
    pallas_call x1, Pallas kernels: 51.6 us -> 37.3 us  [attention_pallas(): pl.pallas_call(attention_forward_kernel, grid=(pair_count,), in_specs=[q_...]
    ppermute x22, waiting for transfers between devices: 22 us -> 33.1 us  [tree_reduce_scatter(): got = lax.ppermute(send, ('clip', 'frame'), pairs)]
    dot_general x1, matrix products: 9.05 us -> 19.7 us  [body(): jnp.dot(hidden_second, full_expand, preferred_element_type=jnp.float32)]
  transfers between devices with their start and end apart: 43 -> 43, of which waited for: 18 -> 22; matrix products, arithmetic and copies ran while one was open for 15% -> 16% of each run, Pallas kernels for 28% -> 20%
where the time goes in v18:
time: 489 us
  Pallas kernels  100 us (20%)
  local copies, waits for them, and re-layouts  95.3 us (19%)
  waiting for transfers between devices  84.7 us (17%)
  matrix products  83 us (17%)
  other arithmetic  60.7 us (12%)
  starting transfers between devices  49.5 us (10%)
  between operations  16.1 us (3%)
    pallas_call x6, Pallas kernels, attention_pallas(): pl.pallas_call(attention_backward_kernel, grid=(span,), in_specs=[qi_spec...  62.7 us
    ppermute x13, waiting for transfers between devices, double(): got = lax.ppermute(data, ('clip', 'frame'), pairs)  42 us
    pallas_call x1, Pallas kernels, attention_pallas(): pl.pallas_call(attention_forward_kernel, grid=(pair_count,), in_specs=[q_...  37.3 us
    ppermute x22, waiting for transfers between devices, tree_reduce_scatter(): got = lax.ppermute(send, ('clip', 'frame'), pairs)  33.1 us
    unnamed x178, local copies, waits for them, and re-layouts  29 us
    ppermute x22, starting transfers between devices, tree_reduce_scatter(): got = lax.ppermute(send, ('clip', 'frame'), pairs)  21.1 us
    dot_general x1, matrix products, body(): jnp.dot(hidden_second, full_expand, preferred_element_type=jnp.float32)  19.7 us
    ppermute x13, starting transfers between devices, double(): got = lax.ppermute(data, ('clip', 'frame'), pairs)  19.5 us
  transfers between devices with their start and end apart: 43, of which 22 were waited for; matrix products, arithmetic and copies ran while one was open for 16% of the time, Pallas kernels for 20%

profile of v18, /device:TPU:0, one launch (start us, length us, event | category | flops | bytes accessed | tf_op | source)
XLA Modules:
  0.0 489.4 jit_solution(4898641337772078514)
XLA Ops:
  12.8 4.1 collective-permute-start.8
  17.0 3.0 collective-permute-start
  25.5 29.5 %collective-permute-done.5 = bf16[2,24,768]{2,1,0:T(8,128)(2,1)S(1)} collective-permute-done((bf16[2,24,768]{2,1,0:T(8,128)(2,1)S(1)}, bf16[2,24,768]{2,1,0:T(8,128)(2,1)S(1)}, u32[]{:S(2)}, u32[]{:S(2)}) %collective-permute-start.5) | collective-permute-done | bytes 73760 | tf_op jit(solution)/shard_map/ppermute | solution.py:339
  60.1 1.8 collective-permute-done.10
  62.4 3.4 collective-permute-done.6
  69.4 3.2 collective-permute-done.7
  72.8 4.0 collective-permute-done.3
  76.8 1.7 fusion.116
  80.8 1.7 fusion.37
  83.2 3.3 maximum_select_fusion
  86.5 1.9 copy-done.15
  90.4 5.5 %add_convert_fusion = bf16[750,2304]{1,0:T(8,128)(2,1)S(1)} fusion(f32[2304]{0:T(1024)S(1)} %pad_maximum_fusion.16, bf16[768,2432]{1,0:T(8,128)(2,1)} %bitcast.326, bf16[1,750,768]{2,1,0:T(8,128)(2,1)S(1)} %copy-done.2, f32[768]{0:T(1024)S(1)} %get-tuple-element.226, f32[768]{0:T(1024)S(1)} %get-tuple-element.227, f32[750]{0:T(1024)S(1)} %add_rsqrt_fusion.2, ...), kind=kOutput, calls=%fused_computation.14 | convolution fusion | flops 2661120000 | bytes 8168304 | tf_op jit(solution)/shard_map/dot_general | solution.py:431
  99.3 3.5 add_convert_fusion.1
  102.8 2.7 fusion.8.k_ref.v_ref
  105.5 37.3 %shard_map.293 = (bf16[768,768]{1,0:T(8,128)(2,1)S(1)}, f32[768,768]{1,0:T(8,128)S(1)}) custom-call(bf16[768,768]{1,0:T(8,128)(2,1)S(1)} %pad.39.q_ref, bf16[1536,1536]{1,0:T(8,128)(2,1)} %fusion.8.k_ref.v_ref, bf16[1536,1536]{1,0:T(8,128)(2,1)} %fusion.8.k_ref.v_ref, f32[1,1536]{1,0:T(1,128)S(1)} %compare_select_fusion.kbias_ref), custom_call_target="tpu_custom_call" | custom-call | tf_op jit(solution)/shard_map/pallas_call | solution.py:161
  144.2 2.5 fusion.121
  148.4 4.8 slice.408
  153.2 8.5 %reshape.1150 = bf16[3072,768]{1,0:T(8,128)(2,1)} reshape(bf16[768,3072]{1,0:T(8,128)(2,1)} %slice.408) | data formatting | bytes 9437184 | tf_op jit(solution)/shard_map/reshape | solution.py:416
  161.7 19.7 %multiply_convert_fusion = (bf16[750,3072]{1,0:T(8,128)(2,1)S(1)}, f32[750,3072]{1,0:T(8,128)}) fusion(f32[3072]{0:T(1024)S(1)} %add.429, bf16[768,6912]{1,0:T(8,128)(2,1)} %all-gather.2.cloned.1.call-done, f32[750,768]{1,0:T(8,128)} %copy-done.6, f32[768]{0:T(1024)S(1)} %get-tuple-element.221, f32[768]{0:T(1024)S(1)} %get-tuple-element.222, ...), kind=kOutput, calls=%fused_computation.12 | convolution fusion | flops 3555648000 | bytes 20877168 | tf_op jit(solution)/shard_map/dot_general | solution.py:451
  181.4 2.2 copy-done.71
  183.6 5.7 %convolution_convert_fusion.2 = bf16[3072,768]{1,0:T(8,128)(2,1)} fusion(bf16[750,3072]{1,0:T(8,128)(2,1)S(1)} %get-tuple-element.279, bf16[1,750,768]{2,1,0:T(8,128)(2,1)S(1)} %copy-done.14), kind=kOutput, calls=%fused_computation.19 | convolution fusion | flops 3541303296 | bytes 10478592 | tf_op jit(solution)/shard_map/dot_general | solution.py:461
  189.3 8.5 %concatenate.309 = bf16[2,2,2,2,2,24,3072]{6,5,4,3,2,1,0:T(8,128)(2,1)} reshape(bf16[3072,768]{1,0:T(8,128)(2,1)} %convolution_convert_fusion.2) | data formatting | bytes 9437184 | tf_op jit(solution)/shard_map/concatenate | solution.py:481
  197.8 9.4 %fusion.122 = (bf16[3072]{0:T(1024)(128)(2,1)S(1)}, bf16[750,3072]{1,0:T(8,128)(2,1)S(1)}) fusion(f32[750,3072]{1,0:T(8,128)} %get-tuple-element.280, f32[3072]{0:T(1024)S(1)} %add.429, bf16[3072,768]{1,0:T(8,128)(2,1)} %reshape.1150, bf16[1,750,768]{2,1,0:T(8,128)(2,1)S(1)} %copy-done.14), kind=kOutput, calls=%fused_computation.323 | convolution fusion | flops 3566588928 | bytes 19713024 | tf_op jit(solution)/shard_map/dot_general | solution.py:465
  207.3 5.0 %convolution_convert_fusion.1 = bf16[768,3072]{1,0:T(8,128)(2,1)S(1)} fusion(bf16[750,3072]{1,0:T(8,128)(2,1)S(1)} %get-tuple-element.283, f32[750,768]{1,0:T(8,128)S(1)} %copy-done.7, f32[768]{0:T(1024)S(1)} %copy-done.65, f32[768]{0:T(1024)S(1)} %get-tuple-element.222, f32[750]{0:T(1024)S(1)} %add_rsqrt_fusion, f32[750]{0:T(1024)S(1)} %broadcast_multiply_fusion.4), kind=kOutput, calls=%fused_computation.18 | convolution fusion | flops 3544183296 | bytes 11642736 | tf_op jit(solution)/shard_map/dot_general | solution.py:467
  212.3 7.3 %multiply_reduce_fusion = (bf16[768]{0:T(1024)(128)(2,1)}, f32[750]{0:T(1024)S(1)}, f32[750]{0:T(1024)S(1)}, bf16[768]{0:T(1024)(128)(2,1)S(1)}, f32[750,768]{1,0:T(8,128)S(1)}) fusion(f32[750,768]{1,0:T(8,128)S(1)} %copy-done.7, f32[750]{0:T(1024)S(1)} %add_rsqrt_fusion, f32[750]{0:T(1024)S(1)} %broadcast_multiply_fusion.4, ...), kind=kOutput, calls=%fused_computation.64 | convolution fusion | flops 3544124928 | bytes 13952736 | tf_op jit(solution)/shard_map/dot_general | solution.py:471
  222.7 8.3 %pad_maximum_fusion = bf16[2,2,2,2,2,24,6912]{6,5,4,3,2,1,0:T(8,128)(2,1)} fusion(bf16[2,2,2,2,2,24,768]{6,5,4,3,2,1,0:T(8,128)(2,1)S(1)} %bitcast.330, bf16[2,2,2,2,2,24,3072]{6,5,4,3,2,1,0:T(8,128)(2,1)S(1)} %bitcast.324, bf16[2,2,2,2,2,24,3072]{6,5,4,3,2,1,0:T(8,128)(2,1)S(1)} %bitcast.319), kind=kLoop, calls=%fused_computation.1 | loop fusion | flops 31850496 | bytes 21233664 | tf_op jit(solution)/shard_map/concatenate | solution.py:481
  231.0 8.7 %constant_dynamic-slice_fusion.1 = (bf16[2,2,2,1,2,24,6912]{6,5,4,3,2,1,0:T(8,128)(2,1)}, bf16[2,2,2,1,2,24,6912]{6,5,4,3,2,1,0:T(8,128)(2,1)}) fusion(bf16[2,2,2,2,2,24,6912]{6,5,4,3,2,1,0:T(8,128)(2,1)} %pad_maximum_fusion, s32[]{:T(128)S(6)} %select_n.403, s32[]{:T(128)S(6)} %select_n.404), kind=kLoop, calls=%fused_computation.282 | loop fusion | bytes 21233672 | tf_op jit(solution)/shard_map/jit(dynamic_index_in_dim)/dynamic_slice | solution.py:313
  239.7 5.2 %copy.175 = bf16[2,2,2,1,2,24,6912]{6,5,0,4,2,1,3:T(8,128)(2,1)} copy(bf16[2,2,2,1,2,24,6912]{6,5,4,3,2,1,0:T(8,128)(2,1)} %get-tuple-element.239) | data formatting | bytes 10616832
  248.7 3.1 convolution_convert_fusion.4
  251.7 2.6 collective-permute-done.14
  254.3 5.3 %convert_add_fusion = f32[2,2,2,2,24,6912]{5,4,0,3,2,1:T(8,128)S(1)} fusion(bf16[2,2,2,2,24,6912]{5,4,0,3,2,1:T(8,128)(2,1)} %collective-permute-done.14, bf16[2,2,2,1,2,24,6912]{6,5,4,3,2,1,0:T(8,128)(2,1)} %get-tuple-element.238), kind=kLoop, calls=%fused_computation.2 | loop fusion | flops 7962624 | bytes 21233664 | tf_op jit(solution)/shard_map/add | solution.py:321
  259.7 4.9 fusion.117
  264.5 3.1 fusion.42
  267.7 8.5 %fusion.41 = bf16[1,750,768]{2,1,0:T(8,128)(2,1)} fusion(f32[750,768]{1,0:T(8,128)S(1)} %copy-done.8, bf16[750,3072]{1,0:T(8,128)(2,1)} %copy-done.71, bf16[3072,768]{1,0:T(8,128)(2,1)} %reshape.1150, f32[768]{0:T(1024)S(1)} %copy-done.63), kind=kOutput, calls=%fused_computation.82 | convolution fusion | flops 3540672000 | bytes 12785664 | tf_op jit(solution)/shard_map/dot_general | solution.py:455
  276.2 10.5 %shard_map.294 = (f32[768,128]{1,0:T(8,128)S(1)}, f32[1536,128]{1,0:T(8,128)S(1)}, f32[1536,128]{1,0:T(8,128)S(1)}) custom-call(bf16[768,768]{1,0:T(8,128)(2,1)S(1)} %pad.39.q_ref, bf16[1536,1536]{1,0:T(8,128)(2,1)} %fusion.8.k_ref.v_ref, bf16[1536,1536]{1,0:T(8,128)(2,1)} %fusion.8.k_ref.v_ref, bf16[768,768]{1,0:T(8,128)(2,1)S(1)} %pad.41.do_ref, ...), custom_call_target="tpu_custom_call" | custom-call | tf_op jit(solution)/shard_map/pallas_call | solution.py:180
  287.7 2.4 collective-permute-start.23
  290.1 3.0 fusion.43
  297.6 2.2 collective-permute-done.23
  299.8 1.8 fusion.62
  301.7 10.4 %shard_map.295 = (f32[768,128]{1,0:T(8,128)S(1)}, f32[1536,128]{1,0:T(8,128)S(1)}, f32[1536,128]{1,0:T(8,128)S(1)}) custom-call(bf16[768,768]{1,0:T(8,128)(2,1)S(1)} %pad.39.q_ref, bf16[1536,1536]{1,0:T(8,128)(2,1)} %fusion.8.k_ref.v_ref, bf16[1536,1536]{1,0:T(8,128)(2,1)} %fusion.8.k_ref.v_ref, bf16[768,768]{1,0:T(8,128)(2,1)S(1)} %pad.42.do_ref, ...), custom_call_target="tpu_custom_call" | custom-call | tf_op jit(solution)/shard_map/pallas_call | solution.py:180
  312.3 2.4 bitcast_add_fusion.1
  314.7 9.8 %collective-permute-done.16 = bf16[2,2,2,24,3456]{4,3,0,2,1:T(8,128)(2,1)} collective-permute-done((bf16[2,2,2,24,3456]{4,3,0,2,1:T(8,128)(2,1)}, bf16[2,2,2,24,3456]{4,3,0,2,1:T(8,128)(2,1)}, u32[]{:S(2)}, u32[]{:S(2)}) %collective-permute-start.16) | collective-permute-done | bytes 1327136 | tf_op jit(solution)/shard_map/ppermute | solution.py:320
  326.2 1.8 collective-permute-start.18
  329.0 10.5 %shard_map.296 = (f32[768,128]{1,0:T(8,128)S(1)}, f32[1536,128]{1,0:T(8,128)S(1)}, f32[1536,128]{1,0:T(8,128)S(1)}) custom-call(bf16[768,768]{1,0:T(8,128)(2,1)S(1)} %pad.39.q_ref, bf16[1536,1536]{1,0:T(8,128)(2,1)} %fusion.8.k_ref.v_ref, bf16[1536,1536]{1,0:T(8,128)(2,1)} %fusion.8.k_ref.v_ref, bf16[768,768]{1,0:T(8,128)(2,1)S(1)} %pad.43.do_ref, ...), custom_call_target="tpu_custom_call" | custom-call | tf_op jit(solution)/shard_map/pallas_call | solution.py:180
  342.4 1.8 collective-permute-done.17
  346.6 10.3 %shard_map.297 = (f32[768,128]{1,0:T(8,128)S(1)}, f32[1536,128]{1,0:T(8,128)S(1)}, f32[1536,128]{1,0:T(8,128)S(1)}) custom-call(bf16[768,768]{1,0:T(8,128)(2,1)S(1)} %pad.39.q_ref, bf16[1536,1536]{1,0:T(8,128)(2,1)} %fusion.8.k_ref.v_ref, bf16[1536,1536]{1,0:T(8,128)(2,1)} %fusion.8.k_ref.v_ref, bf16[768,768]{1,0:T(8,128)(2,1)S(1)} %pad.44.do_ref, ...), custom_call_target="tpu_custom_call" | custom-call | tf_op jit(solution)/shard_map/pallas_call | solution.py:180
  361.1 2.9 collective-permute-start.21
  364.2 10.7 %shard_map.298 = (f32[768,128]{1,0:T(8,128)S(1)}, f32[1536,128]{1,0:T(8,128)S(1)}, f32[1536,128]{1,0:T(8,128)S(1)}) custom-call(bf16[768,768]{1,0:T(8,128)(2,1)S(1)} %pad.39.q_ref, bf16[1536,1536]{1,0:T(8,128)(2,1)} %fusion.8.k_ref.v_ref, bf16[1536,1536]{1,0:T(8,128)(2,1)} %fusion.8.k_ref.v_ref, bf16[768,768]{1,0:T(8,128)(2,1)S(1)} %pad.45.do_ref, ...), custom_call_target="tpu_custom_call" | custom-call | tf_op jit(solution)/shard_map/pallas_call | solution.py:180
  386.2 10.3 %shard_map.299 = (f32[768,128]{1,0:T(8,128)S(1)}, f32[1536,128]{1,0:T(8,128)S(1)}, f32[1536,128]{1,0:T(8,128)S(1)}) custom-call(bf16[768,768]{1,0:T(8,128)(2,1)S(1)} %pad.39.q_ref, bf16[1536,1536]{1,0:T(8,128)(2,1)} %fusion.8.k_ref.v_ref, bf16[1536,1536]{1,0:T(8,128)(2,1)} %fusion.8.k_ref.v_ref, bf16[768,768]{1,0:T(8,128)(2,1)S(1)} %pad.46.do_ref, ...), custom_call_target="tpu_custom_call" | custom-call | tf_op jit(solution)/shard_map/pallas_call | solution.py:180
  402.8 7.3 %collective-permute-done.27 = bf16[750,256]{1,0:T(8,128)(2,1)S(1)} collective-permute-done((bf16[750,256]{1,0:T(8,128)(2,1)S(1)}, bf16[750,256]{1,0:T(8,128)(2,1)S(1)}, u32[]{:S(2)}, u32[]{:S(2)}) %collective-permute-start.27) | collective-permute-done | bytes 384032 | tf_op jit(solution)/shard_map/ppermute | solution.py:512
  410.9 1.8 copy-done.13
  414.0 4.6 fusion.32
  418.6 2.5 reduce.2
  421.2 7.0 %convolution_convert_fusion = bf16[768,2304]{1,0:T(8,128)(2,1)} fusion(bf16[750,2304]{1,0:T(8,128)(2,1)} %copy-done.13, bf16[1,750,768]{2,1,0:T(8,128)(2,1)S(1)} %copy-done.3, f32[768]{0:T(1024)S(1)} %copy-done.62, f32[768]{0:T(1024)S(1)} %copy-done.56, f32[750]{0:T(1024)S(1)} %copy-done.58, f32[750]{0:T(1024)S(1)} %copy-done.54), kind=kOutput, calls=%fused_computation.17 | convolution fusion | flops 2659433472 | bytes 8159088 | tf_op jit(solution)/shard_map/dot_general | solution.py:528
  429.7 7.7 %concatenate.321 = bf16[768,2432]{1,0:T(8,128)(2,1)} concatenate(bf16[768,2304]{1,0:T(8,128)(2,1)} %convolution_convert_fusion, bf16[768,1]{1,0:T(8,128)(2,1)S(1)} %stack.415, bf16[768,1]{1,0:T(8,128)(2,1)S(1)} %stack.416, bf16[768,1]{1,0:T(8,128)(2,1)S(1)} %stack.417, bf16[768,1]{1,0:T(8,128)(2,1)S(1)} %stack.418, bf16[768,1]{1,0:T(8,128)(2,1)S(1)} %copy-done.43, ...), dimensions={1} | concatenate | bytes 7471104 | tf_op jit(solution)/shard_map/concatenate | solution.py:561
  437.5 1.8 dynamic-slice_bitcast_fusion
  445.9 1.8 fusion.46
  447.9 1.7 collective-permute-start.34
  450.7 2.3 collective-permute-done.38
  454.3 2.7 collective-permute-done.34
  458.1 2.5 collective-permute-done.30
  464.4 3.4 collective-permute-done.40
  468.3 2.6 collective-permute-start.37
  478.4 2.2 collective-permute-done.33
  (427 shorter events, 100.7 us)
Async XLA Ops:
  7.2 12.8 %copy-start.2 = (bf16[1,750,768]{2,1,0:T(8,128)(2,1)S(1)}, bf16[1,750,768]{2,1,0:T(8,128)(2,1)}, u32[]{:S(2)}) copy-start(bf16[1,750,768]{2,1,0:T(8,128)(2,1)} %param.14) | copy-start | bytes 3456004
  7.2 137.0 %all-gather.2.cloned.1.call-start = ((), (), s32[]{:S(2)}) async-start(), calls=%async_computation | async-start | bytes 10948608 | tf_op jit(solution)/shard_map/all_gather | solution.py:409
  12.8 8.7 %collective-permute-start.8 = (bf16[24,768]{1,0:T(8,128)(2,1)S(1)}, bf16[24,768]{1,0:T(8,128)(2,1)S(1)}, u32[]{:S(2)}, u32[]{:S(2)}) collective-permute-start(bf16[24,768]{1,0:T(8,128)(2,1)S(1)} %get-tuple-element.259), channel_id=1, source_target_pairs={{0,16},{1,17},{2,18},{3,19},{4,20},{5,21},{6,22},{7,23},{8,24},{9,... | collective-permute-start | bytes 110600 | tf_op jit(solution)/shard_map/ppermute | solution.py:339
  16.9 6.2 %collective-permute-start.4 = (bf16[24,768]{1,0:T(8,128)(2,1)S(1)}, bf16[24,768]{1,0:T(8,128)(2,1)S(1)}, u32[]{:S(2)}, u32[]{:S(2)}) collective-permute-start(bf16[24,768]{1,0:T(8,128)(2,1)S(1)} %get-tuple-element.265), channel_id=1, source_target_pairs={{0,16},{1,17},{2,18},{3,19},{4,20},{5,21},{6,22},{7,23},{8,24},{9,... | collective-permute-start | bytes 110600 | tf_op jit(solution)/shard_map/ppermute | solution.py:339
  17.0 6.9 %collective-permute-start = (bf16[24,896]{1,0:T(8,128)(2,1)S(1)}, bf16[24,896]{1,0:T(8,128)(2,1)S(1)}, u32[]{:S(2)}, u32[]{:S(2)}) collective-permute-start(bf16[24,896]{1,0:T(8,128)(2,1)S(1)} %get-tuple-element.262), channel_id=1, source_target_pairs={{0,16},{1,17},{2,18},{3,19},{4,20},{5,21},{6,22},{7,23},{8,24},{9,... | collective-permute-start | bytes 129032 | tf_op jit(solution)/shard_map/ppermute | solution.py:339
  20.0 59.3 %collective-permute-start.13 = (bf16[1,750,768]{2,1,0:T(8,128)(2,1)S(1)}, bf16[1,750,768]{2,1,0:T(8,128)(2,1)}, u32[]{:S(2)}, u32[]{:S(2)}) collective-permute-start(bf16[1,750,768]{2,1,0:T(8,128)(2,1)S(1)} %copy-done.2), channel_id=1, source_target_pairs={{0,1},{1,0},{2,3},{3,2},{4,5},{5,4},{6,7},{7,6},{8,9},{9,8},{10,11... | collective-permute-start | bytes 3456008 | tf_op jit(solution)/shard_map/ppermute | solution.py:423
  21.6 35.1 %collective-permute-start.9 = (bf16[2,24,768]{2,1,0:T(8,128)(2,1)S(1)}, bf16[2,24,768]{2,1,0:T(8,128)(2,1)S(1)}, u32[]{:S(2)}, u32[]{:S(2)}) collective-permute-start(bf16[2,24,768]{2,1,0:T(8,128)(2,1)S(1)} %maximum_select_fusion.18), channel_id=1, source_target_pairs={{0,4},{1,5},{2,6},{3,7},{4,0},{5,1},{6,2},{7,3},{8,12},{9,13},{10,... | collective-permute-start | bytes 221192 | tf_op jit(solution)/shard_map/ppermute | solution.py:339
  23.2 31.8 %collective-permute-start.5 = (bf16[2,24,768]{2,1,0:T(8,128)(2,1)S(1)}, bf16[2,24,768]{2,1,0:T(8,128)(2,1)S(1)}, u32[]{:S(2)}, u32[]{:S(2)}) collective-permute-start(bf16[2,24,768]{2,1,0:T(8,128)(2,1)S(1)} %maximum_select_fusion.17), channel_id=1, source_target_pairs={{0,1},{1,0},{2,3},{3,2},{4,5},{5,4},{6,7},{7,6},{8,9},{9,8},{10,11... | collective-permute-start | bytes 221192 | tf_op jit(solution)/shard_map/ppermute | solution.py:339
  23.9 34.4 %collective-permute-start.1 = (bf16[2,24,896]{2,1,0:T(8,128)(2,1)S(1)}, bf16[2,24,896]{2,1,0:T(8,128)(2,1)S(1)}, u32[]{:S(2)}, u32[]{:S(2)}) collective-permute-start(bf16[2,24,896]{2,1,0:T(8,128)(2,1)S(1)} %maximum_select_fusion.15), channel_id=1, source_target_pairs={{0,8},{1,9},{2,10},{3,11},{4,12},{5,13},{6,14},{7,15},{8,0},{9,1},... | collective-permute-start | bytes 258056 | tf_op jit(solution)/shard_map/ppermute | solution.py:339
  55.0 10.8 %collective-permute-start.6 = (bf16[2,2,24,768]{3,2,0,1:T(8,128)(2,1)S(1)}, bf16[2,2,24,768]{3,2,0,1:T(8,128)(2,1)S(1)}, u32[]{:S(2)}, u32[]{:S(2)}) collective-permute-start(bf16[2,2,24,768]{3,2,0,1:T(8,128)(2,1)S(1)} %maximum_select_fusion.12), channel_id=1, source_target_pairs={{0,8},{1,9},{2,10},{3,11},{4,12},{5,13},{6,14},{7,15},{8,0},{9,1},... | collective-permute-start | bytes 442376 | tf_op jit(solution)/shard_map/ppermute | solution.py:339
  56.7 5.2 %collective-permute-start.10 = (bf16[2,2,24,768]{3,2,1,0:T(8,128)(2,1)S(1)}, bf16[2,2,24,768]{3,2,1,0:T(8,128)(2,1)S(1)}, u32[]{:S(2)}, u32[]{:S(2)}) collective-permute-start(bf16[2,2,24,768]{3,2,1,0:T(8,128)(2,1)S(1)} %maximum_select_fusion.13), channel_id=1, source_target_pairs={{0,1},{1,0},{2,3},{3,2},{4,5},{5,4},{6,7},{7,6},{8,9},{9,8},{10,11... | collective-permute-start | bytes 442376 | tf_op jit(solution)/shard_map/ppermute | solution.py:339
  58.5 9.1 %collective-permute-start.2 = (bf16[2,2,24,896]{3,2,0,1:T(8,128)(2,1)S(1)}, bf16[2,2,24,896]{3,2,0,1:T(8,128)(2,1)S(1)}, u32[]{:S(2)}, u32[]{:S(2)}) collective-permute-start(bf16[2,2,24,896]{3,2,0,1:T(8,128)(2,1)S(1)} %maximum_select_fusion.10), channel_id=1, source_target_pairs={{0,4},{1,5},{2,6},{3,7},{4,0},{5,1},{6,2},{7,3},{8,12},{9,13},{10,... | collective-permute-start | bytes 516104 | tf_op jit(solution)/shard_map/ppermute | solution.py:339
  61.9 10.8 %collective-permute-start.11 = (bf16[2,2,2,24,768]{4,3,2,1,0:T(8,128)(2,1)S(1)}, bf16[2,2,2,24,768]{4,3,2,1,0:T(8,128)(2,1)S(1)}, u32[]{:S(2)}, u32[]{:S(2)}) collective-permute-start(bf16[2,2,2,24,768]{4,3,2,1,0:T(8,128)(2,1)S(1)} %maximum_select_fusion.8), channel_id=1, source_target_pairs={{0,8},{1,9},{2,10},{3,11},{4,12},{5,13},{6,14},{7,15},{8,0},{9,1},... | collective-permute-start | bytes 884744 | tf_op jit(solution)/shard_map/ppermute | solution.py:339
  65.9 6.8 %collective-permute-start.7 = (bf16[2,2,2,24,768]{4,3,0,2,1:T(8,128)(2,1)S(1)}, bf16[2,2,2,24,768]{4,3,0,2,1:T(8,128)(2,1)S(1)}, u32[]{:S(2)}, u32[]{:S(2)}) collective-permute-start(bf16[2,2,2,24,768]{4,3,0,2,1:T(8,128)(2,1)S(1)} %maximum_select_fusion.7), channel_id=1, source_target_pairs={{0,4},{1,5},{2,6},{3,7},{4,0},{5,1},{6,2},{7,3},{8,12},{9,13},{10,... | collective-permute-start | bytes 884744 | tf_op jit(solution)/shard_map/ppermute | solution.py:339
  67.7 9.1 %collective-permute-start.3 = (bf16[2,2,2,24,896]{4,3,0,1,2:T(8,128)(2,1)S(1)}, bf16[2,2,2,24,896]{4,3,0,1,2:T(8,128)(2,1)S(1)}, u32[]{:S(2)}, u32[]{:S(2)}) collective-permute-start(bf16[2,2,2,24,896]{4,3,0,1,2:T(8,128)(2,1)S(1)} %maximum_select_fusion.5), channel_id=1, source_target_pairs={{0,1},{1,0},{2,3},{3,2},{4,5},{5,4},{6,7},{7,6},{8,9},{9,8},{10,11... | collective-permute-start | bytes 1032200 | tf_op jit(solution)/shard_map/ppermute | solution.py:339
  78.5 4.7 collective-permute-start.12
  78.7 11.7 %copy-start.53 = (f32[750]{0:T(1024)}, f32[750]{0:T(1024)S(1)}, u32[]{:S(2)}) copy-start(f32[750]{0:T(1024)S(1)} %broadcast_multiply_fusion.6) | copy-start | bytes 9004
  79.3 11.1 %copy-start.57 = (f32[750]{0:T(1024)}, f32[750]{0:T(1024)S(1)}, u32[]{:S(2)}) copy-start(f32[750]{0:T(1024)S(1)} %add_rsqrt_fusion.2) | copy-start | bytes 9004
  90.4 71.4 %copy-start.64 = (f32[768]{0:T(1024)}, f32[768]{0:T(1024)S(1)}, u32[]{:S(2)}) copy-start(f32[768]{0:T(1024)S(1)} %get-tuple-element.221) | copy-start | bytes 9220
  161.7 21.9 %copy-start.14 = (bf16[1,750,768]{2,1,0:T(8,128)(2,1)S(1)}, bf16[1,750,768]{2,1,0:T(8,128)(2,1)}, u32[]{:S(2)}) copy-start(bf16[1,750,768]{2,1,0:T(8,128)(2,1)} %param.15) | copy-start | bytes 3456004
  197.8 9.5 %copy-start.7 = (f32[750,768]{1,0:T(8,128)S(1)}, f32[750,768]{1,0:T(8,128)}, u32[]{:S(2)}) copy-start(f32[750,768]{1,0:T(8,128)} %copy-done.6) | copy-start | bytes 6912004
  197.8 9.5 %copy-start.65 = (f32[768]{0:T(1024)S(1)}, f32[768]{0:T(1024)}, u32[]{:S(2)}) copy-start(f32[768]{0:T(1024)} %copy-done.64) | copy-start | bytes 9220
  244.9 9.4 %collective-permute-start.14 = (bf16[2,2,2,2,24,6912]{5,4,0,3,2,1:T(8,128)(2,1)}, bf16[2,2,2,2,24,6912]{5,4,0,3,2,1:T(8,128)(2,1)}, u32[]{:S(2)}, u32[]{:S(2)}) collective-permute-start(bf16[2,2,2,2,24,6912]{5,4,0,3,2,1:T(8,128)(2,1)} %bitcast.317), channel_id=1, source_target_pairs={{0,2},{1,3},{2,0},{3,1},{4,6},{5,7},{6,4},{7,5},{8,10},{9,11},{10,... | collective-permute-start | bytes 15925256 | tf_op jit(solution)/shard_map/ppermute | solution.py:320
  267.6 44.6 %collective-permute-start.15 = (bf16[2,2,2,24,3456]{4,3,0,2,1:T(8,128)(2,1)}, bf16[2,2,2,24,3456]{4,3,0,2,1:T(8,128)(2,1)}, u32[]{:S(2)}, u32[]{:S(2)}) collective-permute-start(bf16[2,2,2,24,3456]{4,3,0,2,1:T(8,128)(2,1)} %fusion.42), channel_id=1, source_target_pairs={{0,4},{1,5},{2,6},{3,7},{4,0},{5,1},{6,2},{7,3},{8,12},{9,13},{10,... | collective-permute-start | bytes 3981320 | tf_op jit(solution)/shard_map/ppermute | solution.py:320
  287.7 12.0 %collective-permute-start.23 = (bf16[750,256]{1,0:T(8,128)(2,1)}, bf16[750,256]{1,0:T(8,128)(2,1)S(1)}, u32[]{:S(2)}, u32[]{:S(2)}) collective-permute-start(bf16[750,256]{1,0:T(8,128)(2,1)} %fusion.68), channel_id=1, source_target_pairs={{0,1},{1,0},{2,3},{3,2},{4,5},{5,4},{6,7},{7,6},{8,9},{9,8},{10,11... | collective-permute-start | bytes 1152008 | tf_op jit(solution)/shard_map/ppermute | solution.py:512
  293.1 31.4 %collective-permute-start.16 = (bf16[2,2,2,24,3456]{4,3,0,2,1:T(8,128)(2,1)}, bf16[2,2,2,24,3456]{4,3,0,2,1:T(8,128)(2,1)}, u32[]{:S(2)}, u32[]{:S(2)}) collective-permute-start(bf16[2,2,2,24,3456]{4,3,0,2,1:T(8,128)(2,1)} %fusion.43), channel_id=1, source_target_pairs={{0,8},{1,9},{2,10},{3,11},{4,12},{5,13},{6,14},{7,15},{8,0},{9,1},... | collective-permute-start | bytes 3981320 | tf_op jit(solution)/shard_map/ppermute | solution.py:320
  301.6 22.9 %slice-start.2 = ((s8[5308416]{0:T(1024)(128)(4,1)}), s8[4194304]{0:T(1024)(128)(4,1)S(1)}, s32[]{:S(2)}) async-start(s8[5308416]{0:T(1024)(128)(4,1)} %bitcast.320), calls=%async_computation.3 | async-start | bytes 8388608
  301.7 22.8 %slice-start.3 = ((s8[5308416]{0:T(1024)(128)(4,1)}), s8[1114112]{0:T(1024)(128)(4,1)S(1)}, s32[]{:S(2)}) async-start(s8[5308416]{0:T(1024)(128)(4,1)} %bitcast.320), calls=%async_computation.4 | async-start | bytes 2228224
  326.2 16.1 %collective-permute-start.18 = (bf16[2,2,24,3456]{3,2,0,1:T(8,128)(2,1)S(1)}, bf16[2,2,24,3456]{3,2,0,1:T(8,128)(2,1)S(1)}, u32[]{:S(2)}, u32[]{:S(2)}) collective-permute-start(bf16[2,2,24,3456]{3,2,0,1:T(8,128)(2,1)S(1)} %fusion.70), channel_id=1, source_target_pairs={{0,4},{1,5},{2,6},{3,7},{4,0},{5,1},{6,2},{7,3},{8,12},{9,13},{10,... | collective-permute-start | bytes 1990664 | tf_op jit(solution)/shard_map/ppermute | solution.py:320
  328.2 12.3 %collective-permute-start.24 = (bf16[750,256]{1,0:T(8,128)(2,1)S(1)}, bf16[750,256]{1,0:T(8,128)(2,1)S(1)}, u32[]{:S(2)}, u32[]{:S(2)}) collective-permute-start(bf16[750,256]{1,0:T(8,128)(2,1)S(1)} %slice.581), channel_id=1, source_target_pairs={{0,1},{1,0},{2,3},{3,2},{4,5},{5,4},{6,7},{7,6},{8,9},{9,8},{10,11... | collective-permute-start | bytes 1152008 | tf_op jit(solution)/shard_map/ppermute | solution.py:512
  328.6 15.6 %collective-permute-start.17 = (bf16[2,2,24,3456]{3,2,0,1:T(8,128)(2,1)S(1)}, bf16[2,2,24,3456]{3,2,0,1:T(8,128)(2,1)S(1)}, u32[]{:S(2)}, u32[]{:S(2)}) collective-permute-start(bf16[2,2,24,3456]{3,2,0,1:T(8,128)(2,1)S(1)} %fusion.69), channel_id=1, source_target_pairs={{0,8},{1,9},{2,10},{3,11},{4,12},{5,13},{6,14},{7,15},{8,0},{9,1},... | collective-permute-start | bytes 1990664 | tf_op jit(solution)/shard_map/ppermute | solution.py:320
  344.4 15.1 %collective-permute-start.20 = (bf16[2,24,3456]{2,1,0:T(8,128)(2,1)S(1)}, bf16[2,24,3456]{2,1,0:T(8,128)(2,1)S(1)}, u32[]{:S(2)}, u32[]{:S(2)}) collective-permute-start(bf16[2,24,3456]{2,1,0:T(8,128)(2,1)S(1)} %fusion.73), channel_id=1, source_target_pairs={{0,1},{1,0},{2,3},{3,2},{4,5},{5,4},{6,7},{7,6},{8,9},{9,8},{10,11... | collective-permute-start | bytes 995336 | tf_op jit(solution)/shard_map/ppermute | solution.py:320
  345.9 15.0 %collective-permute-start.19 = (bf16[2,24,3456]{2,1,0:T(8,128)(2,1)S(1)}, bf16[2,24,3456]{2,1,0:T(8,128)(2,1)S(1)}, u32[]{:S(2)}, u32[]{:S(2)}) collective-permute-start(bf16[2,24,3456]{2,1,0:T(8,128)(2,1)S(1)} %fusion.72), channel_id=1, source_target_pairs={{0,1},{1,0},{2,3},{3,2},{4,5},{5,4},{6,7},{7,6},{8,9},{9,8},{10,11... | collective-permute-start | bytes 995336 | tf_op jit(solution)/shard_map/ppermute | solution.py:320
  357.2 22.3 %collective-permute-start.25 = (bf16[750,256]{1,0:T(8,128)(2,1)S(1)}, bf16[750,256]{1,0:T(8,128)(2,1)S(1)}, u32[]{:S(2)}, u32[]{:S(2)}) collective-permute-start(bf16[750,256]{1,0:T(8,128)(2,1)S(1)} %slice.580), channel_id=1, source_target_pairs={{0,1},{1,0},{2,3},{3,2},{4,5},{5,4},{6,7},{7,6},{8,9},{9,8},{10,11... | collective-permute-start | bytes 1152008 | tf_op jit(solution)/shard_map/ppermute | solution.py:512
  361.1 19.3 %collective-permute-start.22 = (bf16[24,3456]{1,0:T(8,128)(2,1)S(1)}, bf16[24,3456]{1,0:T(8,128)(2,1)S(1)}, u32[]{:S(2)}, u32[]{:S(2)}) collective-permute-start(bf16[24,3456]{1,0:T(8,128)(2,1)S(1)} %fusion.89), channel_id=1, source_target_pairs={{0,16},{1,17},{2,18},{3,19},{4,20},{5,21},{6,22},{7,23},{8,24},{9,... | collective-permute-start | bytes 497672 | tf_op jit(solution)/shard_map/ppermute | solution.py:320
  361.1 19.2 %collective-permute-start.21 = (bf16[24,3456]{1,0:T(8,128)(2,1)S(1)}, bf16[24,3456]{1,0:T(8,128)(2,1)S(1)}, u32[]{:S(2)}, u32[]{:S(2)}) collective-permute-start(bf16[24,3456]{1,0:T(8,128)(2,1)S(1)} %fusion.88), channel_id=1, source_target_pairs={{0,16},{1,17},{2,18},{3,19},{4,20},{5,21},{6,22},{7,23},{8,24},{9,... | collective-permute-start | bytes 497672 | tf_op jit(solution)/shard_map/ppermute | solution.py:320
  377.6 24.1 %collective-permute-start.26 = (bf16[750,256]{1,0:T(8,128)(2,1)}, bf16[750,256]{1,0:T(8,128)(2,1)}, u32[]{:S(2)}, u32[]{:S(2)}) collective-permute-start(bf16[750,256]{1,0:T(8,128)(2,1)} %slice.579), channel_id=1, source_target_pairs={{0,1},{1,0},{2,3},{3,2},{4,5},{5,4},{6,7},{7,6},{8,9},{9,8},{10,11... | collective-permute-start | bytes 1152008 | tf_op jit(solution)/shard_map/ppermute | solution.py:512
  384.5 12.0 %copy-start.47 = (f32[24,768]{1,0:T(8,128)}, f32[24,768]{1,0:T(8,128)S(1)}, u32[]{:S(2)}) copy-start(f32[24,768]{1,0:T(8,128)S(1)} %get-tuple-element.231) | copy-start | bytes 221188
  396.7 13.7 %collective-permute-start.28 = (bf16[750,256]{1,0:T(8,128)(2,1)S(1)}, bf16[750,256]{1,0:T(8,128)(2,1)S(1)}, u32[]{:S(2)}, u32[]{:S(2)}) collective-permute-start(bf16[750,256]{1,0:T(8,128)(2,1)S(1)} %fusion.63), channel_id=1, source_target_pairs={{0,1},{1,0},{2,3},{3,2},{4,5},{5,4},{6,7},{7,6},{8,9},{9,8},{10,11... | collective-permute-start | bytes 1152008 | tf_op jit(solution)/shard_map/ppermute | solution.py:512
  399.5 10.6 %collective-permute-start.27 = (bf16[750,256]{1,0:T(8,128)(2,1)S(1)}, bf16[750,256]{1,0:T(8,128)(2,1)S(1)}, u32[]{:S(2)}, u32[]{:S(2)}) collective-permute-start(bf16[750,256]{1,0:T(8,128)(2,1)S(1)} %slice.578), channel_id=1, source_target_pairs={{0,1},{1,0},{2,3},{3,2},{4,5},{5,4},{6,7},{7,6},{8,9},{9,8},{10,11... | collective-permute-start | bytes 1152008 | tf_op jit(solution)/shard_map/ppermute | solution.py:512
  421.2 8.5 %copy-start.41 = (bf16[768,1]{1,0:T(8,128)(2,1)S(1)}, bf16[768,1]{1,0:T(8,128)(2,1)}, u32[]{:S(2)}) copy-start(bf16[768,1]{1,0:T(8,128)(2,1)} %stack.422) | copy-start | bytes 4612
  421.2 8.5 %copy-start.42 = (bf16[768,4]{1,0:T(8,128)(2,1)S(1)}, bf16[768,4]{1,0:T(8,128)(2,1)}, u32[]{:S(2)}) copy-start(bf16[768,4]{1,0:T(8,128)(2,1)} %reshape.1154) | copy-start | bytes 18436
  421.2 8.5 %copy-start.43 = (bf16[768,1]{1,0:T(8,128)(2,1)S(1)}, bf16[768,1]{1,0:T(8,128)(2,1)}, u32[]{:S(2)}) copy-start(bf16[768,1]{1,0:T(8,128)(2,1)} %stack.419) | copy-start | bytes 4612
  439.3 3.9 collective-permute-start.29
  443.9 9.1 %collective-permute-start.38 = (bf16[2,2,2,24,768]{4,3,2,1,0:T(8,128)(2,1)S(1)}, bf16[2,2,2,24,768]{4,3,2,1,0:T(8,128)(2,1)S(1)}, u32[]{:S(2)}, u32[]{:S(2)}) collective-permute-start(bf16[2,2,2,24,768]{4,3,2,1,0:T(8,128)(2,1)S(1)} %fusion.83), channel_id=1, source_target_pairs={{0,8},{1,9},{2,10},{3,11},{4,12},{5,13},{6,14},{7,15},{8,0},{9,1},... | collective-permute-start | bytes 884744 | tf_op jit(solution)/shard_map/ppermute | solution.py:320
  447.9 9.1 %collective-permute-start.34 = (bf16[2,2,2,24,768]{4,3,2,1,0:T(8,128)(2,1)S(1)}, bf16[2,2,2,24,768]{4,3,2,1,0:T(8,128)(2,1)S(1)}, u32[]{:S(2)}, u32[]{:S(2)}) collective-permute-start(bf16[2,2,2,24,768]{4,3,2,1,0:T(8,128)(2,1)S(1)} %fusion.82), channel_id=1, source_target_pairs={{0,4},{1,5},{2,6},{3,7},{4,0},{5,1},{6,2},{7,3},{8,12},{9,13},{10,... | collective-permute-start | bytes 884744 | tf_op jit(solution)/shard_map/ppermute | solution.py:320
  449.6 11.0 %collective-permute-start.30 = (bf16[2,2,2,24,896]{4,3,2,1,0:T(8,128)(2,1)S(1)}, bf16[2,2,2,24,896]{4,3,2,1,0:T(8,128)(2,1)S(1)}, u32[]{:S(2)}, u32[]{:S(2)}) collective-permute-start(bf16[2,2,2,24,896]{4,3,2,1,0:T(8,128)(2,1)S(1)} %fusion.71), channel_id=1, source_target_pairs={{0,1},{1,0},{2,3},{3,2},{4,5},{5,4},{6,7},{7,6},{8,9},{9,8},{10,11... | collective-permute-start | bytes 1032200 | tf_op jit(solution)/shard_map/ppermute | solution.py:320
  453.2 9.5 %collective-permute-start.39 = (bf16[2,2,24,768]{3,2,1,0:T(8,128)(2,1)S(1)}, bf16[2,2,24,768]{3,2,1,0:T(8,128)(2,1)S(1)}, u32[]{:S(2)}, u32[]{:S(2)}) collective-permute-start(bf16[2,2,24,768]{3,2,1,0:T(8,128)(2,1)S(1)} %fusion.91), channel_id=1, source_target_pairs={{0,1},{1,0},{2,3},{3,2},{4,5},{5,4},{6,7},{7,6},{8,9},{9,8},{10,11... | collective-permute-start | bytes 442376 | tf_op jit(solution)/shard_map/ppermute | solution.py:320
  457.1 6.1 %collective-permute-start.35 = (bf16[2,2,24,768]{3,2,1,0:T(8,128)(2,1)S(1)}, bf16[2,2,24,768]{3,2,1,0:T(8,128)(2,1)S(1)}, u32[]{:S(2)}, u32[]{:S(2)}) collective-permute-start(bf16[2,2,24,768]{3,2,1,0:T(8,128)(2,1)S(1)} %fusion.90), channel_id=1, source_target_pairs={{0,8},{1,9},{2,10},{3,11},{4,12},{5,13},{6,14},{7,15},{8,0},{9,1},... | collective-permute-start | bytes 442376 | tf_op jit(solution)/shard_map/ppermute | solution.py:320
  460.7 12.4 %copy-start.67 = (f32[2,96]{1,0:T(2,128)S(1)}, f32[2,96]{1,0:T(2,128)}, u32[]{:S(2)}) copy-start(f32[2,96]{1,0:T(2,128)} %param.26) | copy-start | bytes 2308
  460.7 12.4 %copy-start.70 = (f32[96]{0:T(128)S(1)}, f32[96]{0:T(128)}, u32[]{:S(2)}) copy-start(f32[96]{0:T(128)} %param.20) | copy-start | bytes 1156
  460.7 12.9 %copy-start.50 = (f32[24,8]{1,0:T(8,128)S(1)}, f32[24,8]{1,0:T(8,128)}, u32[]{:S(2)}) copy-start(f32[24,8]{1,0:T(8,128)} %copy.152) | copy-start | bytes 2308
  460.7 12.9 %copy-start.51 = (f32[1,24,8]{2,1,0:T(8,128)S(1)}, f32[1,24,8]{2,1,0:T(8,128)}, u32[]{:S(2)}) copy-start(f32[1,24,8]{2,1,0:T(8,128)} %copy.162) | copy-start | bytes 2308
  460.7 12.9 %copy-start.52 = (f32[1,24,8]{2,1,0:T(8,128)S(1)}, f32[1,24,8]{2,1,0:T(8,128)}, u32[]{:S(2)}) copy-start(f32[1,24,8]{2,1,0:T(8,128)} %copy.161) | copy-start | bytes 2308
  460.8 10.2 %collective-permute-start.31 = (bf16[2,2,24,896]{3,2,1,0:T(8,128)(2,1)S(1)}, bf16[2,2,24,896]{3,2,1,0:T(8,128)(2,1)S(1)}, u32[]{:S(2)}, u32[]{:S(2)}) collective-permute-start(bf16[2,2,24,896]{3,2,1,0:T(8,128)(2,1)S(1)} %fusion.87), channel_id=1, source_target_pairs={{0,4},{1,5},{2,6},{3,7},{4,0},{5,1},{6,2},{7,3},{8,12},{9,13},{10,... | collective-permute-start | bytes 516104 | tf_op jit(solution)/shard_map/ppermute | solution.py:320
  462.7 17.9 %copy-start.37 = (f32[2,24,2304]{2,1,0:T(8,128)S(1)}, f32[2,24,2304]{2,1,0:T(8,128)}, u32[]{:S(2)}) copy-start(f32[2,24,2304]{2,1,0:T(8,128)} %param.22) | copy-start | bytes 1327108
  462.7 5.1 %collective-permute-start.40 = (bf16[2,24,768]{2,1,0:T(8,128)(2,1)S(1)}, bf16[2,24,768]{2,1,0:T(8,128)(2,1)S(1)}, u32[]{:S(2)}, u32[]{:S(2)}) collective-permute-start(bf16[2,24,768]{2,1,0:T(8,128)(2,1)S(1)} %fusion.96), channel_id=1, source_target_pairs={{0,4},{1,5},{2,6},{3,7},{4,0},{5,1},{6,2},{7,3},{8,12},{9,13},{10,... | collective-permute-start | bytes 221192 | tf_op jit(solution)/shard_map/ppermute | solution.py:320
  463.3 17.4 %copy-start.40 = (f32[24,2304]{1,0:T(8,128)S(1)}, f32[24,2304]{1,0:T(8,128)}, u32[]{:S(2)}) copy-start(f32[24,2304]{1,0:T(8,128)} %param.16) | copy-start | bytes 663556
  463.3 5.0 %collective-permute-start.36 = (bf16[2,24,768]{2,1,0:T(8,128)(2,1)S(1)}, bf16[2,24,768]{2,1,0:T(8,128)(2,1)S(1)}, u32[]{:S(2)}, u32[]{:S(2)}) collective-permute-start(bf16[2,24,768]{2,1,0:T(8,128)(2,1)S(1)} %fusion.95), channel_id=1, source_target_pairs={{0,1},{1,0},{2,3},{3,2},{4,5},{5,4},{6,7},{7,6},{8,9},{9,8},{10,11... | collective-permute-start | bytes 221192 | tf_op jit(solution)/shard_map/ppermute | solution.py:320
  467.8 4.9 %collective-permute-start.41 = (bf16[24,768]{1,0:T(8,128)(2,1)S(1)}, bf16[24,768]{1,0:T(8,128)(2,1)S(1)}, u32[]{:S(2)}, u32[]{:S(2)}) collective-permute-start(bf16[24,768]{1,0:T(8,128)(2,1)S(1)} %fusion.102), channel_id=1, source_target_pairs={{0,16},{1,17},{2,18},{3,19},{4,20},{5,21},{6,22},{7,23},{8,24},{9,... | collective-permute-start | bytes 110600 | tf_op jit(solution)/shard_map/ppermute | solution.py:320
  468.3 5.7 %collective-permute-start.37 = (bf16[24,768]{1,0:T(8,128)(2,1)S(1)}, bf16[24,768]{1,0:T(8,128)(2,1)S(1)}, u32[]{:S(2)}, u32[]{:S(2)}) collective-permute-start(bf16[24,768]{1,0:T(8,128)(2,1)S(1)} %fusion.101), channel_id=1, source_target_pairs={{0,16},{1,17},{2,18},{3,19},{4,20},{5,21},{6,22},{7,23},{8,24},{9,... | collective-permute-start | bytes 110600 | tf_op jit(solution)/shard_map/ppermute | solution.py:320
  471.0 4.6 collective-permute-start.32
  473.0 9.4 %copy-start.69 = (f32[96]{0:T(128)}, f32[96]{0:T(128)S(1)}, u32[]{:S(2)}) copy-start(f32[96]{0:T(128)S(1)} %reshape.1157) | copy-start | bytes 1156
  475.6 5.0 %collective-permute-start.33 = (bf16[24,896]{1,0:T(8,128)(2,1)S(1)}, bf16[24,896]{1,0:T(8,128)(2,1)S(1)}, u32[]{:S(2)}, u32[]{:S(2)}) collective-permute-start(bf16[24,896]{1,0:T(8,128)(2,1)S(1)} %fusion.100), channel_id=1, source_target_pairs={{0,16},{1,17},{2,18},{3,19},{4,20},{5,21},{6,22},{7,23},{8,24},{9,... | collective-permute-start | bytes 129032 | tf_op jit(solution)/shard_map/ppermute | solution.py:320
  (56 other events, 183.8 us)
Sparse Core Ops, SparseCore 0:
  11.5 97.3 all-gather.1

commit v19 on v18

--- a/solution.py
+++ b/solution.py
@@ -501,7 +501,7 @@
     hooks.update({index: piece_hook(index) for index in hooked})
     pieces = [run_piece(0, grad_mixed)]
     owned_late, tied = tree_reduce_scatter(
-        late_terms, (3456, 3456), late_orders, (bit_count, core_bit), hooks
+        late_terms, (2304, 2304, 2304), rotated_orders, (bit_count, core_bit), hooks
     )
     pieces += [tied[index][0] for index in hooked]
     last_mixed = tied[hooked[-1]][1] if hooked else grad_mixed

time: 489 us -> 472 us (0.965); the launches traced: 489 us -> 467 us
  matrix products: 83 us -> 68.5 us
  local copies, waits for them, and re-layouts: 95.3 us -> 90.4 us
    dot_general x1, matrix products: 19.7 us -> 7.8 us  [body(): jnp.dot(hidden_second, full_expand, preferred_element_type=jnp.float32)]
    unnamed x178 -> x194, local copies, waits for them, and re-layouts: 29 us -> 20.5 us
    ppermute x22 -> x26, starting transfers between devices: 21.1 us -> 25.9 us  [tree_reduce_scatter(): got = lax.ppermute(send, ('clip', 'frame'), pairs)]
    add x22 -> x26, other arithmetic: 10.4 us -> 7.09 us  [tree_reduce_scatter(): keep + got.astype(jnp.float32)]
    ppermute x22 -> x26, waiting for transfers between devices: 33.1 us -> 30 us  [tree_reduce_scatter(): got = lax.ppermute(send, ('clip', 'frame'), pairs)]
  transfers between devices with their start and end apart: 43 -> 47, of which waited for: 22 -> 22; matrix products, arithmetic and copies ran while one was open for 16% -> 17% of each run, Pallas kernels for 20% -> 22%
where the time goes in v19:
time: 472 us; the launch traced here: 467 us
  Pallas kernels  101 us (21%)
  local copies, waits for them, and re-layouts  90.4 us (19%)
  waiting for transfers between devices  80.8 us (17%)
  matrix products  68.5 us (15%)
  other arithmetic  58.1 us (12%)
  starting transfers between devices  51.7 us (11%)
  between operations  16.6 us (4%)
    pallas_call x6, Pallas kernels, attention_pallas(): pl.pallas_call(attention_backward_kernel, grid=(span,), in_specs=[qi_spec...  63.4 us
    ppermute x13, waiting for transfers between devices, double(): got = lax.ppermute(data, ('clip', 'frame'), pairs)  44 us
    pallas_call x1, Pallas kernels, attention_pallas(): pl.pallas_call(attention_forward_kernel, grid=(pair_count,), in_specs=[q_...  37.3 us
    ppermute x26, waiting for transfers between devices, tree_reduce_scatter(): got = lax.ppermute(send, ('clip', 'frame'), pairs)  30 us
    ppermute x26, starting transfers between devices, tree_reduce_scatter(): got = lax.ppermute(send, ('clip', 'frame'), pairs)  25.9 us
    unnamed x194, local copies, waits for them, and re-layouts  20.5 us
    ppermute x13, starting transfers between devices, double(): got = lax.ppermute(data, ('clip', 'frame'), pairs)  18 us
  transfers between devices with their start and end apart: 47, of which 22 were waited for; matrix products, arithmetic and copies ran while one was open for 17% of the time, Pallas kernels for 22%

profile of v19, /device:TPU:0, one launch (start us, length us, event | category | flops | bytes accessed | tf_op | source)
XLA Modules:
  0.0 466.7 jit_solution(17516165313123895527)
XLA Ops:
  11.5 4.1 collective-permute-start.8
  15.7 3.0 collective-permute-start.4
  25.8 29.5 %collective-permute-done.5 = bf16[2,24,768]{2,1,0:T(8,128)(2,1)S(1)} collective-permute-done((bf16[2,24,768]{2,1,0:T(8,128)(2,1)S(1)}, bf16[2,24,768]{2,1,0:T(8,128)(2,1)S(1)}, u32[]{:S(2)}, u32[]{:S(2)}) %collective-permute-start.5) | collective-permute-done | bytes 73760 | tf_op jit(solution)/shard_map/ppermute | solution.py:339
  55.3 1.6 collective-permute-start.6
  59.3 7.7 %collective-permute-done.6 = bf16[2,2,24,768]{3,2,0,1:T(8,128)(2,1)S(1)} collective-permute-done((bf16[2,2,24,768]{3,2,0,1:T(8,128)(2,1)S(1)}, bf16[2,2,24,768]{3,2,0,1:T(8,128)(2,1)S(1)}, u32[]{:S(2)}, u32[]{:S(2)}) %collective-permute-start.6) | collective-permute-done | bytes 147488 | tf_op jit(solution)/shard_map/ppermute | solution.py:339
  71.4 2.4 collective-permute-done.7
  73.9 2.0 collective-permute-done.3
  76.0 1.7 fusion.120
  80.0 1.8 fusion.37
  82.4 3.3 maximum_select_fusion
  86.8 2.0 slice_reduce_fusion
  89.4 3.5 add_convert_fusion
  93.1 1.6 copy-done.15
  96.1 4.3 add_convert_fusion.1
  100.5 3.0 fusion.8.k_ref.v_ref
  103.5 37.3 %shard_map.293 = (bf16[768,768]{1,0:T(8,128)(2,1)S(1)}, f32[768,768]{1,0:T(8,128)S(1)}) custom-call(bf16[768,768]{1,0:T(8,128)(2,1)S(1)} %pad.39.q_ref, bf16[1536,1536]{1,0:T(8,128)(2,1)} %fusion.8.k_ref.v_ref, bf16[1536,1536]{1,0:T(8,128)(2,1)} %fusion.8.k_ref.v_ref, f32[1,1536]{1,0:T(1,128)S(1)} %compare_select_fusion.kbias_ref), custom_call_target="tpu_custom_call" | custom-call | tf_op jit(solution)/shard_map/pallas_call | solution.py:161
  142.2 2.5 fusion.125
  146.4 4.8 %slice.414 = bf16[768,3072]{1,0:T(8,128)(2,1)} slice(bf16[768,6912]{1,0:T(8,128)(2,1)} %all-gather.2.cloned.1.call-done), slice={[0:768], [3840:6912]} | slice | bytes 9437184 | tf_op jit(solution)/shard_map/slice | solution.py:416
  151.2 8.6 %reshape.1154 = bf16[3072,768]{1,0:T(8,128)(2,1)} reshape(bf16[768,3072]{1,0:T(8,128)(2,1)} %slice.414) | data formatting | bytes 9437184 | tf_op jit(solution)/shard_map/reshape | solution.py:416
  159.8 7.8 %multiply_convert_fusion = (bf16[750,3072]{1,0:T(8,128)(2,1)S(1)}, f32[750,3072]{1,0:T(8,128)S(1)}) fusion(f32[3072]{0:T(1024)S(1)} %add.451, bf16[768,6912]{1,0:T(8,128)(2,1)} %all-gather.2.cloned.1.call-done, f32[750,768]{1,0:T(8,128)} %copy-done.12, f32[768]{0:T(1024)S(1)} %get-tuple-element.229, f32[768]{0:T(1024)S(1)} %get-tuple-element.230, ...), kind=kOutput, calls=%fused_computation.12 | convolution fusion | flops 3555648000 | bytes 20877168 | tf_op jit(solution)/shard_map/dot_general | solution.py:451
  167.7 8.3 %fusion.126 = (bf16[3072]{0:T(1024)(128)(2,1)}, bf16[750,3072]{1,0:T(8,128)(2,1)S(1)}) fusion(f32[750,3072]{1,0:T(8,128)S(1)} %get-tuple-element.288, f32[3072]{0:T(1024)S(1)} %add.451, bf16[3072,768]{1,0:T(8,128)(2,1)S(1)} %copy-done.18, bf16[1,750,768]{2,1,0:T(8,128)(2,1)S(1)} %copy-done.19), kind=kOutput, calls=%fused_computation.336 | convolution fusion | flops 3566588928 | bytes 19713024 | tf_op jit(solution)/shard_map/dot_general | solution.py:465
  175.9 6.4 %convolution_convert_fusion.1 = bf16[768,3072]{1,0:T(8,128)(2,1)} fusion(bf16[750,3072]{1,0:T(8,128)(2,1)S(1)} %get-tuple-element.291, f32[750,768]{1,0:T(8,128)S(1)} %copy-done.13, f32[768]{0:T(1024)S(1)} %get-tuple-element.229, f32[768]{0:T(1024)S(1)} %get-tuple-element.230, f32[750]{0:T(1024)S(1)} %add_rsqrt_fusion, f32[750]{0:T(1024)S(1)} %broadcast_multiply_fusion.4), kind=kOutput, calls=%fused_computation.18 | convolution fusion | flops 3544183296 | bytes 11642736 | tf_op jit(solution)/shard_map/dot_general | solution.py:467
  182.3 7.3 %multiply_reduce_fusion = (bf16[768]{0:T(1024)(128)(2,1)}, f32[750]{0:T(1024)S(1)}, f32[750]{0:T(1024)S(1)}, bf16[768]{0:T(1024)(128)(2,1)}, f32[750,768]{1,0:T(8,128)S(1)}) fusion(f32[750,768]{1,0:T(8,128)S(1)} %copy-done.13, f32[750]{0:T(1024)S(1)} %add_rsqrt_fusion, f32[750]{0:T(1024)S(1)} %broadcast_multiply_fusion.4, f32[768]{0:T(1024)S(1)} %get-tuple-element.230, ...), kind=kOutput, calls=%fused_computation.60 | convolution fusion | flops 3544124928 | bytes 13952736 | tf_op jit(solution)/shard_map/dot_general | solution.py:471
  190.7 2.2 convolution_convert_fusion.3
  192.9 5.9 %convolution_convert_fusion.2 = bf16[3072,768]{1,0:T(8,128)(2,1)} fusion(bf16[750,3072]{1,0:T(8,128)(2,1)S(1)} %get-tuple-element.287, bf16[1,750,768]{2,1,0:T(8,128)(2,1)S(1)} %copy-done.19), kind=kOutput, calls=%fused_computation.19 | convolution fusion | flops 3541303296 | bytes 10478592 | tf_op jit(solution)/shard_map/dot_general | solution.py:461
  198.7 8.6 %concatenate.313 = bf16[2,2,2,2,2,24,3072]{6,5,4,3,2,1,0:T(8,128)(2,1)} reshape(bf16[3072,768]{1,0:T(8,128)(2,1)} %convolution_convert_fusion.2) | data formatting | bytes 9437184 | tf_op jit(solution)/shard_map/concatenate | solution.py:481
  207.3 8.8 %pad_maximum_fusion = bf16[2,2,2,2,2,24,6912]{6,5,4,3,2,1,0:T(8,128)(2,1)} fusion(bf16[2,2,2,2,2,24,768]{6,5,4,3,2,1,0:T(8,128)(2,1)S(1)} %bitcast.344, bf16[2,2,2,2,2,24,3072]{6,5,4,3,2,1,0:T(8,128)(2,1)} %bitcast.338, bf16[2,2,2,2,2,24,3072]{6,5,4,3,2,1,0:T(8,128)(2,1)} %concatenate.313), kind=kLoop, calls=%fused_computation.1 | loop fusion | flops 31850496 | bytes 21233664 | tf_op jit(solution)/shard_map/concatenate | solution.py:481
  216.1 8.7 %constant_dynamic-slice_fusion.1 = (bf16[2,2,2,1,2,24,6912]{6,5,4,3,2,1,0:T(8,128)(2,1)}, bf16[2,2,2,1,2,24,6912]{6,5,4,3,2,1,0:T(8,128)(2,1)}) fusion(bf16[2,2,2,2,2,24,6912]{6,5,4,3,2,1,0:T(8,128)(2,1)} %pad_maximum_fusion, s32[]{:T(128)S(6)} %select_n.413, s32[]{:T(128)S(6)} %select_n.414), kind=kLoop, calls=%fused_computation.291 | loop fusion | bytes 21233672 | tf_op jit(solution)/shard_map/jit(dynamic_index_in_dim)/dynamic_slice | solution.py:313
  224.8 5.1 %copy.180 = bf16[2,2,2,1,2,24,6912]{6,5,0,2,4,1,3:T(8,128)(2,1)} copy(bf16[2,2,2,1,2,24,6912]{6,5,4,3,2,1,0:T(8,128)(2,1)} %get-tuple-element.247) | data formatting | bytes 10616832
  231.7 3.2 convolution_convert_fusion.4
  235.0 10.7 %shard_map.294 = (f32[768,128]{1,0:T(8,128)S(1)}, f32[1536,128]{1,0:T(8,128)S(1)}, f32[1536,128]{1,0:T(8,128)S(1)}) custom-call(bf16[768,768]{1,0:T(8,128)(2,1)S(1)} %pad.39.q_ref, bf16[1536,1536]{1,0:T(8,128)(2,1)} %fusion.8.k_ref.v_ref, bf16[1536,1536]{1,0:T(8,128)(2,1)} %fusion.8.k_ref.v_ref, bf16[768,768]{1,0:T(8,128)(2,1)S(1)} %pad.41.do_ref, ...), custom_call_target="tpu_custom_call" | custom-call | tf_op jit(solution)/shard_map/pallas_call | solution.py:180
  246.7 2.4 collective-permute-start.27
  249.1 7.1 %fusion.41 = bf16[1,750,768]{2,1,0:T(8,128)(2,1)} fusion(f32[750,768]{1,0:T(8,128)S(1)} %copy-done.14, bf16[750,3072]{1,0:T(8,128)(2,1)} %copy-done.81, bf16[3072,768]{1,0:T(8,128)(2,1)S(1)} %bitcast.337, f32[768]{0:T(1024)S(1)} %copy-done.70), kind=kOutput, calls=%fused_computation.84 | convolution fusion | flops 3540672000 | bytes 12785664 | tf_op jit(solution)/shard_map/dot_general | solution.py:455
  260.7 1.9 fusion.63
  262.6 5.3 %convert_add_fusion = f32[2,2,2,2,24,6912]{5,4,0,2,3,1:T(8,128)S(1)} fusion(bf16[2,2,2,2,24,6912]{5,4,0,2,3,1:T(8,128)(2,1)} %collective-permute-done.14, bf16[2,2,2,1,2,24,6912]{6,5,4,3,2,1,0:T(8,128)(2,1)} %get-tuple-element.246), kind=kLoop, calls=%fused_computation.2 | loop fusion | flops 7962624 | bytes 21233664 | tf_op jit(solution)/shard_map/add | solution.py:321
  267.9 4.8 %copy.145 = f32[2,2,2,2,24,6912]{5,4,0,1,2,3:T(8,128)} copy(f32[2,2,2,2,24,6912]{5,4,0,2,3,1:T(8,128)S(1)} %convert_add_fusion) | data formatting | bytes 21233664 | tf_op jit(solution)/shard_map/optimization_barrier | solution.py:323
  272.8 2.2 slice.416
  281.9 10.5 %shard_map.295 = (f32[768,128]{1,0:T(8,128)S(1)}, f32[1536,128]{1,0:T(8,128)S(1)}, f32[1536,128]{1,0:T(8,128)S(1)}) custom-call(bf16[768,768]{1,0:T(8,128)(2,1)S(1)} %pad.39.q_ref, bf16[1536,1536]{1,0:T(8,128)(2,1)} %fusion.8.k_ref.v_ref, bf16[1536,1536]{1,0:T(8,128)(2,1)} %fusion.8.k_ref.v_ref, bf16[768,768]{1,0:T(8,128)(2,1)S(1)} %pad.42.do_ref, ...), custom_call_target="tpu_custom_call" | custom-call | tf_op jit(solution)/shard_map/pallas_call | solution.py:180
  292.6 6.0 %collective-permute-done.15 = bf16[2,2,2,24,2304]{4,3,0,1,2:T(8,128)(2,1)S(1)} collective-permute-done((bf16[2,2,2,24,2304]{4,3,0,1,2:T(8,128)(2,1)}, bf16[2,2,2,24,2304]{4,3,0,1,2:T(8,128)(2,1)S(1)}, u32[]{:S(2)}, u32[]{:S(2)}) %collective-permute-start.15) | collective-permute-done | bytes 884768 | tf_op jit(solution)/shard_map/ppermute | solution.py:320
  298.8 1.6 collective-permute-done.16
  301.1 1.6 collective-permute-start.18
  306.3 10.3 %shard_map.296 = (f32[768,128]{1,0:T(8,128)S(1)}, f32[1536,128]{1,0:T(8,128)S(1)}, f32[1536,128]{1,0:T(8,128)S(1)}) custom-call(bf16[768,768]{1,0:T(8,128)(2,1)S(1)} %pad.39.q_ref, bf16[1536,1536]{1,0:T(8,128)(2,1)} %fusion.8.k_ref.v_ref, bf16[1536,1536]{1,0:T(8,128)(2,1)} %fusion.8.k_ref.v_ref, bf16[768,768]{1,0:T(8,128)(2,1)S(1)} %pad.43.do_ref, ...), custom_call_target="tpu_custom_call" | custom-call | tf_op jit(solution)/shard_map/pallas_call | solution.py:180
  318.5 4.3 collective-permute-done.20
  325.3 1.8 collective-permute-start.23
  327.3 11.0 %shard_map.297 = (f32[768,128]{1,0:T(8,128)S(1)}, f32[1536,128]{1,0:T(8,128)S(1)}, f32[1536,128]{1,0:T(8,128)S(1)}) custom-call(bf16[768,768]{1,0:T(8,128)(2,1)S(1)} %pad.39.q_ref, bf16[1536,1536]{1,0:T(8,128)(2,1)} %fusion.8.k_ref.v_ref, bf16[1536,1536]{1,0:T(8,128)(2,1)} %fusion.8.k_ref.v_ref, bf16[768,768]{1,0:T(8,128)(2,1)S(1)} %pad.44.do_ref, ...), custom_call_target="tpu_custom_call" | custom-call | tf_op jit(solution)/shard_map/pallas_call | solution.py:180
  342.0 1.8 collective-permute-start.25
  345.2 10.3 %shard_map.298 = (f32[768,128]{1,0:T(8,128)S(1)}, f32[1536,128]{1,0:T(8,128)S(1)}, f32[1536,128]{1,0:T(8,128)S(1)}) custom-call(bf16[768,768]{1,0:T(8,128)(2,1)S(1)} %pad.39.q_ref, bf16[1536,1536]{1,0:T(8,128)(2,1)} %fusion.8.k_ref.v_ref, bf16[1536,1536]{1,0:T(8,128)(2,1)} %fusion.8.k_ref.v_ref, bf16[768,768]{1,0:T(8,128)(2,1)S(1)} %pad.45.do_ref, ...), custom_call_target="tpu_custom_call" | custom-call | tf_op jit(solution)/shard_map/pallas_call | solution.py:180
  362.6 10.6 %shard_map.299 = (f32[768,128]{1,0:T(8,128)S(1)}, f32[1536,128]{1,0:T(8,128)S(1)}, f32[1536,128]{1,0:T(8,128)S(1)}) custom-call(bf16[768,768]{1,0:T(8,128)(2,1)S(1)} %pad.39.q_ref, bf16[1536,1536]{1,0:T(8,128)(2,1)} %fusion.8.k_ref.v_ref, bf16[1536,1536]{1,0:T(8,128)(2,1)} %fusion.8.k_ref.v_ref, bf16[768,768]{1,0:T(8,128)(2,1)S(1)} %pad.46.do_ref, ...), custom_call_target="tpu_custom_call" | custom-call | tf_op jit(solution)/shard_map/pallas_call | solution.py:180
  374.9 1.9 fusion.42
  385.1 2.9 collective-permute-done.31
  388.1 3.9 collective-permute-done.32
  392.6 5.3 %fusion.32 = (bf16[768]{0:T(1024)(128)(2,1)S(1)}, f32[750]{0:T(1024)}, f32[750]{0:T(1024)}, bf16[768]{0:T(1024)(128)(2,1)S(1)}, f32[750,768]{1,0:T(8,128)}) fusion(bf16[1,750,768]{2,1,0:T(8,128)(2,1)S(1)} %copy-done.9, f32[750]{0:T(1024)S(1)} %copy-done.62, f32[750]{0:T(1024)S(1)} %copy-done.57, f32[768]{0:T(1024)S(1)} %copy-done.59, ...), kind=kOutput, calls=%fused_computation.51 | convolution fusion | flops 2659964928 | bytes 10484592 | tf_op jit(solution)/shard_map/dot_general | solution.py:534
  397.9 4.7 %convolution_convert_fusion = bf16[768,2304]{1,0:T(8,128)(2,1)} fusion(bf16[750,2304]{1,0:T(8,128)(2,1)S(1)} %slice_dynamic-update-slice_fusion.2, bf16[1,750,768]{2,1,0:T(8,128)(2,1)S(1)} %copy-done.9, f32[768]{0:T(1024)S(1)} %copy-done.69, f32[768]{0:T(1024)S(1)} %copy-done.59, f32[750]{0:T(1024)S(1)} %copy-done.62, f32[750]{0:T(1024)S(1)} %copy-done.57), kind=kOutput, calls=%fused_computation.17 | convolution fusion | flops 2659433472 | bytes 8159088 | tf_op jit(solution)/shard_map/dot_general | solution.py:528
  402.7 2.6 reduce.2
  406.7 7.7 %concatenate.325 = bf16[768,2432]{1,0:T(8,128)(2,1)} concatenate(bf16[768,2304]{1,0:T(8,128)(2,1)} %convolution_convert_fusion, bf16[768,1]{1,0:T(8,128)(2,1)S(1)} %stack.415, bf16[768,1]{1,0:T(8,128)(2,1)S(1)} %stack.416, bf16[768,1]{1,0:T(8,128)(2,1)S(1)} %stack.417, bf16[768,1]{1,0:T(8,128)(2,1)S(1)} %stack.418, bf16[768,1]{1,0:T(8,128)(2,1)S(1)} %copy-done.47, ...), dimensions={1} | concatenate | bytes 7471104 | tf_op jit(solution)/shard_map/concatenate | solution.py:561
  414.5 1.8 dynamic-slice_bitcast_fusion
  422.9 1.8 fusion.44
  424.9 1.8 collective-permute-start.38
  427.1 3.0 collective-permute-done.42
  430.9 3.1 collective-permute-done.38
  435.4 2.3 collective-permute-done.34
  441.0 3.8 collective-permute-done.44
  445.8 2.3 collective-permute-start.41
  455.6 2.1 collective-permute-done.37
  (460 shorter events, 97.8 us)
Async XLA Ops:
  7.2 11.5 %copy-start.8 = (bf16[1,750,768]{2,1,0:T(8,128)(2,1)S(1)}, bf16[1,750,768]{2,1,0:T(8,128)(2,1)}, u32[]{:S(2)}) copy-start(bf16[1,750,768]{2,1,0:T(8,128)(2,1)} %param.14) | copy-start | bytes 3456004
  7.2 134.9 %all-gather.2.cloned.1.call-start = ((), (), s32[]{:S(2)}) async-start(), calls=%async_computation | async-start | bytes 10948608 | tf_op jit(solution)/shard_map/all_gather | solution.py:409
  11.5 8.7 %collective-permute-start.8 = (bf16[24,768]{1,0:T(8,128)(2,1)S(1)}, bf16[24,768]{1,0:T(8,128)(2,1)S(1)}, u32[]{:S(2)}, u32[]{:S(2)}) collective-permute-start(bf16[24,768]{1,0:T(8,128)(2,1)S(1)} %get-tuple-element.267), channel_id=1, source_target_pairs={{0,16},{1,17},{2,18},{3,19},{4,20},{5,21},{6,22},{7,23},{8,24},{9,... | collective-permute-start | bytes 110600 | tf_op jit(solution)/shard_map/ppermute | solution.py:339
  15.6 8.3 %collective-permute-start = (bf16[24,896]{1,0:T(8,128)(2,1)S(1)}, bf16[24,896]{1,0:T(8,128)(2,1)S(1)}, u32[]{:S(2)}, u32[]{:S(2)}) collective-permute-start(bf16[24,896]{1,0:T(8,128)(2,1)S(1)} %get-tuple-element.270), channel_id=1, source_target_pairs={{0,16},{1,17},{2,18},{3,19},{4,20},{5,21},{6,22},{7,23},{8,24},{9,... | collective-permute-start | bytes 129032 | tf_op jit(solution)/shard_map/ppermute | solution.py:339
  15.7 6.6 %collective-permute-start.4 = (bf16[24,768]{1,0:T(8,128)(2,1)S(1)}, bf16[24,768]{1,0:T(8,128)(2,1)S(1)}, u32[]{:S(2)}, u32[]{:S(2)}) collective-permute-start(bf16[24,768]{1,0:T(8,128)(2,1)S(1)} %get-tuple-element.273), channel_id=1, source_target_pairs={{0,16},{1,17},{2,18},{3,19},{4,20},{5,21},{6,22},{7,23},{8,24},{9,... | collective-permute-start | bytes 110600 | tf_op jit(solution)/shard_map/ppermute | solution.py:339
  18.7 59.8 %collective-permute-start.13 = (bf16[1,750,768]{2,1,0:T(8,128)(2,1)S(1)}, bf16[1,750,768]{2,1,0:T(8,128)(2,1)}, u32[]{:S(2)}, u32[]{:S(2)}) collective-permute-start(bf16[1,750,768]{2,1,0:T(8,128)(2,1)S(1)} %copy-done.8), channel_id=1, source_target_pairs={{0,1},{1,0},{2,3},{3,2},{4,5},{5,4},{6,7},{7,6},{8,9},{9,8},{10,11... | collective-permute-start | bytes 3456008 | tf_op jit(solution)/shard_map/ppermute | solution.py:423
  20.3 4.4 collective-permute-start.9
  22.4 32.9 %collective-permute-start.5 = (bf16[2,24,768]{2,1,0:T(8,128)(2,1)S(1)}, bf16[2,24,768]{2,1,0:T(8,128)(2,1)S(1)}, u32[]{:S(2)}, u32[]{:S(2)}) collective-permute-start(bf16[2,24,768]{2,1,0:T(8,128)(2,1)S(1)} %maximum_select_fusion.17), channel_id=1, source_target_pairs={{0,1},{1,0},{2,3},{3,2},{4,5},{5,4},{6,7},{7,6},{8,9},{9,8},{10,11... | collective-permute-start | bytes 221192 | tf_op jit(solution)/shard_map/ppermute | solution.py:339
  24.0 33.1 %collective-permute-start.1 = (bf16[2,24,896]{2,1,0:T(8,128)(2,1)S(1)}, bf16[2,24,896]{2,1,0:T(8,128)(2,1)S(1)}, u32[]{:S(2)}, u32[]{:S(2)}) collective-permute-start(bf16[2,24,896]{2,1,0:T(8,128)(2,1)S(1)} %maximum_select_fusion.15), channel_id=1, source_target_pairs={{0,8},{1,9},{2,10},{3,11},{4,12},{5,13},{6,14},{7,15},{8,0},{9,1},... | collective-permute-start | bytes 258056 | tf_op jit(solution)/shard_map/ppermute | solution.py:339
  24.7 34.0 %collective-permute-start.10 = (bf16[2,2,24,768]{3,2,1,0:T(8,128)(2,1)S(1)}, bf16[2,2,24,768]{3,2,1,0:T(8,128)(2,1)S(1)}, u32[]{:S(2)}, u32[]{:S(2)}) collective-permute-start(bf16[2,2,24,768]{3,2,1,0:T(8,128)(2,1)S(1)} %maximum_select_fusion.13), channel_id=1, source_target_pairs={{0,1},{1,0},{2,3},{3,2},{4,5},{5,4},{6,7},{7,6},{8,9},{9,8},{10,11... | collective-permute-start | bytes 442376 | tf_op jit(solution)/shard_map/ppermute | solution.py:339
  55.3 11.7 %collective-permute-start.6 = (bf16[2,2,24,768]{3,2,0,1:T(8,128)(2,1)S(1)}, bf16[2,2,24,768]{3,2,0,1:T(8,128)(2,1)S(1)}, u32[]{:S(2)}, u32[]{:S(2)}) collective-permute-start(bf16[2,2,24,768]{3,2,0,1:T(8,128)(2,1)S(1)} %maximum_select_fusion.12), channel_id=1, source_target_pairs={{0,8},{1,9},{2,10},{3,11},{4,12},{5,13},{6,14},{7,15},{8,0},{9,1},... | collective-permute-start | bytes 442376 | tf_op jit(solution)/shard_map/ppermute | solution.py:339
  57.2 11.4 %collective-permute-start.2 = (bf16[2,2,24,896]{3,2,0,1:T(8,128)(2,1)S(1)}, bf16[2,2,24,896]{3,2,0,1:T(8,128)(2,1)S(1)}, u32[]{:S(2)}, u32[]{:S(2)}) collective-permute-start(bf16[2,2,24,896]{3,2,0,1:T(8,128)(2,1)S(1)} %maximum_select_fusion.10), channel_id=1, source_target_pairs={{0,4},{1,5},{2,6},{3,7},{4,0},{5,1},{6,2},{7,3},{8,12},{9,13},{10,... | collective-permute-start | bytes 516104 | tf_op jit(solution)/shard_map/ppermute | solution.py:339
  58.8 12.6 %collective-permute-start.11 = (bf16[2,2,2,24,768]{4,3,2,1,0:T(8,128)(2,1)S(1)}, bf16[2,2,2,24,768]{4,3,2,1,0:T(8,128)(2,1)S(1)}, u32[]{:S(2)}, u32[]{:S(2)}) collective-permute-start(bf16[2,2,2,24,768]{4,3,2,1,0:T(8,128)(2,1)S(1)} %maximum_select_fusion.8), channel_id=1, source_target_pairs={{0,8},{1,9},{2,10},{3,11},{4,12},{5,13},{6,14},{7,15},{8,0},{9,1},... | collective-permute-start | bytes 884744 | tf_op jit(solution)/shard_map/ppermute | solution.py:339
  67.1 6.8 %collective-permute-start.7 = (bf16[2,2,2,24,768]{4,3,0,2,1:T(8,128)(2,1)S(1)}, bf16[2,2,2,24,768]{4,3,0,2,1:T(8,128)(2,1)S(1)}, u32[]{:S(2)}, u32[]{:S(2)}) collective-permute-start(bf16[2,2,2,24,768]{4,3,0,2,1:T(8,128)(2,1)S(1)} %maximum_select_fusion.7), channel_id=1, source_target_pairs={{0,4},{1,5},{2,6},{3,7},{4,0},{5,1},{6,2},{7,3},{8,12},{9,13},{10,... | collective-permute-start | bytes 884744 | tf_op jit(solution)/shard_map/ppermute | solution.py:339
  68.7 7.3 %collective-permute-start.3 = (bf16[2,2,2,24,896]{4,3,0,1,2:T(8,128)(2,1)S(1)}, bf16[2,2,2,24,896]{4,3,0,1,2:T(8,128)(2,1)S(1)}, u32[]{:S(2)}, u32[]{:S(2)}) collective-permute-start(bf16[2,2,2,24,896]{4,3,0,1,2:T(8,128)(2,1)S(1)} %maximum_select_fusion.5), channel_id=1, source_target_pairs={{0,1},{1,0},{2,3},{3,2},{4,5},{5,4},{6,7},{7,6},{8,9},{9,8},{10,11... | collective-permute-start | bytes 1032200 | tf_op jit(solution)/shard_map/ppermute | solution.py:339
  77.7 4.7 %collective-permute-start.12 = (bf16[2,2,2,2,24,2432]{5,4,3,2,1,0:T(8,128)(2,1)}, bf16[2,2,2,2,24,2432]{5,4,3,2,1,0:T(8,128)(2,1)}, u32[]{:S(2)}, u32[]{:S(2)}) collective-permute-start(bf16[2,2,2,2,24,2432]{5,4,3,2,1,0:T(8,128)(2,1)} %get-tuple-element.251), channel_id=1, source_target_pairs={{0,2},{1,3},{2,0},{3,1},{4,6},{5,7},{6,4},{7,5},{8,10},{9,11},{10,... | collective-permute-start | bytes 5603336 | tf_op jit(solution)/shard_map/ppermute | solution.py:339
  77.9 11.5 %copy-start.56 = (f32[750]{0:T(1024)}, f32[750]{0:T(1024)S(1)}, u32[]{:S(2)}) copy-start(f32[750]{0:T(1024)S(1)} %broadcast_multiply_fusion.6) | copy-start | bytes 9004
  78.4 11.0 %copy-start.61 = (f32[750]{0:T(1024)}, f32[750]{0:T(1024)S(1)}, u32[]{:S(2)}) copy-start(f32[750]{0:T(1024)S(1)} %add_rsqrt_fusion.2) | copy-start | bytes 9004
  103.5 38.7 %copy-start.71 = (f32[768]{0:T(1024)S(1)}, f32[768]{0:T(1024)}, u32[]{:S(2)}) copy-start(f32[768]{0:T(1024)} %get-tuple-element.231) | copy-start | bytes 9220
  167.6 25.2 %copy-start.81 = (bf16[750,3072]{1,0:T(8,128)(2,1)}, bf16[750,3072]{1,0:T(8,128)(2,1)S(1)}, u32[]{:S(2)}) copy-start(bf16[750,3072]{1,0:T(8,128)(2,1)S(1)} %get-tuple-element.287) | copy-start | bytes 13824004
  229.9 32.7 %collective-permute-start.14 = (bf16[2,2,2,2,24,6912]{5,4,0,2,3,1:T(8,128)(2,1)}, bf16[2,2,2,2,24,6912]{5,4,0,2,3,1:T(8,128)(2,1)}, u32[]{:S(2)}, u32[]{:S(2)}) collective-permute-start(bf16[2,2,2,2,24,6912]{5,4,0,2,3,1:T(8,128)(2,1)} %bitcast.333), channel_id=1, source_target_pairs={{0,2},{1,3},{2,0},{3,1},{4,6},{5,7},{6,4},{7,5},{8,10},{9,11},{10,... | collective-permute-start | bytes 15925256 | tf_op jit(solution)/shard_map/ppermute | solution.py:320
  231.7 17.4 %slice-start.1 = ((s8[4718592]{0:T(1024)(128)(4,1)}), s8[4194304]{0:T(1024)(128)(4,1)S(1)}, s32[]{:S(2)}) async-start(s8[4718592]{0:T(1024)(128)(4,1)} %bitcast.336), calls=%async_computation.2 | async-start | bytes 8388608
  235.0 14.1 %slice-start.2 = ((s8[4718592]{0:T(1024)(128)(4,1)}), s8[524288]{0:T(1024)(128)(4,1)S(1)}, s32[]{:S(2)}) async-start(s8[4718592]{0:T(1024)(128)(4,1)} %bitcast.336), calls=%async_computation.3 | async-start | bytes 1048576
  245.9 10.3 %copy-start.16 = (f32[1500,128]{1,0:T(8,128)}, f32[1500,128]{1,0:T(8,128)S(1)}, u32[]{:S(2)}) copy-start(f32[1500,128]{1,0:T(8,128)S(1)} %slice.346) | copy-start | bytes 2304004
  246.7 13.9 %collective-permute-start.27 = (bf16[750,256]{1,0:T(8,128)(2,1)}, bf16[750,256]{1,0:T(8,128)(2,1)}, u32[]{:S(2)}, u32[]{:S(2)}) collective-permute-start(bf16[750,256]{1,0:T(8,128)(2,1)} %fusion.69), channel_id=1, source_target_pairs={{0,1},{1,0},{2,3},{3,2},{4,5},{5,4},{6,7},{7,6},{8,9},{9,8},{10,11... | collective-permute-start | bytes 1152008 | tf_op jit(solution)/shard_map/ppermute | solution.py:512
  249.1 8.8 %copy-start.76 = (bf16[768]{0:T(1024)(128)(2,1)S(1)}, bf16[768]{0:T(1024)(128)(2,1)}, u32[]{:S(2)}) copy-start(bf16[768]{0:T(1024)(128)(2,1)} %get-tuple-element.226) | copy-start | bytes 4612
  249.1 9.6 %copy-start.67 = (bf16[3072]{0:T(1024)(128)(2,1)S(1)}, bf16[3072]{0:T(1024)(128)(2,1)}, u32[]{:S(2)}) copy-start(bf16[3072]{0:T(1024)(128)(2,1)} %get-tuple-element.290) | copy-start | bytes 18436
  277.1 21.5 %collective-permute-start.15 = (bf16[2,2,2,24,2304]{4,3,0,1,2:T(8,128)(2,1)}, bf16[2,2,2,24,2304]{4,3,0,1,2:T(8,128)(2,1)S(1)}, u32[]{:S(2)}, u32[]{:S(2)}) collective-permute-start(bf16[2,2,2,24,2304]{4,3,0,1,2:T(8,128)(2,1)} %fusion.55), channel_id=1, source_target_pairs={{0,1},{1,0},{2,3},{3,2},{4,5},{5,4},{6,7},{7,6},{8,9},{9,8},{10,11... | collective-permute-start | bytes 2654216 | tf_op jit(solution)/shard_map/ppermute | solution.py:320
  279.1 21.3 %collective-permute-start.16 = (bf16[2,2,2,24,2304]{4,3,0,2,1:T(8,128)(2,1)S(1)}, bf16[2,2,2,24,2304]{4,3,0,2,1:T(8,128)(2,1)S(1)}, u32[]{:S(2)}, u32[]{:S(2)}) collective-permute-start(bf16[2,2,2,24,2304]{4,3,0,2,1:T(8,128)(2,1)S(1)} %fusion.56), channel_id=1, source_target_pairs={{0,4},{1,5},{2,6},{3,7},{4,0},{5,1},{6,2},{7,3},{8,12},{9,13},{10,... | collective-permute-start | bytes 2654216 | tf_op jit(solution)/shard_map/ppermute | solution.py:320
  279.3 21.4 %collective-permute-start.17 = (bf16[2,2,2,24,2304]{4,3,0,1,2:T(8,128)(2,1)S(1)}, bf16[2,2,2,24,2304]{4,3,0,1,2:T(8,128)(2,1)S(1)}, u32[]{:S(2)}, u32[]{:S(2)}) collective-permute-start(bf16[2,2,2,24,2304]{4,3,0,1,2:T(8,128)(2,1)S(1)} %fusion.57), channel_id=1, source_target_pairs={{0,8},{1,9},{2,10},{3,11},{4,12},{5,13},{6,14},{7,15},{8,0},{9,1},... | collective-permute-start | bytes 2654216 | tf_op jit(solution)/shard_map/ppermute | solution.py:320
  301.1 17.3 %collective-permute-start.18 = (bf16[2,2,24,2304]{3,2,0,1:T(8,128)(2,1)S(1)}, bf16[2,2,24,2304]{3,2,0,1:T(8,128)(2,1)S(1)}, u32[]{:S(2)}, u32[]{:S(2)}) collective-permute-start(bf16[2,2,24,2304]{3,2,0,1:T(8,128)(2,1)S(1)} %fusion.70), channel_id=1, source_target_pairs={{0,4},{1,5},{2,6},{3,7},{4,0},{5,1},{6,2},{7,3},{8,12},{9,13},{10,... | collective-permute-start | bytes 1327112 | tf_op jit(solution)/shard_map/ppermute | solution.py:320
  302.7 15.7 %collective-permute-start.19 = (bf16[2,2,24,2304]{3,2,0,1:T(8,128)(2,1)S(1)}, bf16[2,2,24,2304]{3,2,0,1:T(8,128)(2,1)S(1)}, u32[]{:S(2)}, u32[]{:S(2)}) collective-permute-start(bf16[2,2,24,2304]{3,2,0,1:T(8,128)(2,1)S(1)} %fusion.71), channel_id=1, source_target_pairs={{0,8},{1,9},{2,10},{3,11},{4,12},{5,13},{6,14},{7,15},{8,0},{9,1},... | collective-permute-start | bytes 1327112 | tf_op jit(solution)/shard_map/ppermute | solution.py:320
  304.0 13.5 %collective-permute-start.28 = (bf16[750,256]{1,0:T(8,128)(2,1)}, bf16[750,256]{1,0:T(8,128)(2,1)S(1)}, u32[]{:S(2)}, u32[]{:S(2)}) collective-permute-start(bf16[750,256]{1,0:T(8,128)(2,1)} %slice.588), channel_id=1, source_target_pairs={{0,1},{1,0},{2,3},{3,2},{4,5},{5,4},{6,7},{7,6},{8,9},{9,8},{10,11... | collective-permute-start | bytes 1152008 | tf_op jit(solution)/shard_map/ppermute | solution.py:512
  304.7 18.1 %collective-permute-start.20 = (bf16[2,2,24,2304]{3,2,0,1:T(8,128)(2,1)S(1)}, bf16[2,2,24,2304]{3,2,0,1:T(8,128)(2,1)S(1)}, u32[]{:S(2)}, u32[]{:S(2)}) collective-permute-start(bf16[2,2,24,2304]{3,2,0,1:T(8,128)(2,1)S(1)} %fusion.72), channel_id=1, source_target_pairs={{0,1},{1,0},{2,3},{3,2},{4,5},{5,4},{6,7},{7,6},{8,9},{9,8},{10,11... | collective-permute-start | bytes 1327112 | tf_op jit(solution)/shard_map/ppermute | solution.py:320
  323.0 17.6 %collective-permute-start.21 = (bf16[2,24,2304]{2,1,0:T(8,128)(2,1)S(1)}, bf16[2,24,2304]{2,1,0:T(8,128)(2,1)S(1)}, u32[]{:S(2)}, u32[]{:S(2)}) collective-permute-start(bf16[2,24,2304]{2,1,0:T(8,128)(2,1)S(1)} %fusion.87), channel_id=1, source_target_pairs={{0,8},{1,9},{2,10},{3,11},{4,12},{5,13},{6,14},{7,15},{8,0},{9,1},... | collective-permute-start | bytes 663560 | tf_op jit(solution)/shard_map/ppermute | solution.py:320
  324.5 16.1 %collective-permute-start.22 = (bf16[2,24,2304]{2,1,0:T(8,128)(2,1)S(1)}, bf16[2,24,2304]{2,1,0:T(8,128)(2,1)S(1)}, u32[]{:S(2)}, u32[]{:S(2)}) collective-permute-start(bf16[2,24,2304]{2,1,0:T(8,128)(2,1)S(1)} %fusion.88), channel_id=1, source_target_pairs={{0,1},{1,0},{2,3},{3,2},{4,5},{5,4},{6,7},{7,6},{8,9},{9,8},{10,11... | collective-permute-start | bytes 663560 | tf_op jit(solution)/shard_map/ppermute | solution.py:320
  325.3 15.3 %collective-permute-start.23 = (bf16[2,24,2304]{2,1,0:T(8,128)(2,1)S(1)}, bf16[2,24,2304]{2,1,0:T(8,128)(2,1)S(1)}, u32[]{:S(2)}, u32[]{:S(2)}) collective-permute-start(bf16[2,24,2304]{2,1,0:T(8,128)(2,1)S(1)} %fusion.89), channel_id=1, source_target_pairs={{0,4},{1,5},{2,6},{3,7},{4,0},{5,1},{6,2},{7,3},{8,12},{9,13},{10,... | collective-permute-start | bytes 663560 | tf_op jit(solution)/shard_map/ppermute | solution.py:320
  327.2 11.2 %copy-start.23 = (f32[1500,256]{1,0:T(8,128)}, f32[1500,256]{1,0:T(8,128)S(1)}, u32[]{:S(2)}) copy-start(f32[1500,256]{1,0:T(8,128)S(1)} %constant_dynamic-update-slice_fusion.6) | copy-start | bytes 4608004
  339.3 43.4 %collective-permute-start.29 = (bf16[750,256]{1,0:T(8,128)(2,1)}, bf16[750,256]{1,0:T(8,128)(2,1)}, u32[]{:S(2)}, u32[]{:S(2)}) collective-permute-start(bf16[750,256]{1,0:T(8,128)(2,1)} %slice.587), channel_id=1, source_target_pairs={{0,1},{1,0},{2,3},{3,2},{4,5},{5,4},{6,7},{7,6},{8,9},{9,8},{10,11... | collective-permute-start | bytes 1152008 | tf_op jit(solution)/shard_map/ppermute | solution.py:512
  340.7 19.1 %collective-permute-start.24 = (bf16[24,2304]{1,0:T(8,128)(2,1)S(1)}, bf16[24,2304]{1,0:T(8,128)(2,1)S(1)}, u32[]{:S(2)}, u32[]{:S(2)}) collective-permute-start(bf16[24,2304]{1,0:T(8,128)(2,1)S(1)} %fusion.93), channel_id=1, source_target_pairs={{0,16},{1,17},{2,18},{3,19},{4,20},{5,21},{6,22},{7,23},{8,24},{9,... | collective-permute-start | bytes 331784 | tf_op jit(solution)/shard_map/ppermute | solution.py:320
  342.0 17.8 %collective-permute-start.25 = (bf16[24,2304]{1,0:T(8,128)(2,1)S(1)}, bf16[24,2304]{1,0:T(8,128)(2,1)S(1)}, u32[]{:S(2)}, u32[]{:S(2)}) collective-permute-start(bf16[24,2304]{1,0:T(8,128)(2,1)S(1)} %fusion.94), channel_id=1, source_target_pairs={{0,16},{1,17},{2,18},{3,19},{4,20},{5,21},{6,22},{7,23},{8,24},{9,... | collective-permute-start | bytes 331784 | tf_op jit(solution)/shard_map/ppermute | solution.py:320
  343.8 16.1 %collective-permute-start.26 = (bf16[24,2304]{1,0:T(8,128)(2,1)S(1)}, bf16[24,2304]{1,0:T(8,128)(2,1)S(1)}, u32[]{:S(2)}, u32[]{:S(2)}) collective-permute-start(bf16[24,2304]{1,0:T(8,128)(2,1)S(1)} %fusion.95), channel_id=1, source_target_pairs={{0,16},{1,17},{2,18},{3,19},{4,20},{5,21},{6,22},{7,23},{8,24},{9,... | collective-permute-start | bytes 331784 | tf_op jit(solution)/shard_map/ppermute | solution.py:320
  358.2 25.7 %collective-permute-start.30 = (bf16[750,256]{1,0:T(8,128)(2,1)}, bf16[750,256]{1,0:T(8,128)(2,1)}, u32[]{:S(2)}, u32[]{:S(2)}) collective-permute-start(bf16[750,256]{1,0:T(8,128)(2,1)} %slice.586), channel_id=1, source_target_pairs={{0,1},{1,0},{2,3},{3,2},{4,5},{5,4},{6,7},{7,6},{8,9},{9,8},{10,11... | collective-permute-start | bytes 1152008 | tf_op jit(solution)/shard_map/ppermute | solution.py:512
  362.6 10.6 %copy-start.31 = (f32[750,128]{1,0:T(8,128)S(1)}, f32[750,128]{1,0:T(8,128)}, u32[]{:S(2)}) copy-start(f32[750,128]{1,0:T(8,128)} %slice.341) | copy-start | bytes 1152004
  377.0 10.9 %collective-permute-start.31 = (bf16[750,256]{1,0:T(8,128)(2,1)S(1)}, bf16[750,256]{1,0:T(8,128)(2,1)S(1)}, u32[]{:S(2)}, u32[]{:S(2)}) collective-permute-start(bf16[750,256]{1,0:T(8,128)(2,1)S(1)} %slice.585), channel_id=1, source_target_pairs={{0,1},{1,0},{2,3},{3,2},{4,5},{5,4},{6,7},{7,6},{8,9},{9,8},{10,11... | collective-permute-start | bytes 1152008 | tf_op jit(solution)/shard_map/ppermute | solution.py:512
  378.6 13.5 %collective-permute-start.32 = (bf16[750,256]{1,0:T(8,128)(2,1)S(1)}, bf16[750,256]{1,0:T(8,128)(2,1)S(1)}, u32[]{:S(2)}, u32[]{:S(2)}) collective-permute-start(bf16[750,256]{1,0:T(8,128)(2,1)S(1)} %fusion.64), channel_id=1, source_target_pairs={{0,1},{1,0},{2,3},{3,2},{4,5},{5,4},{6,7},{7,6},{8,9},{9,8},{10,11... | collective-permute-start | bytes 1152008 | tf_op jit(solution)/shard_map/ppermute | solution.py:512
  416.3 3.9 collective-permute-start.33
  420.9 9.2 %collective-permute-start.42 = (bf16[2,2,2,24,768]{4,3,2,1,0:T(8,128)(2,1)S(1)}, bf16[2,2,2,24,768]{4,3,2,1,0:T(8,128)(2,1)S(1)}, u32[]{:S(2)}, u32[]{:S(2)}) collective-permute-start(bf16[2,2,2,24,768]{4,3,2,1,0:T(8,128)(2,1)S(1)} %fusion.83), channel_id=1, source_target_pairs={{0,8},{1,9},{2,10},{3,11},{4,12},{5,13},{6,14},{7,15},{8,0},{9,1},... | collective-permute-start | bytes 884744 | tf_op jit(solution)/shard_map/ppermute | solution.py:320
  424.9 9.2 %collective-permute-start.38 = (bf16[2,2,2,24,768]{4,3,2,1,0:T(8,128)(2,1)S(1)}, bf16[2,2,2,24,768]{4,3,2,1,0:T(8,128)(2,1)S(1)}, u32[]{:S(2)}, u32[]{:S(2)}) collective-permute-start(bf16[2,2,2,24,768]{4,3,2,1,0:T(8,128)(2,1)S(1)} %fusion.82), channel_id=1, source_target_pairs={{0,4},{1,5},{2,6},{3,7},{4,0},{5,1},{6,2},{7,3},{8,12},{9,13},{10,... | collective-permute-start | bytes 884744 | tf_op jit(solution)/shard_map/ppermute | solution.py:320
  426.7 11.0 %collective-permute-start.34 = (bf16[2,2,2,24,896]{4,3,2,1,0:T(8,128)(2,1)S(1)}, bf16[2,2,2,24,896]{4,3,2,1,0:T(8,128)(2,1)S(1)}, u32[]{:S(2)}, u32[]{:S(2)}) collective-permute-start(bf16[2,2,2,24,896]{4,3,2,1,0:T(8,128)(2,1)S(1)} %fusion.73), channel_id=1, source_target_pairs={{0,1},{1,0},{2,3},{3,2},{4,5},{5,4},{6,7},{7,6},{8,9},{9,8},{10,11... | collective-permute-start | bytes 1032200 | tf_op jit(solution)/shard_map/ppermute | solution.py:320
  430.2 9.6 %collective-permute-start.43 = (bf16[2,2,24,768]{3,2,1,0:T(8,128)(2,1)S(1)}, bf16[2,2,24,768]{3,2,1,0:T(8,128)(2,1)S(1)}, u32[]{:S(2)}, u32[]{:S(2)}) collective-permute-start(bf16[2,2,24,768]{3,2,1,0:T(8,128)(2,1)S(1)} %fusion.92), channel_id=1, source_target_pairs={{0,1},{1,0},{2,3},{3,2},{4,5},{5,4},{6,7},{7,6},{8,9},{9,8},{10,11... | collective-permute-start | bytes 442376 | tf_op jit(solution)/shard_map/ppermute | solution.py:320
  434.2 6.1 %collective-permute-start.39 = (bf16[2,2,24,768]{3,2,1,0:T(8,128)(2,1)S(1)}, bf16[2,2,24,768]{3,2,1,0:T(8,128)(2,1)S(1)}, u32[]{:S(2)}, u32[]{:S(2)}) collective-permute-start(bf16[2,2,24,768]{3,2,1,0:T(8,128)(2,1)S(1)} %fusion.91), channel_id=1, source_target_pairs={{0,8},{1,9},{2,10},{3,11},{4,12},{5,13},{6,14},{7,15},{8,0},{9,1},... | collective-permute-start | bytes 442376 | tf_op jit(solution)/shard_map/ppermute | solution.py:320
  437.8 12.5 %copy-start.75 = (f32[2,96]{1,0:T(2,128)S(1)}, f32[2,96]{1,0:T(2,128)}, u32[]{:S(2)}) copy-start(f32[2,96]{1,0:T(2,128)} %param.26) | copy-start | bytes 2308
  437.8 12.5 %copy-start.80 = (f32[96]{0:T(128)S(1)}, f32[96]{0:T(128)}, u32[]{:S(2)}) copy-start(f32[96]{0:T(128)} %param.20) | copy-start | bytes 1156
  437.8 10.2 %collective-permute-start.35 = (bf16[2,2,24,896]{3,2,1,0:T(8,128)(2,1)S(1)}, bf16[2,2,24,896]{3,2,1,0:T(8,128)(2,1)S(1)}, u32[]{:S(2)}, u32[]{:S(2)}) collective-permute-start(bf16[2,2,24,896]{3,2,1,0:T(8,128)(2,1)S(1)} %fusion.90), channel_id=1, source_target_pairs={{0,4},{1,5},{2,6},{3,7},{4,0},{5,1},{6,2},{7,3},{8,12},{9,13},{10,... | collective-permute-start | bytes 516104 | tf_op jit(solution)/shard_map/ppermute | solution.py:320
  439.8 17.9 %copy-start.42 = (f32[2,24,2304]{2,1,0:T(8,128)S(1)}, f32[2,24,2304]{2,1,0:T(8,128)}, u32[]{:S(2)}) copy-start(f32[2,24,2304]{2,1,0:T(8,128)} %param.22) | copy-start | bytes 1327108
  439.9 5.0 %collective-permute-start.44 = (bf16[2,24,768]{2,1,0:T(8,128)(2,1)S(1)}, bf16[2,24,768]{2,1,0:T(8,128)(2,1)S(1)}, u32[]{:S(2)}, u32[]{:S(2)}) collective-permute-start(bf16[2,24,768]{2,1,0:T(8,128)(2,1)S(1)} %fusion.100), channel_id=1, source_target_pairs={{0,4},{1,5},{2,6},{3,7},{4,0},{5,1},{6,2},{7,3},{8,12},{9,13},{10,... | collective-permute-start | bytes 221192 | tf_op jit(solution)/shard_map/ppermute | solution.py:320
  440.3 17.5 %copy-start.45 = (f32[24,2304]{1,0:T(8,128)S(1)}, f32[24,2304]{1,0:T(8,128)}, u32[]{:S(2)}) copy-start(f32[24,2304]{1,0:T(8,128)} %param.16) | copy-start | bytes 663556
  440.3 5.4 %collective-permute-start.40 = (bf16[2,24,768]{2,1,0:T(8,128)(2,1)S(1)}, bf16[2,24,768]{2,1,0:T(8,128)(2,1)S(1)}, u32[]{:S(2)}, u32[]{:S(2)}) collective-permute-start(bf16[2,24,768]{2,1,0:T(8,128)(2,1)S(1)} %fusion.99), channel_id=1, source_target_pairs={{0,1},{1,0},{2,3},{3,2},{4,5},{5,4},{6,7},{7,6},{8,9},{9,8},{10,11... | collective-permute-start | bytes 221192 | tf_op jit(solution)/shard_map/ppermute | solution.py:320
  444.9 5.0 %collective-permute-start.45 = (bf16[24,768]{1,0:T(8,128)(2,1)S(1)}, bf16[24,768]{1,0:T(8,128)(2,1)S(1)}, u32[]{:S(2)}, u32[]{:S(2)}) collective-permute-start(bf16[24,768]{1,0:T(8,128)(2,1)S(1)} %fusion.106), channel_id=1, source_target_pairs={{0,16},{1,17},{2,18},{3,19},{4,20},{5,21},{6,22},{7,23},{8,24},{9,... | collective-permute-start | bytes 110600 | tf_op jit(solution)/shard_map/ppermute | solution.py:320
  445.8 5.5 %collective-permute-start.41 = (bf16[24,768]{1,0:T(8,128)(2,1)S(1)}, bf16[24,768]{1,0:T(8,128)(2,1)S(1)}, u32[]{:S(2)}, u32[]{:S(2)}) collective-permute-start(bf16[24,768]{1,0:T(8,128)(2,1)S(1)} %fusion.105), channel_id=1, source_target_pairs={{0,16},{1,17},{2,18},{3,19},{4,20},{5,21},{6,22},{7,23},{8,24},{9,... | collective-permute-start | bytes 110600 | tf_op jit(solution)/shard_map/ppermute | solution.py:320
  448.1 4.6 collective-permute-start.36
  450.2 9.3 %copy-start.78 = (f32[96]{0:T(128)}, f32[96]{0:T(128)S(1)}, u32[]{:S(2)}) copy-start(f32[96]{0:T(128)S(1)} %reshape.1161) | copy-start | bytes 1156
  452.7 5.0 %collective-permute-start.37 = (bf16[24,896]{1,0:T(8,128)(2,1)S(1)}, bf16[24,896]{1,0:T(8,128)(2,1)S(1)}, u32[]{:S(2)}, u32[]{:S(2)}) collective-permute-start(bf16[24,896]{1,0:T(8,128)(2,1)S(1)} %fusion.104), channel_id=1, source_target_pairs={{0,16},{1,17},{2,18},{3,19},{4,20},{5,21},{6,22},{7,23},{8,24},{9,... | collective-permute-start | bytes 129032 | tf_op jit(solution)/shard_map/ppermute | solution.py:320
  (68 other events, 259.6 us)
Sparse Core Ops, SparseCore 0:
  11.6 98.3 all-gather.1

commit v20 on v19

--- a/solution.py
+++ b/solution.py
@@ -501,7 +501,7 @@
     hooks.update({index: piece_hook(index) for index in hooked})
     pieces = [run_piece(0, grad_mixed)]
     owned_late, tied = tree_reduce_scatter(
-        late_terms, (2304, 2304, 2304), rotated_orders, (bit_count, core_bit), hooks
+        late_terms, (1152,) * 6, rotated_orders * 2, (bit_count, core_bit), hooks
     )
     pieces += [tied[index][0] for index in hooked]
     last_mixed = tied[hooked[-1]][1] if hooked else grad_mixed

time: 472 us -> 516 us (1.093)
  starting transfers between devices: 51.7 us -> 71 us
  local copies, waits for them, and re-layouts: 90.4 us -> 106 us
  other arithmetic: 58.1 us -> 63.3 us
    ppermute x26 -> x38, starting transfers between devices: 25.9 us -> 40.9 us  [tree_reduce_scatter(): got = lax.ppermute(send, ('clip', 'frame'), pairs)]
    unnamed x194 -> x188, local copies, waits for them, and re-layouts: 20.5 us -> 28.7 us
    add x26 -> x38, other arithmetic: 7.09 us -> 11.8 us  [tree_reduce_scatter(): keep + got.astype(jnp.float32)]
    ppermute x26 -> x38, waiting for transfers between devices: 30 us -> 33.8 us  [tree_reduce_scatter(): got = lax.ppermute(send, ('clip', 'frame'), pairs)]
  transfers between devices with their start and end apart: 47 -> 59, of which waited for: 22 -> 23; matrix products, arithmetic and copies ran while one was open for 17% -> 17% of each run, Pallas kernels for 22% -> 18%
where the time goes in v20:
time: 516 us; the launch traced here: 510 us
  local copies, waits for them, and re-layouts  106 us (21%)
  Pallas kernels  101 us (20%)
  waiting for transfers between devices  80.1 us (16%)
  matrix products  72.6 us (14%)
  starting transfers between devices  71 us (14%)
  other arithmetic  63.3 us (12%)
  between operations  16.6 us (3%)
    pallas_call x6, Pallas kernels, attention_pallas(): pl.pallas_call(attention_backward_kernel, grid=(span,), in_specs=[qi_spec...  63.4 us
    ppermute x13, waiting for transfers between devices, double(): got = lax.ppermute(data, ('clip', 'frame'), pairs)  42 us
    ppermute x38, starting transfers between devices, tree_reduce_scatter(): got = lax.ppermute(send, ('clip', 'frame'), pairs)  40.9 us
    pallas_call x1, Pallas kernels, attention_pallas(): pl.pallas_call(attention_forward_kernel, grid=(pair_count,), in_specs=[q_...  37.3 us
    ppermute x38, waiting for transfers between devices, tree_reduce_scatter(): got = lax.ppermute(send, ('clip', 'frame'), pairs)  33.8 us
    unnamed x188, local copies, waits for them, and re-layouts  28.7 us
    ppermute x13, starting transfers between devices, double(): got = lax.ppermute(data, ('clip', 'frame'), pairs)  19.5 us
    add x38, other arithmetic, tree_reduce_scatter(): keep + got.astype(jnp.float32)  11.8 us
  transfers between devices with their start and end apart: 59, of which 23 were waited for; matrix products, arithmetic and copies ran while one was open for 17% of the time, Pallas kernels for 18%

profile of v20, /device:TPU:0, one launch (start us, length us, event | category | flops | bytes accessed | tf_op | source)
XLA Modules:
  0.0 510.5 jit_solution(16812284346961580328)
XLA Ops:
  12.8 4.1 collective-permute-start.8
  17.0 3.0 collective-permute-start
  25.5 29.5 %collective-permute-done.5 = bf16[2,24,768]{2,1,0:T(8,128)(2,1)S(1)} collective-permute-done((bf16[2,24,768]{2,1,0:T(8,128)(2,1)S(1)}, bf16[2,24,768]{2,1,0:T(8,128)(2,1)S(1)}, u32[]{:S(2)}, u32[]{:S(2)}) %collective-permute-start.5) | collective-permute-done | bytes 73760 | tf_op jit(solution)/shard_map/ppermute | solution.py:339
  60.1 1.8 collective-permute-done.10
  62.4 3.4 collective-permute-done.6
  69.4 3.2 collective-permute-done.7
  72.8 4.0 collective-permute-done.3
  83.1 2.9 maximum_select_fusion
  86.0 1.8 copy-done.17
  89.9 5.5 %add_convert_fusion = bf16[750,2304]{1,0:T(8,128)(2,1)S(1)} fusion(f32[2304]{0:T(1024)S(1)} %pad_maximum_fusion.20, bf16[768,2432]{1,0:T(8,128)(2,1)} %bitcast.390, bf16[1,750,768]{2,1,0:T(8,128)(2,1)S(1)} %copy-done.2, f32[768]{0:T(1024)S(1)} %get-tuple-element.258, f32[768]{0:T(1024)S(1)} %get-tuple-element.259, f32[750]{0:T(1024)S(1)} %add_rsqrt_fusion.2, ...), kind=kOutput, calls=%fused_computation.14 | convolution fusion | flops 2661120000 | bytes 8168304 | tf_op jit(solution)/shard_map/dot_general | solution.py:431
  98.8 3.5 add_convert_fusion.1
  102.3 2.8 fusion.8.k_ref.v_ref
  105.1 37.3 %shard_map.293 = (bf16[768,768]{1,0:T(8,128)(2,1)S(1)}, f32[768,768]{1,0:T(8,128)S(1)}) custom-call(bf16[768,768]{1,0:T(8,128)(2,1)S(1)} %pad.39.q_ref, bf16[1536,1536]{1,0:T(8,128)(2,1)} %fusion.8.k_ref.v_ref, bf16[1536,1536]{1,0:T(8,128)(2,1)} %fusion.8.k_ref.v_ref, f32[1,1536]{1,0:T(1,128)S(1)} %compare_select_fusion.kbias_ref), custom_call_target="tpu_custom_call" | custom-call | tf_op jit(solution)/shard_map/pallas_call | solution.py:161
  143.8 2.5 fusion.137
  148.0 4.8 slice.426
  152.8 8.5 %reshape.1166 = bf16[3072,768]{1,0:T(8,128)(2,1)} reshape(bf16[768,3072]{1,0:T(8,128)(2,1)} %slice.426) | data formatting | bytes 9437184 | tf_op jit(solution)/shard_map/reshape | solution.py:416
  161.2 9.4 %multiply_convert_fusion = (bf16[750,3072]{1,0:T(8,128)(2,1)S(1)}, f32[750,3072]{1,0:T(8,128)}) fusion(f32[3072]{0:T(1024)S(1)} %add.511, bf16[768,6912]{1,0:T(8,128)(2,1)} %all-gather.2.cloned.1.call-done, f32[750,768]{1,0:T(8,128)} %copy-done.6, f32[768]{0:T(1024)S(1)} %get-tuple-element.253, f32[768]{0:T(1024)S(1)} %get-tuple-element.254, ...), kind=kOutput, calls=%fused_computation.12 | convolution fusion | flops 3555648000 | bytes 20877168 | tf_op jit(solution)/shard_map/dot_general | solution.py:451
  170.7 2.2 copy-done.76
  172.9 5.7 %convolution_convert_fusion.2 = bf16[3072,768]{1,0:T(8,128)(2,1)} fusion(bf16[750,3072]{1,0:T(8,128)(2,1)S(1)} %get-tuple-element.313, bf16[1,750,768]{2,1,0:T(8,128)(2,1)S(1)} %copy-done.16), kind=kOutput, calls=%fused_computation.19 | convolution fusion | flops 3541303296 | bytes 10478592 | tf_op jit(solution)/shard_map/dot_general | solution.py:461
  178.6 8.5 %concatenate.313 = bf16[2,2,2,2,2,24,3072]{6,5,4,3,2,1,0:T(8,128)(2,1)} reshape(bf16[3072,768]{1,0:T(8,128)(2,1)} %convolution_convert_fusion.2) | data formatting | bytes 9437184 | tf_op jit(solution)/shard_map/concatenate | solution.py:481
  187.1 10.0 %fusion.138 = (bf16[3072]{0:T(1024)(128)(2,1)}, bf16[750,3072]{1,0:T(8,128)(2,1)S(1)}) fusion(f32[750,3072]{1,0:T(8,128)} %get-tuple-element.314, f32[3072]{0:T(1024)S(1)} %add.511, bf16[3072,768]{1,0:T(8,128)(2,1)} %reshape.1166, bf16[1,750,768]{2,1,0:T(8,128)(2,1)S(1)} %copy-done.16), kind=kOutput, calls=%fused_computation.375 | convolution fusion | flops 3566588928 | bytes 19713024 | tf_op jit(solution)/shard_map/dot_general | solution.py:465
  197.1 5.1 %convolution_convert_fusion.1 = bf16[768,3072]{1,0:T(8,128)(2,1)S(1)} fusion(bf16[750,3072]{1,0:T(8,128)(2,1)S(1)} %get-tuple-element.317, f32[750,768]{1,0:T(8,128)S(1)} %copy-done.7, f32[768]{0:T(1024)S(1)} %get-tuple-element.253, f32[768]{0:T(1024)S(1)} %get-tuple-element.254, f32[750]{0:T(1024)S(1)} %add_rsqrt_fusion, f32[750]{0:T(1024)S(1)} %broadcast_multiply_fusion.4), kind=kOutput, calls=%fused_computation.18 | convolution fusion | flops 3544183296 | bytes 11642736 | tf_op jit(solution)/shard_map/dot_general | solution.py:467
  202.2 7.3 %multiply_reduce_fusion = (bf16[768]{0:T(1024)(128)(2,1)}, f32[750]{0:T(1024)S(1)}, f32[750]{0:T(1024)S(1)}, bf16[768]{0:T(1024)(128)(2,1)}, f32[750,768]{1,0:T(8,128)S(1)}) fusion(f32[750,768]{1,0:T(8,128)S(1)} %copy-done.7, f32[750]{0:T(1024)S(1)} %add_rsqrt_fusion, f32[750]{0:T(1024)S(1)} %broadcast_multiply_fusion.4, f32[768]{0:T(1024)S(1)} %get-tuple-element.254, ...), kind=kOutput, calls=%fused_computation.60 | convolution fusion | flops 3544124928 | bytes 13952736 | tf_op jit(solution)/shard_map/dot_general | solution.py:471
  212.6 8.0 %pad_maximum_fusion = bf16[2,2,2,2,2,24,6912]{6,5,4,3,2,1,0:T(8,128)(2,1)} fusion(bf16[2,2,2,2,2,24,768]{6,5,4,3,2,1,0:T(8,128)(2,1)S(1)} %bitcast.394, bf16[2,2,2,2,2,24,3072]{6,5,4,3,2,1,0:T(8,128)(2,1)S(1)} %bitcast.388, bf16[2,2,2,2,2,24,3072]{6,5,4,3,2,1,0:T(8,128)(2,1)S(1)} %bitcast.383), kind=kLoop, calls=%fused_computation.1 | loop fusion | flops 31850496 | bytes 21233664 | tf_op jit(solution)/shard_map/concatenate | solution.py:481
  220.6 8.6 %constant_dynamic-slice_fusion.1 = (bf16[2,2,2,1,2,24,6912]{6,5,4,3,2,1,0:T(8,128)(2,1)}, bf16[2,2,2,1,2,24,6912]{6,5,4,3,2,1,0:T(8,128)(2,1)}) fusion(bf16[2,2,2,2,2,24,6912]{6,5,4,3,2,1,0:T(8,128)(2,1)} %pad_maximum_fusion, s32[]{:T(128)S(6)} %select_n.437, s32[]{:T(128)S(6)} %select_n.438), kind=kLoop, calls=%fused_computation.327 | loop fusion | bytes 21233672 | tf_op jit(solution)/shard_map/jit(dynamic_index_in_dim)/dynamic_slice | solution.py:313
  229.2 5.2 %copy.185 = bf16[2,2,2,1,2,24,6912]{6,5,0,2,4,1,3:T(8,128)(2,1)} copy(bf16[2,2,2,1,2,24,6912]{6,5,4,3,2,1,0:T(8,128)(2,1)} %get-tuple-element.273) | data formatting | bytes 10616832
  236.2 3.2 convolution_convert_fusion.4
  239.5 10.6 %shard_map.294 = (f32[768,128]{1,0:T(8,128)S(1)}, f32[1536,128]{1,0:T(8,128)S(1)}, f32[1536,128]{1,0:T(8,128)S(1)}) custom-call(bf16[768,768]{1,0:T(8,128)(2,1)S(1)} %pad.39.q_ref, bf16[1536,1536]{1,0:T(8,128)(2,1)} %fusion.8.k_ref.v_ref, bf16[1536,1536]{1,0:T(8,128)(2,1)} %fusion.8.k_ref.v_ref, bf16[768,768]{1,0:T(8,128)(2,1)S(1)} %pad.41.do_ref, ...), custom_call_target="tpu_custom_call" | custom-call | tf_op jit(solution)/shard_map/pallas_call | solution.py:180
  251.0 2.4 collective-permute-start.39
  253.5 7.1 %fusion.41 = bf16[1,750,768]{2,1,0:T(8,128)(2,1)} fusion(f32[750,768]{1,0:T(8,128)S(1)} %copy-done.8, bf16[750,3072]{1,0:T(8,128)(2,1)} %copy-done.76, bf16[3072,768]{1,0:T(8,128)(2,1)S(1)} %bitcast.387, f32[768]{0:T(1024)S(1)} %copy-done.68), kind=kOutput, calls=%fused_computation.78 | convolution fusion | flops 3540672000 | bytes 12785664 | tf_op jit(solution)/shard_map/dot_general | solution.py:455
  266.4 1.9 fusion.60
  268.4 5.3 %convert_add_fusion = f32[2,2,2,2,24,6912]{5,4,0,2,3,1:T(8,128)S(1)} fusion(bf16[2,2,2,2,24,6912]{5,4,0,2,3,1:T(8,128)(2,1)} %collective-permute-done.14, bf16[2,2,2,1,2,24,6912]{6,5,4,3,2,1,0:T(8,128)(2,1)} %get-tuple-element.272), kind=kLoop, calls=%fused_computation.2 | loop fusion | flops 7962624 | bytes 21233664 | tf_op jit(solution)/shard_map/add | solution.py:321
  273.7 3.1 fusion.133
  276.8 4.8 copy.150
  281.5 4.7 copy.149
  286.4 10.8 %shard_map.295 = (f32[768,128]{1,0:T(8,128)S(1)}, f32[1536,128]{1,0:T(8,128)S(1)}, f32[1536,128]{1,0:T(8,128)S(1)}) custom-call(bf16[768,768]{1,0:T(8,128)(2,1)S(1)} %pad.39.q_ref, bf16[1536,1536]{1,0:T(8,128)(2,1)} %fusion.8.k_ref.v_ref, bf16[1536,1536]{1,0:T(8,128)(2,1)} %fusion.8.k_ref.v_ref, bf16[768,768]{1,0:T(8,128)(2,1)S(1)} %pad.42.do_ref, ...), custom_call_target="tpu_custom_call" | custom-call | tf_op jit(solution)/shard_map/pallas_call | solution.py:180
  300.6 1.8 collective-permute-start.20
  305.6 2.0 collective-permute-start.16
  307.6 4.3 collective-permute-done.17
  313.1 7.2 %collective-permute-done.20 = bf16[2,2,2,24,1152]{4,3,0,1,2:T(8,128)(2,1)S(1)} collective-permute-done((bf16[2,2,2,24,1152]{4,3,0,1,2:T(8,128)(2,1)S(1)}, bf16[2,2,2,24,1152]{4,3,0,1,2:T(8,128)(2,1)S(1)}, u32[]{:S(2)}, u32[]{:S(2)}) %collective-permute-start.20) | collective-permute-done | bytes 442400 | tf_op jit(solution)/shard_map/ppermute | solution.py:320
  328.9 10.3 %shard_map.296 = (f32[768,128]{1,0:T(8,128)S(1)}, f32[1536,128]{1,0:T(8,128)S(1)}, f32[1536,128]{1,0:T(8,128)S(1)}) custom-call(bf16[768,768]{1,0:T(8,128)(2,1)S(1)} %pad.39.q_ref, bf16[1536,1536]{1,0:T(8,128)(2,1)} %fusion.8.k_ref.v_ref, bf16[1536,1536]{1,0:T(8,128)(2,1)} %fusion.8.k_ref.v_ref, bf16[768,768]{1,0:T(8,128)(2,1)S(1)} %pad.43.do_ref, ...), custom_call_target="tpu_custom_call" | custom-call | tf_op jit(solution)/shard_map/pallas_call | solution.py:180
  341.9 1.8 collective-permute-start.21
  354.6 10.5 %shard_map.297 = (f32[768,128]{1,0:T(8,128)S(1)}, f32[1536,128]{1,0:T(8,128)S(1)}, f32[1536,128]{1,0:T(8,128)S(1)}) custom-call(bf16[768,768]{1,0:T(8,128)(2,1)S(1)} %pad.39.q_ref, bf16[1536,1536]{1,0:T(8,128)(2,1)} %fusion.8.k_ref.v_ref, bf16[1536,1536]{1,0:T(8,128)(2,1)} %fusion.8.k_ref.v_ref, bf16[768,768]{1,0:T(8,128)(2,1)S(1)} %pad.44.do_ref, ...), custom_call_target="tpu_custom_call" | custom-call | tf_op jit(solution)/shard_map/pallas_call | solution.py:180
  370.1 1.8 collective-permute-done.28
  373.9 2.9 collective-permute-start.37
  377.1 10.8 %shard_map.298 = (f32[768,128]{1,0:T(8,128)S(1)}, f32[1536,128]{1,0:T(8,128)S(1)}, f32[1536,128]{1,0:T(8,128)S(1)}) custom-call(bf16[768,768]{1,0:T(8,128)(2,1)S(1)} %pad.39.q_ref, bf16[1536,1536]{1,0:T(8,128)(2,1)} %fusion.8.k_ref.v_ref, bf16[1536,1536]{1,0:T(8,128)(2,1)} %fusion.8.k_ref.v_ref, bf16[768,768]{1,0:T(8,128)(2,1)S(1)} %pad.45.do_ref, ...), custom_call_target="tpu_custom_call" | custom-call | tf_op jit(solution)/shard_map/pallas_call | solution.py:180
  391.3 2.9 collective-permute-start.35
  394.2 1.8 fusion.65
  396.1 2.9 collective-permute-start.33
  408.7 10.5 %shard_map.299 = (f32[768,128]{1,0:T(8,128)S(1)}, f32[1536,128]{1,0:T(8,128)S(1)}, f32[1536,128]{1,0:T(8,128)S(1)}) custom-call(bf16[768,768]{1,0:T(8,128)(2,1)S(1)} %pad.39.q_ref, bf16[1536,1536]{1,0:T(8,128)(2,1)} %fusion.8.k_ref.v_ref, bf16[1536,1536]{1,0:T(8,128)(2,1)} %fusion.8.k_ref.v_ref, bf16[768,768]{1,0:T(8,128)(2,1)S(1)} %pad.46.do_ref, ...), custom_call_target="tpu_custom_call" | custom-call | tf_op jit(solution)/shard_map/pallas_call | solution.py:180
  427.1 4.2 collective-permute-done.43
  432.0 1.8 copy-done.11
  435.1 5.3 %fusion.32 = (bf16[768]{0:T(1024)(128)(2,1)S(1)}, f32[750]{0:T(1024)}, f32[750]{0:T(1024)}, bf16[768]{0:T(1024)(128)(2,1)}, f32[750,768]{1,0:T(8,128)}) fusion(bf16[1,750,768]{2,1,0:T(8,128)(2,1)S(1)} %copy-done.3, f32[750]{0:T(1024)S(1)} %copy-done.60, f32[750]{0:T(1024)S(1)} %copy-done.55, f32[768]{0:T(1024)S(1)} %copy-done.57, ...), kind=kOutput, calls=%fused_computation.51 | convolution fusion | flops 2659964928 | bytes 10484592 | tf_op jit(solution)/shard_map/dot_general | solution.py:534
  440.4 2.5 reduce.2
  443.0 6.9 %convolution_convert_fusion = bf16[768,2304]{1,0:T(8,128)(2,1)} fusion(bf16[750,2304]{1,0:T(8,128)(2,1)} %copy-done.11, bf16[1,750,768]{2,1,0:T(8,128)(2,1)S(1)} %copy-done.3, f32[768]{0:T(1024)S(1)} %copy-done.67, f32[768]{0:T(1024)S(1)} %copy-done.57, f32[750]{0:T(1024)S(1)} %copy-done.60, f32[750]{0:T(1024)S(1)} %copy-done.55), kind=kOutput, calls=%fused_computation.17 | convolution fusion | flops 2659433472 | bytes 8159088 | tf_op jit(solution)/shard_map/dot_general | solution.py:528
  451.3 7.9 %concatenate.325 = bf16[768,2432]{1,0:T(8,128)(2,1)} concatenate(bf16[768,2304]{1,0:T(8,128)(2,1)} %convolution_convert_fusion, bf16[768,1]{1,0:T(8,128)(2,1)S(1)} %stack.415, bf16[768,1]{1,0:T(8,128)(2,1)S(1)} %stack.416, bf16[768,1]{1,0:T(8,128)(2,1)S(1)} %stack.417, bf16[768,1]{1,0:T(8,128)(2,1)S(1)} %stack.418, bf16[768,1]{1,0:T(8,128)(2,1)S(1)} %copy-done.48, ...), dimensions={1} | concatenate | bytes 7471104 | tf_op jit(solution)/shard_map/concatenate | solution.py:561
  459.3 1.8 dynamic-slice_bitcast_fusion
  467.8 1.8 fusion.44
  471.3 3.6 collective-permute-done.54
  476.5 2.4 collective-permute-done.50
  479.1 2.1 collective-permute-done.46
  481.3 1.8 collective-permute-start.47
  483.3 1.8 collective-permute-start.56
  499.4 2.2 collective-permute-done.49
  (505 shorter events, 133.9 us)
Async XLA Ops:
  7.2 136.6 %all-gather.2.cloned.1.call-start = ((), (), s32[]{:S(2)}) async-start(), calls=%async_computation | async-start | bytes 10948608 | tf_op jit(solution)/shard_map/all_gather | solution.py:409
  12.8 8.7 %collective-permute-start.8 = (bf16[24,768]{1,0:T(8,128)(2,1)S(1)}, bf16[24,768]{1,0:T(8,128)(2,1)S(1)}, u32[]{:S(2)}, u32[]{:S(2)}) collective-permute-start(bf16[24,768]{1,0:T(8,128)(2,1)S(1)} %get-tuple-element.292), channel_id=1, source_target_pairs={{0,16},{1,17},{2,18},{3,19},{4,20},{5,21},{6,22},{7,23},{8,24},{9,... | collective-permute-start | bytes 110600 | tf_op jit(solution)/shard_map/ppermute | solution.py:339
  16.9 6.2 %collective-permute-start.4 = (bf16[24,768]{1,0:T(8,128)(2,1)S(1)}, bf16[24,768]{1,0:T(8,128)(2,1)S(1)}, u32[]{:S(2)}, u32[]{:S(2)}) collective-permute-start(bf16[24,768]{1,0:T(8,128)(2,1)S(1)} %get-tuple-element.299), channel_id=1, source_target_pairs={{0,16},{1,17},{2,18},{3,19},{4,20},{5,21},{6,22},{7,23},{8,24},{9,... | collective-permute-start | bytes 110600 | tf_op jit(solution)/shard_map/ppermute | solution.py:339
  17.0 6.9 %collective-permute-start = (bf16[24,896]{1,0:T(8,128)(2,1)S(1)}, bf16[24,896]{1,0:T(8,128)(2,1)S(1)}, u32[]{:S(2)}, u32[]{:S(2)}) collective-permute-start(bf16[24,896]{1,0:T(8,128)(2,1)S(1)} %get-tuple-element.296), channel_id=1, source_target_pairs={{0,16},{1,17},{2,18},{3,19},{4,20},{5,21},{6,22},{7,23},{8,24},{9,... | collective-permute-start | bytes 129032 | tf_op jit(solution)/shard_map/ppermute | solution.py:339
  20.0 59.3 %collective-permute-start.13 = (bf16[1,750,768]{2,1,0:T(8,128)(2,1)S(1)}, bf16[1,750,768]{2,1,0:T(8,128)(2,1)}, u32[]{:S(2)}, u32[]{:S(2)}) collective-permute-start(bf16[1,750,768]{2,1,0:T(8,128)(2,1)S(1)} %copy-done.2), channel_id=1, source_target_pairs={{0,1},{1,0},{2,3},{3,2},{4,5},{5,4},{6,7},{7,6},{8,9},{9,8},{10,11... | collective-permute-start | bytes 3456008 | tf_op jit(solution)/shard_map/ppermute | solution.py:423
  21.6 35.1 %collective-permute-start.9 = (bf16[2,24,768]{2,1,0:T(8,128)(2,1)S(1)}, bf16[2,24,768]{2,1,0:T(8,128)(2,1)S(1)}, u32[]{:S(2)}, u32[]{:S(2)}) collective-permute-start(bf16[2,24,768]{2,1,0:T(8,128)(2,1)S(1)} %maximum_select_fusion.18), channel_id=1, source_target_pairs={{0,4},{1,5},{2,6},{3,7},{4,0},{5,1},{6,2},{7,3},{8,12},{9,13},{10,... | collective-permute-start | bytes 221192 | tf_op jit(solution)/shard_map/ppermute | solution.py:339
  23.2 31.8 %collective-permute-start.5 = (bf16[2,24,768]{2,1,0:T(8,128)(2,1)S(1)}, bf16[2,24,768]{2,1,0:T(8,128)(2,1)S(1)}, u32[]{:S(2)}, u32[]{:S(2)}) collective-permute-start(bf16[2,24,768]{2,1,0:T(8,128)(2,1)S(1)} %maximum_select_fusion.17), channel_id=1, source_target_pairs={{0,1},{1,0},{2,3},{3,2},{4,5},{5,4},{6,7},{7,6},{8,9},{9,8},{10,11... | collective-permute-start | bytes 221192 | tf_op jit(solution)/shard_map/ppermute | solution.py:339
  23.9 34.4 %collective-permute-start.1 = (bf16[2,24,896]{2,1,0:T(8,128)(2,1)S(1)}, bf16[2,24,896]{2,1,0:T(8,128)(2,1)S(1)}, u32[]{:S(2)}, u32[]{:S(2)}) collective-permute-start(bf16[2,24,896]{2,1,0:T(8,128)(2,1)S(1)} %maximum_select_fusion.15), channel_id=1, source_target_pairs={{0,8},{1,9},{2,10},{3,11},{4,12},{5,13},{6,14},{7,15},{8,0},{9,1},... | collective-permute-start | bytes 258056 | tf_op jit(solution)/shard_map/ppermute | solution.py:339
  55.0 10.8 %collective-permute-start.6 = (bf16[2,2,24,768]{3,2,0,1:T(8,128)(2,1)S(1)}, bf16[2,2,24,768]{3,2,0,1:T(8,128)(2,1)S(1)}, u32[]{:S(2)}, u32[]{:S(2)}) collective-permute-start(bf16[2,2,24,768]{3,2,0,1:T(8,128)(2,1)S(1)} %maximum_select_fusion.12), channel_id=1, source_target_pairs={{0,8},{1,9},{2,10},{3,11},{4,12},{5,13},{6,14},{7,15},{8,0},{9,1},... | collective-permute-start | bytes 442376 | tf_op jit(solution)/shard_map/ppermute | solution.py:339
  56.7 5.2 %collective-permute-start.10 = (bf16[2,2,24,768]{3,2,1,0:T(8,128)(2,1)S(1)}, bf16[2,2,24,768]{3,2,1,0:T(8,128)(2,1)S(1)}, u32[]{:S(2)}, u32[]{:S(2)}) collective-permute-start(bf16[2,2,24,768]{3,2,1,0:T(8,128)(2,1)S(1)} %maximum_select_fusion.13), channel_id=1, source_target_pairs={{0,1},{1,0},{2,3},{3,2},{4,5},{5,4},{6,7},{7,6},{8,9},{9,8},{10,11... | collective-permute-start | bytes 442376 | tf_op jit(solution)/shard_map/ppermute | solution.py:339
  58.5 9.1 %collective-permute-start.2 = (bf16[2,2,24,896]{3,2,0,1:T(8,128)(2,1)S(1)}, bf16[2,2,24,896]{3,2,0,1:T(8,128)(2,1)S(1)}, u32[]{:S(2)}, u32[]{:S(2)}) collective-permute-start(bf16[2,2,24,896]{3,2,0,1:T(8,128)(2,1)S(1)} %maximum_select_fusion.10), channel_id=1, source_target_pairs={{0,4},{1,5},{2,6},{3,7},{4,0},{5,1},{6,2},{7,3},{8,12},{9,13},{10,... | collective-permute-start | bytes 516104 | tf_op jit(solution)/shard_map/ppermute | solution.py:339
  61.9 10.8 %collective-permute-start.11 = (bf16[2,2,2,24,768]{4,3,2,1,0:T(8,128)(2,1)S(1)}, bf16[2,2,2,24,768]{4,3,2,1,0:T(8,128)(2,1)S(1)}, u32[]{:S(2)}, u32[]{:S(2)}) collective-permute-start(bf16[2,2,2,24,768]{4,3,2,1,0:T(8,128)(2,1)S(1)} %maximum_select_fusion.8), channel_id=1, source_target_pairs={{0,8},{1,9},{2,10},{3,11},{4,12},{5,13},{6,14},{7,15},{8,0},{9,1},... | collective-permute-start | bytes 884744 | tf_op jit(solution)/shard_map/ppermute | solution.py:339
  65.9 6.8 %collective-permute-start.7 = (bf16[2,2,2,24,768]{4,3,0,2,1:T(8,128)(2,1)S(1)}, bf16[2,2,2,24,768]{4,3,0,2,1:T(8,128)(2,1)S(1)}, u32[]{:S(2)}, u32[]{:S(2)}) collective-permute-start(bf16[2,2,2,24,768]{4,3,0,2,1:T(8,128)(2,1)S(1)} %maximum_select_fusion.7), channel_id=1, source_target_pairs={{0,4},{1,5},{2,6},{3,7},{4,0},{5,1},{6,2},{7,3},{8,12},{9,13},{10,... | collective-permute-start | bytes 884744 | tf_op jit(solution)/shard_map/ppermute | solution.py:339
  67.7 9.1 %collective-permute-start.3 = (bf16[2,2,2,24,896]{4,3,0,1,2:T(8,128)(2,1)S(1)}, bf16[2,2,2,24,896]{4,3,0,1,2:T(8,128)(2,1)S(1)}, u32[]{:S(2)}, u32[]{:S(2)}) collective-permute-start(bf16[2,2,2,24,896]{4,3,0,1,2:T(8,128)(2,1)S(1)} %maximum_select_fusion.5), channel_id=1, source_target_pairs={{0,1},{1,0},{2,3},{3,2},{4,5},{5,4},{6,7},{7,6},{8,9},{9,8},{10,11... | collective-permute-start | bytes 1032200 | tf_op jit(solution)/shard_map/ppermute | solution.py:339
  78.5 4.7 collective-permute-start.12
  234.4 34.0 %collective-permute-start.14 = (bf16[2,2,2,2,24,6912]{5,4,0,2,3,1:T(8,128)(2,1)}, bf16[2,2,2,2,24,6912]{5,4,0,2,3,1:T(8,128)(2,1)}, u32[]{:S(2)}, u32[]{:S(2)}) collective-permute-start(bf16[2,2,2,2,24,6912]{5,4,0,2,3,1:T(8,128)(2,1)} %bitcast.381), channel_id=1, source_target_pairs={{0,2},{1,3},{2,0},{3,1},{4,6},{5,7},{6,4},{7,5},{8,10},{9,11},{10,... | collective-permute-start | bytes 15925256 | tf_op jit(solution)/shard_map/ppermute | solution.py:320
  236.2 17.3 %slice-start.3 = ((s8[4718592]{0:T(1024)(128)(4,1)}), s8[4194304]{0:T(1024)(128)(4,1)S(1)}, s32[]{:S(2)}) async-start(s8[4718592]{0:T(1024)(128)(4,1)} %bitcast.386), calls=%async_computation.4 | async-start | bytes 8388608
  239.5 14.0 %slice-start.4 = ((s8[4718592]{0:T(1024)(128)(4,1)}), s8[524288]{0:T(1024)(128)(4,1)S(1)}, s32[]{:S(2)}) async-start(s8[4718592]{0:T(1024)(128)(4,1)} %bitcast.386), calls=%async_computation.5 | async-start | bytes 1048576
  251.0 15.4 %collective-permute-start.39 = (bf16[750,256]{1,0:T(8,128)(2,1)}, bf16[750,256]{1,0:T(8,128)(2,1)}, u32[]{:S(2)}, u32[]{:S(2)}) collective-permute-start(bf16[750,256]{1,0:T(8,128)(2,1)} %fusion.66), channel_id=1, source_target_pairs={{0,1},{1,0},{2,3},{3,2},{4,5},{5,4},{6,7},{7,6},{8,9},{9,8},{10,11... | collective-permute-start | bytes 1152008 | tf_op jit(solution)/shard_map/ppermute | solution.py:512
  298.8 13.1 %collective-permute-start.17 = (bf16[2,2,2,24,1152]{4,3,0,1,2:T(8,128)(2,1)S(1)}, bf16[2,2,2,24,1152]{4,3,0,1,2:T(8,128)(2,1)S(1)}, u32[]{:S(2)}, u32[]{:S(2)}) collective-permute-start(bf16[2,2,2,24,1152]{4,3,0,1,2:T(8,128)(2,1)S(1)} %fusion.69), channel_id=1, source_target_pairs={{0,8},{1,9},{2,10},{3,11},{4,12},{5,13},{6,14},{7,15},{8,0},{9,1},... | collective-permute-start | bytes 1327112 | tf_op jit(solution)/shard_map/ppermute | solution.py:320
  299.3 22.8 %collective-permute-start.18 = (bf16[2,2,2,24,1152]{4,3,0,2,1:T(8,128)(2,1)S(1)}, bf16[2,2,2,24,1152]{4,3,0,2,1:T(8,128)(2,1)S(1)}, u32[]{:S(2)}, u32[]{:S(2)}) collective-permute-start(bf16[2,2,2,24,1152]{4,3,0,2,1:T(8,128)(2,1)S(1)} %fusion.70), channel_id=1, source_target_pairs={{0,1},{1,0},{2,3},{3,2},{4,5},{5,4},{6,7},{7,6},{8,9},{9,8},{10,11... | collective-permute-start | bytes 1327112 | tf_op jit(solution)/shard_map/ppermute | solution.py:320
  300.5 19.9 %collective-permute-start.19 = (bf16[2,2,2,24,1152]{4,3,0,2,1:T(8,128)(2,1)S(1)}, bf16[2,2,2,24,1152]{4,3,0,2,1:T(8,128)(2,1)S(1)}, u32[]{:S(2)}, u32[]{:S(2)}) collective-permute-start(bf16[2,2,2,24,1152]{4,3,0,2,1:T(8,128)(2,1)S(1)} %fusion.71), channel_id=1, source_target_pairs={{0,4},{1,5},{2,6},{3,7},{4,0},{5,1},{6,2},{7,3},{8,12},{9,13},{10,... | collective-permute-start | bytes 1327112 | tf_op jit(solution)/shard_map/ppermute | solution.py:320
  300.6 19.7 %collective-permute-start.20 = (bf16[2,2,2,24,1152]{4,3,0,1,2:T(8,128)(2,1)S(1)}, bf16[2,2,2,24,1152]{4,3,0,1,2:T(8,128)(2,1)S(1)}, u32[]{:S(2)}, u32[]{:S(2)}) collective-permute-start(bf16[2,2,2,24,1152]{4,3,0,1,2:T(8,128)(2,1)S(1)} %fusion.72), channel_id=1, source_target_pairs={{0,8},{1,9},{2,10},{3,11},{4,12},{5,13},{6,14},{7,15},{8,0},{9,1},... | collective-permute-start | bytes 1327112 | tf_op jit(solution)/shard_map/ppermute | solution.py:320
  305.6 16.4 %collective-permute-start.16 = (bf16[2,2,2,24,1152]{4,3,0,2,1:T(8,128)(2,1)S(1)}, bf16[2,2,2,24,1152]{4,3,0,2,1:T(8,128)(2,1)S(1)}, u32[]{:S(2)}, u32[]{:S(2)}) collective-permute-start(bf16[2,2,2,24,1152]{4,3,0,2,1:T(8,128)(2,1)S(1)} %fusion.68), channel_id=1, source_target_pairs={{0,4},{1,5},{2,6},{3,7},{4,0},{5,1},{6,2},{7,3},{8,12},{9,13},{10,... | collective-permute-start | bytes 1327112 | tf_op jit(solution)/shard_map/ppermute | solution.py:320
  311.9 10.2 %collective-permute-start.15 = (bf16[2,2,2,24,1152]{4,3,0,1,2:T(8,128)(2,1)S(1)}, bf16[2,2,2,24,1152]{4,3,0,1,2:T(8,128)(2,1)S(1)}, u32[]{:S(2)}, u32[]{:S(2)}) collective-permute-start(bf16[2,2,2,24,1152]{4,3,0,1,2:T(8,128)(2,1)S(1)} %fusion.67), channel_id=1, source_target_pairs={{0,1},{1,0},{2,3},{3,2},{4,5},{5,4},{6,7},{7,6},{8,9},{9,8},{10,11... | collective-permute-start | bytes 1327112 | tf_op jit(solution)/shard_map/ppermute | solution.py:320
  324.5 17.4 %collective-permute-start.26 = (bf16[2,2,24,1152]{3,2,0,1:T(8,128)(2,1)}, bf16[2,2,24,1152]{3,2,0,1:T(8,128)(2,1)}, u32[]{:S(2)}, u32[]{:S(2)}) collective-permute-start(bf16[2,2,24,1152]{3,2,0,1:T(8,128)(2,1)} %fusion.92), channel_id=1, source_target_pairs={{0,1},{1,0},{2,3},{3,2},{4,5},{5,4},{6,7},{7,6},{8,9},{9,8},{10,11... | collective-permute-start | bytes 663560 | tf_op jit(solution)/shard_map/ppermute | solution.py:320
  325.9 18.8 %collective-permute-start.25 = (bf16[2,2,24,1152]{3,2,0,1:T(8,128)(2,1)}, bf16[2,2,24,1152]{3,2,0,1:T(8,128)(2,1)}, u32[]{:S(2)}, u32[]{:S(2)}) collective-permute-start(bf16[2,2,24,1152]{3,2,0,1:T(8,128)(2,1)} %fusion.91), channel_id=1, source_target_pairs={{0,8},{1,9},{2,10},{3,11},{4,12},{5,13},{6,14},{7,15},{8,0},{9,1},... | collective-permute-start | bytes 663560 | tf_op jit(solution)/shard_map/ppermute | solution.py:320
  326.6 20.6 %collective-permute-start.24 = (bf16[2,2,24,1152]{3,2,0,1:T(8,128)(2,1)}, bf16[2,2,24,1152]{3,2,0,1:T(8,128)(2,1)}, u32[]{:S(2)}, u32[]{:S(2)}) collective-permute-start(bf16[2,2,24,1152]{3,2,0,1:T(8,128)(2,1)} %fusion.90), channel_id=1, source_target_pairs={{0,4},{1,5},{2,6},{3,7},{4,0},{5,1},{6,2},{7,3},{8,12},{9,13},{10,... | collective-permute-start | bytes 663560 | tf_op jit(solution)/shard_map/ppermute | solution.py:320
  326.8 21.3 %collective-permute-start.23 = (bf16[2,2,24,1152]{3,2,0,1:T(8,128)(2,1)S(1)}, bf16[2,2,24,1152]{3,2,0,1:T(8,128)(2,1)}, u32[]{:S(2)}, u32[]{:S(2)}) collective-permute-start(bf16[2,2,24,1152]{3,2,0,1:T(8,128)(2,1)S(1)} %fusion.89), channel_id=1, source_target_pairs={{0,1},{1,0},{2,3},{3,2},{4,5},{5,4},{6,7},{7,6},{8,9},{9,8},{10,11... | collective-permute-start | bytes 663560 | tf_op jit(solution)/shard_map/ppermute | solution.py:320
  328.2 21.0 %collective-permute-start.22 = (bf16[2,2,24,1152]{3,2,0,1:T(8,128)(2,1)S(1)}, bf16[2,2,24,1152]{3,2,0,1:T(8,128)(2,1)}, u32[]{:S(2)}, u32[]{:S(2)}) collective-permute-start(bf16[2,2,24,1152]{3,2,0,1:T(8,128)(2,1)S(1)} %fusion.88), channel_id=1, source_target_pairs={{0,8},{1,9},{2,10},{3,11},{4,12},{5,13},{6,14},{7,15},{8,0},{9,1},... | collective-permute-start | bytes 663560 | tf_op jit(solution)/shard_map/ppermute | solution.py:320
  341.9 8.2 %collective-permute-start.21 = (bf16[2,2,24,1152]{3,2,0,1:T(8,128)(2,1)S(1)}, bf16[2,2,24,1152]{3,2,0,1:T(8,128)(2,1)S(1)}, u32[]{:S(2)}, u32[]{:S(2)}) collective-permute-start(bf16[2,2,24,1152]{3,2,0,1:T(8,128)(2,1)S(1)} %fusion.87), channel_id=1, source_target_pairs={{0,4},{1,5},{2,6},{3,7},{4,0},{5,1},{6,2},{7,3},{8,12},{9,13},{10,... | collective-permute-start | bytes 663560 | tf_op jit(solution)/shard_map/ppermute | solution.py:320
  344.7 46.6 %collective-permute-start.40 = (bf16[750,256]{1,0:T(8,128)(2,1)}, bf16[750,256]{1,0:T(8,128)(2,1)}, u32[]{:S(2)}, u32[]{:S(2)}) collective-permute-start(bf16[750,256]{1,0:T(8,128)(2,1)} %slice.601), channel_id=1, source_target_pairs={{0,1},{1,0},{2,3},{3,2},{4,5},{5,4},{6,7},{7,6},{8,9},{9,8},{10,11... | collective-permute-start | bytes 1152008 | tf_op jit(solution)/shard_map/ppermute | solution.py:512
  350.4 16.7 %collective-permute-start.32 = (bf16[2,24,1152]{2,1,0:T(8,128)(2,1)S(1)}, bf16[2,24,1152]{2,1,0:T(8,128)(2,1)S(1)}, u32[]{:S(2)}, u32[]{:S(2)}) collective-permute-start(bf16[2,24,1152]{2,1,0:T(8,128)(2,1)S(1)} %fusion.101), channel_id=1, source_target_pairs={{0,4},{1,5},{2,6},{3,7},{4,0},{5,1},{6,2},{7,3},{8,12},{9,13},{10,... | collective-permute-start | bytes 331784 | tf_op jit(solution)/shard_map/ppermute | solution.py:320
  350.5 17.3 %collective-permute-start.31 = (bf16[2,24,1152]{2,1,0:T(8,128)(2,1)S(1)}, bf16[2,24,1152]{2,1,0:T(8,128)(2,1)S(1)}, u32[]{:S(2)}, u32[]{:S(2)}) collective-permute-start(bf16[2,24,1152]{2,1,0:T(8,128)(2,1)S(1)} %fusion.100), channel_id=1, source_target_pairs={{0,1},{1,0},{2,3},{3,2},{4,5},{5,4},{6,7},{7,6},{8,9},{9,8},{10,11... | collective-permute-start | bytes 331784 | tf_op jit(solution)/shard_map/ppermute | solution.py:320
  351.4 17.9 %collective-permute-start.30 = (bf16[2,24,1152]{2,1,0:T(8,128)(2,1)S(1)}, bf16[2,24,1152]{2,1,0:T(8,128)(2,1)S(1)}, u32[]{:S(2)}, u32[]{:S(2)}) collective-permute-start(bf16[2,24,1152]{2,1,0:T(8,128)(2,1)S(1)} %fusion.99), channel_id=1, source_target_pairs={{0,8},{1,9},{2,10},{3,11},{4,12},{5,13},{6,14},{7,15},{8,0},{9,1},... | collective-permute-start | bytes 331784 | tf_op jit(solution)/shard_map/ppermute | solution.py:320
  352.8 17.2 %collective-permute-start.29 = (bf16[2,24,1152]{2,1,0:T(8,128)(2,1)S(1)}, bf16[2,24,1152]{2,1,0:T(8,128)(2,1)S(1)}, u32[]{:S(2)}, u32[]{:S(2)}) collective-permute-start(bf16[2,24,1152]{2,1,0:T(8,128)(2,1)S(1)} %fusion.98), channel_id=1, source_target_pairs={{0,4},{1,5},{2,6},{3,7},{4,0},{5,1},{6,2},{7,3},{8,12},{9,13},{10,... | collective-permute-start | bytes 331784 | tf_op jit(solution)/shard_map/ppermute | solution.py:320
  367.2 4.7 collective-permute-start.28
  367.8 5.8 %collective-permute-start.27 = (bf16[2,24,1152]{2,1,0:T(8,128)(2,1)S(1)}, bf16[2,24,1152]{2,1,0:T(8,128)(2,1)S(1)}, u32[]{:S(2)}, u32[]{:S(2)}) collective-permute-start(bf16[2,24,1152]{2,1,0:T(8,128)(2,1)S(1)} %fusion.96), channel_id=1, source_target_pairs={{0,8},{1,9},{2,10},{3,11},{4,12},{5,13},{6,14},{7,15},{8,0},{9,1},... | collective-permute-start | bytes 331784 | tf_op jit(solution)/shard_map/ppermute | solution.py:320
  369.3 55.5 %collective-permute-start.41 = (bf16[750,256]{1,0:T(8,128)(2,1)}, bf16[750,256]{1,0:T(8,128)(2,1)}, u32[]{:S(2)}, u32[]{:S(2)}) collective-permute-start(bf16[750,256]{1,0:T(8,128)(2,1)} %slice.600), channel_id=1, source_target_pairs={{0,1},{1,0},{2,3},{3,2},{4,5},{5,4},{6,7},{7,6},{8,9},{9,8},{10,11... | collective-permute-start | bytes 1152008 | tf_op jit(solution)/shard_map/ppermute | solution.py:512
  373.8 22.2 %collective-permute-start.38 = (bf16[24,1152]{1,0:T(8,128)(2,1)S(1)}, bf16[24,1152]{1,0:T(8,128)(2,1)S(1)}, u32[]{:S(2)}, u32[]{:S(2)}) collective-permute-start(bf16[24,1152]{1,0:T(8,128)(2,1)S(1)} %fusion.114), channel_id=1, source_target_pairs={{0,16},{1,17},{2,18},{3,19},{4,20},{5,21},{6,22},{7,23},{8,24},{9,... | collective-permute-start | bytes 165896 | tf_op jit(solution)/shard_map/ppermute | solution.py:320
  373.9 22.2 %collective-permute-start.37 = (bf16[24,1152]{1,0:T(8,128)(2,1)S(1)}, bf16[24,1152]{1,0:T(8,128)(2,1)S(1)}, u32[]{:S(2)}, u32[]{:S(2)}) collective-permute-start(bf16[24,1152]{1,0:T(8,128)(2,1)S(1)} %fusion.113), channel_id=1, source_target_pairs={{0,16},{1,17},{2,18},{3,19},{4,20},{5,21},{6,22},{7,23},{8,24},{9,... | collective-permute-start | bytes 165896 | tf_op jit(solution)/shard_map/ppermute | solution.py:320
  376.8 22.3 %collective-permute-start.36 = (bf16[24,1152]{1,0:T(8,128)(2,1)S(1)}, bf16[24,1152]{1,0:T(8,128)(2,1)S(1)}, u32[]{:S(2)}, u32[]{:S(2)}) collective-permute-start(bf16[24,1152]{1,0:T(8,128)(2,1)S(1)} %fusion.112), channel_id=1, source_target_pairs={{0,16},{1,17},{2,18},{3,19},{4,20},{5,21},{6,22},{7,23},{8,24},{9,... | collective-permute-start | bytes 165896 | tf_op jit(solution)/shard_map/ppermute | solution.py:320
  389.6 13.3 %copy-start.34 = (f32[2,24,3072]{2,1,0:T(8,128)S(1)}, f32[2,24,3072]{2,1,0:T(8,128)}, u32[]{:S(2)}) copy-start(f32[2,24,3072]{2,1,0:T(8,128)} %param.24) | copy-start | bytes 1769476
  391.3 9.4 %collective-permute-start.35 = (bf16[24,1152]{1,0:T(8,128)(2,1)S(1)}, bf16[24,1152]{1,0:T(8,128)(2,1)S(1)}, u32[]{:S(2)}, u32[]{:S(2)}) collective-permute-start(bf16[24,1152]{1,0:T(8,128)(2,1)S(1)} %fusion.111), channel_id=1, source_target_pairs={{0,16},{1,17},{2,18},{3,19},{4,20},{5,21},{6,22},{7,23},{8,24},{9,... | collective-permute-start | bytes 165896 | tf_op jit(solution)/shard_map/ppermute | solution.py:320
  396.0 6.2 %collective-permute-start.34 = (bf16[24,1152]{1,0:T(8,128)(2,1)S(1)}, bf16[24,1152]{1,0:T(8,128)(2,1)S(1)}, u32[]{:S(2)}, u32[]{:S(2)}) collective-permute-start(bf16[24,1152]{1,0:T(8,128)(2,1)S(1)} %fusion.110), channel_id=1, source_target_pairs={{0,16},{1,17},{2,18},{3,19},{4,20},{5,21},{6,22},{7,23},{8,24},{9,... | collective-permute-start | bytes 165896 | tf_op jit(solution)/shard_map/ppermute | solution.py:320
  396.1 6.7 %collective-permute-start.33 = (bf16[24,1152]{1,0:T(8,128)(2,1)S(1)}, bf16[24,1152]{1,0:T(8,128)(2,1)S(1)}, u32[]{:S(2)}, u32[]{:S(2)}) collective-permute-start(bf16[24,1152]{1,0:T(8,128)(2,1)S(1)} %fusion.109), channel_id=1, source_target_pairs={{0,16},{1,17},{2,18},{3,19},{4,20},{5,21},{6,22},{7,23},{8,24},{9,... | collective-permute-start | bytes 165896 | tf_op jit(solution)/shard_map/ppermute | solution.py:320
  399.1 26.9 %collective-permute-start.42 = (bf16[750,256]{1,0:T(8,128)(2,1)}, bf16[750,256]{1,0:T(8,128)(2,1)}, u32[]{:S(2)}, u32[]{:S(2)}) collective-permute-start(bf16[750,256]{1,0:T(8,128)(2,1)} %slice.599), channel_id=1, source_target_pairs={{0,1},{1,0},{2,3},{3,2},{4,5},{5,4},{6,7},{7,6},{8,9},{9,8},{10,11... | collective-permute-start | bytes 1152008 | tf_op jit(solution)/shard_map/ppermute | solution.py:512
  419.4 12.1 %collective-permute-start.44 = (bf16[750,256]{1,0:T(8,128)(2,1)S(1)}, bf16[750,256]{1,0:T(8,128)(2,1)S(1)}, u32[]{:S(2)}, u32[]{:S(2)}) collective-permute-start(bf16[750,256]{1,0:T(8,128)(2,1)S(1)} %fusion.61), channel_id=1, source_target_pairs={{0,1},{1,0},{2,3},{3,2},{4,5},{5,4},{6,7},{7,6},{8,9},{9,8},{10,11... | collective-permute-start | bytes 1152008 | tf_op jit(solution)/shard_map/ppermute | solution.py:512
  422.3 9.0 %collective-permute-start.43 = (bf16[750,256]{1,0:T(8,128)(2,1)S(1)}, bf16[750,256]{1,0:T(8,128)(2,1)S(1)}, u32[]{:S(2)}, u32[]{:S(2)}) collective-permute-start(bf16[750,256]{1,0:T(8,128)(2,1)S(1)} %slice.598), channel_id=1, source_target_pairs={{0,1},{1,0},{2,3},{3,2},{4,5},{5,4},{6,7},{7,6},{8,9},{9,8},{10,11... | collective-permute-start | bytes 1152008 | tf_op jit(solution)/shard_map/ppermute | solution.py:512
  461.1 3.9 collective-permute-start.45
  465.8 9.2 %collective-permute-start.54 = (bf16[2,2,2,24,768]{4,3,2,1,0:T(8,128)(2,1)S(1)}, bf16[2,2,2,24,768]{4,3,2,1,0:T(8,128)(2,1)S(1)}, u32[]{:S(2)}, u32[]{:S(2)}) collective-permute-start(bf16[2,2,2,24,768]{4,3,2,1,0:T(8,128)(2,1)S(1)} %fusion.83), channel_id=1, source_target_pairs={{0,8},{1,9},{2,10},{3,11},{4,12},{5,13},{6,14},{7,15},{8,0},{9,1},... | collective-permute-start | bytes 884744 | tf_op jit(solution)/shard_map/ppermute | solution.py:320
  469.7 9.2 %collective-permute-start.50 = (bf16[2,2,2,24,768]{4,3,2,1,0:T(8,128)(2,1)S(1)}, bf16[2,2,2,24,768]{4,3,2,1,0:T(8,128)(2,1)S(1)}, u32[]{:S(2)}, u32[]{:S(2)}) collective-permute-start(bf16[2,2,2,24,768]{4,3,2,1,0:T(8,128)(2,1)S(1)} %fusion.82), channel_id=1, source_target_pairs={{0,4},{1,5},{2,6},{3,7},{4,0},{5,1},{6,2},{7,3},{8,12},{9,13},{10,... | collective-permute-start | bytes 884744 | tf_op jit(solution)/shard_map/ppermute | solution.py:320
  470.1 11.0 %collective-permute-start.46 = (bf16[2,2,2,24,896]{4,3,2,1,0:T(8,128)(2,1)S(1)}, bf16[2,2,2,24,896]{4,3,2,1,0:T(8,128)(2,1)S(1)}, u32[]{:S(2)}, u32[]{:S(2)}) collective-permute-start(bf16[2,2,2,24,896]{4,3,2,1,0:T(8,128)(2,1)S(1)} %fusion.73), channel_id=1, source_target_pairs={{0,1},{1,0},{2,3},{3,2},{4,5},{5,4},{6,7},{7,6},{8,9},{9,8},{10,11... | collective-permute-start | bytes 1032200 | tf_op jit(solution)/shard_map/ppermute | solution.py:320
  475.1 8.2 %collective-permute-start.55 = (bf16[2,2,24,768]{3,2,1,0:T(8,128)(2,1)S(1)}, bf16[2,2,24,768]{3,2,1,0:T(8,128)(2,1)S(1)}, u32[]{:S(2)}, u32[]{:S(2)}) collective-permute-start(bf16[2,2,24,768]{3,2,1,0:T(8,128)(2,1)S(1)} %fusion.95), channel_id=1, source_target_pairs={{0,1},{1,0},{2,3},{3,2},{4,5},{5,4},{6,7},{7,6},{8,9},{9,8},{10,11... | collective-permute-start | bytes 442376 | tf_op jit(solution)/shard_map/ppermute | solution.py:320
  479.0 6.1 %collective-permute-start.51 = (bf16[2,2,24,768]{3,2,1,0:T(8,128)(2,1)S(1)}, bf16[2,2,24,768]{3,2,1,0:T(8,128)(2,1)S(1)}, u32[]{:S(2)}, u32[]{:S(2)}) collective-permute-start(bf16[2,2,24,768]{3,2,1,0:T(8,128)(2,1)S(1)} %fusion.94), channel_id=1, source_target_pairs={{0,8},{1,9},{2,10},{3,11},{4,12},{5,13},{6,14},{7,15},{8,0},{9,1},... | collective-permute-start | bytes 442376 | tf_op jit(solution)/shard_map/ppermute | solution.py:320
  481.3 10.2 %collective-permute-start.47 = (bf16[2,2,24,896]{3,2,1,0:T(8,128)(2,1)S(1)}, bf16[2,2,24,896]{3,2,1,0:T(8,128)(2,1)S(1)}, u32[]{:S(2)}, u32[]{:S(2)}) collective-permute-start(bf16[2,2,24,896]{3,2,1,0:T(8,128)(2,1)S(1)} %fusion.93), channel_id=1, source_target_pairs={{0,4},{1,5},{2,6},{3,7},{4,0},{5,1},{6,2},{7,3},{8,12},{9,13},{10,... | collective-permute-start | bytes 516104 | tf_op jit(solution)/shard_map/ppermute | solution.py:320
  483.3 18.3 %copy-start.42 = (f32[2,24,2304]{2,1,0:T(8,128)S(1)}, f32[2,24,2304]{2,1,0:T(8,128)}, u32[]{:S(2)}) copy-start(f32[2,24,2304]{2,1,0:T(8,128)} %param.22) | copy-start | bytes 1327108
  483.3 5.0 collective-permute-start.56
  485.1 16.5 %copy-start.45 = (f32[24,2304]{1,0:T(8,128)S(1)}, f32[24,2304]{1,0:T(8,128)}, u32[]{:S(2)}) copy-start(f32[24,2304]{1,0:T(8,128)} %param.16) | copy-start | bytes 663556
  485.2 4.6 collective-permute-start.52
  488.4 5.1 collective-permute-start.57
  489.8 4.9 collective-permute-start.53
  491.5 4.6 collective-permute-start.48
  496.1 5.4 %collective-permute-start.49 = (bf16[24,896]{1,0:T(8,128)(2,1)S(1)}, bf16[24,896]{1,0:T(8,128)(2,1)S(1)}, u32[]{:S(2)}, u32[]{:S(2)}) collective-permute-start(bf16[24,896]{1,0:T(8,128)(2,1)S(1)} %fusion.116), channel_id=1, source_target_pairs={{0,16},{1,17},{2,18},{3,19},{4,20},{5,21},{6,22},{7,23},{8,24},{9,... | collective-permute-start | bytes 129032 | tf_op jit(solution)/shard_map/ppermute | solution.py:320
  (77 other events, 386.5 us)
Sparse Core Ops, SparseCore 0:
  11.5 97.3 all-gather.1
